TPU v7x, 32 devices: a whole 2x2x4 slice. The times are simulated.
32 devices in a mesh: rep: 2 (over core), fsdp: 16 (over z, y, x).
Axes of the slice: x: 2, y: 2, z: 4, core: 2. Of those that a mesh axis runs over, the one named last changes fastest.
Arguments:
- hidden_in: bfloat16 [4096, 768], P(('rep', 'fsdp')), may hold values from -6 to 6
- targets: bfloat16 [4096, 768], P(('rep', 'fsdp')), may hold values from -6 to 6
- doc_ids: int32 [4096], P(('rep', 'fsdp')), may hold values from 0 to 15, as said below
- seg_nums: int32 [32], P(('rep', 'fsdp')), may hold values from 0 to 15, as said below
- valid_flags: int32 [4096], P(('rep', 'fsdp')), may hold values from 0 to 1, as said below
- seg_mats: bfloat16 [768, 9216], P('fsdp')
- seg_vecs: bfloat16 [9216], P('fsdp')
- cls_mats: bfloat16 [768, 9216], P('fsdp')
- cls_vecs: bfloat16 [9216], P('fsdp')
- seg_pos: bfloat16 [16, 768], replicated, may hold values from -3 to 3
Outputs:
- output: bfloat16 [4096, 768], P(('rep', 'fsdp'))
- input_grad: bfloat16 [4096, 768], P(('rep', 'fsdp'))
- seg_mats_grad: float32 [768, 9216], P('fsdp')
- seg_vecs_grad: float32 [9216], P('fsdp')
- cls_mats_grad: float32 [768, 9216], P('fsdp')
- cls_vecs_grad: float32 [9216], P('fsdp')
- seg_pos_grad: float32 [16, 768], replicated
- loss: float32 [], replicated
Inputs may be any that keep to these rules, and one draw needn't show every extreme that they name: `doc_ids`: all slots of one aligned segment of 128 slots share an id; within each sequence of 2048 slots a segment's id is the index, counted from the sequence's start, of the first segment of its document, and a fully padded segment carries its own index. `seg_nums`: A segment's index within its document; 0 for a fully padded segment. `valid_flags`: in each segment the valid slots come first; a segment is fully padded or holds one document's tokens with its first slot valid; only a document's last segment is partly padded, and fully padded segments follow all documents of their sequence.
All inputs are finite; a program needn't handle non-finite values.
Results may differ from a plain program's by a relative error of at most 0.014.
Values may be sent and summed in bfloat16 or wider, within the bound.
No kernel may reach another device: no remote copies, remote signals or barrier semaphores. Data moves between devices by JAX's collectives and lax.ppermute only.
A program may use at most 192 MiB of HBM per device.

v0:
```python
import jax
import jax.numpy as jnp
from jax import lax
from jax.sharding import PartitionSpec as P

HEADS = 12
HEAD_DIM = 64
FF = 3072
SEG = 128
SEQ = 2048


NORM_EPS = 1e-05
MASK_FILL = -1e30
SQRT_HALF = 0.7071067811865476
INV_SQRT_TWO_PI = 0.3989422804014327


def swapped(value, axis, apart):
    mask = 2**apart
    pairs = [(source, source ^ mask) for source in range(lax.axis_size(axis))]
    return lax.ppermute(value, axis, pairs)


def product_plain(left_side, right_side):
    return jnp.dot(left_side, right_side, preferred_element_type=jnp.float32)


def product_left(left_side, right_side):
    return lax.dot_general(
        left_side, right_side, (((0,), (0,)), ((), ())), preferred_element_type=jnp.float32
    )


def product_right(left_side, right_side):
    return lax.dot_general(
        left_side, right_side, (((1,), (1,)), ((), ())), preferred_element_type=jnp.float32
    )


def row_total(array_in):
    return jnp.sum(array_in.astype(jnp.float32), axis=0)


def unpack_weights(gathered, model_width, ff_width):
    matrix, vector = gathered
    vector = vector.astype(jnp.float32)
    pieces = tuple(
        (vector[offset * model_width : (offset + 1) * model_width] for offset in range(8))
    )
    return (
        (
            matrix[:, : 3 * model_width],
            matrix[:, 3 * model_width : 4 * model_width],
            matrix[:, 4 * model_width : 4 * model_width + ff_width],
            matrix[:, 4 * model_width + ff_width :],
        )
        + pieces
        + (vector[8 * model_width :],)
    )


def norm_forward(summed, gain_vec, shift_vec):
    row_mean = jnp.mean(summed, axis=-1, keepdims=True)
    centered = summed - row_mean
    inv_dev = lax.rsqrt(jnp.mean(centered * centered, axis=-1, keepdims=True) + NORM_EPS)
    normed = centered * inv_dev
    return (normed * gain_vec + shift_vec, normed, inv_dev)


def norm_backward(grad_out, normed, inv_dev, gain_vec):
    scaled = grad_out * gain_vec
    mean_one = jnp.mean(scaled, axis=-1, keepdims=True)
    mean_two = jnp.mean(scaled * normed, axis=-1, keepdims=True)
    grad_in = inv_dev * (scaled - mean_one - normed * mean_two)
    return (grad_in, jnp.sum(grad_out * normed, axis=0), jnp.sum(grad_out, axis=0))


def gelu_value(before):
    return 0.5 * before * (1.0 + lax.erf(before * SQRT_HALF))


def gelu_slope(before):
    return (
        0.5 * (1.0 + lax.erf(before * SQRT_HALF))
        + before * jnp.exp(-0.5 * before * before) * INV_SQRT_TWO_PI
    )


def attention_scores(queries, keys_in, allowed, score_scale):
    raw_scores = (
        jnp.einsum("bqhe,bkhe->bhqk", queries, keys_in, preferred_element_type=jnp.float32)
        * score_scale
    )
    return jnp.where(allowed, raw_scores, MASK_FILL)


def attention_forward(queries, keys_in, values, allowed, score_scale):
    scores = attention_scores(queries, keys_in, allowed, score_scale)
    row_top = jnp.max(scores, axis=-1, keepdims=True)
    log_total = row_top + jnp.log(jnp.sum(jnp.exp(scores - row_top), axis=-1, keepdims=True))
    weights = jnp.exp(scores - log_total).astype(jnp.bfloat16)
    mixed_rows = jnp.einsum("bhqk,bkhe->bqhe", weights, values, preferred_element_type=jnp.float32)
    return (mixed_rows, log_total)


def attention_backward(queries, keys_in, values, allowed, score_scale, log_total, grad_mixed):
    probabilities = jnp.exp(attention_scores(queries, keys_in, allowed, score_scale) - log_total)
    grad_probs = jnp.einsum(
        "bqhe,bkhe->bhqk", grad_mixed, values, preferred_element_type=jnp.float32
    )
    inner_sum = jnp.sum(grad_probs * probabilities, axis=-1, keepdims=True)
    grad_scores = (probabilities * (grad_probs - inner_sum)).astype(jnp.bfloat16)
    grad_query = (
        jnp.einsum("bhqk,bkhe->bqhe", grad_scores, keys_in, preferred_element_type=jnp.float32)
        * score_scale
    )
    grad_key = (
        jnp.einsum("bhqk,bqhe->bkhe", grad_scores, queries, preferred_element_type=jnp.float32)
        * score_scale
    )
    grad_value = jnp.einsum(
        "bhqk,bqhe->bkhe",
        probabilities.astype(jnp.bfloat16),
        grad_mixed,
        preferred_element_type=jnp.float32,
    )
    return (grad_query, grad_key, grad_value)


def block_forward(rows_in, unpacked, attend):
    (
        qkv_weight,
        out_weight,
        up_weight,
        down_weight,
        query_bias,
        value_bias,
        out_bias,
        down_bias,
        gain_first,
        shift_first,
        gain_second,
        shift_second,
        up_bias,
    ) = unpacked
    model_width = rows_in.shape[1]
    inputs = rows_in.astype(jnp.bfloat16)
    projected = product_plain(inputs, qkv_weight)
    queries = (projected[:, :model_width] + query_bias).astype(jnp.bfloat16)
    keys_in = projected[:, model_width : 2 * model_width].astype(jnp.bfloat16)
    values = (projected[:, 2 * model_width :] + value_bias).astype(jnp.bfloat16)
    mixed_rows, attend_kept = attend(queries, keys_in, values)
    mixed_rows = mixed_rows.astype(jnp.bfloat16)
    summed_first = rows_in + product_plain(mixed_rows, out_weight) + out_bias
    first_out, normed_first, inv_first = norm_forward(summed_first, gain_first, shift_first)
    first_low = first_out.astype(jnp.bfloat16)
    pre_act = product_plain(first_low, up_weight) + up_bias
    activated = gelu_value(pre_act).astype(jnp.bfloat16)
    summed_second = first_out + product_right(activated, down_weight) + down_bias
    block_out, normed_second, inv_second = norm_forward(summed_second, gain_second, shift_second)
    saved_state = (
        inputs,
        queries,
        keys_in,
        values,
        attend_kept,
        mixed_rows,
        normed_first,
        inv_first,
        first_low,
        pre_act,
        activated,
        normed_second,
        inv_second,
    )
    return (block_out, saved_state)


def block_backward(grad_out, unpacked, saved_state, attend_back):
    (
        qkv_weight,
        out_weight,
        up_weight,
        down_weight,
        query_bias,
        value_bias,
        out_bias,
        down_bias,
        gain_first,
        shift_first,
        gain_second,
        shift_second,
        up_bias,
    ) = unpacked
    (
        inputs,
        queries,
        keys_in,
        values,
        attend_kept,
        mixed_rows,
        normed_first,
        inv_first,
        first_low,
        pre_act,
        activated,
        normed_second,
        inv_second,
    ) = saved_state
    grad_second, grad_gain_second, grad_shift_second = norm_backward(
        grad_out, normed_second, inv_second, gain_second
    )
    second_low = grad_second.astype(jnp.bfloat16)
    grad_down = product_left(second_low, activated)
    grad_pre = (product_plain(second_low, down_weight) * gelu_slope(pre_act)).astype(jnp.bfloat16)
    grad_up = product_left(first_low, grad_pre)
    grad_first = grad_second + product_right(grad_pre, up_weight)
    grad_summed, grad_gain_first, grad_shift_first = norm_backward(
        grad_first, normed_first, inv_first, gain_first
    )
    branch_low = grad_summed.astype(jnp.bfloat16)
    grad_out_weight = product_left(mixed_rows, branch_low)
    grad_mixed = product_right(branch_low, out_weight).astype(jnp.bfloat16)
    grad_query, grad_key, grad_value = attend_back(
        queries, keys_in, values, attend_kept, grad_mixed
    )
    grad_proj = jnp.concatenate([grad_query, grad_key, grad_value], axis=1)
    grad_qkv = product_left(inputs, grad_proj)
    grad_rows = grad_summed + product_right(grad_proj, qkv_weight)
    vector_grad = jnp.concatenate(
        [
            row_total(grad_query),
            row_total(grad_value),
            row_total(branch_low),
            row_total(second_low),
            grad_gain_first,
            grad_shift_first,
            grad_gain_second,
            grad_shift_second,
            row_total(grad_pre),
        ]
    )
    return (grad_rows, grad_qkv, grad_out_weight, grad_up, grad_down, vector_grad)


def local(
    hidden_in,
    targets,
    doc_ids,
    seg_nums,
    valid_flags,
    seg_mats,
    seg_vecs,
    cls_mats,
    cls_vecs,
    seg_pos,
):
    tok_rows, model_width = hidden_in.shape
    ff_width = FF
    seg_len = SEG
    group_span = SEQ // tok_rows
    seg_count = tok_rows // seg_len
    score_scale = HEAD_DIM ** (-0.5)
    head_shape = (HEADS, HEAD_DIM)
    live_rows = valid_flags.astype(jnp.float32)
    rank_full = lax.axis_index("fsdp")
    seg_gathered = (
        lax.all_gather(seg_mats, "fsdp", axis=0, tiled=True),
        lax.all_gather(seg_vecs, "fsdp", axis=0, tiled=True),
    )
    seg_unpacked = unpack_weights(seg_gathered, model_width, ff_width)
    cls_gathered = (
        lax.all_gather(cls_mats, "fsdp", axis=0, tiled=True),
        lax.all_gather(cls_vecs, "fsdp", axis=0, tiled=True),
    )
    cls_unpacked = unpack_weights(cls_gathered, model_width, ff_width)
    seg_allowed = (live_rows.reshape(seg_count, 1, 1, seg_len) > 0.5) | jnp.eye(seg_len, dtype=bool)
    seg_shape = (seg_count, seg_len) + head_shape

    def seg_attend(queries, keys_in, values):
        mixed_rows, log_total = attention_forward(
            queries.reshape(seg_shape),
            keys_in.reshape(seg_shape),
            values.reshape(seg_shape),
            seg_allowed,
            score_scale,
        )
        return (mixed_rows.reshape(tok_rows, model_width), log_total)

    def seg_attend_back(queries, keys_in, values, log_total, grad_mixed):
        grad_parts = attention_backward(
            queries.reshape(seg_shape),
            keys_in.reshape(seg_shape),
            values.reshape(seg_shape),
            seg_allowed,
            score_scale,
            log_total,
            grad_mixed.reshape(seg_shape),
        )
        return tuple(
            (
                grad_part.reshape(tok_rows, model_width).astype(jnp.bfloat16)
                for grad_part in grad_parts
            )
        )

    first_out, seg_saved = block_forward(hidden_in.astype(jnp.float32), seg_unpacked, seg_attend)
    first_grid = first_out.reshape(seg_count, seg_len, model_width)
    position_hot = (seg_nums[:, None] == jnp.arange(seg_pos.shape[0])[None, :]).astype(jnp.float32)
    position_rows = jnp.sum(
        position_hot[:, :, None] * seg_pos.astype(jnp.float32)[None, :, :], axis=1
    )
    heads_in = first_grid[:, 0, :] + position_rows
    lead_live = live_rows.reshape(seg_count, seg_len)[:, 0]
    lead_doc = doc_ids.reshape(seg_count, seg_len)[:, 0]
    lead_labels = jnp.where(lead_live > 0.5, lead_doc, -1).astype(jnp.bfloat16)
    lead_doc_low = lead_doc.astype(jnp.bfloat16)
    bit_count = group_span.bit_length() - 1
    key_total = group_span * seg_count
    own_slot = rank_full % group_span * seg_count + jnp.arange(seg_count)
    query_shape = (1, seg_count) + head_shape
    key_shape = (1, key_total) + head_shape

    def cls_attend(queries, keys_in, values):
        paired = jnp.concatenate([keys_in, values], axis=1)
        labels = lead_labels
        for bit_level in range(bit_count):
            other_pair, other_labels = swapped((paired, labels), "fsdp", bit_level)
            upper_half = rank_full // (1 << bit_level) % 2 == 1
            paired = jnp.where(
                upper_half,
                jnp.concatenate([other_pair, paired]),
                jnp.concatenate([paired, other_pair]),
            )
            labels = jnp.where(
                upper_half,
                jnp.concatenate([other_labels, labels]),
                jnp.concatenate([labels, other_labels]),
            )
        allowed = (labels[None, :] == lead_doc_low[:, None]) | (
            jnp.arange(key_total)[None, :] == own_slot[:, None]
        )
        allowed = allowed[None, None]
        mixed_rows, log_total = attention_forward(
            queries.reshape(query_shape),
            paired[:, :model_width].reshape(key_shape),
            paired[:, model_width:].reshape(key_shape),
            allowed,
            score_scale,
        )
        return (mixed_rows.reshape(seg_count, model_width), (paired, allowed, log_total))

    def cls_attend_back(queries, keys_in, values, attend_kept, grad_mixed):
        paired, allowed, log_total = attend_kept
        grad_query, grad_key, grad_value = attention_backward(
            queries.reshape(query_shape),
            paired[:, :model_width].reshape(key_shape),
            paired[:, model_width:].reshape(key_shape),
            allowed,
            score_scale,
            log_total,
            grad_mixed.reshape(query_shape),
        )
        grad_pair = jnp.concatenate(
            [grad_key.reshape(key_total, model_width), grad_value.reshape(key_total, model_width)],
            axis=1,
        )
        for bit_level in reversed(range(bit_count)):
            half_rows = grad_pair.shape[0] // 2
            upper_half = rank_full // (1 << bit_level) % 2 == 1
            kept_half = jnp.where(upper_half, grad_pair[half_rows:], grad_pair[:half_rows])
            sent_half = jnp.where(upper_half, grad_pair[:half_rows], grad_pair[half_rows:])
            grad_pair = kept_half + swapped(
                sent_half.astype(jnp.bfloat16), "fsdp", bit_level
            ).astype(sent_half.dtype)
        grad_pair = grad_pair.astype(jnp.bfloat16)
        return (
            grad_query.reshape(seg_count, model_width).astype(jnp.bfloat16),
            grad_pair[:, :model_width],
            grad_pair[:, model_width:],
        )

    top_out, cls_saved = block_forward(heads_in, cls_unpacked, cls_attend)
    combined = jnp.concatenate([top_out[:, None, :], first_grid[:, 1:, :]], axis=1).reshape(
        tok_rows, model_width
    )
    output_rows = combined * live_rows[:, None]
    diff_rows = (output_rows - targets.astype(jnp.float32)) * live_rows[:, None]
    count_all, square_all = lax.psum(
        (jnp.sum(live_rows), jnp.sum(diff_rows * diff_rows)), ("rep", "fsdp")
    )
    loss_value = square_all / (count_all * model_width)
    slots_all = tok_rows * lax.axis_size("rep") * lax.axis_size("fsdp")
    grad_grid = (diff_rows * (slots_all / count_all)).reshape(seg_count, seg_len, model_width)
    cls_back = unpack_weights(
        (
            lax.all_gather(cls_mats, "fsdp", axis=0, tiled=True),
            lax.all_gather(cls_vecs, "fsdp", axis=0, tiled=True),
        ),
        model_width,
        ff_width,
    )
    heads_grad, cls_g_qkv, cls_g_out, cls_g_up, cls_g_down, cls_g_vec = block_backward(
        grad_grid[:, 0, :], cls_back, cls_saved, cls_attend_back
    )
    pos_local = jnp.sum(position_hot[:, :, None] * heads_grad[:, None, :], axis=0)
    seg_grad_out = jnp.concatenate([heads_grad[:, None, :], grad_grid[:, 1:, :]], axis=1).reshape(
        tok_rows, model_width
    )
    seg_back = unpack_weights(
        (
            lax.all_gather(seg_mats, "fsdp", axis=0, tiled=True),
            lax.all_gather(seg_vecs, "fsdp", axis=0, tiled=True),
        ),
        model_width,
        ff_width,
    )
    input_grad, seg_g_qkv, seg_g_out, seg_g_up, seg_g_down, seg_g_vec = block_backward(
        seg_grad_out, seg_back, seg_saved, seg_attend_back
    )
    owner_rows = tuple(
        (
            lax.psum_scatter(seg_g_qkv, "fsdp", scatter_dimension=0, tiled=True),
            lax.psum_scatter(seg_g_out, "fsdp", scatter_dimension=0, tiled=True),
            lax.psum_scatter(seg_g_up, "fsdp", scatter_dimension=0, tiled=True),
            lax.psum_scatter(seg_g_down, "fsdp", scatter_dimension=0, tiled=True),
            lax.psum_scatter(seg_g_vec, "fsdp", scatter_dimension=0, tiled=True),
            lax.psum_scatter(cls_g_qkv, "fsdp", scatter_dimension=0, tiled=True),
            lax.psum_scatter(cls_g_out, "fsdp", scatter_dimension=0, tiled=True),
            lax.psum_scatter(cls_g_up, "fsdp", scatter_dimension=0, tiled=True),
            lax.psum_scatter(cls_g_down, "fsdp", scatter_dimension=0, tiled=True),
            lax.psum_scatter(cls_g_vec, "fsdp", scatter_dimension=0, tiled=True),
        )
    )
    replica_share = (
        lax.psum_scatter(
            owner_rows[0].astype(jnp.bfloat16), "rep", scatter_dimension=1, tiled=True
        ).astype(jnp.float32),
        lax.psum_scatter(
            owner_rows[1].astype(jnp.bfloat16), "rep", scatter_dimension=1, tiled=True
        ).astype(jnp.float32),
        lax.psum_scatter(
            owner_rows[2].astype(jnp.bfloat16), "rep", scatter_dimension=1, tiled=True
        ).astype(jnp.float32),
        lax.psum_scatter(
            owner_rows[3].astype(jnp.bfloat16), "rep", scatter_dimension=1, tiled=True
        ).astype(jnp.float32),
        lax.psum_scatter(
            owner_rows[4].astype(jnp.bfloat16), "rep", scatter_dimension=0, tiled=True
        ).astype(jnp.float32),
        lax.psum_scatter(
            owner_rows[5].astype(jnp.bfloat16), "rep", scatter_dimension=1, tiled=True
        ).astype(jnp.float32),
        lax.psum_scatter(
            owner_rows[6].astype(jnp.bfloat16), "rep", scatter_dimension=1, tiled=True
        ).astype(jnp.float32),
        lax.psum_scatter(
            owner_rows[7].astype(jnp.bfloat16), "rep", scatter_dimension=1, tiled=True
        ).astype(jnp.float32),
        lax.psum_scatter(
            owner_rows[8].astype(jnp.bfloat16), "rep", scatter_dimension=1, tiled=True
        ).astype(jnp.float32),
        lax.psum_scatter(
            owner_rows[9].astype(jnp.bfloat16), "rep", scatter_dimension=0, tiled=True
        ).astype(jnp.float32),
    )
    all_summed = (
        lax.all_gather(replica_share[0].astype(jnp.bfloat16), "rep", axis=1, tiled=True).astype(
            jnp.float32
        ),
        lax.all_gather(replica_share[1].astype(jnp.bfloat16), "rep", axis=1, tiled=True).astype(
            jnp.float32
        ),
        lax.all_gather(replica_share[2].astype(jnp.bfloat16), "rep", axis=1, tiled=True).astype(
            jnp.float32
        ),
        lax.all_gather(replica_share[3].astype(jnp.bfloat16), "rep", axis=1, tiled=True).astype(
            jnp.float32
        ),
        lax.all_gather(replica_share[4].astype(jnp.bfloat16), "rep", axis=0, tiled=True).astype(
            jnp.float32
        ),
        lax.all_gather(replica_share[5].astype(jnp.bfloat16), "rep", axis=1, tiled=True).astype(
            jnp.float32
        ),
        lax.all_gather(replica_share[6].astype(jnp.bfloat16), "rep", axis=1, tiled=True).astype(
            jnp.float32
        ),
        lax.all_gather(replica_share[7].astype(jnp.bfloat16), "rep", axis=1, tiled=True).astype(
            jnp.float32
        ),
        lax.all_gather(replica_share[8].astype(jnp.bfloat16), "rep", axis=1, tiled=True).astype(
            jnp.float32
        ),
        lax.all_gather(replica_share[9].astype(jnp.bfloat16), "rep", axis=0, tiled=True).astype(
            jnp.float32
        ),
    )
    seg_summed = all_summed[:5]
    cls_summed = all_summed[5:]
    pos_total = lax.psum(pos_local, ("rep", "fsdp"))
    seg_mat_grad = jnp.concatenate(
        [seg_summed[0], seg_summed[1], seg_summed[2], seg_summed[3]], axis=1
    )
    cls_mat_grad = jnp.concatenate(
        [cls_summed[0], cls_summed[1], cls_summed[2], cls_summed[3]], axis=1
    )
    return (
        output_rows.astype(jnp.bfloat16),
        input_grad.astype(jnp.bfloat16),
        seg_mat_grad,
        seg_summed[4],
        cls_mat_grad,
        cls_summed[4],
        pos_total,
        loss_value,
    )


def solution(mesh):
    in_specs = (
        P(("rep", "fsdp"), None),
        P(("rep", "fsdp"), None),
        P(("rep", "fsdp")),
        P(("rep", "fsdp")),
        P(("rep", "fsdp")),
        P("fsdp", None),
        P("fsdp"),
        P("fsdp", None),
        P("fsdp"),
        P(),
    )
    out_specs = (
        P(("rep", "fsdp"), None),
        P(("rep", "fsdp"), None),
        P("fsdp", None),
        P("fsdp"),
        P("fsdp", None),
        P("fsdp"),
        P(),
        P(),
    )
    return jax.shard_map(local, mesh=mesh, in_specs=in_specs, out_specs=out_specs, check_vma=False)
```

profile of v0, /device:TPU:13, one launch (start us, length us, event | category | flops | bytes accessed | tf_op | source)
XLA Modules:
  0.0 1791.7 jit_solution(8329649650462088503)
XLA Ops:
  13.3 42.2 %psum.21 = f32[]{:T(128)} all-reduce(f32[]{:T(128)} %convert_reduce_fusion.6), channel_id=1, replica_groups=mesh['rep'=2,'fsdp'=16] {'rep','fsdp'}, use_global_device_ids=true, to_apply=%region_14.15 | all-reduce | flops 1 | bytes 8 | tf_op jit(solution)/shard_map/psum | solution.py:390
  59.9 53.5 %all-reduce.10 = (bf16[9216]{0:T(1024)(128)(2,1)S(1)}, bf16[9216]{0:T(1024)(128)(2,1)S(1)}) all-reduce(bf16[9216]{0:T(1024)(128)(2,1)S(1)} %dynamic-update-slice, bf16[9216]{0:T(1024)(128)(2,1)S(1)} %dynamic-update-slice.1), channel_id=1, replica_groups=mesh['rep'=2,'fsdp'=16] {'fsdp'}, use_global_device_ids=true, to_apply=%add | all-reduce | flops 18432 | bytes 73728
  116.3 63.8 %all-gather.3.cloned.1.call-done = bf16[768,9216]{1,0:T(8,128)(2,1)} async-done(((bf16[48,9216]{1,0:T(8,128)(2,1)}), bf16[768,9216]{1,0:T(8,128)(2,1)}) %all-gather.3.cloned.1.call-update) | async-done | bytes 14155792 | tf_op jit(solution)/shard_map/all_gather | solution.py:269
  189.5 4.9 fusion.150
  195.4 152.5 %all-gather.5.cloned.1.call-done = bf16[768,9216]{1,0:T(8,128)(2,1)} async-done(((bf16[48,9216]{1,0:T(8,128)(2,1)}), bf16[768,9216]{1,0:T(8,128)(2,1)}) %all-gather.5.cloned.1.call-update) | async-done | bytes 14155792 | tf_op jit(solution)/shard_map/all_gather | solution.py:274
  372.8 3.7 fusion.62
  388.4 3.7 fusion.59
  419.5 3.8 convert_reduce_fusion
  423.3 4.4 multiply_reduce_fusion.3
  433.6 3.9 convolution_bitcast_fusion
  437.5 8.1 copy.83
  450.3 4.7 broadcast_multiply_fusion
  455.8 4.7 broadcast_multiply_fusion.1
  461.9 5.0 fusion.112
  467.0 73.6 %reduce-scatter.39.cloned.1.call-done = f32[48,768]{1,0:T(8,128)} async-done(((f32[768,768]{1,0:T(8,128)}), f32[48,768]{1,0:T(8,128)}) %reduce-scatter.39.cloned.1.call-update) | async-done | bytes 147472 | tf_op jit(solution)/shard_map/reduce_scatter | solution.py:430
  542.4 131.3 %reduce-scatter.27.cloned.1.call-done = f32[48,768]{1,0:T(8,128)} async-done(((f32[768,768]{1,0:T(8,128)}), f32[48,768]{1,0:T(8,128)}) %reduce-scatter.27.cloned.1.call-update) | async-done | bytes 147472 | tf_op jit(solution)/shard_map/reduce_scatter | solution.py:425
  675.5 153.3 %reduce-scatter.49.cloned.1.call-done = f32[48,2304]{1,0:T(8,128)} async-done(((f32[768,2304]{1,0:T(8,128)}), f32[48,2304]{1,0:T(8,128)}) %reduce-scatter.49.cloned.1.call-update) | async-done | bytes 442384 | tf_op jit(solution)/shard_map/reduce_scatter | solution.py:424
  831.0 153.2 %reduce-scatter.37.cloned.1.call-done = f32[48,2304]{1,0:T(8,128)} async-done(((f32[768,2304]{1,0:T(8,128)}), f32[48,2304]{1,0:T(8,128)}) %reduce-scatter.37.cloned.1.call-update) | async-done | bytes 442384 | tf_op jit(solution)/shard_map/reduce_scatter | solution.py:429
  986.6 5.1 fusion.122
  994.6 165.9 %reduce-scatter.45.cloned.1.call-done = f32[48,3072]{1,0:T(8,128)} async-done(((f32[768,3072]{1,0:T(8,128)}), f32[48,3072]{1,0:T(8,128)}) %reduce-scatter.45.cloned.1.call-update) | async-done | bytes 589840 | tf_op jit(solution)/shard_map/reduce_scatter | solution.py:432
  1162.5 174.9 %reduce-scatter.41.cloned.1.call-done = f32[48,3072]{1,0:T(8,128)} async-done(((f32[768,3072]{1,0:T(8,128)}), f32[48,3072]{1,0:T(8,128)}) %reduce-scatter.41.cloned.1.call-update) | async-done | bytes 589840 | tf_op jit(solution)/shard_map/reduce_scatter | solution.py:431
  1339.4 173.5 %reduce-scatter.33.cloned.1.call-done = f32[48,3072]{1,0:T(8,128)} async-done(((f32[768,3072]{1,0:T(8,128)}), f32[48,3072]{1,0:T(8,128)}) %reduce-scatter.33.cloned.1.call-update) | async-done | bytes 589840 | tf_op jit(solution)/shard_map/reduce_scatter | solution.py:427
  1514.8 52.6 %all-reduce.9 = (bf16[9216]{0:T(1024)(128)(2,1)S(1)}, bf16[9216]{0:T(1024)(128)(2,1)S(1)}) all-reduce(f32[9216]{0:T(1024)S(1)} %constant_dynamic-update-slice_fusion.6, f32[9216]{0:T(1024)S(1)} %constant_dynamic-update-slice_fusion.7), channel_id=10, replica_groups=mesh['rep'=2,'fsdp'=16] {'fsdp'}, use_global_device_ids=true, to_apply=%region_42.43.clone | all-reduce | flops 18432 | bytes 110592
  1567.5 17.7 all-reduce.12
  1589.4 48.9 %all-reduce.8 = (f32[16,768]{1,0:T(8,128)}, f32[]{:T(128)}) all-reduce(f32[16,768]{1,0:T(8,128)S(1)} %broadcast_multiply_fusion.4, f32[]{:T(128)} %get-tuple-element.59), channel_id=1, replica_groups=mesh['rep'=2,'fsdp'=16] {'rep','fsdp'}, use_global_device_ids=true, to_apply=%region_54.55 | all-reduce | flops 12289 | bytes 98312 | tf_op jit(solution)/shard_map/psum | solution.py:502
  1638.9 4.0 fusion.51
  1643.8 4.4 all_gather.56
  1657.3 78.4 %reduce-scatter.29.cloned.1.call-done = f32[48,3072]{1,0:T(8,128)} async-done(((f32[768,3072]{1,0:T(8,128)}), f32[48,3072]{1,0:T(8,128)}) %reduce-scatter.29.cloned.1.call-update) | async-done | bytes 589840 | tf_op jit(solution)/shard_map/reduce_scatter | solution.py:426
  1737.6 9.0 reduce-scatter.47.cloned.1.call-done
  1748.9 8.7 reduce-scatter.43.cloned.1.call-done
  1761.2 7.9 reduce-scatter.35.cloned.1.call-done
  1771.4 8.7 reduce-scatter.31.cloned.1.call-done
  (322 shorter events, 133.4 us)
Async XLA Ops:
  7.2 173.0 %all-gather.3.cloned.1.call-start = ((), (), s32[]{:S(2)}) async-start(), calls=%async_computation.16 | async-start | bytes 15040512 | tf_op jit(solution)/shard_map/all_gather | solution.py:269
  7.9 340.0 %all-gather.5.cloned.1.call-start = ((), (), s32[]{:S(2)}) async-start(), calls=%async_computation.17 | async-start | bytes 15040512 | tf_op jit(solution)/shard_map/all_gather | solution.py:274
  8.6 531.9 %reduce-scatter.39.cloned.1.call-start = ((), (), s32[]{:S(2)}) async-start(), calls=%async_computation.24 | async-start | bytes 2506752 | tf_op jit(solution)/shard_map/reduce_scatter | solution.py:430
  11.3 339.6 %collective-permute-start.4 = (bf16[1]{0:T(256)(128)(2,1)}, bf16[1]{0:T(256)(128)(2,1)}, u32[]{:S(2)}, u32[]{:S(2)}) collective-permute-start(bf16[1]{0:T(256)(128)(2,1)} %bitcast.11), channel_id=1, source_target_pairs={{0,1},{1,0},{2,3},{3,2},{4,5},{5,4},{6,7},{7,6},{8,9},{9,8},{10,11... | collective-permute-start | bytes 14 | tf_op jit(solution)/shard_map/ppermute | solution.py:22
  350.6 2.5 collective-permute-start
  351.6 2.4 collective-permute-start.5
  353.2 3.1 collective-permute-start.1
  354.1 3.8 collective-permute-start.6
  356.3 3.3 collective-permute-start.2
  358.0 3.3 collective-permute-start.7
  359.6 3.7 collective-permute-start.3
  398.7 4.6 collective-permute-start.8
  404.0 2.6 collective-permute-start.9
  406.7 2.5 collective-permute-start.10
  407.5 266.2 %reduce-scatter.27.cloned.1.call-start = ((), (), s32[]{:S(2)}) async-start(), calls=%async_computation.18 | async-start | bytes 2506752 | tf_op jit(solution)/shard_map/reduce_scatter | solution.py:425
  409.2 2.5 collective-permute-start.11
  429.9 398.9 %reduce-scatter.49.cloned.1.call-start = ((), (), s32[]{:S(2)}) async-start(), calls=%async_computation.29 | async-start | bytes 7520256 | tf_op jit(solution)/shard_map/reduce_scatter | solution.py:424
  445.6 538.6 %reduce-scatter.37.cloned.1.call-start = ((), (), s32[]{:S(2)}) async-start(), calls=%async_computation.23 | async-start | bytes 7520256 | tf_op jit(solution)/shard_map/reduce_scatter | solution.py:429
  449.6 710.9 %reduce-scatter.45.cloned.1.call-start = ((), (), s32[]{:S(2)}) async-start(), calls=%async_computation.27 | async-start | bytes 10027008 | tf_op jit(solution)/shard_map/reduce_scatter | solution.py:432
  455.1 882.3 %reduce-scatter.41.cloned.1.call-start = ((), (), s32[]{:S(2)}) async-start(), calls=%async_computation.25 | async-start | bytes 10027008 | tf_op jit(solution)/shard_map/reduce_scatter | solution.py:431
  460.5 1052.4 %reduce-scatter.33.cloned.1.call-start = ((), (), s32[]{:S(2)}) async-start(), calls=%async_computation.21 | async-start | bytes 10027008 | tf_op jit(solution)/shard_map/reduce_scatter | solution.py:427
  466.9 1176.0 %reduce-scatter.57.cloned.1.call-start = ((), (), s32[]{:S(2)}) async-start(), calls=%async_computation.33 | async-start | bytes 294912
  542.3 1105.9 %reduce-scatter.53.cloned.1.call-start = ((), (), s32[]{:S(2)}) async-start(), calls=%async_computation.31 | async-start | bytes 294912
  675.5 975.6 %reduce-scatter.51.cloned.1.call-start = ((), (), s32[]{:S(2)}) async-start(), calls=%async_computation.30 | async-start | bytes 884736
  831.0 821.3 %reduce-scatter.55.cloned.1.call-start = ((), (), s32[]{:S(2)}) async-start(), calls=%async_computation.32 | async-start | bytes 884736
  986.4 749.4 %reduce-scatter.29.cloned.1.call-start = ((), (), s32[]{:S(2)}) async-start(), calls=%async_computation.19 | async-start | bytes 10027008 | tf_op jit(solution)/shard_map/reduce_scatter | solution.py:426
  991.7 347.5 %copy-start.16 = (f32[768]{0:T(1024)S(1)}, f32[768]{0:T(1024)}, u32[]{:S(2)}) copy-start(f32[768]{0:T(1024)} %get-tuple-element.62) | copy-start | bytes 9220
  991.7 347.6 %copy-start.28 = (f32[16]{0:T(128)S(1)}, f32[16]{0:T(128)}, u32[]{:S(2)}) copy-start(f32[16]{0:T(128)} %copy-done.27) | copy-start | bytes 196
  991.8 754.8 %reduce-scatter.47.cloned.1.call-start = ((), (), s32[]{:S(2)}) async-start(), calls=%async_computation.28 | async-start | bytes 442368 | tf_op jit(solution)/shard_map/reduce_scatter | solution.py:461
  1162.4 595.2 %reduce-scatter.43.cloned.1.call-start = ((), (), s32[]{:S(2)}) async-start(), calls=%async_computation.26 | async-start | bytes 442368 | tf_op jit(solution)/shard_map/reduce_scatter | solution.py:458
  1339.2 429.9 %reduce-scatter.35.cloned.1.call-start = ((), (), s32[]{:S(2)}) async-start(), calls=%async_computation.22 | async-start | bytes 442368 | tf_op jit(solution)/shard_map/reduce_scatter | solution.py:446
  1514.7 265.3 %reduce-scatter.31.cloned.1.call-start = ((), (), s32[]{:S(2)}) async-start(), calls=%async_computation.20 | async-start | bytes 442368 | tf_op jit(solution)/shard_map/reduce_scatter | solution.py:443
  (27 other events, 475.0 us)
Sparse Core Ops, SparseCore 0:
  10.8 169.3 all-gather.2
  183.0 164.9 all-gather.4
  407.6 132.9 reduce-scatter.38
  546.1 127.5 reduce-scatter.26
  678.9 149.9 reduce-scatter.48
  834.0 150.1 reduce-scatter.36
  989.9 170.5 reduce-scatter.44
  1167.1 170.2 reduce-scatter.40
  1343.1 169.7 reduce-scatter.32
  1515.1 8.8 reduce-scatter.56
  1526.2 8.6 reduce-scatter.52
  1537.8 9.1 reduce-scatter.50
  1549.3 9.1 reduce-scatter.54
  1565.0 170.7 reduce-scatter.28
  1737.8 8.7 reduce-scatter.46
  1748.7 8.8 reduce-scatter.42
  1760.2 8.8 reduce-scatter.34
  1771.2 8.8 reduce-scatter.30
where the time goes:
time: 1790 us
  waiting for transfers between devices  1360 us (76%)
  blocking collectives  237 us (13%)
  matrix products  67.6 us (4%)
  other arithmetic  51.5 us (3%)
  local copies, waits for them, and re-layouts  30.8 us (2%)
  between operations  28.2 us (2%)
    reduce_scatter x1, waiting for transfers between devices, local(): lax.psum_scatter(cls_g_up, 'fsdp', scatter_dimension=0, tiled=True)  175 us
    reduce_scatter x1, waiting for transfers between devices, local(): lax.psum_scatter(seg_g_down, 'fsdp', scatter_dimension=0, tiled=True)  174 us
    reduce_scatter x1, waiting for transfers between devices, local(): lax.psum_scatter(cls_g_down, 'fsdp', scatter_dimension=0, tiled=True)  166 us
    reduce_scatter x1, waiting for transfers between devices, local(): lax.psum_scatter(seg_g_qkv, 'fsdp', scatter_dimension=0, tiled=True)  153 us
    reduce_scatter x1, waiting for transfers between devices, local(): lax.psum_scatter(cls_g_qkv, 'fsdp', scatter_dimension=0, tiled=True)  153 us
    all_gather x1, waiting for transfers between devices, local(): lax.all_gather(cls_mats, 'fsdp', axis=0, tiled=True)  153 us
    reduce_scatter x1, waiting for transfers between devices, local(): lax.psum_scatter(seg_g_out, 'fsdp', scatter_dimension=0, tiled=True)  131 us
    unnamed x4, blocking collectives  126 us
  transfers between devices with their start and end apart: 30, of which 21 were waited for; matrix products, arithmetic and copies ran while one was open for 6% of the time, Pallas kernels for 0%

commit v1 on v0

--- a/solution.py
+++ b/solution.py
@@ -212,21 +212,17 @@
         grad_out, normed_second, inv_second, gain_second
     )
     second_low = grad_second.astype(jnp.bfloat16)
-    grad_down = product_left(second_low, activated)
     grad_pre = (product_plain(second_low, down_weight) * gelu_slope(pre_act)).astype(jnp.bfloat16)
-    grad_up = product_left(first_low, grad_pre)
     grad_first = grad_second + product_right(grad_pre, up_weight)
     grad_summed, grad_gain_first, grad_shift_first = norm_backward(
         grad_first, normed_first, inv_first, gain_first
     )
     branch_low = grad_summed.astype(jnp.bfloat16)
-    grad_out_weight = product_left(mixed_rows, branch_low)
     grad_mixed = product_right(branch_low, out_weight).astype(jnp.bfloat16)
     grad_query, grad_key, grad_value = attend_back(
         queries, keys_in, values, attend_kept, grad_mixed
     )
     grad_proj = jnp.concatenate([grad_query, grad_key, grad_value], axis=1)
-    grad_qkv = product_left(inputs, grad_proj)
     grad_rows = grad_summed + product_right(grad_proj, qkv_weight)
     vector_grad = jnp.concatenate(
         [
@@ -241,7 +237,29 @@
             row_total(grad_pre),
         ]
     )
-    return (grad_rows, grad_qkv, grad_out_weight, grad_up, grad_down, vector_grad)
+    weight_rows = (
+        inputs,
+        grad_proj,
+        mixed_rows,
+        branch_low,
+        first_low,
+        grad_pre,
+        second_low,
+        activated,
+    )
+    return (grad_rows, weight_rows, vector_grad)
+
+
+def weight_products(weight_rows):
+    inputs, grad_proj, mixed_rows, branch_low, first_low, grad_pre, second_low, activated = (
+        weight_rows
+    )
+    return (
+        product_left(inputs, grad_proj),
+        product_left(mixed_rows, branch_low),
+        product_left(first_low, grad_pre),
+        product_left(second_low, activated),
+    )
 
 
 def local(
@@ -401,9 +419,10 @@
         model_width,
         ff_width,
     )
-    heads_grad, cls_g_qkv, cls_g_out, cls_g_up, cls_g_down, cls_g_vec = block_backward(
+    heads_grad, cls_weight_rows, cls_g_vec = block_backward(
         grad_grid[:, 0, :], cls_back, cls_saved, cls_attend_back
     )
+    cls_g_qkv, cls_g_out, cls_g_up, cls_g_down = weight_products(cls_weight_rows)
     pos_local = jnp.sum(position_hot[:, :, None] * heads_grad[:, None, :], axis=0)
     seg_grad_out = jnp.concatenate([heads_grad[:, None, :], grad_grid[:, 1:, :]], axis=1).reshape(
         tok_rows, model_width
@@ -416,9 +435,10 @@
         model_width,
         ff_width,
     )
-    input_grad, seg_g_qkv, seg_g_out, seg_g_up, seg_g_down, seg_g_vec = block_backward(
+    input_grad, seg_weight_rows, seg_g_vec = block_backward(
         seg_grad_out, seg_back, seg_saved, seg_attend_back
     )
+    seg_g_qkv, seg_g_out, seg_g_up, seg_g_down = weight_products(seg_weight_rows)
     owner_rows = tuple(
         (
             lax.psum_scatter(seg_g_qkv, "fsdp", scatter_dimension=0, tiled=True),
@@ -518,6 +538,479 @@
     )
 
 
+LINE = 4
+PLANE = 4
+CORES = 2
+
+
+def line_pairs(apart):
+    total = LINE * PLANE
+    return [(source, (source + apart * PLANE) % total) for source in range(total)]
+
+
+def plane_pairs(mask):
+    return [(source, source ^ mask) for source in range(LINE * PLANE)]
+
+
+def along_line(value, apart):
+    return lax.ppermute(value, "fsdp", line_pairs(apart))
+
+
+def in_plane(value, mask):
+    return lax.ppermute(value, "fsdp", plane_pairs(mask))
+
+
+def other_core(value):
+    return lax.ppermute(value, "rep", [(0, 1), (1, 0)])
+
+
+def placed(whole, piece, *where):
+    return lax.dynamic_update_slice(whole, piece, where)
+
+
+def one_of(stack, index):
+    return lax.dynamic_index_in_dim(stack, index, 0, keepdims=False)
+
+
+def line_gather(piece, line_at):
+    whole = jnp.zeros((LINE,) + piece.shape, piece.dtype)
+    zeros = (0,) * piece.ndim
+    whole = placed(whole, piece[None], line_at, *zeros)
+    for apart in range(1, LINE):
+        whole = placed(
+            whole, along_line(piece, apart)[None], (line_at - apart) % LINE, *zeros
+        )
+    return whole
+
+
+def plane_gather(piece, plane_at):
+    whole = jnp.zeros((PLANE,) + piece.shape, piece.dtype)
+    zeros = (0,) * piece.ndim
+    whole = placed(whole, piece[None], plane_at, *zeros)
+    for mask in range(1, PLANE):
+        whole = placed(whole, in_plane(piece, mask)[None], plane_at ^ mask, *zeros)
+    return whole
+
+
+def plane_sum(piece):
+    return piece + in_plane(piece, 1) + in_plane(piece, 2) + in_plane(piece, 3)
+
+
+def weight_gather(piece, line_at, plane_at, core_at):
+    rows, columns = piece.shape
+    line = line_gather(piece, line_at)
+    half = LINE // 2
+    from_x, from_y = in_plane(line, 1), in_plane(line, 2)
+    far_low, far_high = in_plane(from_x[:half], 2), in_plane(from_y[half:], 1)
+    whole = jnp.zeros((LINE, PLANE, CORES, rows, columns), piece.dtype)
+    for block, at, low in (
+        (line, plane_at, 0),
+        (from_x, plane_at ^ 1, 0),
+        (from_y, plane_at ^ 2, 0),
+        (far_low, plane_at ^ 3, 0),
+        (far_high, plane_at ^ 3, half),
+    ):
+        whole = placed(whole, block[:, None, None], low, at, core_at, 0, 0)
+        whole = placed(whole, other_core(block)[:, None, None], low, at, 1 - core_at, 0, 0)
+    return whole.reshape(LINE * PLANE * CORES * rows, columns)
+
+
+def plane_reduce(part_of):
+    half = LINE // 2
+    far = part_of(3).astype(jnp.bfloat16)
+    from_y, from_x = in_plane(far[:half], 2), in_plane(far[half:], 1)
+    to_x, to_y = part_of(1), part_of(2)
+    to_x = jnp.concatenate([to_x[:half] + from_y.astype(jnp.float32), to_x[half:]])
+    to_y = jnp.concatenate([to_y[:half], to_y[half:] + from_x.astype(jnp.float32)])
+    got_x = in_plane(to_x.astype(jnp.bfloat16), 1)
+    got_y = in_plane(to_y.astype(jnp.bfloat16), 2)
+    kept = part_of(0) + got_x.astype(jnp.float32) + got_y.astype(jnp.float32)
+    sent = kept.astype(jnp.bfloat16)
+    total = kept[0]
+    for apart in range(1, LINE):
+        total = total + along_line(sent[apart], apart).astype(jnp.float32)
+    return total
+
+
+def slice_local(
+    hidden_in,
+    targets,
+    doc_ids,
+    seg_nums,
+    valid_flags,
+    seg_mats,
+    seg_vecs,
+    cls_mats,
+    cls_vecs,
+    seg_pos,
+):
+    tok_rows, model_width = hidden_in.shape
+    ff_width = FF
+    score_scale = HEAD_DIM ** (-0.5)
+    low, wide = jnp.bfloat16, jnp.float32
+    rank = lax.axis_index("fsdp")
+    core_at = lax.axis_index("rep")
+    line_at, plane_at = rank // PLANE, rank % PLANE
+    group = LINE * PLANE
+    own_rows, total_columns = seg_mats.shape
+    half_rows = own_rows // CORES
+    live_rows = valid_flags.astype(wide)
+
+    seg_half = one_of(seg_mats.reshape(CORES, half_rows, total_columns), core_at)
+    cls_half = one_of(cls_mats.reshape(CORES, half_rows, total_columns), core_at)
+    vec_size = seg_vecs.shape[0]
+    lanes = 128
+    vec_block = jnp.concatenate([seg_vecs, cls_vecs]).reshape(2 * vec_size // lanes, lanes)
+    count_row = jnp.full((1, lanes), jnp.sum(live_rows), wide).astype(low)
+    vec_block = jnp.concatenate(
+        [
+            vec_block,
+            count_row,
+            jnp.zeros((half_rows - vec_block.shape[0] - 1, lanes), low),
+        ]
+    )
+    edges = (0, 3 * model_width, 4 * model_width + ff_width, total_columns)
+    where_at = (line_at, plane_at, core_at)
+    qkv_full = weight_gather(
+        jnp.concatenate([seg_half[:, : edges[1]], vec_block], axis=1), *where_at
+    )
+    up_full = weight_gather(seg_half[:, edges[1] : edges[2]], *where_at)
+    down_full = weight_gather(
+        jnp.concatenate(
+            [seg_half[:, edges[2] :], cls_half[:, 3 * model_width : 4 * model_width]], axis=1
+        ),
+        *where_at,
+    )
+    qkv_weight = qkv_full[:, : edges[1]]
+    vec_rows = qkv_full[:, edges[1] :].reshape(group, CORES, half_rows, lanes)
+    vec_count = 2 * vec_size // lanes
+    count_all = jnp.sum(vec_rows[:, :, vec_count, 0].astype(wide))
+    both_vecs = vec_rows[:, 0, :vec_count].reshape(group, 2 * vec_size).astype(wide)
+    seg_vector = both_vecs[:, :vec_size].reshape(group * vec_size)
+    cls_vector = both_vecs[:, vec_size:].reshape(group * vec_size)
+    out_weight, up_weight = up_full[:, :model_width], up_full[:, model_width:]
+    down_weight, cls_out_full = down_full[:, :ff_width], down_full[:, ff_width:]
+
+    def pieces_of(vector):
+        return tuple(
+            vector[offset * model_width : (offset + 1) * model_width] for offset in range(8)
+        ) + (vector[8 * model_width :],)
+
+    seg_unpacked = (qkv_weight, out_weight, up_weight, down_weight) + pieces_of(seg_vector)
+
+    head_part = model_width // PLANE
+    ff_part = ff_width // PLANE
+    quarters = jnp.concatenate(
+        [
+            cls_half[:, : 3 * model_width]
+            .reshape(half_rows, 3, PLANE, head_part)
+            .transpose(2, 0, 1, 3)
+            .reshape(PLANE, half_rows, 3 * head_part),
+            cls_half[:, 4 * model_width : 4 * model_width + ff_width]
+            .reshape(half_rows, PLANE, ff_part)
+            .transpose(1, 0, 2),
+            cls_half[:, 4 * model_width + ff_width :]
+            .reshape(half_rows, PLANE, ff_part)
+            .transpose(1, 0, 2),
+        ],
+        axis=2,
+    )
+    quarter_width = quarters.shape[2]
+    plane_rows = jnp.zeros((PLANE, half_rows, quarter_width), low)
+    plane_rows = placed(plane_rows, one_of(quarters, plane_at)[None], plane_at, 0, 0)
+    for mask in range(1, PLANE):
+        plane_rows = placed(
+            plane_rows,
+            in_plane(one_of(quarters, plane_at ^ mask), mask)[None],
+            plane_at ^ mask,
+            0,
+            0,
+        )
+    quarter_rows = line_gather(plane_rows, line_at)[:, :, None]
+    quarter_full = jnp.zeros((LINE, PLANE, CORES, half_rows, quarter_width), low)
+    quarter_full = placed(quarter_full, quarter_rows, 0, 0, core_at, 0, 0)
+    quarter_full = placed(quarter_full, other_core(quarter_rows), 0, 0, 1 - core_at, 0, 0)
+    quarter_full = quarter_full.reshape(model_width, quarter_width)
+    cls_qkv = quarter_full[:, : 3 * head_part]
+    cls_up = quarter_full[:, 3 * head_part : 3 * head_part + ff_part]
+    cls_down = quarter_full[:, 3 * head_part + ff_part :]
+    cls_out = one_of(cls_out_full.reshape(PLANE, head_part, model_width), plane_at)
+
+    seg_allowed = (live_rows.reshape(1, 1, 1, tok_rows) > 0.5) | jnp.eye(tok_rows, dtype=bool)
+    seg_shape = (1, tok_rows, HEADS, HEAD_DIM)
+
+    def seg_attend(queries, keys_in, values):
+        mixed_rows, log_total = attention_forward(
+            queries.reshape(seg_shape),
+            keys_in.reshape(seg_shape),
+            values.reshape(seg_shape),
+            seg_allowed,
+            score_scale,
+        )
+        return (mixed_rows.reshape(tok_rows, model_width), log_total)
+
+    def seg_attend_back(queries, keys_in, values, log_total, grad_mixed):
+        grad_parts = attention_backward(
+            queries.reshape(seg_shape),
+            keys_in.reshape(seg_shape),
+            values.reshape(seg_shape),
+            seg_allowed,
+            score_scale,
+            log_total,
+            grad_mixed.reshape(seg_shape),
+        )
+        return tuple(part.reshape(tok_rows, model_width).astype(low) for part in grad_parts)
+
+    first_out, seg_saved = block_forward(hidden_in.astype(wide), seg_unpacked, seg_attend)
+    not_head = (jnp.arange(tok_rows) > 0).astype(wide)[:, None]
+    target_rows = targets.astype(wide)
+    plain_diff = (first_out * live_rows[:, None] - target_rows) * live_rows[:, None]
+    rest_square = jnp.sum(plain_diff * plain_diff * not_head)
+
+    own_num = seg_nums.astype(wide)
+    position_hot = (seg_nums[:, None] == jnp.arange(seg_pos.shape[0])[None, :]).astype(wide)
+    position_row = jnp.sum(position_hot[:, :, None] * seg_pos.astype(wide)[None, :, :], axis=1)
+    facts = jnp.concatenate(
+        [
+            live_rows[:1],
+            doc_ids[:1].astype(wide),
+            own_num,
+            rest_square[None],
+            jnp.zeros((lanes - 4,), wide),
+        ]
+    )[None]
+    head_row = jnp.concatenate([first_out[:1] + position_row, target_rows[:1], facts], axis=1)
+    all_heads = plane_gather(line_gather(head_row, line_at), plane_at)
+    all_heads = all_heads.transpose(1, 0, 2, 3).reshape(group, head_row.shape[1])
+    heads_in = all_heads[:, :model_width]
+    head_targets = all_heads[:, model_width : 2 * model_width]
+    head_facts = all_heads[:, 2 * model_width :]
+    head_live, head_doc, head_num = (head_facts[:, at] for at in range(3))
+    rest_total = jnp.sum(head_facts[:, 3])
+
+    (
+        query_bias,
+        value_bias,
+        out_bias,
+        down_bias,
+        gain_first,
+        shift_first,
+        gain_second,
+        shift_second,
+        up_bias,
+    ) = pieces_of(cls_vector)
+    query_bias = one_of(query_bias.reshape(PLANE, head_part), plane_at)
+    value_bias = one_of(value_bias.reshape(PLANE, head_part), plane_at)
+    up_bias = one_of(up_bias.reshape(PLANE, ff_part), plane_at)
+    allowed = ((head_live[None, :] > 0.5) & (head_doc[:, None] == head_doc[None, :])) | jnp.eye(
+        group, dtype=bool
+    )
+    allowed = allowed[None, None]
+    part_shape = (1, group, HEADS // PLANE, HEAD_DIM)
+    cls_inputs = heads_in.astype(low)
+    projected = product_plain(cls_inputs, cls_qkv)
+    queries = (projected[:, :head_part] + query_bias).astype(low).reshape(part_shape)
+    keys_in = projected[:, head_part : 2 * head_part].astype(low).reshape(part_shape)
+    values = (projected[:, 2 * head_part :] + value_bias).astype(low).reshape(part_shape)
+    mixed, log_total = attention_forward(queries, keys_in, values, allowed, score_scale)
+    mixed = mixed.reshape(group, head_part).astype(low)
+    summed_first = heads_in + plane_sum(product_plain(mixed, cls_out)) + out_bias
+    cls_first, normed_first, inv_first = norm_forward(summed_first, gain_first, shift_first)
+    cls_first_low = cls_first.astype(low)
+    pre_act = product_plain(cls_first_low, cls_up) + up_bias
+    activated = gelu_value(pre_act).astype(low)
+    summed_second = cls_first + plane_sum(product_right(activated, cls_down)) + down_bias
+    top_out, normed_second, inv_second = norm_forward(summed_second, gain_second, shift_second)
+
+    out_scale = (tok_rows * group * CORES) / count_all
+    head_diff = (top_out * head_live[:, None] - head_targets) * head_live[:, None]
+    square_all = rest_total + jnp.sum(head_diff * head_diff)
+    square_all = square_all + other_core(jnp.full((8, lanes), square_all))[0, 0]
+    loss_value = square_all / (count_all * model_width)
+    top_row = lax.dynamic_slice(top_out, (rank, 0), (1, model_width))
+    output_rows = jnp.concatenate([top_row, first_out[1:]]) * live_rows[:, None]
+
+    grad_top = head_diff * out_scale
+    grad_second, grad_gain_second, grad_shift_second = norm_backward(
+        grad_top, normed_second, inv_second, gain_second
+    )
+    second_low = grad_second.astype(low)
+    grad_pre = (product_plain(second_low, cls_down) * gelu_slope(pre_act)).astype(low)
+    grad_first = grad_second + plane_sum(product_right(grad_pre, cls_up))
+    grad_summed, grad_gain_first, grad_shift_first = norm_backward(
+        grad_first, normed_first, inv_first, gain_first
+    )
+    branch_low = grad_summed.astype(low)
+    grad_mixed = product_right(branch_low, cls_out).astype(low).reshape(part_shape)
+    grad_parts = attention_backward(
+        queries, keys_in, values, allowed, score_scale, log_total, grad_mixed
+    )
+    grad_proj = jnp.concatenate(
+        [part.reshape(group, head_part).astype(low) for part in grad_parts], axis=1
+    )
+    heads_grad = grad_summed + plane_sum(product_right(grad_proj, cls_qkv))
+    head_row_grad = lax.dynamic_slice(heads_grad, (rank, 0), (1, model_width))
+    number_hot = (jnp.arange(seg_pos.shape[0])[:, None] == head_num[None, :]).astype(wide)
+    pos_local = jnp.dot(number_hot, heads_grad, precision=lax.Precision.HIGHEST)
+    pos_total = pos_local + other_core(pos_local)
+
+    shared = plane_gather(
+        jnp.concatenate([grad_proj, mixed, grad_pre, activated], axis=1), plane_at
+    )
+    shared = shared.transpose(1, 0, 2)
+    cuts = (0, head_part, 2 * head_part, 3 * head_part, 4 * head_part)
+    pieces = [shared[:, :, cuts[at] : cuts[at + 1]].reshape(group, model_width) for at in range(4)]
+    pieces += [
+        shared[:, :, cuts[4] : cuts[4] + ff_part].reshape(group, ff_width),
+        shared[:, :, cuts[4] + ff_part :].reshape(group, ff_width),
+    ]
+    grad_q, grad_k, grad_v, mixed_all, grad_pre_all, activated_all = pieces
+    row_data = jnp.concatenate(
+        [
+            cls_inputs,
+            grad_q,
+            grad_k,
+            grad_v,
+            mixed_all,
+            branch_low,
+            cls_first_low,
+            grad_pre_all,
+            second_low,
+            activated_all,
+        ],
+        axis=1,
+    )
+    row_data = jnp.concatenate([row_data, other_core(row_data)])
+    sizes = (
+        model_width,
+        3 * model_width,
+        model_width,
+        model_width,
+        model_width,
+        ff_width,
+        model_width,
+        ff_width,
+    )
+    row_parts, start = [], 0
+    for size in sizes:
+        row_parts.append(row_data[:, start : start + size])
+        start += size
+    own_hot = (
+        jnp.arange(model_width)[:, None] == rank * own_rows + jnp.arange(own_rows)[None, :]
+    ).astype(low)
+
+    def own_features(values_in):
+        return product_plain(values_in, own_hot).astype(low)
+
+    cls_mat_grad = jnp.concatenate(
+        [
+            product_left(own_features(row_parts[left]), row_parts[right])
+            for left, right in ((0, 1), (2, 3), (4, 5), (6, 7))
+        ],
+        axis=1,
+    )
+    norm_grads = jnp.stack(
+        [grad_gain_first, grad_shift_first, grad_gain_second, grad_shift_second]
+    )
+    norm_grads = norm_grads + other_core(norm_grads)
+    cls_vec_all = jnp.concatenate(
+        [
+            row_total(row_parts[1][:, :model_width]),
+            row_total(row_parts[1][:, 2 * model_width :]),
+            row_total(row_parts[3]),
+            row_total(row_parts[6]),
+            norm_grads.reshape(4 * model_width),
+            row_total(row_parts[5]),
+        ]
+    )
+    cls_vec_grad = one_of(cls_vec_all.reshape(group, vec_size), rank)
+
+    seg_grad_out = jnp.concatenate([head_row_grad, (plain_diff * out_scale)[1:]])
+    input_grad, seg_rows, vector_grad = block_backward(
+        seg_grad_out, seg_unpacked, seg_saved, seg_attend_back
+    )
+    seg_inputs, seg_proj, seg_mixed, seg_branch, seg_first, seg_pre, seg_second, seg_act = seg_rows
+
+    def both_cores(values_in):
+        return jnp.concatenate([values_in, other_core(values_in)])
+
+    def own_half(values_in):
+        halves = values_in.reshape(tok_rows, CORES, -1).transpose(1, 0, 2)
+        return jnp.concatenate(
+            [one_of(halves, core_at), other_core(one_of(halves, 1 - core_at))]
+        )
+
+    column = jnp.arange(model_width)
+    mask_of, step_of, row_of = (
+        column // (LINE * own_rows),
+        column // own_rows % LINE,
+        column % own_rows,
+    )
+    source = ((line_at + step_of) % LINE * PLANE + (plane_at ^ mask_of)) * own_rows + row_of
+    order_hot = (jnp.arange(model_width)[:, None] == source[None, :]).astype(low)
+
+    def ordered(values_in):
+        return product_plain(values_in, order_hot).astype(low)
+
+    vec_parts = vector_grad.reshape(group, vec_size).astype(low)
+    rank_order = source.reshape(group, own_rows)[:, 0] // own_rows
+    rank_hot = (rank_order[:, None] == jnp.arange(group)[None, :]).astype(low)
+    vec_parts = product_plain(rank_hot, vec_parts)
+    vec_lines = -(-vec_size // lanes)
+    vec_parts = jnp.pad(vec_parts, ((0, 0), (0, vec_lines * lanes - vec_size)))
+    vec_parts = jnp.pad(
+        vec_parts.reshape(PLANE, LINE, vec_lines, lanes),
+        ((0, 0), (0, 0), (0, own_rows - vec_lines), (0, 0)),
+    )
+
+    def reduced(pairs_in, extra):
+        ready = [(ordered(both_cores(left)), own_half(right)) for left, right in pairs_in]
+        span = LINE * own_rows
+
+        def part_of(mask):
+            parts = [
+                product_left(left[:, mask * span : (mask + 1) * span], right).reshape(
+                    LINE, own_rows, right.shape[1]
+                )
+                for left, right in ready
+            ]
+            if extra is not None:
+                parts.append(extra[mask])
+            return jnp.concatenate(parts, axis=2)
+
+        return plane_reduce(part_of)
+
+    mlp_sum = reduced(((seg_first, seg_pre), (seg_second, seg_act)), None)
+    attn_sum = reduced(((seg_inputs, seg_proj), (seg_mixed, seg_branch)), vec_parts)
+    mine = jnp.concatenate([attn_sum, mlp_sum], axis=1)
+    theirs = other_core(mine)
+    first_half = jnp.where(core_at == 0, mine, theirs)
+    second_half = jnp.where(core_at == 0, theirs, mine)
+    qkv_half, out_half = 3 * model_width // CORES, model_width // CORES
+    up_half = ff_width // CORES
+    widths = (qkv_half, out_half, lanes, up_half, up_half)
+    starts = [sum(widths[:at]) for at in range(6)]
+    columns = []
+    for at in (0, 1, 3, 4):
+        columns += [
+            first_half[:, starts[at] : starts[at + 1]],
+            second_half[:, starts[at] : starts[at + 1]],
+        ]
+    seg_mat_grad = jnp.concatenate(columns, axis=1)
+    seg_vec_grad = (mine + theirs)[:vec_lines, starts[2] : starts[3]]
+    seg_vec_grad = seg_vec_grad.reshape(vec_lines * lanes)[:vec_size]
+    return (
+        output_rows.astype(low),
+        input_grad.astype(low),
+        seg_mat_grad,
+        seg_vec_grad,
+        cls_mat_grad,
+        cls_vec_grad,
+        pos_total,
+        loss_value,
+    )
+
+
 def solution(mesh):
     in_specs = (
         P(("rep", "fsdp"), None),
@@ -541,4 +1034,6 @@
         P(),
         P(),
     )
-    return jax.shard_map(local, mesh=mesh, in_specs=in_specs, out_specs=out_specs, check_vma=False)
+    one_slice = dict(mesh.shape) == {"rep": CORES, "fsdp": LINE * PLANE}
+    body = slice_local if one_slice else local
+    return jax.shard_map(body, mesh=mesh, in_specs=in_specs, out_specs=out_specs, check_vma=False)

time: 1790 us -> 440 us (0.25)
  waiting for transfers between devices: 1360 us -> 134 us
  blocking collectives: 237 us -> 0 us
  starting transfers between devices: 15.7 us -> 86.1 us
  local copies, waits for them, and re-layouts: 30.8 us -> 93 us
  between operations: 28.2 us -> 9.03 us
    reduce_scatter x12 -> x0, waiting for transfers between devices: 1140 us -> none  [the longest x1 175 us: local(): lax.psum_scatter(cls_g_up, 'fsdp', scatter_dimension=0, tiled=True)]
    all_gather x2 -> x0, waiting for transfers between devices: 216 us -> none  [the longest x1 153 us: local(): lax.all_gather(cls_mats, 'fsdp', axis=0, tiled=True)]
    ppermute x12 -> x91, waiting for transfers between devices: 4.73 us -> 134 us  [the longest x41 73.5 us: in_plane(): return lax.ppermute(value, 'fsdp', plane_pairs(mask))]
    unnamed x4 -> x0, blocking collectives: 126 us -> none
    psum x2 -> x0, blocking collectives: 91 us -> none  [the longest x1 48.9 us: local(): pos_total = lax.psum(pos_local, ('rep', 'fsdp'))]
    ppermute x12 -> x91, starting transfers between devices: 14.5 us -> 86.1 us  [the longest x41 31.4 us: in_plane(): return lax.ppermute(value, 'fsdp', plane_pairs(mask))]
    dynamic_update_slice x0 -> x60, local copies, waits for them, and re-layouts: none -> 35.4 us  [placed(): return lax.dynamic_update_slice(whole, piece, where)]
    all_gather x8 -> x0, blocking collectives: 19.3 us -> none  [the longest x1 4.42 us: local(): lax.all_gather(replica_share[6].astype(jnp.bfloat16), 'rep', axis=1, tile...]
  transfers between devices with their start and end apart: 30 -> 91, of which waited for: 21 -> 24; matrix products, arithmetic and copies ran while one was open for 6% -> 45% of each run, Pallas kernels for 0% -> 0%
where the time goes in v1:
time: 440 us; the launch traced here: 434 us
  waiting for transfers between devices  134 us (30%)
  local copies, waits for them, and re-layouts  93 us (21%)
  starting transfers between devices  86.1 us (20%)
  matrix products  69.6 us (16%)
  other arithmetic  42.1 us (10%)
  between operations  9.03 us (2%)
    ppermute x41, waiting for transfers between devices, in_plane(): return lax.ppermute(value, 'fsdp', plane_pairs(mask))  73.5 us
    ppermute x21, waiting for transfers between devices, along_line(): return lax.ppermute(value, 'fsdp', line_pairs(apart))  57.8 us
    dynamic_update_slice x60, local copies, waits for them, and re-layouts, placed(): return lax.dynamic_update_slice(whole, piece, where)  35.4 us
    ppermute x41, starting transfers between devices, in_plane(): return lax.ppermute(value, 'fsdp', plane_pairs(mask))  31.4 us
    ppermute x29, starting transfers between devices, other_core(): return lax.ppermute(value, 'rep', [(0, 1), (1, 0)])  31 us
    ppermute x21, starting transfers between devices, along_line(): return lax.ppermute(value, 'fsdp', line_pairs(apart))  23.8 us
    dot_general x13, matrix products, product_plain(): return jnp.dot(left_side, right_side, preferred_element_type=jnp.float32)  22.6 us
    dot_general x20, matrix products, product_left(): lax.dot_general(left_side, right_side, (((0,), (0,)), ((), ())), preferre...  21.8 us
  transfers between devices with their start and end apart: 91, of which 24 were waited for; matrix products, arithmetic and copies ran while one was open for 45% of the time, Pallas kernels for 0%

profile of v1, /device:TPU:13, one launch (start us, length us, event | category | flops | bytes accessed | tf_op | source)
XLA Modules:
  0.0 434.2 jit_solution(7090411817356596119)
XLA Ops:
  21.3 3.1 collective-permute-done.43
  25.2 3.6 collective-permute-done.44
  28.8 2.7 collective-permute-start.1
  43.2 9.5 %collective-permute-start.61 = (bf16[128,768]{1,0:T(8,128)(2,1)S(1)}, bf16[128,768]{1,0:T(8,128)(2,1)S(1)}, u32[]{:S(2)}, u32[]{:S(2)}) collective-permute-start(bf16[128,768]{1,0:T(8,128)(2,1)S(1)} %copy-done.67), channel_id=1, source_target_pairs={{0,16},{16,0},{1,17},{17,1},{2,18},{18,2},{3,19},{19,3},{4,20},{20... | collective-permute-start | bytes 589832 | tf_op jit(solution)/shard_map/ppermute | solution.py:564
  55.2 3.9 collective-permute-start.46
  62.8 3.0 collective-permute-done.45
  66.0 25.8 %collective-permute-done.46 = bf16[4,24,2112]{2,1,0:T(8,128)(2,1)S(1)} collective-permute-done((bf16[4,24,2112]{2,1,0:T(8,128)(2,1)}, bf16[4,24,2112]{2,1,0:T(8,128)(2,1)S(1)}, u32[]{:S(2)}, u32[]{:S(2)}) %collective-permute-start.46) | collective-permute-done | bytes 405536 | tf_op jit(solution)/shard_map/ppermute | solution.py:556
  92.2 2.6 collective-permute-done.47
  99.8 12.7 %collective-permute-done.28 = bf16[4,24,3840]{2,1,0:T(8,128)(2,1)S(1)} collective-permute-done((bf16[4,24,3840]{2,1,0:T(8,128)(2,1)S(1)}, bf16[4,24,3840]{2,1,0:T(8,128)(2,1)S(1)}, u32[]{:S(2)}, u32[]{:S(2)}) %collective-permute-start.28) | collective-permute-done | bytes 737312 | tf_op jit(solution)/shard_map/ppermute | solution.py:560
  113.2 15.2 %collective-permute-done.16 = bf16[4,24,3840]{2,1,0:T(8,128)(2,1)} collective-permute-done((bf16[4,24,3840]{2,1,0:T(8,128)(2,1)S(1)}, bf16[4,24,3840]{2,1,0:T(8,128)(2,1)}, u32[]{:S(2)}, u32[]{:S(2)}) %collective-permute-start.16) | collective-permute-done | bytes 737312 | tf_op jit(solution)/shard_map/ppermute | solution.py:560
  156.2 4.6 %collective-permute-done.20 = bf16[2,24,3840]{2,1,0:T(8,128)(2,1)S(1)} collective-permute-done((bf16[2,24,3840]{2,1,0:T(8,128)(2,1)}, bf16[2,24,3840]{2,1,0:T(8,128)(2,1)S(1)}, u32[]{:S(2)}, u32[]{:S(2)}) %collective-permute-start.20) | collective-permute-done | bytes 368672 | tf_op jit(solution)/shard_map/ppermute | solution.py:560
  164.9 5.0 %collective-permute-done.22 = bf16[2,24,3840]{2,1,0:T(8,128)(2,1)S(1)} collective-permute-done((bf16[2,24,3840]{2,1,0:T(8,128)(2,1)S(1)}, bf16[2,24,3840]{2,1,0:T(8,128)(2,1)S(1)}, u32[]{:S(2)}, u32[]{:S(2)}) %collective-permute-start.22) | collective-permute-done | bytes 368672 | tf_op jit(solution)/shard_map/ppermute | solution.py:560
  187.6 4.2 fusion.291
  197.3 2.6 reshape.720
  205.7 2.4 slice.587
  213.1 2.9 constant_dynamic-update-slice_fusion.11
  232.7 2.4 fusion.33
  242.6 4.2 collective-permute-start.90
  274.7 5.4 %fusion.295 = (bf16[3072]{0:T(1024)(128)(2,1)}, bf16[128,3072]{1,0:T(8,128)(2,1)}) fusion(f32[128,3072]{1,0:T(8,128)S(1)} %copy-done.137, bf16[128,768]{1,0:T(8,128)(2,1)} %get-tuple-element.45, bf16[768,3840]{1,0:T(8,128)(2,1)} %bitcast.411), kind=kOutput, calls=%fused_computation.586 | convolution fusion | flops 608302080 | bytes 7280640 | tf_op jit(solution)/shard_map/dot_general | solution.py:26
  280.1 2.6 reshape.718
  282.7 5.0 %multiply_reduce_fusion.2 = (bf16[768]{0:T(1024)(128)(2,1)}, f32[128]{0:T(128)S(1)}, f32[128]{0:T(128)S(1)}, bf16[768]{0:T(1024)(128)(2,1)}, f32[128,768]{1,0:T(8,128)S(1)}) fusion(f32[128,768]{1,0:T(8,128)S(1)} %copy-done.14, f32[128]{0:T(128)S(1)} %copy-done.124, f32[128]{0:T(128)S(1)} %copy-done.116, f32[768]{0:T(1024)S(1)} %copy-done.80, ...), kind=kOutput, calls=%fused_computation.216 | convolution fusion | flops 604961024 | bytes 6692864 | tf_op jit(solution)/shard_map/dot_general | solution.py:36
  302.8 4.0 fusion.60
  320.0 2.4 fusion.143
  340.2 2.4 fusion.145
  363.3 4.7 %collective-permute-done.66 = bf16[4,48,1664]{2,1,0:T(8,128)(2,1)} collective-permute-done((bf16[4,48,1664]{2,1,0:T(8,128)(2,1)}, bf16[4,48,1664]{2,1,0:T(8,128)(2,1)}, u32[]{:S(2)}, u32[]{:S(2)}) %collective-permute-start.66) | collective-permute-done | bytes 639008 | tf_op jit(solution)/shard_map/ppermute | solution.py:560
  368.0 2.9 collective-permute-done.68
  373.7 3.0 collective-permute-start.70
  376.7 16.7 %collective-permute-done.77 = bf16[4,48,3072]{2,1,0:T(8,128)(2,1)} collective-permute-done((bf16[4,48,3072]{2,1,0:T(8,128)(2,1)S(1)}, bf16[4,48,3072]{2,1,0:T(8,128)(2,1)}, u32[]{:S(2)}, u32[]{:S(2)}) %collective-permute-start.77) | collective-permute-done | bytes 1179680 | tf_op jit(solution)/shard_map/ppermute | solution.py:560
  393.3 2.9 collective-permute-done.79
  399.5 3.0 collective-permute-start.81
  404.9 17.1 %collective-permute-done.81 = bf16[48,3072]{1,0:T(8,128)(2,1)S(1)} collective-permute-done((bf16[48,3072]{1,0:T(8,128)(2,1)S(1)}, bf16[48,3072]{1,0:T(8,128)(2,1)S(1)}, u32[]{:S(2)}, u32[]{:S(2)}) %collective-permute-start.81) | collective-permute-done | bytes 294944 | tf_op jit(solution)/shard_map/ppermute | solution.py:556
  422.0 5.3 %collective-permute-done.82 = bf16[48,3072]{1,0:T(8,128)(2,1)S(1)} collective-permute-done((bf16[48,3072]{1,0:T(8,128)(2,1)S(1)}, bf16[48,3072]{1,0:T(8,128)(2,1)S(1)}, u32[]{:S(2)}, u32[]{:S(2)}) %collective-permute-start.82) | collective-permute-done | bytes 294944 | tf_op jit(solution)/shard_map/ppermute | solution.py:556
  (794 shorter events, 237.8 us)
Async XLA Ops:
  2.9 39.2 %collective-permute-start.24 = (bf16[24,3840]{1,0:T(8,128)(2,1)S(1)}, bf16[24,3840]{1,0:T(8,128)(2,1)}, u32[]{:S(2)}, u32[]{:S(2)}) collective-permute-start(bf16[24,3840]{1,0:T(8,128)(2,1)S(1)} %pad_maximum_fusion.18), channel_id=1, source_target_pairs={{0,4},{1,5},{2,6},{3,7},{4,8},{5,9},{6,10},{7,11},{8,12},{9,13},{1... | collective-permute-start | bytes 552968 | tf_op jit(solution)/shard_map/ppermute | solution.py:556
  4.3 38.9 %collective-permute-start.25 = (bf16[24,3840]{1,0:T(8,128)(2,1)S(1)}, bf16[24,3840]{1,0:T(8,128)(2,1)}, u32[]{:S(2)}, u32[]{:S(2)}) collective-permute-start(bf16[24,3840]{1,0:T(8,128)(2,1)S(1)} %pad_maximum_fusion.18), channel_id=1, source_target_pairs={{0,8},{1,9},{2,10},{3,11},{4,12},{5,13},{6,14},{7,15},{8,0},{9,1},... | collective-permute-start | bytes 552968 | tf_op jit(solution)/shard_map/ppermute | solution.py:556
  5.4 48.3 %collective-permute-start.26 = (bf16[24,3840]{1,0:T(8,128)(2,1)S(1)}, bf16[24,3840]{1,0:T(8,128)(2,1)}, u32[]{:S(2)}, u32[]{:S(2)}) collective-permute-start(bf16[24,3840]{1,0:T(8,128)(2,1)S(1)} %pad_maximum_fusion.18), channel_id=1, source_target_pairs={{0,12},{1,13},{2,14},{3,15},{4,0},{5,1},{6,2},{7,3},{8,4},{9,5},{1... | collective-permute-start | bytes 552968 | tf_op jit(solution)/shard_map/ppermute | solution.py:556
  8.8 24.5 %collective-permute-start = (bf16[24,2432]{1,0:T(8,128)(2,1)}, bf16[24,2432]{1,0:T(8,128)(2,1)}, u32[]{:S(2)}, u32[]{:S(2)}) collective-permute-start(bf16[24,2432]{1,0:T(8,128)(2,1)} %maximum_maximum_fusion), channel_id=1, source_target_pairs={{0,4},{1,5},{2,6},{3,7},{4,8},{5,9},{6,10},{7,11},{8,12},{9,13},{1... | collective-permute-start | bytes 350216 | tf_op jit(solution)/shard_map/ppermute | solution.py:556
  55.2 36.5 %collective-permute-start.46 = (bf16[4,24,2112]{2,1,0:T(8,128)(2,1)}, bf16[4,24,2112]{2,1,0:T(8,128)(2,1)S(1)}, u32[]{:S(2)}, u32[]{:S(2)}) collective-permute-start(bf16[4,24,2112]{2,1,0:T(8,128)(2,1)} %bitcast_dynamic-update-slice_fusion.46), channel_id=1, source_target_pairs={{0,8},{1,9},{2,10},{3,11},{4,12},{5,13},{6,14},{7,15},{8,0},{9,1},... | collective-permute-start | bytes 1216520 | tf_op jit(solution)/shard_map/ppermute | solution.py:556
  59.2 35.7 %collective-permute-start.47 = (bf16[4,24,2112]{2,1,0:T(8,128)(2,1)}, bf16[4,24,2112]{2,1,0:T(8,128)(2,1)S(1)}, u32[]{:S(2)}, u32[]{:S(2)}) collective-permute-start(bf16[4,24,2112]{2,1,0:T(8,128)(2,1)} %bitcast_dynamic-update-slice_fusion.46), channel_id=1, source_target_pairs={{0,12},{1,13},{2,14},{3,15},{4,0},{5,1},{6,2},{7,3},{8,4},{9,5},{1... | collective-permute-start | bytes 1216520 | tf_op jit(solution)/shard_map/ppermute | solution.py:556
  59.7 35.9 %collective-permute-start.3 = (bf16[4,24,2432]{2,1,0:T(8,128)(2,1)}, bf16[4,24,2432]{2,1,0:T(8,128)(2,1)S(1)}, u32[]{:S(2)}, u32[]{:S(2)}) collective-permute-start(bf16[4,24,2432]{2,1,0:T(8,128)(2,1)} %bitcast_dynamic-update-slice_fusion.42), channel_id=1, source_target_pairs={{0,16},{16,0},{1,17},{17,1},{2,18},{18,2},{3,19},{19,3},{4,20},{20... | collective-permute-start | bytes 1400840 | tf_op jit(solution)/shard_map/ppermute | solution.py:564
  60.9 35.1 %collective-permute-start.4 = (bf16[4,24,2432]{2,1,0:T(8,128)(2,1)}, bf16[4,24,2432]{2,1,0:T(8,128)(2,1)S(1)}, u32[]{:S(2)}, u32[]{:S(2)}) collective-permute-start(bf16[4,24,2432]{2,1,0:T(8,128)(2,1)} %bitcast_dynamic-update-slice_fusion.42), channel_id=1, source_target_pairs={{0,1},{1,0},{2,3},{3,2},{4,5},{5,4},{6,7},{7,6},{8,9},{9,8},{10,11... | collective-permute-start | bytes 1400840 | tf_op jit(solution)/shard_map/ppermute | solution.py:560
  65.7 31.4 %collective-permute-start.6 = (bf16[4,24,2432]{2,1,0:T(8,128)(2,1)}, bf16[4,24,2432]{2,1,0:T(8,128)(2,1)S(1)}, u32[]{:S(2)}, u32[]{:S(2)}) collective-permute-start(bf16[4,24,2432]{2,1,0:T(8,128)(2,1)} %bitcast_dynamic-update-slice_fusion.42), channel_id=1, source_target_pairs={{0,2},{1,3},{2,0},{3,1},{4,6},{5,7},{6,4},{7,5},{8,10},{9,11},{10,... | collective-permute-start | bytes 1400840 | tf_op jit(solution)/shard_map/ppermute | solution.py:560
  95.7 39.0 %collective-permute-start.30 = (bf16[4,24,3840]{2,1,0:T(8,128)(2,1)S(1)}, bf16[4,24,3840]{2,1,0:T(8,128)(2,1)S(1)}, u32[]{:S(2)}, u32[]{:S(2)}) collective-permute-start(bf16[4,24,3840]{2,1,0:T(8,128)(2,1)S(1)} %bitcast_dynamic-update-slice_fusion.34), channel_id=1, source_target_pairs={{0,2},{1,3},{2,0},{3,1},{4,6},{5,7},{6,4},{7,5},{8,10},{9,11},{10,... | collective-permute-start | bytes 2211848 | tf_op jit(solution)/shard_map/ppermute | solution.py:560
  97.1 31.3 %collective-permute-start.16 = (bf16[4,24,3840]{2,1,0:T(8,128)(2,1)S(1)}, bf16[4,24,3840]{2,1,0:T(8,128)(2,1)}, u32[]{:S(2)}, u32[]{:S(2)}) collective-permute-start(bf16[4,24,3840]{2,1,0:T(8,128)(2,1)S(1)} %bitcast_dynamic-update-slice_fusion.38), channel_id=1, source_target_pairs={{0,1},{1,0},{2,3},{3,2},{4,5},{5,4},{6,7},{7,6},{8,9},{9,8},{10,11... | collective-permute-start | bytes 2211848 | tf_op jit(solution)/shard_map/ppermute | solution.py:560
  98.5 37.5 %collective-permute-start.18 = (bf16[4,24,3840]{2,1,0:T(8,128)(2,1)S(1)}, bf16[4,24,3840]{2,1,0:T(8,128)(2,1)S(1)}, u32[]{:S(2)}, u32[]{:S(2)}) collective-permute-start(bf16[4,24,3840]{2,1,0:T(8,128)(2,1)S(1)} %bitcast_dynamic-update-slice_fusion.38), channel_id=1, source_target_pairs={{0,2},{1,3},{2,0},{3,1},{4,6},{5,7},{6,4},{7,5},{8,10},{9,11},{10,... | collective-permute-start | bytes 2211848 | tf_op jit(solution)/shard_map/ppermute | solution.py:560
  112.5 23.0 %collective-permute-start.8 = (bf16[2,24,2432]{2,1,0:T(8,128)(2,1)S(1)}, bf16[2,24,2432]{2,1,0:T(8,128)(2,1)S(1)}, u32[]{:S(2)}, u32[]{:S(2)}) collective-permute-start(bf16[2,24,2432]{2,1,0:T(8,128)(2,1)S(1)} %slice.544), channel_id=1, source_target_pairs={{0,2},{1,3},{2,0},{3,1},{4,6},{5,7},{6,4},{7,5},{8,10},{9,11},{10,... | collective-permute-start | bytes 700424 | tf_op jit(solution)/shard_map/ppermute | solution.py:560
  112.8 23.1 %collective-permute-start.10 = (bf16[2,24,2432]{2,1,0:T(8,128)(2,1)S(1)}, bf16[2,24,2432]{2,1,0:T(8,128)(2,1)S(1)}, u32[]{:S(2)}, u32[]{:S(2)}) collective-permute-start(bf16[2,24,2432]{2,1,0:T(8,128)(2,1)S(1)} %slice.545), channel_id=1, source_target_pairs={{0,1},{1,0},{2,3},{3,2},{4,5},{5,4},{6,7},{7,6},{8,9},{9,8},{10,11... | collective-permute-start | bytes 700424 | tf_op jit(solution)/shard_map/ppermute | solution.py:560
  134.6 78.5 %collective-permute-start.48 = (bf16[4,4,1,24,2112]{4,3,2,1,0:T(8,128)(2,1)S(1)}, bf16[4,4,1,24,2112]{4,3,2,1,0:T(8,128)(2,1)}, u32[]{:S(2)}, u32[]{:S(2)}) collective-permute-start(bf16[4,4,1,24,2112]{4,3,2,1,0:T(8,128)(2,1)S(1)} %bitcast_dynamic-update-slice_fusion.21), channel_id=1, source_target_pairs={{0,16},{16,0},{1,17},{17,1},{2,18},{18,2},{3,19},{19,3},{4,20},{20... | collective-permute-start | bytes 4866056 | tf_op jit(solution)/shard_map/ppermute | solution.py:564
  137.2 36.2 %collective-permute-start.32 = (bf16[2,24,3840]{2,1,0:T(8,128)(2,1)}, bf16[2,24,3840]{2,1,0:T(8,128)(2,1)}, u32[]{:S(2)}, u32[]{:S(2)}) collective-permute-start(bf16[2,24,3840]{2,1,0:T(8,128)(2,1)} %slice.566), channel_id=1, source_target_pairs={{0,2},{1,3},{2,0},{3,1},{4,6},{5,7},{6,4},{7,5},{8,10},{9,11},{10,... | collective-permute-start | bytes 1105928 | tf_op jit(solution)/shard_map/ppermute | solution.py:560
  138.8 35.0 %collective-permute-start.34 = (bf16[2,24,3840]{2,1,0:T(8,128)(2,1)}, bf16[2,24,3840]{2,1,0:T(8,128)(2,1)}, u32[]{:S(2)}, u32[]{:S(2)}) collective-permute-start(bf16[2,24,3840]{2,1,0:T(8,128)(2,1)} %slice.567), channel_id=1, source_target_pairs={{0,1},{1,0},{2,3},{3,2},{4,5},{5,4},{6,7},{7,6},{8,9},{9,8},{10,11... | collective-permute-start | bytes 1105928 | tf_op jit(solution)/shard_map/ppermute | solution.py:560
  196.2 36.4 %collective-permute-start.72 = (bf16[128,768]{1,0:T(8,128)(2,1)}, bf16[128,768]{1,0:T(8,128)(2,1)}, u32[]{:S(2)}, u32[]{:S(2)}) collective-permute-start(bf16[128,768]{1,0:T(8,128)(2,1)} %copy-done.69), channel_id=1, source_target_pairs={{0,16},{16,0},{1,17},{17,1},{2,18},{18,2},{3,19},{19,3},{4,20},{20... | collective-permute-start | bytes 589832 | tf_op jit(solution)/shard_map/ppermute | solution.py:564
  210.0 109.9 %collective-permute-start.75 = (bf16[128,1536]{1,0:T(8,128)(2,1)}, bf16[128,1536]{1,0:T(8,128)(2,1)}, u32[]{:S(2)}, u32[]{:S(2)}) collective-permute-start(bf16[128,1536]{1,0:T(8,128)(2,1)} %bitcast.475), channel_id=1, source_target_pairs={{0,16},{16,0},{1,17},{17,1},{2,18},{18,2},{3,19},{19,3},{4,20},{20... | collective-permute-start | bytes 1179656 | tf_op jit(solution)/shard_map/ppermute | solution.py:564
  265.5 42.2 %collective-permute-start.84 = (bf16[16,2304]{1,0:T(8,128)(2,1)}, bf16[16,2304]{1,0:T(8,128)(2,1)}, u32[]{:S(2)}, u32[]{:S(2)}) collective-permute-start(bf16[16,2304]{1,0:T(8,128)(2,1)} %concatenate.159), channel_id=1, source_target_pairs={{0,1},{1,0},{2,3},{3,2},{4,5},{5,4},{6,7},{7,6},{8,9},{9,8},{10,11... | collective-permute-start | bytes 221192 | tf_op jit(solution)/shard_map/ppermute | solution.py:560
  268.2 40.6 %collective-permute-start.85 = (bf16[16,2304]{1,0:T(8,128)(2,1)}, bf16[16,2304]{1,0:T(8,128)(2,1)}, u32[]{:S(2)}, u32[]{:S(2)}) collective-permute-start(bf16[16,2304]{1,0:T(8,128)(2,1)} %concatenate.159), channel_id=1, source_target_pairs={{0,2},{1,3},{2,0},{3,1},{4,6},{5,7},{6,4},{7,5},{8,10},{9,11},{10,... | collective-permute-start | bytes 221192 | tf_op jit(solution)/shard_map/ppermute | solution.py:560
  268.3 42.0 %collective-permute-start.86 = (bf16[16,2304]{1,0:T(8,128)(2,1)}, bf16[16,2304]{1,0:T(8,128)(2,1)}, u32[]{:S(2)}, u32[]{:S(2)}) collective-permute-start(bf16[16,2304]{1,0:T(8,128)(2,1)} %concatenate.159), channel_id=1, source_target_pairs={{0,3},{1,2},{2,1},{3,0},{4,7},{5,6},{6,5},{7,4},{8,11},{9,10},{10,... | collective-permute-start | bytes 221192 | tf_op jit(solution)/shard_map/ppermute | solution.py:560
  272.5 45.7 %collective-permute-start.74 = (bf16[128,768]{1,0:T(8,128)(2,1)}, bf16[128,768]{1,0:T(8,128)(2,1)}, u32[]{:S(2)}, u32[]{:S(2)}) collective-permute-start(bf16[128,768]{1,0:T(8,128)(2,1)} %get-tuple-element.45), channel_id=1, source_target_pairs={{0,16},{16,0},{1,17},{17,1},{2,18},{18,2},{3,19},{19,3},{4,20},{20... | collective-permute-start | bytes 589832 | tf_op jit(solution)/shard_map/ppermute | solution.py:564
  308.8 24.7 %collective-permute-start.73 = (bf16[128,1536]{1,0:T(8,128)(2,1)}, bf16[128,1536]{1,0:T(8,128)(2,1)}, u32[]{:S(2)}, u32[]{:S(2)}) collective-permute-start(bf16[128,1536]{1,0:T(8,128)(2,1)} %bitcast.385), channel_id=1, source_target_pairs={{0,16},{16,0},{1,17},{17,1},{2,18},{18,2},{3,19},{19,3},{4,20},{20... | collective-permute-start | bytes 1179656 | tf_op jit(solution)/shard_map/ppermute | solution.py:564
  316.4 28.5 %collective-permute-start.87 = (bf16[16,12288]{1,0:T(8,128)(2,1)S(1)}, bf16[16,12288]{1,0:T(8,128)(2,1)S(1)}, u32[]{:S(2)}, u32[]{:S(2)}) collective-permute-start(bf16[16,12288]{1,0:T(8,128)(2,1)S(1)} %constant_dynamic-update-slice_fusion), channel_id=1, source_target_pairs={{0,16},{16,0},{1,17},{17,1},{2,18},{18,2},{3,19},{19,3},{4,20},{20... | collective-permute-start | bytes 1179656 | tf_op jit(solution)/shard_map/ppermute | solution.py:564
  330.6 24.1 %collective-permute-start.67 = (bf16[2,48,1664]{2,1,0:T(8,128)(2,1)}, bf16[2,48,1664]{2,1,0:T(8,128)(2,1)}, u32[]{:S(2)}, u32[]{:S(2)}) collective-permute-start(bf16[2,48,1664]{2,1,0:T(8,128)(2,1)} %get-tuple-element.81), channel_id=1, source_target_pairs={{0,1},{1,0},{2,3},{3,2},{4,5},{5,4},{6,7},{7,6},{8,9},{9,8},{10,11... | collective-permute-start | bytes 958472 | tf_op jit(solution)/shard_map/ppermute | solution.py:560
  358.2 35.1 %collective-permute-start.77 = (bf16[4,48,3072]{2,1,0:T(8,128)(2,1)S(1)}, bf16[4,48,3072]{2,1,0:T(8,128)(2,1)}, u32[]{:S(2)}, u32[]{:S(2)}) collective-permute-start(bf16[4,48,3072]{2,1,0:T(8,128)(2,1)S(1)} %pad_maximum_fusion.5), channel_id=1, source_target_pairs={{0,1},{1,0},{2,3},{3,2},{4,5},{5,4},{6,7},{7,6},{8,9},{9,8},{10,11... | collective-permute-start | bytes 3538952 | tf_op jit(solution)/shard_map/ppermute | solution.py:560
  361.8 34.5 %collective-permute-start.79 = (bf16[4,48,3072]{2,1,0:T(8,128)(2,1)}, bf16[4,48,3072]{2,1,0:T(8,128)(2,1)}, u32[]{:S(2)}, u32[]{:S(2)}) collective-permute-start(bf16[4,48,3072]{2,1,0:T(8,128)(2,1)} %pad_maximum_fusion.6), channel_id=1, source_target_pairs={{0,2},{1,3},{2,0},{3,1},{4,6},{5,7},{6,4},{7,5},{8,10},{9,11},{10,... | collective-permute-start | bytes 3538952 | tf_op jit(solution)/shard_map/ppermute | solution.py:560
  372.6 29.8 %collective-permute-start.69 = (bf16[48,1664]{1,0:T(8,128)(2,1)S(1)}, bf16[48,1664]{1,0:T(8,128)(2,1)S(1)}, u32[]{:S(2)}, u32[]{:S(2)}) collective-permute-start(bf16[48,1664]{1,0:T(8,128)(2,1)S(1)} %get-tuple-element.77), channel_id=1, source_target_pairs={{0,4},{1,5},{2,6},{3,7},{4,8},{5,9},{6,10},{7,11},{8,12},{9,13},{1... | collective-permute-start | bytes 479240 | tf_op jit(solution)/shard_map/ppermute | solution.py:556
  373.7 28.8 %collective-permute-start.70 = (bf16[48,1664]{1,0:T(8,128)(2,1)S(1)}, bf16[48,1664]{1,0:T(8,128)(2,1)S(1)}, u32[]{:S(2)}, u32[]{:S(2)}) collective-permute-start(bf16[48,1664]{1,0:T(8,128)(2,1)S(1)} %get-tuple-element.79), channel_id=1, source_target_pairs={{0,8},{1,9},{2,10},{3,11},{4,12},{5,13},{6,14},{7,15},{8,0},{9,1},... | collective-permute-start | bytes 479240 | tf_op jit(solution)/shard_map/ppermute | solution.py:556
  376.7 25.8 %collective-permute-start.71 = (bf16[48,1664]{1,0:T(8,128)(2,1)S(1)}, bf16[48,1664]{1,0:T(8,128)(2,1)S(1)}, u32[]{:S(2)}, u32[]{:S(2)}) collective-permute-start(bf16[48,1664]{1,0:T(8,128)(2,1)S(1)} %get-tuple-element.78), channel_id=1, source_target_pairs={{0,12},{1,13},{2,14},{3,15},{4,0},{5,1},{6,2},{7,3},{8,4},{9,5},{1... | collective-permute-start | bytes 479240 | tf_op jit(solution)/shard_map/ppermute | solution.py:556
  402.5 24.8 %collective-permute-start.82 = (bf16[48,3072]{1,0:T(8,128)(2,1)S(1)}, bf16[48,3072]{1,0:T(8,128)(2,1)S(1)}, u32[]{:S(2)}, u32[]{:S(2)}) collective-permute-start(bf16[48,3072]{1,0:T(8,128)(2,1)S(1)} %get-tuple-element.63), channel_id=1, source_target_pairs={{0,12},{1,13},{2,14},{3,15},{4,0},{5,1},{6,2},{7,3},{8,4},{9,5},{1... | collective-permute-start | bytes 884744 | tf_op jit(solution)/shard_map/ppermute | solution.py:556
  (198 other events, 1532.8 us)

commit v2 on v0

--- a/solution.py
+++ b/solution.py
@@ -1,6 +1,10 @@
+import math
+
 import jax
 import jax.numpy as jnp
 from jax import lax
+from jax.experimental import pallas as pl
+from jax.experimental.pallas import tpu as pltpu
 from jax.sharding import PartitionSpec as P
 
 HEADS = 12
@@ -212,21 +216,17 @@
         grad_out, normed_second, inv_second, gain_second
     )
     second_low = grad_second.astype(jnp.bfloat16)
-    grad_down = product_left(second_low, activated)
     grad_pre = (product_plain(second_low, down_weight) * gelu_slope(pre_act)).astype(jnp.bfloat16)
-    grad_up = product_left(first_low, grad_pre)
     grad_first = grad_second + product_right(grad_pre, up_weight)
     grad_summed, grad_gain_first, grad_shift_first = norm_backward(
         grad_first, normed_first, inv_first, gain_first
     )
     branch_low = grad_summed.astype(jnp.bfloat16)
-    grad_out_weight = product_left(mixed_rows, branch_low)
     grad_mixed = product_right(branch_low, out_weight).astype(jnp.bfloat16)
     grad_query, grad_key, grad_value = attend_back(
         queries, keys_in, values, attend_kept, grad_mixed
     )
     grad_proj = jnp.concatenate([grad_query, grad_key, grad_value], axis=1)
-    grad_qkv = product_left(inputs, grad_proj)
     grad_rows = grad_summed + product_right(grad_proj, qkv_weight)
     vector_grad = jnp.concatenate(
         [
@@ -241,7 +241,29 @@
             row_total(grad_pre),
         ]
     )
-    return (grad_rows, grad_qkv, grad_out_weight, grad_up, grad_down, vector_grad)
+    weight_rows = (
+        inputs,
+        grad_proj,
+        mixed_rows,
+        branch_low,
+        first_low,
+        grad_pre,
+        second_low,
+        activated,
+    )
+    return (grad_rows, weight_rows, vector_grad)
+
+
+def weight_products(weight_rows):
+    inputs, grad_proj, mixed_rows, branch_low, first_low, grad_pre, second_low, activated = (
+        weight_rows
+    )
+    return (
+        product_left(inputs, grad_proj),
+        product_left(mixed_rows, branch_low),
+        product_left(first_low, grad_pre),
+        product_left(second_low, activated),
+    )
 
 
 def local(
@@ -401,9 +423,10 @@
         model_width,
         ff_width,
     )
-    heads_grad, cls_g_qkv, cls_g_out, cls_g_up, cls_g_down, cls_g_vec = block_backward(
+    heads_grad, cls_weight_rows, cls_g_vec = block_backward(
         grad_grid[:, 0, :], cls_back, cls_saved, cls_attend_back
     )
+    cls_g_qkv, cls_g_out, cls_g_up, cls_g_down = weight_products(cls_weight_rows)
     pos_local = jnp.sum(position_hot[:, :, None] * heads_grad[:, None, :], axis=0)
     seg_grad_out = jnp.concatenate([heads_grad[:, None, :], grad_grid[:, 1:, :]], axis=1).reshape(
         tok_rows, model_width
@@ -416,9 +439,10 @@
         model_width,
         ff_width,
     )
-    input_grad, seg_g_qkv, seg_g_out, seg_g_up, seg_g_down, seg_g_vec = block_backward(
+    input_grad, seg_weight_rows, seg_g_vec = block_backward(
         seg_grad_out, seg_back, seg_saved, seg_attend_back
     )
+    seg_g_qkv, seg_g_out, seg_g_up, seg_g_down = weight_products(seg_weight_rows)
     owner_rows = tuple(
         (
             lax.psum_scatter(seg_g_qkv, "fsdp", scatter_dimension=0, tiled=True),
@@ -518,6 +542,1161 @@
     )
 
 
+LINE = 4
+PLANE = 4
+CORES = 2
+LANES = 128
+GROUP = LINE * PLANE
+LOW, WIDE = jnp.bfloat16, jnp.float32
+MODEL = HEADS * HEAD_DIM
+SPAN = 2 * LANES
+TILE_START = (0, 1, 3, 4)
+
+
+def line_pairs(apart):
+    return [(source, (source + apart * PLANE) % GROUP) for source in range(GROUP)]
+
+
+def plane_pairs(mask):
+    return [(source, source ^ mask) for source in range(GROUP)]
+
+
+def along_line(value, apart):
+    return lax.ppermute(value, "fsdp", line_pairs(apart))
+
+
+def in_plane(value, mask):
+    return lax.ppermute(value, "fsdp", plane_pairs(mask))
+
+
+def other_core(value):
+    return lax.ppermute(value, "rep", [(0, 1), (1, 0)])
+
+
+def shape_of(dims, dtype=WIDE):
+    return jax.ShapeDtypeStruct(dims, dtype)
+
+
+def run_kernel(body, name, outs, where, blocks, arrays, scratch=(), outs_far=False, flops=0):
+    in_specs = [pl.BlockSpec(memory_space=pltpu.SMEM)]
+    in_specs += [pl.BlockSpec(memory_space=pl.ANY)] * len(blocks)
+    in_specs += [pl.BlockSpec(memory_space=pltpu.VMEM)] * len(arrays)
+    out_space = pl.ANY if outs_far else pltpu.VMEM
+    moved = sum(x.size * x.dtype.itemsize for x in list(blocks) + list(arrays))
+    moved += sum(math.prod(o.shape) * jnp.dtype(o.dtype).itemsize for o in outs)
+    return pl.pallas_call(
+        body,
+        name=name,
+        out_shape=tuple(outs),
+        in_specs=in_specs,
+        out_specs=tuple(pl.BlockSpec(memory_space=out_space) for _ in outs),
+        scratch_shapes=list(scratch),
+        cost_estimate=pl.CostEstimate(flops=flops, bytes_accessed=moved, transcendentals=0),
+        compiler_params=pltpu.CompilerParams(vmem_limit_bytes=VMEM_BYTES),
+    )(where, *blocks, *arrays)
+
+
+VMEM_BYTES = 48 * 1024 * 1024
+BLOCK_PLAN = (
+    (0, 0, LINE),
+    (1, 0, LINE),
+    (2, 0, LINE),
+    (3, 0, LINE // 2),
+    (3, LINE // 2, LINE // 2),
+)
+WEIGHT_COPIES = LINE * PLANE * CORES
+
+
+def start_weight(where, blocks, scratch, sems):
+    line_at, plane_at, core_at = where[0], where[1], where[2]
+    copies = []
+    for block_at, block in enumerate(blocks):
+        mask, first, count = BLOCK_PLAN[block_at % len(BLOCK_PLAN)]
+        core = core_at if block_at < len(BLOCK_PLAN) else 1 - core_at
+        for step in range(count):
+            target = scratch.at[(line_at + LINE - first - step) % LINE, plane_at ^ mask, core]
+            copies.append(pltpu.make_async_copy(block.at[step], target, sems.at[len(copies)]))
+    for copy in copies:
+        copy.start()
+    return copies
+
+
+def wait_all(copies):
+    for copy in copies:
+        copy.wait()
+
+
+def rows_view(scratch, first, last):
+    value = scratch[:, :, :, :, first:last]
+    return value.reshape(LINE * PLANE * CORES * value.shape[3], last - first)
+
+
+def weight_scratch(rows, columns):
+    return [
+        pltpu.VMEM((LINE, PLANE, CORES, rows, columns), LOW),
+        pltpu.SemaphoreType.DMA((WEIGHT_COPIES,)),
+    ]
+
+
+def prepare_kernel(where, seg, cls, vecs, first_out, second_out, third_out, quarter_out, kept):
+    core_at, plane_at = where[2], where[1]
+    half = seg.shape[1]
+    qkv = 3 * MODEL
+    own = seg[core_at]
+    own_cls = cls[core_at]
+    first_out[:, :qkv] = own[:, :qkv]
+    first_out[:, qkv:] = vecs[...]
+    second_out[...] = own[:, qkv : 4 * MODEL + FF]
+    third_out[:, :FF] = own[:, 4 * MODEL + FF :]
+    third_out[:, FF:] = own_cls[:, qkv : 4 * MODEL]
+    part = FF // PLANE
+    for at in range(PLANE):
+        first = TILE_START[at] * LANES
+        for piece in range(3):
+            kept[at, :, piece * SPAN : (piece + 1) * SPAN] = own_cls[
+                :, piece * MODEL + first : piece * MODEL + first + SPAN
+            ]
+        for piece in range(2):
+            start = 4 * MODEL + piece * FF + at * part
+            kept[at, :, 3 * SPAN + piece * part : 3 * SPAN + (piece + 1) * part] = own_cls[
+                :, start : start + part
+            ]
+    for mask in range(PLANE):
+        quarter_out[mask] = kept[plane_at ^ mask]
+
+
+def lane_mask(rows, head):
+    lane = lax.broadcasted_iota(jnp.int32, (rows, LANES), 1)
+    return (lane < HEAD_DIM) if head == 0 else (lane >= HEAD_DIM)
+
+
+def masked(value, mask):
+    return jnp.where(mask, value, jnp.zeros_like(value))
+
+
+def head_probabilities(query, key, allowed):
+    scores = product_right(query, key) * HEAD_DIM ** (-0.5)
+    scores = jnp.where(allowed, scores, MASK_FILL)
+    raised = jnp.exp(scores - jnp.max(scores, axis=-1, keepdims=True))
+    return raised / jnp.sum(raised, axis=-1, keepdims=True)
+
+
+def attend_tiles(qkv, width, allowed):
+    rows = qkv.shape[0]
+    mixed = []
+    for tile in range(width // LANES):
+        at = tile * LANES
+        query, key, value = (
+            qkv[:, piece * width + at : piece * width + at + LANES] for piece in range(3)
+        )
+        total = jnp.zeros((rows, LANES), WIDE)
+        for head in range(2):
+            mask = lane_mask(rows, head)
+            weights = head_probabilities(masked(query, mask), key, allowed).astype(LOW)
+            total = total + product_plain(weights, masked(value, mask))
+        mixed.append(total.astype(LOW))
+    return mixed
+
+
+def attend_tiles_back(qkv, grad_mixed, width, allowed):
+    rows = qkv.shape[0]
+    scale = HEAD_DIM ** (-0.5)
+    results = ([], [], [])
+    for tile in range(width // LANES):
+        at = tile * LANES
+        query, key, value = (
+            qkv[:, piece * width + at : piece * width + at + LANES] for piece in range(3)
+        )
+        grad = grad_mixed[:, at : at + LANES]
+        totals = [jnp.zeros((rows, LANES), WIDE) for _ in range(3)]
+        for head in range(2):
+            mask = lane_mask(rows, head)
+            query_low, key_low, grad_low = (masked(x, mask) for x in (query, key, grad))
+            chance = head_probabilities(query_low, key, allowed)
+            grad_chance = product_right(grad_low, value)
+            inner = jnp.sum(grad_chance * chance, axis=-1, keepdims=True)
+            grad_scores = (chance * (grad_chance - inner)).astype(LOW)
+            totals[0] = totals[0] + product_plain(grad_scores, key_low)
+            totals[1] = totals[1] + product_left(grad_scores, query_low)
+            totals[2] = totals[2] + product_left(chance.astype(LOW), grad_low)
+        results[0].append((totals[0] * scale).astype(LOW))
+        results[1].append((totals[1] * scale).astype(LOW))
+        results[2].append(totals[2].astype(LOW))
+    return results[0] + results[1] + results[2]
+
+
+def token_allowed(live_row):
+    shape = (SEG, SEG)
+    same = lax.broadcasted_iota(jnp.int32, shape, 0) == lax.broadcasted_iota(jnp.int32, shape, 1)
+    return (live_row > 0.5) | same
+
+
+def qkv_kernel(where, *refs):
+    blocks = refs[:10]
+    hidden, live_row, qkv_out, both_out, vectors_out, count_out, weight, sems, flat = refs[10:]
+    copies = start_weight(where, blocks, weight, sems)
+    wait_all(copies)
+    qkv = 3 * MODEL
+    piece = (8 * MODEL + FF) // GROUP
+    lines = -(-piece // LANES)
+    count = jnp.zeros((1, LANES), WIDE)
+    for chip in range(GROUP):
+        at = (chip // PLANE, chip % PLANE)
+        rows = weight[at[0], at[1], 0, 0:16, qkv:].astype(WIDE)
+        for block in range(2):
+            joined = jnp.concatenate(
+                [rows[block * lines + r : block * lines + r + 1] for r in range(lines)], axis=1
+            )
+            flat[block : block + 1, chip * piece : (chip + 1) * piece] = joined[:, :piece]
+        for core in range(CORES):
+            rows_core = weight[at[0], at[1], core, 0:16, qkv:].astype(WIDE)
+            count = count + rows_core[2 * lines : 2 * lines + 1]
+    rows_each = (8 * MODEL + FF) // MODEL
+    for block in range(2):
+        for row in range(rows_each):
+            vectors_out[block * rows_each + row : block * rows_each + row + 1, :] = flat[
+                block : block + 1, row * MODEL : (row + 1) * MODEL
+            ]
+    count_out[...] = jnp.broadcast_to(count, count_out.shape)
+    inputs = hidden[...]
+    projected = product_plain(inputs, rows_view(weight, 0, qkv))
+    qkv_out[:, :MODEL] = (projected[:, :MODEL] + vectors_out[0:1, :]).astype(LOW)
+    qkv_out[:, MODEL : 2 * MODEL] = projected[:, MODEL : 2 * MODEL].astype(LOW)
+    qkv_out[:, 2 * MODEL :] = (projected[:, 2 * MODEL :] + vectors_out[1:2, :]).astype(LOW)
+    both_out[:, :MODEL] = inputs
+    for tile, value in enumerate(attend_tiles(qkv_out[...], MODEL, token_allowed(live_row[...]))):
+        both_out[:, MODEL + tile * LANES : MODEL + (tile + 1) * LANES] = value
+
+
+def norm_rows(summed):
+    row_mean = jnp.mean(summed, axis=-1, keepdims=True)
+    centered = summed - row_mean
+    inv_dev = lax.rsqrt(jnp.mean(centered * centered, axis=-1, keepdims=True) + NORM_EPS)
+    return centered * inv_dev, inv_dev
+
+
+def norm_rows_back(grad_out, normed, inv_dev, gain):
+    scaled = grad_out * gain
+    mean_one = jnp.mean(scaled, axis=-1, keepdims=True)
+    mean_two = jnp.mean(scaled * normed, axis=-1, keepdims=True)
+    return inv_dev * (scaled - mean_one - normed * mean_two)
+
+
+def column_sum(value):
+    return jnp.sum(value.astype(WIDE), axis=0, keepdims=True)
+
+
+def four_rows(vectors, first):
+    return jnp.concatenate([vectors[first + at : first + at + 1, :] for at in range(4)], axis=1)
+
+
+def gelu_both(before):
+    half = 0.5 * (1.0 + lax.erf(before * SQRT_HALF))
+    slope = half + before * jnp.exp(-0.5 * before * before) * INV_SQRT_TWO_PI
+    return before * half, slope
+
+
+def up_kernel(where, *refs):
+    blocks = refs[:10]
+    hidden, both, vectors, normed_out, inv_out, slope_out, act_out, send_out = refs[10:18]
+    weight, sems = refs[18:]
+    copies = start_weight(where, blocks, weight, sems)
+    wait_all(copies)
+    core_at = where[2]
+    branch = product_plain(both[:, MODEL:], rows_view(weight, 0, MODEL))
+    normed, inv_dev = norm_rows(hidden[...].astype(WIDE) + branch + vectors[2:3, :])
+    normed_out[...] = normed
+    inv_out[...] = inv_dev
+    first_low = (normed * vectors[4:5, :] + vectors[5:6, :]).astype(LOW)
+    send_out[:, :MODEL] = first_low
+    chunk = MODEL
+    for at in range(FF // chunk):
+        first = MODEL + at * chunk
+        before = product_plain(first_low, rows_view(weight, first, first + chunk))
+        value, slope = gelu_both(before + vectors[8 + at : 9 + at, :])
+        act_out[:, at * chunk : (at + 1) * chunk] = value.astype(LOW)
+        slope_out[:, at * chunk : (at + 1) * chunk] = slope
+    half = FF // CORES
+    sent = pl.multiple_of((1 - core_at) * half, LANES)
+    send_out[:, MODEL:] = act_out[:, pl.ds(sent, half)]
+
+
+def down_kernel(where, *refs):
+    blocks = refs[:10]
+    act, normed_first, vectors, targets, live, seg_pos = refs[10:16]
+    normed_out, inv_out, diff_out, rows_out, head_out, cls_out = refs[16:22]
+    weight, sems = refs[22:]
+    copies = start_weight(where, blocks, weight, sems)
+    wait_all(copies)
+    plane_at, doc, number = where[1], where[3], where[4]
+    first = normed_first[...] * vectors[4:5, :] + vectors[5:6, :]
+    down = product_right(act[...], rows_view(weight, 0, FF))
+    normed, inv_dev = norm_rows(first + down + vectors[3:4, :])
+    normed_out[...] = normed
+    inv_out[...] = inv_dev
+    rows = normed * vectors[6:7, :] + vectors[7:8, :]
+    live_rows = live[...]
+    target_rows = targets[...].astype(WIDE)
+    output = rows * live_rows
+    rows_out[...] = output
+    diff = (output - target_rows) * live_rows
+    row_at = lax.broadcasted_iota(jnp.int32, (SEG, 1), 0)
+    diff = jnp.where(row_at > 0, diff, 0.0)
+    diff_out[...] = diff
+    table = seg_pos[...].astype(WIDE)
+    chosen = lax.broadcasted_iota(jnp.int32, table.shape, 0) == number
+    position = jnp.sum(jnp.where(chosen, table, 0.0), axis=0, keepdims=True)
+    head_out[:, :MODEL] = rows[0:1, :] + position
+    head_out[:, MODEL : 2 * MODEL] = target_rows[0:1, :]
+    square = jnp.sum(column_sum(diff * diff), axis=1, keepdims=True)
+    lane = lax.broadcasted_iota(jnp.int32, (1, LANES), 1)
+    facts = jnp.where(lane == 0, live_rows[0:1, :], 0.0)
+    facts = jnp.where(lane == 1, doc.astype(WIDE), facts)
+    facts = jnp.where(lane == 2, number.astype(WIDE), facts)
+    facts = jnp.where(lane == 3, square, facts)
+    head_out[:, 2 * MODEL :] = facts
+    part = weight[plane_at, :, :, :, FF:].reshape(3, HEAD_DIM, MODEL)
+    cls_out[...] = jnp.zeros_like(cls_out)
+    cls_out[pl.ds(plane_at % 2, 3)] = part
+
+
+def mlp_back_kernel(where, *refs):
+    up_blocks, down_blocks = refs[:10], refs[10:20]
+    diff, count, normed, inv_dev, vectors, slope = refs[20:26]
+    grad_out, pre_out, send_out, sums_out = refs[26:30]
+    up_weight, up_sems, down_weight, down_sems = refs[30:]
+    down_copies = start_weight(where, down_blocks, down_weight, down_sems)
+    up_copies = start_weight(where, up_blocks, up_weight, up_sems)
+    core_at = where[2]
+    scale = (SEG * GROUP * CORES) / count[0:1, 0:1]
+    grad_top = diff[...] * scale
+    normed_rows = normed[...]
+    grad = norm_rows_back(grad_top, normed_rows, inv_dev[...], vectors[6:7, :])
+    second = grad.astype(LOW)
+    sums_out[1:2, 0:MODEL] = column_sum(second)
+    sums_out[1:2, MODEL : 2 * MODEL] = column_sum(grad_top * normed_rows)
+    sums_out[1:2, 2 * MODEL : 3 * MODEL] = column_sum(grad_top)
+    send_out[:, :MODEL] = second
+    wait_all(down_copies)
+    chunk = MODEL
+    for at in range(FF // chunk):
+        columns = slice(at * chunk, (at + 1) * chunk)
+        before = product_plain(second, rows_view(down_weight, at * chunk, (at + 1) * chunk))
+        pre = (before * slope[:, columns]).astype(LOW)
+        pre_out[:, columns] = pre
+        sums_out[0:1, columns] = column_sum(pre)
+    wait_all(up_copies)
+    grad_out[...] = grad + product_right(pre_out[...], rows_view(up_weight, MODEL, MODEL + FF))
+    half = FF // CORES
+    sent = pl.multiple_of((1 - core_at) * half, LANES)
+    send_out[:, MODEL:] = pre_out[:, pl.ds(sent, half)]
+
+
+def scatter_parts(where, parts, outs, sems):
+    line_at, plane_at = where[0], where[1]
+    far_low, far_high, to_x, to_y, kept = outs
+    half = LINE // 2
+    copies = []
+    for mask in range(PLANE):
+        for step in range(LINE):
+            source = parts.at[(line_at + step) % LINE * PLANE + (plane_at ^ mask)]
+            if mask == 3:
+                target = far_low.at[step] if step < half else far_high.at[step - half]
+            else:
+                target = (kept, to_x, to_y)[mask].at[step]
+            copies.append(pltpu.make_async_copy(source, target, sems.at[len(copies)]))
+    for copy in copies:
+        copy.start()
+    wait_all(copies)
+
+
+def mlp_weight_kernel(where, *refs):
+    first, first_got, second, second_got, pre, act = refs[:6]
+    outs = refs[6:11]
+    left, right, parts, sems = refs[11:]
+    core_at = where[2]
+    half = FF // CORES
+    kept = pl.multiple_of(core_at * half, LANES)
+    rows = GROUP * CORES * 24
+    for at, (own, got, tail, got_tail) in enumerate(
+        ((first, first_got, pre, second_got), (second, second_got, act, first_got))
+    ):
+        left[:SEG] = own[:, :MODEL]
+        left[SEG:] = got[:, :MODEL]
+        right[:SEG] = tail[:, pl.ds(kept, half)]
+        right[SEG:] = got_tail[:, MODEL:]
+        for piece in range(half // MODEL):
+            start = piece * MODEL
+            product = product_left(left[...], right[:, start : start + MODEL]).astype(LOW)
+            parts[:, :, at * half + start : at * half + start + MODEL] = product.reshape(
+                GROUP, rows // GROUP, MODEL
+            )
+    scatter_parts(where, parts, outs, sems)
+
+
+def attn_weight_kernel(where, *refs):
+    both, both_got, proj, got, branch = refs[:5]
+    outs = refs[5:10]
+    left, right, parts, sems = refs[10:]
+    core_at = where[2]
+    rows = MODEL
+    qkv_half, out_half = 3 * MODEL // CORES, MODEL // CORES
+    left[:SEG] = both[...]
+    left[SEG:] = both_got[...]
+    right[:SEG, :qkv_half] = proj[:, pl.ds(pl.multiple_of(core_at * qkv_half, LANES), qkv_half)]
+    right[:SEG, qkv_half:] = branch[:, pl.ds(pl.multiple_of(core_at * out_half, LANES), out_half)]
+    right[SEG:] = got[...]
+    for piece in range(4):
+        start = piece * out_half
+        side = left[:, :MODEL] if piece < 3 else left[:, MODEL:]
+        product = product_left(side, right[:, start : start + out_half]).astype(LOW)
+        parts[:, :, start : start + out_half] = product.reshape(GROUP, rows // GROUP, out_half)
+    scatter_parts(where, parts, outs, sems)
+
+
+def fold_kernel(where, kept, got_x, got_y, own_out, *sent):
+    for step in range(LINE):
+        total = (
+            kept[step].astype(WIDE) + got_x[step].astype(WIDE) + got_y[step].astype(WIDE)
+        )
+        if step == 0:
+            own_out[...] = total
+        else:
+            sent[step - 1][...] = total.astype(LOW)
+
+
+def reduce_parts(where, parts):
+    far_low, far_high, to_x, to_y, kept = parts
+    half = LINE // 2
+    from_y, from_x = in_plane(far_low, 2), in_plane(far_high, 1)
+    to_x = to_x.at[:half].add(from_y)
+    to_y = to_y.at[half:].add(from_x)
+    got_x, got_y = in_plane(to_x, 1), in_plane(to_y, 2)
+    _, rows, columns = kept.shape
+    folded = run_kernel(
+        fold_kernel,
+        "fold",
+        [shape_of((rows, columns))] + [shape_of((rows, columns), LOW)] * (LINE - 1),
+        where,
+        (),
+        (kept, got_x, got_y),
+    )
+    total = folded[0]
+    for apart in range(1, LINE):
+        total = total + along_line(folded[apart], apart).astype(WIDE)
+    return total
+
+
+def seg_back_kernel(where, *refs):
+    qkv_blocks, up_blocks, down_blocks = refs[:10], refs[10:20], refs[20:30]
+    (
+        dheads,
+        top_row,
+        grad_first,
+        normed_second,
+        inv_second,
+        slope,
+        normed_first,
+        inv_first,
+        first_low,
+        act,
+        qkv,
+        vectors,
+        live_row,
+        sums_in,
+        out_rows,
+    ) = refs[30:45]
+    input_out, proj_out, branch_out, send_out, head_out, output_out = refs[45:51]
+    qkv_weight, qkv_sems, up_weight, up_sems, down_weight, down_sems, mixed_grad = refs[51:]
+    down_copies = start_weight(where, down_blocks, down_weight, down_sems)
+    up_copies = start_weight(where, up_blocks, up_weight, up_sems)
+    qkv_copies = start_weight(where, qkv_blocks, qkv_weight, qkv_sems)
+    core_at = where[2]
+    few = 16
+    row_at = lax.broadcasted_iota(jnp.int32, (few, 1), 0)
+    grad_top = dheads[...]
+    normed_head = normed_second[0:1, :]
+    grad = norm_rows_back(grad_top, normed_head, inv_second[0:1, :], vectors[6:7, :])
+    second = grad.astype(LOW)
+    second_few = jnp.where(row_at == 0, grad, 0.0).astype(LOW)
+    head_out[:, 0:MODEL] = first_low[0:1, :MODEL]
+    head_out[:, MODEL : 2 * MODEL] = second
+    wait_all(down_copies)
+    chunk = MODEL
+    pre_parts = []
+    base = 2 * MODEL
+    for at in range(FF // chunk):
+        columns = slice(at * chunk, (at + 1) * chunk)
+        before = product_plain(second_few, rows_view(down_weight, at * chunk, (at + 1) * chunk))
+        pre = (before * slope[0:few, columns]).astype(LOW)
+        pre_parts.append(pre)
+        head_out[:, base + at * chunk : base + (at + 1) * chunk] = pre[0:1, :]
+    head_out[:, base + FF : base + 2 * FF] = act[0:1, :]
+    wait_all(up_copies)
+    pre_few = jnp.concatenate(pre_parts, axis=1)
+    head_first = product_right(pre_few, rows_view(up_weight, MODEL, MODEL + FF))[0:1, :] + grad
+    all_rows = lax.broadcasted_iota(jnp.int32, (SEG, 1), 0)
+    grad_rows = jnp.where(all_rows == 0, head_first, grad_first[...])
+    normed = normed_first[...]
+    grad_summed = norm_rows_back(grad_rows, normed, inv_first[...], vectors[4:5, :])
+    branch = grad_summed.astype(LOW)
+    branch_out[...] = branch
+    mixed_grad[...] = product_right(branch, rows_view(up_weight, 0, MODEL)).astype(LOW)
+    pieces = attend_tiles_back(qkv[...], mixed_grad[...], MODEL, token_allowed(live_row[...]))
+    for tile, value in enumerate(pieces):
+        proj_out[:, tile * LANES : (tile + 1) * LANES] = value
+    wait_all(qkv_copies)
+    grad_in = grad_summed + product_right(proj_out[...], rows_view(qkv_weight, 0, 3 * MODEL))
+    input_out[...] = grad_in.astype(LOW)
+    qkv_half, out_half = 3 * MODEL // CORES, MODEL // CORES
+    other = 1 - core_at
+    send_out[:, :qkv_half] = proj_out[:, pl.ds(pl.multiple_of(other * qkv_half, LANES), qkv_half)]
+    send_out[:, qkv_half:] = branch_out[
+        :, pl.ds(pl.multiple_of(other * out_half, LANES), out_half)
+    ]
+    sums = (
+        column_sum(proj_out[:, :MODEL]),
+        column_sum(proj_out[:, 2 * MODEL :]),
+        column_sum(branch),
+        sums_in[1:2, 0:MODEL] + second.astype(WIDE),
+        column_sum(grad_rows * normed),
+        column_sum(grad_rows),
+        sums_in[1:2, MODEL : 2 * MODEL] + grad_top * normed_head,
+        sums_in[1:2, 2 * MODEL : 3 * MODEL] + grad_top,
+    )
+    base = 2 * MODEL + 2 * FF
+    for at, value in enumerate(sums):
+        head_out[:, base + at * MODEL : base + (at + 1) * MODEL] = value.astype(LOW)
+    base = base + 8 * MODEL
+    for at, pre in enumerate(pre_parts):
+        columns = slice(at * chunk, (at + 1) * chunk)
+        total = sums_in[0:1, columns] + column_sum(pre)
+        head_out[:, base + at * chunk : base + (at + 1) * chunk] = total.astype(LOW)
+    live_head = live_row[0:1, 0:1]
+    output_out[...] = jnp.where(all_rows == 0, top_row[...] * live_head, out_rows[...]).astype(LOW)
+
+
+def cls_weight_kernel(where, *refs):
+    blocks = refs[: LINE * CORES]
+    out, sems = refs[LINE * CORES :]
+    line_at, plane_at, core_at = where[0], where[1], where[2]
+    copies = []
+    for block_at, block in enumerate(blocks):
+        step, core = block_at % LINE, (core_at if block_at < LINE else 1 - core_at)
+        for mask in range(PLANE):
+            target = out.at[(line_at + LINE - step) % LINE, plane_at ^ mask, core]
+            copies.append(pltpu.make_async_copy(block.at[mask], target, sems.at[len(copies)]))
+    for copy in copies:
+        copy.start()
+    wait_all(copies)
+
+
+def row_from_column(column, size):
+    shape = (size, size)
+    same = lax.broadcasted_iota(jnp.int32, shape, 0) == lax.broadcasted_iota(jnp.int32, shape, 1)
+    return jnp.sum(jnp.where(same, column, 0.0), axis=0, keepdims=True)
+
+
+def head_allowed(heads):
+    facts = heads[:, 2 * MODEL :]
+    live, doc = facts[:, 0:1], facts[:, 1:2]
+    shape = (GROUP, GROUP)
+    same = lax.broadcasted_iota(jnp.int32, shape, 0) == lax.broadcasted_iota(jnp.int32, shape, 1)
+    live_row, doc_row = row_from_column(live, GROUP), row_from_column(doc, GROUP)
+    return ((live_row > 0.5) & (doc == doc_row)) | same
+
+
+def quarter_mask(plane_at):
+    lane = lax.broadcasted_iota(jnp.int32, (GROUP, SPAN), 1)
+    first = (plane_at % 2) * HEAD_DIM
+    return (lane >= first) & (lane < first + 3 * HEAD_DIM)
+
+
+def plane_piece(vectors, row, plane_at):
+    value = jnp.zeros((1, SPAN), WIDE)
+    for at in range(PLANE):
+        first = TILE_START[at] * LANES
+        value = jnp.where(plane_at == at, vectors[row : row + 1, first : first + SPAN], value)
+    return value
+
+
+def cls_attend_kernel(where, *refs):
+    stacks, vectors, weight, out_weight = refs[:4], refs[4], refs[5], refs[6]
+    heads_out, qkv_out, mixed_out, part_out = refs[7:]
+    line_at, plane_at = where[0], where[1]
+    for mask, stack in enumerate(stacks):
+        for step in range(LINE):
+            row = (line_at + LINE - step) % LINE * PLANE + (plane_at ^ mask)
+            heads_out[pl.ds(row, 1), :] = stack[step : step + 1, :]
+    heads = heads_out[...]
+    inputs = heads[:, :MODEL].astype(LOW)
+    projected = product_plain(inputs, weight[:, : 3 * SPAN])
+    query = projected[:, :SPAN] + plane_piece(vectors, 12, plane_at)
+    value = projected[:, 2 * SPAN :] + plane_piece(vectors, 13, plane_at)
+    qkv_out[:, :SPAN] = query.astype(LOW)
+    qkv_out[:, SPAN : 2 * SPAN] = projected[:, SPAN : 2 * SPAN].astype(LOW)
+    qkv_out[:, 2 * SPAN :] = value.astype(LOW)
+    mixed = attend_tiles(qkv_out[...], SPAN, head_allowed(heads))
+    mixed = masked(jnp.concatenate(mixed, axis=1), quarter_mask(plane_at))
+    mixed_out[...] = mixed
+    part_out[...] = product_plain(mixed, out_weight[...])
+
+
+def cls_mlp_kernel(where, *refs):
+    heads, own, got_one, got_two, got_three, vectors, weight = refs[:7]
+    normed_out, inv_out, low_out, act_out, slope_out, part_out = refs[7:]
+    plane_at = where[1]
+    branch = own[...] + got_one[...] + got_two[...] + got_three[...]
+    normed, inv_dev = norm_rows(heads[:, :MODEL] + branch + vectors[14:15, :])
+    normed_out[...] = normed
+    inv_out[...] = inv_dev
+    low = (normed * vectors[16:17, :] + vectors[17:18, :]).astype(LOW)
+    low_out[...] = low
+    part = FF // PLANE
+    first = 3 * SPAN
+    bias = vectors[pl.ds(20 + plane_at, 1), :]
+    before = product_plain(low, weight[:, first : first + part]) + bias
+    value, slope = gelu_both(before)
+    act = value.astype(LOW)
+    act_out[...] = act
+    slope_out[...] = slope
+    part_out[...] = product_right(act, weight[:, first + part :])
+
+
+def cls_top_kernel(where, *refs):
+    heads, own, got_one, got_two, got_three, vectors, weight = refs[:7]
+    normed_first, count, slope = refs[7:10]
+    top_out, square_out, grad_out, second_out, pre_out, part_out, sums_out = refs[10:17]
+    held = refs[17]
+    rank = where[0] * PLANE + where[1]
+    first = normed_first[...] * vectors[16:17, :] + vectors[17:18, :]
+    down = own[...] + got_one[...] + got_two[...] + got_three[...]
+    normed, inv_dev = norm_rows(first + down + vectors[15:16, :])
+    rows = normed * vectors[18:19, :] + vectors[19:20, :]
+    held[...] = rows
+    top_out[...] = held[pl.ds(rank, 1), :]
+    facts = heads[:, 2 * MODEL :]
+    live = facts[:, 0:1]
+    diff = (rows * live - heads[:, MODEL : 2 * MODEL]) * live
+    square = jnp.sum(column_sum(diff * diff), axis=1, keepdims=True)
+    square = square + jnp.sum(facts[:, 3:4], axis=0, keepdims=True)
+    square_out[...] = jnp.broadcast_to(square, square_out.shape)
+    grad_top = diff * ((SEG * GROUP * CORES) / count[0:1, 0:1])
+    grad = norm_rows_back(grad_top, normed, inv_dev, vectors[18:19, :])
+    sums_out[0:1, :] = column_sum(grad_top * normed)
+    sums_out[1:2, :] = column_sum(grad_top)
+    grad_out[...] = grad
+    second = grad.astype(LOW)
+    second_out[...] = second
+    part = FF // PLANE
+    at = 3 * SPAN
+    pre = (product_plain(second, weight[:, at + part :]) * slope[...]).astype(LOW)
+    pre_out[...] = pre
+    part_out[...] = product_right(pre, weight[:, at : at + part])
+
+
+def cls_attend_back_kernel(where, *refs):
+    heads, own, got_one, got_two, got_three, vectors, weight, out_weight = refs[:8]
+    grad_in, normed_first, inv_first, qkv = refs[8:12]
+    grad_out, branch_out, proj_out, part_out, sums_out = refs[12:]
+    plane_at = where[1]
+    grad_first = grad_in[...] + own[...] + got_one[...] + got_two[...] + got_three[...]
+    normed = normed_first[...]
+    grad = norm_rows_back(grad_first, normed, inv_first[...], vectors[16:17, :])
+    sums_out[0:1, :] = column_sum(grad_first * normed)
+    sums_out[1:2, :] = column_sum(grad_first)
+    grad_out[...] = grad
+    branch = grad.astype(LOW)
+    branch_out[...] = branch
+    mask = quarter_mask(plane_at)
+    mixed_grad = masked(product_right(branch, out_weight[...]).astype(LOW), mask)
+    pieces = attend_tiles_back(qkv[...], mixed_grad, SPAN, head_allowed(heads[...]))
+    tiles = SPAN // LANES
+    for piece in range(3):
+        joined = jnp.concatenate(pieces[piece * tiles : (piece + 1) * tiles], axis=1)
+        proj_out[:, piece * SPAN : (piece + 1) * SPAN] = masked(joined, mask)
+    part_out[...] = product_right(proj_out[...], weight[:, : 3 * SPAN])
+
+
+def cls_end_kernel(where, *refs):
+    heads, grad, own, got_one, got_two, got_three = refs[:6]
+    square, sums_back, sums_top = refs[6:9]
+    row_out, shared_out, held = refs[9:]
+    rank = where[0] * PLANE + where[1]
+    total = grad[...] + own[...] + got_one[...] + got_two[...] + got_three[...]
+    held[...] = total
+    row_out[...] = held[pl.ds(rank, 1), :]
+    number = row_from_column(heads[:, 2 * MODEL + 2 : 2 * MODEL + 3], GROUP)
+    entry = lax.broadcasted_iota(jnp.int32, (GROUP, GROUP), 0).astype(WIDE)
+    hot = (entry == number).astype(WIDE)
+    shared_out[0:GROUP, :] = jnp.dot(hot, total, precision=lax.Precision.HIGHEST)
+    shared_out[GROUP : GROUP + 1, 0:LANES] = square[0:1, :]
+    shared_out[GROUP + 1 : GROUP + 3, :] = sums_back[0:2, :]
+    shared_out[GROUP + 3 : GROUP + 5, :] = sums_top[0:2, :]
+
+
+def cls_rows_kernel(where, *refs):
+    packs = refs[:4]
+    heads, branch, low, second = refs[4:8]
+    out, kept = refs[8:]
+    plane_at = where[1]
+    for mask, pack in enumerate(packs):
+        kept[plane_at ^ mask] = pack[...]
+    starts = (MODEL, 2 * MODEL, 3 * MODEL, 4 * MODEL)
+    out[:, 0:MODEL] = heads[:, :MODEL].astype(LOW)
+    for piece, start in enumerate(starts):
+        from_at = piece * SPAN
+        for tile in range(MODEL // LANES):
+            total = None
+            for at in range(PLANE):
+                inner = tile - TILE_START[at]
+                if inner in (0, 1):
+                    first = from_at + inner * LANES
+                    value = kept[at, :, first : first + LANES]
+                    total = value if total is None else total + value
+            out[:, start + tile * LANES : start + (tile + 1) * LANES] = total
+    out[:, 5 * MODEL : 6 * MODEL] = branch[...]
+    out[:, 6 * MODEL : 7 * MODEL] = low[...]
+    out[:, 7 * MODEL + FF : 8 * MODEL + FF] = second[...]
+    part = FF // PLANE
+    for at in range(PLANE):
+        first = 4 * SPAN
+        out[:, 7 * MODEL + at * part : 7 * MODEL + (at + 1) * part] = kept[
+            at, :, first : first + part
+        ]
+        out[:, 8 * MODEL + FF + at * part : 8 * MODEL + FF + (at + 1) * part] = kept[
+            at, :, first + part : first + 2 * part
+        ]
+
+
+def own_features(rank, width):
+    shape = (MODEL, width)
+    feature = lax.broadcasted_iota(jnp.int32, shape, 0)
+    column = lax.broadcasted_iota(jnp.int32, shape, 1)
+    return (feature == rank * width + column).astype(LOW)
+
+
+def cls_owner_kernel(where, *refs):
+    own, got, mats_out, vecs_out, rows = refs
+    rank = where[0] * PLANE + where[1]
+    width = mats_out.shape[0]
+    rows[:GROUP] = own[...]
+    rows[GROUP:] = got[...]
+    chosen = own_features(rank, width)
+    plan = (
+        (0, MODEL, 3 * MODEL, 0),
+        (4 * MODEL, 5 * MODEL, MODEL, 3 * MODEL),
+        (6 * MODEL, 7 * MODEL, FF, 4 * MODEL),
+        (7 * MODEL + FF, 8 * MODEL + FF, FF, 4 * MODEL + FF),
+    )
+    for left, right, size, target in plan:
+        side = product_plain(rows[:, left : left + MODEL], chosen).astype(LOW)
+        mats_out[:, target : target + size] = product_left(side, rows[:, right : right + size])
+    vecs_out[...] = jnp.zeros_like(vecs_out)
+    for at, start in ((0, MODEL), (1, 3 * MODEL), (2, 5 * MODEL), (3, 7 * MODEL + FF)):
+        vecs_out[at : at + 1, :] = column_sum(rows[:, start : start + MODEL])
+    for at in range(FF // MODEL):
+        start = 7 * MODEL + at * MODEL
+        vecs_out[8 + at : 9 + at, :] = column_sum(rows[:, start : start + MODEL])
+
+
+def seg_owner_kernel(where, *refs):
+    attn, attn_got, mlp, mlp_got = refs[:4]
+    own_rows, got_rows = refs[4:6]
+    mats_out, vecs_out, rows = refs[6:]
+    core_at = where[2]
+    rank = where[0] * PLANE + where[1]
+    width = mats_out.shape[0]
+    rows[:GROUP] = own_rows[...]
+    rows[GROUP:] = got_rows[...]
+    chosen = own_features(rank, width)
+    qkv_half, out_half, half = 3 * MODEL // CORES, MODEL // CORES, FF // CORES
+    own_at, got_at = core_at, 1 - core_at
+
+    def put(base, size, own, got):
+        mats_out[:, pl.ds(pl.multiple_of(base + own_at * size, LANES), size)] = own
+        mats_out[:, pl.ds(pl.multiple_of(base + got_at * size, LANES), size)] = got
+
+    put(0, qkv_half, attn[:, :qkv_half], attn_got[:, :qkv_half])
+    put(3 * MODEL, out_half, attn[:, qkv_half:], attn_got[:, qkv_half:])
+    put(4 * MODEL, half, mlp[:, :half], mlp_got[:, :half])
+    put(4 * MODEL + FF, half, mlp[:, half:], mlp_got[:, half:])
+    for left, right, target in (
+        (0, 2 * MODEL, 4 * MODEL),
+        (MODEL, 2 * MODEL + FF, 4 * MODEL + FF),
+    ):
+        side = product_plain(rows[:, left : left + MODEL], chosen).astype(LOW)
+        mats_out[:, target : target + FF] = mats_out[:, target : target + FF] + product_left(
+            side, rows[:, right : right + FF]
+        )
+    base = 2 * MODEL + 2 * FF
+    for at in range(8 + FF // MODEL):
+        start = base + at * MODEL
+        vecs_out[at : at + 1, :] = column_sum(rows[:, start : start + MODEL])
+
+
+def plane_parts(part):
+    return (part,) + tuple(in_plane(part, mask) for mask in range(1, PLANE))
+
+
+def weight_blocks(piece):
+    line = jnp.stack([piece] + [along_line(piece, apart) for apart in range(1, LINE)])
+    half = LINE // 2
+    from_x, from_y = in_plane(line, 1), in_plane(line, 2)
+    far_low, far_high = in_plane(from_x[:half], 2), in_plane(from_y[half:], 1)
+    own = (line, from_x, from_y, far_low, far_high)
+    return own + tuple(other_core(block) for block in own)
+
+
+def slice_local(
+    hidden_in,
+    targets,
+    doc_ids,
+    seg_nums,
+    valid_flags,
+    seg_mats,
+    seg_vecs,
+    cls_mats,
+    cls_vecs,
+    seg_pos,
+):
+    rank, core_at = lax.axis_index("fsdp"), lax.axis_index("rep")
+    line_at, plane_at = rank // PLANE, rank % PLANE
+    where = jnp.stack([line_at, plane_at, core_at, doc_ids[0], seg_nums[0]]).astype(jnp.int32)
+    own_rows, total_columns = seg_mats.shape
+    half_rows = own_rows // CORES
+    vec_size = seg_vecs.shape[0]
+    vec_lines = -(-vec_size // LANES)
+    live = valid_flags.astype(WIDE)
+    live_row, live_column = live[None, :], live[:, None]
+
+    pad = vec_lines * LANES - vec_size
+    vec_block = jnp.stack([jnp.pad(seg_vecs, (0, pad)), jnp.pad(cls_vecs, (0, pad))])
+    vec_block = vec_block.reshape(2 * vec_lines, LANES)
+    count_row = jnp.full((1, LANES), jnp.sum(live), WIDE).astype(LOW)
+    blank = jnp.zeros((half_rows - 2 * vec_lines - 1, LANES), LOW)
+    vec_block = jnp.concatenate([vec_block, count_row, blank])
+    qkv_columns, up_columns, down_columns = 3 * MODEL + LANES, MODEL + FF, FF + MODEL
+    quarter = 3 * SPAN + 2 * FF // PLANE
+    first_piece, second_piece, third_piece, quarters = run_kernel(
+        prepare_kernel,
+        "prepare",
+        [
+            shape_of((half_rows, qkv_columns), LOW),
+            shape_of((half_rows, up_columns), LOW),
+            shape_of((half_rows, down_columns), LOW),
+            shape_of((PLANE, half_rows, quarter), LOW),
+        ],
+        where,
+        (),
+        (
+            seg_mats.reshape(CORES, half_rows, total_columns),
+            cls_mats.reshape(CORES, half_rows, total_columns),
+            vec_block,
+        ),
+        [pltpu.VMEM((PLANE, half_rows, quarter), LOW)],
+    )
+    qkv_blocks = weight_blocks(first_piece)
+    up_blocks = weight_blocks(second_piece)
+    down_blocks = weight_blocks(third_piece)
+    own_plane = jnp.stack(
+        [quarters[0]] + [in_plane(quarters[mask], mask) for mask in range(1, PLANE)]
+    )
+    cls_line = (own_plane,) + tuple(along_line(own_plane, apart) for apart in range(1, LINE))
+    cls_line = cls_line + tuple(other_core(block) for block in cls_line)
+
+    qkv, both, vectors, count = run_kernel(
+        qkv_kernel,
+        "seg_qkv",
+        [
+            shape_of((SEG, 3 * MODEL), LOW),
+            shape_of((SEG, 2 * MODEL), LOW),
+            shape_of((2 * (8 * MODEL + FF) // MODEL, MODEL)),
+            shape_of((8, LANES)),
+        ],
+        where,
+        qkv_blocks,
+        (hidden_in, live_row),
+        weight_scratch(half_rows, qkv_columns) + [pltpu.VMEM((2, 8 * MODEL + FF), WIDE)],
+        flops=2 * SEG * MODEL * 3 * MODEL,
+    )
+    both_got = other_core(both)
+    normed_first, inv_first, slope, act, first_send = run_kernel(
+        up_kernel,
+        "seg_up",
+        [
+            shape_of((SEG, MODEL)),
+            shape_of((SEG, 1)),
+            shape_of((SEG, FF)),
+            shape_of((SEG, FF), LOW),
+            shape_of((SEG, MODEL + FF // CORES), LOW),
+        ],
+        where,
+        up_blocks,
+        (hidden_in, both, vectors),
+        weight_scratch(half_rows, up_columns),
+        flops=2 * SEG * MODEL * up_columns,
+    )
+    first_got = other_core(first_send)
+    normed_second, inv_second, diff, out_rows, head_row, cls_out = run_kernel(
+        down_kernel,
+        "seg_down",
+        [
+            shape_of((SEG, MODEL)),
+            shape_of((SEG, 1)),
+            shape_of((SEG, MODEL)),
+            shape_of((SEG, MODEL)),
+            shape_of((1, 2 * MODEL + LANES)),
+            shape_of((4, HEAD_DIM, MODEL), LOW),
+        ],
+        where,
+        down_blocks,
+        (act, normed_first, vectors, targets, live_column, seg_pos),
+        weight_scratch(half_rows, down_columns),
+        flops=2 * SEG * MODEL * FF,
+    )
+    cls_out = cls_out.reshape(SPAN, MODEL)
+    cls_weight = run_kernel(
+        cls_weight_kernel,
+        "head_weight",
+        [shape_of((LINE, PLANE, CORES, half_rows, quarter), LOW)],
+        where,
+        cls_line,
+        (),
+        [pltpu.SemaphoreType.DMA((WEIGHT_COPIES,))],
+    )[0].reshape(MODEL, quarter)
+
+    head_stack = jnp.concatenate(
+        [head_row] + [along_line(head_row, apart) for apart in range(1, LINE)]
+    )
+    heads, cls_qkv, cls_mixed, part = run_kernel(
+        cls_attend_kernel,
+        "head_attend",
+        [
+            shape_of((GROUP, 2 * MODEL + LANES)),
+            shape_of((GROUP, 3 * SPAN), LOW),
+            shape_of((GROUP, SPAN), LOW),
+            shape_of((GROUP, MODEL)),
+        ],
+        where,
+        (),
+        plane_parts(head_stack) + (vectors, cls_weight, cls_out),
+    )
+    grad_first, pre, second_send, sums = run_kernel(
+        mlp_back_kernel,
+        "seg_mlp_back",
+        [
+            shape_of((SEG, MODEL)),
+            shape_of((SEG, FF), LOW),
+            shape_of((SEG, MODEL + FF // CORES), LOW),
+            shape_of((2, FF)),
+        ],
+        where,
+        up_blocks + down_blocks,
+        (diff, count, normed_second, inv_second, vectors, slope),
+        weight_scratch(half_rows, up_columns) + weight_scratch(half_rows, down_columns),
+        flops=4 * SEG * MODEL * FF,
+    )
+    second_got = other_core(second_send)
+    part_rows = LINE // 2
+
+    def part_shapes(columns):
+        return [
+            shape_of((count_of, own_rows, columns), LOW)
+            for count_of in (part_rows, part_rows, LINE, LINE, LINE)
+        ]
+
+    mlp_parts = run_kernel(
+        mlp_weight_kernel,
+        "seg_mlp_weight",
+        part_shapes(FF),
+        where,
+        (),
+        (first_send, first_got, second_send, second_got, pre, act),
+        [
+            pltpu.VMEM((2 * SEG, MODEL), LOW),
+            pltpu.VMEM((2 * SEG, FF // CORES), LOW),
+            pltpu.VMEM((GROUP, own_rows, FF), LOW),
+            pltpu.SemaphoreType.DMA((GROUP,)),
+        ],
+        outs_far=True,
+        flops=4 * SEG * MODEL * FF,
+    )
+    mlp_sum = reduce_parts(where, mlp_parts)
+
+    cls_normed, cls_inv, cls_low, cls_act, cls_slope, part = run_kernel(
+        cls_mlp_kernel,
+        "head_mlp",
+        [
+            shape_of((GROUP, MODEL)),
+            shape_of((GROUP, 1)),
+            shape_of((GROUP, MODEL), LOW),
+            shape_of((GROUP, FF // PLANE), LOW),
+            shape_of((GROUP, FF // PLANE)),
+            shape_of((GROUP, MODEL)),
+        ],
+        where,
+        (),
+        (heads,) + plane_parts(part) + (vectors, cls_weight),
+    )
+    top_row, square, cls_grad, cls_second, cls_pre, part, top_sums = run_kernel(
+        cls_top_kernel,
+        "head_top",
+        [
+            shape_of((1, MODEL)),
+            shape_of((8, LANES)),
+            shape_of((GROUP, MODEL)),
+            shape_of((GROUP, MODEL), LOW),
+            shape_of((GROUP, FF // PLANE), LOW),
+            shape_of((GROUP, MODEL)),
+            shape_of((2, MODEL)),
+        ],
+        where,
+        (),
+        (heads,) + plane_parts(part) + (vectors, cls_weight, cls_normed, count, cls_slope),
+        [pltpu.VMEM((GROUP, MODEL), WIDE)],
+    )
+    cls_grad, cls_branch, cls_proj, part, back_sums = run_kernel(
+        cls_attend_back_kernel,
+        "head_attend_back",
+        [
+            shape_of((GROUP, MODEL)),
+            shape_of((GROUP, MODEL), LOW),
+            shape_of((GROUP, 3 * SPAN), LOW),
+            shape_of((GROUP, MODEL)),
+            shape_of((2, MODEL)),
+        ],
+        where,
+        (),
+        (heads,)
+        + plane_parts(part)
+        + (vectors, cls_weight, cls_out, cls_grad, cls_normed, cls_inv, cls_qkv),
+    )
+    dheads, shared = run_kernel(
+        cls_end_kernel,
+        "head_end",
+        [shape_of((1, MODEL)), shape_of((GROUP + 8, MODEL))],
+        where,
+        (),
+        (heads, cls_grad) + plane_parts(part) + (square, back_sums, top_sums),
+        [pltpu.VMEM((GROUP, MODEL), WIDE)],
+    )
+
+    head_width = 2 * MODEL + 2 * FF + 8 * MODEL + FF
+    input_grad, proj, branch, attn_send, head_data, output = run_kernel(
+        seg_back_kernel,
+        "seg_back",
+        [
+            shape_of((SEG, MODEL), LOW),
+            shape_of((SEG, 3 * MODEL), LOW),
+            shape_of((SEG, MODEL), LOW),
+            shape_of((SEG, 2 * MODEL), LOW),
+            shape_of((1, head_width), LOW),
+            shape_of((SEG, MODEL), LOW),
+        ],
+        where,
+        qkv_blocks + up_blocks + down_blocks,
+        (
+            dheads,
+            top_row,
+            grad_first,
+            normed_second,
+            inv_second,
+            slope,
+            normed_first,
+            inv_first,
+            first_send,
+            act,
+            qkv,
+            vectors,
+            live_row,
+            sums,
+            out_rows,
+        ),
+        weight_scratch(half_rows, qkv_columns)
+        + weight_scratch(half_rows, up_columns)
+        + weight_scratch(half_rows, down_columns)
+        + [pltpu.VMEM((SEG, MODEL), LOW)],
+        flops=4 * SEG * MODEL * 4 * MODEL,
+    )
+    attn_got = other_core(attn_send)
+    attn_parts = run_kernel(
+        attn_weight_kernel,
+        "seg_attn_weight",
+        part_shapes(2 * MODEL),
+        where,
+        (),
+        (both, both_got, proj, attn_got, branch),
+        [
+            pltpu.VMEM((2 * SEG, 2 * MODEL), LOW),
+            pltpu.VMEM((2 * SEG, 2 * MODEL), LOW),
+            pltpu.VMEM((GROUP, own_rows, 2 * MODEL), LOW),
+            pltpu.SemaphoreType.DMA((GROUP,)),
+        ],
+        outs_far=True,
+        flops=4 * SEG * MODEL * 2 * MODEL,
+    )
+    attn_sum = reduce_parts(where, attn_parts)
+
+    pack = jnp.concatenate([cls_proj, cls_mixed, cls_pre, cls_act], axis=1)
+    row_width = 6 * MODEL + 2 * MODEL + 2 * FF
+    cls_rows = run_kernel(
+        cls_rows_kernel,
+        "head_rows",
+        [shape_of((GROUP, row_width), LOW)],
+        where,
+        (),
+        plane_parts(pack) + (heads, cls_branch, cls_low, cls_second),
+        [pltpu.VMEM((PLANE,) + pack.shape, LOW)],
+    )[0]
+    vec_rows = (8 * MODEL + FF) // MODEL
+    cls_mats_grad, cls_vec_rows = run_kernel(
+        cls_owner_kernel,
+        "head_owner",
+        [shape_of((own_rows, total_columns)), shape_of((vec_rows, MODEL))],
+        where,
+        (),
+        (cls_rows, other_core(cls_rows)),
+        [pltpu.VMEM((CORES * GROUP, row_width), LOW)],
+        flops=64 * own_rows * total_columns,
+    )
+    shared = shared + other_core(shared)
+    pos_total = shared[:GROUP]
+    loss_value = shared[GROUP, 0] / (count[0, 0] * MODEL)
+    norm_grads = shared[GROUP + 1 : GROUP + 5]
+    cls_vec_rows = jnp.concatenate([cls_vec_rows[:4], norm_grads, cls_vec_rows[8:]])
+
+    head_line = jnp.concatenate(
+        [head_data] + [along_line(head_data, apart) for apart in range(1, LINE)]
+    )
+    head_all = jnp.concatenate(plane_parts(head_line))
+    seg_mats_grad, seg_vec_rows = run_kernel(
+        seg_owner_kernel,
+        "seg_owner",
+        [shape_of((own_rows, total_columns)), shape_of((vec_rows, MODEL))],
+        where,
+        (),
+        (attn_sum, other_core(attn_sum), mlp_sum, other_core(mlp_sum))
+        + (head_all, other_core(head_all)),
+        [pltpu.VMEM((CORES * GROUP, head_width), LOW)],
+        flops=64 * own_rows * total_columns,
+    )
+
+    def own_vector(rows):
+        return lax.dynamic_index_in_dim(rows.reshape(GROUP, vec_size), rank, 0, keepdims=False)
+
+    return (
+        output,
+        input_grad,
+        seg_mats_grad,
+        own_vector(seg_vec_rows),
+        cls_mats_grad,
+        own_vector(cls_vec_rows),
+        pos_total,
+        loss_value,
+    )
+
+
 def solution(mesh):
     in_specs = (
         P(("rep", "fsdp"), None),
@@ -541,4 +1720,6 @@
         P(),
         P(),
     )
-    return jax.shard_map(local, mesh=mesh, in_specs=in_specs, out_specs=out_specs, check_vma=False)
+    one_slice = dict(mesh.shape) == {"rep": CORES, "fsdp": LINE * PLANE}
+    body = slice_local if one_slice else local
+    return jax.shard_map(body, mesh=mesh, in_specs=in_specs, out_specs=out_specs, check_vma=False)

time: 1790 us -> 417 us (0.23)
  waiting for transfers between devices: 1360 us -> 181 us
  blocking collectives: 237 us -> 0 us
  starting transfers between devices: 15.7 us -> 102 us
  Pallas kernels: 0 us -> 81 us
  matrix products: 67.6 us -> 0 us
  other arithmetic: 51.5 us -> 8.28 us
  between operations: 28.2 us -> 4.61 us
    reduce_scatter x12 -> x0, waiting for transfers between devices: 1140 us -> none  [the longest x1 175 us: local(): lax.psum_scatter(cls_g_up, 'fsdp', scatter_dimension=0, tiled=True)]
    all_gather x2 -> x0, waiting for transfers between devices: 216 us -> none  [the longest x1 153 us: local(): lax.all_gather(cls_mats, 'fsdp', axis=0, tiled=True)]
    ppermute x12 -> x96, waiting for transfers between devices: 4.73 us -> 181 us  [the longest x44 117 us: in_plane(): return lax.ppermute(value, 'fsdp', plane_pairs(mask))]
    unnamed x4 -> x0, blocking collectives: 126 us -> none
    psum x2 -> x0, blocking collectives: 91 us -> none  [the longest x1 48.9 us: local(): pos_total = lax.psum(pos_local, ('rep', 'fsdp'))]
    ppermute x12 -> x96, starting transfers between devices: 14.5 us -> 102 us  [the longest x28 39.3 us: other_core(): return lax.ppermute(value, 'rep', [(0, 1), (1, 0)])]
    pallas_call x0 -> x19, Pallas kernels: none -> 81 us  [run_kernel(): pl.pallas_call(body, name=name, out_shape=tuple(outs), in_specs=in_specs,...]
    dot_general x30 -> x0, matrix products: 67.6 us -> none  [the longest x8 27.5 us: product_right(): lax.dot_general(left_side, right_side, (((1,), (1,)), ((), ())), preferre...]
  transfers between devices with their start and end apart: 30 -> 96, of which waited for: 21 -> 34; matrix products, arithmetic and copies ran while one was open for 6% -> 4% of each run, Pallas kernels for 0% -> 19%
where the time goes in v2:
time: 417 us; the launch traced here: 415 us
  waiting for transfers between devices  181 us (43%)
  starting transfers between devices  102 us (24%)
  Pallas kernels  81 us (19%)
  local copies, waits for them, and re-layouts  38.6 us (9%)
  other arithmetic  8.28 us (2%)
  between operations  4.61 us (1%)
    ppermute x44, waiting for transfers between devices, in_plane(): return lax.ppermute(value, 'fsdp', plane_pairs(mask))  117 us
    pallas_call x19, Pallas kernels, run_kernel(): pl.pallas_call(body, name=name, out_shape=tuple(outs), in_specs=in_specs,...  81 us
    ppermute x24, waiting for transfers between devices, along_line(): return lax.ppermute(value, 'fsdp', line_pairs(apart))  63.4 us
    ppermute x28, starting transfers between devices, other_core(): return lax.ppermute(value, 'rep', [(0, 1), (1, 0)])  39.3 us
    ppermute x44, starting transfers between devices, in_plane(): return lax.ppermute(value, 'fsdp', plane_pairs(mask))  37.5 us
    unnamed x149, local copies, waits for them, and re-layouts  26.6 us
    ppermute x24, starting transfers between devices, along_line(): return lax.ppermute(value, 'fsdp', line_pairs(apart))  25.1 us
  transfers between devices with their start and end apart: 96, of which 34 were waited for; matrix products, arithmetic and copies ran while one was open for 4% of the time, Pallas kernels for 19%

profile of v2, /device:TPU:13, one launch (start us, length us, event | category | flops | bytes accessed | tf_op | source)
XLA Modules:
  0.0 415.2 jit_solution(11650368551658611873)
XLA Ops:
  12.5 3.1 collective-permute-start.13
  19.0 11.1 %collective-permute-done.2 = bf16[24,2432]{1,0:T(8,128)(2,1)S(1)} collective-permute-done((bf16[24,2432]{1,0:T(8,128)(2,1)S(1)}, bf16[24,2432]{1,0:T(8,128)(2,1)S(1)}, u32[]{:S(2)}, u32[]{:S(2)}) %collective-permute-start.2) | collective-permute-done | bytes 116768 | tf_op jit(solution)/shard_map/ppermute | solution.py:565
  35.3 8.8 %collective-permute-done.44 = bf16[24,2304]{1,0:T(8,128)(2,1)S(1)} collective-permute-done((bf16[24,2304]{1,0:T(8,128)(2,1)S(1)}, bf16[24,2304]{1,0:T(8,128)(2,1)S(1)}, u32[]{:S(2)}, u32[]{:S(2)}) %collective-permute-start.44) | collective-permute-done | bytes 110624 | tf_op jit(solution)/shard_map/ppermute | solution.py:569
  50.6 6.7 %collective-permute-done.25 = bf16[24,3840]{1,0:T(8,128)(2,1)S(1)} collective-permute-done((bf16[24,3840]{1,0:T(8,128)(2,1)S(1)}, bf16[24,3840]{1,0:T(8,128)(2,1)S(1)}, u32[]{:S(2)}, u32[]{:S(2)}) %collective-permute-start.25) | collective-permute-done | bytes 184352 | tf_op jit(solution)/shard_map/ppermute | solution.py:565
  58.2 20.1 %collective-permute-done.26 = bf16[24,3840]{1,0:T(8,128)(2,1)S(1)} collective-permute-done((bf16[24,3840]{1,0:T(8,128)(2,1)S(1)}, bf16[24,3840]{1,0:T(8,128)(2,1)S(1)}, u32[]{:S(2)}, u32[]{:S(2)}) %collective-permute-start.26) | collective-permute-done | bytes 184352 | tf_op jit(solution)/shard_map/ppermute | solution.py:565
  80.9 8.8 %collective-permute-done.4.refs_2_ = bf16[4,24,2432]{2,1,0:T(8,128)(2,1)S(1)} collective-permute-done((bf16[4,24,2432]{2,1,0:T(8,128)(2,1)S(1)}, bf16[4,24,2432]{2,1,0:T(8,128)(2,1)S(1)}, u32[]{:S(2)}, u32[]{:S(2)}) %collective-permute-start.4) | collective-permute-done | bytes 466976 | tf_op jit(solution)/shard_map/ppermute | solution.py:569
  92.4 4.4 %collective-permute-done.46.refs_2_ = bf16[4,24,2304]{2,1,0:T(8,128)(2,1)S(1)} collective-permute-done((bf16[4,24,2304]{2,1,0:T(8,128)(2,1)}, bf16[4,24,2304]{2,1,0:T(8,128)(2,1)S(1)}, u32[]{:S(2)}, u32[]{:S(2)}) %collective-permute-start.46) | collective-permute-done | bytes 442400 | tf_op jit(solution)/shard_map/ppermute | solution.py:565
  102.3 9.9 %collective-permute-done.5.refs_3_ = bf16[2,24,2432]{2,1,0:T(8,128)(2,1)S(1)} collective-permute-done((bf16[2,24,2432]{2,1,0:T(8,128)(2,1)S(1)}, bf16[2,24,2432]{2,1,0:T(8,128)(2,1)S(1)}, u32[]{:S(2)}, u32[]{:S(2)}) %collective-permute-start.5) | collective-permute-done | bytes 233504 | tf_op jit(solution)/shard_map/ppermute | solution.py:569
  113.7 3.5 collective-permute-start.31
  117.9 9.5 %collective-permute-done.27.refs_1_.refs_11_.refs_21_ = bf16[4,24,3840]{2,1,0:T(8,128)(2,1)} collective-permute-done((bf16[4,24,3840]{2,1,0:T(8,128)(2,1)S(1)}, bf16[4,24,3840]{2,1,0:T(8,128)(2,1)}, u32[]{:S(2)}, u32[]{:S(2)}) %collective-permute-start.27) | collective-permute-done | bytes 737312 | tf_op jit(solution)/shard_map/ppermute | solution.py:569
  128.8 5.9 %collective-permute-start.10 = (bf16[2,24,2432]{2,1,0:T(8,128)(2,1)S(1)}, bf16[2,24,2432]{2,1,0:T(8,128)(2,1)S(1)}, u32[]{:S(2)}, u32[]{:S(2)}) collective-permute-start(bf16[2,24,2432]{2,1,0:T(8,128)(2,1)S(1)} %collective-permute-done.5.refs_3_), channel_id=1, source_target_pairs={{0,16},{16,0},{1,17},{17,1},{2,18},{18,2},{3,19},{19,3},{4,20},{20... | collective-permute-start | bytes 700424 | tf_op jit(solution)/shard_map/ppermute | solution.py:573
  144.4 4.6 %collective-permute-done.29.refs_3_.refs_13_.refs_23_ = bf16[2,24,3840]{2,1,0:T(8,128)(2,1)} collective-permute-done((bf16[2,24,3840]{2,1,0:T(8,128)(2,1)S(1)}, bf16[2,24,3840]{2,1,0:T(8,128)(2,1)}, u32[]{:S(2)}, u32[]{:S(2)}) %collective-permute-start.29) | collective-permute-done | bytes 368672 | tf_op jit(solution)/shard_map/ppermute | solution.py:569
  167.3 8.5 %seg_qkv.1 = (bf16[128,2304]{1,0:T(8,128)(2,1)S(1)}, bf16[128,1536]{1,0:T(8,128)(2,1)S(1)}, f32[24,768]{1,0:T(8,128)S(1)}, f32[8,128]{1,0:T(8,128)S(1)}) custom-call(s32[5]{0:T(128)S(1)} %stack.81.where, bf16[4,24,2432]{2,1,0:T(8,128)(2,1)S(1)} %pad_maximum_fusion.2.refs_0_, bf16[4,24,2432]{2,1,0:T(8,128)(2,1)S(1)} %copy-done.19, ...), custom_call_target="tpu_custom_call" | custom-call | flops 452984832 | bytes 4993536 | tf_op jit(solution)/shard_map/seg_qkv/pallas_call | solution.py:587
  176.0 10.3 %seg_up.1 = (f32[128,768]{1,0:T(8,128)S(1)}, f32[128,1]{1,0:T(8,128)S(1)}, f32[128,3072]{1,0:T(8,128)}, bf16[128,3072]{1,0:T(8,128)(2,1)}, bf16[128,2304]{1,0:T(8,128)(2,1)S(1)}) custom-call(s32[5]{0:T(128)S(1)} %stack.81.where, bf16[4,24,3840]{2,1,0:T(8,128)(2,1)S(1)} %pad_maximum_fusion.refs_0_.refs_10_, ...), custom_call_target="tpu_custom_call" | custom-call | flops 754974720 | bytes 9904640 | tf_op jit(solution)/shard_map/seg_up/pallas_call | solution.py:587
  187.3 7.2 %seg_down.1 = (f32[128,768]{1,0:T(8,128)S(1)}, f32[128,1]{1,0:T(8,128)S(1)}, f32[128,768]{1,0:T(8,128)S(1)}, f32[128,768]{1,0:T(8,128)S(1)}, f32[1,1664]{1,0:T(1,128)S(1)}, /*index=5*/bf16[4,64,768]{2,1,0:T(8,128)(2,1)S(1)}) custom-call(s32[5]{0:T(128)S(1)} %stack.81.where, bf16[4,24,3840]{2,1,0:T(8,128)(2,1)S(1)} %pad_maximum_fusion.1.refs_0_.refs_10_.refs_20_, ...), custom_call_target="tpu_custom_call" | custom-call | flops 603979776 | bytes 8953344 | tf_op jit(solution)/shard_map/seg_down/pallas_call | solution.py:587
  197.7 8.4 %seg_mlp_back.1 = (f32[128,768]{1,0:T(8,128)S(1)}, bf16[128,3072]{1,0:T(8,128)(2,1)}, bf16[128,2304]{1,0:T(8,128)(2,1)S(1)}, f32[2,3072]{1,0:T(2,128)S(1)}) custom-call(s32[5]{0:T(128)S(1)} %stack.81.where, bf16[4,24,3840]{2,1,0:T(8,128)(2,1)S(1)} %pad_maximum_fusion.refs_0_.refs_10_, bf16[4,24,3840]{2,1,0:T(8,128)(2,1)} %copy-done.4, ...), custom_call_target="tpu_custom_call" | custom-call | flops 1207959552 | bytes 16028160 | tf_op jit(solution)/shard_map/seg_mlp_back/pallas_call | solution.py:587
  210.5 6.0 %head_weight.1 = bf16[4,4,2,24,2304]{4,3,2,1,0:T(8,128)(2,1)} custom-call(s32[5]{0:T(128)S(1)} %stack.81.where, bf16[4,24,2304]{2,1,0:T(8,128)(2,1)} %pad_maximum_fusion.3.refs_0_, bf16[4,24,2304]{2,1,0:T(8,128)(2,1)S(1)} %copy-done.47, bf16[4,24,2304]{2,1,0:T(8,128)(2,1)S(1)} %copy-done.49, bf16[4,24,2304]{2,1,0:T(8,128)(2,1)} %collective-permute-done.47.refs_3_, ...), custom_call_target="tpu_custom_call" | custom-call | bytes 7077888 | tf_op jit(solution)/shard_map/head_weight/pallas_call | solution.py:587
  243.7 6.8 %collective-permute-start.64 = (bf16[128,1536]{1,0:T(8,128)(2,1)S(1)}, bf16[128,1536]{1,0:T(8,128)(2,1)S(1)}, u32[]{:S(2)}, u32[]{:S(2)}) collective-permute-start(bf16[128,1536]{1,0:T(8,128)(2,1)S(1)} %copy-done.53), channel_id=1, source_target_pairs={{0,16},{16,0},{1,17},{17,1},{2,18},{18,2},{3,19},{19,3},{4,20},{20... | collective-permute-start | bytes 1179656 | tf_op jit(solution)/shard_map/ppermute | solution.py:573
  251.4 3.9 seg_mlp_weight.1
  257.0 15.8 %seg_back.1 = (bf16[128,768]{1,0:T(8,128)(2,1)}, bf16[128,2304]{1,0:T(8,128)(2,1)}, bf16[128,768]{1,0:T(8,128)(2,1)S(1)}, bf16[128,1536]{1,0:T(8,128)(2,1)S(1)},...) custom-call(s32[5]{0:T(128)S(1)} %stack.81.where, bf16[4,24,2432]{2,1,0:T(8,128)(2,1)} %copy-done.8, ...), custom_call_target="tpu_custom_call" | custom-call | flops 1207959552 | bytes 22356480 | tf_op jit(solution)/shard_map/seg_back/pallas_call | solution.py:587
  272.7 3.1 collective-permute-start.65
  291.4 3.5 seg_attn_weight.1
  295.5 14.5 %collective-permute-done.76 = bf16[2,48,3072]{2,1,0:T(8,128)(2,1)S(1)} collective-permute-done((bf16[2,48,3072]{2,1,0:T(8,128)(2,1)S(1)}, bf16[2,48,3072]{2,1,0:T(8,128)(2,1)S(1)}, u32[]{:S(2)}, u32[]{:S(2)}) %collective-permute-start.76) | collective-permute-done | bytes 589856 | tf_op jit(solution)/shard_map/ppermute | solution.py:569
  313.2 6.6 %collective-permute-done.68 = bf16[2,48,1536]{2,1,0:T(8,128)(2,1)S(1)} collective-permute-done((bf16[2,48,1536]{2,1,0:T(8,128)(2,1)S(1)}, bf16[2,48,1536]{2,1,0:T(8,128)(2,1)S(1)}, u32[]{:S(2)}, u32[]{:S(2)}) %collective-permute-start.68) | collective-permute-done | bytes 294944 | tf_op jit(solution)/shard_map/ppermute | solution.py:569
  321.7 24.6 %collective-permute-done.66 = bf16[2,48,1536]{2,1,0:T(8,128)(2,1)S(1)} collective-permute-done((bf16[2,48,1536]{2,1,0:T(8,128)(2,1)S(1)}, bf16[2,48,1536]{2,1,0:T(8,128)(2,1)S(1)}, u32[]{:S(2)}, u32[]{:S(2)}) %collective-permute-start.66) | collective-permute-done | bytes 294944 | tf_op jit(solution)/shard_map/ppermute | solution.py:569
  354.5 11.8 %collective-permute-done.88 = bf16[4,16896]{1,0:T(4,128)(2,1)S(1)} collective-permute-done((bf16[4,16896]{1,0:T(4,128)(2,1)S(1)}, bf16[4,16896]{1,0:T(4,128)(2,1)S(1)}, u32[]{:S(2)}, u32[]{:S(2)}) %collective-permute-start.88) | collective-permute-done | bytes 135200 | tf_op jit(solution)/shard_map/ppermute | solution.py:569
  372.8 3.8 concatenate.30.refs_4_
  377.6 3.0 head_owner.1
  380.6 4.2 %collective-permute-start.90 = (bf16[16,16896]{1,0:T(8,128)(2,1)S(1)}, bf16[16,16896]{1,0:T(8,128)(2,1)}, u32[]{:S(2)}, u32[]{:S(2)}) collective-permute-start(bf16[16,16896]{1,0:T(8,128)(2,1)S(1)} %concatenate.30.refs_4_), channel_id=1, source_target_pairs={{0,16},{16,0},{1,17},{17,1},{2,18},{18,2},{3,19},{19,3},{4,20},{20... | collective-permute-start | bytes 1622024 | tf_op jit(solution)/shard_map/ppermute | solution.py:573
  390.5 11.5 %collective-permute-done.82 = bf16[48,3072]{1,0:T(8,128)(2,1)} collective-permute-done((bf16[48,3072]{1,0:T(8,128)(2,1)}, bf16[48,3072]{1,0:T(8,128)(2,1)}, u32[]{:S(2)}, u32[]{:S(2)}) %collective-permute-start.82) | collective-permute-done | bytes 294944 | tf_op jit(solution)/shard_map/ppermute | solution.py:565
  404.0 4.2 %collective-permute-done.72 = bf16[48,1536]{1,0:T(8,128)(2,1)S(1)} collective-permute-done((bf16[48,1536]{1,0:T(8,128)(2,1)S(1)}, bf16[48,1536]{1,0:T(8,128)(2,1)S(1)}, u32[]{:S(2)}, u32[]{:S(2)}) %collective-permute-start.72) | collective-permute-done | bytes 147488 | tf_op jit(solution)/shard_map/ppermute | solution.py:565
  410.1 3.2 seg_owner.1
  (374 shorter events, 153.4 us)
Async XLA Ops:
  12.4 31.7 %collective-permute-start.12 = (bf16[24,3840]{1,0:T(8,128)(2,1)S(1)}, bf16[24,3840]{1,0:T(8,128)(2,1)S(1)}, u32[]{:S(2)}, u32[]{:S(2)}) collective-permute-start(bf16[24,3840]{1,0:T(8,128)(2,1)S(1)} %get-tuple-element.132), channel_id=1, source_target_pairs={{0,4},{1,5},{2,6},{3,7},{4,8},{5,9},{6,10},{7,11},{8,12},{9,13},{1... | collective-permute-start | bytes 552968 | tf_op jit(solution)/shard_map/ppermute | solution.py:565
  12.5 31.7 %collective-permute-start.13 = (bf16[24,3840]{1,0:T(8,128)(2,1)S(1)}, bf16[24,3840]{1,0:T(8,128)(2,1)S(1)}, u32[]{:S(2)}, u32[]{:S(2)}) collective-permute-start(bf16[24,3840]{1,0:T(8,128)(2,1)S(1)} %get-tuple-element.132), channel_id=1, source_target_pairs={{0,8},{1,9},{2,10},{3,11},{4,12},{5,13},{6,14},{7,15},{8,0},{9,1},... | collective-permute-start | bytes 552968 | tf_op jit(solution)/shard_map/ppermute | solution.py:565
  30.1 49.5 %collective-permute-start.3 = (bf16[4,24,2432]{2,1,0:T(8,128)(2,1)S(1)}, bf16[4,24,2432]{2,1,0:T(8,128)(2,1)S(1)}, u32[]{:S(2)}, u32[]{:S(2)}) collective-permute-start(bf16[4,24,2432]{2,1,0:T(8,128)(2,1)S(1)} %pad_maximum_fusion.2.refs_0_), channel_id=1, source_target_pairs={{0,1},{1,0},{2,3},{3,2},{4,5},{5,4},{6,7},{7,6},{8,9},{9,8},{10,11... | collective-permute-start | bytes 1400840 | tf_op jit(solution)/shard_map/ppermute | solution.py:569
  44.1 34.2 %collective-permute-start.26 = (bf16[24,3840]{1,0:T(8,128)(2,1)S(1)}, bf16[24,3840]{1,0:T(8,128)(2,1)S(1)}, u32[]{:S(2)}, u32[]{:S(2)}) collective-permute-start(bf16[24,3840]{1,0:T(8,128)(2,1)S(1)} %get-tuple-element.133), channel_id=1, source_target_pairs={{0,12},{1,13},{2,14},{3,15},{4,0},{5,1},{6,2},{7,3},{8,4},{9,5},{1... | collective-permute-start | bytes 552968 | tf_op jit(solution)/shard_map/ppermute | solution.py:565
  46.5 44.6 %collective-permute-start.45 = (bf16[4,24,2304]{2,1,0:T(8,128)(2,1)}, bf16[4,24,2304]{2,1,0:T(8,128)(2,1)S(1)}, u32[]{:S(2)}, u32[]{:S(2)}) collective-permute-start(bf16[4,24,2304]{2,1,0:T(8,128)(2,1)} %pad_maximum_fusion.3.refs_0_), channel_id=1, source_target_pairs={{0,4},{1,5},{2,6},{3,7},{4,8},{5,9},{6,10},{7,11},{8,12},{9,13},{1... | collective-permute-start | bytes 1327112 | tf_op jit(solution)/shard_map/ppermute | solution.py:565
  48.5 48.3 %collective-permute-start.46 = (bf16[4,24,2304]{2,1,0:T(8,128)(2,1)}, bf16[4,24,2304]{2,1,0:T(8,128)(2,1)S(1)}, u32[]{:S(2)}, u32[]{:S(2)}) collective-permute-start(bf16[4,24,2304]{2,1,0:T(8,128)(2,1)} %pad_maximum_fusion.3.refs_0_), channel_id=1, source_target_pairs={{0,8},{1,9},{2,10},{3,11},{4,12},{5,13},{6,14},{7,15},{8,0},{9,1},... | collective-permute-start | bytes 1327112 | tf_op jit(solution)/shard_map/ppermute | solution.py:565
  57.3 41.6 %collective-permute-start.47 = (bf16[4,24,2304]{2,1,0:T(8,128)(2,1)}, bf16[4,24,2304]{2,1,0:T(8,128)(2,1)}, u32[]{:S(2)}, u32[]{:S(2)}) collective-permute-start(bf16[4,24,2304]{2,1,0:T(8,128)(2,1)} %pad_maximum_fusion.3.refs_0_), channel_id=1, source_target_pairs={{0,12},{1,13},{2,14},{3,15},{4,0},{5,1},{6,2},{7,3},{8,4},{9,5},{1... | collective-permute-start | bytes 1327112 | tf_op jit(solution)/shard_map/ppermute | solution.py:565
  89.8 23.9 %collective-permute-start.15 = (bf16[4,24,3840]{2,1,0:T(8,128)(2,1)S(1)}, bf16[4,24,3840]{2,1,0:T(8,128)(2,1)S(1)}, u32[]{:S(2)}, u32[]{:S(2)}) collective-permute-start(bf16[4,24,3840]{2,1,0:T(8,128)(2,1)S(1)} %pad_maximum_fusion.refs_0_.refs_10_), channel_id=1, source_target_pairs={{0,1},{1,0},{2,3},{3,2},{4,5},{5,4},{6,7},{7,6},{8,9},{9,8},{10,11... | collective-permute-start | bytes 2211848 | tf_op jit(solution)/shard_map/ppermute | solution.py:569
  91.1 26.0 %collective-permute-start.16 = (bf16[4,24,3840]{2,1,0:T(8,128)(2,1)S(1)}, bf16[4,24,3840]{2,1,0:T(8,128)(2,1)S(1)}, u32[]{:S(2)}, u32[]{:S(2)}) collective-permute-start(bf16[4,24,3840]{2,1,0:T(8,128)(2,1)S(1)} %pad_maximum_fusion.refs_0_.refs_10_), channel_id=1, source_target_pairs={{0,2},{1,3},{2,0},{3,1},{4,6},{5,7},{6,4},{7,5},{8,10},{9,11},{10,... | collective-permute-start | bytes 2211848 | tf_op jit(solution)/shard_map/ppermute | solution.py:569
  152.9 34.1 %collective-permute-start.32 = (bf16[4,24,3840]{2,1,0:T(8,128)(2,1)}, bf16[4,24,3840]{2,1,0:T(8,128)(2,1)}, u32[]{:S(2)}, u32[]{:S(2)}) collective-permute-start(bf16[4,24,3840]{2,1,0:T(8,128)(2,1)} %collective-permute-done.27.refs_1_.refs_11_.refs_21_), channel_id=1, source_target_pairs={{0,16},{16,0},{1,17},{17,1},{2,18},{18,2},{3,19},{19,3},{4,20},{20... | collective-permute-start | bytes 2211848 | tf_op jit(solution)/shard_map/ppermute | solution.py:573
  155.0 32.3 %collective-permute-start.33 = (bf16[4,24,3840]{2,1,0:T(8,128)(2,1)}, bf16[4,24,3840]{2,1,0:T(8,128)(2,1)}, u32[]{:S(2)}, u32[]{:S(2)}) collective-permute-start(bf16[4,24,3840]{2,1,0:T(8,128)(2,1)} %collective-permute-done.28.refs_2_.refs_12_.refs_22_), channel_id=1, source_target_pairs={{0,16},{16,0},{1,17},{17,1},{2,18},{18,2},{3,19},{19,3},{4,20},{20... | collective-permute-start | bytes 2211848 | tf_op jit(solution)/shard_map/ppermute | solution.py:573
  155.7 39.5 %collective-permute-start.48 = (bf16[4,24,2304]{2,1,0:T(8,128)(2,1)}, bf16[4,24,2304]{2,1,0:T(8,128)(2,1)}, u32[]{:S(2)}, u32[]{:S(2)}) collective-permute-start(bf16[4,24,2304]{2,1,0:T(8,128)(2,1)} %pad_maximum_fusion.3.refs_0_), channel_id=1, source_target_pairs={{0,16},{16,0},{1,17},{17,1},{2,18},{18,2},{3,19},{19,3},{4,20},{20... | collective-permute-start | bytes 1327112 | tf_op jit(solution)/shard_map/ppermute | solution.py:573
  156.2 30.1 %collective-permute-start.34 = (bf16[2,24,3840]{2,1,0:T(8,128)(2,1)}, bf16[2,24,3840]{2,1,0:T(8,128)(2,1)}, u32[]{:S(2)}, u32[]{:S(2)}) collective-permute-start(bf16[2,24,3840]{2,1,0:T(8,128)(2,1)} %collective-permute-done.29.refs_3_.refs_13_.refs_23_), channel_id=1, source_target_pairs={{0,16},{16,0},{1,17},{17,1},{2,18},{18,2},{3,19},{19,3},{4,20},{20... | collective-permute-start | bytes 1105928 | tf_op jit(solution)/shard_map/ppermute | solution.py:573
  156.3 30.4 %collective-permute-start.35 = (bf16[2,24,3840]{2,1,0:T(8,128)(2,1)}, bf16[2,24,3840]{2,1,0:T(8,128)(2,1)}, u32[]{:S(2)}, u32[]{:S(2)}) collective-permute-start(bf16[2,24,3840]{2,1,0:T(8,128)(2,1)} %collective-permute-done.30.refs_4_.refs_14_.refs_24_), channel_id=1, source_target_pairs={{0,16},{16,0},{1,17},{17,1},{2,18},{18,2},{3,19},{19,3},{4,20},{20... | collective-permute-start | bytes 1105928 | tf_op jit(solution)/shard_map/ppermute | solution.py:573
  186.4 21.4 %collective-permute-start.49 = (bf16[4,24,2304]{2,1,0:T(8,128)(2,1)S(1)}, bf16[4,24,2304]{2,1,0:T(8,128)(2,1)S(1)}, u32[]{:S(2)}, u32[]{:S(2)}) collective-permute-start(bf16[4,24,2304]{2,1,0:T(8,128)(2,1)S(1)} %copy-done.47), channel_id=1, source_target_pairs={{0,16},{16,0},{1,17},{17,1},{2,18},{18,2},{3,19},{19,3},{4,20},{20... | collective-permute-start | bytes 1327112 | tf_op jit(solution)/shard_map/ppermute | solution.py:573
  206.2 45.2 %collective-permute-start.75 = (bf16[128,2304]{1,0:T(8,128)(2,1)S(1)}, bf16[128,2304]{1,0:T(8,128)(2,1)S(1)}, u32[]{:S(2)}, u32[]{:S(2)}) collective-permute-start(bf16[128,2304]{1,0:T(8,128)(2,1)S(1)} %get-tuple-element.182.refs_2_), channel_id=1, source_target_pairs={{0,16},{16,0},{1,17},{17,1},{2,18},{18,2},{3,19},{19,3},{4,20},{20... | collective-permute-start | bytes 1769480 | tf_op jit(solution)/shard_map/ppermute | solution.py:573
  207.6 43.7 %collective-permute-start.74 = (bf16[128,2304]{1,0:T(8,128)(2,1)S(1)}, bf16[128,2304]{1,0:T(8,128)(2,1)S(1)}, u32[]{:S(2)}, u32[]{:S(2)}) collective-permute-start(bf16[128,2304]{1,0:T(8,128)(2,1)S(1)} %get-tuple-element.164.refs_38_.refs_0_), channel_id=1, source_target_pairs={{0,16},{16,0},{1,17},{17,1},{2,18},{18,2},{3,19},{19,3},{4,20},{20... | collective-permute-start | bytes 1769480 | tf_op jit(solution)/shard_map/ppermute | solution.py:573
  243.7 42.4 %collective-permute-start.64 = (bf16[128,1536]{1,0:T(8,128)(2,1)S(1)}, bf16[128,1536]{1,0:T(8,128)(2,1)S(1)}, u32[]{:S(2)}, u32[]{:S(2)}) collective-permute-start(bf16[128,1536]{1,0:T(8,128)(2,1)S(1)} %copy-done.53), channel_id=1, source_target_pairs={{0,16},{16,0},{1,17},{17,1},{2,18},{18,2},{3,19},{19,3},{4,20},{20... | collective-permute-start | bytes 1179656 | tf_op jit(solution)/shard_map/ppermute | solution.py:573
  255.4 39.6 %collective-permute-start.78 = (bf16[2,48,3072]{2,1,0:T(8,128)(2,1)S(1)}, bf16[2,48,3072]{2,1,0:T(8,128)(2,1)S(1)}, u32[]{:S(2)}, u32[]{:S(2)}) collective-permute-start(bf16[2,48,3072]{2,1,0:T(8,128)(2,1)S(1)} %get-tuple-element.188), channel_id=1, source_target_pairs={{0,1},{1,0},{2,3},{3,2},{4,5},{5,4},{6,7},{7,6},{8,9},{9,8},{10,11... | collective-permute-start | bytes 1769480 | tf_op jit(solution)/shard_map/ppermute | solution.py:569
  281.3 29.8 %collective-permute-start.84 = (bf16[1,16896]{1,0:T(2,128)(2,1)S(1)}, bf16[1,16896]{1,0:T(2,128)(2,1)S(1)}, u32[]{:S(2)}, u32[]{:S(2)}) collective-permute-start(bf16[1,16896]{1,0:T(2,128)(2,1)S(1)} %get-tuple-element.193), channel_id=1, source_target_pairs={{0,4},{1,5},{2,6},{3,7},{4,8},{5,9},{6,10},{7,11},{8,12},{9,13},{1... | collective-permute-start | bytes 101384 | tf_op jit(solution)/shard_map/ppermute | solution.py:565
  284.2 28.4 %collective-permute-start.85 = (bf16[1,16896]{1,0:T(2,128)(2,1)S(1)}, bf16[1,16896]{1,0:T(2,128)(2,1)S(1)}, u32[]{:S(2)}, u32[]{:S(2)}) collective-permute-start(bf16[1,16896]{1,0:T(2,128)(2,1)S(1)} %get-tuple-element.193), channel_id=1, source_target_pairs={{0,8},{1,9},{2,10},{3,11},{4,12},{5,13},{6,14},{7,15},{8,0},{9,1},... | collective-permute-start | bytes 101384 | tf_op jit(solution)/shard_map/ppermute | solution.py:565
  286.1 26.6 %collective-permute-start.86 = (bf16[1,16896]{1,0:T(2,128)(2,1)S(1)}, bf16[1,16896]{1,0:T(2,128)(2,1)S(1)}, u32[]{:S(2)}, u32[]{:S(2)}) collective-permute-start(bf16[1,16896]{1,0:T(2,128)(2,1)S(1)} %get-tuple-element.193), channel_id=1, source_target_pairs={{0,12},{1,13},{2,14},{3,15},{4,0},{5,1},{6,2},{7,3},{8,4},{9,5},{1... | collective-permute-start | bytes 101384 | tf_op jit(solution)/shard_map/ppermute | solution.py:565
  287.8 60.4 %collective-permute-start.95 = (f32[24,768]{1,0:T(8,128)S(1)}, f32[24,768]{1,0:T(8,128)S(1)}, u32[]{:S(2)}, u32[]{:S(2)}) collective-permute-start(f32[24,768]{1,0:T(8,128)S(1)} %get-tuple-element.205), channel_id=1, source_target_pairs={{0,16},{16,0},{1,17},{17,1},{2,18},{18,2},{3,19},{19,3},{4,20},{20... | collective-permute-start | bytes 221192 | tf_op jit(solution)/shard_map/ppermute | solution.py:573
  310.0 59.0 %collective-permute-start.94 = (bf16[16,12288]{1,0:T(8,128)(2,1)S(1)}, bf16[16,12288]{1,0:T(8,128)(2,1)S(1)}, u32[]{:S(2)}, u32[]{:S(2)}) collective-permute-start(bf16[16,12288]{1,0:T(8,128)(2,1)S(1)} %head_rows.1.refs_0_), channel_id=1, source_target_pairs={{0,16},{16,0},{1,17},{17,1},{2,18},{18,2},{3,19},{19,3},{4,20},{20... | collective-permute-start | bytes 1179656 | tf_op jit(solution)/shard_map/ppermute | solution.py:573
  312.6 37.6 %collective-permute-start.79 = (bf16[4,48,3072]{2,1,0:T(8,128)(2,1)S(1)}, bf16[4,48,3072]{2,1,0:T(8,128)(2,1)S(1)}, u32[]{:S(2)}, u32[]{:S(2)}) collective-permute-start(bf16[4,48,3072]{2,1,0:T(8,128)(2,1)S(1)} %add_dynamic-update-slice_fusion), channel_id=1, source_target_pairs={{0,2},{1,3},{2,0},{3,1},{4,6},{5,7},{6,4},{7,5},{8,10},{9,11},{10,... | collective-permute-start | bytes 3538952 | tf_op jit(solution)/shard_map/ppermute | solution.py:569
  312.8 38.2 %collective-permute-start.77 = (bf16[4,48,3072]{2,1,0:T(8,128)(2,1)S(1)}, bf16[4,48,3072]{2,1,0:T(8,128)(2,1)S(1)}, u32[]{:S(2)}, u32[]{:S(2)}) collective-permute-start(bf16[4,48,3072]{2,1,0:T(8,128)(2,1)S(1)} %add_dynamic-update-slice_fusion.1), channel_id=1, source_target_pairs={{0,1},{1,0},{2,3},{3,2},{4,5},{5,4},{6,7},{7,6},{8,9},{9,8},{10,11... | collective-permute-start | bytes 3538952 | tf_op jit(solution)/shard_map/ppermute | solution.py:569
  319.8 26.4 %collective-permute-start.66 = (bf16[2,48,1536]{2,1,0:T(8,128)(2,1)S(1)}, bf16[2,48,1536]{2,1,0:T(8,128)(2,1)S(1)}, u32[]{:S(2)}, u32[]{:S(2)}) collective-permute-start(bf16[2,48,1536]{2,1,0:T(8,128)(2,1)S(1)} %get-tuple-element.175), channel_id=1, source_target_pairs={{0,2},{1,3},{2,0},{3,1},{4,6},{5,7},{6,4},{7,5},{8,10},{9,11},{10,... | collective-permute-start | bytes 884744 | tf_op jit(solution)/shard_map/ppermute | solution.py:569
  348.2 32.4 %collective-permute-start.69 = (bf16[4,48,1536]{2,1,0:T(8,128)(2,1)}, bf16[4,48,1536]{2,1,0:T(8,128)(2,1)S(1)}, u32[]{:S(2)}, u32[]{:S(2)}) collective-permute-start(bf16[4,48,1536]{2,1,0:T(8,128)(2,1)} %add_dynamic-update-slice_fusion.2), channel_id=1, source_target_pairs={{0,2},{1,3},{2,0},{3,1},{4,6},{5,7},{6,4},{7,5},{8,10},{9,11},{10,... | collective-permute-start | bytes 1769480 | tf_op jit(solution)/shard_map/ppermute | solution.py:569
  350.1 34.7 %collective-permute-start.67 = (bf16[4,48,1536]{2,1,0:T(8,128)(2,1)}, bf16[4,48,1536]{2,1,0:T(8,128)(2,1)S(1)}, u32[]{:S(2)}, u32[]{:S(2)}) collective-permute-start(bf16[4,48,1536]{2,1,0:T(8,128)(2,1)} %add_dynamic-update-slice_fusion.3), channel_id=1, source_target_pairs={{0,1},{1,0},{2,3},{3,2},{4,5},{5,4},{6,7},{7,6},{8,9},{9,8},{10,11... | collective-permute-start | bytes 1769480 | tf_op jit(solution)/shard_map/ppermute | solution.py:569
  366.3 22.6 %collective-permute-start.81 = (bf16[48,3072]{1,0:T(8,128)(2,1)}, bf16[48,3072]{1,0:T(8,128)(2,1)}, u32[]{:S(2)}, u32[]{:S(2)}) collective-permute-start(bf16[48,3072]{1,0:T(8,128)(2,1)} %get-tuple-element.191), channel_id=1, source_target_pairs={{0,8},{1,9},{2,10},{3,11},{4,12},{5,13},{6,14},{7,15},{8,0},{9,1},... | collective-permute-start | bytes 884744 | tf_op jit(solution)/shard_map/ppermute | solution.py:565
  369.7 32.3 %collective-permute-start.82 = (bf16[48,3072]{1,0:T(8,128)(2,1)}, bf16[48,3072]{1,0:T(8,128)(2,1)}, u32[]{:S(2)}, u32[]{:S(2)}) collective-permute-start(bf16[48,3072]{1,0:T(8,128)(2,1)} %get-tuple-element.192), channel_id=1, source_target_pairs={{0,12},{1,13},{2,14},{3,15},{4,0},{5,1},{6,2},{7,3},{8,4},{9,5},{1... | collective-permute-start | bytes 884744 | tf_op jit(solution)/shard_map/ppermute | solution.py:565
  380.6 29.1 %collective-permute-start.90 = (bf16[16,16896]{1,0:T(8,128)(2,1)S(1)}, bf16[16,16896]{1,0:T(8,128)(2,1)}, u32[]{:S(2)}, u32[]{:S(2)}) collective-permute-start(bf16[16,16896]{1,0:T(8,128)(2,1)S(1)} %concatenate.30.refs_4_), channel_id=1, source_target_pairs={{0,16},{16,0},{1,17},{17,1},{2,18},{18,2},{3,19},{19,3},{4,20},{20... | collective-permute-start | bytes 1622024 | tf_op jit(solution)/shard_map/ppermute | solution.py:573
  (137 other events, 1838.6 us)

commit v3 on v2

--- a/solution.py
+++ b/solution.py
@@ -573,6 +573,10 @@
     return lax.ppermute(value, "rep", [(0, 1), (1, 0)])
 
 
+def after(value, *events):
+    return lax.optimization_barrier((value,) + events)[0]
+
+
 def shape_of(dims, dtype=WIDE):
     return jax.ShapeDtypeStruct(dims, dtype)
 
@@ -596,29 +600,16 @@
     )(where, *blocks, *arrays)
 
 
-VMEM_BYTES = 48 * 1024 * 1024
-BLOCK_PLAN = (
-    (0, 0, LINE),
-    (1, 0, LINE),
-    (2, 0, LINE),
-    (3, 0, LINE // 2),
-    (3, LINE // 2, LINE // 2),
-)
-WEIGHT_COPIES = LINE * PLANE * CORES
-
-
-def start_weight(where, blocks, scratch, sems):
-    line_at, plane_at, core_at = where[0], where[1], where[2]
-    copies = []
-    for block_at, block in enumerate(blocks):
-        mask, first, count = BLOCK_PLAN[block_at % len(BLOCK_PLAN)]
-        core = core_at if block_at < len(BLOCK_PLAN) else 1 - core_at
-        for step in range(count):
-            target = scratch.at[(line_at + LINE - first - step) % LINE, plane_at ^ mask, core]
-            copies.append(pltpu.make_async_copy(block.at[step], target, sems.at[len(copies)]))
-    for copy in copies:
-        copy.start()
-    return copies
+VMEM_BYTES = 24 * 1024 * 1024
+HALF = MODEL // CORES
+FF_HALF = FF // CORES
+OWN = MODEL // GROUP
+QUARTER = 3 * SPAN + 2 * FF // LINE
+QUARTER_HALF = QUARTER // CORES
+
+
+def aligned(start):
+    return pl.multiple_of(start, LANES)
 
 
 def wait_all(copies):
@@ -626,43 +617,91 @@
         copy.wait()
 
 
-def rows_view(scratch, first, last):
-    value = scratch[:, :, :, :, first:last]
-    return value.reshape(LINE * PLANE * CORES * value.shape[3], last - first)
-
-
-def weight_scratch(rows, columns):
-    return [
-        pltpu.VMEM((LINE, PLANE, CORES, rows, columns), LOW),
-        pltpu.SemaphoreType.DMA((WEIGHT_COPIES,)),
+def run_copies(pairs, sems):
+    copies = [
+        pltpu.make_async_copy(source, target, sems.at[at])
+        for at, (source, target) in enumerate(pairs)
     ]
-
-
-def prepare_kernel(where, seg, cls, vecs, first_out, second_out, third_out, quarter_out, kept):
-    core_at, plane_at = where[2], where[1]
-    half = seg.shape[1]
-    qkv = 3 * MODEL
-    own = seg[core_at]
-    own_cls = cls[core_at]
-    first_out[:, :qkv] = own[:, :qkv]
-    first_out[:, qkv:] = vecs[...]
-    second_out[...] = own[:, qkv : 4 * MODEL + FF]
-    third_out[:, :FF] = own[:, 4 * MODEL + FF :]
-    third_out[:, FF:] = own_cls[:, qkv : 4 * MODEL]
-    part = FF // PLANE
-    for at in range(PLANE):
+    for copy in copies:
+        copy.start()
+    wait_all(copies)
+
+
+def gather_blocks(where, refs, base, width, targets):
+    line_at, plane_at = where[0], where[1]
+    half = LINE // 2
+    for mask in range(PLANE):
+        for step in range(LINE):
+            if mask == 0:
+                ref, offset = refs[step], 0
+            elif mask == 3:
+                ref = refs[LINE + 3] if step < half else refs[LINE + 2]
+                offset = step % half * width
+            else:
+                ref, offset = refs[LINE + mask - 1], base + step * width
+            chip = (line_at + LINE - step) % LINE * PLANE + (plane_at ^ mask)
+            for whole, first, last in targets:
+                whole[chip] = ref[:, offset + first : offset + last]
+
+
+def whole_rows(ref):
+    value = ref[...]
+    return value.reshape(value.shape[0] * value.shape[1], value.shape[2])
+
+
+def prepare_first_kernel(where, seg, seg_vec, cls_vec, live_row, out, sems):
+    core_at = where[2]
+    pairs = []
+    for piece in range(4):
+        source = seg.at[:, pl.ds(aligned(piece * MODEL + core_at * HALF), HALF)]
+        pairs.append((source, out.at[:, piece * HALF : (piece + 1) * HALF]))
+    run_copies(pairs, sems)
+    size = seg_vec.shape[1]
+    lines = -(-size // LANES)
+    block = jnp.zeros((OWN, LANES), WIDE)
+    row_at = lax.broadcasted_iota(jnp.int32, (OWN, LANES), 0)
+    for which, vec in enumerate((seg_vec, cls_vec)):
+        for line in range(lines):
+            width = min(LANES, size - line * LANES)
+            value = vec[:, line * LANES : line * LANES + width].astype(WIDE)
+            if width < LANES:
+                value = jnp.concatenate([value, jnp.zeros((1, LANES - width), WIDE)], axis=1)
+            block = jnp.where(row_at == which * lines + line, value, block)
+    count = jnp.sum(live_row[...], axis=1, keepdims=True)
+    block = jnp.where(row_at == 2 * lines, count, block)
+    out[:, 4 * HALF :] = block.astype(LOW)
+
+
+def prepare_rest_kernel(where, seg, cls, *refs):
+    second_out, third_out = refs[:2]
+    step_outs, out_half = refs[2 : 2 + LINE], refs[2 + LINE]
+    quarters, sems = refs[3 + LINE :]
+    line_at, core_at = where[0], where[2]
+    start = core_at * FF_HALF
+    pairs = [
+        (seg.at[:, pl.ds(aligned(4 * MODEL + start), FF_HALF)], second_out),
+        (seg.at[:, pl.ds(aligned(4 * MODEL + FF + start), FF_HALF)], third_out),
+        (cls.at[:, pl.ds(aligned(3 * MODEL + core_at * HALF), HALF)], out_half),
+    ]
+    part = FF // LINE
+    for at in range(LINE):
         first = TILE_START[at] * LANES
-        for piece in range(3):
-            kept[at, :, piece * SPAN : (piece + 1) * SPAN] = own_cls[
-                :, piece * MODEL + first : piece * MODEL + first + SPAN
-            ]
-        for piece in range(2):
-            start = 4 * MODEL + piece * FF + at * part
-            kept[at, :, 3 * SPAN + piece * part : 3 * SPAN + (piece + 1) * part] = own_cls[
-                :, start : start + part
-            ]
-    for mask in range(PLANE):
-        quarter_out[mask] = kept[plane_at ^ mask]
+        plan = [(piece * MODEL + first, SPAN, piece * SPAN) for piece in range(3)]
+        plan += [
+            (4 * MODEL + piece * FF + at * part, part, 3 * SPAN + piece * part)
+            for piece in range(2)
+        ]
+        for source, size, target in plan:
+            pairs.append(
+                (
+                    cls.at[:, source : source + size],
+                    quarters.at[at, :, target : target + size],
+                )
+            )
+    run_copies(pairs, sems)
+    lanes = pl.ds(aligned(core_at * QUARTER_HALF), QUARTER_HALF)
+    for step, out in enumerate(step_outs):
+        out[...] = quarters[(line_at + step) % LINE, :, lanes]
 
 
 def lane_mask(rows, head):
@@ -732,25 +771,33 @@
 
 
 def qkv_kernel(where, *refs):
-    blocks = refs[:10]
-    hidden, live_row, qkv_out, both_out, vectors_out, count_out, weight, sems, flat = refs[10:]
-    copies = start_weight(where, blocks, weight, sems)
-    wait_all(copies)
-    qkv = 3 * MODEL
+    blocks = refs[:8]
+    hidden, hidden_got, live_row, live_got = refs[8:12]
+    weight, out_half, qkv_out, mixed_out, vectors_out, count_out = refs[12:18]
+    vec_rows, flat, inputs = refs[18:]
+    core_at = where[2]
+    gather_blocks(
+        where,
+        blocks,
+        0,
+        4 * HALF + LANES,
+        (
+            (weight, 0, 3 * HALF),
+            (out_half, 3 * HALF, 4 * HALF),
+            (vec_rows, 4 * HALF, 4 * HALF + LANES),
+        ),
+    )
     piece = (8 * MODEL + FF) // GROUP
     lines = -(-piece // LANES)
     count = jnp.zeros((1, LANES), WIDE)
     for chip in range(GROUP):
-        at = (chip // PLANE, chip % PLANE)
-        rows = weight[at[0], at[1], 0, 0:16, qkv:].astype(WIDE)
+        rows = vec_rows[chip, 0:16, :].astype(WIDE)
         for block in range(2):
             joined = jnp.concatenate(
                 [rows[block * lines + r : block * lines + r + 1] for r in range(lines)], axis=1
             )
             flat[block : block + 1, chip * piece : (chip + 1) * piece] = joined[:, :piece]
-        for core in range(CORES):
-            rows_core = weight[at[0], at[1], core, 0:16, qkv:].astype(WIDE)
-            count = count + rows_core[2 * lines : 2 * lines + 1]
+        count = count + rows[2 * lines : 2 * lines + 1]
     rows_each = (8 * MODEL + FF) // MODEL
     for block in range(2):
         for row in range(rows_each):
@@ -758,14 +805,18 @@
                 block : block + 1, row * MODEL : (row + 1) * MODEL
             ]
     count_out[...] = jnp.broadcast_to(count, count_out.shape)
-    inputs = hidden[...]
-    projected = product_plain(inputs, rows_view(weight, 0, qkv))
-    qkv_out[:, :MODEL] = (projected[:, :MODEL] + vectors_out[0:1, :]).astype(LOW)
-    qkv_out[:, MODEL : 2 * MODEL] = projected[:, MODEL : 2 * MODEL].astype(LOW)
-    qkv_out[:, 2 * MODEL :] = (projected[:, 2 * MODEL :] + vectors_out[1:2, :]).astype(LOW)
-    both_out[:, :MODEL] = inputs
-    for tile, value in enumerate(attend_tiles(qkv_out[...], MODEL, token_allowed(live_row[...]))):
-        both_out[:, MODEL + tile * LANES : MODEL + (tile + 1) * LANES] = value
+    inputs[:SEG] = hidden[...]
+    inputs[SEG:] = hidden_got[...]
+    projected = product_plain(inputs[...], whole_rows(weight))
+    lanes = pl.ds(aligned(core_at * HALF), HALF)
+    qkv_out[:, :HALF] = (projected[:, :HALF] + vectors_out[0:1, lanes]).astype(LOW)
+    qkv_out[:, HALF : 2 * HALF] = projected[:, HALF : 2 * HALF].astype(LOW)
+    qkv_out[:, 2 * HALF :] = (projected[:, 2 * HALF :] + vectors_out[1:2, lanes]).astype(LOW)
+    for part, live in enumerate((live_row, live_got)):
+        rows = slice(part * SEG, (part + 1) * SEG)
+        tiles = attend_tiles(qkv_out[rows, :], HALF, token_allowed(live[...]))
+        for tile, value in enumerate(tiles):
+            mixed_out[rows, tile * LANES : (tile + 1) * LANES] = value
 
 
 def norm_rows(summed):
@@ -796,42 +847,55 @@
     return before * half, slope
 
 
-def up_kernel(where, *refs):
-    blocks = refs[:10]
-    hidden, both, vectors, normed_out, inv_out, slope_out, act_out, send_out = refs[10:18]
-    weight, sems = refs[18:]
-    copies = start_weight(where, blocks, weight, sems)
-    wait_all(copies)
+def out_kernel(where, hidden, mixed, mixed_got, half, half_got, vectors, *outs):
+    full_out, mixed_full, normed_out, inv_out, low_out = outs
     core_at = where[2]
-    branch = product_plain(both[:, MODEL:], rows_view(weight, 0, MODEL))
+    own, other = aligned(core_at * HALF), aligned((1 - core_at) * HALF)
+    full_out[:, pl.ds(own, HALF)] = half[...]
+    full_out[:, pl.ds(other, HALF)] = half_got[...]
+    mixed_full[:, pl.ds(own, HALF)] = mixed[...]
+    mixed_full[:SEG, pl.ds(other, HALF)] = mixed_got[SEG:, :]
+    mixed_full[SEG:, pl.ds(other, HALF)] = mixed_got[:SEG, :]
+    branch = product_plain(mixed_full[:SEG, :], full_out[...])
     normed, inv_dev = norm_rows(hidden[...].astype(WIDE) + branch + vectors[2:3, :])
     normed_out[...] = normed
     inv_out[...] = inv_dev
-    first_low = (normed * vectors[4:5, :] + vectors[5:6, :]).astype(LOW)
-    send_out[:, :MODEL] = first_low
-    chunk = MODEL
-    for at in range(FF // chunk):
-        first = MODEL + at * chunk
-        before = product_plain(first_low, rows_view(weight, first, first + chunk))
-        value, slope = gelu_both(before + vectors[8 + at : 9 + at, :])
-        act_out[:, at * chunk : (at + 1) * chunk] = value.astype(LOW)
-        slope_out[:, at * chunk : (at + 1) * chunk] = slope
-    half = FF // CORES
-    sent = pl.multiple_of((1 - core_at) * half, LANES)
-    send_out[:, MODEL:] = act_out[:, pl.ds(sent, half)]
+    low_out[...] = (normed * vectors[4:5, :] + vectors[5:6, :]).astype(LOW)
+
+
+def up_kernel(where, *refs):
+    blocks = refs[:8]
+    low, low_got, vectors = refs[8:11]
+    weight, act_out, slope_out, both = refs[11:]
+    core_at = where[2]
+    gather_blocks(where, blocks, 2 * (4 * HALF + LANES), FF_HALF, ((weight, 0, FF_HALF),))
+    both[:SEG] = low[...]
+    both[SEG:] = low_got[...]
+    for at in range(FF_HALF // MODEL):
+        columns = slice(at * MODEL, (at + 1) * MODEL)
+        held = weight[:, :, columns]
+        before = product_plain(both[...], held.reshape(MODEL, MODEL))
+        bias = vectors[pl.ds(8 + core_at * (FF_HALF // MODEL) + at, 1), :]
+        value, slope = gelu_both(before + bias)
+        act_out[:, columns] = value.astype(LOW)
+        slope_out[:, columns] = slope
 
 
 def down_kernel(where, *refs):
-    blocks = refs[:10]
-    act, normed_first, vectors, targets, live, seg_pos = refs[10:16]
-    normed_out, inv_out, diff_out, rows_out, head_out, cls_out = refs[16:22]
-    weight, sems = refs[22:]
-    copies = start_weight(where, blocks, weight, sems)
-    wait_all(copies)
-    plane_at, doc, number = where[1], where[3], where[4]
+    blocks, act = refs[:8], refs[8]
+    weight, own_out, send_out = refs[9:]
+    gather_blocks(where, blocks, 2 * FF_HALF, FF_HALF, ((weight, 0, FF_HALF),))
+    partial = product_right(act[...], whole_rows(weight))
+    own_out[...] = partial[:SEG]
+    send_out[...] = partial[SEG:]
+
+
+def seg_rows_kernel(where, *refs):
+    own, got, normed_first, vectors, targets, live, seg_pos = refs[:7]
+    normed_out, inv_out, diff_out, rows_out, head_out = refs[7:]
+    doc, number = where[3], where[4]
     first = normed_first[...] * vectors[4:5, :] + vectors[5:6, :]
-    down = product_right(act[...], rows_view(weight, 0, FF))
-    normed, inv_dev = norm_rows(first + down + vectors[3:4, :])
+    normed, inv_dev = norm_rows(first + own[...] + got[...] + vectors[3:4, :])
     normed_out[...] = normed
     inv_out[...] = inv_dev
     rows = normed * vectors[6:7, :] + vectors[7:8, :]
@@ -855,41 +919,35 @@
     facts = jnp.where(lane == 2, number.astype(WIDE), facts)
     facts = jnp.where(lane == 3, square, facts)
     head_out[:, 2 * MODEL :] = facts
-    part = weight[plane_at, :, :, :, FF:].reshape(3, HEAD_DIM, MODEL)
-    cls_out[...] = jnp.zeros_like(cls_out)
-    cls_out[pl.ds(plane_at % 2, 3)] = part
-
-
-def mlp_back_kernel(where, *refs):
-    up_blocks, down_blocks = refs[:10], refs[10:20]
-    diff, count, normed, inv_dev, vectors, slope = refs[20:26]
-    grad_out, pre_out, send_out, sums_out = refs[26:30]
-    up_weight, up_sems, down_weight, down_sems = refs[30:]
-    down_copies = start_weight(where, down_blocks, down_weight, down_sems)
-    up_copies = start_weight(where, up_blocks, up_weight, up_sems)
-    core_at = where[2]
-    scale = (SEG * GROUP * CORES) / count[0:1, 0:1]
-    grad_top = diff[...] * scale
+
+
+def second_norm_kernel(where, diff, count, normed, inv_dev, vectors, grad_out, low_out, sums_out):
+    grad_top = diff[...] * ((SEG * GROUP * CORES) / count[0:1, 0:1])
     normed_rows = normed[...]
     grad = norm_rows_back(grad_top, normed_rows, inv_dev[...], vectors[6:7, :])
-    second = grad.astype(LOW)
-    sums_out[1:2, 0:MODEL] = column_sum(second)
-    sums_out[1:2, MODEL : 2 * MODEL] = column_sum(grad_top * normed_rows)
-    sums_out[1:2, 2 * MODEL : 3 * MODEL] = column_sum(grad_top)
-    send_out[:, :MODEL] = second
-    wait_all(down_copies)
-    chunk = MODEL
-    for at in range(FF // chunk):
-        columns = slice(at * chunk, (at + 1) * chunk)
-        before = product_plain(second, rows_view(down_weight, at * chunk, (at + 1) * chunk))
+    low = grad.astype(LOW)
+    grad_out[...] = grad
+    low_out[...] = low
+    sums_out[0:1, :] = column_sum(low)
+    sums_out[1:2, :] = column_sum(grad_top * normed_rows)
+    sums_out[2:3, :] = column_sum(grad_top)
+
+
+def mlp_back_kernel(where, *refs):
+    low, low_got, down_weight, up_weight, slope = refs[:5]
+    pre_out, own_out, send_out, sums_out, both = refs[5:]
+    both[:SEG] = low[...]
+    both[SEG:] = low_got[...]
+    for at in range(FF_HALF // MODEL):
+        columns = slice(at * MODEL, (at + 1) * MODEL)
+        held = down_weight[:, :, columns]
+        before = product_plain(both[...], held.reshape(MODEL, MODEL))
         pre = (before * slope[:, columns]).astype(LOW)
         pre_out[:, columns] = pre
-        sums_out[0:1, columns] = column_sum(pre)
-    wait_all(up_copies)
-    grad_out[...] = grad + product_right(pre_out[...], rows_view(up_weight, MODEL, MODEL + FF))
-    half = FF // CORES
-    sent = pl.multiple_of((1 - core_at) * half, LANES)
-    send_out[:, MODEL:] = pre_out[:, pl.ds(sent, half)]
+        sums_out[at : at + 1, :] = column_sum(pre)
+    partial = product_right(pre_out[...], whole_rows(up_weight))
+    own_out[...] = partial[:SEG]
+    send_out[...] = partial[SEG:]
 
 
 def scatter_parts(where, parts, outs, sems):
@@ -913,182 +971,198 @@
 def mlp_weight_kernel(where, *refs):
     first, first_got, second, second_got, pre, act = refs[:6]
     outs = refs[6:11]
+    left, parts, sems = refs[11:]
+    for at, (own, got, right) in enumerate(((first, first_got, pre), (second, second_got, act))):
+        left[:SEG] = own[...]
+        left[SEG:] = got[...]
+        for piece in range(FF_HALF // MODEL):
+            start = piece * MODEL
+            product = product_left(left[...], right[:, start : start + MODEL]).astype(LOW)
+            target = at * FF_HALF + start
+            parts[:, :, target : target + MODEL] = product.reshape(GROUP, OWN, MODEL)
+    scatter_parts(where, parts, outs, sems)
+
+
+def attn_weight_kernel(where, *refs):
+    hidden, hidden_got, mixed, proj, branch, got = refs[:6]
+    outs = refs[6:11]
     left, right, parts, sems = refs[11:]
     core_at = where[2]
-    half = FF // CORES
-    kept = pl.multiple_of(core_at * half, LANES)
-    rows = GROUP * CORES * 24
-    for at, (own, got, tail, got_tail) in enumerate(
-        ((first, first_got, pre, second_got), (second, second_got, act, first_got))
-    ):
-        left[:SEG] = own[:, :MODEL]
-        left[SEG:] = got[:, :MODEL]
-        right[:SEG] = tail[:, pl.ds(kept, half)]
-        right[SEG:] = got_tail[:, MODEL:]
-        for piece in range(half // MODEL):
-            start = piece * MODEL
-            product = product_left(left[...], right[:, start : start + MODEL]).astype(LOW)
-            parts[:, :, at * half + start : at * half + start + MODEL] = product.reshape(
-                GROUP, rows // GROUP, MODEL
-            )
+    left[:SEG] = hidden[...]
+    left[SEG:] = hidden_got[...]
+    right[:SEG] = branch[:, pl.ds(aligned(core_at * HALF), HALF)]
+    right[SEG:] = got[:, HALF:]
+    for piece in range(4):
+        start = piece * HALF
+        if piece < 3:
+            product = product_left(left[...], proj[:, start : start + HALF])
+        else:
+            product = product_left(mixed[...], right[...])
+        parts[:, :, start : start + HALF] = product.astype(LOW).reshape(GROUP, OWN, HALF)
     scatter_parts(where, parts, outs, sems)
 
 
-def attn_weight_kernel(where, *refs):
-    both, both_got, proj, got, branch = refs[:5]
-    outs = refs[5:10]
-    left, right, parts, sems = refs[10:]
-    core_at = where[2]
-    rows = MODEL
-    qkv_half, out_half = 3 * MODEL // CORES, MODEL // CORES
-    left[:SEG] = both[...]
-    left[SEG:] = both_got[...]
-    right[:SEG, :qkv_half] = proj[:, pl.ds(pl.multiple_of(core_at * qkv_half, LANES), qkv_half)]
-    right[:SEG, qkv_half:] = branch[:, pl.ds(pl.multiple_of(core_at * out_half, LANES), out_half)]
-    right[SEG:] = got[...]
-    for piece in range(4):
-        start = piece * out_half
-        side = left[:, :MODEL] if piece < 3 else left[:, MODEL:]
-        product = product_left(side, right[:, start : start + out_half]).astype(LOW)
-        parts[:, :, start : start + out_half] = product.reshape(GROUP, rows // GROUP, out_half)
-    scatter_parts(where, parts, outs, sems)
-
-
-def fold_kernel(where, kept, got_x, got_y, own_out, *sent):
+def fold_kernel(where, kept, got_x, got_y, *refs):
+    extra, own_out, sent = refs[: -LINE], refs[-LINE], refs[1 - LINE :]
+    rows = kept.shape[1]
     for step in range(LINE):
-        total = (
-            kept[step].astype(WIDE) + got_x[step].astype(WIDE) + got_y[step].astype(WIDE)
-        )
+        total = kept[step].astype(WIDE) + got_x[step].astype(WIDE) + got_y[step].astype(WIDE)
         if step == 0:
             own_out[...] = total
-        else:
-            sent[step - 1][...] = total.astype(LOW)
-
-
-def reduce_parts(where, parts):
-    far_low, far_high, to_x, to_y, kept = parts
-    half = LINE // 2
-    from_y, from_x = in_plane(far_low, 2), in_plane(far_high, 1)
-    to_x = to_x.at[:half].add(from_y)
-    to_y = to_y.at[half:].add(from_x)
-    got_x, got_y = in_plane(to_x, 1), in_plane(to_y, 2)
+            continue
+        out = sent[step - 1]
+        out[:rows, :] = total.astype(LOW)
+        if extra:
+            out[rows:, :] = jnp.zeros_like(out[rows:, :])
+            out[rows:, : extra[0].shape[1]] = extra[0][...]
+
+
+def reduce_far(parts):
+    return in_plane(parts[0], 2), in_plane(parts[1], 1)
+
+
+def reduce_add(where, parts, far):
+    shape = parts[2].shape
+    return run_kernel(
+        add_far_kernel,
+        "add_far",
+        [shape_of(shape, LOW)] * 2,
+        where,
+        (),
+        tuple(far) + (parts[2], parts[3]),
+    )
+
+
+def reduce_fold(where, kept, got, *extra):
     _, rows, columns = kept.shape
-    folded = run_kernel(
+    more = sum(value.shape[0] for value in extra)
+    return run_kernel(
         fold_kernel,
         "fold",
-        [shape_of((rows, columns))] + [shape_of((rows, columns), LOW)] * (LINE - 1),
-        where,
-        (),
-        (kept, got_x, got_y),
-    )
-    total = folded[0]
-    for apart in range(1, LINE):
-        total = total + along_line(folded[apart], apart).astype(WIDE)
+        [shape_of((rows, columns))] + [shape_of((rows + more, columns), LOW)] * (LINE - 1),
+        where,
+        (),
+        (kept,) + tuple(got) + extra,
+    )
+
+
+def reduce_line(own, pieces):
+    total = own
+    for piece in pieces:
+        total = total + piece[: own.shape[0]].astype(WIDE)
     return total
 
 
-def seg_back_kernel(where, *refs):
-    qkv_blocks, up_blocks, down_blocks = refs[:10], refs[10:20], refs[20:30]
-    (
-        dheads,
-        top_row,
-        grad_first,
-        normed_second,
-        inv_second,
-        slope,
-        normed_first,
-        inv_first,
-        first_low,
-        act,
-        qkv,
-        vectors,
-        live_row,
-        sums_in,
-        out_rows,
-    ) = refs[30:45]
-    input_out, proj_out, branch_out, send_out, head_out, output_out = refs[45:51]
-    qkv_weight, qkv_sems, up_weight, up_sems, down_weight, down_sems, mixed_grad = refs[51:]
-    down_copies = start_weight(where, down_blocks, down_weight, down_sems)
-    up_copies = start_weight(where, up_blocks, up_weight, up_sems)
-    qkv_copies = start_weight(where, qkv_blocks, qkv_weight, qkv_sems)
-    core_at = where[2]
+def head_back_kernel(where, *refs):
+    grad, grad_got, down_weight, up_weight, slope, act, low, low_got = refs[:8]
+    own_out, send_out, data_out = refs[8:]
     few = 16
     row_at = lax.broadcasted_iota(jnp.int32, (few, 1), 0)
-    grad_top = dheads[...]
-    normed_head = normed_second[0:1, :]
-    grad = norm_rows_back(grad_top, normed_head, inv_second[0:1, :], vectors[6:7, :])
-    second = grad.astype(LOW)
-    second_few = jnp.where(row_at == 0, grad, 0.0).astype(LOW)
-    head_out[:, 0:MODEL] = first_low[0:1, :MODEL]
-    head_out[:, MODEL : 2 * MODEL] = second
-    wait_all(down_copies)
-    chunk = MODEL
-    pre_parts = []
-    base = 2 * MODEL
-    for at in range(FF // chunk):
-        columns = slice(at * chunk, (at + 1) * chunk)
-        before = product_plain(second_few, rows_view(down_weight, at * chunk, (at + 1) * chunk))
-        pre = (before * slope[0:few, columns]).astype(LOW)
-        pre_parts.append(pre)
-        head_out[:, base + at * chunk : base + (at + 1) * chunk] = pre[0:1, :]
-    head_out[:, base + FF : base + 2 * FF] = act[0:1, :]
-    wait_all(up_copies)
-    pre_few = jnp.concatenate(pre_parts, axis=1)
-    head_first = product_right(pre_few, rows_view(up_weight, MODEL, MODEL + FF))[0:1, :] + grad
-    all_rows = lax.broadcasted_iota(jnp.int32, (SEG, 1), 0)
-    grad_rows = jnp.where(all_rows == 0, head_first, grad_first[...])
-    normed = normed_first[...]
-    grad_summed = norm_rows_back(grad_rows, normed, inv_first[...], vectors[4:5, :])
-    branch = grad_summed.astype(LOW)
+
+    def two_rows(first, second):
+        return jnp.where(row_at == 0, first, jnp.where(row_at == 1, second, 0.0))
+
+    second = two_rows(grad[...], grad_got[...]).astype(LOW)
+    data_out[0:1, :] = low[0:1, :].astype(WIDE)
+    data_out[1:2, :] = low_got[0:1, :].astype(WIDE)
+    data_out[2:4, :] = second[0:2].astype(WIDE)
+    partial = jnp.zeros((few, MODEL), WIDE)
+    for at in range(FF_HALF // MODEL):
+        columns = slice(at * MODEL, (at + 1) * MODEL)
+        before = product_plain(second, down_weight[:, :, columns].reshape(MODEL, MODEL))
+        slopes = two_rows(slope[0:1, columns], slope[SEG : SEG + 1, columns])
+        pre = (before * slopes).astype(LOW)
+        partial = partial + product_right(pre, up_weight[:, :, columns].reshape(MODEL, MODEL))
+        data_out[4 + 2 * at : 6 + 2 * at, :] = pre[0:2].astype(WIDE)
+        data_out[8 + 2 * at : 9 + 2 * at, :] = act[0:1, columns].astype(WIDE)
+        data_out[9 + 2 * at : 10 + 2 * at, :] = act[SEG : SEG + 1, columns].astype(WIDE)
+    own_out[...] = partial[0:1]
+    send_out[...] = partial[1:2]
+
+
+def first_norm_kernel(where, *refs):
+    second_grad, own, got, head_grad, head_own, head_got = refs[:6]
+    normed_rows, inv_dev, vectors, out_weight = refs[6:10]
+    grad_out, branch_out, mixed_out, send_out, sums_out = refs[10:]
+    core_at = where[2]
+    grad_rows = second_grad[...] + own[...] + got[...]
+    head = head_grad[...] + head_own[...] + head_got[...]
+    row_at = lax.broadcasted_iota(jnp.int32, (SEG, 1), 0)
+    grad_rows = jnp.where(row_at == 0, head, grad_rows)
+    normed = normed_rows[...]
+    grad = norm_rows_back(grad_rows, normed, inv_dev[...], vectors[4:5, :])
+    grad_out[...] = grad
+    branch = grad.astype(LOW)
     branch_out[...] = branch
-    mixed_grad[...] = product_right(branch, rows_view(up_weight, 0, MODEL)).astype(LOW)
-    pieces = attend_tiles_back(qkv[...], mixed_grad[...], MODEL, token_allowed(live_row[...]))
-    for tile, value in enumerate(pieces):
-        proj_out[:, tile * LANES : (tile + 1) * LANES] = value
-    wait_all(qkv_copies)
-    grad_in = grad_summed + product_right(proj_out[...], rows_view(qkv_weight, 0, 3 * MODEL))
-    input_out[...] = grad_in.astype(LOW)
-    qkv_half, out_half = 3 * MODEL // CORES, MODEL // CORES
-    other = 1 - core_at
-    send_out[:, :qkv_half] = proj_out[:, pl.ds(pl.multiple_of(other * qkv_half, LANES), qkv_half)]
-    send_out[:, qkv_half:] = branch_out[
-        :, pl.ds(pl.multiple_of(other * out_half, LANES), out_half)
-    ]
-    sums = (
-        column_sum(proj_out[:, :MODEL]),
-        column_sum(proj_out[:, 2 * MODEL :]),
-        column_sum(branch),
-        sums_in[1:2, 0:MODEL] + second.astype(WIDE),
-        column_sum(grad_rows * normed),
-        column_sum(grad_rows),
-        sums_in[1:2, MODEL : 2 * MODEL] + grad_top * normed_head,
-        sums_in[1:2, 2 * MODEL : 3 * MODEL] + grad_top,
-    )
-    base = 2 * MODEL + 2 * FF
-    for at, value in enumerate(sums):
-        head_out[:, base + at * MODEL : base + (at + 1) * MODEL] = value.astype(LOW)
-    base = base + 8 * MODEL
-    for at, pre in enumerate(pre_parts):
-        columns = slice(at * chunk, (at + 1) * chunk)
-        total = sums_in[0:1, columns] + column_sum(pre)
-        head_out[:, base + at * chunk : base + (at + 1) * chunk] = total.astype(LOW)
-    live_head = live_row[0:1, 0:1]
-    output_out[...] = jnp.where(all_rows == 0, top_row[...] * live_head, out_rows[...]).astype(LOW)
-
-
-def cls_weight_kernel(where, *refs):
-    blocks = refs[: LINE * CORES]
-    out, sems = refs[LINE * CORES :]
-    line_at, plane_at, core_at = where[0], where[1], where[2]
-    copies = []
-    for block_at, block in enumerate(blocks):
-        step, core = block_at % LINE, (core_at if block_at < LINE else 1 - core_at)
-        for mask in range(PLANE):
-            target = out.at[(line_at + LINE - step) % LINE, plane_at ^ mask, core]
-            copies.append(pltpu.make_async_copy(block.at[mask], target, sems.at[len(copies)]))
-    for copy in copies:
-        copy.start()
-    wait_all(copies)
+    mixed_out[...] = product_right(branch, out_weight[...]).astype(LOW)
+    other = pl.ds(aligned((1 - core_at) * HALF), HALF)
+    send_out[:, :HALF] = mixed_out[:, other]
+    send_out[:, HALF:] = branch_out[:, other]
+    sums_out[0:1, :] = column_sum(branch)
+    sums_out[1:2, :] = column_sum(grad_rows * normed)
+    sums_out[2:3, :] = column_sum(grad_rows)
+
+
+def attn_back_kernel(where, *refs):
+    qkv, mixed_grad, got, live_row, live_got, weight = refs[:6]
+    sums_first, sums_second, sums_up, head_top, head_normed, data = refs[6:12]
+    proj_out, own_out, send_out, payload_out, rows = refs[12:]
+    core_at = where[2]
+    lanes = pl.ds(aligned(core_at * HALF), HALF)
+    for part, live in enumerate((live_row, live_got)):
+        at = slice(part * SEG, (part + 1) * SEG)
+        grad = mixed_grad[:, lanes] if part == 0 else got[:, :HALF]
+        pieces = attend_tiles_back(qkv[at, :], grad, HALF, token_allowed(live[...]))
+        for tile, value in enumerate(pieces):
+            proj_out[at, tile * LANES : (tile + 1) * LANES] = value
+    partial = product_right(proj_out[...], whole_rows(weight))
+    own_out[...] = partial[:SEG]
+    send_out[...] = partial[SEG:]
+    rows[...] = jnp.zeros_like(rows)
+    rows[0:12, :] = data[0:12, :]
+    rows[12:13, lanes] = column_sum(proj_out[:, :HALF])
+    rows[13:14, lanes] = column_sum(proj_out[:, 2 * HALF :])
+    rows[14:15, :] = sums_first[0:1, :]
+    rows[15:16, :] = sums_second[0:1, :] + data[2:3, :]
+    rows[16:18, :] = sums_first[1:3, :]
+    rows[18:19, :] = sums_second[1:2, :] + head_top[...] * head_normed[0:1, :]
+    rows[19:20, :] = sums_second[2:3, :] + head_top[...]
+    for at in range(FF_HALF // MODEL):
+        total = sums_up[at : at + 1, :] + data[4 + 2 * at : 5 + 2 * at, :]
+        total = total + data[5 + 2 * at : 6 + 2 * at, :]
+        rows[pl.ds(20 + core_at * (FF_HALF // MODEL) + at, 1), :] = total
+    payload_out[...] = rows[...].astype(LOW)
+
+
+def cls_gather_kernel(where, *refs):
+    blocks = refs[:8]
+    own_out, from_x, from_y, far_x = refs[8], refs[4], refs[5], refs[6]
+    weight_out, out_rows = refs[9:]
+    plane_at = where[1]
+    gather_blocks(where, blocks, 0, QUARTER_HALF, ((weight_out, 0, QUARTER_HALF),))
+    first = LINE * QUARTER_HALF
+    out_rows[plane_at] = own_out[...]
+    out_rows[plane_at ^ 1] = from_x[:, first : first + HALF]
+    out_rows[plane_at ^ 2] = from_y[:, first : first + HALF]
+    first = LINE // 2 * QUARTER_HALF
+    out_rows[plane_at ^ 3] = far_x[:, first : first + HALF]
+
+
+def cls_weight_kernel(where, own, got, out_half, out_got, weight_out, out_full):
+    line_at, core_at = where[0], where[2]
+    out_full[...] = jnp.zeros_like(out_full)
+    for value, part, core in ((own, out_half, core_at), (got, out_got, 1 - core_at)):
+        weight_out[:, :, pl.ds(aligned(core * QUARTER_HALF), QUARTER_HALF)] = value[...]
+        rows = part[...].reshape(3, HEAD_DIM, HALF)
+        out_full[pl.ds(line_at % 2, 3), :, pl.ds(aligned(core * HALF), HALF)] = rows
+
+
+def add_far_kernel(where, far_low, far_high, to_x, to_y, x_out, y_out):
+    half = LINE // 2
+    x_out[:half] = to_x[:half] + far_low[...]
+    x_out[half:] = to_x[half:]
+    y_out[:half] = to_y[:half]
+    y_out[half:] = to_y[half:] + far_high[...]
 
 
 def row_from_column(column, size):
@@ -1106,17 +1180,17 @@
     return ((live_row > 0.5) & (doc == doc_row)) | same
 
 
-def quarter_mask(plane_at):
+def quarter_mask(quarter):
     lane = lax.broadcasted_iota(jnp.int32, (GROUP, SPAN), 1)
-    first = (plane_at % 2) * HEAD_DIM
+    first = (quarter % 2) * HEAD_DIM
     return (lane >= first) & (lane < first + 3 * HEAD_DIM)
 
 
-def plane_piece(vectors, row, plane_at):
+def quarter_piece(vectors, row, quarter):
     value = jnp.zeros((1, SPAN), WIDE)
-    for at in range(PLANE):
+    for at in range(LINE):
         first = TILE_START[at] * LANES
-        value = jnp.where(plane_at == at, vectors[row : row + 1, first : first + SPAN], value)
+        value = jnp.where(quarter == at, vectors[row : row + 1, first : first + SPAN], value)
     return value
 
 
@@ -1124,20 +1198,20 @@
     stacks, vectors, weight, out_weight = refs[:4], refs[4], refs[5], refs[6]
     heads_out, qkv_out, mixed_out, part_out = refs[7:]
     line_at, plane_at = where[0], where[1]
-    for mask, stack in enumerate(stacks):
-        for step in range(LINE):
+    for step, stack in enumerate(stacks):
+        for mask in range(PLANE):
             row = (line_at + LINE - step) % LINE * PLANE + (plane_at ^ mask)
-            heads_out[pl.ds(row, 1), :] = stack[step : step + 1, :]
+            heads_out[pl.ds(row, 1), :] = stack[mask : mask + 1, :]
     heads = heads_out[...]
     inputs = heads[:, :MODEL].astype(LOW)
     projected = product_plain(inputs, weight[:, : 3 * SPAN])
-    query = projected[:, :SPAN] + plane_piece(vectors, 12, plane_at)
-    value = projected[:, 2 * SPAN :] + plane_piece(vectors, 13, plane_at)
+    query = projected[:, :SPAN] + quarter_piece(vectors, 12, line_at)
+    value = projected[:, 2 * SPAN :] + quarter_piece(vectors, 13, line_at)
     qkv_out[:, :SPAN] = query.astype(LOW)
     qkv_out[:, SPAN : 2 * SPAN] = projected[:, SPAN : 2 * SPAN].astype(LOW)
     qkv_out[:, 2 * SPAN :] = value.astype(LOW)
     mixed = attend_tiles(qkv_out[...], SPAN, head_allowed(heads))
-    mixed = masked(jnp.concatenate(mixed, axis=1), quarter_mask(plane_at))
+    mixed = masked(jnp.concatenate(mixed, axis=1), quarter_mask(line_at))
     mixed_out[...] = mixed
     part_out[...] = product_plain(mixed, out_weight[...])
 
@@ -1145,16 +1219,16 @@
 def cls_mlp_kernel(where, *refs):
     heads, own, got_one, got_two, got_three, vectors, weight = refs[:7]
     normed_out, inv_out, low_out, act_out, slope_out, part_out = refs[7:]
-    plane_at = where[1]
+    line_at = where[0]
     branch = own[...] + got_one[...] + got_two[...] + got_three[...]
     normed, inv_dev = norm_rows(heads[:, :MODEL] + branch + vectors[14:15, :])
     normed_out[...] = normed
     inv_out[...] = inv_dev
     low = (normed * vectors[16:17, :] + vectors[17:18, :]).astype(LOW)
     low_out[...] = low
-    part = FF // PLANE
+    part = FF // LINE
     first = 3 * SPAN
-    bias = vectors[pl.ds(20 + plane_at, 1), :]
+    bias = vectors[pl.ds(20 + line_at, 1), :]
     before = product_plain(low, weight[:, first : first + part]) + bias
     value, slope = gelu_both(before)
     act = value.astype(LOW)
@@ -1188,7 +1262,7 @@
     grad_out[...] = grad
     second = grad.astype(LOW)
     second_out[...] = second
-    part = FF // PLANE
+    part = FF // LINE
     at = 3 * SPAN
     pre = (product_plain(second, weight[:, at + part :]) * slope[...]).astype(LOW)
     pre_out[...] = pre
@@ -1199,7 +1273,7 @@
     heads, own, got_one, got_two, got_three, vectors, weight, out_weight = refs[:8]
     grad_in, normed_first, inv_first, qkv = refs[8:12]
     grad_out, branch_out, proj_out, part_out, sums_out = refs[12:]
-    plane_at = where[1]
+    line_at = where[0]
     grad_first = grad_in[...] + own[...] + got_one[...] + got_two[...] + got_three[...]
     normed = normed_first[...]
     grad = norm_rows_back(grad_first, normed, inv_first[...], vectors[16:17, :])
@@ -1208,7 +1282,7 @@
     grad_out[...] = grad
     branch = grad.astype(LOW)
     branch_out[...] = branch
-    mask = quarter_mask(plane_at)
+    mask = quarter_mask(line_at)
     mixed_grad = masked(product_right(branch, out_weight[...]).astype(LOW), mask)
     pieces = attend_tiles_back(qkv[...], mixed_grad, SPAN, head_allowed(heads[...]))
     tiles = SPAN // LANES
@@ -1221,11 +1295,16 @@
 def cls_end_kernel(where, *refs):
     heads, grad, own, got_one, got_two, got_three = refs[:6]
     square, sums_back, sums_top = refs[6:9]
-    row_out, shared_out, held = refs[9:]
+    normed_second, inv_second, vectors = refs[9:12]
+    row_out, second_out, shared_out, held = refs[12:]
     rank = where[0] * PLANE + where[1]
     total = grad[...] + own[...] + got_one[...] + got_two[...] + got_three[...]
     held[...] = total
-    row_out[...] = held[pl.ds(rank, 1), :]
+    row = held[pl.ds(rank, 1), :]
+    row_out[...] = row
+    second_out[...] = norm_rows_back(
+        row, normed_second[0:1, :], inv_second[0:1, :], vectors[6:7, :]
+    )
     number = row_from_column(heads[:, 2 * MODEL + 2 : 2 * MODEL + 3], GROUP)
     entry = lax.broadcasted_iota(jnp.int32, (GROUP, GROUP), 0).astype(WIDE)
     hot = (entry == number).astype(WIDE)
@@ -1239,9 +1318,11 @@
     packs = refs[:4]
     heads, branch, low, second = refs[4:8]
     out, kept = refs[8:]
-    plane_at = where[1]
-    for mask, pack in enumerate(packs):
-        kept[plane_at ^ mask] = pack[...]
+    line_at = where[0]
+    rows, width = kept.shape[1:]
+    for step, pack in enumerate(packs):
+        first = pack.shape[0] - rows
+        kept[(line_at + LINE - step) % LINE] = pack[first:, :width]
     starts = (MODEL, 2 * MODEL, 3 * MODEL, 4 * MODEL)
     out[:, 0:MODEL] = heads[:, :MODEL].astype(LOW)
     for piece, start in enumerate(starts):
@@ -1258,7 +1339,7 @@
     out[:, 5 * MODEL : 6 * MODEL] = branch[...]
     out[:, 6 * MODEL : 7 * MODEL] = low[...]
     out[:, 7 * MODEL + FF : 8 * MODEL + FF] = second[...]
-    part = FF // PLANE
+    part = FF // LINE
     for at in range(PLANE):
         first = 4 * SPAN
         out[:, 7 * MODEL + at * part : 7 * MODEL + (at + 1) * part] = kept[
@@ -1300,52 +1381,57 @@
         vecs_out[8 + at : 9 + at, :] = column_sum(rows[:, start : start + MODEL])
 
 
-def seg_owner_kernel(where, *refs):
-    attn, attn_got, mlp, mlp_got = refs[:4]
-    own_rows, got_rows = refs[4:6]
-    mats_out, vecs_out, rows = refs[6:]
+def head_share_kernel(where, *refs):
+    packs, mlp = refs[:4], refs[4]
+    mine_out, vecs_out, rows = refs[5:]
+    rank = where[0] * PLANE + where[1]
+    count = LINE * 24
+    for at, pack in enumerate(packs):
+        rows[at * count : (at + 1) * count] = pack[...]
+    total = PLANE * count
+
+    def chosen(base, apart):
+        shape = (CORES * GROUP, total)
+        row = lax.broadcasted_iota(jnp.int32, shape, 0)
+        column = lax.broadcasted_iota(jnp.int32, shape, 1)
+        hot = (column == row // 2 * 24 + base + row % 2 * apart).astype(LOW)
+        return product_plain(hot, rows[...]).astype(LOW)
+
+    own = own_features(rank, OWN)
+    for at, (left, right) in enumerate(((0, 4), (2, 8))):
+        side = product_plain(chosen(left, 1), own).astype(LOW)
+        for piece in range(FF_HALF // MODEL):
+            columns = slice(at * FF_HALF + piece * MODEL, at * FF_HALF + (piece + 1) * MODEL)
+            share = product_left(side, chosen(right + 2 * piece, 1))
+            mine_out[:, columns] = mlp[:, columns] + share
+    shape = (16, total)
+    row = lax.broadcasted_iota(jnp.int32, shape, 0)
+    column = lax.broadcasted_iota(jnp.int32, shape, 1)
+    hot = ((column % 24 == row + 12) & (row < 12)).astype(LOW)
+    vecs_out[...] = product_plain(hot, rows[...])
+
+
+def seg_owner_kernel(where, attn, attn_got, mlp, mlp_got, mats_out):
     core_at = where[2]
-    rank = where[0] * PLANE + where[1]
-    width = mats_out.shape[0]
-    rows[:GROUP] = own_rows[...]
-    rows[GROUP:] = got_rows[...]
-    chosen = own_features(rank, width)
-    qkv_half, out_half, half = 3 * MODEL // CORES, MODEL // CORES, FF // CORES
-    own_at, got_at = core_at, 1 - core_at
 
     def put(base, size, own, got):
-        mats_out[:, pl.ds(pl.multiple_of(base + own_at * size, LANES), size)] = own
-        mats_out[:, pl.ds(pl.multiple_of(base + got_at * size, LANES), size)] = got
-
-    put(0, qkv_half, attn[:, :qkv_half], attn_got[:, :qkv_half])
-    put(3 * MODEL, out_half, attn[:, qkv_half:], attn_got[:, qkv_half:])
-    put(4 * MODEL, half, mlp[:, :half], mlp_got[:, :half])
-    put(4 * MODEL + FF, half, mlp[:, half:], mlp_got[:, half:])
-    for left, right, target in (
-        (0, 2 * MODEL, 4 * MODEL),
-        (MODEL, 2 * MODEL + FF, 4 * MODEL + FF),
-    ):
-        side = product_plain(rows[:, left : left + MODEL], chosen).astype(LOW)
-        mats_out[:, target : target + FF] = mats_out[:, target : target + FF] + product_left(
-            side, rows[:, right : right + FF]
-        )
-    base = 2 * MODEL + 2 * FF
-    for at in range(8 + FF // MODEL):
-        start = base + at * MODEL
-        vecs_out[at : at + 1, :] = column_sum(rows[:, start : start + MODEL])
+        mats_out[:, pl.ds(aligned(base + core_at * size), size)] = own
+        mats_out[:, pl.ds(aligned(base + (1 - core_at) * size), size)] = got
+
+    for piece in range(4):
+        columns = slice(piece * HALF, (piece + 1) * HALF)
+        put(piece * MODEL, HALF, attn[:, columns], attn_got[:, columns])
+    for piece in range(2):
+        columns = slice(piece * FF_HALF, (piece + 1) * FF_HALF)
+        put(4 * MODEL + piece * FF, FF_HALF, mlp[:, columns], mlp_got[:, columns])
 
 
 def plane_parts(part):
     return (part,) + tuple(in_plane(part, mask) for mask in range(1, PLANE))
 
 
-def weight_blocks(piece):
-    line = jnp.stack([piece] + [along_line(piece, apart) for apart in range(1, LINE)])
-    half = LINE // 2
-    from_x, from_y = in_plane(line, 1), in_plane(line, 2)
-    far_low, far_high = in_plane(from_x[:half], 2), in_plane(from_y[half:], 1)
-    own = (line, from_x, from_y, far_low, far_high)
-    return own + tuple(other_core(block) for block in own)
+def line_parts(part):
+    return (part,) + tuple(along_line(part, apart) for apart in range(1, LINE))
 
 
 def slice_local(
@@ -1364,111 +1450,241 @@
     line_at, plane_at = rank // PLANE, rank % PLANE
     where = jnp.stack([line_at, plane_at, core_at, doc_ids[0], seg_nums[0]]).astype(jnp.int32)
     own_rows, total_columns = seg_mats.shape
-    half_rows = own_rows // CORES
     vec_size = seg_vecs.shape[0]
-    vec_lines = -(-vec_size // LANES)
     live = valid_flags.astype(WIDE)
     live_row, live_column = live[None, :], live[:, None]
-
-    pad = vec_lines * LANES - vec_size
-    vec_block = jnp.stack([jnp.pad(seg_vecs, (0, pad)), jnp.pad(cls_vecs, (0, pad))])
-    vec_block = vec_block.reshape(2 * vec_lines, LANES)
-    count_row = jnp.full((1, LANES), jnp.sum(live), WIDE).astype(LOW)
-    blank = jnp.zeros((half_rows - 2 * vec_lines - 1, LANES), LOW)
-    vec_block = jnp.concatenate([vec_block, count_row, blank])
-    qkv_columns, up_columns, down_columns = 3 * MODEL + LANES, MODEL + FF, FF + MODEL
-    quarter = 3 * SPAN + 2 * FF // PLANE
-    first_piece, second_piece, third_piece, quarters = run_kernel(
-        prepare_kernel,
-        "prepare",
+    both_rows = CORES * SEG
+    first_columns = 4 * HALF + LANES
+
+    first_piece = run_kernel(
+        prepare_first_kernel,
+        "prepare_first",
+        [shape_of((own_rows, first_columns), LOW)],
+        where,
+        (seg_mats,),
+        (seg_vecs[None], cls_vecs[None], live_row),
+        [pltpu.SemaphoreType.DMA((4,))],
+    )[0]
+    first_line = line_parts(first_piece)
+    rest = run_kernel(
+        prepare_rest_kernel,
+        "prepare_rest",
+        [shape_of((own_rows, FF_HALF), LOW)] * 2
+        + [shape_of((own_rows, QUARTER_HALF), LOW)] * LINE
+        + [shape_of((own_rows, HALF), LOW)],
+        where,
+        (seg_mats, cls_mats),
+        (),
         [
-            shape_of((half_rows, qkv_columns), LOW),
-            shape_of((half_rows, up_columns), LOW),
-            shape_of((half_rows, down_columns), LOW),
-            shape_of((PLANE, half_rows, quarter), LOW),
+            pltpu.VMEM((LINE, own_rows, QUARTER), LOW),
+            pltpu.SemaphoreType.DMA((3 + 5 * LINE,)),
         ],
-        where,
-        (),
-        (
-            seg_mats.reshape(CORES, half_rows, total_columns),
-            cls_mats.reshape(CORES, half_rows, total_columns),
-            vec_block,
-        ),
-        [pltpu.VMEM((PLANE, half_rows, quarter), LOW)],
-    )
-    qkv_blocks = weight_blocks(first_piece)
-    up_blocks = weight_blocks(second_piece)
-    down_blocks = weight_blocks(third_piece)
-    own_plane = jnp.stack(
-        [quarters[0]] + [in_plane(quarters[mask], mask) for mask in range(1, PLANE)]
-    )
-    cls_line = (own_plane,) + tuple(along_line(own_plane, apart) for apart in range(1, LINE))
-    cls_line = cls_line + tuple(other_core(block) for block in cls_line)
-
-    qkv, both, vectors, count = run_kernel(
+    )
+    second_piece, third_piece, quarters, cls_out_piece = rest[0], rest[1], rest[2:-1], rest[-1]
+
+    def joined(*pieces):
+        return jnp.concatenate(pieces, axis=1)
+
+    def sent_both(to_x, to_y):
+        return in_plane(to_x, 1), in_plane(to_y, 2)
+
+    first_sent = joined(*first_line)
+    first_x, first_y = sent_both(first_sent, first_sent)
+    second_line = line_parts(after(second_piece, *first_line[1:]))
+    size = 2 * first_columns
+    second_x, second_y = sent_both(
+        joined(first_y[:, size:], *second_line), joined(first_x[:, :size], *second_line)
+    )
+    third_line = line_parts(after(third_piece, first_x, first_y, *second_line[1:]))
+    start, size = size, 2 * FF_HALF
+    third_x, third_y = sent_both(
+        joined(second_y[:, start + size :], *third_line),
+        joined(second_x[:, start : start + size], *third_line),
+    )
+    cls_line = (quarters[0],) + tuple(
+        along_line(after(quarters[apart], second_x, second_y, *third_line[1:]), apart)
+        for apart in range(1, LINE)
+    )
+
+    hidden_got, live_got = other_core(hidden_in), other_core(live_row)
+    qkv_weight, out_half, qkv, mixed, vectors, count = run_kernel(
         qkv_kernel,
         "seg_qkv",
         [
-            shape_of((SEG, 3 * MODEL), LOW),
-            shape_of((SEG, 2 * MODEL), LOW),
+            shape_of((GROUP, own_rows, 3 * HALF), LOW),
+            shape_of((GROUP, own_rows, HALF), LOW),
+            shape_of((both_rows, 3 * HALF), LOW),
+            shape_of((both_rows, HALF), LOW),
             shape_of((2 * (8 * MODEL + FF) // MODEL, MODEL)),
             shape_of((8, LANES)),
         ],
         where,
-        qkv_blocks,
-        (hidden_in, live_row),
-        weight_scratch(half_rows, qkv_columns) + [pltpu.VMEM((2, 8 * MODEL + FF), WIDE)],
+        (),
+        first_line
+        + (first_x, first_y, second_x, second_y)
+        + (hidden_in, hidden_got, live_row, live_got),
+        [
+            pltpu.VMEM((GROUP, own_rows, LANES), LOW),
+            pltpu.VMEM((2, 8 * MODEL + FF), WIDE),
+            pltpu.VMEM((both_rows, MODEL), LOW),
+        ],
         flops=2 * SEG * MODEL * 3 * MODEL,
     )
-    both_got = other_core(both)
-    normed_first, inv_first, slope, act, first_send = run_kernel(
+    count = count + other_core(count)
+    out_half = out_half.reshape(MODEL, HALF)
+    out_weight, mixed_full, normed_first, inv_first, first_low = run_kernel(
+        out_kernel,
+        "seg_out",
+        [
+            shape_of((MODEL, MODEL), LOW),
+            shape_of((both_rows, MODEL), LOW),
+            shape_of((SEG, MODEL)),
+            shape_of((SEG, 1)),
+            shape_of((SEG, MODEL), LOW),
+        ],
+        where,
+        (),
+        (hidden_in, mixed, other_core(mixed), out_half, other_core(out_half), vectors),
+        flops=2 * SEG * MODEL * MODEL,
+    )
+    first_got = other_core(first_low)
+    third_x, third_y = after(third_x, first_low), after(third_y, first_low)
+    up_weight, act, slope = run_kernel(
         up_kernel,
         "seg_up",
         [
-            shape_of((SEG, MODEL)),
-            shape_of((SEG, 1)),
-            shape_of((SEG, FF)),
-            shape_of((SEG, FF), LOW),
-            shape_of((SEG, MODEL + FF // CORES), LOW),
+            shape_of((GROUP, own_rows, FF_HALF), LOW),
+            shape_of((both_rows, FF_HALF), LOW),
+            shape_of((both_rows, FF_HALF)),
         ],
         where,
-        up_blocks,
-        (hidden_in, both, vectors),
-        weight_scratch(half_rows, up_columns),
-        flops=2 * SEG * MODEL * up_columns,
-    )
-    first_got = other_core(first_send)
-    normed_second, inv_second, diff, out_rows, head_row, cls_out = run_kernel(
+        (),
+        second_line
+        + (second_x, second_y, third_x, third_y)
+        + (first_low, first_got, vectors),
+        [pltpu.VMEM((both_rows, MODEL), LOW)],
+        flops=2 * SEG * MODEL * FF,
+    )
+    fourth_x, fourth_y = sent_both(third_y[:, 2 * size :], third_x[:, size : 2 * size])
+    fourth_x, fourth_y = after(fourth_x, act), after(fourth_y, act)
+    cls_sent = joined(*cls_line, cls_out_piece)
+    cls_sent = after(cls_sent, fourth_x, fourth_y)
+    cls_x, cls_y = sent_both(cls_sent, cls_sent)
+    down_weight, down_own, down_send = run_kernel(
         down_kernel,
         "seg_down",
+        [
+            shape_of((GROUP, own_rows, FF_HALF), LOW),
+            shape_of((SEG, MODEL)),
+            shape_of((SEG, MODEL)),
+        ],
+        where,
+        (),
+        third_line + (third_x, third_y, fourth_x, fourth_y) + (act,),
+        flops=2 * SEG * MODEL * FF,
+    )
+    normed_second, inv_second, diff, out_rows, head_row = run_kernel(
+        seg_rows_kernel,
+        "seg_rows",
         [
             shape_of((SEG, MODEL)),
             shape_of((SEG, 1)),
             shape_of((SEG, MODEL)),
             shape_of((SEG, MODEL)),
             shape_of((1, 2 * MODEL + LANES)),
+        ],
+        where,
+        (),
+        (
+            down_own,
+            other_core(down_send),
+            normed_first,
+            vectors,
+            targets,
+            live_column,
+            seg_pos,
+        ),
+    )
+    head_planes = plane_parts(head_row)
+    size = LINE // 2 * QUARTER_HALF
+    cls_far = sent_both(
+        after(cls_y[:, size:], *head_planes[1:]), after(cls_x[:, :size], *head_planes[1:])
+    )
+
+    second_grad, second_low, second_sums = run_kernel(
+        second_norm_kernel,
+        "seg_second_norm",
+        [shape_of((SEG, MODEL)), shape_of((SEG, MODEL), LOW), shape_of((3, MODEL))],
+        where,
+        (),
+        (diff, count, normed_second, inv_second, vectors),
+    )
+    second_got = after(other_core(second_low), head_planes[1])
+    pre, first_grad_own, first_grad_send, up_sums = run_kernel(
+        mlp_back_kernel,
+        "seg_mlp_back",
+        [
+            shape_of((both_rows, FF_HALF), LOW),
+            shape_of((SEG, MODEL)),
+            shape_of((SEG, MODEL)),
+            shape_of((FF_HALF // MODEL, MODEL)),
+        ],
+        where,
+        (),
+        (second_low, second_got, down_weight, up_weight, slope),
+        [pltpu.VMEM((both_rows, MODEL), LOW)],
+        flops=4 * SEG * MODEL * FF,
+    )
+    head_stack = jnp.concatenate([head_planes[0]] + [after(got, pre) for got in head_planes[1:]])
+    head_lines = line_parts(head_stack)
+    cls_half, cls_out_half = run_kernel(
+        cls_gather_kernel,
+        "head_gather",
+        [
+            shape_of((GROUP, own_rows, QUARTER_HALF), LOW),
+            shape_of((PLANE, own_rows, HALF), LOW),
+        ],
+        where,
+        (),
+        cls_line + (cls_x, cls_y) + cls_far + (cls_out_piece,),
+    )
+    cls_weight, cls_out = run_kernel(
+        cls_weight_kernel,
+        "head_weight",
+        [
+            shape_of((GROUP, own_rows, QUARTER), LOW),
             shape_of((4, HEAD_DIM, MODEL), LOW),
         ],
         where,
-        down_blocks,
-        (act, normed_first, vectors, targets, live_column, seg_pos),
-        weight_scratch(half_rows, down_columns),
-        flops=2 * SEG * MODEL * FF,
-    )
+        (),
+        (cls_half, other_core(cls_half), cls_out_half, other_core(cls_out_half)),
+    )
+    cls_weight = cls_weight.reshape(MODEL, QUARTER)
     cls_out = cls_out.reshape(SPAN, MODEL)
-    cls_weight = run_kernel(
-        cls_weight_kernel,
-        "head_weight",
-        [shape_of((LINE, PLANE, CORES, half_rows, quarter), LOW)],
-        where,
-        cls_line,
-        (),
-        [pltpu.SemaphoreType.DMA((WEIGHT_COPIES,))],
-    )[0].reshape(MODEL, quarter)
-
-    head_stack = jnp.concatenate(
-        [head_row] + [along_line(head_row, apart) for apart in range(1, LINE)]
-    )
+    first_grad_got = other_core(first_grad_send)
+
+    def part_shapes(columns):
+        return [
+            shape_of((count_of, own_rows, columns), LOW)
+            for count_of in (LINE // 2, LINE // 2, LINE, LINE, LINE)
+        ]
+
+    mlp_parts = run_kernel(
+        mlp_weight_kernel,
+        "seg_mlp_weight",
+        part_shapes(FF),
+        where,
+        (),
+        (first_low, first_got, second_low, second_got, after(pre, head_lines[1]), act),
+        [
+            pltpu.VMEM((both_rows, MODEL), LOW),
+            pltpu.VMEM((GROUP, own_rows, FF), LOW),
+            pltpu.SemaphoreType.DMA((GROUP,)),
+        ],
+        outs_far=True,
+        flops=4 * SEG * MODEL * FF,
+    )
+    mlp_far = reduce_far(tuple(after(part, *cls_far) for part in mlp_parts[:2]))
     heads, cls_qkv, cls_mixed, part = run_kernel(
         cls_attend_kernel,
         "head_attend",
@@ -1480,50 +1696,9 @@
         ],
         where,
         (),
-        plane_parts(head_stack) + (vectors, cls_weight, cls_out),
-    )
-    grad_first, pre, second_send, sums = run_kernel(
-        mlp_back_kernel,
-        "seg_mlp_back",
-        [
-            shape_of((SEG, MODEL)),
-            shape_of((SEG, FF), LOW),
-            shape_of((SEG, MODEL + FF // CORES), LOW),
-            shape_of((2, FF)),
-        ],
-        where,
-        up_blocks + down_blocks,
-        (diff, count, normed_second, inv_second, vectors, slope),
-        weight_scratch(half_rows, up_columns) + weight_scratch(half_rows, down_columns),
-        flops=4 * SEG * MODEL * FF,
-    )
-    second_got = other_core(second_send)
-    part_rows = LINE // 2
-
-    def part_shapes(columns):
-        return [
-            shape_of((count_of, own_rows, columns), LOW)
-            for count_of in (part_rows, part_rows, LINE, LINE, LINE)
-        ]
-
-    mlp_parts = run_kernel(
-        mlp_weight_kernel,
-        "seg_mlp_weight",
-        part_shapes(FF),
-        where,
-        (),
-        (first_send, first_got, second_send, second_got, pre, act),
-        [
-            pltpu.VMEM((2 * SEG, MODEL), LOW),
-            pltpu.VMEM((2 * SEG, FF // CORES), LOW),
-            pltpu.VMEM((GROUP, own_rows, FF), LOW),
-            pltpu.SemaphoreType.DMA((GROUP,)),
-        ],
-        outs_far=True,
-        flops=4 * SEG * MODEL * FF,
-    )
-    mlp_sum = reduce_parts(where, mlp_parts)
-
+        tuple(after(got, mlp_parts[0], first_grad_got) for got in head_lines)
+        + (vectors, cls_weight, cls_out),
+    )
     cls_normed, cls_inv, cls_low, cls_act, cls_slope, part = run_kernel(
         cls_mlp_kernel,
         "head_mlp",
@@ -1531,14 +1706,18 @@
             shape_of((GROUP, MODEL)),
             shape_of((GROUP, 1)),
             shape_of((GROUP, MODEL), LOW),
-            shape_of((GROUP, FF // PLANE), LOW),
-            shape_of((GROUP, FF // PLANE)),
+            shape_of((GROUP, FF // LINE), LOW),
+            shape_of((GROUP, FF // LINE)),
             shape_of((GROUP, MODEL)),
         ],
         where,
         (),
-        (heads,) + plane_parts(part) + (vectors, cls_weight),
-    )
+        (heads,) + line_parts(part) + (vectors, cls_weight),
+    )
+    cls_parts = line_parts(part)
+    mlp_far = tuple(after(got, cls_low) for got in mlp_far)
+    mlp_sent = reduce_add(where, mlp_parts, mlp_far)
+    mlp_plane = sent_both(*mlp_sent)
     top_row, square, cls_grad, cls_second, cls_pre, part, top_sums = run_kernel(
         cls_top_kernel,
         "head_top",
@@ -1547,13 +1726,15 @@
             shape_of((8, LANES)),
             shape_of((GROUP, MODEL)),
             shape_of((GROUP, MODEL), LOW),
-            shape_of((GROUP, FF // PLANE), LOW),
+            shape_of((GROUP, FF // LINE), LOW),
             shape_of((GROUP, MODEL)),
             shape_of((2, MODEL)),
         ],
         where,
         (),
-        (heads,) + plane_parts(part) + (vectors, cls_weight, cls_normed, count, cls_slope),
+        (heads, cls_parts[0], cls_parts[1])
+        + tuple(after(got, *mlp_sent) for got in cls_parts[2:])
+        + (vectors, cls_weight, cls_normed, count, cls_slope),
         [pltpu.VMEM((GROUP, MODEL), WIDE)],
     )
     cls_grad, cls_branch, cls_proj, part, back_sums = run_kernel(
@@ -1569,85 +1750,153 @@
         where,
         (),
         (heads,)
-        + plane_parts(part)
+        + line_parts(part)
         + (vectors, cls_weight, cls_out, cls_grad, cls_normed, cls_inv, cls_qkv),
     )
-    dheads, shared = run_kernel(
+    dheads, head_grad, shared = run_kernel(
         cls_end_kernel,
         "head_end",
-        [shape_of((1, MODEL)), shape_of((GROUP + 8, MODEL))],
-        where,
-        (),
-        (heads, cls_grad) + plane_parts(part) + (square, back_sums, top_sums),
+        [shape_of((1, MODEL)), shape_of((1, MODEL)), shape_of((GROUP + 8, MODEL))],
+        where,
+        (),
+        (heads, cls_grad)
+        + line_parts(part)
+        + (square, back_sums, top_sums, normed_second, inv_second, vectors),
         [pltpu.VMEM((GROUP, MODEL), WIDE)],
     )
 
-    head_width = 2 * MODEL + 2 * FF + 8 * MODEL + FF
-    input_grad, proj, branch, attn_send, head_data, output = run_kernel(
-        seg_back_kernel,
-        "seg_back",
+    head_own, head_send, head_data = run_kernel(
+        head_back_kernel,
+        "seg_head_back",
+        [shape_of((1, MODEL)), shape_of((1, MODEL)), shape_of((12, MODEL))],
+        where,
+        (),
+        (
+            head_grad,
+            other_core(head_grad),
+            down_weight,
+            up_weight,
+            slope,
+            act,
+            first_low,
+            first_got,
+        ),
+    )
+    grad_summed, branch, mixed_grad, attn_send, first_sums = run_kernel(
+        first_norm_kernel,
+        "seg_first_norm",
         [
+            shape_of((SEG, MODEL)),
             shape_of((SEG, MODEL), LOW),
-            shape_of((SEG, 3 * MODEL), LOW),
             shape_of((SEG, MODEL), LOW),
-            shape_of((SEG, 2 * MODEL), LOW),
-            shape_of((1, head_width), LOW),
             shape_of((SEG, MODEL), LOW),
+            shape_of((3, MODEL)),
         ],
         where,
-        qkv_blocks + up_blocks + down_blocks,
+        (),
         (
-            dheads,
-            top_row,
-            grad_first,
-            normed_second,
-            inv_second,
-            slope,
+            second_grad,
+            first_grad_own,
+            first_grad_got,
+            head_grad,
+            head_own,
+            other_core(head_send),
             normed_first,
             inv_first,
-            first_send,
-            act,
+            vectors,
+            out_weight,
+        ),
+    )
+    pack = jnp.concatenate([cls_proj, cls_mixed, cls_pre, cls_act], axis=1)
+    mlp_plane = [after(got, branch) for got in mlp_plane]
+    mlp_own, *mlp_sent = reduce_fold(where, mlp_parts[4], mlp_plane, pack)
+    mlp_got = [along_line(mlp_sent[apart - 1], apart) for apart in range(1, LINE)]
+    shared = shared + other_core(shared)
+    attn_got = after(other_core(attn_send), mlp_own, shared)
+    proj, input_own, input_send, payload = run_kernel(
+        attn_back_kernel,
+        "seg_attn_back",
+        [
+            shape_of((both_rows, 3 * HALF), LOW),
+            shape_of((SEG, MODEL)),
+            shape_of((SEG, MODEL)),
+            shape_of((24, MODEL), LOW),
+        ],
+        where,
+        (),
+        (
             qkv,
-            vectors,
+            mixed_grad,
+            attn_got,
             live_row,
-            sums,
-            out_rows,
+            live_got,
+            qkv_weight,
+            first_sums,
+            second_sums,
+            up_sums,
+            dheads,
+            normed_second,
+            head_data,
         ),
-        weight_scratch(half_rows, qkv_columns)
-        + weight_scratch(half_rows, up_columns)
-        + weight_scratch(half_rows, down_columns)
-        + [pltpu.VMEM((SEG, MODEL), LOW)],
-        flops=4 * SEG * MODEL * 4 * MODEL,
-    )
-    attn_got = other_core(attn_send)
+        [pltpu.VMEM((24, MODEL), WIDE)],
+        flops=4 * SEG * MODEL * 3 * MODEL,
+    )
     attn_parts = run_kernel(
         attn_weight_kernel,
         "seg_attn_weight",
-        part_shapes(2 * MODEL),
-        where,
-        (),
-        (both, both_got, proj, attn_got, branch),
+        part_shapes(4 * HALF),
+        where,
+        (),
+        (hidden_in, hidden_got, mixed_full, proj, branch, attn_got),
         [
-            pltpu.VMEM((2 * SEG, 2 * MODEL), LOW),
-            pltpu.VMEM((2 * SEG, 2 * MODEL), LOW),
-            pltpu.VMEM((GROUP, own_rows, 2 * MODEL), LOW),
+            pltpu.VMEM((both_rows, MODEL), LOW),
+            pltpu.VMEM((both_rows, HALF), LOW),
+            pltpu.VMEM((GROUP, own_rows, 4 * HALF), LOW),
             pltpu.SemaphoreType.DMA((GROUP,)),
         ],
         outs_far=True,
         flops=4 * SEG * MODEL * 2 * MODEL,
     )
-    attn_sum = reduce_parts(where, attn_parts)
-
-    pack = jnp.concatenate([cls_proj, cls_mixed, cls_pre, cls_act], axis=1)
-    row_width = 6 * MODEL + 2 * MODEL + 2 * FF
+    attn_far = reduce_far(tuple(after(part, mlp_got[-1]) for part in attn_parts[:2]))
+    input_grad = (grad_summed + input_own + other_core(input_send)).astype(LOW)
+    row_at = jnp.arange(SEG)[:, None]
+    output = jnp.where(row_at == 0, top_row * live_row[:, :1], out_rows).astype(LOW)
+    attn_sent = reduce_add(where, attn_parts, attn_far)
+    attn_plane = sent_both(*(after(part, mlp_got[1]) for part in attn_sent))
+    mlp_got = [after(got, attn_plane[0]) for got in mlp_got]
+    mlp_sum = reduce_line(mlp_own, mlp_got)
+    payload_line = jnp.concatenate(line_parts(after(payload, *attn_plane)))
+    mlp_mine, own_vecs = run_kernel(
+        head_share_kernel,
+        "seg_head_share",
+        [shape_of((own_rows, FF)), shape_of((16, MODEL))],
+        where,
+        (),
+        plane_parts(payload_line) + (mlp_sum,),
+        [pltpu.VMEM((GROUP * 24, MODEL), LOW)],
+    )
+    attn_own, *attn_sent = reduce_fold(where, attn_parts[4], attn_plane)
+    attn_sum = reduce_line(
+        attn_own, [along_line(attn_sent[apart - 1], apart) for apart in range(1, LINE)]
+    )
+    seg_mats_grad = run_kernel(
+        seg_owner_kernel,
+        "seg_owner",
+        [shape_of((own_rows, total_columns))],
+        where,
+        (),
+        (attn_sum, other_core(attn_sum), mlp_mine, other_core(mlp_mine)),
+    )[0]
+
+    row_width = 8 * MODEL + 2 * FF
     cls_rows = run_kernel(
         cls_rows_kernel,
         "head_rows",
         [shape_of((GROUP, row_width), LOW)],
         where,
         (),
-        plane_parts(pack) + (heads, cls_branch, cls_low, cls_second),
-        [pltpu.VMEM((PLANE,) + pack.shape, LOW)],
+        (pack,) + tuple(mlp_got) + (heads, cls_branch, cls_low, cls_second),
+        [pltpu.VMEM((LINE,) + pack.shape, LOW)],
     )[0]
     vec_rows = (8 * MODEL + FF) // MODEL
     cls_mats_grad, cls_vec_rows = run_kernel(
@@ -1660,27 +1909,12 @@
         [pltpu.VMEM((CORES * GROUP, row_width), LOW)],
         flops=64 * own_rows * total_columns,
     )
-    shared = shared + other_core(shared)
     pos_total = shared[:GROUP]
     loss_value = shared[GROUP, 0] / (count[0, 0] * MODEL)
-    norm_grads = shared[GROUP + 1 : GROUP + 5]
-    cls_vec_rows = jnp.concatenate([cls_vec_rows[:4], norm_grads, cls_vec_rows[8:]])
-
-    head_line = jnp.concatenate(
-        [head_data] + [along_line(head_data, apart) for apart in range(1, LINE)]
-    )
-    head_all = jnp.concatenate(plane_parts(head_line))
-    seg_mats_grad, seg_vec_rows = run_kernel(
-        seg_owner_kernel,
-        "seg_owner",
-        [shape_of((own_rows, total_columns)), shape_of((vec_rows, MODEL))],
-        where,
-        (),
-        (attn_sum, other_core(attn_sum), mlp_sum, other_core(mlp_sum))
-        + (head_all, other_core(head_all)),
-        [pltpu.VMEM((CORES * GROUP, head_width), LOW)],
-        flops=64 * own_rows * total_columns,
-    )
+    cls_vec_rows = jnp.concatenate(
+        [cls_vec_rows[:4], shared[GROUP + 1 : GROUP + 5], cls_vec_rows[8:]]
+    )
+    seg_vec_rows = (own_vecs + other_core(own_vecs))[:vec_rows]
 
     def own_vector(rows):
         return lax.dynamic_index_in_dim(rows.reshape(GROUP, vec_size), rank, 0, keepdims=False)

time: 417 us -> 290 us (0.70)
  waiting for transfers between devices: 181 us -> 97.4 us
  Pallas kernels: 81 us -> 52.2 us
  local copies, waits for them, and re-layouts: 38.6 us -> 23.5 us
  other arithmetic: 8.28 us -> 3.15 us
    ppermute x44 -> x26, waiting for transfers between devices: 117 us -> 49.1 us  [in_plane(): return lax.ppermute(value, 'fsdp', plane_pairs(mask))]
    pallas_call x19 -> x29, Pallas kernels: 81 us -> 52.2 us  [run_kernel(): pl.pallas_call(body, name=name, out_shape=tuple(outs), in_specs=in_specs,...]
    ppermute x24 -> x36, starting transfers between devices: 25.1 us -> 53 us  [along_line(): return lax.ppermute(value, 'fsdp', line_pairs(apart))]
    ppermute x24 -> x36, waiting for transfers between devices: 63.4 us -> 39.1 us  [along_line(): return lax.ppermute(value, 'fsdp', line_pairs(apart))]
    ppermute x44 -> x26, starting transfers between devices: 37.5 us -> 23 us  [in_plane(): return lax.ppermute(value, 'fsdp', plane_pairs(mask))]
    unnamed x149 -> x134, local copies, waits for them, and re-layouts: 26.6 us -> 15.6 us
    ppermute x28 -> x20, starting transfers between devices: 39.3 us -> 30.5 us  [other_core(): return lax.ppermute(value, 'rep', [(0, 1), (1, 0)])]
    ppermute x28 -> x20, waiting for transfers between devices: 0.57 us -> 9.23 us  [other_core(): return lax.ppermute(value, 'rep', [(0, 1), (1, 0)])]
  transfers between devices with their start and end apart: 96 -> 82, of which waited for: 34 -> 36; matrix products, arithmetic and copies ran while one was open for 4% -> 4% of each run, Pallas kernels for 19% -> 16%
where the time goes in v3:
time: 290 us; the launch traced here: 287 us
  starting transfers between devices  106 us (37%)
  waiting for transfers between devices  97.4 us (34%)
  Pallas kernels  52.2 us (18%)
  local copies, waits for them, and re-layouts  23.5 us (8%)
  between operations  4.63 us (2%)
  other arithmetic  3.15 us (1%)
    ppermute x36, starting transfers between devices, along_line(): return lax.ppermute(value, 'fsdp', line_pairs(apart))  53 us
    pallas_call x29, Pallas kernels, run_kernel(): pl.pallas_call(body, name=name, out_shape=tuple(outs), in_specs=in_specs,...  52.2 us
    ppermute x26, waiting for transfers between devices, in_plane(): return lax.ppermute(value, 'fsdp', plane_pairs(mask))  49.1 us
    ppermute x36, waiting for transfers between devices, along_line(): return lax.ppermute(value, 'fsdp', line_pairs(apart))  39.1 us
    ppermute x20, starting transfers between devices, other_core(): return lax.ppermute(value, 'rep', [(0, 1), (1, 0)])  30.5 us
    ppermute x26, starting transfers between devices, in_plane(): return lax.ppermute(value, 'fsdp', plane_pairs(mask))  23 us
    unnamed x134, local copies, waits for them, and re-layouts  15.6 us
    ppermute x20, waiting for transfers between devices, other_core(): return lax.ppermute(value, 'rep', [(0, 1), (1, 0)])  9.23 us
  transfers between devices with their start and end apart: 82, of which 36 were waited for; matrix products, arithmetic and copies ran while one was open for 4% of the time, Pallas kernels for 16%

profile of v3, /device:TPU:13, one launch (start us, length us, event | category | flops | bytes accessed | tf_op | source)
XLA Modules:
  0.0 287.4 jit_solution(15757580722508859776)
XLA Ops:
  6.2 2.3 collective-permute-start.1
  11.0 7.3 %collective-permute-done.1.refs_2_ = bf16[48,1664]{1,0:T(8,128)(2,1)S(1)} collective-permute-done((bf16[48,1664]{1,0:T(8,128)(2,1)S(1)}, bf16[48,1664]{1,0:T(8,128)(2,1)S(1)}, u32[]{:S(2)}, u32[]{:S(2)}) %collective-permute-start.1) | collective-permute-done | bytes 159776 | tf_op jit(solution)/shard_map/ppermute | solution.py:565
  18.3 3.6 %collective-permute-done.refs_1_ = bf16[48,1664]{1,0:T(8,128)(2,1)S(1)} collective-permute-done((bf16[48,1664]{1,0:T(8,128)(2,1)S(1)}, bf16[48,1664]{1,0:T(8,128)(2,1)S(1)}, u32[]{:S(2)}, u32[]{:S(2)}) %collective-permute-start) | collective-permute-done | bytes 159776 | tf_op jit(solution)/shard_map/ppermute | solution.py:565
  25.7 2.2 collective-permute-start.6
  27.9 8.6 %collective-permute-done.3.refs_4_ = bf16[48,6656]{1,0:T(8,128)(2,1)S(1)} collective-permute-done((bf16[48,6656]{1,0:T(8,128)(2,1)S(1)}, bf16[48,6656]{1,0:T(8,128)(2,1)S(1)}, u32[]{:S(2)}, u32[]{:S(2)}) %collective-permute-start.3) | collective-permute-done | bytes 639008 | tf_op jit(solution)/shard_map/ppermute | solution.py:569
  45.8 12.9 %collective-permute-done.13.refs_6_.refs_4_ = bf16[48,9472]{1,0:T(8,128)(2,1)S(1)} collective-permute-done((bf16[48,9472]{1,0:T(8,128)(2,1)S(1)}, bf16[48,9472]{1,0:T(8,128)(2,1)S(1)}, u32[]{:S(2)}, u32[]{:S(2)}) %collective-permute-start.13) | collective-permute-done | bytes 909344 | tf_op jit(solution)/shard_map/ppermute | solution.py:569
  63.1 2.3 collective-permute-start.18
  65.7 3.5 %collective-permute-start.15 = (f32[1,128]{1,0:T(1,128)S(1)}, f32[1,128]{1,0:T(1,128)S(1)}, u32[]{:S(2)}, u32[]{:S(2)}) collective-permute-start(f32[1,128]{1,0:T(1,128)S(1)} %get-tuple-element.309.live_row.refs_10_.refs_3_), channel_id=1, source_target_pairs={{0,16},{16,0},{1,17},{17,1},{2,18},{18,2},{3,19},{19,3},{4,20},{20... | collective-permute-start | bytes 1544 | tf_op jit(solution)/shard_map/ppermute | solution.py:573
  71.4 3.4 %seg_qkv.1 = (bf16[16,48,1152]{2,1,0:T(8,128)(2,1)S(1)}, bf16[16,48,384]{2,1,0:T(8,128)(2,1)S(1)}, bf16[256,1152]{1,0:T(8,128)(2,1)S(1)}, bf16[256,384]{1,0:T(8,...) custom-call(s32[5]{0:T(128)S(1)} %stack.15.where, bf16[48,1664]{1,0:T(8,128)(2,1)S(1)} %prepare_first.1.refs_0_, ...), custom_call_target="tpu_custom_call" | custom-call | flops 452984832 | bytes 7353344 | tf_op jit(solution)/shard_map/seg_qkv/pallas_call | solution.py:591
  80.5 6.6 %collective-permute-done.33.refs_2_ = bf16[48,1152]{1,0:T(8,128)(2,1)S(1)} collective-permute-done((bf16[48,1152]{1,0:T(8,128)(2,1)S(1)}, bf16[48,1152]{1,0:T(8,128)(2,1)S(1)}, u32[]{:S(2)}, u32[]{:S(2)}) %collective-permute-start.33) | collective-permute-done | bytes 110624 | tf_op jit(solution)/shard_map/ppermute | solution.py:565
  97.9 3.5 %collective-permute-done.21.refs_7_ = bf16[48,3072]{1,0:T(8,128)(2,1)S(1)} collective-permute-done((bf16[48,3072]{1,0:T(8,128)(2,1)S(1)}, bf16[48,3072]{1,0:T(8,128)(2,1)S(1)}, u32[]{:S(2)}, u32[]{:S(2)}) %collective-permute-start.21) | collective-permute-done | bytes 294944 | tf_op jit(solution)/shard_map/ppermute | solution.py:569
  102.0 2.3 seg_down.1
  122.2 3.8 %collective-permute-done.38.refs_7_ = bf16[48,2304]{1,0:T(8,128)(2,1)S(1)} collective-permute-done((bf16[48,2304]{1,0:T(8,128)(2,1)S(1)}, bf16[48,2304]{1,0:T(8,128)(2,1)S(1)}, u32[]{:S(2)}, u32[]{:S(2)}) %collective-permute-start.38) | collective-permute-done | bytes 221216 | tf_op jit(solution)/shard_map/ppermute | solution.py:569
  128.2 3.0 %collective-permute-start.39 = (bf16[16,48,1152]{2,1,0:T(8,128)(2,1)S(1)}, bf16[16,48,1152]{2,1,0:T(8,128)(2,1)S(1)}, u32[]{:S(2)}, u32[]{:S(2)}) collective-permute-start(bf16[16,48,1152]{2,1,0:T(8,128)(2,1)S(1)} %get-tuple-element.197.own), channel_id=1, source_target_pairs={{0,16},{16,0},{1,17},{17,1},{2,18},{18,2},{3,19},{19,3},{4,20},{20... | collective-permute-start | bytes 5308424 | tf_op jit(solution)/shard_map/ppermute | solution.py:573
  131.3 3.2 %collective-permute-done.24 = f32[8,128]{1,0:T(8,128)S(1)} collective-permute-done((f32[8,128]{1,0:T(8,128)S(1)}, f32[8,128]{1,0:T(8,128)S(1)}, u32[]{:S(2)}, u32[]{:S(2)}) %collective-permute-start.24) | collective-permute-done | bytes 4128 | tf_op jit(solution)/shard_map/ppermute | solution.py:573
  139.3 2.7 collective-permute-done.28.refs_1_
  142.0 3.1 %seg_mlp_weight.1 = (bf16[2,48,3072]{2,1,0:T(8,128)(2,1)S(1)}, bf16[2,48,3072]{2,1,0:T(8,128)(2,1)S(1)}, bf16[4,48,3072]{2,1,0:T(8,128)(2,1)S(1)}, bf16[4,48,307...) custom-call(s32[5]{0:T(128)S(1)} %stack.15.where, bf16[128,768]{1,0:T(8,128)(2,1)S(1)} %copy-done.13, ...), custom_call_target="tpu_custom_call" | custom-call | flops 1207959552 | bytes 7077888 | tf_op jit(solution)/shard_map/seg_mlp_weight/pallas_call | solution.py:591
  149.7 2.5 collective-permute-start.31
  154.0 4.4 %collective-permute-start.30 = (f32[4,1664]{1,0:T(4,128)S(1)}, f32[4,1664]{1,0:T(4,128)S(1)}, u32[]{:S(2)}, u32[]{:S(2)}) collective-permute-start(f32[4,1664]{1,0:T(4,128)S(1)} %pad_maximum_fusion.2.refs_0_), channel_id=1, source_target_pairs={{0,8},{1,9},{2,10},{3,11},{4,12},{5,13},{6,14},{7,15},{8,0},{9,1},... | collective-permute-start | bytes 79880 | tf_op jit(solution)/shard_map/ppermute | solution.py:565
  164.6 2.3 collective-permute-start.41
  185.6 2.3 head_attend_back.1
  194.8 6.7 %collective-permute-start.55 = (f32[1,768]{1,0:T(1,128)S(1)}, f32[1,768]{1,0:T(1,128)S(1)}, u32[]{:S(2)}, u32[]{:S(2)}) collective-permute-start(f32[1,768]{1,0:T(1,128)S(1)} %get-tuple-element.231.refs_0_.refs_3_), channel_id=1, source_target_pairs={{0,16},{16,0},{1,17},{17,1},{2,18},{18,2},{3,19},{19,3},{4,20},{20... | collective-permute-start | bytes 9224 | tf_op jit(solution)/shard_map/ppermute | solution.py:573
  212.7 4.4 %seg_attn_back.1 = (bf16[256,1152]{1,0:T(8,128)(2,1)S(1)}, f32[128,768]{1,0:T(8,128)S(1)}, f32[128,768]{1,0:T(8,128)S(1)}, bf16[24,768]{1,0:T(8,128)(2,1)S(1)}) custom-call(s32[5]{0:T(128)S(1)} %stack.15.where, bf16[256,1152]{1,0:T(8,128)(2,1)S(1)} %copy-done.51, bf16[128,768]{1,0:T(8,128)(2,1)S(1)} %get-tuple-element.238.refs_1_, ...), custom_call_target="tpu_custom_call" | custom-call | flops 905969664 | bytes 4624384 | tf_op jit(solution)/shard_map/seg_attn_back/pallas_call | solution.py:591
  217.2 4.8 %seg_attn_weight.1 = (bf16[2,48,1536]{2,1,0:T(8,128)(2,1)S(1)}, bf16[2,48,1536]{2,1,0:T(8,128)(2,1)S(1)}, bf16[4,48,1536]{2,1,0:T(8,128)(2,1)S(1)}, bf16[4,48,15...) custom-call(s32[5]{0:T(128)S(1)} %stack.15.where, bf16[128,768]{1,0:T(8,128)(2,1)S(1)} %copy-done.11, ...), custom_call_target="tpu_custom_call" | custom-call | flops 603979776 | bytes 4128768 | tf_op jit(solution)/shard_map/seg_attn_weight/pallas_call | solution.py:591
  224.5 5.5 %collective-permute-done.64.far_high = bf16[2,48,1536]{2,1,0:T(8,128)(2,1)S(1)} collective-permute-done((bf16[2,48,1536]{2,1,0:T(8,128)(2,1)S(1)}, bf16[2,48,1536]{2,1,0:T(8,128)(2,1)S(1)}, u32[]{:S(2)}, u32[]{:S(2)}) %collective-permute-start.64) | collective-permute-done | bytes 294944 | tf_op jit(solution)/shard_map/ppermute | solution.py:569
  232.6 3.5 %collective-permute-done.65.refs_2_ = bf16[64,3072]{1,0:T(8,128)(2,1)S(1)} collective-permute-done((bf16[64,3072]{1,0:T(8,128)(2,1)S(1)}, bf16[64,3072]{1,0:T(8,128)(2,1)S(1)}, u32[]{:S(2)}, u32[]{:S(2)}) %collective-permute-start.65) | collective-permute-done | bytes 393248 | tf_op jit(solution)/shard_map/ppermute | solution.py:565
  243.5 7.4 %collective-permute-done.67.got_y = bf16[4,48,1536]{2,1,0:T(8,128)(2,1)} collective-permute-done((bf16[4,48,1536]{2,1,0:T(8,128)(2,1)}, bf16[4,48,1536]{2,1,0:T(8,128)(2,1)}, u32[]{:S(2)}, u32[]{:S(2)}) %collective-permute-start.67) | collective-permute-done | bytes 589856 | tf_op jit(solution)/shard_map/ppermute | solution.py:569
  251.8 3.1 %collective-permute-start.73 = (bf16[24,768]{1,0:T(8,128)(2,1)S(1)}, bf16[24,768]{1,0:T(8,128)(2,1)S(1)}, u32[]{:S(2)}, u32[]{:S(2)}) collective-permute-start(bf16[24,768]{1,0:T(8,128)(2,1)S(1)} %get-tuple-element.279), channel_id=1, source_target_pairs={{0,8},{1,9},{2,10},{3,11},{4,12},{5,13},{6,14},{7,15},{8,0},{9,1},... | collective-permute-start | bytes 110600 | tf_op jit(solution)/shard_map/ppermute | solution.py:565
  254.9 2.4 collective-permute-start.72
  263.7 2.7 collective-permute-start.69
  270.7 4.7 %collective-permute-start.81 = (bf16[16,12288]{1,0:T(8,128)(2,1)S(1)}, bf16[16,12288]{1,0:T(8,128)(2,1)S(1)}, u32[]{:S(2)}, u32[]{:S(2)}) collective-permute-start(bf16[16,12288]{1,0:T(8,128)(2,1)S(1)} %head_rows.1.refs_0_), channel_id=1, source_target_pairs={{0,16},{16,0},{1,17},{17,1},{2,18},{18,2},{3,19},{19,3},{4,20},{20... | collective-permute-start | bytes 1179656 | tf_op jit(solution)/shard_map/ppermute | solution.py:573
  280.7 3.0 %head_owner.1 = (f32[48,9216]{1,0:T(8,128)}, f32[12,768]{1,0:T(8,128)S(1)}) custom-call(s32[5]{0:T(128)S(1)} %stack.15.where, bf16[16,12288]{1,0:T(8,128)(2,1)S(1)} %head_rows.1.refs_0_, bf16[16,12288]{1,0:T(8,128)(2,1)S(1)} %collective-permute-done.81.refs_1_), custom_call_target="tpu_custom_call" | custom-call | flops 28311552 | bytes 2592768 | tf_op jit(solution)/shard_map/head_owner/pallas_call | solution.py:591
  (330 shorter events, 148.7 us)
Async XLA Ops:
  6.2 12.1 %collective-permute-start.1 = (bf16[48,1664]{1,0:T(8,128)(2,1)S(1)}, bf16[48,1664]{1,0:T(8,128)(2,1)S(1)}, u32[]{:S(2)}, u32[]{:S(2)}) collective-permute-start(bf16[48,1664]{1,0:T(8,128)(2,1)S(1)} %prepare_first.1.refs_0_), channel_id=1, source_target_pairs={{0,8},{1,9},{2,10},{3,11},{4,12},{5,13},{6,14},{7,15},{8,0},{9,1},... | collective-permute-start | bytes 479240 | tf_op jit(solution)/shard_map/ppermute | solution.py:565
  8.5 13.4 %collective-permute-start = (bf16[48,1664]{1,0:T(8,128)(2,1)S(1)}, bf16[48,1664]{1,0:T(8,128)(2,1)S(1)}, u32[]{:S(2)}, u32[]{:S(2)}) collective-permute-start(bf16[48,1664]{1,0:T(8,128)(2,1)S(1)} %prepare_first.1.refs_0_), channel_id=1, source_target_pairs={{0,4},{1,5},{2,6},{3,7},{4,8},{5,9},{6,10},{7,11},{8,12},{9,13},{1... | collective-permute-start | bytes 479240 | tf_op jit(solution)/shard_map/ppermute | solution.py:565
  21.9 14.7 %collective-permute-start.3 = (bf16[48,6656]{1,0:T(8,128)(2,1)S(1)}, bf16[48,6656]{1,0:T(8,128)(2,1)S(1)}, u32[]{:S(2)}, u32[]{:S(2)}) collective-permute-start(bf16[48,6656]{1,0:T(8,128)(2,1)S(1)} %pad_maximum_fusion), channel_id=1, source_target_pairs={{0,1},{1,0},{2,3},{3,2},{4,5},{5,4},{6,7},{7,6},{8,9},{9,8},{10,11... | collective-permute-start | bytes 1916936 | tf_op jit(solution)/shard_map/ppermute | solution.py:569
  24.3 14.4 %collective-permute-start.4 = (bf16[48,6656]{1,0:T(8,128)(2,1)S(1)}, bf16[48,6656]{1,0:T(8,128)(2,1)S(1)}, u32[]{:S(2)}, u32[]{:S(2)}) collective-permute-start(bf16[48,6656]{1,0:T(8,128)(2,1)S(1)} %pad_maximum_fusion), channel_id=1, source_target_pairs={{0,2},{1,3},{2,0},{3,1},{4,6},{5,7},{6,4},{7,5},{8,10},{9,11},{10,... | collective-permute-start | bytes 1916936 | tf_op jit(solution)/shard_map/ppermute | solution.py:569
  24.6 14.6 %collective-permute-start.7 = (bf16[48,1536]{1,0:T(8,128)(2,1)S(1)}, bf16[48,1536]{1,0:T(8,128)(2,1)S(1)}, u32[]{:S(2)}, u32[]{:S(2)}) collective-permute-start(bf16[48,1536]{1,0:T(8,128)(2,1)S(1)} %get-tuple-element.151.refs_0_), channel_id=1, source_target_pairs={{0,12},{1,13},{2,14},{3,15},{4,0},{5,1},{6,2},{7,3},{8,4},{9,5},{1... | collective-permute-start | bytes 442376 | tf_op jit(solution)/shard_map/ppermute | solution.py:565
  25.7 13.4 %collective-permute-start.6 = (bf16[48,1536]{1,0:T(8,128)(2,1)S(1)}, bf16[48,1536]{1,0:T(8,128)(2,1)S(1)}, u32[]{:S(2)}, u32[]{:S(2)}) collective-permute-start(bf16[48,1536]{1,0:T(8,128)(2,1)S(1)} %get-tuple-element.151.refs_0_), channel_id=1, source_target_pairs={{0,8},{1,9},{2,10},{3,11},{4,12},{5,13},{6,14},{7,15},{8,0},{9,1},... | collective-permute-start | bytes 442376 | tf_op jit(solution)/shard_map/ppermute | solution.py:565
  27.9 11.1 %collective-permute-start.5 = (bf16[48,1536]{1,0:T(8,128)(2,1)S(1)}, bf16[48,1536]{1,0:T(8,128)(2,1)S(1)}, u32[]{:S(2)}, u32[]{:S(2)}) collective-permute-start(bf16[48,1536]{1,0:T(8,128)(2,1)S(1)} %get-tuple-element.151.refs_0_), channel_id=1, source_target_pairs={{0,4},{1,5},{2,6},{3,7},{4,8},{5,9},{6,10},{7,11},{8,12},{9,13},{1... | collective-permute-start | bytes 442376 | tf_op jit(solution)/shard_map/ppermute | solution.py:565
  39.2 19.6 %collective-permute-start.13 = (bf16[48,9472]{1,0:T(8,128)(2,1)S(1)}, bf16[48,9472]{1,0:T(8,128)(2,1)S(1)}, u32[]{:S(2)}, u32[]{:S(2)}) collective-permute-start(bf16[48,9472]{1,0:T(8,128)(2,1)S(1)} %get-tuple-element.298), channel_id=1, source_target_pairs={{0,1},{1,0},{2,3},{3,2},{4,5},{5,4},{6,7},{7,6},{8,9},{9,8},{10,11... | collective-permute-start | bytes 2727944 | tf_op jit(solution)/shard_map/ppermute | solution.py:569
  39.5 21.5 %collective-permute-start.11 = (bf16[48,9472]{1,0:T(8,128)(2,1)S(1)}, bf16[48,9472]{1,0:T(8,128)(2,1)S(1)}, u32[]{:S(2)}, u32[]{:S(2)}) collective-permute-start(bf16[48,9472]{1,0:T(8,128)(2,1)S(1)} %get-tuple-element.299), channel_id=1, source_target_pairs={{0,2},{1,3},{2,0},{3,1},{4,6},{5,7},{6,4},{7,5},{8,10},{9,11},{10,... | collective-permute-start | bytes 2727944 | tf_op jit(solution)/shard_map/ppermute | solution.py:569
  40.7 30.7 %collective-permute-start.14 = (bf16[128,768]{1,0:T(8,128)(2,1)S(1)}, bf16[128,768]{1,0:T(8,128)(2,1)S(1)}, u32[]{:S(2)}, u32[]{:S(2)}) collective-permute-start(bf16[128,768]{1,0:T(8,128)(2,1)S(1)} %copy-done.11), channel_id=1, source_target_pairs={{0,16},{16,0},{1,17},{17,1},{2,18},{18,2},{3,19},{19,3},{4,20},{20... | collective-permute-start | bytes 589832 | tf_op jit(solution)/shard_map/ppermute | solution.py:573
  42.4 20.7 %collective-permute-start.10 = (bf16[48,1536]{1,0:T(8,128)(2,1)S(1)}, bf16[48,1536]{1,0:T(8,128)(2,1)S(1)}, u32[]{:S(2)}, u32[]{:S(2)}) collective-permute-start(bf16[48,1536]{1,0:T(8,128)(2,1)S(1)} %get-tuple-element.152.refs_0_), channel_id=1, source_target_pairs={{0,12},{1,13},{2,14},{3,15},{4,0},{5,1},{6,2},{7,3},{8,4},{9,5},{1... | collective-permute-start | bytes 442376 | tf_op jit(solution)/shard_map/ppermute | solution.py:565
  44.4 18.7 %collective-permute-start.9 = (bf16[48,1536]{1,0:T(8,128)(2,1)S(1)}, bf16[48,1536]{1,0:T(8,128)(2,1)S(1)}, u32[]{:S(2)}, u32[]{:S(2)}) collective-permute-start(bf16[48,1536]{1,0:T(8,128)(2,1)S(1)} %get-tuple-element.152.refs_0_), channel_id=1, source_target_pairs={{0,8},{1,9},{2,10},{3,11},{4,12},{5,13},{6,14},{7,15},{8,0},{9,1},... | collective-permute-start | bytes 442376 | tf_op jit(solution)/shard_map/ppermute | solution.py:565
  63.1 28.8 %collective-permute-start.18 = (bf16[48,9216]{1,0:T(8,128)(2,1)S(1)}, bf16[48,9216]{1,0:T(8,128)(2,1)S(1)}, u32[]{:S(2)}, u32[]{:S(2)}) collective-permute-start(bf16[48,9216]{1,0:T(8,128)(2,1)S(1)} %get-tuple-element.290), channel_id=1, source_target_pairs={{0,2},{1,3},{2,0},{3,1},{4,6},{5,7},{6,4},{7,5},{8,10},{9,11},{10,... | collective-permute-start | bytes 2654216 | tf_op jit(solution)/shard_map/ppermute | solution.py:569
  65.5 26.5 %collective-permute-start.12 = (bf16[48,9216]{1,0:T(8,128)(2,1)S(1)}, bf16[48,9216]{1,0:T(8,128)(2,1)S(1)}, u32[]{:S(2)}, u32[]{:S(2)}) collective-permute-start(bf16[48,9216]{1,0:T(8,128)(2,1)S(1)} %get-tuple-element.291), channel_id=1, source_target_pairs={{0,1},{1,0},{2,3},{3,2},{4,5},{5,4},{6,7},{7,6},{8,9},{9,8},{10,11... | collective-permute-start | bytes 2654216 | tf_op jit(solution)/shard_map/ppermute | solution.py:569
  76.9 11.8 %collective-permute-start.17 = (bf16[768,384]{1,0:T(8,128)(2,1)S(1)}, bf16[768,384]{1,0:T(8,128)(2,1)S(1)}, u32[]{:S(2)}, u32[]{:S(2)}) collective-permute-start(bf16[768,384]{1,0:T(8,128)(2,1)S(1)} %bitcast.20), channel_id=1, source_target_pairs={{0,16},{16,0},{1,17},{17,1},{2,18},{18,2},{3,19},{19,3},{4,20},{20... | collective-permute-start | bytes 1769480 | tf_op jit(solution)/shard_map/ppermute | solution.py:573
  79.6 13.9 %collective-permute-start.34 = (bf16[48,1152]{1,0:T(8,128)(2,1)S(1)}, bf16[48,1152]{1,0:T(8,128)(2,1)S(1)}, u32[]{:S(2)}, u32[]{:S(2)}) collective-permute-start(bf16[48,1152]{1,0:T(8,128)(2,1)S(1)} %get-tuple-element.192), channel_id=1, source_target_pairs={{0,12},{1,13},{2,14},{3,15},{4,0},{5,1},{6,2},{7,3},{8,4},{9,5},{1... | collective-permute-start | bytes 331784 | tf_op jit(solution)/shard_map/ppermute | solution.py:565
  101.4 15.7 %collective-permute-start.36 = (bf16[48,4992]{1,0:T(8,128)(2,1)}, bf16[48,4992]{1,0:T(8,128)(2,1)}, u32[]{:S(2)}, u32[]{:S(2)}) collective-permute-start(bf16[48,4992]{1,0:T(8,128)(2,1)} %constant_dynamic-update-slice_fusion.16), channel_id=1, source_target_pairs={{0,2},{1,3},{2,0},{3,1},{4,6},{5,7},{6,4},{7,5},{8,10},{9,11},{10,... | collective-permute-start | bytes 1437704 | tf_op jit(solution)/shard_map/ppermute | solution.py:569
  101.7 18.3 %collective-permute-start.35 = (bf16[48,4992]{1,0:T(8,128)(2,1)}, bf16[48,4992]{1,0:T(8,128)(2,1)}, u32[]{:S(2)}, u32[]{:S(2)}) collective-permute-start(bf16[48,4992]{1,0:T(8,128)(2,1)} %constant_dynamic-update-slice_fusion.16), channel_id=1, source_target_pairs={{0,1},{1,0},{2,3},{3,2},{4,5},{5,4},{6,7},{7,6},{8,9},{9,8},{10,11... | collective-permute-start | bytes 1437704 | tf_op jit(solution)/shard_map/ppermute | solution.py:569
  128.2 31.8 %collective-permute-start.39 = (bf16[16,48,1152]{2,1,0:T(8,128)(2,1)S(1)}, bf16[16,48,1152]{2,1,0:T(8,128)(2,1)S(1)}, u32[]{:S(2)}, u32[]{:S(2)}) collective-permute-start(bf16[16,48,1152]{2,1,0:T(8,128)(2,1)S(1)} %get-tuple-element.197.own), channel_id=1, source_target_pairs={{0,16},{16,0},{1,17},{17,1},{2,18},{18,2},{3,19},{19,3},{4,20},{20... | collective-permute-start | bytes 5308424 | tf_op jit(solution)/shard_map/ppermute | solution.py:573
  145.1 25.4 %collective-permute-start.46 = (bf16[2,48,3072]{2,1,0:T(8,128)(2,1)S(1)}, bf16[2,48,3072]{2,1,0:T(8,128)(2,1)S(1)}, u32[]{:S(2)}, u32[]{:S(2)}) collective-permute-start(bf16[2,48,3072]{2,1,0:T(8,128)(2,1)S(1)} %get-tuple-element.204), channel_id=1, source_target_pairs={{0,2},{1,3},{2,0},{3,1},{4,6},{5,7},{6,4},{7,5},{8,10},{9,11},{10,... | collective-permute-start | bytes 1769480 | tf_op jit(solution)/shard_map/ppermute | solution.py:569
  146.4 24.1 %collective-permute-start.47 = (bf16[2,48,3072]{2,1,0:T(8,128)(2,1)S(1)}, bf16[2,48,3072]{2,1,0:T(8,128)(2,1)S(1)}, u32[]{:S(2)}, u32[]{:S(2)}) collective-permute-start(bf16[2,48,3072]{2,1,0:T(8,128)(2,1)S(1)} %get-tuple-element.208), channel_id=1, source_target_pairs={{0,1},{1,0},{2,3},{3,2},{4,5},{5,4},{6,7},{7,6},{8,9},{9,8},{10,11... | collective-permute-start | bytes 1769480 | tf_op jit(solution)/shard_map/ppermute | solution.py:569
  171.2 35.2 %collective-permute-start.58 = (bf16[4,48,3072]{2,1,0:T(8,128)(2,1)S(1)}, bf16[4,48,3072]{2,1,0:T(8,128)(2,1)S(1)}, u32[]{:S(2)}, u32[]{:S(2)}) collective-permute-start(bf16[4,48,3072]{2,1,0:T(8,128)(2,1)S(1)} %get-tuple-element.212), channel_id=1, source_target_pairs={{0,1},{1,0},{2,3},{3,2},{4,5},{5,4},{6,7},{7,6},{8,9},{9,8},{10,11... | collective-permute-start | bytes 3538952 | tf_op jit(solution)/shard_map/ppermute | solution.py:569
  171.5 34.9 %collective-permute-start.59 = (bf16[4,48,3072]{2,1,0:T(8,128)(2,1)S(1)}, bf16[4,48,3072]{2,1,0:T(8,128)(2,1)S(1)}, u32[]{:S(2)}, u32[]{:S(2)}) collective-permute-start(bf16[4,48,3072]{2,1,0:T(8,128)(2,1)S(1)} %get-tuple-element.213), channel_id=1, source_target_pairs={{0,2},{1,3},{2,0},{3,1},{4,6},{5,7},{6,4},{7,5},{8,10},{9,11},{10,... | collective-permute-start | bytes 3538952 | tf_op jit(solution)/shard_map/ppermute | solution.py:569
  207.5 14.5 %collective-permute-start.62 = (bf16[64,3072]{1,0:T(8,128)(2,1)S(1)}, bf16[64,3072]{1,0:T(8,128)(2,1)S(1)}, u32[]{:S(2)}, u32[]{:S(2)}) collective-permute-start(bf16[64,3072]{1,0:T(8,128)(2,1)S(1)} %get-tuple-element.263), channel_id=1, source_target_pairs={{0,12},{1,13},{2,14},{3,15},{4,0},{5,1},{6,2},{7,3},{8,4},{9,5},{1... | collective-permute-start | bytes 1179656 | tf_op jit(solution)/shard_map/ppermute | solution.py:565
  212.0 24.1 %collective-permute-start.65 = (bf16[64,3072]{1,0:T(8,128)(2,1)S(1)}, bf16[64,3072]{1,0:T(8,128)(2,1)S(1)}, u32[]{:S(2)}, u32[]{:S(2)}) collective-permute-start(bf16[64,3072]{1,0:T(8,128)(2,1)S(1)} %get-tuple-element.270), channel_id=1, source_target_pairs={{0,8},{1,9},{2,10},{3,11},{4,12},{5,13},{6,14},{7,15},{8,0},{9,1},... | collective-permute-start | bytes 1179656 | tf_op jit(solution)/shard_map/ppermute | solution.py:565
  236.1 14.7 %collective-permute-start.67 = (bf16[4,48,1536]{2,1,0:T(8,128)(2,1)}, bf16[4,48,1536]{2,1,0:T(8,128)(2,1)}, u32[]{:S(2)}, u32[]{:S(2)}) collective-permute-start(bf16[4,48,1536]{2,1,0:T(8,128)(2,1)} %get-tuple-element.273), channel_id=1, source_target_pairs={{0,2},{1,3},{2,0},{3,1},{4,6},{5,7},{6,4},{7,5},{8,10},{9,11},{10,... | collective-permute-start | bytes 1769480 | tf_op jit(solution)/shard_map/ppermute | solution.py:569
  237.3 14.4 %collective-permute-start.66 = (bf16[4,48,1536]{2,1,0:T(8,128)(2,1)}, bf16[4,48,1536]{2,1,0:T(8,128)(2,1)}, u32[]{:S(2)}, u32[]{:S(2)}) collective-permute-start(bf16[4,48,1536]{2,1,0:T(8,128)(2,1)} %get-tuple-element.271), channel_id=1, source_target_pairs={{0,1},{1,0},{2,3},{3,2},{4,5},{5,4},{6,7},{7,6},{8,9},{9,8},{10,11... | collective-permute-start | bytes 1769480 | tf_op jit(solution)/shard_map/ppermute | solution.py:569
  242.4 17.5 %collective-permute-start.61 = (f32[128,768]{1,0:T(8,128)}, f32[128,768]{1,0:T(8,128)S(1)}, u32[]{:S(2)}, u32[]{:S(2)}) collective-permute-start(f32[128,768]{1,0:T(8,128)} %copy-done.55), channel_id=1, source_target_pairs={{0,16},{16,0},{1,17},{17,1},{2,18},{18,2},{3,19},{19,3},{4,20},{20... | collective-permute-start | bytes 1179656 | tf_op jit(solution)/shard_map/ppermute | solution.py:573
  243.5 17.1 %collective-permute-start.78 = (bf16[64,3072]{1,0:T(8,128)(2,1)}, bf16[64,3072]{1,0:T(8,128)(2,1)S(1)}, u32[]{:S(2)}, u32[]{:S(2)}) collective-permute-start(bf16[64,3072]{1,0:T(8,128)(2,1)} %copy-done.54), channel_id=1, source_target_pairs={{0,4},{1,5},{2,6},{3,7},{4,8},{5,9},{6,10},{7,11},{8,12},{9,13},{1... | collective-permute-start | bytes 1179656 | tf_op jit(solution)/shard_map/ppermute | solution.py:565
  262.1 16.8 %collective-permute-start.68 = (bf16[48,1536]{1,0:T(8,128)(2,1)S(1)}, bf16[48,1536]{1,0:T(8,128)(2,1)S(1)}, u32[]{:S(2)}, u32[]{:S(2)}) collective-permute-start(bf16[48,1536]{1,0:T(8,128)(2,1)S(1)} %get-tuple-element.275), channel_id=1, source_target_pairs={{0,4},{1,5},{2,6},{3,7},{4,8},{5,9},{6,10},{7,11},{8,12},{9,13},{1... | collective-permute-start | bytes 442376 | tf_op jit(solution)/shard_map/ppermute | solution.py:565
  263.7 15.3 %collective-permute-start.69 = (bf16[48,1536]{1,0:T(8,128)(2,1)S(1)}, bf16[48,1536]{1,0:T(8,128)(2,1)S(1)}, u32[]{:S(2)}, u32[]{:S(2)}) collective-permute-start(bf16[48,1536]{1,0:T(8,128)(2,1)S(1)} %get-tuple-element.276), channel_id=1, source_target_pairs={{0,8},{1,9},{2,10},{3,11},{4,12},{5,13},{6,14},{7,15},{8,0},{9,1},... | collective-permute-start | bytes 442376 | tf_op jit(solution)/shard_map/ppermute | solution.py:565
  266.4 12.6 %collective-permute-start.70 = (bf16[48,1536]{1,0:T(8,128)(2,1)S(1)}, bf16[48,1536]{1,0:T(8,128)(2,1)S(1)}, u32[]{:S(2)}, u32[]{:S(2)}) collective-permute-start(bf16[48,1536]{1,0:T(8,128)(2,1)S(1)} %get-tuple-element.277), channel_id=1, source_target_pairs={{0,12},{1,13},{2,14},{3,15},{4,0},{5,1},{6,2},{7,3},{8,4},{9,5},{1... | collective-permute-start | bytes 442376 | tf_op jit(solution)/shard_map/ppermute | solution.py:565
  (107 other events, 829.3 us)

commit v4 on v3

--- a/solution.py
+++ b/solution.py
@@ -581,11 +581,11 @@
     return jax.ShapeDtypeStruct(dims, dtype)
 
 
-def run_kernel(body, name, outs, where, blocks, arrays, scratch=(), outs_far=False, flops=0):
+def run_kernel(body, name, outs, where, blocks, arrays, scratch=(), far=(), flops=0):
     in_specs = [pl.BlockSpec(memory_space=pltpu.SMEM)]
-    in_specs += [pl.BlockSpec(memory_space=pl.ANY)] * len(blocks)
+    in_specs += [pl.BlockSpec(memory_space=pltpu.HBM)] * len(blocks)
     in_specs += [pl.BlockSpec(memory_space=pltpu.VMEM)] * len(arrays)
-    out_space = pl.ANY if outs_far else pltpu.VMEM
+    spaces = [pltpu.HBM if at in far else pltpu.VMEM for at in range(len(outs))]
     moved = sum(x.size * x.dtype.itemsize for x in list(blocks) + list(arrays))
     moved += sum(math.prod(o.shape) * jnp.dtype(o.dtype).itemsize for o in outs)
     return pl.pallas_call(
@@ -593,7 +593,7 @@
         name=name,
         out_shape=tuple(outs),
         in_specs=in_specs,
-        out_specs=tuple(pl.BlockSpec(memory_space=out_space) for _ in outs),
+        out_specs=tuple(pl.BlockSpec(memory_space=space) for space in spaces),
         scratch_shapes=list(scratch),
         cost_estimate=pl.CostEstimate(flops=flops, bytes_accessed=moved, transcendentals=0),
         compiler_params=pltpu.CompilerParams(vmem_limit_bytes=VMEM_BYTES),
@@ -649,25 +649,27 @@
     return value.reshape(value.shape[0] * value.shape[1], value.shape[2])
 
 
-def prepare_first_kernel(where, seg, seg_vec, cls_vec, live_row, out, sems):
+def prepare_first_kernel(where, seg, vecs, flags, out, live_out, sems):
     core_at = where[2]
     pairs = []
     for piece in range(4):
         source = seg.at[:, pl.ds(aligned(piece * MODEL + core_at * HALF), HALF)]
         pairs.append((source, out.at[:, piece * HALF : (piece + 1) * HALF]))
     run_copies(pairs, sems)
-    size = seg_vec.shape[1]
+    size = vecs.shape[1]
     lines = -(-size // LANES)
     block = jnp.zeros((OWN, LANES), WIDE)
     row_at = lax.broadcasted_iota(jnp.int32, (OWN, LANES), 0)
-    for which, vec in enumerate((seg_vec, cls_vec)):
+    for which in range(2):
         for line in range(lines):
             width = min(LANES, size - line * LANES)
-            value = vec[:, line * LANES : line * LANES + width].astype(WIDE)
+            value = vecs[which : which + 1, line * LANES : line * LANES + width]
             if width < LANES:
                 value = jnp.concatenate([value, jnp.zeros((1, LANES - width), WIDE)], axis=1)
             block = jnp.where(row_at == which * lines + line, value, block)
-    count = jnp.sum(live_row[...], axis=1, keepdims=True)
+    live = flags[...].astype(WIDE)
+    live_out[...] = live
+    count = jnp.sum(live, axis=1, keepdims=True)
     block = jnp.where(row_at == 2 * lines, count, block)
     out[:, 4 * HALF :] = block.astype(LOW)
 
@@ -773,8 +775,8 @@
 def qkv_kernel(where, *refs):
     blocks = refs[:8]
     hidden, hidden_got, live_row, live_got = refs[8:12]
-    weight, out_half, qkv_out, mixed_out, vectors_out, count_out = refs[12:18]
-    vec_rows, flat, inputs = refs[18:]
+    weight_out, out_half, qkv_out, mixed_out, vectors_out, count_out = refs[12:18]
+    vec_rows, flat, inputs, weight, sem = refs[18:]
     core_at = where[2]
     gather_blocks(
         where,
@@ -787,6 +789,8 @@
             (vec_rows, 4 * HALF, 4 * HALF + LANES),
         ),
     )
+    stored = pltpu.make_async_copy(weight, weight_out, sem)
+    stored.start()
     piece = (8 * MODEL + FF) // GROUP
     lines = -(-piece // LANES)
     count = jnp.zeros((1, LANES), WIDE)
@@ -817,6 +821,7 @@
         tiles = attend_tiles(qkv_out[rows, :], HALF, token_allowed(live[...]))
         for tile, value in enumerate(tiles):
             mixed_out[rows, tile * LANES : (tile + 1) * LANES] = value
+    stored.wait()
 
 
 def norm_rows(summed):
@@ -848,11 +853,13 @@
 
 
 def out_kernel(where, hidden, mixed, mixed_got, half, half_got, vectors, *outs):
-    full_out, mixed_full, normed_out, inv_out, low_out = outs
+    full_store, mixed_full, normed_out, inv_out, low_out, full_out, sem = outs
     core_at = where[2]
     own, other = aligned(core_at * HALF), aligned((1 - core_at) * HALF)
     full_out[:, pl.ds(own, HALF)] = half[...]
     full_out[:, pl.ds(other, HALF)] = half_got[...]
+    stored = pltpu.make_async_copy(full_out, full_store, sem)
+    stored.start()
     mixed_full[:, pl.ds(own, HALF)] = mixed[...]
     mixed_full[:SEG, pl.ds(other, HALF)] = mixed_got[SEG:, :]
     mixed_full[SEG:, pl.ds(other, HALF)] = mixed_got[:SEG, :]
@@ -861,16 +868,18 @@
     normed_out[...] = normed
     inv_out[...] = inv_dev
     low_out[...] = (normed * vectors[4:5, :] + vectors[5:6, :]).astype(LOW)
+    stored.wait()
 
 
 def up_kernel(where, *refs):
     blocks = refs[:8]
     low, low_got, vectors = refs[8:11]
-    weight, act_out, slope_out, both = refs[11:]
+    weight, act_out, slope_store, both, slope_out, sems = refs[11:]
     core_at = where[2]
     gather_blocks(where, blocks, 2 * (4 * HALF + LANES), FF_HALF, ((weight, 0, FF_HALF),))
     both[:SEG] = low[...]
     both[SEG:] = low_got[...]
+    stored = []
     for at in range(FF_HALF // MODEL):
         columns = slice(at * MODEL, (at + 1) * MODEL)
         held = weight[:, :, columns]
@@ -879,15 +888,25 @@
         value, slope = gelu_both(before + bias)
         act_out[:, columns] = value.astype(LOW)
         slope_out[:, columns] = slope
+        stored.append(
+            pltpu.make_async_copy(
+                slope_out.at[:, columns], slope_store.at[:, columns], sems.at[at]
+            )
+        )
+        stored[-1].start()
+    wait_all(stored)
 
 
 def down_kernel(where, *refs):
     blocks, act = refs[:8], refs[8]
-    weight, own_out, send_out = refs[9:]
+    store, own_out, send_out, weight, sem = refs[9:]
     gather_blocks(where, blocks, 2 * FF_HALF, FF_HALF, ((weight, 0, FF_HALF),))
+    stored = pltpu.make_async_copy(weight, store, sem)
+    stored.start()
     partial = product_right(act[...], whole_rows(weight))
     own_out[...] = partial[:SEG]
     send_out[...] = partial[SEG:]
+    stored.wait()
 
 
 def seg_rows_kernel(where, *refs):
@@ -899,7 +918,9 @@
     normed_out[...] = normed
     inv_out[...] = inv_dev
     rows = normed * vectors[6:7, :] + vectors[7:8, :]
-    live_rows = live[...]
+    shape = (SEG, SEG)
+    same = lax.broadcasted_iota(jnp.int32, shape, 0) == lax.broadcasted_iota(jnp.int32, shape, 1)
+    live_rows = jnp.sum(jnp.where(same, live[...], 0.0), axis=1, keepdims=True)
     target_rows = targets[...].astype(WIDE)
     output = rows * live_rows
     rows_out[...] = output
@@ -1357,8 +1378,18 @@
     return (feature == rank * width + column).astype(LOW)
 
 
+def own_vector(rank, pieces, out, flat):
+    size = out.shape[1]
+    for at, piece in enumerate(pieces):
+        flat[:, at * MODEL : (at + 1) * MODEL] = piece
+    value = jnp.zeros((1, size), WIDE)
+    for chip in range(GROUP):
+        value = jnp.where(rank == chip, flat[:, chip * size : (chip + 1) * size], value)
+    out[...] = value
+
+
 def cls_owner_kernel(where, *refs):
-    own, got, mats_out, vecs_out, rows = refs
+    own, got, shared, mats_out, vec_out, rows, flat = refs
     rank = where[0] * PLANE + where[1]
     width = mats_out.shape[0]
     rows[:GROUP] = own[...]
@@ -1373,12 +1404,12 @@
     for left, right, size, target in plan:
         side = product_plain(rows[:, left : left + MODEL], chosen).astype(LOW)
         mats_out[:, target : target + size] = product_left(side, rows[:, right : right + size])
-    vecs_out[...] = jnp.zeros_like(vecs_out)
-    for at, start in ((0, MODEL), (1, 3 * MODEL), (2, 5 * MODEL), (3, 7 * MODEL + FF)):
-        vecs_out[at : at + 1, :] = column_sum(rows[:, start : start + MODEL])
-    for at in range(FF // MODEL):
-        start = 7 * MODEL + at * MODEL
-        vecs_out[8 + at : 9 + at, :] = column_sum(rows[:, start : start + MODEL])
+    starts = (MODEL, 3 * MODEL, 5 * MODEL, 7 * MODEL + FF)
+    pieces = [column_sum(rows[:, start : start + MODEL]) for start in starts]
+    pieces += [shared[GROUP + 1 + at : GROUP + 2 + at, :] for at in range(4)]
+    starts = [7 * MODEL + at * MODEL for at in range(FF // MODEL)]
+    pieces += [column_sum(rows[:, start : start + MODEL]) for start in starts]
+    own_vector(rank, pieces, vec_out, flat)
 
 
 def head_share_kernel(where, *refs):
@@ -1411,8 +1442,13 @@
     vecs_out[...] = product_plain(hot, rows[...])
 
 
-def seg_owner_kernel(where, attn, attn_got, mlp, mlp_got, mats_out):
+def seg_owner_kernel(where, *refs):
+    attn, attn_got, mlp, mlp_got, vecs, vecs_got, mats_out, vec_out, flat = refs
     core_at = where[2]
+    rank = where[0] * PLANE + where[1]
+    rows = (8 * MODEL + FF) // MODEL
+    pieces = [vecs[at : at + 1, :] + vecs_got[at : at + 1, :] for at in range(rows)]
+    own_vector(rank, pieces, vec_out, flat)
 
     def put(base, size, own, got):
         mats_out[:, pl.ds(aligned(base + core_at * size), size)] = own
@@ -1451,20 +1487,18 @@
     where = jnp.stack([line_at, plane_at, core_at, doc_ids[0], seg_nums[0]]).astype(jnp.int32)
     own_rows, total_columns = seg_mats.shape
     vec_size = seg_vecs.shape[0]
-    live = valid_flags.astype(WIDE)
-    live_row, live_column = live[None, :], live[:, None]
     both_rows = CORES * SEG
     first_columns = 4 * HALF + LANES
 
-    first_piece = run_kernel(
+    first_piece, live_row = run_kernel(
         prepare_first_kernel,
         "prepare_first",
-        [shape_of((own_rows, first_columns), LOW)],
+        [shape_of((own_rows, first_columns), LOW), shape_of((1, SEG))],
         where,
         (seg_mats,),
-        (seg_vecs[None], cls_vecs[None], live_row),
+        (jnp.stack([seg_vecs, cls_vecs]).astype(WIDE), valid_flags[None]),
         [pltpu.SemaphoreType.DMA((4,))],
-    )[0]
+    )
     first_line = line_parts(first_piece)
     rest = run_kernel(
         prepare_rest_kernel,
@@ -1488,9 +1522,10 @@
     def sent_both(to_x, to_y):
         return in_plane(to_x, 1), in_plane(to_y, 2)
 
+    hidden_got, live_got = other_core(hidden_in), other_core(live_row)
     first_sent = joined(*first_line)
     first_x, first_y = sent_both(first_sent, first_sent)
-    second_line = line_parts(after(second_piece, *first_line[1:]))
+    second_line = line_parts(after(second_piece, hidden_got, live_got, *first_line[1:]))
     size = 2 * first_columns
     second_x, second_y = sent_both(
         joined(first_y[:, size:], *second_line), joined(first_x[:, :size], *second_line)
@@ -1506,7 +1541,6 @@
         for apart in range(1, LINE)
     )
 
-    hidden_got, live_got = other_core(hidden_in), other_core(live_row)
     qkv_weight, out_half, qkv, mixed, vectors, count = run_kernel(
         qkv_kernel,
         "seg_qkv",
@@ -1527,7 +1561,10 @@
             pltpu.VMEM((GROUP, own_rows, LANES), LOW),
             pltpu.VMEM((2, 8 * MODEL + FF), WIDE),
             pltpu.VMEM((both_rows, MODEL), LOW),
+            pltpu.VMEM((GROUP, own_rows, 3 * HALF), LOW),
+            pltpu.SemaphoreType.DMA(()),
         ],
+        far=(0,),
         flops=2 * SEG * MODEL * 3 * MODEL,
     )
     count = count + other_core(count)
@@ -1545,9 +1582,11 @@
         where,
         (),
         (hidden_in, mixed, other_core(mixed), out_half, other_core(out_half), vectors),
+        [pltpu.VMEM((MODEL, MODEL), LOW), pltpu.SemaphoreType.DMA(())],
+        far=(0,),
         flops=2 * SEG * MODEL * MODEL,
     )
-    first_got = other_core(first_low)
+    first_got = after(other_core(first_low), count)
     third_x, third_y = after(third_x, first_low), after(third_y, first_low)
     up_weight, act, slope = run_kernel(
         up_kernel,
@@ -1562,7 +1601,12 @@
         second_line
         + (second_x, second_y, third_x, third_y)
         + (first_low, first_got, vectors),
-        [pltpu.VMEM((both_rows, MODEL), LOW)],
+        [
+            pltpu.VMEM((both_rows, MODEL), LOW),
+            pltpu.VMEM((both_rows, FF_HALF), WIDE),
+            pltpu.SemaphoreType.DMA((FF_HALF // MODEL,)),
+        ],
+        far=(2,),
         flops=2 * SEG * MODEL * FF,
     )
     fourth_x, fourth_y = sent_both(third_y[:, 2 * size :], third_x[:, size : 2 * size])
@@ -1581,6 +1625,8 @@
         where,
         (),
         third_line + (third_x, third_y, fourth_x, fourth_y) + (act,),
+        [pltpu.VMEM((GROUP, own_rows, FF_HALF), LOW), pltpu.SemaphoreType.DMA(())],
+        far=(0,),
         flops=2 * SEG * MODEL * FF,
     )
     normed_second, inv_second, diff, out_rows, head_row = run_kernel(
@@ -1601,11 +1647,12 @@
             normed_first,
             vectors,
             targets,
-            live_column,
+            live_row,
             seg_pos,
         ),
     )
     head_planes = plane_parts(head_row)
+    head_lines = line_parts(jnp.concatenate(head_planes))
     size = LINE // 2 * QUARTER_HALF
     cls_far = sent_both(
         after(cls_y[:, size:], *head_planes[1:]), after(cls_x[:, :size], *head_planes[1:])
@@ -1619,7 +1666,18 @@
         (),
         (diff, count, normed_second, inv_second, vectors),
     )
-    second_got = after(other_core(second_low), head_planes[1])
+    cls_half, cls_out_half = run_kernel(
+        cls_gather_kernel,
+        "head_gather",
+        [
+            shape_of((GROUP, own_rows, QUARTER_HALF), LOW),
+            shape_of((PLANE, own_rows, HALF), LOW),
+        ],
+        where,
+        (),
+        cls_line + (cls_x, cls_y) + cls_far + (cls_out_piece,),
+    )
+    second_got = after(other_core(second_low), head_lines[2], head_lines[3], cls_half)
     pre, first_grad_own, first_grad_send, up_sums = run_kernel(
         mlp_back_kernel,
         "seg_mlp_back",
@@ -1635,19 +1693,6 @@
         [pltpu.VMEM((both_rows, MODEL), LOW)],
         flops=4 * SEG * MODEL * FF,
     )
-    head_stack = jnp.concatenate([head_planes[0]] + [after(got, pre) for got in head_planes[1:]])
-    head_lines = line_parts(head_stack)
-    cls_half, cls_out_half = run_kernel(
-        cls_gather_kernel,
-        "head_gather",
-        [
-            shape_of((GROUP, own_rows, QUARTER_HALF), LOW),
-            shape_of((PLANE, own_rows, HALF), LOW),
-        ],
-        where,
-        (),
-        cls_line + (cls_x, cls_y) + cls_far + (cls_out_piece,),
-    )
     cls_weight, cls_out = run_kernel(
         cls_weight_kernel,
         "head_weight",
@@ -1675,13 +1720,13 @@
         part_shapes(FF),
         where,
         (),
-        (first_low, first_got, second_low, second_got, after(pre, head_lines[1]), act),
+        (first_low, first_got, second_low, second_got, pre, act),
         [
             pltpu.VMEM((both_rows, MODEL), LOW),
             pltpu.VMEM((GROUP, own_rows, FF), LOW),
             pltpu.SemaphoreType.DMA((GROUP,)),
         ],
-        outs_far=True,
+        far=range(5),
         flops=4 * SEG * MODEL * FF,
     )
     mlp_far = reduce_far(tuple(after(part, *cls_far) for part in mlp_parts[:2]))
@@ -1854,39 +1899,44 @@
             pltpu.VMEM((GROUP, own_rows, 4 * HALF), LOW),
             pltpu.SemaphoreType.DMA((GROUP,)),
         ],
-        outs_far=True,
+        far=range(5),
         flops=4 * SEG * MODEL * 2 * MODEL,
     )
     attn_far = reduce_far(tuple(after(part, mlp_got[-1]) for part in attn_parts[:2]))
     input_grad = (grad_summed + input_own + other_core(input_send)).astype(LOW)
     row_at = jnp.arange(SEG)[:, None]
     output = jnp.where(row_at == 0, top_row * live_row[:, :1], out_rows).astype(LOW)
+    payload_parts = line_parts(after(payload, attn_parts[0]))
+    attn_far = tuple(after(got, payload_parts[1]) for got in attn_far)
     attn_sent = reduce_add(where, attn_parts, attn_far)
     attn_plane = sent_both(*(after(part, mlp_got[1]) for part in attn_sent))
     mlp_got = [after(got, attn_plane[0]) for got in mlp_got]
     mlp_sum = reduce_line(mlp_own, mlp_got)
-    payload_line = jnp.concatenate(line_parts(after(payload, *attn_plane)))
+    payload_line = jnp.concatenate(payload_parts)
     mlp_mine, own_vecs = run_kernel(
         head_share_kernel,
         "seg_head_share",
         [shape_of((own_rows, FF)), shape_of((16, MODEL))],
         where,
         (),
-        plane_parts(payload_line) + (mlp_sum,),
+        plane_parts(after(payload_line, *attn_plane)) + (mlp_sum,),
         [pltpu.VMEM((GROUP * 24, MODEL), LOW)],
     )
     attn_own, *attn_sent = reduce_fold(where, attn_parts[4], attn_plane)
     attn_sum = reduce_line(
         attn_own, [along_line(attn_sent[apart - 1], apart) for apart in range(1, LINE)]
     )
-    seg_mats_grad = run_kernel(
+    flat = pltpu.VMEM((1, 8 * MODEL + FF), WIDE)
+    seg_mats_grad, seg_vec_grad = run_kernel(
         seg_owner_kernel,
         "seg_owner",
-        [shape_of((own_rows, total_columns))],
-        where,
-        (),
-        (attn_sum, other_core(attn_sum), mlp_mine, other_core(mlp_mine)),
-    )[0]
+        [shape_of((own_rows, total_columns)), shape_of((1, vec_size))],
+        where,
+        (),
+        (attn_sum, other_core(attn_sum), mlp_mine, other_core(mlp_mine))
+        + (own_vecs, other_core(own_vecs)),
+        [flat],
+    )
 
     row_width = 8 * MODEL + 2 * FF
     cls_rows = run_kernel(
@@ -1898,34 +1948,26 @@
         (pack,) + tuple(mlp_got) + (heads, cls_branch, cls_low, cls_second),
         [pltpu.VMEM((LINE,) + pack.shape, LOW)],
     )[0]
-    vec_rows = (8 * MODEL + FF) // MODEL
-    cls_mats_grad, cls_vec_rows = run_kernel(
+    cls_mats_grad, cls_vec_grad = run_kernel(
         cls_owner_kernel,
         "head_owner",
-        [shape_of((own_rows, total_columns)), shape_of((vec_rows, MODEL))],
-        where,
-        (),
-        (cls_rows, other_core(cls_rows)),
-        [pltpu.VMEM((CORES * GROUP, row_width), LOW)],
+        [shape_of((own_rows, total_columns)), shape_of((1, vec_size))],
+        where,
+        (),
+        (cls_rows, other_core(cls_rows), shared),
+        [pltpu.VMEM((CORES * GROUP, row_width), LOW), flat],
         flops=64 * own_rows * total_columns,
     )
     pos_total = shared[:GROUP]
     loss_value = shared[GROUP, 0] / (count[0, 0] * MODEL)
-    cls_vec_rows = jnp.concatenate(
-        [cls_vec_rows[:4], shared[GROUP + 1 : GROUP + 5], cls_vec_rows[8:]]
-    )
-    seg_vec_rows = (own_vecs + other_core(own_vecs))[:vec_rows]
-
-    def own_vector(rows):
-        return lax.dynamic_index_in_dim(rows.reshape(GROUP, vec_size), rank, 0, keepdims=False)
 
     return (
         output,
         input_grad,
         seg_mats_grad,
-        own_vector(seg_vec_rows),
+        seg_vec_grad.reshape(vec_size),
         cls_mats_grad,
-        own_vector(cls_vec_rows),
+        cls_vec_grad.reshape(vec_size),
         pos_total,
         loss_value,
     )

time: 290 us -> 267 us (0.921)
  local copies, waits for them, and re-layouts: 23.5 us -> 6.07 us
  starting transfers between devices: 106 us -> 101 us
  waiting for transfers between devices: 97.4 us -> 101 us
    ppermute x36, waiting for transfers between devices: 39.1 us -> 53.2 us  [along_line(): return lax.ppermute(value, 'fsdp', line_pairs(apart))]
    unnamed x134 -> x32, local copies, waits for them, and re-layouts: 15.6 us -> 2.17 us
    ppermute x26, waiting for transfers between devices: 49.1 us -> 40.8 us  [in_plane(): return lax.ppermute(value, 'fsdp', plane_pairs(mask))]
  transfers between devices with their start and end apart: 82 -> 82, of which waited for: 36 -> 31; matrix products, arithmetic and copies ran while one was open for 4% -> 2% of each run, Pallas kernels for 16% -> 17%
where the time goes in v4:
time: 267 us
  starting transfers between devices  101 us (38%)
  waiting for transfers between devices  101 us (38%)
  Pallas kernels  51 us (19%)
  local copies, waits for them, and re-layouts  6.07 us (2%)
  between operations  4.29 us (2%)
  other arithmetic  3.06 us (1%)
    ppermute x36, waiting for transfers between devices, along_line(): return lax.ppermute(value, 'fsdp', line_pairs(apart))  53.2 us
    pallas_call x29, Pallas kernels, run_kernel(): pl.pallas_call(body, name=name, out_shape=tuple(outs), in_specs=in_specs,...  51 us
    ppermute x36, starting transfers between devices, along_line(): return lax.ppermute(value, 'fsdp', line_pairs(apart))  50.2 us
    ppermute x26, waiting for transfers between devices, in_plane(): return lax.ppermute(value, 'fsdp', plane_pairs(mask))  40.8 us
    ppermute x20, starting transfers between devices, other_core(): return lax.ppermute(value, 'rep', [(0, 1), (1, 0)])  29.8 us
    ppermute x26, starting transfers between devices, in_plane(): return lax.ppermute(value, 'fsdp', plane_pairs(mask))  20.6 us
    ppermute x20, waiting for transfers between devices, other_core(): return lax.ppermute(value, 'rep', [(0, 1), (1, 0)])  7.42 us
  transfers between devices with their start and end apart: 82, of which 31 were waited for; matrix products, arithmetic and copies ran while one was open for 2% of the time, Pallas kernels for 17%

profile of v4, /device:TPU:13, one launch (start us, length us, event | category | flops | bytes accessed | tf_op | source)
XLA Modules:
  0.0 266.6 jit_solution(4508498249462295077)
XLA Ops:
  6.2 2.3 collective-permute-start.1
  10.7 11.1 %collective-permute-done.refs_1_ = bf16[48,1664]{1,0:T(8,128)(2,1)S(1)} collective-permute-done((bf16[48,1664]{1,0:T(8,128)(2,1)S(1)}, bf16[48,1664]{1,0:T(8,128)(2,1)S(1)}, u32[]{:S(2)}, u32[]{:S(2)}) %collective-permute-start) | collective-permute-done | bytes 159776 | tf_op jit(solution)/shard_map/ppermute | solution.py:565
  27.0 2.6 collective-permute-start.8
  29.6 7.0 %collective-permute-done.3.refs_4_ = bf16[48,6656]{1,0:T(8,128)(2,1)S(1)} collective-permute-done((bf16[48,6656]{1,0:T(8,128)(2,1)S(1)}, bf16[48,6656]{1,0:T(8,128)(2,1)S(1)}, u32[]{:S(2)}, u32[]{:S(2)}) %collective-permute-start.3) | collective-permute-done | bytes 639008 | tf_op jit(solution)/shard_map/ppermute | solution.py:569
  36.6 4.7 %collective-permute-done.4.refs_5_ = bf16[48,6656]{1,0:T(8,128)(2,1)S(1)} collective-permute-done((bf16[48,6656]{1,0:T(8,128)(2,1)S(1)}, bf16[48,6656]{1,0:T(8,128)(2,1)S(1)}, u32[]{:S(2)}, u32[]{:S(2)}) %collective-permute-start.4) | collective-permute-done | bytes 639008 | tf_op jit(solution)/shard_map/ppermute | solution.py:569
  45.7 16.2 %collective-permute-done.15.refs_6_.refs_4_ = bf16[48,9472]{1,0:T(8,128)(2,1)S(1)} collective-permute-done((bf16[48,9472]{1,0:T(8,128)(2,1)S(1)}, bf16[48,9472]{1,0:T(8,128)(2,1)S(1)}, u32[]{:S(2)}, u32[]{:S(2)}) %collective-permute-start.15) | collective-permute-done | bytes 909344 | tf_op jit(solution)/shard_map/ppermute | solution.py:569
  66.2 3.9 %seg_qkv.1 = (bf16[16,48,1152]{2,1,0:T(8,128)(2,1)S(1)}, bf16[16,48,384]{2,1,0:T(8,128)(2,1)S(1)}, bf16[256,1152]{1,0:T(8,128)(2,1)S(1)}, bf16[256,384]{1,0:T(8,...) custom-call(s32[5]{0:T(128)S(1)} %stack.24.where, bf16[48,1664]{1,0:T(8,128)(2,1)S(1)} %get-tuple-element.154.refs_0_, ...), custom_call_target="tpu_custom_call" | custom-call | flops 452984832 | bytes 7353344 | tf_op jit(solution)/shard_map/seg_qkv/pallas_call | solution.py:591
  70.1 3.3 %collective-permute-start.21 = (f32[8,128]{1,0:T(8,128)S(1)}, f32[8,128]{1,0:T(8,128)S(1)}, u32[]{:S(2)}, u32[]{:S(2)}) collective-permute-start(f32[8,128]{1,0:T(8,128)S(1)} %get-tuple-element.165), channel_id=1, source_target_pairs={{0,16},{16,0},{1,17},{17,1},{2,18},{18,2},{3,19},{19,3},{4,20},{20... | collective-permute-start | bytes 12296 | tf_op jit(solution)/shard_map/ppermute | solution.py:573
  75.9 6.4 %collective-permute-done.31.refs_2_ = bf16[48,1152]{1,0:T(8,128)(2,1)S(1)} collective-permute-done((bf16[48,1152]{1,0:T(8,128)(2,1)S(1)}, bf16[48,1152]{1,0:T(8,128)(2,1)S(1)}, u32[]{:S(2)}, u32[]{:S(2)}) %collective-permute-start.31) | collective-permute-done | bytes 110624 | tf_op jit(solution)/shard_map/ppermute | solution.py:565
  89.4 4.9 %collective-permute-done.22.refs_7_ = bf16[48,3072]{1,0:T(8,128)(2,1)S(1)} collective-permute-done((bf16[48,3072]{1,0:T(8,128)(2,1)S(1)}, bf16[48,3072]{1,0:T(8,128)(2,1)S(1)}, u32[]{:S(2)}, u32[]{:S(2)}) %collective-permute-start.22) | collective-permute-done | bytes 294944 | tf_op jit(solution)/shard_map/ppermute | solution.py:569
  108.7 4.6 %collective-permute-done.36.refs_7_ = bf16[48,2304]{1,0:T(8,128)(2,1)S(1)} collective-permute-done((bf16[48,2304]{1,0:T(8,128)(2,1)S(1)}, bf16[48,2304]{1,0:T(8,128)(2,1)S(1)}, u32[]{:S(2)}, u32[]{:S(2)}) %collective-permute-start.36) | collective-permute-done | bytes 221216 | tf_op jit(solution)/shard_map/ppermute | solution.py:569
  114.1 3.4 %collective-permute-start.39 = (bf16[16,48,1152]{2,1,0:T(8,128)(2,1)S(1)}, bf16[16,48,1152]{2,1,0:T(8,128)(2,1)S(1)}, u32[]{:S(2)}, u32[]{:S(2)}) collective-permute-start(bf16[16,48,1152]{2,1,0:T(8,128)(2,1)S(1)} %get-tuple-element.189.own), channel_id=1, source_target_pairs={{0,16},{16,0},{1,17},{17,1},{2,18},{18,2},{3,19},{19,3},{4,20},{20... | collective-permute-start | bytes 5308424 | tf_op jit(solution)/shard_map/ppermute | solution.py:573
  118.7 3.1 %collective-permute-start.28 = (f32[4,1664]{1,0:T(4,128)S(1)}, f32[4,1664]{1,0:T(4,128)S(1)}, u32[]{:S(2)}, u32[]{:S(2)}) collective-permute-start(f32[4,1664]{1,0:T(4,128)S(1)} %pad_maximum_fusion.1.refs_0_), channel_id=1, source_target_pairs={{0,8},{1,9},{2,10},{3,11},{4,12},{5,13},{6,14},{7,15},{8,0},{9,1},... | collective-permute-start | bytes 79880 | tf_op jit(solution)/shard_map/ppermute | solution.py:565
  125.4 3.1 %seg_mlp_weight.1 = (bf16[2,48,3072]{2,1,0:T(8,128)(2,1)S(1)}, bf16[2,48,3072]{2,1,0:T(8,128)(2,1)S(1)}, bf16[4,48,3072]{2,1,0:T(8,128)(2,1)S(1)}, bf16[4,48,307...) custom-call(s32[5]{0:T(128)S(1)} %stack.24.where, bf16[128,768]{1,0:T(8,128)(2,1)S(1)} %get-tuple-element.162.refs_8_.refs_0_.refs_6_, ...), custom_call_target="tpu_custom_call" | custom-call | flops 1207959552 | bytes 7077888 | tf_op jit(solution)/shard_map/seg_mlp_weight/pallas_call | solution.py:591
  133.2 2.6 collective-permute-start.38
  135.8 2.7 %collective-permute-done.38.refs_1_ = f32[4,1664]{1,0:T(4,128)S(1)} collective-permute-done((f32[4,1664]{1,0:T(4,128)S(1)}, f32[4,1664]{1,0:T(4,128)S(1)}, u32[]{:S(2)}, u32[]{:S(2)}) %collective-permute-start.38) | collective-permute-done | bytes 26656 | tf_op jit(solution)/shard_map/ppermute | solution.py:565
  141.0 3.0 %collective-permute-start.43 = (f32[16,768]{1,0:T(8,128)S(1)}, f32[16,768]{1,0:T(8,128)S(1)}, u32[]{:S(2)}, u32[]{:S(2)}) collective-permute-start(f32[16,768]{1,0:T(8,128)S(1)} %get-tuple-element.205.refs_1_), channel_id=1, source_target_pairs={{0,12},{1,13},{2,14},{3,15},{4,0},{5,1},{6,2},{7,3},{8,4},{9,5},{1... | collective-permute-start | bytes 147464 | tf_op jit(solution)/shard_map/ppermute | solution.py:565
  145.2 2.6 collective-permute-done.42.refs_3_
  159.5 2.4 collective-permute-start.51
  163.5 2.3 collective-permute-done.50.refs_3_
  165.8 2.3 head_attend_back.1
  174.8 6.7 %collective-permute-start.55 = (f32[1,768]{1,0:T(1,128)S(1)}, f32[1,768]{1,0:T(1,128)S(1)}, u32[]{:S(2)}, u32[]{:S(2)}) collective-permute-start(f32[1,768]{1,0:T(1,128)S(1)} %get-tuple-element.234.refs_0_.refs_3_), channel_id=1, source_target_pairs={{0,16},{16,0},{1,17},{17,1},{2,18},{18,2},{3,19},{19,3},{4,20},{20... | collective-permute-start | bytes 9224 | tf_op jit(solution)/shard_map/ppermute | solution.py:573
  187.4 2.4 collective-permute-start.62
  192.4 4.4 %seg_attn_back.1 = (bf16[256,1152]{1,0:T(8,128)(2,1)S(1)}, f32[128,768]{1,0:T(8,128)S(1)}, f32[128,768]{1,0:T(8,128)S(1)}, bf16[24,768]{1,0:T(8,128)(2,1)S(1)}) custom-call(s32[5]{0:T(128)S(1)} %stack.24.where, bf16[256,1152]{1,0:T(8,128)(2,1)S(1)} %get-tuple-element.240.refs_0_, bf16[128,768]{1,0:T(8,128)(2,1)S(1)} %get-tuple-element.241.refs_1_, ...), custom_call_target="tpu_custom_call" | custom-call | flops 905969664 | bytes 4624384 | tf_op jit(solution)/shard_map/seg_attn_back/pallas_call | solution.py:591
  196.8 4.8 %seg_attn_weight.1 = (bf16[2,48,1536]{2,1,0:T(8,128)(2,1)S(1)}, bf16[2,48,1536]{2,1,0:T(8,128)(2,1)S(1)}, bf16[4,48,1536]{2,1,0:T(8,128)(2,1)S(1)}, bf16[4,48,15...) custom-call(s32[5]{0:T(128)S(1)} %stack.24.where, bf16[128,768]{1,0:T(8,128)(2,1)S(1)} %copy-done.2, ...), custom_call_target="tpu_custom_call" | custom-call | flops 603979776 | bytes 4128768 | tf_op jit(solution)/shard_map/seg_attn_weight/pallas_call | solution.py:591
  204.6 12.5 %collective-permute-done.64 = bf16[24,768]{1,0:T(8,128)(2,1)S(1)} collective-permute-done((bf16[24,768]{1,0:T(8,128)(2,1)S(1)}, bf16[24,768]{1,0:T(8,128)(2,1)S(1)}, u32[]{:S(2)}, u32[]{:S(2)}) %collective-permute-start.64) | collective-permute-done | bytes 36896 | tf_op jit(solution)/shard_map/ppermute | solution.py:565
  222.5 8.9 %collective-permute-done.74 = bf16[24,768]{1,0:T(8,128)(2,1)S(1)} collective-permute-done((bf16[24,768]{1,0:T(8,128)(2,1)S(1)}, bf16[24,768]{1,0:T(8,128)(2,1)S(1)}, u32[]{:S(2)}, u32[]{:S(2)}) %collective-permute-start.74) | collective-permute-done | bytes 36896 | tf_op jit(solution)/shard_map/ppermute | solution.py:565
  237.7 2.3 collective-permute-start.69
  241.9 3.1 %collective-permute-start.61 = (f32[128,768]{1,0:T(8,128)S(1)}, f32[128,768]{1,0:T(8,128)S(1)}, u32[]{:S(2)}, u32[]{:S(2)}) collective-permute-start(f32[128,768]{1,0:T(8,128)S(1)} %get-tuple-element.261), channel_id=1, source_target_pairs={{0,16},{16,0},{1,17},{17,1},{2,18},{18,2},{3,19},{19,3},{4,20},{20... | collective-permute-start | bytes 1179656 | tf_op jit(solution)/shard_map/ppermute | solution.py:573
  247.2 4.7 %collective-permute-start.79 = (f32[48,3072]{1,0:T(8,128)S(1)}, f32[48,3072]{1,0:T(8,128)S(1)}, u32[]{:S(2)}, u32[]{:S(2)}) collective-permute-start(f32[48,3072]{1,0:T(8,128)S(1)} %get-tuple-element.290.refs_2_), channel_id=1, source_target_pairs={{0,16},{16,0},{1,17},{17,1},{2,18},{18,2},{3,19},{19,3},{4,20},{20... | collective-permute-start | bytes 1769480 | tf_op jit(solution)/shard_map/ppermute | solution.py:573
  258.2 3.2 %head_owner.1 = (f32[48,9216]{1,0:T(8,128)}, f32[1,576]{1,0:T(1,128)S(1)}) custom-call(s32[5]{0:T(128)S(1)} %stack.24.where, bf16[16,12288]{1,0:T(8,128)(2,1)S(1)} %head_rows.1.refs_0_, bf16[16,12288]{1,0:T(8,128)(2,1)S(1)} %collective-permute-done.81.refs_1_, f32[24,768]{1,0:T(8,128)S(1)} %add.37.refs_2_), custom_call_target="tpu_custom_call" | custom-call | flops 28311552 | bytes 2631936 | tf_op jit(solution)/shard_map/head_owner/pallas_call | solution.py:591
  262.0 2.9 %seg_owner.1 = (f32[48,9216]{1,0:T(8,128)}, f32[1,576]{1,0:T(1,128)S(1)}) custom-call(s32[5]{0:T(128)S(1)} %stack.24.where, f32[48,1536]{1,0:T(8,128)S(1)} %convert_add_fusion.1.refs_0_, f32[48,1536]{1,0:T(8,128)S(1)} %collective-permute-done.72.refs_1_, f32[48,3072]{1,0:T(8,128)S(1)} %get-tuple-element.290.refs_2_, ...), custom_call_target="tpu_custom_call" | custom-call | bytes 3639552 | tf_op jit(solution)/shard_map/seg_owner/pallas_call | solution.py:591
  (221 shorter events, 111.8 us)
Async XLA Ops:
  5.9 15.9 %collective-permute-start.2 = (bf16[48,1664]{1,0:T(8,128)(2,1)S(1)}, bf16[48,1664]{1,0:T(8,128)(2,1)S(1)}, u32[]{:S(2)}, u32[]{:S(2)}) collective-permute-start(bf16[48,1664]{1,0:T(8,128)(2,1)S(1)} %get-tuple-element.154.refs_0_), channel_id=1, source_target_pairs={{0,12},{1,13},{2,14},{3,15},{4,0},{5,1},{6,2},{7,3},{8,4},{9,5},{1... | collective-permute-start | bytes 479240 | tf_op jit(solution)/shard_map/ppermute | solution.py:565
  6.2 15.7 %collective-permute-start.1 = (bf16[48,1664]{1,0:T(8,128)(2,1)S(1)}, bf16[48,1664]{1,0:T(8,128)(2,1)S(1)}, u32[]{:S(2)}, u32[]{:S(2)}) collective-permute-start(bf16[48,1664]{1,0:T(8,128)(2,1)S(1)} %get-tuple-element.154.refs_0_), channel_id=1, source_target_pairs={{0,8},{1,9},{2,10},{3,11},{4,12},{5,13},{6,14},{7,15},{8,0},{9,1},... | collective-permute-start | bytes 479240 | tf_op jit(solution)/shard_map/ppermute | solution.py:565
  8.5 13.4 %collective-permute-start = (bf16[48,1664]{1,0:T(8,128)(2,1)S(1)}, bf16[48,1664]{1,0:T(8,128)(2,1)S(1)}, u32[]{:S(2)}, u32[]{:S(2)}) collective-permute-start(bf16[48,1664]{1,0:T(8,128)(2,1)S(1)} %get-tuple-element.154.refs_0_), channel_id=1, source_target_pairs={{0,4},{1,5},{2,6},{3,7},{4,8},{5,9},{6,10},{7,11},{8,12},{9,13},{1... | collective-permute-start | bytes 479240 | tf_op jit(solution)/shard_map/ppermute | solution.py:565
  21.9 14.7 %collective-permute-start.3 = (bf16[48,6656]{1,0:T(8,128)(2,1)S(1)}, bf16[48,6656]{1,0:T(8,128)(2,1)S(1)}, u32[]{:S(2)}, u32[]{:S(2)}) collective-permute-start(bf16[48,6656]{1,0:T(8,128)(2,1)S(1)} %constant_dynamic-update-slice_fusion), channel_id=1, source_target_pairs={{0,1},{1,0},{2,3},{3,2},{4,5},{5,4},{6,7},{7,6},{8,9},{9,8},{10,11... | collective-permute-start | bytes 1916936 | tf_op jit(solution)/shard_map/ppermute | solution.py:569
  25.9 15.5 %collective-permute-start.4 = (bf16[48,6656]{1,0:T(8,128)(2,1)S(1)}, bf16[48,6656]{1,0:T(8,128)(2,1)S(1)}, u32[]{:S(2)}, u32[]{:S(2)}) collective-permute-start(bf16[48,6656]{1,0:T(8,128)(2,1)S(1)} %constant_dynamic-update-slice_fusion), channel_id=1, source_target_pairs={{0,2},{1,3},{2,0},{3,1},{4,6},{5,7},{6,4},{7,5},{8,10},{9,11},{10,... | collective-permute-start | bytes 1916936 | tf_op jit(solution)/shard_map/ppermute | solution.py:569
  26.2 15.3 %collective-permute-start.9 = (bf16[48,1536]{1,0:T(8,128)(2,1)S(1)}, bf16[48,1536]{1,0:T(8,128)(2,1)S(1)}, u32[]{:S(2)}, u32[]{:S(2)}) collective-permute-start(bf16[48,1536]{1,0:T(8,128)(2,1)S(1)} %get-tuple-element.157.refs_0_), channel_id=1, source_target_pairs={{0,12},{1,13},{2,14},{3,15},{4,0},{5,1},{6,2},{7,3},{8,4},{9,5},{1... | collective-permute-start | bytes 442376 | tf_op jit(solution)/shard_map/ppermute | solution.py:565
  27.0 14.5 %collective-permute-start.8 = (bf16[48,1536]{1,0:T(8,128)(2,1)S(1)}, bf16[48,1536]{1,0:T(8,128)(2,1)S(1)}, u32[]{:S(2)}, u32[]{:S(2)}) collective-permute-start(bf16[48,1536]{1,0:T(8,128)(2,1)S(1)} %get-tuple-element.157.refs_0_), channel_id=1, source_target_pairs={{0,8},{1,9},{2,10},{3,11},{4,12},{5,13},{6,14},{7,15},{8,0},{9,1},... | collective-permute-start | bytes 442376 | tf_op jit(solution)/shard_map/ppermute | solution.py:565
  41.5 20.4 %collective-permute-start.15 = (bf16[48,9472]{1,0:T(8,128)(2,1)S(1)}, bf16[48,9472]{1,0:T(8,128)(2,1)S(1)}, u32[]{:S(2)}, u32[]{:S(2)}) collective-permute-start(bf16[48,9472]{1,0:T(8,128)(2,1)S(1)} %get-tuple-element.306), channel_id=1, source_target_pairs={{0,1},{1,0},{2,3},{3,2},{4,5},{5,4},{6,7},{7,6},{8,9},{9,8},{10,11... | collective-permute-start | bytes 2727944 | tf_op jit(solution)/shard_map/ppermute | solution.py:569
  41.9 20.1 %collective-permute-start.13 = (bf16[48,9472]{1,0:T(8,128)(2,1)S(1)}, bf16[48,9472]{1,0:T(8,128)(2,1)S(1)}, u32[]{:S(2)}, u32[]{:S(2)}) collective-permute-start(bf16[48,9472]{1,0:T(8,128)(2,1)S(1)} %get-tuple-element.307), channel_id=1, source_target_pairs={{0,2},{1,3},{2,0},{3,1},{4,6},{5,7},{6,4},{7,5},{8,10},{9,11},{10,... | collective-permute-start | bytes 2727944 | tf_op jit(solution)/shard_map/ppermute | solution.py:569
  42.3 19.8 %collective-permute-start.12 = (bf16[48,1536]{1,0:T(8,128)(2,1)S(1)}, bf16[48,1536]{1,0:T(8,128)(2,1)S(1)}, u32[]{:S(2)}, u32[]{:S(2)}) collective-permute-start(bf16[48,1536]{1,0:T(8,128)(2,1)S(1)} %get-tuple-element.158.refs_0_), channel_id=1, source_target_pairs={{0,12},{1,13},{2,14},{3,15},{4,0},{5,1},{6,2},{7,3},{8,4},{9,5},{1... | collective-permute-start | bytes 442376 | tf_op jit(solution)/shard_map/ppermute | solution.py:565
  44.1 18.0 %collective-permute-start.11 = (bf16[48,1536]{1,0:T(8,128)(2,1)S(1)}, bf16[48,1536]{1,0:T(8,128)(2,1)S(1)}, u32[]{:S(2)}, u32[]{:S(2)}) collective-permute-start(bf16[48,1536]{1,0:T(8,128)(2,1)S(1)} %get-tuple-element.158.refs_0_), channel_id=1, source_target_pairs={{0,8},{1,9},{2,10},{3,11},{4,12},{5,13},{6,14},{7,15},{8,0},{9,1},... | collective-permute-start | bytes 442376 | tf_op jit(solution)/shard_map/ppermute | solution.py:565
  45.7 16.3 %collective-permute-start.10 = (bf16[48,1536]{1,0:T(8,128)(2,1)S(1)}, bf16[48,1536]{1,0:T(8,128)(2,1)S(1)}, u32[]{:S(2)}, u32[]{:S(2)}) collective-permute-start(bf16[48,1536]{1,0:T(8,128)(2,1)S(1)} %get-tuple-element.158.refs_0_), channel_id=1, source_target_pairs={{0,4},{1,5},{2,6},{3,7},{4,8},{5,9},{6,10},{7,11},{8,12},{9,13},{1... | collective-permute-start | bytes 442376 | tf_op jit(solution)/shard_map/ppermute | solution.py:565
  62.1 23.7 %collective-permute-start.18 = (bf16[48,9216]{1,0:T(8,128)(2,1)S(1)}, bf16[48,9216]{1,0:T(8,128)(2,1)S(1)}, u32[]{:S(2)}, u32[]{:S(2)}) collective-permute-start(bf16[48,9216]{1,0:T(8,128)(2,1)S(1)} %get-tuple-element.298), channel_id=1, source_target_pairs={{0,2},{1,3},{2,0},{3,1},{4,6},{5,7},{6,4},{7,5},{8,10},{9,11},{10,... | collective-permute-start | bytes 2654216 | tf_op jit(solution)/shard_map/ppermute | solution.py:569
  62.8 23.0 %collective-permute-start.14 = (bf16[48,9216]{1,0:T(8,128)(2,1)S(1)}, bf16[48,9216]{1,0:T(8,128)(2,1)S(1)}, u32[]{:S(2)}, u32[]{:S(2)}) collective-permute-start(bf16[48,9216]{1,0:T(8,128)(2,1)S(1)} %get-tuple-element.299), channel_id=1, source_target_pairs={{0,1},{1,0},{2,3},{3,2},{4,5},{5,4},{6,7},{7,6},{8,9},{9,8},{10,11... | collective-permute-start | bytes 2654216 | tf_op jit(solution)/shard_map/ppermute | solution.py:569
  95.5 12.7 %collective-permute-start.33 = (bf16[48,4992]{1,0:T(8,128)(2,1)S(1)}, bf16[48,4992]{1,0:T(8,128)(2,1)S(1)}, u32[]{:S(2)}, u32[]{:S(2)}) collective-permute-start(bf16[48,4992]{1,0:T(8,128)(2,1)S(1)} %constant_dynamic-update-slice_fusion.20), channel_id=1, source_target_pairs={{0,1},{1,0},{2,3},{3,2},{4,5},{5,4},{6,7},{7,6},{8,9},{9,8},{10,11... | collective-permute-start | bytes 1437704 | tf_op jit(solution)/shard_map/ppermute | solution.py:569
  114.1 24.4 %collective-permute-start.39 = (bf16[16,48,1152]{2,1,0:T(8,128)(2,1)S(1)}, bf16[16,48,1152]{2,1,0:T(8,128)(2,1)S(1)}, u32[]{:S(2)}, u32[]{:S(2)}) collective-permute-start(bf16[16,48,1152]{2,1,0:T(8,128)(2,1)S(1)} %get-tuple-element.189.own), channel_id=1, source_target_pairs={{0,16},{16,0},{1,17},{17,1},{2,18},{18,2},{3,19},{19,3},{4,20},{20... | collective-permute-start | bytes 5308424 | tf_op jit(solution)/shard_map/ppermute | solution.py:573
  128.5 20.7 %collective-permute-start.46 = (bf16[2,48,3072]{2,1,0:T(8,128)(2,1)S(1)}, bf16[2,48,3072]{2,1,0:T(8,128)(2,1)S(1)}, u32[]{:S(2)}, u32[]{:S(2)}) collective-permute-start(bf16[2,48,3072]{2,1,0:T(8,128)(2,1)S(1)} %get-tuple-element.207), channel_id=1, source_target_pairs={{0,2},{1,3},{2,0},{3,1},{4,6},{5,7},{6,4},{7,5},{8,10},{9,11},{10,... | collective-permute-start | bytes 1769480 | tf_op jit(solution)/shard_map/ppermute | solution.py:569
  129.6 19.6 %collective-permute-start.47 = (bf16[2,48,3072]{2,1,0:T(8,128)(2,1)S(1)}, bf16[2,48,3072]{2,1,0:T(8,128)(2,1)S(1)}, u32[]{:S(2)}, u32[]{:S(2)}) collective-permute-start(bf16[2,48,3072]{2,1,0:T(8,128)(2,1)S(1)} %get-tuple-element.211), channel_id=1, source_target_pairs={{0,1},{1,0},{2,3},{3,2},{4,5},{5,4},{6,7},{7,6},{8,9},{9,8},{10,11... | collective-permute-start | bytes 1769480 | tf_op jit(solution)/shard_map/ppermute | solution.py:569
  150.0 36.4 %collective-permute-start.58 = (bf16[4,48,3072]{2,1,0:T(8,128)(2,1)S(1)}, bf16[4,48,3072]{2,1,0:T(8,128)(2,1)S(1)}, u32[]{:S(2)}, u32[]{:S(2)}) collective-permute-start(bf16[4,48,3072]{2,1,0:T(8,128)(2,1)S(1)} %get-tuple-element.215), channel_id=1, source_target_pairs={{0,1},{1,0},{2,3},{3,2},{4,5},{5,4},{6,7},{7,6},{8,9},{9,8},{10,11... | collective-permute-start | bytes 3538952 | tf_op jit(solution)/shard_map/ppermute | solution.py:569
  151.2 35.2 %collective-permute-start.59 = (bf16[4,48,3072]{2,1,0:T(8,128)(2,1)S(1)}, bf16[4,48,3072]{2,1,0:T(8,128)(2,1)S(1)}, u32[]{:S(2)}, u32[]{:S(2)}) collective-permute-start(bf16[4,48,3072]{2,1,0:T(8,128)(2,1)S(1)} %get-tuple-element.216), channel_id=1, source_target_pairs={{0,2},{1,3},{2,0},{3,1},{4,6},{5,7},{6,4},{7,5},{8,10},{9,11},{10,... | collective-permute-start | bytes 3538952 | tf_op jit(solution)/shard_map/ppermute | solution.py:569
  187.4 14.3 %collective-permute-start.62 = (bf16[64,3072]{1,0:T(8,128)(2,1)S(1)}, bf16[64,3072]{1,0:T(8,128)(2,1)S(1)}, u32[]{:S(2)}, u32[]{:S(2)}) collective-permute-start(bf16[64,3072]{1,0:T(8,128)(2,1)S(1)} %get-tuple-element.266), channel_id=1, source_target_pairs={{0,12},{1,13},{2,14},{3,15},{4,0},{5,1},{6,2},{7,3},{8,4},{9,5},{1... | collective-permute-start | bytes 1179656 | tf_op jit(solution)/shard_map/ppermute | solution.py:565
  191.7 26.1 %collective-permute-start.66 = (bf16[64,3072]{1,0:T(8,128)(2,1)S(1)}, bf16[64,3072]{1,0:T(8,128)(2,1)S(1)}, u32[]{:S(2)}, u32[]{:S(2)}) collective-permute-start(bf16[64,3072]{1,0:T(8,128)(2,1)S(1)} %get-tuple-element.277), channel_id=1, source_target_pairs={{0,8},{1,9},{2,10},{3,11},{4,12},{5,13},{6,14},{7,15},{8,0},{9,1},... | collective-permute-start | bytes 1179656 | tf_op jit(solution)/shard_map/ppermute | solution.py:565
  201.6 15.4 %collective-permute-start.63 = (bf16[2,48,1536]{2,1,0:T(8,128)(2,1)S(1)}, bf16[2,48,1536]{2,1,0:T(8,128)(2,1)S(1)}, u32[]{:S(2)}, u32[]{:S(2)}) collective-permute-start(bf16[2,48,1536]{2,1,0:T(8,128)(2,1)S(1)} %get-tuple-element.267), channel_id=1, source_target_pairs={{0,2},{1,3},{2,0},{3,1},{4,6},{5,7},{6,4},{7,5},{8,10},{9,11},{10,... | collective-permute-start | bytes 884744 | tf_op jit(solution)/shard_map/ppermute | solution.py:569
  202.7 14.3 %collective-permute-start.65 = (bf16[2,48,1536]{2,1,0:T(8,128)(2,1)S(1)}, bf16[2,48,1536]{2,1,0:T(8,128)(2,1)S(1)}, u32[]{:S(2)}, u32[]{:S(2)}) collective-permute-start(bf16[2,48,1536]{2,1,0:T(8,128)(2,1)S(1)} %get-tuple-element.272), channel_id=1, source_target_pairs={{0,1},{1,0},{2,3},{3,2},{4,5},{5,4},{6,7},{7,6},{8,9},{9,8},{10,11... | collective-permute-start | bytes 884744 | tf_op jit(solution)/shard_map/ppermute | solution.py:569
  203.0 14.1 %collective-permute-start.64 = (bf16[24,768]{1,0:T(8,128)(2,1)S(1)}, bf16[24,768]{1,0:T(8,128)(2,1)S(1)}, u32[]{:S(2)}, u32[]{:S(2)}) collective-permute-start(bf16[24,768]{1,0:T(8,128)(2,1)S(1)} %get-tuple-element.269), channel_id=1, source_target_pairs={{0,4},{1,5},{2,6},{3,7},{4,8},{5,9},{6,10},{7,11},{8,12},{9,13},{1... | collective-permute-start | bytes 110600 | tf_op jit(solution)/shard_map/ppermute | solution.py:565
  217.7 14.5 %collective-permute-start.68 = (bf16[4,48,1536]{2,1,0:T(8,128)(2,1)S(1)}, bf16[4,48,1536]{2,1,0:T(8,128)(2,1)S(1)}, u32[]{:S(2)}, u32[]{:S(2)}) collective-permute-start(bf16[4,48,1536]{2,1,0:T(8,128)(2,1)S(1)} %get-tuple-element.280), channel_id=1, source_target_pairs={{0,2},{1,3},{2,0},{3,1},{4,6},{5,7},{6,4},{7,5},{8,10},{9,11},{10,... | collective-permute-start | bytes 1769480 | tf_op jit(solution)/shard_map/ppermute | solution.py:569
  218.8 14.1 %collective-permute-start.67 = (bf16[4,48,1536]{2,1,0:T(8,128)(2,1)S(1)}, bf16[4,48,1536]{2,1,0:T(8,128)(2,1)S(1)}, u32[]{:S(2)}, u32[]{:S(2)}) collective-permute-start(bf16[4,48,1536]{2,1,0:T(8,128)(2,1)S(1)} %get-tuple-element.278), channel_id=1, source_target_pairs={{0,1},{1,0},{2,3},{3,2},{4,5},{5,4},{6,7},{7,6},{8,9},{9,8},{10,11... | collective-permute-start | bytes 1769480 | tf_op jit(solution)/shard_map/ppermute | solution.py:569
  219.1 17.8 %collective-permute-start.78 = (bf16[64,3072]{1,0:T(8,128)(2,1)S(1)}, bf16[64,3072]{1,0:T(8,128)(2,1)S(1)}, u32[]{:S(2)}, u32[]{:S(2)}) collective-permute-start(bf16[64,3072]{1,0:T(8,128)(2,1)S(1)} %get-tuple-element.286), channel_id=1, source_target_pairs={{0,4},{1,5},{2,6},{3,7},{4,8},{5,9},{6,10},{7,11},{8,12},{9,13},{1... | collective-permute-start | bytes 1179656 | tf_op jit(solution)/shard_map/ppermute | solution.py:565
  240.8 12.9 %collective-permute-start.71 = (bf16[48,1536]{1,0:T(8,128)(2,1)S(1)}, bf16[48,1536]{1,0:T(8,128)(2,1)S(1)}, u32[]{:S(2)}, u32[]{:S(2)}) collective-permute-start(bf16[48,1536]{1,0:T(8,128)(2,1)S(1)} %get-tuple-element.284), channel_id=1, source_target_pairs={{0,12},{1,13},{2,14},{3,15},{4,0},{5,1},{6,2},{7,3},{8,4},{9,5},{1... | collective-permute-start | bytes 442376 | tf_op jit(solution)/shard_map/ppermute | solution.py:565
  241.9 15.5 %collective-permute-start.61 = (f32[128,768]{1,0:T(8,128)S(1)}, f32[128,768]{1,0:T(8,128)S(1)}, u32[]{:S(2)}, u32[]{:S(2)}) collective-permute-start(f32[128,768]{1,0:T(8,128)S(1)} %get-tuple-element.261), channel_id=1, source_target_pairs={{0,16},{16,0},{1,17},{17,1},{2,18},{18,2},{3,19},{19,3},{4,20},{20... | collective-permute-start | bytes 1179656 | tf_op jit(solution)/shard_map/ppermute | solution.py:573
  245.0 13.2 %collective-permute-start.81 = (bf16[16,12288]{1,0:T(8,128)(2,1)S(1)}, bf16[16,12288]{1,0:T(8,128)(2,1)S(1)}, u32[]{:S(2)}, u32[]{:S(2)}) collective-permute-start(bf16[16,12288]{1,0:T(8,128)(2,1)S(1)} %head_rows.1.refs_0_), channel_id=1, source_target_pairs={{0,16},{16,0},{1,17},{17,1},{2,18},{18,2},{3,19},{19,3},{4,20},{20... | collective-permute-start | bytes 1179656 | tf_op jit(solution)/shard_map/ppermute | solution.py:573
  247.2 14.8 %collective-permute-start.79 = (f32[48,3072]{1,0:T(8,128)S(1)}, f32[48,3072]{1,0:T(8,128)S(1)}, u32[]{:S(2)}, u32[]{:S(2)}) collective-permute-start(f32[48,3072]{1,0:T(8,128)S(1)} %get-tuple-element.290.refs_2_), channel_id=1, source_target_pairs={{0,16},{16,0},{1,17},{17,1},{2,18},{18,2},{3,19},{19,3},{4,20},{20... | collective-permute-start | bytes 1769480 | tf_op jit(solution)/shard_map/ppermute | solution.py:573
  (56 other events, 338.6 us)

commit v5 on v4

--- a/solution.py
+++ b/solution.py
@@ -676,9 +676,9 @@
 
 def prepare_rest_kernel(where, seg, cls, *refs):
     second_out, third_out = refs[:2]
-    step_outs, out_half = refs[2 : 2 + LINE], refs[2 + LINE]
-    quarters, sems = refs[3 + LINE :]
-    line_at, core_at = where[0], where[2]
+    step_outs, out_half, order_out = refs[2 : 2 + LINE], refs[2 + LINE], refs[3 + LINE]
+    quarters, sems = refs[4 + LINE :]
+    line_at, plane_at, core_at = where[0], where[1], where[2]
     start = core_at * FF_HALF
     pairs = [
         (seg.at[:, pl.ds(aligned(4 * MODEL + start), FF_HALF)], second_out),
@@ -704,6 +704,15 @@
     lanes = pl.ds(aligned(core_at * QUARTER_HALF), QUARTER_HALF)
     for step, out in enumerate(step_outs):
         out[...] = quarters[(line_at + step) % LINE, :, lanes]
+    column = lax.broadcasted_iota(jnp.int32, (1, SPAN), 1)
+    feature = lax.broadcasted_iota(jnp.int32, (MODEL, SPAN), 0)
+    turn = sum((column >= OWN * step).astype(jnp.int32) for step in range(1, LINE))
+    held = column - OWN * turn
+    turn = (line_at + turn) % LINE
+    for mask in range(PLANE):
+        source = (turn * PLANE + (plane_at ^ mask)) * OWN + held
+        source = jnp.where(column < OWN * LINE, source, -1)
+        order_out[:, mask * SPAN : (mask + 1) * SPAN] = (feature == source).astype(LOW)
 
 
 def lane_mask(rows, head):
@@ -774,9 +783,9 @@
 
 def qkv_kernel(where, *refs):
     blocks = refs[:8]
-    hidden, hidden_got, live_row, live_got = refs[8:12]
-    weight_out, out_half, qkv_out, mixed_out, vectors_out, count_out = refs[12:18]
-    vec_rows, flat, inputs, weight, sem = refs[18:]
+    hidden, hidden_got, live_row, live_got, order = refs[8:13]
+    weight, out_half, qkv_out, mixed_out, vectors_out, count_out, ordered_out = refs[13:20]
+    vec_rows, flat, inputs = refs[20:]
     core_at = where[2]
     gather_blocks(
         where,
@@ -789,8 +798,6 @@
             (vec_rows, 4 * HALF, 4 * HALF + LANES),
         ),
     )
-    stored = pltpu.make_async_copy(weight, weight_out, sem)
-    stored.start()
     piece = (8 * MODEL + FF) // GROUP
     lines = -(-piece // LANES)
     count = jnp.zeros((1, LANES), WIDE)
@@ -821,7 +828,7 @@
         tiles = attend_tiles(qkv_out[rows, :], HALF, token_allowed(live[...]))
         for tile, value in enumerate(tiles):
             mixed_out[rows, tile * LANES : (tile + 1) * LANES] = value
-    stored.wait()
+    ordered_out[...] = product_plain(inputs[...], order[...]).astype(LOW)
 
 
 def norm_rows(summed):
@@ -852,14 +859,12 @@
     return before * half, slope
 
 
-def out_kernel(where, hidden, mixed, mixed_got, half, half_got, vectors, *outs):
-    full_store, mixed_full, normed_out, inv_out, low_out, full_out, sem = outs
+def out_kernel(where, hidden, mixed, mixed_got, half, half_got, vectors, order, *outs):
+    full_out, ordered_out, normed_out, inv_out, low_out, mixed_full = outs
     core_at = where[2]
     own, other = aligned(core_at * HALF), aligned((1 - core_at) * HALF)
     full_out[:, pl.ds(own, HALF)] = half[...]
     full_out[:, pl.ds(other, HALF)] = half_got[...]
-    stored = pltpu.make_async_copy(full_out, full_store, sem)
-    stored.start()
     mixed_full[:, pl.ds(own, HALF)] = mixed[...]
     mixed_full[:SEG, pl.ds(other, HALF)] = mixed_got[SEG:, :]
     mixed_full[SEG:, pl.ds(other, HALF)] = mixed_got[:SEG, :]
@@ -868,18 +873,17 @@
     normed_out[...] = normed
     inv_out[...] = inv_dev
     low_out[...] = (normed * vectors[4:5, :] + vectors[5:6, :]).astype(LOW)
-    stored.wait()
+    ordered_out[...] = product_plain(mixed_full[...], order[...]).astype(LOW)
 
 
 def up_kernel(where, *refs):
     blocks = refs[:8]
     low, low_got, vectors = refs[8:11]
-    weight, act_out, slope_store, both, slope_out, sems = refs[11:]
+    weight, act_out, slope_out, both = refs[11:]
     core_at = where[2]
     gather_blocks(where, blocks, 2 * (4 * HALF + LANES), FF_HALF, ((weight, 0, FF_HALF),))
     both[:SEG] = low[...]
     both[SEG:] = low_got[...]
-    stored = []
     for at in range(FF_HALF // MODEL):
         columns = slice(at * MODEL, (at + 1) * MODEL)
         held = weight[:, :, columns]
@@ -888,25 +892,15 @@
         value, slope = gelu_both(before + bias)
         act_out[:, columns] = value.astype(LOW)
         slope_out[:, columns] = slope
-        stored.append(
-            pltpu.make_async_copy(
-                slope_out.at[:, columns], slope_store.at[:, columns], sems.at[at]
-            )
-        )
-        stored[-1].start()
-    wait_all(stored)
 
 
 def down_kernel(where, *refs):
     blocks, act = refs[:8], refs[8]
-    store, own_out, send_out, weight, sem = refs[9:]
+    weight, own_out, send_out = refs[9:]
     gather_blocks(where, blocks, 2 * FF_HALF, FF_HALF, ((weight, 0, FF_HALF),))
-    stored = pltpu.make_async_copy(weight, store, sem)
-    stored.start()
     partial = product_right(act[...], whole_rows(weight))
     own_out[...] = partial[:SEG]
     send_out[...] = partial[SEG:]
-    stored.wait()
 
 
 def seg_rows_kernel(where, *refs):
@@ -1004,23 +998,34 @@
     scatter_parts(where, parts, outs, sems)
 
 
-def attn_weight_kernel(where, *refs):
-    hidden, hidden_got, mixed, proj, branch, got = refs[:6]
-    outs = refs[6:11]
-    left, right, parts, sems = refs[11:]
-    core_at = where[2]
-    left[:SEG] = hidden[...]
-    left[SEG:] = hidden_got[...]
-    right[:SEG] = branch[:, pl.ds(aligned(core_at * HALF), HALF)]
-    right[SEG:] = got[:, HALF:]
+def attn_product(where, refs, mask, piece):
+    hidden, mixed, proj, branch, got = refs
+    lanes = slice(mask * SPAN, (mask + 1) * SPAN)
+    if piece < 3:
+        right = proj[:, piece * HALF : (piece + 1) * HALF]
+        product = product_left(hidden[:, lanes], right)
+    else:
+        own = branch[:, pl.ds(aligned(where[2] * HALF), HALF)]
+        product = product_left(mixed[:SEG, lanes], own)
+        product = product + product_left(mixed[SEG:, lanes], got[:, HALF:])
+    return product[: LINE * OWN].astype(LOW).reshape(LINE, OWN, HALF)
+
+
+def attn_far_kernel(where, *refs):
+    low_out, high_out = refs[5:]
+    half = LINE // 2
     for piece in range(4):
-        start = piece * HALF
-        if piece < 3:
-            product = product_left(left[...], proj[:, start : start + HALF])
-        else:
-            product = product_left(mixed[...], right[...])
-        parts[:, :, start : start + HALF] = product.astype(LOW).reshape(GROUP, OWN, HALF)
-    scatter_parts(where, parts, outs, sems)
+        columns = slice(piece * HALF, (piece + 1) * HALF)
+        product = attn_product(where, refs[:5], 3, piece)
+        low_out[:, :, columns] = product[:half]
+        high_out[:, :, columns] = product[half:]
+
+
+def attn_near_kernel(where, *refs):
+    for mask, out in ((1, refs[5]), (2, refs[6]), (0, refs[7])):
+        for piece in range(4):
+            columns = slice(piece * HALF, (piece + 1) * HALF)
+            out[:, :, columns] = attn_product(where, refs[:5], mask, piece)
 
 
 def fold_kernel(where, kept, got_x, got_y, *refs):
@@ -1442,24 +1447,50 @@
     vecs_out[...] = product_plain(hot, rows[...])
 
 
-def seg_owner_kernel(where, *refs):
-    attn, attn_got, mlp, mlp_got, vecs, vecs_got, mats_out, vec_out, flat = refs
-    core_at = where[2]
+def seg_vec_kernel(where, vecs, vecs_got, vec_out, flat):
     rank = where[0] * PLANE + where[1]
     rows = (8 * MODEL + FF) // MODEL
     pieces = [vecs[at : at + 1, :] + vecs_got[at : at + 1, :] for at in range(rows)]
     own_vector(rank, pieces, vec_out, flat)
 
-    def put(base, size, own, got):
-        mats_out[:, pl.ds(aligned(base + core_at * size), size)] = own
-        mats_out[:, pl.ds(aligned(base + (1 - core_at) * size), size)] = got
-
+
+def column_copies(where, out, base, size, own, got, first):
+    core_at = where[2]
+    lanes = slice(first, first + size)
+    return [
+        (own.at[:, lanes], out.at[:, pl.ds(aligned(base + core_at * size), size)]),
+        (got.at[:, lanes], out.at[:, pl.ds(aligned(base + (1 - core_at) * size), size)]),
+    ]
+
+
+def mlp_store_kernel(where, mlp, mlp_got, out, sems):
+    pairs = []
+    for piece in range(2):
+        base = 4 * MODEL + piece * FF
+        pairs += column_copies(where, out, base, FF_HALF, mlp, mlp_got, piece * FF_HALF)
+    run_copies(pairs, sems)
+
+
+def attn_store_kernel(where, attn, attn_got, filled, out, sems):
+    pairs = []
     for piece in range(4):
-        columns = slice(piece * HALF, (piece + 1) * HALF)
-        put(piece * MODEL, HALF, attn[:, columns], attn_got[:, columns])
-    for piece in range(2):
-        columns = slice(piece * FF_HALF, (piece + 1) * FF_HALF)
-        put(4 * MODEL + piece * FF, FF_HALF, mlp[:, columns], mlp_got[:, columns])
+        pairs += column_copies(where, out, piece * MODEL, HALF, attn, attn_got, piece * HALF)
+    run_copies(pairs, sems)
+
+
+def store_attn(where, attn, attn_got, filled):
+    far = pl.BlockSpec(memory_space=pl.ANY)
+    near = pl.BlockSpec(memory_space=pltpu.VMEM)
+    return pl.pallas_call(
+        attn_store_kernel,
+        name="seg_attn_store",
+        out_shape=shape_of(filled.shape),
+        in_specs=[pl.BlockSpec(memory_space=pltpu.SMEM), near, near, far],
+        out_specs=far,
+        scratch_shapes=[pltpu.SemaphoreType.DMA((8,))],
+        input_output_aliases={3: 0},
+        compiler_params=pltpu.CompilerParams(vmem_limit_bytes=VMEM_BYTES),
+    )(where, attn, attn_got, filled)
 
 
 def plane_parts(part):
@@ -1505,7 +1536,7 @@
         "prepare_rest",
         [shape_of((own_rows, FF_HALF), LOW)] * 2
         + [shape_of((own_rows, QUARTER_HALF), LOW)] * LINE
-        + [shape_of((own_rows, HALF), LOW)],
+        + [shape_of((own_rows, HALF), LOW), shape_of((MODEL, PLANE * SPAN), LOW)],
         where,
         (seg_mats, cls_mats),
         (),
@@ -1514,7 +1545,13 @@
             pltpu.SemaphoreType.DMA((3 + 5 * LINE,)),
         ],
     )
-    second_piece, third_piece, quarters, cls_out_piece = rest[0], rest[1], rest[2:-1], rest[-1]
+    second_piece, third_piece, quarters, cls_out_piece, order = (
+        rest[0],
+        rest[1],
+        rest[2:-2],
+        rest[-2],
+        rest[-1],
+    )
 
     def joined(*pieces):
         return jnp.concatenate(pieces, axis=1)
@@ -1523,7 +1560,7 @@
         return in_plane(to_x, 1), in_plane(to_y, 2)
 
     hidden_got, live_got = other_core(hidden_in), other_core(live_row)
-    first_sent = joined(*first_line)
+    first_sent = after(joined(*first_line), second_piece)
     first_x, first_y = sent_both(first_sent, first_sent)
     second_line = line_parts(after(second_piece, hidden_got, live_got, *first_line[1:]))
     size = 2 * first_columns
@@ -1541,7 +1578,7 @@
         for apart in range(1, LINE)
     )
 
-    qkv_weight, out_half, qkv, mixed, vectors, count = run_kernel(
+    qkv_weight, out_half, qkv, mixed, vectors, count, hidden_ordered = run_kernel(
         qkv_kernel,
         "seg_qkv",
         [
@@ -1551,39 +1588,36 @@
             shape_of((both_rows, HALF), LOW),
             shape_of((2 * (8 * MODEL + FF) // MODEL, MODEL)),
             shape_of((8, LANES)),
+            shape_of((both_rows, PLANE * SPAN), LOW),
         ],
         where,
         (),
         first_line
         + (first_x, first_y, second_x, second_y)
-        + (hidden_in, hidden_got, live_row, live_got),
+        + (hidden_in, hidden_got, live_row, live_got, order),
         [
             pltpu.VMEM((GROUP, own_rows, LANES), LOW),
             pltpu.VMEM((2, 8 * MODEL + FF), WIDE),
             pltpu.VMEM((both_rows, MODEL), LOW),
-            pltpu.VMEM((GROUP, own_rows, 3 * HALF), LOW),
-            pltpu.SemaphoreType.DMA(()),
         ],
-        far=(0,),
         flops=2 * SEG * MODEL * 3 * MODEL,
     )
     count = count + other_core(count)
     out_half = out_half.reshape(MODEL, HALF)
-    out_weight, mixed_full, normed_first, inv_first, first_low = run_kernel(
+    out_weight, mixed_ordered, normed_first, inv_first, first_low = run_kernel(
         out_kernel,
         "seg_out",
         [
             shape_of((MODEL, MODEL), LOW),
-            shape_of((both_rows, MODEL), LOW),
+            shape_of((both_rows, PLANE * SPAN), LOW),
             shape_of((SEG, MODEL)),
             shape_of((SEG, 1)),
             shape_of((SEG, MODEL), LOW),
         ],
         where,
         (),
-        (hidden_in, mixed, other_core(mixed), out_half, other_core(out_half), vectors),
-        [pltpu.VMEM((MODEL, MODEL), LOW), pltpu.SemaphoreType.DMA(())],
-        far=(0,),
+        (hidden_in, mixed, other_core(mixed), out_half, other_core(out_half), vectors, order),
+        [pltpu.VMEM((both_rows, MODEL), LOW)],
         flops=2 * SEG * MODEL * MODEL,
     )
     first_got = after(other_core(first_low), count)
@@ -1601,12 +1635,7 @@
         second_line
         + (second_x, second_y, third_x, third_y)
         + (first_low, first_got, vectors),
-        [
-            pltpu.VMEM((both_rows, MODEL), LOW),
-            pltpu.VMEM((both_rows, FF_HALF), WIDE),
-            pltpu.SemaphoreType.DMA((FF_HALF // MODEL,)),
-        ],
-        far=(2,),
+        [pltpu.VMEM((both_rows, MODEL), LOW)],
         flops=2 * SEG * MODEL * FF,
     )
     fourth_x, fourth_y = sent_both(third_y[:, 2 * size :], third_x[:, size : 2 * size])
@@ -1625,8 +1654,6 @@
         where,
         (),
         third_line + (third_x, third_y, fourth_x, fourth_y) + (act,),
-        [pltpu.VMEM((GROUP, own_rows, FF_HALF), LOW), pltpu.SemaphoreType.DMA(())],
-        far=(0,),
         flops=2 * SEG * MODEL * FF,
     )
     normed_second, inv_second, diff, out_rows, head_row = run_kernel(
@@ -1666,6 +1693,8 @@
         (),
         (diff, count, normed_second, inv_second, vectors),
     )
+    second_got = other_core(second_low)
+    cls_far = tuple(after(got, second_got, *head_lines[1:]) for got in cls_far)
     cls_half, cls_out_half = run_kernel(
         cls_gather_kernel,
         "head_gather",
@@ -1677,7 +1706,7 @@
         (),
         cls_line + (cls_x, cls_y) + cls_far + (cls_out_piece,),
     )
-    second_got = after(other_core(second_low), head_lines[2], head_lines[3], cls_half)
+    second_got = after(second_got, cls_half)
     pre, first_grad_own, first_grad_send, up_sums = run_kernel(
         mlp_back_kernel,
         "seg_mlp_back",
@@ -1798,6 +1827,11 @@
         + line_parts(part)
         + (vectors, cls_weight, cls_out, cls_grad, cls_normed, cls_inv, cls_qkv),
     )
+    end_parts = line_parts(part)
+    pack = jnp.concatenate([cls_proj, cls_mixed, cls_pre, cls_act], axis=1)
+    mlp_plane = [after(got, *end_parts[1:]) for got in mlp_plane]
+    mlp_own, *mlp_sent = reduce_fold(where, mlp_parts[4], mlp_plane, pack)
+    mlp_got = [along_line(mlp_sent[apart - 1], apart) for apart in range(1, LINE)]
     dheads, head_grad, shared = run_kernel(
         cls_end_kernel,
         "head_end",
@@ -1805,7 +1839,8 @@
         where,
         (),
         (heads, cls_grad)
-        + line_parts(part)
+        + (after(end_parts[0], mlp_own),)
+        + end_parts[1:]
         + (square, back_sums, top_sums, normed_second, inv_second, vectors),
         [pltpu.VMEM((GROUP, MODEL), WIDE)],
     )
@@ -1852,12 +1887,7 @@
             out_weight,
         ),
     )
-    pack = jnp.concatenate([cls_proj, cls_mixed, cls_pre, cls_act], axis=1)
-    mlp_plane = [after(got, branch) for got in mlp_plane]
-    mlp_own, *mlp_sent = reduce_fold(where, mlp_parts[4], mlp_plane, pack)
-    mlp_got = [along_line(mlp_sent[apart - 1], apart) for apart in range(1, LINE)]
-    shared = shared + other_core(shared)
-    attn_got = after(other_core(attn_send), mlp_own, shared)
+    attn_got = after(other_core(attn_send), mlp_own)
     proj, input_own, input_send, payload = run_kernel(
         attn_back_kernel,
         "seg_attn_back",
@@ -1886,32 +1916,50 @@
         [pltpu.VMEM((24, MODEL), WIDE)],
         flops=4 * SEG * MODEL * 3 * MODEL,
     )
-    attn_parts = run_kernel(
-        attn_weight_kernel,
-        "seg_attn_weight",
-        part_shapes(4 * HALF),
-        where,
-        (),
-        (hidden_in, hidden_got, mixed_full, proj, branch, attn_got),
-        [
-            pltpu.VMEM((both_rows, MODEL), LOW),
-            pltpu.VMEM((both_rows, HALF), LOW),
-            pltpu.VMEM((GROUP, own_rows, 4 * HALF), LOW),
-            pltpu.SemaphoreType.DMA((GROUP,)),
-        ],
-        far=range(5),
-        flops=4 * SEG * MODEL * 2 * MODEL,
-    )
-    attn_far = reduce_far(tuple(after(part, mlp_got[-1]) for part in attn_parts[:2]))
+    attn_data = (hidden_ordered, mixed_ordered, proj, branch, attn_got)
+    attn_far = run_kernel(
+        attn_far_kernel,
+        "seg_attn_far",
+        part_shapes(4 * HALF)[:2],
+        where,
+        (),
+        attn_data,
+        flops=SEG * MODEL * 2 * MODEL,
+    )
+    attn_far = reduce_far(tuple(after(part, mlp_got[-1]) for part in attn_far))
+    attn_near = run_kernel(
+        attn_near_kernel,
+        "seg_attn_near",
+        part_shapes(4 * HALF)[2:],
+        where,
+        (),
+        attn_data,
+        flops=3 * SEG * MODEL * 2 * MODEL,
+    )
     input_grad = (grad_summed + input_own + other_core(input_send)).astype(LOW)
     row_at = jnp.arange(SEG)[:, None]
     output = jnp.where(row_at == 0, top_row * live_row[:, :1], out_rows).astype(LOW)
-    payload_parts = line_parts(after(payload, attn_parts[0]))
+    payload_parts = line_parts(after(payload, attn_near[0]))
     attn_far = tuple(after(got, payload_parts[1]) for got in attn_far)
-    attn_sent = reduce_add(where, attn_parts, attn_far)
+    attn_sent = reduce_add(where, (None, None) + tuple(attn_near), attn_far)
     attn_plane = sent_both(*(after(part, mlp_got[1]) for part in attn_sent))
     mlp_got = [after(got, attn_plane[0]) for got in mlp_got]
     mlp_sum = reduce_line(mlp_own, mlp_got)
+    shared = after(shared, attn_sent[0])
+    shared = shared + other_core(shared)
+    row_width = 8 * MODEL + 2 * FF
+    cls_rows = run_kernel(
+        cls_rows_kernel,
+        "head_rows",
+        [shape_of((GROUP, row_width), LOW)],
+        where,
+        (),
+        (pack,) + tuple(mlp_got) + (heads, cls_branch, cls_low, cls_second),
+        [pltpu.VMEM((LINE,) + pack.shape, LOW)],
+    )[0]
+    attn_plane = tuple(after(got, cls_rows) for got in attn_plane)
+    attn_own, *attn_sent = reduce_fold(where, attn_near[2], attn_plane)
+    attn_lines = [along_line(attn_sent[apart - 1], apart) for apart in range(1, LINE)]
     payload_line = jnp.concatenate(payload_parts)
     mlp_mine, own_vecs = run_kernel(
         head_share_kernel,
@@ -1919,55 +1967,58 @@
         [shape_of((own_rows, FF)), shape_of((16, MODEL))],
         where,
         (),
-        plane_parts(after(payload_line, *attn_plane)) + (mlp_sum,),
+        tuple(
+            after(got, attn_lines[0]) for got in plane_parts(after(payload_line, *attn_plane))
+        )
+        + (mlp_sum,),
         [pltpu.VMEM((GROUP * 24, MODEL), LOW)],
     )
-    attn_own, *attn_sent = reduce_fold(where, attn_parts[4], attn_plane)
-    attn_sum = reduce_line(
-        attn_own, [along_line(attn_sent[apart - 1], apart) for apart in range(1, LINE)]
-    )
     flat = pltpu.VMEM((1, 8 * MODEL + FF), WIDE)
-    seg_mats_grad, seg_vec_grad = run_kernel(
-        seg_owner_kernel,
-        "seg_owner",
-        [shape_of((own_rows, total_columns)), shape_of((1, vec_size))],
-        where,
-        (),
-        (attn_sum, other_core(attn_sum), mlp_mine, other_core(mlp_mine))
-        + (own_vecs, other_core(own_vecs)),
+    seg_vec_grad = run_kernel(
+        seg_vec_kernel,
+        "seg_vector",
+        [shape_of((1, vec_size))],
+        where,
+        (),
+        (own_vecs, other_core(own_vecs)),
         [flat],
-    )
-
-    row_width = 8 * MODEL + 2 * FF
-    cls_rows = run_kernel(
-        cls_rows_kernel,
-        "head_rows",
-        [shape_of((GROUP, row_width), LOW)],
-        where,
-        (),
-        (pack,) + tuple(mlp_got) + (heads, cls_branch, cls_low, cls_second),
-        [pltpu.VMEM((LINE,) + pack.shape, LOW)],
+    )[0].reshape(vec_size)
+    seg_mats_grad = run_kernel(
+        mlp_store_kernel,
+        "seg_mlp_store",
+        [shape_of((own_rows, total_columns))],
+        where,
+        (),
+        (mlp_mine, other_core(mlp_mine)),
+        [pltpu.SemaphoreType.DMA((4,))],
+        far=(0,),
     )[0]
+
     cls_mats_grad, cls_vec_grad = run_kernel(
         cls_owner_kernel,
         "head_owner",
         [shape_of((own_rows, total_columns)), shape_of((1, vec_size))],
         where,
         (),
-        (cls_rows, other_core(cls_rows), shared),
+        (cls_rows, other_core(cls_rows), after(shared, attn_lines[1])),
         [pltpu.VMEM((CORES * GROUP, row_width), LOW), flat],
         flops=64 * own_rows * total_columns,
     )
+    cls_vec_grad = cls_vec_grad.reshape(vec_size)
     pos_total = shared[:GROUP]
     loss_value = shared[GROUP, 0] / (count[0, 0] * MODEL)
+    ready = (output, input_grad, cls_mats_grad, cls_vec_grad, pos_total, seg_vec_grad)
+    attn_lines[-1] = after(attn_lines[-1], seg_mats_grad, *ready)
+    attn_sum = reduce_line(attn_own, attn_lines)
+    seg_mats_grad = store_attn(where, attn_sum, other_core(attn_sum), seg_mats_grad)
 
     return (
         output,
         input_grad,
         seg_mats_grad,
-        seg_vec_grad.reshape(vec_size),
+        seg_vec_grad,
         cls_mats_grad,
-        cls_vec_grad.reshape(vec_size),
+        cls_vec_grad,
         pos_total,
         loss_value,
     )

time: 267 us -> 259 us (0.970)
  waiting for transfers between devices: 101 us -> 88.6 us
  starting transfers between devices: 101 us -> 105 us
    ppermute x36, waiting for transfers between devices: 53.2 us -> 45.3 us  [along_line(): return lax.ppermute(value, 'fsdp', line_pairs(apart))]
    ppermute x26, waiting for transfers between devices: 40.8 us -> 35.5 us  [in_plane(): return lax.ppermute(value, 'fsdp', plane_pairs(mask))]
    ppermute x36, starting transfers between devices: 50.2 us -> 54.1 us  [along_line(): return lax.ppermute(value, 'fsdp', line_pairs(apart))]
    pallas_call x29 -> x31, Pallas kernels: 51 us -> 49.1 us  [run_kernel(): pl.pallas_call(body, name=name, out_shape=tuple(outs), in_specs=in_specs,...]
  transfers between devices with their start and end apart: 82 -> 82, of which waited for: 31 -> 35; matrix products, arithmetic and copies ran while one was open for 2% -> 2% of each run, Pallas kernels for 17% -> 18%
where the time goes in v5:
time: 259 us; the launch traced here: 257 us
  starting transfers between devices  105 us (41%)
  waiting for transfers between devices  88.6 us (34%)
  Pallas kernels  50.5 us (19%)
  local copies, waits for them, and re-layouts  6 us (2%)
  between operations  4.34 us (2%)
  other arithmetic  3.08 us (1%)
    ppermute x36, starting transfers between devices, along_line(): return lax.ppermute(value, 'fsdp', line_pairs(apart))  54.1 us
    pallas_call x31, Pallas kernels, run_kernel(): pl.pallas_call(body, name=name, out_shape=tuple(outs), in_specs=in_specs,...  49.1 us
    ppermute x36, waiting for transfers between devices, along_line(): return lax.ppermute(value, 'fsdp', line_pairs(apart))  45.3 us
    ppermute x26, waiting for transfers between devices, in_plane(): return lax.ppermute(value, 'fsdp', plane_pairs(mask))  35.5 us
    ppermute x20, starting transfers between devices, other_core(): return lax.ppermute(value, 'rep', [(0, 1), (1, 0)])  29.9 us
    ppermute x26, starting transfers between devices, in_plane(): return lax.ppermute(value, 'fsdp', plane_pairs(mask))  21 us
    ppermute x20, waiting for transfers between devices, other_core(): return lax.ppermute(value, 'rep', [(0, 1), (1, 0)])  7.73 us
  transfers between devices with their start and end apart: 82, of which 35 were waited for; matrix products, arithmetic and copies ran while one was open for 2% of the time, Pallas kernels for 18%

profile of v5, /device:TPU:13, one launch (start us, length us, event | category | flops | bytes accessed | tf_op | source)
XLA Modules:
  0.0 257.4 jit_solution(12807507075984636334)
XLA Ops:
  6.2 2.3 collective-permute-start.1
  12.1 6.2 %collective-permute-done.1.refs_2_ = bf16[48,1664]{1,0:T(8,128)(2,1)S(1)} collective-permute-done((bf16[48,1664]{1,0:T(8,128)(2,1)S(1)}, bf16[48,1664]{1,0:T(8,128)(2,1)S(1)}, u32[]{:S(2)}, u32[]{:S(2)}) %collective-permute-start.1) | collective-permute-done | bytes 159776 | tf_op jit(solution)/shard_map/ppermute | solution.py:565
  18.3 3.6 %collective-permute-done.refs_1_ = bf16[48,1664]{1,0:T(8,128)(2,1)S(1)} collective-permute-done((bf16[48,1664]{1,0:T(8,128)(2,1)S(1)}, bf16[48,1664]{1,0:T(8,128)(2,1)S(1)}, u32[]{:S(2)}, u32[]{:S(2)}) %collective-permute-start) | collective-permute-done | bytes 159776 | tf_op jit(solution)/shard_map/ppermute | solution.py:565
  26.7 2.5 collective-permute-start.8
  29.3 7.3 %collective-permute-done.3.refs_4_ = bf16[48,6656]{1,0:T(8,128)(2,1)S(1)} collective-permute-done((bf16[48,6656]{1,0:T(8,128)(2,1)S(1)}, bf16[48,6656]{1,0:T(8,128)(2,1)S(1)}, u32[]{:S(2)}, u32[]{:S(2)}) %collective-permute-start.3) | collective-permute-done | bytes 639008 | tf_op jit(solution)/shard_map/ppermute | solution.py:569
  36.6 3.6 %collective-permute-done.4.refs_5_ = bf16[48,6656]{1,0:T(8,128)(2,1)S(1)} collective-permute-done((bf16[48,6656]{1,0:T(8,128)(2,1)S(1)}, bf16[48,6656]{1,0:T(8,128)(2,1)S(1)}, u32[]{:S(2)}, u32[]{:S(2)}) %collective-permute-start.4) | collective-permute-done | bytes 639008 | tf_op jit(solution)/shard_map/ppermute | solution.py:569
  44.5 16.4 %collective-permute-done.15.refs_6_.refs_4_ = bf16[48,9472]{1,0:T(8,128)(2,1)S(1)} collective-permute-done((bf16[48,9472]{1,0:T(8,128)(2,1)S(1)}, bf16[48,9472]{1,0:T(8,128)(2,1)S(1)}, u32[]{:S(2)}, u32[]{:S(2)}) %collective-permute-start.15) | collective-permute-done | bytes 909344 | tf_op jit(solution)/shard_map/ppermute | solution.py:569
  62.9 2.2 collective-permute-start.28
  65.1 3.8 %seg_qkv.1 = (bf16[16,48,1152]{2,1,0:T(8,128)(2,1)S(1)}, bf16[16,48,384]{2,1,0:T(8,128)(2,1)S(1)}, bf16[256,1152]{1,0:T(8,128)(2,1)S(1)}, bf16[256,384]{1,0:T(8,...) custom-call(s32[5]{0:T(128)S(1)} %stack.24.where, ...), custom_call_target="tpu_custom_call" | custom-call | flops 452984832 | bytes 9450496 | tf_op jit(solution)/shard_map/seg_qkv/pallas_call | solution.py:591
  68.9 3.2 %collective-permute-start.21 = (f32[8,128]{1,0:T(8,128)S(1)}, f32[8,128]{1,0:T(8,128)S(1)}, u32[]{:S(2)}, u32[]{:S(2)}) collective-permute-start(f32[8,128]{1,0:T(8,128)S(1)} %get-tuple-element.180), channel_id=1, source_target_pairs={{0,16},{16,0},{1,17},{17,1},{2,18},{18,2},{3,19},{19,3},{4,20},{20... | collective-permute-start | bytes 12296 | tf_op jit(solution)/shard_map/ppermute | solution.py:573
  74.8 6.3 %collective-permute-done.29.refs_2_ = bf16[48,1152]{1,0:T(8,128)(2,1)S(1)} collective-permute-done((bf16[48,1152]{1,0:T(8,128)(2,1)S(1)}, bf16[48,1152]{1,0:T(8,128)(2,1)S(1)}, u32[]{:S(2)}, u32[]{:S(2)}) %collective-permute-start.29) | collective-permute-done | bytes 110624 | tf_op jit(solution)/shard_map/ppermute | solution.py:565
  88.0 5.1 %collective-permute-done.22.refs_7_ = bf16[48,3072]{1,0:T(8,128)(2,1)S(1)} collective-permute-done((bf16[48,3072]{1,0:T(8,128)(2,1)S(1)}, bf16[48,3072]{1,0:T(8,128)(2,1)S(1)}, u32[]{:S(2)}, u32[]{:S(2)}) %collective-permute-start.22) | collective-permute-done | bytes 294944 | tf_op jit(solution)/shard_map/ppermute | solution.py:569
  109.3 3.1 %collective-permute-start.35 = (f32[4,1664]{1,0:T(4,128)S(1)}, f32[4,1664]{1,0:T(4,128)S(1)}, u32[]{:S(2)}, u32[]{:S(2)}) collective-permute-start(f32[4,1664]{1,0:T(4,128)S(1)} %pad_maximum_fusion.2.refs_0_), channel_id=1, source_target_pairs={{0,8},{1,9},{2,10},{3,11},{4,12},{5,13},{6,14},{7,15},{8,0},{9,1},... | collective-permute-start | bytes 79880 | tf_op jit(solution)/shard_map/ppermute | solution.py:565
  112.5 2.3 collective-permute-start.34
  116.8 2.4 collective-permute-start.39
  121.3 3.1 %seg_mlp_weight.1 = (bf16[2,48,3072]{2,1,0:T(8,128)(2,1)S(1)}, bf16[2,48,3072]{2,1,0:T(8,128)(2,1)S(1)}, bf16[4,48,3072]{2,1,0:T(8,128)(2,1)S(1)}, bf16[4,48,307...) custom-call(s32[5]{0:T(128)S(1)} %stack.24.where, bf16[128,768]{1,0:T(8,128)(2,1)S(1)} %get-tuple-element.177.refs_8_.refs_0_.refs_6_, ...), custom_call_target="tpu_custom_call" | custom-call | flops 1207959552 | bytes 7077888 | tf_op jit(solution)/shard_map/seg_mlp_weight/pallas_call | solution.py:591
  130.6 3.8 %collective-permute-start.43 = (f32[16,768]{1,0:T(8,128)S(1)}, f32[16,768]{1,0:T(8,128)S(1)}, u32[]{:S(2)}, u32[]{:S(2)}) collective-permute-start(f32[16,768]{1,0:T(8,128)S(1)} %get-tuple-element.222.refs_1_), channel_id=1, source_target_pairs={{0,12},{1,13},{2,14},{3,15},{4,0},{5,1},{6,2},{7,3},{8,4},{9,5},{1... | collective-permute-start | bytes 147464 | tf_op jit(solution)/shard_map/ppermute | solution.py:565
  135.1 2.3 collective-permute-start.41
  143.5 3.0 %collective-permute-start.48 = (f32[16,768]{1,0:T(8,128)S(1)}, f32[16,768]{1,0:T(8,128)S(1)}, u32[]{:S(2)}, u32[]{:S(2)}) collective-permute-start(f32[16,768]{1,0:T(8,128)S(1)} %get-tuple-element.223.refs_1_), channel_id=1, source_target_pairs={{0,12},{1,13},{2,14},{3,15},{4,0},{5,1},{6,2},{7,3},{8,4},{9,5},{1... | collective-permute-start | bytes 147464 | tf_op jit(solution)/shard_map/ppermute | solution.py:565
  147.0 2.4 collective-permute-start.44
  154.4 2.2 collective-permute-start.50
  160.2 2.3 head_attend_back.1
  165.7 2.2 collective-permute-done.54.refs_4_
  169.8 2.8 %collective-permute-start.61 = (bf16[64,3072]{1,0:T(8,128)(2,1)S(1)}, bf16[64,3072]{1,0:T(8,128)(2,1)S(1)}, u32[]{:S(2)}, u32[]{:S(2)}) collective-permute-start(bf16[64,3072]{1,0:T(8,128)(2,1)S(1)} %get-tuple-element.284), channel_id=1, source_target_pairs={{0,12},{1,13},{2,14},{3,15},{4,0},{5,1},{6,2},{7,3},{8,4},{9,5},{1... | collective-permute-start | bytes 1179656 | tf_op jit(solution)/shard_map/ppermute | solution.py:565
  173.4 3.4 %collective-permute-start.57 = (f32[1,768]{1,0:T(1,128)S(1)}, f32[1,768]{1,0:T(1,128)S(1)}, u32[]{:S(2)}, u32[]{:S(2)}) collective-permute-start(f32[1,768]{1,0:T(1,128)S(1)} %get-tuple-element.260.refs_0_.refs_3_), channel_id=1, source_target_pairs={{0,16},{16,0},{1,17},{17,1},{2,18},{18,2},{3,19},{19,3},{4,20},{20... | collective-permute-start | bytes 9224 | tf_op jit(solution)/shard_map/ppermute | solution.py:573
  183.1 4.4 %seg_attn_back.1 = (bf16[256,1152]{1,0:T(8,128)(2,1)S(1)}, f32[128,768]{1,0:T(8,128)S(1)}, f32[128,768]{1,0:T(8,128)S(1)}, bf16[24,768]{1,0:T(8,128)(2,1)S(1)}) custom-call(s32[5]{0:T(128)S(1)} %stack.24.where, bf16[256,1152]{1,0:T(8,128)(2,1)S(1)} %get-tuple-element.266.refs_0_, bf16[128,768]{1,0:T(8,128)(2,1)S(1)} %get-tuple-element.267.refs_1_, ...), custom_call_target="tpu_custom_call" | custom-call | flops 905969664 | bytes 4624384 | tf_op jit(solution)/shard_map/seg_attn_back/pallas_call | solution.py:591
  192.9 7.7 %collective-permute-done.63 = bf16[24,768]{1,0:T(8,128)(2,1)S(1)} collective-permute-done((bf16[24,768]{1,0:T(8,128)(2,1)S(1)}, bf16[24,768]{1,0:T(8,128)(2,1)S(1)}, u32[]{:S(2)}, u32[]{:S(2)}) %collective-permute-start.63) | collective-permute-done | bytes 36896 | tf_op jit(solution)/shard_map/ppermute | solution.py:565
  202.6 2.2 collective-permute-start.67
  207.9 10.9 %collective-permute-start.60 = (f32[128,768]{1,0:T(8,128)S(1)}, f32[128,768]{1,0:T(8,128)S(1)}, u32[]{:S(2)}, u32[]{:S(2)}) collective-permute-start(f32[128,768]{1,0:T(8,128)S(1)} %get-tuple-element.277), channel_id=1, source_target_pairs={{0,16},{16,0},{1,17},{17,1},{2,18},{18,2},{3,19},{19,3},{4,20},{20... | collective-permute-start | bytes 1179656 | tf_op jit(solution)/shard_map/ppermute | solution.py:573
  223.5 3.7 %collective-permute-done.69 = bf16[48,1536]{1,0:T(8,128)(2,1)S(1)} collective-permute-done((bf16[48,1536]{1,0:T(8,128)(2,1)S(1)}, bf16[48,1536]{1,0:T(8,128)(2,1)S(1)}, u32[]{:S(2)}, u32[]{:S(2)}) %collective-permute-start.69) | collective-permute-done | bytes 147488 | tf_op jit(solution)/shard_map/ppermute | solution.py:565
  238.0 5.9 %collective-permute-done.70 = bf16[48,1536]{1,0:T(8,128)(2,1)S(1)} collective-permute-done((bf16[48,1536]{1,0:T(8,128)(2,1)S(1)}, bf16[48,1536]{1,0:T(8,128)(2,1)S(1)}, u32[]{:S(2)}, u32[]{:S(2)}) %collective-permute-start.70) | collective-permute-done | bytes 147488 | tf_op jit(solution)/shard_map/ppermute | solution.py:565
  246.2 3.2 %head_owner.1 = (f32[48,9216]{1,0:T(8,128)}, f32[1,576]{1,0:T(1,128)S(1)}) custom-call(s32[5]{0:T(128)S(1)} %stack.24.where, bf16[16,12288]{1,0:T(8,128)(2,1)S(1)} %head_rows.1.refs_0_, bf16[16,12288]{1,0:T(8,128)(2,1)S(1)} %collective-permute-done.78.refs_1_, f32[24,768]{1,0:T(8,128)S(1)} %add.44.refs_2_), custom_call_target="tpu_custom_call" | custom-call | flops 28311552 | bytes 2631936 | tf_op jit(solution)/shard_map/head_owner/pallas_call | solution.py:591
  (221 shorter events, 117.2 us)
Async XLA Ops:
  6.2 12.1 %collective-permute-start.1 = (bf16[48,1664]{1,0:T(8,128)(2,1)S(1)}, bf16[48,1664]{1,0:T(8,128)(2,1)S(1)}, u32[]{:S(2)}, u32[]{:S(2)}) collective-permute-start(bf16[48,1664]{1,0:T(8,128)(2,1)S(1)} %get-tuple-element.167.refs_0_), channel_id=1, source_target_pairs={{0,8},{1,9},{2,10},{3,11},{4,12},{5,13},{6,14},{7,15},{8,0},{9,1},... | collective-permute-start | bytes 479240 | tf_op jit(solution)/shard_map/ppermute | solution.py:565
  8.5 13.4 %collective-permute-start = (bf16[48,1664]{1,0:T(8,128)(2,1)S(1)}, bf16[48,1664]{1,0:T(8,128)(2,1)S(1)}, u32[]{:S(2)}, u32[]{:S(2)}) collective-permute-start(bf16[48,1664]{1,0:T(8,128)(2,1)S(1)} %get-tuple-element.167.refs_0_), channel_id=1, source_target_pairs={{0,4},{1,5},{2,6},{3,7},{4,8},{5,9},{6,10},{7,11},{8,12},{9,13},{1... | collective-permute-start | bytes 479240 | tf_op jit(solution)/shard_map/ppermute | solution.py:565
  21.9 14.7 %collective-permute-start.3 = (bf16[48,6656]{1,0:T(8,128)(2,1)S(1)}, bf16[48,6656]{1,0:T(8,128)(2,1)S(1)}, u32[]{:S(2)}, u32[]{:S(2)}) collective-permute-start(bf16[48,6656]{1,0:T(8,128)(2,1)S(1)} %pad_maximum_fusion), channel_id=1, source_target_pairs={{0,1},{1,0},{2,3},{3,2},{4,5},{5,4},{6,7},{7,6},{8,9},{9,8},{10,11... | collective-permute-start | bytes 1916936 | tf_op jit(solution)/shard_map/ppermute | solution.py:569
  24.7 15.4 %collective-permute-start.4 = (bf16[48,6656]{1,0:T(8,128)(2,1)S(1)}, bf16[48,6656]{1,0:T(8,128)(2,1)S(1)}, u32[]{:S(2)}, u32[]{:S(2)}) collective-permute-start(bf16[48,6656]{1,0:T(8,128)(2,1)S(1)} %pad_maximum_fusion), channel_id=1, source_target_pairs={{0,2},{1,3},{2,0},{3,1},{4,6},{5,7},{6,4},{7,5},{8,10},{9,11},{10,... | collective-permute-start | bytes 1916936 | tf_op jit(solution)/shard_map/ppermute | solution.py:569
  25.9 14.6 %collective-permute-start.9 = (bf16[48,1536]{1,0:T(8,128)(2,1)S(1)}, bf16[48,1536]{1,0:T(8,128)(2,1)S(1)}, u32[]{:S(2)}, u32[]{:S(2)}) collective-permute-start(bf16[48,1536]{1,0:T(8,128)(2,1)S(1)} %get-tuple-element.171.refs_0_), channel_id=1, source_target_pairs={{0,12},{1,13},{2,14},{3,15},{4,0},{5,1},{6,2},{7,3},{8,4},{9,5},{1... | collective-permute-start | bytes 442376 | tf_op jit(solution)/shard_map/ppermute | solution.py:565
  26.7 13.7 %collective-permute-start.8 = (bf16[48,1536]{1,0:T(8,128)(2,1)S(1)}, bf16[48,1536]{1,0:T(8,128)(2,1)S(1)}, u32[]{:S(2)}, u32[]{:S(2)}) collective-permute-start(bf16[48,1536]{1,0:T(8,128)(2,1)S(1)} %get-tuple-element.171.refs_0_), channel_id=1, source_target_pairs={{0,8},{1,9},{2,10},{3,11},{4,12},{5,13},{6,14},{7,15},{8,0},{9,1},... | collective-permute-start | bytes 442376 | tf_op jit(solution)/shard_map/ppermute | solution.py:565
  40.5 20.5 %collective-permute-start.15 = (bf16[48,9472]{1,0:T(8,128)(2,1)S(1)}, bf16[48,9472]{1,0:T(8,128)(2,1)S(1)}, u32[]{:S(2)}, u32[]{:S(2)}) collective-permute-start(bf16[48,9472]{1,0:T(8,128)(2,1)S(1)} %get-tuple-element.332), channel_id=1, source_target_pairs={{0,1},{1,0},{2,3},{3,2},{4,5},{5,4},{6,7},{7,6},{8,9},{9,8},{10,11... | collective-permute-start | bytes 2727944 | tf_op jit(solution)/shard_map/ppermute | solution.py:569
  40.8 20.2 %collective-permute-start.13 = (bf16[48,9472]{1,0:T(8,128)(2,1)S(1)}, bf16[48,9472]{1,0:T(8,128)(2,1)S(1)}, u32[]{:S(2)}, u32[]{:S(2)}) collective-permute-start(bf16[48,9472]{1,0:T(8,128)(2,1)S(1)} %get-tuple-element.333), channel_id=1, source_target_pairs={{0,2},{1,3},{2,0},{3,1},{4,6},{5,7},{6,4},{7,5},{8,10},{9,11},{10,... | collective-permute-start | bytes 2727944 | tf_op jit(solution)/shard_map/ppermute | solution.py:569
  41.1 20.0 %collective-permute-start.12 = (bf16[48,1536]{1,0:T(8,128)(2,1)S(1)}, bf16[48,1536]{1,0:T(8,128)(2,1)S(1)}, u32[]{:S(2)}, u32[]{:S(2)}) collective-permute-start(bf16[48,1536]{1,0:T(8,128)(2,1)S(1)} %get-tuple-element.172.refs_0_), channel_id=1, source_target_pairs={{0,12},{1,13},{2,14},{3,15},{4,0},{5,1},{6,2},{7,3},{8,4},{9,5},{1... | collective-permute-start | bytes 442376 | tf_op jit(solution)/shard_map/ppermute | solution.py:565
  43.1 18.0 %collective-permute-start.11 = (bf16[48,1536]{1,0:T(8,128)(2,1)S(1)}, bf16[48,1536]{1,0:T(8,128)(2,1)S(1)}, u32[]{:S(2)}, u32[]{:S(2)}) collective-permute-start(bf16[48,1536]{1,0:T(8,128)(2,1)S(1)} %get-tuple-element.172.refs_0_), channel_id=1, source_target_pairs={{0,8},{1,9},{2,10},{3,11},{4,12},{5,13},{6,14},{7,15},{8,0},{9,1},... | collective-permute-start | bytes 442376 | tf_op jit(solution)/shard_map/ppermute | solution.py:565
  44.5 16.5 %collective-permute-start.10 = (bf16[48,1536]{1,0:T(8,128)(2,1)S(1)}, bf16[48,1536]{1,0:T(8,128)(2,1)S(1)}, u32[]{:S(2)}, u32[]{:S(2)}) collective-permute-start(bf16[48,1536]{1,0:T(8,128)(2,1)S(1)} %get-tuple-element.172.refs_0_), channel_id=1, source_target_pairs={{0,4},{1,5},{2,6},{3,7},{4,8},{5,9},{6,10},{7,11},{8,12},{9,13},{1... | collective-permute-start | bytes 442376 | tf_op jit(solution)/shard_map/ppermute | solution.py:565
  61.2 23.4 %collective-permute-start.18 = (bf16[48,9216]{1,0:T(8,128)(2,1)S(1)}, bf16[48,9216]{1,0:T(8,128)(2,1)S(1)}, u32[]{:S(2)}, u32[]{:S(2)}) collective-permute-start(bf16[48,9216]{1,0:T(8,128)(2,1)S(1)} %get-tuple-element.324), channel_id=1, source_target_pairs={{0,2},{1,3},{2,0},{3,1},{4,6},{5,7},{6,4},{7,5},{8,10},{9,11},{10,... | collective-permute-start | bytes 2654216 | tf_op jit(solution)/shard_map/ppermute | solution.py:569
  61.7 22.9 %collective-permute-start.14 = (bf16[48,9216]{1,0:T(8,128)(2,1)S(1)}, bf16[48,9216]{1,0:T(8,128)(2,1)S(1)}, u32[]{:S(2)}, u32[]{:S(2)}) collective-permute-start(bf16[48,9216]{1,0:T(8,128)(2,1)S(1)} %get-tuple-element.325), channel_id=1, source_target_pairs={{0,1},{1,0},{2,3},{3,2},{4,5},{5,4},{6,7},{7,6},{8,9},{9,8},{10,11... | collective-permute-start | bytes 2654216 | tf_op jit(solution)/shard_map/ppermute | solution.py:569
  62.9 11.9 %collective-permute-start.28 = (bf16[48,1152]{1,0:T(8,128)(2,1)S(1)}, bf16[48,1152]{1,0:T(8,128)(2,1)S(1)}, u32[]{:S(2)}, u32[]{:S(2)}) collective-permute-start(bf16[48,1152]{1,0:T(8,128)(2,1)S(1)} %get-tuple-element.195), channel_id=1, source_target_pairs={{0,4},{1,5},{2,6},{3,7},{4,8},{5,9},{6,10},{7,11},{8,12},{9,13},{1... | collective-permute-start | bytes 331784 | tf_op jit(solution)/shard_map/ppermute | solution.py:565
  93.2 11.6 %collective-permute-start.31 = (bf16[48,4992]{1,0:T(8,128)(2,1)S(1)}, bf16[48,4992]{1,0:T(8,128)(2,1)S(1)}, u32[]{:S(2)}, u32[]{:S(2)}) collective-permute-start(bf16[48,4992]{1,0:T(8,128)(2,1)S(1)} %constant_dynamic-update-slice_fusion.16), channel_id=1, source_target_pairs={{0,1},{1,0},{2,3},{3,2},{4,5},{5,4},{6,7},{7,6},{8,9},{9,8},{10,11... | collective-permute-start | bytes 1437704 | tf_op jit(solution)/shard_map/ppermute | solution.py:569
  94.4 12.4 %collective-permute-start.32 = (bf16[48,4992]{1,0:T(8,128)(2,1)S(1)}, bf16[48,4992]{1,0:T(8,128)(2,1)S(1)}, u32[]{:S(2)}, u32[]{:S(2)}) collective-permute-start(bf16[48,4992]{1,0:T(8,128)(2,1)S(1)} %constant_dynamic-update-slice_fusion.16), channel_id=1, source_target_pairs={{0,2},{1,3},{2,0},{3,1},{4,6},{5,7},{6,4},{7,5},{8,10},{9,11},{10,... | collective-permute-start | bytes 1437704 | tf_op jit(solution)/shard_map/ppermute | solution.py:569
  124.4 16.8 %collective-permute-start.46 = (bf16[2,48,3072]{2,1,0:T(8,128)(2,1)S(1)}, bf16[2,48,3072]{2,1,0:T(8,128)(2,1)S(1)}, u32[]{:S(2)}, u32[]{:S(2)}) collective-permute-start(bf16[2,48,3072]{2,1,0:T(8,128)(2,1)S(1)} %get-tuple-element.224), channel_id=1, source_target_pairs={{0,2},{1,3},{2,0},{3,1},{4,6},{5,7},{6,4},{7,5},{8,10},{9,11},{10,... | collective-permute-start | bytes 1769480 | tf_op jit(solution)/shard_map/ppermute | solution.py:569
  125.3 15.9 %collective-permute-start.47 = (bf16[2,48,3072]{2,1,0:T(8,128)(2,1)S(1)}, bf16[2,48,3072]{2,1,0:T(8,128)(2,1)S(1)}, u32[]{:S(2)}, u32[]{:S(2)}) collective-permute-start(bf16[2,48,3072]{2,1,0:T(8,128)(2,1)S(1)} %get-tuple-element.228), channel_id=1, source_target_pairs={{0,1},{1,0},{2,3},{3,2},{4,5},{5,4},{6,7},{7,6},{8,9},{9,8},{10,11... | collective-permute-start | bytes 1769480 | tf_op jit(solution)/shard_map/ppermute | solution.py:569
  142.0 26.3 %collective-permute-start.52 = (bf16[4,48,3072]{2,1,0:T(8,128)(2,1)S(1)}, bf16[4,48,3072]{2,1,0:T(8,128)(2,1)S(1)}, u32[]{:S(2)}, u32[]{:S(2)}) collective-permute-start(bf16[4,48,3072]{2,1,0:T(8,128)(2,1)S(1)} %get-tuple-element.232), channel_id=1, source_target_pairs={{0,1},{1,0},{2,3},{3,2},{4,5},{5,4},{6,7},{7,6},{8,9},{9,8},{10,11... | collective-permute-start | bytes 3538952 | tf_op jit(solution)/shard_map/ppermute | solution.py:569
  142.9 26.0 %collective-permute-start.56 = (bf16[4,48,3072]{2,1,0:T(8,128)(2,1)S(1)}, bf16[4,48,3072]{2,1,0:T(8,128)(2,1)S(1)}, u32[]{:S(2)}, u32[]{:S(2)}) collective-permute-start(bf16[4,48,3072]{2,1,0:T(8,128)(2,1)S(1)} %get-tuple-element.233), channel_id=1, source_target_pairs={{0,2},{1,3},{2,0},{3,1},{4,6},{5,7},{6,4},{7,5},{8,10},{9,11},{10,... | collective-permute-start | bytes 3538952 | tf_op jit(solution)/shard_map/ppermute | solution.py:569
  169.8 18.8 %collective-permute-start.61 = (bf16[64,3072]{1,0:T(8,128)(2,1)S(1)}, bf16[64,3072]{1,0:T(8,128)(2,1)S(1)}, u32[]{:S(2)}, u32[]{:S(2)}) collective-permute-start(bf16[64,3072]{1,0:T(8,128)(2,1)S(1)} %get-tuple-element.284), channel_id=1, source_target_pairs={{0,12},{1,13},{2,14},{3,15},{4,0},{5,1},{6,2},{7,3},{8,4},{9,5},{1... | collective-permute-start | bytes 1179656 | tf_op jit(solution)/shard_map/ppermute | solution.py:565
  182.0 19.2 %collective-permute-start.65 = (bf16[64,3072]{1,0:T(8,128)(2,1)S(1)}, bf16[64,3072]{1,0:T(8,128)(2,1)S(1)}, u32[]{:S(2)}, u32[]{:S(2)}) collective-permute-start(bf16[64,3072]{1,0:T(8,128)(2,1)S(1)} %get-tuple-element.295), channel_id=1, source_target_pairs={{0,8},{1,9},{2,10},{3,11},{4,12},{5,13},{6,14},{7,15},{8,0},{9,1},... | collective-permute-start | bytes 1179656 | tf_op jit(solution)/shard_map/ppermute | solution.py:565
  188.6 12.0 %collective-permute-start.64 = (bf16[2,48,1536]{2,1,0:T(8,128)(2,1)S(1)}, bf16[2,48,1536]{2,1,0:T(8,128)(2,1)S(1)}, u32[]{:S(2)}, u32[]{:S(2)}) collective-permute-start(bf16[2,48,1536]{2,1,0:T(8,128)(2,1)S(1)} %get-tuple-element.291), channel_id=1, source_target_pairs={{0,1},{1,0},{2,3},{3,2},{4,5},{5,4},{6,7},{7,6},{8,9},{9,8},{10,11... | collective-permute-start | bytes 884744 | tf_op jit(solution)/shard_map/ppermute | solution.py:569
  188.9 11.7 %collective-permute-start.62 = (bf16[2,48,1536]{2,1,0:T(8,128)(2,1)S(1)}, bf16[2,48,1536]{2,1,0:T(8,128)(2,1)S(1)}, u32[]{:S(2)}, u32[]{:S(2)}) collective-permute-start(bf16[2,48,1536]{2,1,0:T(8,128)(2,1)S(1)} %get-tuple-element.285), channel_id=1, source_target_pairs={{0,2},{1,3},{2,0},{3,1},{4,6},{5,7},{6,4},{7,5},{8,10},{9,11},{10,... | collective-permute-start | bytes 884744 | tf_op jit(solution)/shard_map/ppermute | solution.py:569
  201.2 17.5 %collective-permute-start.66 = (bf16[4,48,1536]{2,1,0:T(8,128)(2,1)S(1)}, bf16[4,48,1536]{2,1,0:T(8,128)(2,1)S(1)}, u32[]{:S(2)}, u32[]{:S(2)}) collective-permute-start(bf16[4,48,1536]{2,1,0:T(8,128)(2,1)S(1)} %get-tuple-element.296), channel_id=1, source_target_pairs={{0,1},{1,0},{2,3},{3,2},{4,5},{5,4},{6,7},{7,6},{8,9},{9,8},{10,11... | collective-permute-start | bytes 1769480 | tf_op jit(solution)/shard_map/ppermute | solution.py:569
  202.0 17.4 %collective-permute-start.68 = (bf16[4,48,1536]{2,1,0:T(8,128)(2,1)S(1)}, bf16[4,48,1536]{2,1,0:T(8,128)(2,1)S(1)}, u32[]{:S(2)}, u32[]{:S(2)}) collective-permute-start(bf16[4,48,1536]{2,1,0:T(8,128)(2,1)S(1)} %get-tuple-element.305), channel_id=1, source_target_pairs={{0,2},{1,3},{2,0},{3,1},{4,6},{5,7},{6,4},{7,5},{8,10},{9,11},{10,... | collective-permute-start | bytes 1769480 | tf_op jit(solution)/shard_map/ppermute | solution.py:569
  202.6 16.2 %collective-permute-start.67 = (bf16[64,3072]{1,0:T(8,128)(2,1)S(1)}, bf16[64,3072]{1,0:T(8,128)(2,1)S(1)}, u32[]{:S(2)}, u32[]{:S(2)}) collective-permute-start(bf16[64,3072]{1,0:T(8,128)(2,1)S(1)} %get-tuple-element.297), channel_id=1, source_target_pairs={{0,4},{1,5},{2,6},{3,7},{4,8},{5,9},{6,10},{7,11},{8,12},{9,13},{1... | collective-permute-start | bytes 1179656 | tf_op jit(solution)/shard_map/ppermute | solution.py:565
  205.5 13.2 %collective-permute-start.72 = (bf16[24,768]{1,0:T(8,128)(2,1)S(1)}, bf16[24,768]{1,0:T(8,128)(2,1)S(1)}, u32[]{:S(2)}, u32[]{:S(2)}) collective-permute-start(bf16[24,768]{1,0:T(8,128)(2,1)S(1)} %get-tuple-element.288), channel_id=1, source_target_pairs={{0,8},{1,9},{2,10},{3,11},{4,12},{5,13},{6,14},{7,15},{8,0},{9,1},... | collective-permute-start | bytes 110600 | tf_op jit(solution)/shard_map/ppermute | solution.py:565
  207.9 26.5 %collective-permute-start.60 = (f32[128,768]{1,0:T(8,128)S(1)}, f32[128,768]{1,0:T(8,128)S(1)}, u32[]{:S(2)}, u32[]{:S(2)}) collective-permute-start(f32[128,768]{1,0:T(8,128)S(1)} %get-tuple-element.277), channel_id=1, source_target_pairs={{0,16},{16,0},{1,17},{17,1},{2,18},{18,2},{3,19},{19,3},{4,20},{20... | collective-permute-start | bytes 1179656 | tf_op jit(solution)/shard_map/ppermute | solution.py:573
  231.4 18.6 %collective-permute-start.77 = (f32[48,3072]{1,0:T(8,128)S(1)}, f32[48,3072]{1,0:T(8,128)S(1)}, u32[]{:S(2)}, u32[]{:S(2)}) collective-permute-start(f32[48,3072]{1,0:T(8,128)S(1)} %get-tuple-element.316.mlp), channel_id=1, source_target_pairs={{0,16},{16,0},{1,17},{17,1},{2,18},{18,2},{3,19},{19,3},{4,20},{20... | collective-permute-start | bytes 1769480 | tf_op jit(solution)/shard_map/ppermute | solution.py:573
  232.0 14.2 %collective-permute-start.78 = (bf16[16,12288]{1,0:T(8,128)(2,1)S(1)}, bf16[16,12288]{1,0:T(8,128)(2,1)S(1)}, u32[]{:S(2)}, u32[]{:S(2)}) collective-permute-start(bf16[16,12288]{1,0:T(8,128)(2,1)S(1)} %head_rows.1.refs_0_), channel_id=1, source_target_pairs={{0,16},{16,0},{1,17},{17,1},{2,18},{18,2},{3,19},{19,3},{4,20},{20... | collective-permute-start | bytes 1179656 | tf_op jit(solution)/shard_map/ppermute | solution.py:573
  234.4 17.2 %collective-permute-start.71 = (bf16[48,1536]{1,0:T(8,128)(2,1)S(1)}, bf16[48,1536]{1,0:T(8,128)(2,1)S(1)}, u32[]{:S(2)}, u32[]{:S(2)}) collective-permute-start(bf16[48,1536]{1,0:T(8,128)(2,1)S(1)} %get-tuple-element.310), channel_id=1, source_target_pairs={{0,12},{1,13},{2,14},{3,15},{4,0},{5,1},{6,2},{7,3},{8,4},{9,5},{1... | collective-permute-start | bytes 442376 | tf_op jit(solution)/shard_map/ppermute | solution.py:565
  (56 other events, 314.4 us)

commit v6 on v5

--- a/solution.py
+++ b/solution.py
@@ -577,6 +577,10 @@
     return lax.optimization_barrier((value,) + events)[0]
 
 
+def together(*values):
+    return tuple(lax.optimization_barrier(values))
+
+
 def shape_of(dims, dtype=WIDE):
     return jax.ShapeDtypeStruct(dims, dtype)
 
@@ -625,6 +629,52 @@
     for copy in copies:
         copy.start()
     wait_all(copies)
+
+
+FIRST = 4 * HALF + LANES
+OWN_CUT = FIRST + FF_HALF // 2
+LINE_CUTS = (7 * LANES, FF_HALF // 2, FF_HALF // 2)
+WIDTHS = (FIRST, FF_HALF, FF_HALF)
+
+
+def group_pieces(group, refs):
+    own, rest = refs[:LINE], refs[LINE:]
+    own_x, own_y, far_x, far_y, line_x, line_y, late_x, late_y = rest
+    width, cut = WIDTHS[group], LINE_CUTS[group]
+    start = sum(WIDTHS[:group])
+    if group == 0:
+        bases = (sum(WIDTHS) - OWN_CUT, OWN_CUT)
+    else:
+        before, before_cut = WIDTHS[group - 1], LINE_CUTS[group - 1]
+        bases = (2 * before - before_cut, before + before_cut)
+    pieces = {(0, step): [(own[step], 0, 0, width)] for step in range(LINE)}
+    for mask, whole, line, base in ((1, own_x, line_x, bases[0]), (2, own_y, line_y, bases[1])):
+        pieces[mask, 0] = [(whole, start, 0, width)]
+        for step in range(1, LINE):
+            pieces[mask, step] = [(line, base + (step - 1) * width, 0, width)]
+    middle = min(max(OWN_CUT - start, 0), width)
+    far = []
+    if middle > 0:
+        far.append((far_y, start, 0, middle))
+    if middle < width:
+        far.append((far_x, start + middle - OWN_CUT, middle, width))
+    pieces[3, 0] = far
+    pieces[3, 1] = [(late_y, 0, 0, width)]
+    pieces[3, 2] = [(late_y, width, 0, cut), (late_x, 0, cut, width)]
+    pieces[3, 3] = [(late_x, width - cut, 0, width)]
+    return pieces
+
+
+def gather_group(where, group, refs, targets):
+    line_at, plane_at = where[0], where[1]
+    for (mask, step), parts in group_pieces(group, refs).items():
+        chip = (line_at + LINE - step) % LINE * PLANE + (plane_at ^ mask)
+        for whole, first, last in targets:
+            for ref, offset, begin, end in parts:
+                low, high = max(first, begin), min(last, end)
+                if low < high:
+                    source = slice(offset + low - begin, offset + high - begin)
+                    whole[chip, :, low - first : high - first] = ref[:, source]
 
 
 def gather_blocks(where, refs, base, width, targets):
@@ -782,22 +832,24 @@
 
 
 def qkv_kernel(where, *refs):
-    blocks = refs[:8]
-    hidden, hidden_got, live_row, live_got, order = refs[8:13]
-    weight, out_half, qkv_out, mixed_out, vectors_out, count_out, ordered_out = refs[13:20]
-    vec_rows, flat, inputs = refs[20:]
+    blocks = refs[:12]
+    hidden, hidden_got, live_row, live_got, order = refs[12:17]
+    weight, out_low, out_high, qkv_out, mixed_out = refs[17:22]
+    vectors_out, count_out, ordered_out = refs[22:25]
+    vec_rows, flat, inputs, out_half = refs[25:]
     core_at = where[2]
-    gather_blocks(
-        where,
+    gather_group(
+        where,
+        0,
         blocks,
-        0,
-        4 * HALF + LANES,
         (
             (weight, 0, 3 * HALF),
             (out_half, 3 * HALF, 4 * HALF),
             (vec_rows, 4 * HALF, 4 * HALF + LANES),
         ),
     )
+    out_low[...] = out_half[: GROUP // 2]
+    out_high[...] = out_half[GROUP // 2 :]
     piece = (8 * MODEL + FF) // GROUP
     lines = -(-piece // LANES)
     count = jnp.zeros((1, LANES), WIDE)
@@ -859,12 +911,15 @@
     return before * half, slope
 
 
-def out_kernel(where, hidden, mixed, mixed_got, half, half_got, vectors, order, *outs):
-    full_out, ordered_out, normed_out, inv_out, low_out, mixed_full = outs
+def out_kernel(where, hidden, mixed, mixed_got, low, high, low_got, high_got, *refs):
+    vectors, order, full_out, ordered_out, normed_out, inv_out, low_out, mixed_full = refs
     core_at = where[2]
     own, other = aligned(core_at * HALF), aligned((1 - core_at) * HALF)
-    full_out[:, pl.ds(own, HALF)] = half[...]
-    full_out[:, pl.ds(other, HALF)] = half_got[...]
+    rows = MODEL // 2
+    full_out[:rows, pl.ds(own, HALF)] = whole_rows(low)
+    full_out[rows:, pl.ds(own, HALF)] = whole_rows(high)
+    full_out[:rows, pl.ds(other, HALF)] = whole_rows(low_got)
+    full_out[rows:, pl.ds(other, HALF)] = whole_rows(high_got)
     mixed_full[:, pl.ds(own, HALF)] = mixed[...]
     mixed_full[:SEG, pl.ds(other, HALF)] = mixed_got[SEG:, :]
     mixed_full[SEG:, pl.ds(other, HALF)] = mixed_got[:SEG, :]
@@ -877,11 +932,11 @@
 
 
 def up_kernel(where, *refs):
-    blocks = refs[:8]
-    low, low_got, vectors = refs[8:11]
-    weight, act_out, slope_out, both = refs[11:]
+    blocks = refs[:12]
+    low, low_got, vectors = refs[12:15]
+    weight, act_out, slope_out, both = refs[15:]
     core_at = where[2]
-    gather_blocks(where, blocks, 2 * (4 * HALF + LANES), FF_HALF, ((weight, 0, FF_HALF),))
+    gather_group(where, 1, blocks, ((weight, 0, FF_HALF),))
     both[:SEG] = low[...]
     both[SEG:] = low_got[...]
     for at in range(FF_HALF // MODEL):
@@ -895,9 +950,9 @@
 
 
 def down_kernel(where, *refs):
-    blocks, act = refs[:8], refs[8]
-    weight, own_out, send_out = refs[9:]
-    gather_blocks(where, blocks, 2 * FF_HALF, FF_HALF, ((weight, 0, FF_HALF),))
+    blocks, act = refs[:12], refs[12]
+    weight, own_out, send_out = refs[13:]
+    gather_group(where, 2, blocks, ((weight, 0, FF_HALF),))
     partial = product_right(act[...], whole_rows(weight))
     own_out[...] = partial[:SEG]
     send_out[...] = partial[SEG:]
@@ -1022,7 +1077,11 @@
 
 
 def attn_near_kernel(where, *refs):
-    for mask, out in ((1, refs[5]), (2, refs[6]), (0, refs[7])):
+    top_row, out_rows, live_row = refs[5:8]
+    row_at = lax.broadcasted_iota(jnp.int32, (SEG, 1), 0)
+    output = jnp.where(row_at == 0, top_row[...] * live_row[:, 0:1], out_rows[...])
+    refs[11][...] = output.astype(LOW)
+    for mask, out in ((1, refs[8]), (2, refs[9]), (0, refs[10])):
         for piece in range(4):
             columns = slice(piece * HALF, (piece + 1) * HALF)
             out[:, :, columns] = attn_product(where, refs[:5], mask, piece)
@@ -1044,7 +1103,7 @@
 
 
 def reduce_far(parts):
-    return in_plane(parts[0], 2), in_plane(parts[1], 1)
+    return together(in_plane(parts[0], 2), in_plane(parts[1], 1))
 
 
 def reduce_add(where, parts, far):
@@ -1338,6 +1397,22 @@
     shared_out[GROUP : GROUP + 1, 0:LANES] = square[0:1, :]
     shared_out[GROUP + 1 : GROUP + 3, :] = sums_back[0:2, :]
     shared_out[GROUP + 3 : GROUP + 5, :] = sums_top[0:2, :]
+
+
+def head_mlp_kernel(where, *refs):
+    cls_mlp_kernel(where, *refs[:7], *refs[11:17])
+    add_far_kernel(where, *refs[7:11], *refs[17:])
+
+
+def head_end_kernel(where, *refs):
+    cls_end_kernel(where, *refs[:12], *refs[16:19], refs[23])
+    fold_kernel(where, *refs[12:16], *refs[19:23])
+
+
+def attn_add_kernel(where, *refs):
+    far_low, far_high, to_x, to_y, grad, own, got, x_out, y_out, input_out = refs
+    add_far_kernel(where, far_low, far_high, to_x, to_y, x_out, y_out)
+    input_out[...] = (grad[...] + own[...] + got[...]).astype(LOW)
 
 
 def cls_rows_kernel(where, *refs):
@@ -1384,13 +1459,13 @@
 
 
 def own_vector(rank, pieces, out, flat):
-    size = out.shape[1]
+    size = out.shape[0]
     for at, piece in enumerate(pieces):
         flat[:, at * MODEL : (at + 1) * MODEL] = piece
     value = jnp.zeros((1, size), WIDE)
     for chip in range(GROUP):
         value = jnp.where(rank == chip, flat[:, chip * size : (chip + 1) * size], value)
-    out[...] = value
+    out[...] = value.reshape(size)
 
 
 def cls_owner_kernel(where, *refs):
@@ -1447,6 +1522,14 @@
     vecs_out[...] = product_plain(hot, rows[...])
 
 
+def share_owner_kernel(where, *refs):
+    head_share_kernel(where, *refs[:5], *refs[9:11], refs[15])
+    cls_owner_kernel(where, *refs[5:8], *refs[11:13], *refs[16:])
+    shared, count, pos_out, loss_out = refs[7], refs[8], refs[13], refs[14]
+    pos_out[...] = shared[:GROUP, :]
+    loss_out[...] = shared[GROUP : GROUP + 1, 0:1] / (count[0:1, 0:1] * MODEL)
+
+
 def seg_vec_kernel(where, vecs, vecs_got, vec_out, flat):
     rank = where[0] * PLANE + where[1]
     rows = (8 * MODEL + FF) // MODEL
@@ -1463,42 +1546,29 @@
     ]
 
 
-def mlp_store_kernel(where, mlp, mlp_got, out, sems):
+def store_kernel(where, attn, attn_got, mlp, mlp_got, vecs, vecs_got, out, vec_out, flat, sems):
     pairs = []
+    for piece in range(4):
+        pairs += column_copies(where, out, piece * MODEL, HALF, attn, attn_got, piece * HALF)
     for piece in range(2):
         base = 4 * MODEL + piece * FF
         pairs += column_copies(where, out, base, FF_HALF, mlp, mlp_got, piece * FF_HALF)
-    run_copies(pairs, sems)
-
-
-def attn_store_kernel(where, attn, attn_got, filled, out, sems):
-    pairs = []
-    for piece in range(4):
-        pairs += column_copies(where, out, piece * MODEL, HALF, attn, attn_got, piece * HALF)
-    run_copies(pairs, sems)
-
-
-def store_attn(where, attn, attn_got, filled):
-    far = pl.BlockSpec(memory_space=pl.ANY)
-    near = pl.BlockSpec(memory_space=pltpu.VMEM)
-    return pl.pallas_call(
-        attn_store_kernel,
-        name="seg_attn_store",
-        out_shape=shape_of(filled.shape),
-        in_specs=[pl.BlockSpec(memory_space=pltpu.SMEM), near, near, far],
-        out_specs=far,
-        scratch_shapes=[pltpu.SemaphoreType.DMA((8,))],
-        input_output_aliases={3: 0},
-        compiler_params=pltpu.CompilerParams(vmem_limit_bytes=VMEM_BYTES),
-    )(where, attn, attn_got, filled)
+    copies = [
+        pltpu.make_async_copy(source, target, sems.at[at])
+        for at, (source, target) in enumerate(pairs)
+    ]
+    for copy in copies:
+        copy.start()
+    seg_vec_kernel(where, vecs, vecs_got, vec_out, flat)
+    wait_all(copies)
 
 
 def plane_parts(part):
-    return (part,) + tuple(in_plane(part, mask) for mask in range(1, PLANE))
+    return (part,) + together(*(in_plane(part, mask) for mask in range(1, PLANE)))
 
 
 def line_parts(part):
-    return (part,) + tuple(along_line(part, apart) for apart in range(1, LINE))
+    return (part,) + together(*(along_line(part, apart) for apart in range(1, LINE)))
 
 
 def slice_local(
@@ -1519,12 +1589,11 @@
     own_rows, total_columns = seg_mats.shape
     vec_size = seg_vecs.shape[0]
     both_rows = CORES * SEG
-    first_columns = 4 * HALF + LANES
 
     first_piece, live_row = run_kernel(
         prepare_first_kernel,
         "prepare_first",
-        [shape_of((own_rows, first_columns), LOW), shape_of((1, SEG))],
+        [shape_of((own_rows, FIRST), LOW), shape_of((1, SEG))],
         where,
         (seg_mats,),
         (jnp.stack([seg_vecs, cls_vecs]).astype(WIDE), valid_flags[None]),
@@ -1557,33 +1626,51 @@
         return jnp.concatenate(pieces, axis=1)
 
     def sent_both(to_x, to_y):
-        return in_plane(to_x, 1), in_plane(to_y, 2)
-
-    hidden_got, live_got = other_core(hidden_in), other_core(live_row)
-    first_sent = after(joined(*first_line), second_piece)
-    first_x, first_y = sent_both(first_sent, first_sent)
-    second_line = line_parts(after(second_piece, hidden_got, live_got, *first_line[1:]))
-    size = 2 * first_columns
-    second_x, second_y = sent_both(
-        joined(first_y[:, size:], *second_line), joined(first_x[:, :size], *second_line)
-    )
-    third_line = line_parts(after(third_piece, first_x, first_y, *second_line[1:]))
-    start, size = size, 2 * FF_HALF
-    third_x, third_y = sent_both(
-        joined(second_y[:, start + size :], *third_line),
-        joined(second_x[:, start : start + size], *third_line),
-    )
+        to_x, to_y = together(to_x, to_y)
+        return together(in_plane(to_x, 1), in_plane(to_y, 2))
+
+    own_sent = joined(first_piece, second_piece, third_piece)
+    own_x, own_y = sent_both(own_sent, own_sent)
+    first_line = first_line[:1] + tuple(after(got, own_x, own_y) for got in first_line[1:])
+    to_x = joined(own_y[:, OWN_CUT:], *first_line[1:])
+    to_y = joined(own_x[:, :OWN_CUT], *first_line[1:])
+    first_x, first_y = sent_both(to_x, to_y)
+    hidden_got = other_core(after(hidden_in, to_x, to_y))
+    live_got = other_core(after(live_row, to_x, to_y))
+    second_line = line_parts(after(second_piece, hidden_got, live_got, to_x, to_y))
+
+    def halves(group, from_x, from_y):
+        width, cut = WIDTHS[group], LINE_CUTS[group]
+        if group == 0:
+            base_x, base_y = sum(WIDTHS) - OWN_CUT, OWN_CUT
+        else:
+            before, before_cut = WIDTHS[group - 1], LINE_CUTS[group - 1]
+            base_x, base_y = 2 * before - before_cut, before + before_cut
+        return (
+            from_y[:, base_y + width + cut : base_y + 3 * width],
+            from_x[:, base_x : base_x + width + cut],
+        )
+
+    high, low = halves(0, first_x, first_y)
+    to_x, to_y = joined(high, *second_line[1:]), joined(low, *second_line[1:])
+    second_x, second_y = sent_both(to_x, to_y)
+    third_line = line_parts(after(third_piece, to_x, to_y))
+    high, low = halves(1, second_x, second_y)
+    to_x, to_y = joined(high, *third_line[1:]), joined(low, *third_line[1:])
+    third_x, third_y = sent_both(to_x, to_y)
+    own_parts = (own_x, own_y, first_x, first_y)
     cls_line = (quarters[0],) + tuple(
-        along_line(after(quarters[apart], second_x, second_y, *third_line[1:]), apart)
+        along_line(after(quarters[apart], to_x, to_y), apart)
         for apart in range(1, LINE)
     )
 
-    qkv_weight, out_half, qkv, mixed, vectors, count, hidden_ordered = run_kernel(
+    qkv_weight, out_low, out_high, qkv, mixed, vectors, count, hidden_ordered = run_kernel(
         qkv_kernel,
         "seg_qkv",
         [
             shape_of((GROUP, own_rows, 3 * HALF), LOW),
-            shape_of((GROUP, own_rows, HALF), LOW),
+            shape_of((GROUP // 2, own_rows, HALF), LOW),
+            shape_of((GROUP // 2, own_rows, HALF), LOW),
             shape_of((both_rows, 3 * HALF), LOW),
             shape_of((both_rows, HALF), LOW),
             shape_of((2 * (8 * MODEL + FF) // MODEL, MODEL)),
@@ -1593,17 +1680,17 @@
         where,
         (),
         first_line
+        + own_parts
         + (first_x, first_y, second_x, second_y)
         + (hidden_in, hidden_got, live_row, live_got, order),
         [
             pltpu.VMEM((GROUP, own_rows, LANES), LOW),
             pltpu.VMEM((2, 8 * MODEL + FF), WIDE),
             pltpu.VMEM((both_rows, MODEL), LOW),
+            pltpu.VMEM((GROUP, own_rows, HALF), LOW),
         ],
         flops=2 * SEG * MODEL * 3 * MODEL,
     )
-    count = count + other_core(count)
-    out_half = out_half.reshape(MODEL, HALF)
     out_weight, mixed_ordered, normed_first, inv_first, first_low = run_kernel(
         out_kernel,
         "seg_out",
@@ -1616,12 +1703,23 @@
         ],
         where,
         (),
-        (hidden_in, mixed, other_core(mixed), out_half, other_core(out_half), vectors, order),
+        (
+            hidden_in,
+            mixed,
+            after(other_core(mixed), third_x, third_y),
+            out_low,
+            out_high,
+            other_core(out_low),
+            other_core(out_high),
+            vectors,
+            order,
+        ),
         [pltpu.VMEM((both_rows, MODEL), LOW)],
         flops=2 * SEG * MODEL * MODEL,
     )
-    first_got = after(other_core(first_low), count)
-    third_x, third_y = after(third_x, first_low), after(third_y, first_low)
+    fourth_x, fourth_y = sent_both(*halves(2, third_x, third_y))
+    first_got = after(other_core(first_low), fourth_x, fourth_y)
+    count = count + other_core(after(count, first_got))
     up_weight, act, slope = run_kernel(
         up_kernel,
         "seg_up",
@@ -1633,15 +1731,14 @@
         where,
         (),
         second_line
+        + own_parts
         + (second_x, second_y, third_x, third_y)
         + (first_low, first_got, vectors),
         [pltpu.VMEM((both_rows, MODEL), LOW)],
         flops=2 * SEG * MODEL * FF,
     )
-    fourth_x, fourth_y = sent_both(third_y[:, 2 * size :], third_x[:, size : 2 * size])
-    fourth_x, fourth_y = after(fourth_x, act), after(fourth_y, act)
     cls_sent = joined(*cls_line, cls_out_piece)
-    cls_sent = after(cls_sent, fourth_x, fourth_y)
+    cls_sent = after(cls_sent, act)
     cls_x, cls_y = sent_both(cls_sent, cls_sent)
     down_weight, down_own, down_send = run_kernel(
         down_kernel,
@@ -1653,7 +1750,7 @@
         ],
         where,
         (),
-        third_line + (third_x, third_y, fourth_x, fourth_y) + (act,),
+        third_line + own_parts + (third_x, third_y, fourth_x, fourth_y) + (act,),
         flops=2 * SEG * MODEL * FF,
     )
     normed_second, inv_second, diff, out_rows, head_row = run_kernel(
@@ -1694,19 +1791,6 @@
         (diff, count, normed_second, inv_second, vectors),
     )
     second_got = other_core(second_low)
-    cls_far = tuple(after(got, second_got, *head_lines[1:]) for got in cls_far)
-    cls_half, cls_out_half = run_kernel(
-        cls_gather_kernel,
-        "head_gather",
-        [
-            shape_of((GROUP, own_rows, QUARTER_HALF), LOW),
-            shape_of((PLANE, own_rows, HALF), LOW),
-        ],
-        where,
-        (),
-        cls_line + (cls_x, cls_y) + cls_far + (cls_out_piece,),
-    )
-    second_got = after(second_got, cls_half)
     pre, first_grad_own, first_grad_send, up_sums = run_kernel(
         mlp_back_kernel,
         "seg_mlp_back",
@@ -1722,6 +1806,43 @@
         [pltpu.VMEM((both_rows, MODEL), LOW)],
         flops=4 * SEG * MODEL * FF,
     )
+    first_grad_got = other_core(first_grad_send)
+
+    def part_shapes(columns):
+        return [
+            shape_of((count_of, own_rows, columns), LOW)
+            for count_of in (LINE // 2, LINE // 2, LINE, LINE, LINE)
+        ]
+
+    head_lines = head_lines[:1] + together(*(after(got, pre) for got in head_lines[1:]))
+    cls_far = together(*(after(got, *head_lines[1:]) for got in cls_far))
+    cls_half, cls_out_half = run_kernel(
+        cls_gather_kernel,
+        "head_gather",
+        [
+            shape_of((GROUP, own_rows, QUARTER_HALF), LOW),
+            shape_of((PLANE, own_rows, HALF), LOW),
+        ],
+        where,
+        (),
+        cls_line + (cls_x, cls_y) + cls_far + (cls_out_piece,),
+    )
+    mlp_parts = run_kernel(
+        mlp_weight_kernel,
+        "seg_mlp_weight",
+        part_shapes(FF),
+        where,
+        (),
+        (first_low, first_got, second_low, second_got, after(pre, cls_half), act),
+        [
+            pltpu.VMEM((both_rows, MODEL), LOW),
+            pltpu.VMEM((GROUP, own_rows, FF), LOW),
+            pltpu.SemaphoreType.DMA((GROUP,)),
+        ],
+        far=range(5),
+        flops=4 * SEG * MODEL * FF,
+    )
+    mlp_far = reduce_far(tuple(after(part, *cls_far) for part in mlp_parts[:2]))
     cls_weight, cls_out = run_kernel(
         cls_weight_kernel,
         "head_weight",
@@ -1735,30 +1856,6 @@
     )
     cls_weight = cls_weight.reshape(MODEL, QUARTER)
     cls_out = cls_out.reshape(SPAN, MODEL)
-    first_grad_got = other_core(first_grad_send)
-
-    def part_shapes(columns):
-        return [
-            shape_of((count_of, own_rows, columns), LOW)
-            for count_of in (LINE // 2, LINE // 2, LINE, LINE, LINE)
-        ]
-
-    mlp_parts = run_kernel(
-        mlp_weight_kernel,
-        "seg_mlp_weight",
-        part_shapes(FF),
-        where,
-        (),
-        (first_low, first_got, second_low, second_got, pre, act),
-        [
-            pltpu.VMEM((both_rows, MODEL), LOW),
-            pltpu.VMEM((GROUP, own_rows, FF), LOW),
-            pltpu.SemaphoreType.DMA((GROUP,)),
-        ],
-        far=range(5),
-        flops=4 * SEG * MODEL * FF,
-    )
-    mlp_far = reduce_far(tuple(after(part, *cls_far) for part in mlp_parts[:2]))
     heads, cls_qkv, cls_mixed, part = run_kernel(
         cls_attend_kernel,
         "head_attend",
@@ -1773,8 +1870,8 @@
         tuple(after(got, mlp_parts[0], first_grad_got) for got in head_lines)
         + (vectors, cls_weight, cls_out),
     )
-    cls_normed, cls_inv, cls_low, cls_act, cls_slope, part = run_kernel(
-        cls_mlp_kernel,
+    cls_normed, cls_inv, cls_low, cls_act, cls_slope, part, *mlp_sent = run_kernel(
+        head_mlp_kernel,
         "head_mlp",
         [
             shape_of((GROUP, MODEL)),
@@ -1783,15 +1880,15 @@
             shape_of((GROUP, FF // LINE), LOW),
             shape_of((GROUP, FF // LINE)),
             shape_of((GROUP, MODEL)),
+            shape_of(mlp_parts[2].shape, LOW),
+            shape_of(mlp_parts[2].shape, LOW),
         ],
         where,
         (),
-        (heads,) + line_parts(part) + (vectors, cls_weight),
-    )
+        (heads,) + line_parts(part) + (vectors, cls_weight) + mlp_far + tuple(mlp_parts[2:4]),
+    )
+    mlp_plane = sent_both(*mlp_sent)
     cls_parts = line_parts(part)
-    mlp_far = tuple(after(got, cls_low) for got in mlp_far)
-    mlp_sent = reduce_add(where, mlp_parts, mlp_far)
-    mlp_plane = sent_both(*mlp_sent)
     top_row, square, cls_grad, cls_second, cls_pre, part, top_sums = run_kernel(
         cls_top_kernel,
         "head_top",
@@ -1806,11 +1903,12 @@
         ],
         where,
         (),
-        (heads, cls_parts[0], cls_parts[1])
-        + tuple(after(got, *mlp_sent) for got in cls_parts[2:])
+        (heads,)
+        + cls_parts
         + (vectors, cls_weight, cls_normed, count, cls_slope),
         [pltpu.VMEM((GROUP, MODEL), WIDE)],
     )
+    top_parts = line_parts(part)
     cls_grad, cls_branch, cls_proj, part, back_sums = run_kernel(
         cls_attend_back_kernel,
         "head_attend_back",
@@ -1824,26 +1922,29 @@
         where,
         (),
         (heads,)
-        + line_parts(part)
+        + top_parts
         + (vectors, cls_weight, cls_out, cls_grad, cls_normed, cls_inv, cls_qkv),
     )
     end_parts = line_parts(part)
     pack = jnp.concatenate([cls_proj, cls_mixed, cls_pre, cls_act], axis=1)
-    mlp_plane = [after(got, *end_parts[1:]) for got in mlp_plane]
-    mlp_own, *mlp_sent = reduce_fold(where, mlp_parts[4], mlp_plane, pack)
-    mlp_got = [along_line(mlp_sent[apart - 1], apart) for apart in range(1, LINE)]
-    dheads, head_grad, shared = run_kernel(
-        cls_end_kernel,
+    folded = [shape_of((own_rows, FF))] + [shape_of((own_rows + GROUP, FF), LOW)] * (LINE - 1)
+    dheads, head_grad, shared, mlp_own, *mlp_sent = run_kernel(
+        head_end_kernel,
         "head_end",
-        [shape_of((1, MODEL)), shape_of((1, MODEL)), shape_of((GROUP + 8, MODEL))],
+        [shape_of((1, MODEL)), shape_of((1, MODEL)), shape_of((GROUP + 8, MODEL))] + folded,
         where,
         (),
         (heads, cls_grad)
-        + (after(end_parts[0], mlp_own),)
-        + end_parts[1:]
-        + (square, back_sums, top_sums, normed_second, inv_second, vectors),
+        + end_parts
+        + (square, back_sums, top_sums, normed_second, inv_second, vectors)
+        + (mlp_parts[4],)
+        + mlp_plane
+        + (pack,),
         [pltpu.VMEM((GROUP, MODEL), WIDE)],
     )
+    got_three, got_two = along_line(mlp_sent[2], 3), along_line(mlp_sent[1], 2)
+    got_one = along_line(after(mlp_sent[0], got_two), 1)
+    mlp_got = [got_one, got_two, got_three]
 
     head_own, head_send, head_data = run_kernel(
         head_back_kernel,
@@ -1887,7 +1988,7 @@
             out_weight,
         ),
     )
-    attn_got = after(other_core(attn_send), mlp_own)
+    attn_got = other_core(attn_send)
     proj, input_own, input_send, payload = run_kernel(
         attn_back_kernel,
         "seg_attn_back",
@@ -1930,23 +2031,26 @@
     attn_near = run_kernel(
         attn_near_kernel,
         "seg_attn_near",
-        part_shapes(4 * HALF)[2:],
-        where,
-        (),
-        attn_data,
+        part_shapes(4 * HALF)[2:] + [shape_of((SEG, MODEL), LOW)],
+        where,
+        (),
+        attn_data + (after(top_row, got_two), out_rows, live_row),
         flops=3 * SEG * MODEL * 2 * MODEL,
     )
-    input_grad = (grad_summed + input_own + other_core(input_send)).astype(LOW)
-    row_at = jnp.arange(SEG)[:, None]
-    output = jnp.where(row_at == 0, top_row * live_row[:, :1], out_rows).astype(LOW)
-    payload_parts = line_parts(after(payload, attn_near[0]))
-    attn_far = tuple(after(got, payload_parts[1]) for got in attn_far)
-    attn_sent = reduce_add(where, (None, None) + tuple(attn_near), attn_far)
-    attn_plane = sent_both(*(after(part, mlp_got[1]) for part in attn_sent))
+    output = attn_near[3]
+    *attn_sent, input_grad = run_kernel(
+        attn_add_kernel,
+        "seg_attn_add",
+        [shape_of(attn_near[0].shape, LOW)] * 2 + [shape_of((SEG, MODEL), LOW)],
+        where,
+        (),
+        attn_far + tuple(attn_near[:2]) + (grad_summed, input_own, other_core(input_send)),
+    )
+    attn_plane = sent_both(*attn_sent)
+    payload_parts = line_parts(after(payload, *attn_sent))
     mlp_got = [after(got, attn_plane[0]) for got in mlp_got]
     mlp_sum = reduce_line(mlp_own, mlp_got)
-    shared = after(shared, attn_sent[0])
-    shared = shared + other_core(shared)
+    shared = shared + other_core(after(shared, attn_sent[0]))
     row_width = 8 * MODEL + 2 * FF
     cls_rows = run_kernel(
         cls_rows_kernel,
@@ -1957,60 +2061,50 @@
         (pack,) + tuple(mlp_got) + (heads, cls_branch, cls_low, cls_second),
         [pltpu.VMEM((LINE,) + pack.shape, LOW)],
     )[0]
-    attn_plane = tuple(after(got, cls_rows) for got in attn_plane)
+    cls_got = other_core(cls_rows)
+    attn_plane = tuple(after(got, cls_got, output, input_grad, shared) for got in attn_plane)
     attn_own, *attn_sent = reduce_fold(where, attn_near[2], attn_plane)
-    attn_lines = [along_line(attn_sent[apart - 1], apart) for apart in range(1, LINE)]
+    attn_lines = list(
+        together(*(along_line(attn_sent[apart - 1], apart) for apart in range(1, LINE)))
+    )
+    flat = pltpu.VMEM((1, 8 * MODEL + FF), WIDE)
     payload_line = jnp.concatenate(payload_parts)
-    mlp_mine, own_vecs = run_kernel(
-        head_share_kernel,
-        "seg_head_share",
-        [shape_of((own_rows, FF)), shape_of((16, MODEL))],
-        where,
-        (),
-        tuple(
-            after(got, attn_lines[0]) for got in plane_parts(after(payload_line, *attn_plane))
-        )
-        + (mlp_sum,),
-        [pltpu.VMEM((GROUP * 24, MODEL), LOW)],
-    )
-    flat = pltpu.VMEM((1, 8 * MODEL + FF), WIDE)
-    seg_vec_grad = run_kernel(
-        seg_vec_kernel,
-        "seg_vector",
-        [shape_of((1, vec_size))],
-        where,
-        (),
-        (own_vecs, other_core(own_vecs)),
-        [flat],
-    )[0].reshape(vec_size)
-    seg_mats_grad = run_kernel(
-        mlp_store_kernel,
-        "seg_mlp_store",
-        [shape_of((own_rows, total_columns))],
-        where,
-        (),
-        (mlp_mine, other_core(mlp_mine)),
-        [pltpu.SemaphoreType.DMA((4,))],
+    mlp_mine, own_vecs, cls_mats_grad, cls_vec_grad, pos_total, loss_value = run_kernel(
+        share_owner_kernel,
+        "head_owner",
+        [
+            shape_of((own_rows, FF)),
+            shape_of((16, MODEL)),
+            shape_of((own_rows, total_columns)),
+            shape_of((vec_size,)),
+            shape_of((GROUP, MODEL)),
+            shape_of((1, 1)),
+        ],
+        where,
+        (),
+        tuple(after(got, attn_own) for got in plane_parts(after(payload_line, *attn_plane)))
+        + (mlp_sum, cls_rows, cls_got, shared, count),
+        [
+            pltpu.VMEM((GROUP * 24, MODEL), LOW),
+            pltpu.VMEM((CORES * GROUP, row_width), LOW),
+            flat,
+        ],
+        flops=64 * own_rows * total_columns,
+    )
+    loss_value = loss_value.reshape(())
+    attn_lines = together(*(after(got, mlp_mine) for got in attn_lines))
+    attn_sum = reduce_line(attn_own, attn_lines)
+    seg_mats_grad, seg_vec_grad = run_kernel(
+        store_kernel,
+        "seg_owner",
+        [shape_of((own_rows, total_columns)), shape_of((vec_size,))],
+        where,
+        (),
+        (attn_sum, other_core(attn_sum), mlp_mine, other_core(mlp_mine))
+        + (own_vecs, other_core(own_vecs)),
+        [flat, pltpu.SemaphoreType.DMA((12,))],
         far=(0,),
-    )[0]
-
-    cls_mats_grad, cls_vec_grad = run_kernel(
-        cls_owner_kernel,
-        "head_owner",
-        [shape_of((own_rows, total_columns)), shape_of((1, vec_size))],
-        where,
-        (),
-        (cls_rows, other_core(cls_rows), after(shared, attn_lines[1])),
-        [pltpu.VMEM((CORES * GROUP, row_width), LOW), flat],
-        flops=64 * own_rows * total_columns,
-    )
-    cls_vec_grad = cls_vec_grad.reshape(vec_size)
-    pos_total = shared[:GROUP]
-    loss_value = shared[GROUP, 0] / (count[0, 0] * MODEL)
-    ready = (output, input_grad, cls_mats_grad, cls_vec_grad, pos_total, seg_vec_grad)
-    attn_lines[-1] = after(attn_lines[-1], seg_mats_grad, *ready)
-    attn_sum = reduce_line(attn_own, attn_lines)
-    seg_mats_grad = store_attn(where, attn_sum, other_core(attn_sum), seg_mats_grad)
+    )
 
     return (
         output,

time: 259 us -> 252 us (0.973)
    ppermute x26 -> x28, waiting for transfers between devices: 35.5 us -> 18.8 us  [in_plane(): return lax.ppermute(value, 'fsdp', plane_pairs(mask))]
    ppermute x36, waiting for transfers between devices: 45.3 us -> 60.8 us  [along_line(): return lax.ppermute(value, 'fsdp', line_pairs(apart))]
    ppermute x26 -> x28, starting transfers between devices: 21 us -> 24 us  [in_plane(): return lax.ppermute(value, 'fsdp', plane_pairs(mask))]
    ppermute x20 -> x21, starting transfers between devices: 29.9 us -> 28.3 us  [other_core(): return lax.ppermute(value, 'rep', [(0, 1), (1, 0)])]
    ppermute x20 -> x21, waiting for transfers between devices: 7.73 us -> 8.58 us  [other_core(): return lax.ppermute(value, 'rep', [(0, 1), (1, 0)])]
    pallas_call x31 -> x27, Pallas kernels: 49.1 us -> 48.8 us  [run_kernel(): pl.pallas_call(body, name=name, out_shape=tuple(outs), in_specs=in_specs,...]
  transfers between devices with their start and end apart: 82 -> 85, of which waited for: 35 -> 37; matrix products, arithmetic and copies ran while one was open for 2% -> 0% of each run, Pallas kernels for 18% -> 13%
where the time goes in v6:
time: 252 us; the launch traced here: 250 us
  starting transfers between devices  106 us (42%)
  waiting for transfers between devices  88.1 us (35%)
  Pallas kernels  48.8 us (19%)
  local copies, waits for them, and re-layouts  4.71 us (2%)
    ppermute x36, waiting for transfers between devices, along_line(): return lax.ppermute(value, 'fsdp', line_pairs(apart))  60.8 us
    ppermute x36, starting transfers between devices, along_line(): return lax.ppermute(value, 'fsdp', line_pairs(apart))  53.3 us
    pallas_call x27, Pallas kernels, run_kernel(): pl.pallas_call(body, name=name, out_shape=tuple(outs), in_specs=in_specs,...  48.8 us
    ppermute x21, starting transfers between devices, other_core(): return lax.ppermute(value, 'rep', [(0, 1), (1, 0)])  28.3 us
    ppermute x28, starting transfers between devices, in_plane(): return lax.ppermute(value, 'fsdp', plane_pairs(mask))  24 us
    ppermute x28, waiting for transfers between devices, in_plane(): return lax.ppermute(value, 'fsdp', plane_pairs(mask))  18.8 us
    ppermute x21, waiting for transfers between devices, other_core(): return lax.ppermute(value, 'rep', [(0, 1), (1, 0)])  8.58 us
  transfers between devices with their start and end apart: 85, of which 37 were waited for; matrix products, arithmetic and copies ran while one was open for 0% of the time, Pallas kernels for 13%

profile of v6, /device:TPU:13, one launch (start us, length us, event | category | flops | bytes accessed | tf_op | source)
XLA Modules:
  0.0 249.8 jit_solution(14452861870569612727)
XLA Ops:
  14.1 7.2 %collective-permute-done.1.refs_2_ = bf16[48,1664]{1,0:T(8,128)(2,1)S(1)} collective-permute-done((bf16[48,1664]{1,0:T(8,128)(2,1)S(1)}, bf16[48,1664]{1,0:T(8,128)(2,1)S(1)}, u32[]{:S(2)}, u32[]{:S(2)}) %collective-permute-start.1) | collective-permute-done | bytes 159776 | tf_op jit(solution)/shard_map/ppermute | solution.py:565
  21.3 3.9 %collective-permute-done.refs_1_ = bf16[48,1664]{1,0:T(8,128)(2,1)S(1)} collective-permute-done((bf16[48,1664]{1,0:T(8,128)(2,1)S(1)}, bf16[48,1664]{1,0:T(8,128)(2,1)S(1)}, u32[]{:S(2)}, u32[]{:S(2)}) %collective-permute-start) | collective-permute-done | bytes 159776 | tf_op jit(solution)/shard_map/ppermute | solution.py:565
  30.9 2.5 collective-permute-start.10
  33.3 2.8 %collective-permute-done.11.refs_3_ = bf16[48,1536]{1,0:T(8,128)(2,1)S(1)} collective-permute-done((bf16[48,1536]{1,0:T(8,128)(2,1)S(1)}, bf16[48,1536]{1,0:T(8,128)(2,1)S(1)}, u32[]{:S(2)}, u32[]{:S(2)}) %collective-permute-start.11) | collective-permute-done | bytes 147488 | tf_op jit(solution)/shard_map/ppermute | solution.py:565
  36.1 5.2 %collective-permute-done.10.refs_2_ = bf16[48,1536]{1,0:T(8,128)(2,1)S(1)} collective-permute-done((bf16[48,1536]{1,0:T(8,128)(2,1)S(1)}, bf16[48,1536]{1,0:T(8,128)(2,1)S(1)}, u32[]{:S(2)}, u32[]{:S(2)}) %collective-permute-start.10) | collective-permute-done | bytes 147488 | tf_op jit(solution)/shard_map/ppermute | solution.py:565
  41.3 3.2 %collective-permute-done.9.refs_1_ = bf16[48,1536]{1,0:T(8,128)(2,1)S(1)} collective-permute-done((bf16[48,1536]{1,0:T(8,128)(2,1)S(1)}, bf16[48,1536]{1,0:T(8,128)(2,1)S(1)}, u32[]{:S(2)}, u32[]{:S(2)}) %collective-permute-start.9) | collective-permute-done | bytes 147488 | tf_op jit(solution)/shard_map/ppermute | solution.py:565
  51.5 6.6 %collective-permute-done.16.refs_2_ = bf16[48,1536]{1,0:T(8,128)(2,1)S(1)} collective-permute-done((bf16[48,1536]{1,0:T(8,128)(2,1)S(1)}, bf16[48,1536]{1,0:T(8,128)(2,1)S(1)}, u32[]{:S(2)}, u32[]{:S(2)}) %collective-permute-start.16) | collective-permute-done | bytes 147488 | tf_op jit(solution)/shard_map/ppermute | solution.py:565
  58.1 3.2 %collective-permute-done.15.refs_1_ = bf16[48,1536]{1,0:T(8,128)(2,1)S(1)} collective-permute-done((bf16[48,1536]{1,0:T(8,128)(2,1)S(1)}, bf16[48,1536]{1,0:T(8,128)(2,1)S(1)}, u32[]{:S(2)}, u32[]{:S(2)}) %collective-permute-start.15) | collective-permute-done | bytes 147488 | tf_op jit(solution)/shard_map/ppermute | solution.py:565
  67.6 3.9 %seg_qkv.1 = (bf16[16,48,1152]{2,1,0:T(8,128)(2,1)S(1)}, bf16[8,48,384]{2,1,0:T(8,128)(2,1)S(1)}, bf16[8,48,384]{2,1,0:T(8,128)(2,1)S(1)}, bf16[256,1152]{1,0:T(...) custom-call(s32[5]{0:T(128)S(1)} %stack.24.where, ...), custom_call_target="tpu_custom_call" | custom-call | flops 452984832 | bytes 11453440 | tf_op jit(solution)/shard_map/seg_qkv/pallas_call | solution.py:595
  71.5 3.2 %collective-permute-start.20 = (bf16[8,48,384]{2,1,0:T(8,128)(2,1)S(1)}, bf16[8,48,384]{2,1,0:T(8,128)(2,1)S(1)}, u32[]{:S(2)}, u32[]{:S(2)}) collective-permute-start(bf16[8,48,384]{2,1,0:T(8,128)(2,1)S(1)} %get-tuple-element.293.low), channel_id=1, source_target_pairs={{0,16},{16,0},{1,17},{17,1},{2,18},{18,2},{3,19},{19,3},{4,20},{20... | collective-permute-start | bytes 884744 | tf_op jit(solution)/shard_map/ppermute | solution.py:573
  82.6 3.3 %collective-permute-start.24 = (bf16[128,768]{1,0:T(8,128)(2,1)S(1)}, bf16[128,768]{1,0:T(8,128)(2,1)S(1)}, u32[]{:S(2)}, u32[]{:S(2)}) collective-permute-start(bf16[128,768]{1,0:T(8,128)(2,1)S(1)} %get-tuple-element.302.refs_12_.refs_0_.refs_6_), channel_id=1, source_target_pairs={{0,16},{16,0},{1,17},{17,1},{2,18},{18,2},{3,19},{19,3},{4,20},{20... | collective-permute-start | bytes 589832 | tf_op jit(solution)/shard_map/ppermute | solution.py:573
  91.8 3.1 %collective-permute-start.25 = (f32[128,768]{1,0:T(8,128)S(1)}, f32[128,768]{1,0:T(8,128)S(1)}, u32[]{:S(2)}, u32[]{:S(2)}) collective-permute-start(f32[128,768]{1,0:T(8,128)S(1)} %get-tuple-element.306), channel_id=1, source_target_pairs={{0,16},{16,0},{1,17},{17,1},{2,18},{18,2},{3,19},{19,3},{4,20},{20... | collective-permute-start | bytes 1179656 | tf_op jit(solution)/shard_map/ppermute | solution.py:573
  114.1 2.3 collective-permute-start.42
  116.4 3.1 %seg_mlp_weight.1 = (bf16[2,48,3072]{2,1,0:T(8,128)(2,1)S(1)}, bf16[2,48,3072]{2,1,0:T(8,128)(2,1)S(1)}, bf16[4,48,3072]{2,1,0:T(8,128)(2,1)S(1)}, bf16[4,48,307...) custom-call(s32[5]{0:T(128)S(1)} %stack.24.where, bf16[128,768]{1,0:T(8,128)(2,1)S(1)} %get-tuple-element.302.refs_12_.refs_0_.refs_6_, ...), custom_call_target="tpu_custom_call" | custom-call | flops 1207959552 | bytes 7077888 | tf_op jit(solution)/shard_map/seg_mlp_weight/pallas_call | solution.py:595
  125.8 2.9 %collective-permute-start.46 = (f32[16,768]{1,0:T(8,128)S(1)}, f32[16,768]{1,0:T(8,128)S(1)}, u32[]{:S(2)}, u32[]{:S(2)}) collective-permute-start(f32[16,768]{1,0:T(8,128)S(1)} %get-tuple-element.368.refs_1_), channel_id=1, source_target_pairs={{0,12},{1,13},{2,14},{3,15},{4,0},{5,1},{6,2},{7,3},{8,4},{9,5},{1... | collective-permute-start | bytes 147464 | tf_op jit(solution)/shard_map/ppermute | solution.py:565
  129.2 2.3 collective-permute-start.44
  131.5 3.0 %collective-permute-done.47.refs_7_ = bf16[2,48,3072]{2,1,0:T(8,128)(2,1)S(1)} collective-permute-done((bf16[2,48,3072]{2,1,0:T(8,128)(2,1)S(1)}, bf16[2,48,3072]{2,1,0:T(8,128)(2,1)S(1)}, u32[]{:S(2)}, u32[]{:S(2)}) %collective-permute-start.47) | collective-permute-done | bytes 589856 | tf_op jit(solution)/shard_map/ppermute | solution.py:569
  137.8 3.3 %collective-permute-start.51 = (f32[16,768]{1,0:T(8,128)S(1)}, f32[16,768]{1,0:T(8,128)S(1)}, u32[]{:S(2)}, u32[]{:S(2)}) collective-permute-start(f32[16,768]{1,0:T(8,128)S(1)} %get-tuple-element.379.refs_1_), channel_id=1, source_target_pairs={{0,12},{1,13},{2,14},{3,15},{4,0},{5,1},{6,2},{7,3},{8,4},{9,5},{1... | collective-permute-start | bytes 147464 | tf_op jit(solution)/shard_map/ppermute | solution.py:565
  141.2 2.4 collective-permute-start.49
  159.7 2.5 %collective-permute-done.56.refs_4_ = f32[16,768]{1,0:T(8,128)S(1)} collective-permute-done((f32[16,768]{1,0:T(8,128)S(1)}, f32[16,768]{1,0:T(8,128)S(1)}, u32[]{:S(2)}, u32[]{:S(2)}) %collective-permute-start.56) | collective-permute-done | bytes 49184 | tf_op jit(solution)/shard_map/ppermute | solution.py:565
  164.8 3.2 %collective-permute-start.64 = (bf16[64,3072]{1,0:T(8,128)(2,1)S(1)}, bf16[64,3072]{1,0:T(8,128)(2,1)S(1)}, u32[]{:S(2)}, u32[]{:S(2)}) collective-permute-start(bf16[64,3072]{1,0:T(8,128)(2,1)S(1)} %get-tuple-element.432), channel_id=1, source_target_pairs={{0,12},{1,13},{2,14},{3,15},{4,0},{5,1},{6,2},{7,3},{8,4},{9,5},{1... | collective-permute-start | bytes 1179656 | tf_op jit(solution)/shard_map/ppermute | solution.py:565
  168.0 2.7 %collective-permute-start.60 = (f32[1,768]{1,0:T(1,128)S(1)}, f32[1,768]{1,0:T(1,128)S(1)}, u32[]{:S(2)}, u32[]{:S(2)}) collective-permute-start(f32[1,768]{1,0:T(1,128)S(1)} %get-tuple-element.411.refs_0_.refs_3_), channel_id=1, source_target_pairs={{0,16},{16,0},{1,17},{17,1},{2,18},{18,2},{3,19},{19,3},{4,20},{20... | collective-permute-start | bytes 9224 | tf_op jit(solution)/shard_map/ppermute | solution.py:573
  177.0 4.4 %seg_attn_back.1 = (bf16[256,1152]{1,0:T(8,128)(2,1)S(1)}, f32[128,768]{1,0:T(8,128)S(1)}, f32[128,768]{1,0:T(8,128)S(1)}, bf16[24,768]{1,0:T(8,128)(2,1)S(1)}) custom-call(s32[5]{0:T(128)S(1)} %stack.24.where, bf16[256,1152]{1,0:T(8,128)(2,1)S(1)} %get-tuple-element.297.refs_0_, bf16[128,768]{1,0:T(8,128)(2,1)S(1)} %get-tuple-element.416.refs_1_, ...), custom_call_target="tpu_custom_call" | custom-call | flops 905969664 | bytes 4624384 | tf_op jit(solution)/shard_map/seg_attn_back/pallas_call | solution.py:595
  185.2 10.0 %collective-permute-done.63.refs_2_ = bf16[64,3072]{1,0:T(8,128)(2,1)S(1)} collective-permute-done((bf16[64,3072]{1,0:T(8,128)(2,1)S(1)}, bf16[64,3072]{1,0:T(8,128)(2,1)S(1)}, u32[]{:S(2)}, u32[]{:S(2)}) %collective-permute-start.63) | collective-permute-done | bytes 393248 | tf_op jit(solution)/shard_map/ppermute | solution.py:565
  201.5 11.8 %collective-permute-done.68.got_x = bf16[4,48,1536]{2,1,0:T(8,128)(2,1)S(1)} collective-permute-done((bf16[4,48,1536]{2,1,0:T(8,128)(2,1)S(1)}, bf16[4,48,1536]{2,1,0:T(8,128)(2,1)S(1)}, u32[]{:S(2)}, u32[]{:S(2)}) %collective-permute-start.68) | collective-permute-done | bytes 589856 | tf_op jit(solution)/shard_map/ppermute | solution.py:569
  216.5 2.4 collective-permute-start.78
  219.6 2.4 collective-permute-start.76
  229.4 3.7 %collective-permute-done.74 = bf16[48,1536]{1,0:T(8,128)(2,1)S(1)} collective-permute-done((bf16[48,1536]{1,0:T(8,128)(2,1)S(1)}, bf16[48,1536]{1,0:T(8,128)(2,1)S(1)}, u32[]{:S(2)}, u32[]{:S(2)}) %collective-permute-start.74) | collective-permute-done | bytes 147488 | tf_op jit(solution)/shard_map/ppermute | solution.py:565
  233.1 3.1 %collective-permute-done.75 = bf16[48,1536]{1,0:T(8,128)(2,1)S(1)} collective-permute-done((bf16[48,1536]{1,0:T(8,128)(2,1)S(1)}, bf16[48,1536]{1,0:T(8,128)(2,1)S(1)}, u32[]{:S(2)}, u32[]{:S(2)}) %collective-permute-start.75) | collective-permute-done | bytes 147488 | tf_op jit(solution)/shard_map/ppermute | solution.py:565
  236.2 4.4 %head_owner.1 = (f32[48,3072]{1,0:T(8,128)S(1)}, f32[16,768]{1,0:T(8,128)S(1)}, f32[48,9216]{1,0:T(8,128)}, f32[576]{0:T(1024)}, f32[16,768]{1,0:T(8,128)}, /*index=5*/f32[1,1]{1,0:T(1,128)}) custom-call(s32[5]{0:T(128)S(1)} %stack.24.where, bf16[96,768]{1,0:T(8,128)(2,1)S(1)} %pad_maximum_fusion.11.refs_0_, ...), custom_call_target="tpu_custom_call" | custom-call | flops 28311552 | bytes 4503812 | tf_op jit(solution)/shard_map/head_owner/pallas_call | solution.py:595
  240.6 3.5 %collective-permute-start.83 = (f32[48,3072]{1,0:T(8,128)S(1)}, f32[48,3072]{1,0:T(8,128)S(1)}, u32[]{:S(2)}, u32[]{:S(2)}) collective-permute-start(f32[48,3072]{1,0:T(8,128)S(1)} %get-tuple-element.482.mlp), channel_id=1, source_target_pairs={{0,16},{16,0},{1,17},{17,1},{2,18},{18,2},{3,19},{19,3},{4,20},{20... | collective-permute-start | bytes 1769480 | tf_op jit(solution)/shard_map/ppermute | solution.py:573
  246.3 3.3 %seg_owner.1 = (f32[48,9216]{1,0:T(8,128)}, f32[576]{0:T(1024)}) custom-call(s32[5]{0:T(128)S(1)} %stack.24.where, f32[48,1536]{1,0:T(8,128)S(1)} %convert_add_fusion.1.attn, f32[48,1536]{1,0:T(8,128)S(1)} %collective-permute-done.82.attn_got, f32[48,3072]{1,0:T(8,128)S(1)} %get-tuple-element.482.mlp, f32[48,3072]{1,0:T(8,128)S(1)} %collective-permute-done.83.mlp_got, ...), custom_call_target="tpu_custom_call" | custom-call | bytes 3639552 | tf_op jit(solution)/shard_map/seg_owner/pallas_call | solution.py:595
  (212 shorter events, 122.9 us)
Async XLA Ops:
  7.9 17.3 %collective-permute-start.3 = (bf16[48,4736]{1,0:T(8,128)(2,1)S(1)}, bf16[48,4736]{1,0:T(8,128)(2,1)S(1)}, u32[]{:S(2)}, u32[]{:S(2)}) collective-permute-start(bf16[48,4736]{1,0:T(8,128)(2,1)S(1)} %pad_maximum_fusion.10), channel_id=1, source_target_pairs={{0,1},{1,0},{2,3},{3,2},{4,5},{5,4},{6,7},{7,6},{8,9},{9,8},{10,11... | collective-permute-start | bytes 1363976 | tf_op jit(solution)/shard_map/ppermute | solution.py:569
  9.2 16.0 %collective-permute-start.4 = (bf16[48,4736]{1,0:T(8,128)(2,1)S(1)}, bf16[48,4736]{1,0:T(8,128)(2,1)S(1)}, u32[]{:S(2)}, u32[]{:S(2)}) collective-permute-start(bf16[48,4736]{1,0:T(8,128)(2,1)S(1)} %pad_maximum_fusion.10), channel_id=1, source_target_pairs={{0,2},{1,3},{2,0},{3,1},{4,6},{5,7},{6,4},{7,5},{8,10},{9,11},{10,... | collective-permute-start | bytes 1363976 | tf_op jit(solution)/shard_map/ppermute | solution.py:569
  9.6 11.7 %collective-permute-start.1 = (bf16[48,1664]{1,0:T(8,128)(2,1)S(1)}, bf16[48,1664]{1,0:T(8,128)(2,1)S(1)}, u32[]{:S(2)}, u32[]{:S(2)}) collective-permute-start(bf16[48,1664]{1,0:T(8,128)(2,1)S(1)} %get-tuple-element.253.refs_0_), channel_id=1, source_target_pairs={{0,8},{1,9},{2,10},{3,11},{4,12},{5,13},{6,14},{7,15},{8,0},{9,1},... | collective-permute-start | bytes 479240 | tf_op jit(solution)/shard_map/ppermute | solution.py:565
  11.9 13.3 %collective-permute-start = (bf16[48,1664]{1,0:T(8,128)(2,1)S(1)}, bf16[48,1664]{1,0:T(8,128)(2,1)S(1)}, u32[]{:S(2)}, u32[]{:S(2)}) collective-permute-start(bf16[48,1664]{1,0:T(8,128)(2,1)S(1)} %get-tuple-element.253.refs_0_), channel_id=1, source_target_pairs={{0,4},{1,5},{2,6},{3,7},{4,8},{5,9},{6,10},{7,11},{8,12},{9,13},{1... | collective-permute-start | bytes 479240 | tf_op jit(solution)/shard_map/ppermute | solution.py:565
  25.4 19.1 %collective-permute-start.6 = (bf16[48,7424]{1,0:T(8,128)(2,1)S(1)}, bf16[48,7424]{1,0:T(8,128)(2,1)S(1)}, u32[]{:S(2)}, u32[]{:S(2)}) collective-permute-start(bf16[48,7424]{1,0:T(8,128)(2,1)S(1)} %pad_maximum_fusion.6), channel_id=1, source_target_pairs={{0,2},{1,3},{2,0},{3,1},{4,6},{5,7},{6,4},{7,5},{8,10},{9,11},{10,... | collective-permute-start | bytes 2138120 | tf_op jit(solution)/shard_map/ppermute | solution.py:569
  26.7 17.8 %collective-permute-start.5 = (bf16[48,7296]{1,0:T(8,128)(2,1)S(1)}, bf16[48,7296]{1,0:T(8,128)(2,1)S(1)}, u32[]{:S(2)}, u32[]{:S(2)}) collective-permute-start(bf16[48,7296]{1,0:T(8,128)(2,1)S(1)} %pad_maximum_fusion.7), channel_id=1, source_target_pairs={{0,1},{1,0},{2,3},{3,2},{4,5},{5,4},{6,7},{7,6},{8,9},{9,8},{10,11... | collective-permute-start | bytes 2101256 | tf_op jit(solution)/shard_map/ppermute | solution.py:569
  33.3 11.1 %collective-permute-start.9 = (bf16[48,1536]{1,0:T(8,128)(2,1)S(1)}, bf16[48,1536]{1,0:T(8,128)(2,1)S(1)}, u32[]{:S(2)}, u32[]{:S(2)}) collective-permute-start(bf16[48,1536]{1,0:T(8,128)(2,1)S(1)} %get-tuple-element.273.refs_0_), channel_id=1, source_target_pairs={{0,4},{1,5},{2,6},{3,7},{4,8},{5,9},{6,10},{7,11},{8,12},{9,13},{1... | collective-permute-start | bytes 442376 | tf_op jit(solution)/shard_map/ppermute | solution.py:565
  44.6 16.6 %collective-permute-start.13 = (bf16[48,7168]{1,0:T(8,128)(2,1)S(1)}, bf16[48,7168]{1,0:T(8,128)(2,1)S(1)}, u32[]{:S(2)}, u32[]{:S(2)}) collective-permute-start(bf16[48,7168]{1,0:T(8,128)(2,1)S(1)} %pad_maximum_fusion.8), channel_id=1, source_target_pairs={{0,2},{1,3},{2,0},{3,1},{4,6},{5,7},{6,4},{7,5},{8,10},{9,11},{10,... | collective-permute-start | bytes 2064392 | tf_op jit(solution)/shard_map/ppermute | solution.py:569
  44.9 16.3 %collective-permute-start.12 = (bf16[48,7040]{1,0:T(8,128)(2,1)S(1)}, bf16[48,7040]{1,0:T(8,128)(2,1)S(1)}, u32[]{:S(2)}, u32[]{:S(2)}) collective-permute-start(bf16[48,7040]{1,0:T(8,128)(2,1)S(1)} %pad_maximum_fusion.9), channel_id=1, source_target_pairs={{0,1},{1,0},{2,3},{3,2},{4,5},{5,4},{6,7},{7,6},{8,9},{9,8},{10,11... | collective-permute-start | bytes 2027528 | tf_op jit(solution)/shard_map/ppermute | solution.py:569
  49.5 11.7 %collective-permute-start.15 = (bf16[48,1536]{1,0:T(8,128)(2,1)S(1)}, bf16[48,1536]{1,0:T(8,128)(2,1)S(1)}, u32[]{:S(2)}, u32[]{:S(2)}) collective-permute-start(bf16[48,1536]{1,0:T(8,128)(2,1)S(1)} %get-tuple-element.284.refs_0_), channel_id=1, source_target_pairs={{0,4},{1,5},{2,6},{3,7},{4,8},{5,9},{6,10},{7,11},{8,12},{9,13},{1... | collective-permute-start | bytes 442376 | tf_op jit(solution)/shard_map/ppermute | solution.py:565
  61.4 15.2 %collective-permute-start.18 = (bf16[48,6912]{1,0:T(8,128)(2,1)S(1)}, bf16[48,6912]{1,0:T(8,128)(2,1)S(1)}, u32[]{:S(2)}, u32[]{:S(2)}) collective-permute-start(bf16[48,6912]{1,0:T(8,128)(2,1)S(1)} %get-tuple-element.288), channel_id=1, source_target_pairs={{0,1},{1,0},{2,3},{3,2},{4,5},{5,4},{6,7},{7,6},{8,9},{9,8},{10,11... | collective-permute-start | bytes 1990664 | tf_op jit(solution)/shard_map/ppermute | solution.py:569
  62.6 12.1 %collective-permute-start.32 = (bf16[48,1152]{1,0:T(8,128)(2,1)S(1)}, bf16[48,1152]{1,0:T(8,128)(2,1)S(1)}, u32[]{:S(2)}, u32[]{:S(2)}) collective-permute-start(bf16[48,1152]{1,0:T(8,128)(2,1)S(1)} %get-tuple-element.327), channel_id=1, source_target_pairs={{0,4},{1,5},{2,6},{3,7},{4,8},{5,9},{6,10},{7,11},{8,12},{9,13},{1... | collective-permute-start | bytes 331784 | tf_op jit(solution)/shard_map/ppermute | solution.py:565
  64.8 14.5 %collective-permute-start.19 = (bf16[48,6912]{1,0:T(8,128)(2,1)S(1)}, bf16[48,6912]{1,0:T(8,128)(2,1)S(1)}, u32[]{:S(2)}, u32[]{:S(2)}) collective-permute-start(bf16[48,6912]{1,0:T(8,128)(2,1)S(1)} %get-tuple-element.289), channel_id=1, source_target_pairs={{0,2},{1,3},{2,0},{3,1},{4,6},{5,7},{6,4},{7,5},{8,10},{9,11},{10,... | collective-permute-start | bytes 1990664 | tf_op jit(solution)/shard_map/ppermute | solution.py:569
  74.9 11.0 %collective-permute-start.34 = (bf16[48,1152]{1,0:T(8,128)(2,1)S(1)}, bf16[48,1152]{1,0:T(8,128)(2,1)S(1)}, u32[]{:S(2)}, u32[]{:S(2)}) collective-permute-start(bf16[48,1152]{1,0:T(8,128)(2,1)S(1)} %get-tuple-element.331), channel_id=1, source_target_pairs={{0,12},{1,13},{2,14},{3,15},{4,0},{5,1},{6,2},{7,3},{8,4},{9,5},{1... | collective-permute-start | bytes 331784 | tf_op jit(solution)/shard_map/ppermute | solution.py:565
  88.9 13.7 %collective-permute-start.35 = (bf16[48,4992]{1,0:T(8,128)(2,1)S(1)}, bf16[48,4992]{1,0:T(8,128)(2,1)S(1)}, u32[]{:S(2)}, u32[]{:S(2)}) collective-permute-start(bf16[48,4992]{1,0:T(8,128)(2,1)S(1)} %constant_dynamic-update-slice_fusion), channel_id=1, source_target_pairs={{0,1},{1,0},{2,3},{3,2},{4,5},{5,4},{6,7},{7,6},{8,9},{9,8},{10,11... | collective-permute-start | bytes 1437704 | tf_op jit(solution)/shard_map/ppermute | solution.py:569
  89.8 12.8 %collective-permute-start.36 = (bf16[48,4992]{1,0:T(8,128)(2,1)S(1)}, bf16[48,4992]{1,0:T(8,128)(2,1)S(1)}, u32[]{:S(2)}, u32[]{:S(2)}) collective-permute-start(bf16[48,4992]{1,0:T(8,128)(2,1)S(1)} %constant_dynamic-update-slice_fusion), channel_id=1, source_target_pairs={{0,2},{1,3},{2,0},{3,1},{4,6},{5,7},{6,4},{7,5},{8,10},{9,11},{10,... | collective-permute-start | bytes 1437704 | tf_op jit(solution)/shard_map/ppermute | solution.py:569
  102.6 10.7 %collective-permute-start.38 = (bf16[48,2304]{1,0:T(8,128)(2,1)S(1)}, bf16[48,2304]{1,0:T(8,128)(2,1)S(1)}, u32[]{:S(2)}, u32[]{:S(2)}) collective-permute-start(bf16[48,2304]{1,0:T(8,128)(2,1)S(1)} %slice.52), channel_id=1, source_target_pairs={{0,2},{1,3},{2,0},{3,1},{4,6},{5,7},{6,4},{7,5},{8,10},{9,11},{10,... | collective-permute-start | bytes 663560 | tf_op jit(solution)/shard_map/ppermute | solution.py:569
  119.6 15.0 %collective-permute-start.47 = (bf16[2,48,3072]{2,1,0:T(8,128)(2,1)S(1)}, bf16[2,48,3072]{2,1,0:T(8,128)(2,1)S(1)}, u32[]{:S(2)}, u32[]{:S(2)}) collective-permute-start(bf16[2,48,3072]{2,1,0:T(8,128)(2,1)S(1)} %get-tuple-element.372), channel_id=1, source_target_pairs={{0,2},{1,3},{2,0},{3,1},{4,6},{5,7},{6,4},{7,5},{8,10},{9,11},{10,... | collective-permute-start | bytes 1769480 | tf_op jit(solution)/shard_map/ppermute | solution.py:569
  120.5 14.6 %collective-permute-start.48 = (bf16[2,48,3072]{2,1,0:T(8,128)(2,1)S(1)}, bf16[2,48,3072]{2,1,0:T(8,128)(2,1)S(1)}, u32[]{:S(2)}, u32[]{:S(2)}) collective-permute-start(bf16[2,48,3072]{2,1,0:T(8,128)(2,1)S(1)} %get-tuple-element.374), channel_id=1, source_target_pairs={{0,1},{1,0},{2,3},{3,2},{4,5},{5,4},{6,7},{7,6},{8,9},{9,8},{10,11... | collective-permute-start | bytes 1769480 | tf_op jit(solution)/shard_map/ppermute | solution.py:569
  136.6 26.4 %collective-permute-start.58 = (bf16[4,48,3072]{2,1,0:T(8,128)(2,1)S(1)}, bf16[4,48,3072]{2,1,0:T(8,128)(2,1)S(1)}, u32[]{:S(2)}, u32[]{:S(2)}) collective-permute-start(bf16[4,48,3072]{2,1,0:T(8,128)(2,1)S(1)} %get-tuple-element.403), channel_id=1, source_target_pairs={{0,1},{1,0},{2,3},{3,2},{4,5},{5,4},{6,7},{7,6},{8,9},{9,8},{10,11... | collective-permute-start | bytes 3538952 | tf_op jit(solution)/shard_map/ppermute | solution.py:569
  137.3 26.1 %collective-permute-start.59 = (bf16[4,48,3072]{2,1,0:T(8,128)(2,1)S(1)}, bf16[4,48,3072]{2,1,0:T(8,128)(2,1)S(1)}, u32[]{:S(2)}, u32[]{:S(2)}) collective-permute-start(bf16[4,48,3072]{2,1,0:T(8,128)(2,1)S(1)} %get-tuple-element.404), channel_id=1, source_target_pairs={{0,2},{1,3},{2,0},{3,1},{4,6},{5,7},{6,4},{7,5},{8,10},{9,11},{10,... | collective-permute-start | bytes 3538952 | tf_op jit(solution)/shard_map/ppermute | solution.py:569
  164.8 18.1 %collective-permute-start.64 = (bf16[64,3072]{1,0:T(8,128)(2,1)S(1)}, bf16[64,3072]{1,0:T(8,128)(2,1)S(1)}, u32[]{:S(2)}, u32[]{:S(2)}) collective-permute-start(bf16[64,3072]{1,0:T(8,128)(2,1)S(1)} %get-tuple-element.432), channel_id=1, source_target_pairs={{0,12},{1,13},{2,14},{3,15},{4,0},{5,1},{6,2},{7,3},{8,4},{9,5},{1... | collective-permute-start | bytes 1179656 | tf_op jit(solution)/shard_map/ppermute | solution.py:565
  175.9 19.2 %collective-permute-start.63 = (bf16[64,3072]{1,0:T(8,128)(2,1)S(1)}, bf16[64,3072]{1,0:T(8,128)(2,1)S(1)}, u32[]{:S(2)}, u32[]{:S(2)}) collective-permute-start(bf16[64,3072]{1,0:T(8,128)(2,1)S(1)} %get-tuple-element.427), channel_id=1, source_target_pairs={{0,8},{1,9},{2,10},{3,11},{4,12},{5,13},{6,14},{7,15},{8,0},{9,1},... | collective-permute-start | bytes 1179656 | tf_op jit(solution)/shard_map/ppermute | solution.py:565
  181.5 16.0 %collective-permute-start.67 = (f32[128,768]{1,0:T(8,128)S(1)}, f32[128,768]{1,0:T(8,128)S(1)}, u32[]{:S(2)}, u32[]{:S(2)}) collective-permute-start(f32[128,768]{1,0:T(8,128)S(1)} %get-tuple-element.442), channel_id=1, source_target_pairs={{0,16},{16,0},{1,17},{17,1},{2,18},{18,2},{3,19},{19,3},{4,20},{20... | collective-permute-start | bytes 1179656 | tf_op jit(solution)/shard_map/ppermute | solution.py:573
  182.9 14.5 %collective-permute-start.66 = (bf16[2,48,1536]{2,1,0:T(8,128)(2,1)S(1)}, bf16[2,48,1536]{2,1,0:T(8,128)(2,1)S(1)}, u32[]{:S(2)}, u32[]{:S(2)}) collective-permute-start(bf16[2,48,1536]{2,1,0:T(8,128)(2,1)S(1)} %get-tuple-element.435), channel_id=1, source_target_pairs={{0,1},{1,0},{2,3},{3,2},{4,5},{5,4},{6,7},{7,6},{8,9},{9,8},{10,11... | collective-permute-start | bytes 884744 | tf_op jit(solution)/shard_map/ppermute | solution.py:569
  184.2 13.3 %collective-permute-start.65 = (bf16[2,48,1536]{2,1,0:T(8,128)(2,1)S(1)}, bf16[2,48,1536]{2,1,0:T(8,128)(2,1)S(1)}, u32[]{:S(2)}, u32[]{:S(2)}) collective-permute-start(bf16[2,48,1536]{2,1,0:T(8,128)(2,1)S(1)} %get-tuple-element.433), channel_id=1, source_target_pairs={{0,2},{1,3},{2,0},{3,1},{4,6},{5,7},{6,4},{7,5},{8,10},{9,11},{10,... | collective-permute-start | bytes 884744 | tf_op jit(solution)/shard_map/ppermute | solution.py:569
  198.9 14.4 %collective-permute-start.68 = (bf16[4,48,1536]{2,1,0:T(8,128)(2,1)S(1)}, bf16[4,48,1536]{2,1,0:T(8,128)(2,1)S(1)}, u32[]{:S(2)}, u32[]{:S(2)}) collective-permute-start(bf16[4,48,1536]{2,1,0:T(8,128)(2,1)S(1)} %get-tuple-element.447), channel_id=1, source_target_pairs={{0,1},{1,0},{2,3},{3,2},{4,5},{5,4},{6,7},{7,6},{8,9},{9,8},{10,11... | collective-permute-start | bytes 1769480 | tf_op jit(solution)/shard_map/ppermute | solution.py:569
  200.0 14.1 %collective-permute-start.69 = (bf16[4,48,1536]{2,1,0:T(8,128)(2,1)S(1)}, bf16[4,48,1536]{2,1,0:T(8,128)(2,1)S(1)}, u32[]{:S(2)}, u32[]{:S(2)}) collective-permute-start(bf16[4,48,1536]{2,1,0:T(8,128)(2,1)S(1)} %get-tuple-element.448), channel_id=1, source_target_pairs={{0,2},{1,3},{2,0},{3,1},{4,6},{5,7},{6,4},{7,5},{8,10},{9,11},{10,... | collective-permute-start | bytes 1769480 | tf_op jit(solution)/shard_map/ppermute | solution.py:569
  200.6 13.6 %collective-permute-start.70 = (bf16[64,3072]{1,0:T(8,128)(2,1)S(1)}, bf16[64,3072]{1,0:T(8,128)(2,1)S(1)}, u32[]{:S(2)}, u32[]{:S(2)}) collective-permute-start(bf16[64,3072]{1,0:T(8,128)(2,1)S(1)} %get-tuple-element.451), channel_id=1, source_target_pairs={{0,4},{1,5},{2,6},{3,7},{4,8},{5,9},{6,10},{7,11},{8,12},{9,13},{1... | collective-permute-start | bytes 1179656 | tf_op jit(solution)/shard_map/ppermute | solution.py:565
  223.4 12.8 %collective-permute-start.81 = (bf16[96,768]{1,0:T(8,128)(2,1)S(1)}, bf16[96,768]{1,0:T(8,128)(2,1)S(1)}, u32[]{:S(2)}, u32[]{:S(2)}) collective-permute-start(bf16[96,768]{1,0:T(8,128)(2,1)S(1)} %pad_maximum_fusion.11.refs_0_), channel_id=1, source_target_pairs={{0,3},{1,2},{2,1},{3,0},{4,7},{5,6},{6,5},{7,4},{8,11},{9,10},{10,... | collective-permute-start | bytes 442376 | tf_op jit(solution)/shard_map/ppermute | solution.py:569
  224.0 12.1 %collective-permute-start.80 = (bf16[96,768]{1,0:T(8,128)(2,1)S(1)}, bf16[96,768]{1,0:T(8,128)(2,1)S(1)}, u32[]{:S(2)}, u32[]{:S(2)}) collective-permute-start(bf16[96,768]{1,0:T(8,128)(2,1)S(1)} %pad_maximum_fusion.11.refs_0_), channel_id=1, source_target_pairs={{0,2},{1,3},{2,0},{3,1},{4,6},{5,7},{6,4},{7,5},{8,10},{9,11},{10,... | collective-permute-start | bytes 442376 | tf_op jit(solution)/shard_map/ppermute | solution.py:569
  225.0 11.2 %collective-permute-start.79 = (bf16[96,768]{1,0:T(8,128)(2,1)S(1)}, bf16[96,768]{1,0:T(8,128)(2,1)S(1)}, u32[]{:S(2)}, u32[]{:S(2)}) collective-permute-start(bf16[96,768]{1,0:T(8,128)(2,1)S(1)} %pad_maximum_fusion.11.refs_0_), channel_id=1, source_target_pairs={{0,1},{1,0},{2,3},{3,2},{4,5},{5,4},{6,7},{7,6},{8,9},{9,8},{10,11... | collective-permute-start | bytes 442376 | tf_op jit(solution)/shard_map/ppermute | solution.py:569
  (59 other events, 296.0 us)

commit v7 on v6

--- a/solution.py
+++ b/solution.py
@@ -765,6 +765,12 @@
         order_out[:, mask * SPAN : (mask + 1) * SPAN] = (feature == source).astype(LOW)
 
 
+def prepare_kernel(where, seg, cls, vecs, flags, first_out, live_out, *refs):
+    rest, (first_sems, quarters, sems) = refs[:-3], refs[-3:]
+    prepare_first_kernel(where, seg, vecs, flags, first_out, live_out, first_sems)
+    prepare_rest_kernel(where, seg, cls, *rest, quarters, sems)
+
+
 def lane_mask(rows, head):
     lane = lax.broadcasted_iota(jnp.int32, (rows, LANES), 1)
     return (lane < HEAD_DIM) if head == 0 else (lane >= HEAD_DIM)
@@ -1590,30 +1596,23 @@
     vec_size = seg_vecs.shape[0]
     both_rows = CORES * SEG
 
-    first_piece, live_row = run_kernel(
-        prepare_first_kernel,
-        "prepare_first",
-        [shape_of((own_rows, FIRST), LOW), shape_of((1, SEG))],
-        where,
-        (seg_mats,),
-        (jnp.stack([seg_vecs, cls_vecs]).astype(WIDE), valid_flags[None]),
-        [pltpu.SemaphoreType.DMA((4,))],
-    )
-    first_line = line_parts(first_piece)
-    rest = run_kernel(
-        prepare_rest_kernel,
-        "prepare_rest",
-        [shape_of((own_rows, FF_HALF), LOW)] * 2
+    first_piece, live_row, *rest = run_kernel(
+        prepare_kernel,
+        "prepare",
+        [shape_of((own_rows, FIRST), LOW), shape_of((1, SEG))]
+        + [shape_of((own_rows, FF_HALF), LOW)] * 2
         + [shape_of((own_rows, QUARTER_HALF), LOW)] * LINE
         + [shape_of((own_rows, HALF), LOW), shape_of((MODEL, PLANE * SPAN), LOW)],
         where,
         (seg_mats, cls_mats),
-        (),
+        (jnp.stack([seg_vecs, cls_vecs]).astype(WIDE), valid_flags[None]),
         [
+            pltpu.SemaphoreType.DMA((4,)),
             pltpu.VMEM((LINE, own_rows, QUARTER), LOW),
             pltpu.SemaphoreType.DMA((3 + 5 * LINE,)),
         ],
     )
+    first_line = line_parts(first_piece)
     second_piece, third_piece, quarters, cls_out_piece, order = (
         rest[0],
         rest[1],
@@ -1779,7 +1778,7 @@
     head_lines = line_parts(jnp.concatenate(head_planes))
     size = LINE // 2 * QUARTER_HALF
     cls_far = sent_both(
-        after(cls_y[:, size:], *head_planes[1:]), after(cls_x[:, :size], *head_planes[1:])
+        after(cls_y[:, size:], head_lines[3]), after(cls_x[:, :size], head_lines[3])
     )
 
     second_grad, second_low, second_sums = run_kernel(
@@ -1943,8 +1942,8 @@
         [pltpu.VMEM((GROUP, MODEL), WIDE)],
     )
     got_three, got_two = along_line(mlp_sent[2], 3), along_line(mlp_sent[1], 2)
-    got_one = along_line(after(mlp_sent[0], got_two), 1)
-    mlp_got = [got_one, got_two, got_three]
+    mlp_last = mlp_sent[0]
+    mlp_got = [None, got_two, got_three]
 
     head_own, head_send, head_data = run_kernel(
         head_back_kernel,
@@ -2034,7 +2033,7 @@
         part_shapes(4 * HALF)[2:] + [shape_of((SEG, MODEL), LOW)],
         where,
         (),
-        attn_data + (after(top_row, got_two), out_rows, live_row),
+        attn_data + (top_row, out_rows, live_row),
         flops=3 * SEG * MODEL * 2 * MODEL,
     )
     output = attn_near[3]
@@ -2044,10 +2043,13 @@
         [shape_of(attn_near[0].shape, LOW)] * 2 + [shape_of((SEG, MODEL), LOW)],
         where,
         (),
-        attn_far + tuple(attn_near[:2]) + (grad_summed, input_own, other_core(input_send)),
+        attn_far
+        + tuple(attn_near[:2])
+        + (after(grad_summed, got_two), input_own, other_core(input_send)),
     )
     attn_plane = sent_both(*attn_sent)
     payload_parts = line_parts(after(payload, *attn_sent))
+    mlp_got[0] = along_line(after(mlp_last, *payload_parts[1:]), 1)
     mlp_got = [after(got, attn_plane[0]) for got in mlp_got]
     mlp_sum = reduce_line(mlp_own, mlp_got)
     shared = shared + other_core(after(shared, attn_sent[0]))

time: 252 us -> 259 us (1.028)
  waiting for transfers between devices: 88.1 us -> 99 us
  starting transfers between devices: 106 us -> 102 us
    ppermute x28, waiting for transfers between devices: 18.8 us -> 25.8 us  [in_plane(): return lax.ppermute(value, 'fsdp', plane_pairs(mask))]
    ppermute x21, starting transfers between devices: 28.3 us -> 21.7 us  [other_core(): return lax.ppermute(value, 'rep', [(0, 1), (1, 0)])]
    ppermute x36, waiting for transfers between devices: 60.8 us -> 65.5 us  [along_line(): return lax.ppermute(value, 'fsdp', line_pairs(apart))]
    ppermute x36, starting transfers between devices: 53.3 us -> 56.2 us  [along_line(): return lax.ppermute(value, 'fsdp', line_pairs(apart))]
    pallas_call x27 -> x26, Pallas kernels: 48.8 us -> 48.2 us  [run_kernel(): pl.pallas_call(body, name=name, out_shape=tuple(outs), in_specs=in_specs,...]
  transfers between devices with their start and end apart: 85 -> 85, of which waited for: 37 -> 44; matrix products, arithmetic and copies ran while one was open for 0% -> 0% of each run, Pallas kernels for 13% -> 13%
where the time goes in v7:
time: 259 us; the launch traced here: 257 us
  starting transfers between devices  102 us (39%)
  waiting for transfers between devices  99 us (38%)
  Pallas kernels  48.2 us (19%)
  local copies, waits for them, and re-layouts  5.36 us (2%)
    ppermute x36, waiting for transfers between devices, along_line(): return lax.ppermute(value, 'fsdp', line_pairs(apart))  65.5 us
    ppermute x36, starting transfers between devices, along_line(): return lax.ppermute(value, 'fsdp', line_pairs(apart))  56.2 us
    pallas_call x26, Pallas kernels, run_kernel(): pl.pallas_call(body, name=name, out_shape=tuple(outs), in_specs=in_specs,...  48.2 us
    ppermute x28, waiting for transfers between devices, in_plane(): return lax.ppermute(value, 'fsdp', plane_pairs(mask))  25.8 us
    ppermute x28, starting transfers between devices, in_plane(): return lax.ppermute(value, 'fsdp', plane_pairs(mask))  23.6 us
    ppermute x21, starting transfers between devices, other_core(): return lax.ppermute(value, 'rep', [(0, 1), (1, 0)])  21.7 us
    ppermute x21, waiting for transfers between devices, other_core(): return lax.ppermute(value, 'rep', [(0, 1), (1, 0)])  7.7 us
  transfers between devices with their start and end apart: 85, of which 44 were waited for; matrix products, arithmetic and copies ran while one was open for 0% of the time, Pallas kernels for 13%

profile of v7, /device:TPU:13, one launch (start us, length us, event | category | flops | bytes accessed | tf_op | source)
XLA Modules:
  0.0 256.6 jit_solution(6044769212584293722)
XLA Ops:
  14.2 7.2 %collective-permute-done.1.refs_2_ = bf16[48,1664]{1,0:T(8,128)(2,1)S(1)} collective-permute-done((bf16[48,1664]{1,0:T(8,128)(2,1)S(1)}, bf16[48,1664]{1,0:T(8,128)(2,1)S(1)}, u32[]{:S(2)}, u32[]{:S(2)}) %collective-permute-start.1) | collective-permute-done | bytes 159776 | tf_op jit(solution)/shard_map/ppermute | solution.py:565
  21.4 3.9 %collective-permute-done.refs_1_ = bf16[48,1664]{1,0:T(8,128)(2,1)S(1)} collective-permute-done((bf16[48,1664]{1,0:T(8,128)(2,1)S(1)}, bf16[48,1664]{1,0:T(8,128)(2,1)S(1)}, u32[]{:S(2)}, u32[]{:S(2)}) %collective-permute-start) | collective-permute-done | bytes 159776 | tf_op jit(solution)/shard_map/ppermute | solution.py:565
  30.9 2.5 collective-permute-start.10
  33.4 2.8 %collective-permute-done.11.refs_3_ = bf16[48,1536]{1,0:T(8,128)(2,1)S(1)} collective-permute-done((bf16[48,1536]{1,0:T(8,128)(2,1)S(1)}, bf16[48,1536]{1,0:T(8,128)(2,1)S(1)}, u32[]{:S(2)}, u32[]{:S(2)}) %collective-permute-start.11) | collective-permute-done | bytes 147488 | tf_op jit(solution)/shard_map/ppermute | solution.py:565
  36.2 5.2 %collective-permute-done.10.refs_2_ = bf16[48,1536]{1,0:T(8,128)(2,1)S(1)} collective-permute-done((bf16[48,1536]{1,0:T(8,128)(2,1)S(1)}, bf16[48,1536]{1,0:T(8,128)(2,1)S(1)}, u32[]{:S(2)}, u32[]{:S(2)}) %collective-permute-start.10) | collective-permute-done | bytes 147488 | tf_op jit(solution)/shard_map/ppermute | solution.py:565
  41.4 3.2 %collective-permute-done.9.refs_1_ = bf16[48,1536]{1,0:T(8,128)(2,1)S(1)} collective-permute-done((bf16[48,1536]{1,0:T(8,128)(2,1)S(1)}, bf16[48,1536]{1,0:T(8,128)(2,1)S(1)}, u32[]{:S(2)}, u32[]{:S(2)}) %collective-permute-start.9) | collective-permute-done | bytes 147488 | tf_op jit(solution)/shard_map/ppermute | solution.py:565
  46.2 2.3 collective-permute-start.17
  51.6 6.6 %collective-permute-done.16.refs_2_ = bf16[48,1536]{1,0:T(8,128)(2,1)S(1)} collective-permute-done((bf16[48,1536]{1,0:T(8,128)(2,1)S(1)}, bf16[48,1536]{1,0:T(8,128)(2,1)S(1)}, u32[]{:S(2)}, u32[]{:S(2)}) %collective-permute-start.16) | collective-permute-done | bytes 147488 | tf_op jit(solution)/shard_map/ppermute | solution.py:565
  58.1 3.2 %collective-permute-done.15.refs_1_ = bf16[48,1536]{1,0:T(8,128)(2,1)S(1)} collective-permute-done((bf16[48,1536]{1,0:T(8,128)(2,1)S(1)}, bf16[48,1536]{1,0:T(8,128)(2,1)S(1)}, u32[]{:S(2)}, u32[]{:S(2)}) %collective-permute-start.15) | collective-permute-done | bytes 147488 | tf_op jit(solution)/shard_map/ppermute | solution.py:565
  65.8 3.9 %seg_qkv.1 = (bf16[16,48,1152]{2,1,0:T(8,128)(2,1)S(1)}, bf16[8,48,384]{2,1,0:T(8,128)(2,1)S(1)}, bf16[8,48,384]{2,1,0:T(8,128)(2,1)S(1)}, bf16[256,1152]{1,0:T(...) custom-call(s32[5]{0:T(128)S(1)} %stack.24.where, ...), custom_call_target="tpu_custom_call" | custom-call | flops 452984832 | bytes 11453440 | tf_op jit(solution)/shard_map/seg_qkv/pallas_call | solution.py:595
  69.7 2.6 collective-permute-start.20
  98.5 8.1 %collective-permute-done.31 = f32[1,1664]{1,0:T(1,128)S(1)} collective-permute-done((f32[1,1664]{1,0:T(1,128)S(1)}, f32[1,1664]{1,0:T(1,128)S(1)}, u32[]{:S(2)}, u32[]{:S(2)}) %collective-permute-start.31) | collective-permute-done | bytes 6688 | tf_op jit(solution)/shard_map/ppermute | solution.py:569
  118.5 2.4 collective-permute-done.41.refs_7_
  124.1 3.1 %seg_mlp_weight.1 = (bf16[2,48,3072]{2,1,0:T(8,128)(2,1)S(1)}, bf16[2,48,3072]{2,1,0:T(8,128)(2,1)S(1)}, bf16[4,48,3072]{2,1,0:T(8,128)(2,1)S(1)}, bf16[4,48,307...) custom-call(s32[5]{0:T(128)S(1)} %stack.24.where, bf16[128,768]{1,0:T(8,128)(2,1)S(1)} %get-tuple-element.302.refs_12_.refs_0_.refs_6_, ...), custom_call_target="tpu_custom_call" | custom-call | flops 1207959552 | bytes 7077888 | tf_op jit(solution)/shard_map/seg_mlp_weight/pallas_call | solution.py:595
  136.2 2.3 collective-permute-start.44
  138.6 3.7 %collective-permute-done.47.refs_7_ = bf16[2,48,3072]{2,1,0:T(8,128)(2,1)S(1)} collective-permute-done((bf16[2,48,3072]{2,1,0:T(8,128)(2,1)S(1)}, bf16[2,48,3072]{2,1,0:T(8,128)(2,1)S(1)}, u32[]{:S(2)}, u32[]{:S(2)}) %collective-permute-start.47) | collective-permute-done | bytes 589856 | tf_op jit(solution)/shard_map/ppermute | solution.py:569
  148.2 2.4 collective-permute-start.49
  155.7 2.4 collective-permute-start.53
  172.7 2.3 collective-permute-start.63
  175.0 2.7 %collective-permute-start.60 = (f32[1,768]{1,0:T(1,128)S(1)}, f32[1,768]{1,0:T(1,128)S(1)}, u32[]{:S(2)}, u32[]{:S(2)}) collective-permute-start(f32[1,768]{1,0:T(1,128)S(1)} %get-tuple-element.411.refs_0_.refs_3_), channel_id=1, source_target_pairs={{0,16},{16,0},{1,17},{17,1},{2,18},{18,2},{3,19},{19,3},{4,20},{20... | collective-permute-start | bytes 9224 | tf_op jit(solution)/shard_map/ppermute | solution.py:573
  184.0 4.4 %seg_attn_back.1 = (bf16[256,1152]{1,0:T(8,128)(2,1)S(1)}, f32[128,768]{1,0:T(8,128)S(1)}, f32[128,768]{1,0:T(8,128)S(1)}, bf16[24,768]{1,0:T(8,128)(2,1)S(1)}) custom-call(s32[5]{0:T(128)S(1)} %stack.24.where, bf16[256,1152]{1,0:T(8,128)(2,1)S(1)} %get-tuple-element.297.refs_0_, bf16[128,768]{1,0:T(8,128)(2,1)S(1)} %get-tuple-element.416.refs_1_, ...), custom_call_target="tpu_custom_call" | custom-call | flops 905969664 | bytes 4624384 | tf_op jit(solution)/shard_map/seg_attn_back/pallas_call | solution.py:595
  194.1 8.1 %collective-permute-done.66.refs_2_ = bf16[64,3072]{1,0:T(8,128)(2,1)S(1)} collective-permute-done((bf16[64,3072]{1,0:T(8,128)(2,1)S(1)}, bf16[64,3072]{1,0:T(8,128)(2,1)S(1)}, u32[]{:S(2)}, u32[]{:S(2)}) %collective-permute-start.66) | collective-permute-done | bytes 393248 | tf_op jit(solution)/shard_map/ppermute | solution.py:565
  205.0 2.7 %collective-permute-start.72 = (bf16[24,768]{1,0:T(8,128)(2,1)S(1)}, bf16[24,768]{1,0:T(8,128)(2,1)S(1)}, u32[]{:S(2)}, u32[]{:S(2)}) collective-permute-start(bf16[24,768]{1,0:T(8,128)(2,1)S(1)} %get-tuple-element.452), channel_id=1, source_target_pairs={{0,12},{1,13},{2,14},{3,15},{4,0},{5,1},{6,2},{7,3},{8,4},{9,5},{1... | collective-permute-start | bytes 110600 | tf_op jit(solution)/shard_map/ppermute | solution.py:565
  208.1 2.4 collective-permute-start.70
  214.3 3.6 %collective-permute-done.68.got_x = bf16[4,48,1536]{2,1,0:T(8,128)(2,1)S(1)} collective-permute-done((bf16[4,48,1536]{2,1,0:T(8,128)(2,1)S(1)}, bf16[4,48,1536]{2,1,0:T(8,128)(2,1)S(1)}, u32[]{:S(2)}, u32[]{:S(2)}) %collective-permute-start.68) | collective-permute-done | bytes 589856 | tf_op jit(solution)/shard_map/ppermute | solution.py:569
  218.5 2.6 %collective-permute-done.73.refs_1_ = bf16[64,3072]{1,0:T(8,128)(2,1)S(1)} collective-permute-done((bf16[64,3072]{1,0:T(8,128)(2,1)S(1)}, bf16[64,3072]{1,0:T(8,128)(2,1)S(1)}, u32[]{:S(2)}, u32[]{:S(2)}) %collective-permute-start.73) | collective-permute-done | bytes 393248 | tf_op jit(solution)/shard_map/ppermute | solution.py:565
  221.7 2.9 %collective-permute-start.74 = (bf16[16,12288]{1,0:T(8,128)(2,1)S(1)}, bf16[16,12288]{1,0:T(8,128)(2,1)S(1)}, u32[]{:S(2)}, u32[]{:S(2)}) collective-permute-start(bf16[16,12288]{1,0:T(8,128)(2,1)S(1)} %head_rows.1.refs_5_), channel_id=1, source_target_pairs={{0,16},{16,0},{1,17},{17,1},{2,18},{18,2},{3,19},{19,3},{4,20},{20... | collective-permute-start | bytes 1179656 | tf_op jit(solution)/shard_map/ppermute | solution.py:573
  231.6 3.4 %collective-permute-start.77 = (bf16[48,1536]{1,0:T(8,128)(2,1)S(1)}, bf16[48,1536]{1,0:T(8,128)(2,1)S(1)}, u32[]{:S(2)}, u32[]{:S(2)}) collective-permute-start(bf16[48,1536]{1,0:T(8,128)(2,1)S(1)} %get-tuple-element.470), channel_id=1, source_target_pairs={{0,8},{1,9},{2,10},{3,11},{4,12},{5,13},{6,14},{7,15},{8,0},{9,1},... | collective-permute-start | bytes 442376 | tf_op jit(solution)/shard_map/ppermute | solution.py:565
  237.2 5.3 %collective-permute-done.77 = bf16[48,1536]{1,0:T(8,128)(2,1)S(1)} collective-permute-done((bf16[48,1536]{1,0:T(8,128)(2,1)S(1)}, bf16[48,1536]{1,0:T(8,128)(2,1)S(1)}, u32[]{:S(2)}, u32[]{:S(2)}) %collective-permute-start.77) | collective-permute-done | bytes 147488 | tf_op jit(solution)/shard_map/ppermute | solution.py:565
  242.4 3.7 %collective-permute-done.78 = bf16[48,1536]{1,0:T(8,128)(2,1)S(1)} collective-permute-done((bf16[48,1536]{1,0:T(8,128)(2,1)S(1)}, bf16[48,1536]{1,0:T(8,128)(2,1)S(1)}, u32[]{:S(2)}, u32[]{:S(2)}) %collective-permute-start.78) | collective-permute-done | bytes 147488 | tf_op jit(solution)/shard_map/ppermute | solution.py:565
  246.1 4.4 %head_owner.1 = (f32[48,3072]{1,0:T(8,128)S(1)}, f32[16,768]{1,0:T(8,128)S(1)}, f32[48,9216]{1,0:T(8,128)}, f32[576]{0:T(1024)}, f32[16,768]{1,0:T(8,128)}, /*index=5*/f32[1,1]{1,0:T(1,128)}) custom-call(s32[5]{0:T(128)S(1)} %stack.24.where, bf16[96,768]{1,0:T(8,128)(2,1)S(1)} %pad_maximum_fusion.11.refs_0_, ...), custom_call_target="tpu_custom_call" | custom-call | flops 28311552 | bytes 4503812 | tf_op jit(solution)/shard_map/head_owner/pallas_call | solution.py:595
  253.1 3.3 %seg_owner.1 = (f32[48,9216]{1,0:T(8,128)}, f32[576]{0:T(1024)}) custom-call(s32[5]{0:T(128)S(1)} %stack.24.where, f32[48,1536]{1,0:T(8,128)S(1)} %convert_add_fusion.1.attn, f32[48,1536]{1,0:T(8,128)S(1)} %collective-permute-done.82.attn_got, f32[48,3072]{1,0:T(8,128)S(1)} %get-tuple-element.482.mlp, f32[48,3072]{1,0:T(8,128)S(1)} %collective-permute-done.83.mlp_got, ...), custom_call_target="tpu_custom_call" | custom-call | bytes 3639552 | tf_op jit(solution)/shard_map/seg_owner/pallas_call | solution.py:595
  (211 shorter events, 135.2 us)
Async XLA Ops:
  8.0 17.3 %collective-permute-start.3 = (bf16[48,4736]{1,0:T(8,128)(2,1)S(1)}, bf16[48,4736]{1,0:T(8,128)(2,1)S(1)}, u32[]{:S(2)}, u32[]{:S(2)}) collective-permute-start(bf16[48,4736]{1,0:T(8,128)(2,1)S(1)} %pad_maximum_fusion.10), channel_id=1, source_target_pairs={{0,1},{1,0},{2,3},{3,2},{4,5},{5,4},{6,7},{7,6},{8,9},{9,8},{10,11... | collective-permute-start | bytes 1363976 | tf_op jit(solution)/shard_map/ppermute | solution.py:569
  9.3 16.0 %collective-permute-start.4 = (bf16[48,4736]{1,0:T(8,128)(2,1)S(1)}, bf16[48,4736]{1,0:T(8,128)(2,1)S(1)}, u32[]{:S(2)}, u32[]{:S(2)}) collective-permute-start(bf16[48,4736]{1,0:T(8,128)(2,1)S(1)} %pad_maximum_fusion.10), channel_id=1, source_target_pairs={{0,2},{1,3},{2,0},{3,1},{4,6},{5,7},{6,4},{7,5},{8,10},{9,11},{10,... | collective-permute-start | bytes 1363976 | tf_op jit(solution)/shard_map/ppermute | solution.py:569
  9.7 11.7 %collective-permute-start.1 = (bf16[48,1664]{1,0:T(8,128)(2,1)S(1)}, bf16[48,1664]{1,0:T(8,128)(2,1)S(1)}, u32[]{:S(2)}, u32[]{:S(2)}) collective-permute-start(bf16[48,1664]{1,0:T(8,128)(2,1)S(1)} %get-tuple-element.253.refs_0_), channel_id=1, source_target_pairs={{0,8},{1,9},{2,10},{3,11},{4,12},{5,13},{6,14},{7,15},{8,0},{9,1},... | collective-permute-start | bytes 479240 | tf_op jit(solution)/shard_map/ppermute | solution.py:565
  12.0 13.3 %collective-permute-start = (bf16[48,1664]{1,0:T(8,128)(2,1)S(1)}, bf16[48,1664]{1,0:T(8,128)(2,1)S(1)}, u32[]{:S(2)}, u32[]{:S(2)}) collective-permute-start(bf16[48,1664]{1,0:T(8,128)(2,1)S(1)} %get-tuple-element.253.refs_0_), channel_id=1, source_target_pairs={{0,4},{1,5},{2,6},{3,7},{4,8},{5,9},{6,10},{7,11},{8,12},{9,13},{1... | collective-permute-start | bytes 479240 | tf_op jit(solution)/shard_map/ppermute | solution.py:565
  25.5 19.1 %collective-permute-start.6 = (bf16[48,7424]{1,0:T(8,128)(2,1)S(1)}, bf16[48,7424]{1,0:T(8,128)(2,1)S(1)}, u32[]{:S(2)}, u32[]{:S(2)}) collective-permute-start(bf16[48,7424]{1,0:T(8,128)(2,1)S(1)} %pad_maximum_fusion.6), channel_id=1, source_target_pairs={{0,2},{1,3},{2,0},{3,1},{4,6},{5,7},{6,4},{7,5},{8,10},{9,11},{10,... | collective-permute-start | bytes 2138120 | tf_op jit(solution)/shard_map/ppermute | solution.py:569
  26.8 17.8 %collective-permute-start.5 = (bf16[48,7296]{1,0:T(8,128)(2,1)S(1)}, bf16[48,7296]{1,0:T(8,128)(2,1)S(1)}, u32[]{:S(2)}, u32[]{:S(2)}) collective-permute-start(bf16[48,7296]{1,0:T(8,128)(2,1)S(1)} %pad_maximum_fusion.7), channel_id=1, source_target_pairs={{0,1},{1,0},{2,3},{3,2},{4,5},{5,4},{6,7},{7,6},{8,9},{9,8},{10,11... | collective-permute-start | bytes 2101256 | tf_op jit(solution)/shard_map/ppermute | solution.py:569
  33.4 11.1 %collective-permute-start.9 = (bf16[48,1536]{1,0:T(8,128)(2,1)S(1)}, bf16[48,1536]{1,0:T(8,128)(2,1)S(1)}, u32[]{:S(2)}, u32[]{:S(2)}) collective-permute-start(bf16[48,1536]{1,0:T(8,128)(2,1)S(1)} %get-tuple-element.273.refs_0_), channel_id=1, source_target_pairs={{0,4},{1,5},{2,6},{3,7},{4,8},{5,9},{6,10},{7,11},{8,12},{9,13},{1... | collective-permute-start | bytes 442376 | tf_op jit(solution)/shard_map/ppermute | solution.py:565
  44.7 16.6 %collective-permute-start.13 = (bf16[48,7168]{1,0:T(8,128)(2,1)S(1)}, bf16[48,7168]{1,0:T(8,128)(2,1)S(1)}, u32[]{:S(2)}, u32[]{:S(2)}) collective-permute-start(bf16[48,7168]{1,0:T(8,128)(2,1)S(1)} %pad_maximum_fusion.8), channel_id=1, source_target_pairs={{0,2},{1,3},{2,0},{3,1},{4,6},{5,7},{6,4},{7,5},{8,10},{9,11},{10,... | collective-permute-start | bytes 2064392 | tf_op jit(solution)/shard_map/ppermute | solution.py:569
  45.0 16.3 %collective-permute-start.12 = (bf16[48,7040]{1,0:T(8,128)(2,1)S(1)}, bf16[48,7040]{1,0:T(8,128)(2,1)S(1)}, u32[]{:S(2)}, u32[]{:S(2)}) collective-permute-start(bf16[48,7040]{1,0:T(8,128)(2,1)S(1)} %pad_maximum_fusion.9), channel_id=1, source_target_pairs={{0,1},{1,0},{2,3},{3,2},{4,5},{5,4},{6,7},{7,6},{8,9},{9,8},{10,11... | collective-permute-start | bytes 2027528 | tf_op jit(solution)/shard_map/ppermute | solution.py:569
  49.6 11.7 %collective-permute-start.15 = (bf16[48,1536]{1,0:T(8,128)(2,1)S(1)}, bf16[48,1536]{1,0:T(8,128)(2,1)S(1)}, u32[]{:S(2)}, u32[]{:S(2)}) collective-permute-start(bf16[48,1536]{1,0:T(8,128)(2,1)S(1)} %get-tuple-element.284.refs_0_), channel_id=1, source_target_pairs={{0,4},{1,5},{2,6},{3,7},{4,8},{5,9},{6,10},{7,11},{8,12},{9,13},{1... | collective-permute-start | bytes 442376 | tf_op jit(solution)/shard_map/ppermute | solution.py:565
  61.5 15.2 %collective-permute-start.18 = (bf16[48,6912]{1,0:T(8,128)(2,1)S(1)}, bf16[48,6912]{1,0:T(8,128)(2,1)S(1)}, u32[]{:S(2)}, u32[]{:S(2)}) collective-permute-start(bf16[48,6912]{1,0:T(8,128)(2,1)S(1)} %get-tuple-element.288), channel_id=1, source_target_pairs={{0,1},{1,0},{2,3},{3,2},{4,5},{5,4},{6,7},{7,6},{8,9},{9,8},{10,11... | collective-permute-start | bytes 1990664 | tf_op jit(solution)/shard_map/ppermute | solution.py:569
  62.7 16.2 %collective-permute-start.19 = (bf16[48,6912]{1,0:T(8,128)(2,1)S(1)}, bf16[48,6912]{1,0:T(8,128)(2,1)S(1)}, u32[]{:S(2)}, u32[]{:S(2)}) collective-permute-start(bf16[48,6912]{1,0:T(8,128)(2,1)S(1)} %get-tuple-element.289), channel_id=1, source_target_pairs={{0,2},{1,3},{2,0},{3,1},{4,6},{5,7},{6,4},{7,5},{8,10},{9,11},{10,... | collective-permute-start | bytes 1990664 | tf_op jit(solution)/shard_map/ppermute | solution.py:569
  69.7 12.5 %collective-permute-start.20 = (bf16[8,48,384]{2,1,0:T(8,128)(2,1)S(1)}, bf16[8,48,384]{2,1,0:T(8,128)(2,1)S(1)}, u32[]{:S(2)}, u32[]{:S(2)}) collective-permute-start(bf16[8,48,384]{2,1,0:T(8,128)(2,1)S(1)} %get-tuple-element.293.low), channel_id=1, source_target_pairs={{0,16},{16,0},{1,17},{17,1},{2,18},{18,2},{3,19},{19,3},{4,20},{20... | collective-permute-start | bytes 884744 | tf_op jit(solution)/shard_map/ppermute | solution.py:573
  72.4 13.3 %collective-permute-start.33 = (bf16[48,1152]{1,0:T(8,128)(2,1)S(1)}, bf16[48,1152]{1,0:T(8,128)(2,1)S(1)}, u32[]{:S(2)}, u32[]{:S(2)}) collective-permute-start(bf16[48,1152]{1,0:T(8,128)(2,1)S(1)} %get-tuple-element.329), channel_id=1, source_target_pairs={{0,8},{1,9},{2,10},{3,11},{4,12},{5,13},{6,14},{7,15},{8,0},{9,1},... | collective-permute-start | bytes 331784 | tf_op jit(solution)/shard_map/ppermute | solution.py:565
  78.9 14.6 %collective-permute-start.34 = (bf16[48,1152]{1,0:T(8,128)(2,1)S(1)}, bf16[48,1152]{1,0:T(8,128)(2,1)S(1)}, u32[]{:S(2)}, u32[]{:S(2)}) collective-permute-start(bf16[48,1152]{1,0:T(8,128)(2,1)S(1)} %get-tuple-element.331), channel_id=1, source_target_pairs={{0,12},{1,13},{2,14},{3,15},{4,0},{5,1},{6,2},{7,3},{8,4},{9,5},{1... | collective-permute-start | bytes 331784 | tf_op jit(solution)/shard_map/ppermute | solution.py:565
  93.6 21.1 %collective-permute-start.35 = (bf16[48,4992]{1,0:T(8,128)(2,1)S(1)}, bf16[48,4992]{1,0:T(8,128)(2,1)S(1)}, u32[]{:S(2)}, u32[]{:S(2)}) collective-permute-start(bf16[48,4992]{1,0:T(8,128)(2,1)S(1)} %constant_dynamic-update-slice_fusion), channel_id=1, source_target_pairs={{0,1},{1,0},{2,3},{3,2},{4,5},{5,4},{6,7},{7,6},{8,9},{9,8},{10,11... | collective-permute-start | bytes 1437704 | tf_op jit(solution)/shard_map/ppermute | solution.py:569
  93.9 20.8 %collective-permute-start.36 = (bf16[48,4992]{1,0:T(8,128)(2,1)S(1)}, bf16[48,4992]{1,0:T(8,128)(2,1)S(1)}, u32[]{:S(2)}, u32[]{:S(2)}) collective-permute-start(bf16[48,4992]{1,0:T(8,128)(2,1)S(1)} %constant_dynamic-update-slice_fusion), channel_id=1, source_target_pairs={{0,2},{1,3},{2,0},{3,1},{4,6},{5,7},{6,4},{7,5},{8,10},{9,11},{10,... | collective-permute-start | bytes 1437704 | tf_op jit(solution)/shard_map/ppermute | solution.py:569
  127.2 15.0 %collective-permute-start.47 = (bf16[2,48,3072]{2,1,0:T(8,128)(2,1)S(1)}, bf16[2,48,3072]{2,1,0:T(8,128)(2,1)S(1)}, u32[]{:S(2)}, u32[]{:S(2)}) collective-permute-start(bf16[2,48,3072]{2,1,0:T(8,128)(2,1)S(1)} %get-tuple-element.372), channel_id=1, source_target_pairs={{0,2},{1,3},{2,0},{3,1},{4,6},{5,7},{6,4},{7,5},{8,10},{9,11},{10,... | collective-permute-start | bytes 1769480 | tf_op jit(solution)/shard_map/ppermute | solution.py:569
  128.2 14.6 %collective-permute-start.48 = (bf16[2,48,3072]{2,1,0:T(8,128)(2,1)S(1)}, bf16[2,48,3072]{2,1,0:T(8,128)(2,1)S(1)}, u32[]{:S(2)}, u32[]{:S(2)}) collective-permute-start(bf16[2,48,3072]{2,1,0:T(8,128)(2,1)S(1)} %get-tuple-element.374), channel_id=1, source_target_pairs={{0,1},{1,0},{2,3},{3,2},{4,5},{5,4},{6,7},{7,6},{8,9},{9,8},{10,11... | collective-permute-start | bytes 1769480 | tf_op jit(solution)/shard_map/ppermute | solution.py:569
  144.3 26.4 %collective-permute-start.58 = (bf16[4,48,3072]{2,1,0:T(8,128)(2,1)S(1)}, bf16[4,48,3072]{2,1,0:T(8,128)(2,1)S(1)}, u32[]{:S(2)}, u32[]{:S(2)}) collective-permute-start(bf16[4,48,3072]{2,1,0:T(8,128)(2,1)S(1)} %get-tuple-element.403), channel_id=1, source_target_pairs={{0,1},{1,0},{2,3},{3,2},{4,5},{5,4},{6,7},{7,6},{8,9},{9,8},{10,11... | collective-permute-start | bytes 3538952 | tf_op jit(solution)/shard_map/ppermute | solution.py:569
  145.1 26.1 %collective-permute-start.59 = (bf16[4,48,3072]{2,1,0:T(8,128)(2,1)S(1)}, bf16[4,48,3072]{2,1,0:T(8,128)(2,1)S(1)}, u32[]{:S(2)}, u32[]{:S(2)}) collective-permute-start(bf16[4,48,3072]{2,1,0:T(8,128)(2,1)S(1)} %get-tuple-element.404), channel_id=1, source_target_pairs={{0,2},{1,3},{2,0},{3,1},{4,6},{5,7},{6,4},{7,5},{8,10},{9,11},{10,... | collective-permute-start | bytes 3538952 | tf_op jit(solution)/shard_map/ppermute | solution.py:569
  172.7 17.2 %collective-permute-start.63 = (bf16[64,3072]{1,0:T(8,128)(2,1)S(1)}, bf16[64,3072]{1,0:T(8,128)(2,1)S(1)}, u32[]{:S(2)}, u32[]{:S(2)}) collective-permute-start(bf16[64,3072]{1,0:T(8,128)(2,1)S(1)} %get-tuple-element.430), channel_id=1, source_target_pairs={{0,12},{1,13},{2,14},{3,15},{4,0},{5,1},{6,2},{7,3},{8,4},{9,5},{1... | collective-permute-start | bytes 1179656 | tf_op jit(solution)/shard_map/ppermute | solution.py:565
  182.9 19.2 %collective-permute-start.66 = (bf16[64,3072]{1,0:T(8,128)(2,1)S(1)}, bf16[64,3072]{1,0:T(8,128)(2,1)S(1)}, u32[]{:S(2)}, u32[]{:S(2)}) collective-permute-start(bf16[64,3072]{1,0:T(8,128)(2,1)S(1)} %get-tuple-element.439), channel_id=1, source_target_pairs={{0,8},{1,9},{2,10},{3,11},{4,12},{5,13},{6,14},{7,15},{8,0},{9,1},... | collective-permute-start | bytes 1179656 | tf_op jit(solution)/shard_map/ppermute | solution.py:565
  188.4 13.7 %collective-permute-start.67 = (f32[128,768]{1,0:T(8,128)S(1)}, f32[128,768]{1,0:T(8,128)S(1)}, u32[]{:S(2)}, u32[]{:S(2)}) collective-permute-start(f32[128,768]{1,0:T(8,128)S(1)} %get-tuple-element.442), channel_id=1, source_target_pairs={{0,16},{16,0},{1,17},{17,1},{2,18},{18,2},{3,19},{19,3},{4,20},{20... | collective-permute-start | bytes 1179656 | tf_op jit(solution)/shard_map/ppermute | solution.py:573
  189.9 12.3 %collective-permute-start.65 = (bf16[2,48,1536]{2,1,0:T(8,128)(2,1)S(1)}, bf16[2,48,1536]{2,1,0:T(8,128)(2,1)S(1)}, u32[]{:S(2)}, u32[]{:S(2)}) collective-permute-start(bf16[2,48,1536]{2,1,0:T(8,128)(2,1)S(1)} %get-tuple-element.433), channel_id=1, source_target_pairs={{0,1},{1,0},{2,3},{3,2},{4,5},{5,4},{6,7},{7,6},{8,9},{9,8},{10,11... | collective-permute-start | bytes 884744 | tf_op jit(solution)/shard_map/ppermute | solution.py:569
  190.9 11.3 %collective-permute-start.64 = (bf16[2,48,1536]{2,1,0:T(8,128)(2,1)S(1)}, bf16[2,48,1536]{2,1,0:T(8,128)(2,1)S(1)}, u32[]{:S(2)}, u32[]{:S(2)}) collective-permute-start(bf16[2,48,1536]{2,1,0:T(8,128)(2,1)S(1)} %get-tuple-element.431), channel_id=1, source_target_pairs={{0,2},{1,3},{2,0},{3,1},{4,6},{5,7},{6,4},{7,5},{8,10},{9,11},{10,... | collective-permute-start | bytes 884744 | tf_op jit(solution)/shard_map/ppermute | solution.py:569
  203.6 14.4 %collective-permute-start.68 = (bf16[4,48,1536]{2,1,0:T(8,128)(2,1)S(1)}, bf16[4,48,1536]{2,1,0:T(8,128)(2,1)S(1)}, u32[]{:S(2)}, u32[]{:S(2)}) collective-permute-start(bf16[4,48,1536]{2,1,0:T(8,128)(2,1)S(1)} %get-tuple-element.447), channel_id=1, source_target_pairs={{0,1},{1,0},{2,3},{3,2},{4,5},{5,4},{6,7},{7,6},{8,9},{9,8},{10,11... | collective-permute-start | bytes 1769480 | tf_op jit(solution)/shard_map/ppermute | solution.py:569
  204.4 14.1 %collective-permute-start.69 = (bf16[4,48,1536]{2,1,0:T(8,128)(2,1)S(1)}, bf16[4,48,1536]{2,1,0:T(8,128)(2,1)S(1)}, u32[]{:S(2)}, u32[]{:S(2)}) collective-permute-start(bf16[4,48,1536]{2,1,0:T(8,128)(2,1)S(1)} %get-tuple-element.448), channel_id=1, source_target_pairs={{0,2},{1,3},{2,0},{3,1},{4,6},{5,7},{6,4},{7,5},{8,10},{9,11},{10,... | collective-permute-start | bytes 1769480 | tf_op jit(solution)/shard_map/ppermute | solution.py:569
  228.8 17.2 %collective-permute-start.81 = (bf16[96,768]{1,0:T(8,128)(2,1)S(1)}, bf16[96,768]{1,0:T(8,128)(2,1)S(1)}, u32[]{:S(2)}, u32[]{:S(2)}) collective-permute-start(bf16[96,768]{1,0:T(8,128)(2,1)S(1)} %pad_maximum_fusion.11.refs_0_), channel_id=1, source_target_pairs={{0,3},{1,2},{2,1},{3,0},{4,7},{5,6},{6,5},{7,4},{8,11},{9,10},{10,... | collective-permute-start | bytes 442376 | tf_op jit(solution)/shard_map/ppermute | solution.py:569
  230.1 15.9 %collective-permute-start.80 = (bf16[96,768]{1,0:T(8,128)(2,1)S(1)}, bf16[96,768]{1,0:T(8,128)(2,1)S(1)}, u32[]{:S(2)}, u32[]{:S(2)}) collective-permute-start(bf16[96,768]{1,0:T(8,128)(2,1)S(1)} %pad_maximum_fusion.11.refs_0_), channel_id=1, source_target_pairs={{0,2},{1,3},{2,0},{3,1},{4,6},{5,7},{6,4},{7,5},{8,10},{9,11},{10,... | collective-permute-start | bytes 442376 | tf_op jit(solution)/shard_map/ppermute | solution.py:569
  230.6 15.4 %collective-permute-start.79 = (bf16[96,768]{1,0:T(8,128)(2,1)S(1)}, bf16[96,768]{1,0:T(8,128)(2,1)S(1)}, u32[]{:S(2)}, u32[]{:S(2)}) collective-permute-start(bf16[96,768]{1,0:T(8,128)(2,1)S(1)} %pad_maximum_fusion.11.refs_0_), channel_id=1, source_target_pairs={{0,1},{1,0},{2,3},{3,2},{4,5},{5,4},{6,7},{7,6},{8,9},{9,8},{10,11... | collective-permute-start | bytes 442376 | tf_op jit(solution)/shard_map/ppermute | solution.py:569
  235.0 11.1 %collective-permute-start.78 = (bf16[48,1536]{1,0:T(8,128)(2,1)S(1)}, bf16[48,1536]{1,0:T(8,128)(2,1)S(1)}, u32[]{:S(2)}, u32[]{:S(2)}) collective-permute-start(bf16[48,1536]{1,0:T(8,128)(2,1)S(1)} %get-tuple-element.471), channel_id=1, source_target_pairs={{0,12},{1,13},{2,14},{3,15},{4,0},{5,1},{6,2},{7,3},{8,4},{9,5},{1... | collective-permute-start | bytes 442376 | tf_op jit(solution)/shard_map/ppermute | solution.py:565
  (59 other events, 291.5 us)

commit v8 on v7

--- a/solution.py
+++ b/solution.py
@@ -1778,7 +1778,7 @@
     head_lines = line_parts(jnp.concatenate(head_planes))
     size = LINE // 2 * QUARTER_HALF
     cls_far = sent_both(
-        after(cls_y[:, size:], head_lines[3]), after(cls_x[:, :size], head_lines[3])
+        after(cls_y[:, size:], *head_planes[1:]), after(cls_x[:, :size], *head_planes[1:])
     )
 
     second_grad, second_low, second_sums = run_kernel(
@@ -1941,9 +1941,10 @@
         + (pack,),
         [pltpu.VMEM((GROUP, MODEL), WIDE)],
     )
-    got_three, got_two = along_line(mlp_sent[2], 3), along_line(mlp_sent[1], 2)
+    got_three = along_line(mlp_sent[2], 3)
     mlp_last = mlp_sent[0]
-    mlp_got = [None, got_two, got_three]
+    mlp_middle = mlp_sent[1]
+    mlp_got = [None, None, got_three]
 
     head_own, head_send, head_data = run_kernel(
         head_back_kernel,
@@ -2036,6 +2037,9 @@
         attn_data + (top_row, out_rows, live_row),
         flops=3 * SEG * MODEL * 2 * MODEL,
     )
+    payload_parts = line_parts(after(payload, proj))
+    got_two = along_line(after(mlp_middle, *payload_parts[1:]), 2)
+    mlp_got[:2] = [along_line(after(mlp_last, got_two), 1), got_two]
     output = attn_near[3]
     *attn_sent, input_grad = run_kernel(
         attn_add_kernel,
@@ -2045,11 +2049,9 @@
         (),
         attn_far
         + tuple(attn_near[:2])
-        + (after(grad_summed, got_two), input_own, other_core(input_send)),
+        + (grad_summed, input_own, other_core(input_send)),
     )
     attn_plane = sent_both(*attn_sent)
-    payload_parts = line_parts(after(payload, *attn_sent))
-    mlp_got[0] = along_line(after(mlp_last, *payload_parts[1:]), 1)
     mlp_got = [after(got, attn_plane[0]) for got in mlp_got]
     mlp_sum = reduce_line(mlp_own, mlp_got)
     shared = shared + other_core(after(shared, attn_sent[0]))
@@ -2064,7 +2066,7 @@
         [pltpu.VMEM((LINE,) + pack.shape, LOW)],
     )[0]
     cls_got = other_core(cls_rows)
-    attn_plane = tuple(after(got, cls_got, output, input_grad, shared) for got in attn_plane)
+    attn_plane = tuple(after(got, output, input_grad, shared) for got in attn_plane)
     attn_own, *attn_sent = reduce_fold(where, attn_near[2], attn_plane)
     attn_lines = list(
         together(*(along_line(attn_sent[apart - 1], apart) for apart in range(1, LINE)))

time: 259 us -> 250 us (0.965)
  waiting for transfers between devices: 99 us -> 89.1 us
    ppermute x28, waiting for transfers between devices: 25.8 us -> 6.06 us  [in_plane(): return lax.ppermute(value, 'fsdp', plane_pairs(mask))]
    ppermute x36, waiting for transfers between devices: 65.5 us -> 72.9 us  [along_line(): return lax.ppermute(value, 'fsdp', line_pairs(apart))]
    ppermute x21, starting transfers between devices: 21.7 us -> 26.5 us  [other_core(): return lax.ppermute(value, 'rep', [(0, 1), (1, 0)])]
  transfers between devices with their start and end apart: 85 -> 85, of which waited for: 44 -> 40; matrix products, arithmetic and copies ran while one was open for 0% -> 0% of each run, Pallas kernels for 13% -> 13%
where the time goes in v8:
time: 250 us; the launch traced here: 248 us
  starting transfers between devices  103 us (41%)
  waiting for transfers between devices  89.1 us (36%)
  Pallas kernels  48.2 us (19%)
  local copies, waits for them, and re-layouts  5.36 us (2%)
    ppermute x36, waiting for transfers between devices, along_line(): return lax.ppermute(value, 'fsdp', line_pairs(apart))  72.9 us
    ppermute x36, starting transfers between devices, along_line(): return lax.ppermute(value, 'fsdp', line_pairs(apart))  54.5 us
    pallas_call x26, Pallas kernels, run_kernel(): pl.pallas_call(body, name=name, out_shape=tuple(outs), in_specs=in_specs,...  48.2 us
    ppermute x21, starting transfers between devices, other_core(): return lax.ppermute(value, 'rep', [(0, 1), (1, 0)])  26.5 us
    ppermute x28, starting transfers between devices, in_plane(): return lax.ppermute(value, 'fsdp', plane_pairs(mask))  22 us
    ppermute x21, waiting for transfers between devices, other_core(): return lax.ppermute(value, 'rep', [(0, 1), (1, 0)])  10.1 us
    ppermute x28, waiting for transfers between devices, in_plane(): return lax.ppermute(value, 'fsdp', plane_pairs(mask))  6.06 us
  transfers between devices with their start and end apart: 85, of which 40 were waited for; matrix products, arithmetic and copies ran while one was open for 0% of the time, Pallas kernels for 13%

profile of v8, /device:TPU:13, one launch (start us, length us, event | category | flops | bytes accessed | tf_op | source)
XLA Modules:
  0.0 248.2 jit_solution(1339775738671752493)
XLA Ops:
  14.2 7.2 %collective-permute-done.1.refs_2_ = bf16[48,1664]{1,0:T(8,128)(2,1)S(1)} collective-permute-done((bf16[48,1664]{1,0:T(8,128)(2,1)S(1)}, bf16[48,1664]{1,0:T(8,128)(2,1)S(1)}, u32[]{:S(2)}, u32[]{:S(2)}) %collective-permute-start.1) | collective-permute-done | bytes 159776 | tf_op jit(solution)/shard_map/ppermute | solution.py:565
  21.4 3.9 %collective-permute-done.refs_1_ = bf16[48,1664]{1,0:T(8,128)(2,1)S(1)} collective-permute-done((bf16[48,1664]{1,0:T(8,128)(2,1)S(1)}, bf16[48,1664]{1,0:T(8,128)(2,1)S(1)}, u32[]{:S(2)}, u32[]{:S(2)}) %collective-permute-start) | collective-permute-done | bytes 159776 | tf_op jit(solution)/shard_map/ppermute | solution.py:565
  30.9 2.5 collective-permute-start.10
  33.4 2.8 %collective-permute-done.11.refs_3_ = bf16[48,1536]{1,0:T(8,128)(2,1)S(1)} collective-permute-done((bf16[48,1536]{1,0:T(8,128)(2,1)S(1)}, bf16[48,1536]{1,0:T(8,128)(2,1)S(1)}, u32[]{:S(2)}, u32[]{:S(2)}) %collective-permute-start.11) | collective-permute-done | bytes 147488 | tf_op jit(solution)/shard_map/ppermute | solution.py:565
  36.2 5.2 %collective-permute-done.10.refs_2_ = bf16[48,1536]{1,0:T(8,128)(2,1)S(1)} collective-permute-done((bf16[48,1536]{1,0:T(8,128)(2,1)S(1)}, bf16[48,1536]{1,0:T(8,128)(2,1)S(1)}, u32[]{:S(2)}, u32[]{:S(2)}) %collective-permute-start.10) | collective-permute-done | bytes 147488 | tf_op jit(solution)/shard_map/ppermute | solution.py:565
  41.4 3.2 %collective-permute-done.9.refs_1_ = bf16[48,1536]{1,0:T(8,128)(2,1)S(1)} collective-permute-done((bf16[48,1536]{1,0:T(8,128)(2,1)S(1)}, bf16[48,1536]{1,0:T(8,128)(2,1)S(1)}, u32[]{:S(2)}, u32[]{:S(2)}) %collective-permute-start.9) | collective-permute-done | bytes 147488 | tf_op jit(solution)/shard_map/ppermute | solution.py:565
  46.2 2.3 collective-permute-start.17
  51.6 6.6 %collective-permute-done.16.refs_2_ = bf16[48,1536]{1,0:T(8,128)(2,1)S(1)} collective-permute-done((bf16[48,1536]{1,0:T(8,128)(2,1)S(1)}, bf16[48,1536]{1,0:T(8,128)(2,1)S(1)}, u32[]{:S(2)}, u32[]{:S(2)}) %collective-permute-start.16) | collective-permute-done | bytes 147488 | tf_op jit(solution)/shard_map/ppermute | solution.py:565
  58.1 3.2 %collective-permute-done.15.refs_1_ = bf16[48,1536]{1,0:T(8,128)(2,1)S(1)} collective-permute-done((bf16[48,1536]{1,0:T(8,128)(2,1)S(1)}, bf16[48,1536]{1,0:T(8,128)(2,1)S(1)}, u32[]{:S(2)}, u32[]{:S(2)}) %collective-permute-start.15) | collective-permute-done | bytes 147488 | tf_op jit(solution)/shard_map/ppermute | solution.py:565
  67.7 3.9 %seg_qkv.1 = (bf16[16,48,1152]{2,1,0:T(8,128)(2,1)S(1)}, bf16[8,48,384]{2,1,0:T(8,128)(2,1)S(1)}, bf16[8,48,384]{2,1,0:T(8,128)(2,1)S(1)}, bf16[256,1152]{1,0:T(...) custom-call(s32[5]{0:T(128)S(1)} %stack.24.where, ...), custom_call_target="tpu_custom_call" | custom-call | flops 452984832 | bytes 11453440 | tf_op jit(solution)/shard_map/seg_qkv/pallas_call | solution.py:595
  71.6 3.2 %collective-permute-start.20 = (bf16[8,48,384]{2,1,0:T(8,128)(2,1)S(1)}, bf16[8,48,384]{2,1,0:T(8,128)(2,1)S(1)}, u32[]{:S(2)}, u32[]{:S(2)}) collective-permute-start(bf16[8,48,384]{2,1,0:T(8,128)(2,1)S(1)} %get-tuple-element.293.low), channel_id=1, source_target_pairs={{0,16},{16,0},{1,17},{17,1},{2,18},{18,2},{3,19},{19,3},{4,20},{20... | collective-permute-start | bytes 884744 | tf_op jit(solution)/shard_map/ppermute | solution.py:573
  82.6 3.3 %collective-permute-start.24 = (bf16[128,768]{1,0:T(8,128)(2,1)S(1)}, bf16[128,768]{1,0:T(8,128)(2,1)S(1)}, u32[]{:S(2)}, u32[]{:S(2)}) collective-permute-start(bf16[128,768]{1,0:T(8,128)(2,1)S(1)} %get-tuple-element.302.refs_12_.refs_0_.refs_6_), channel_id=1, source_target_pairs={{0,16},{16,0},{1,17},{17,1},{2,18},{18,2},{3,19},{19,3},{4,20},{20... | collective-permute-start | bytes 589832 | tf_op jit(solution)/shard_map/ppermute | solution.py:573
  91.9 3.1 %collective-permute-start.25 = (f32[128,768]{1,0:T(8,128)S(1)}, f32[128,768]{1,0:T(8,128)S(1)}, u32[]{:S(2)}, u32[]{:S(2)}) collective-permute-start(f32[128,768]{1,0:T(8,128)S(1)} %get-tuple-element.306), channel_id=1, source_target_pairs={{0,16},{16,0},{1,17},{17,1},{2,18},{18,2},{3,19},{19,3},{4,20},{20... | collective-permute-start | bytes 1179656 | tf_op jit(solution)/shard_map/ppermute | solution.py:573
  114.2 2.3 collective-permute-start.42
  116.5 3.1 %seg_mlp_weight.1 = (bf16[2,48,3072]{2,1,0:T(8,128)(2,1)S(1)}, bf16[2,48,3072]{2,1,0:T(8,128)(2,1)S(1)}, bf16[4,48,3072]{2,1,0:T(8,128)(2,1)S(1)}, bf16[4,48,307...) custom-call(s32[5]{0:T(128)S(1)} %stack.24.where, bf16[128,768]{1,0:T(8,128)(2,1)S(1)} %get-tuple-element.302.refs_12_.refs_0_.refs_6_, ...), custom_call_target="tpu_custom_call" | custom-call | flops 1207959552 | bytes 7077888 | tf_op jit(solution)/shard_map/seg_mlp_weight/pallas_call | solution.py:595
  125.8 2.9 %collective-permute-start.46 = (f32[16,768]{1,0:T(8,128)S(1)}, f32[16,768]{1,0:T(8,128)S(1)}, u32[]{:S(2)}, u32[]{:S(2)}) collective-permute-start(f32[16,768]{1,0:T(8,128)S(1)} %get-tuple-element.368.refs_1_), channel_id=1, source_target_pairs={{0,12},{1,13},{2,14},{3,15},{4,0},{5,1},{6,2},{7,3},{8,4},{9,5},{1... | collective-permute-start | bytes 147464 | tf_op jit(solution)/shard_map/ppermute | solution.py:565
  129.3 2.3 collective-permute-start.44
  131.6 3.0 %collective-permute-done.47.refs_7_ = bf16[2,48,3072]{2,1,0:T(8,128)(2,1)S(1)} collective-permute-done((bf16[2,48,3072]{2,1,0:T(8,128)(2,1)S(1)}, bf16[2,48,3072]{2,1,0:T(8,128)(2,1)S(1)}, u32[]{:S(2)}, u32[]{:S(2)}) %collective-permute-start.47) | collective-permute-done | bytes 589856 | tf_op jit(solution)/shard_map/ppermute | solution.py:569
  137.9 3.3 %collective-permute-start.51 = (f32[16,768]{1,0:T(8,128)S(1)}, f32[16,768]{1,0:T(8,128)S(1)}, u32[]{:S(2)}, u32[]{:S(2)}) collective-permute-start(f32[16,768]{1,0:T(8,128)S(1)} %get-tuple-element.379.refs_1_), channel_id=1, source_target_pairs={{0,12},{1,13},{2,14},{3,15},{4,0},{5,1},{6,2},{7,3},{8,4},{9,5},{1... | collective-permute-start | bytes 147464 | tf_op jit(solution)/shard_map/ppermute | solution.py:565
  141.3 2.4 collective-permute-start.49
  159.7 2.5 %collective-permute-done.56.refs_4_ = f32[16,768]{1,0:T(8,128)S(1)} collective-permute-done((f32[16,768]{1,0:T(8,128)S(1)}, f32[16,768]{1,0:T(8,128)S(1)}, u32[]{:S(2)}, u32[]{:S(2)}) %collective-permute-start.56) | collective-permute-done | bytes 49184 | tf_op jit(solution)/shard_map/ppermute | solution.py:565
  164.9 3.2 %collective-permute-start.63 = (bf16[64,3072]{1,0:T(8,128)(2,1)S(1)}, bf16[64,3072]{1,0:T(8,128)(2,1)S(1)}, u32[]{:S(2)}, u32[]{:S(2)}) collective-permute-start(bf16[64,3072]{1,0:T(8,128)(2,1)S(1)} %get-tuple-element.430), channel_id=1, source_target_pairs={{0,12},{1,13},{2,14},{3,15},{4,0},{5,1},{6,2},{7,3},{8,4},{9,5},{1... | collective-permute-start | bytes 1179656 | tf_op jit(solution)/shard_map/ppermute | solution.py:565
  168.1 2.7 %collective-permute-start.60 = (f32[1,768]{1,0:T(1,128)S(1)}, f32[1,768]{1,0:T(1,128)S(1)}, u32[]{:S(2)}, u32[]{:S(2)}) collective-permute-start(f32[1,768]{1,0:T(1,128)S(1)} %get-tuple-element.411.refs_0_.refs_3_), channel_id=1, source_target_pairs={{0,16},{16,0},{1,17},{17,1},{2,18},{18,2},{3,19},{19,3},{4,20},{20... | collective-permute-start | bytes 9224 | tf_op jit(solution)/shard_map/ppermute | solution.py:573
  177.1 4.4 %seg_attn_back.1 = (bf16[256,1152]{1,0:T(8,128)(2,1)S(1)}, f32[128,768]{1,0:T(8,128)S(1)}, f32[128,768]{1,0:T(8,128)S(1)}, bf16[24,768]{1,0:T(8,128)(2,1)S(1)}) custom-call(s32[5]{0:T(128)S(1)} %stack.24.where, bf16[256,1152]{1,0:T(8,128)(2,1)S(1)} %get-tuple-element.297.refs_0_, bf16[128,768]{1,0:T(8,128)(2,1)S(1)} %get-tuple-element.416.refs_1_, ...), custom_call_target="tpu_custom_call" | custom-call | flops 905969664 | bytes 4624384 | tf_op jit(solution)/shard_map/seg_attn_back/pallas_call | solution.py:595
  198.1 12.6 %collective-permute-done.79.refs_2_ = bf16[64,3072]{1,0:T(8,128)(2,1)S(1)} collective-permute-done((bf16[64,3072]{1,0:T(8,128)(2,1)S(1)}, bf16[64,3072]{1,0:T(8,128)(2,1)S(1)}, u32[]{:S(2)}, u32[]{:S(2)}) %collective-permute-start.79) | collective-permute-done | bytes 393248 | tf_op jit(solution)/shard_map/ppermute | solution.py:565
  213.9 2.9 %collective-permute-start.70 = (bf16[48,1536]{1,0:T(8,128)(2,1)S(1)}, bf16[48,1536]{1,0:T(8,128)(2,1)S(1)}, u32[]{:S(2)}, u32[]{:S(2)}) collective-permute-start(bf16[48,1536]{1,0:T(8,128)(2,1)S(1)} %get-tuple-element.454), channel_id=1, source_target_pairs={{0,4},{1,5},{2,6},{3,7},{4,8},{5,9},{6,10},{7,11},{8,12},{9,13},{1... | collective-permute-start | bytes 442376 | tf_op jit(solution)/shard_map/ppermute | solution.py:565
  219.5 2.9 %collective-permute-done.80.refs_1_ = bf16[64,3072]{1,0:T(8,128)(2,1)S(1)} collective-permute-done((bf16[64,3072]{1,0:T(8,128)(2,1)S(1)}, bf16[64,3072]{1,0:T(8,128)(2,1)S(1)}, u32[]{:S(2)}, u32[]{:S(2)}) %collective-permute-start.80) | collective-permute-done | bytes 393248 | tf_op jit(solution)/shard_map/ppermute | solution.py:565
  223.2 2.3 collective-permute-done.70
  225.5 3.0 %collective-permute-start.72 = (bf16[48,1536]{1,0:T(8,128)(2,1)S(1)}, bf16[48,1536]{1,0:T(8,128)(2,1)S(1)}, u32[]{:S(2)}, u32[]{:S(2)}) collective-permute-start(bf16[48,1536]{1,0:T(8,128)(2,1)S(1)} %get-tuple-element.456), channel_id=1, source_target_pairs={{0,12},{1,13},{2,14},{3,15},{4,0},{5,1},{6,2},{7,3},{8,4},{9,5},{1... | collective-permute-start | bytes 442376 | tf_op jit(solution)/shard_map/ppermute | solution.py:565
  232.9 4.8 %collective-permute-done.72 = bf16[48,1536]{1,0:T(8,128)(2,1)S(1)} collective-permute-done((bf16[48,1536]{1,0:T(8,128)(2,1)S(1)}, bf16[48,1536]{1,0:T(8,128)(2,1)S(1)}, u32[]{:S(2)}, u32[]{:S(2)}) %collective-permute-start.72) | collective-permute-done | bytes 147488 | tf_op jit(solution)/shard_map/ppermute | solution.py:565
  237.7 4.4 %head_owner.1 = (f32[48,3072]{1,0:T(8,128)S(1)}, f32[16,768]{1,0:T(8,128)S(1)}, f32[48,9216]{1,0:T(8,128)}, f32[576]{0:T(1024)}, f32[16,768]{1,0:T(8,128)}, /*index=5*/f32[1,1]{1,0:T(1,128)}) custom-call(s32[5]{0:T(128)S(1)} %stack.24.where, bf16[96,768]{1,0:T(8,128)(2,1)S(1)} %pad_maximum_fusion.11.refs_0_, ...), custom_call_target="tpu_custom_call" | custom-call | flops 28311552 | bytes 4503812 | tf_op jit(solution)/shard_map/head_owner/pallas_call | solution.py:595
  244.7 3.3 %seg_owner.1 = (f32[48,9216]{1,0:T(8,128)}, f32[576]{0:T(1024)}) custom-call(s32[5]{0:T(128)S(1)} %stack.24.where, f32[48,1536]{1,0:T(8,128)S(1)} %convert_add_fusion.1.attn, f32[48,1536]{1,0:T(8,128)S(1)} %collective-permute-done.82.attn_got, f32[48,3072]{1,0:T(8,128)S(1)} %get-tuple-element.482.mlp, f32[48,3072]{1,0:T(8,128)S(1)} %collective-permute-done.83.mlp_got, ...), custom_call_target="tpu_custom_call" | custom-call | bytes 3639552 | tf_op jit(solution)/shard_map/seg_owner/pallas_call | solution.py:595
  (211 shorter events, 127.5 us)
Async XLA Ops:
  8.0 17.3 %collective-permute-start.3 = (bf16[48,4736]{1,0:T(8,128)(2,1)S(1)}, bf16[48,4736]{1,0:T(8,128)(2,1)S(1)}, u32[]{:S(2)}, u32[]{:S(2)}) collective-permute-start(bf16[48,4736]{1,0:T(8,128)(2,1)S(1)} %pad_maximum_fusion.10), channel_id=1, source_target_pairs={{0,1},{1,0},{2,3},{3,2},{4,5},{5,4},{6,7},{7,6},{8,9},{9,8},{10,11... | collective-permute-start | bytes 1363976 | tf_op jit(solution)/shard_map/ppermute | solution.py:569
  9.3 16.0 %collective-permute-start.4 = (bf16[48,4736]{1,0:T(8,128)(2,1)S(1)}, bf16[48,4736]{1,0:T(8,128)(2,1)S(1)}, u32[]{:S(2)}, u32[]{:S(2)}) collective-permute-start(bf16[48,4736]{1,0:T(8,128)(2,1)S(1)} %pad_maximum_fusion.10), channel_id=1, source_target_pairs={{0,2},{1,3},{2,0},{3,1},{4,6},{5,7},{6,4},{7,5},{8,10},{9,11},{10,... | collective-permute-start | bytes 1363976 | tf_op jit(solution)/shard_map/ppermute | solution.py:569
  9.7 11.7 %collective-permute-start.1 = (bf16[48,1664]{1,0:T(8,128)(2,1)S(1)}, bf16[48,1664]{1,0:T(8,128)(2,1)S(1)}, u32[]{:S(2)}, u32[]{:S(2)}) collective-permute-start(bf16[48,1664]{1,0:T(8,128)(2,1)S(1)} %get-tuple-element.253.refs_0_), channel_id=1, source_target_pairs={{0,8},{1,9},{2,10},{3,11},{4,12},{5,13},{6,14},{7,15},{8,0},{9,1},... | collective-permute-start | bytes 479240 | tf_op jit(solution)/shard_map/ppermute | solution.py:565
  12.0 13.3 %collective-permute-start = (bf16[48,1664]{1,0:T(8,128)(2,1)S(1)}, bf16[48,1664]{1,0:T(8,128)(2,1)S(1)}, u32[]{:S(2)}, u32[]{:S(2)}) collective-permute-start(bf16[48,1664]{1,0:T(8,128)(2,1)S(1)} %get-tuple-element.253.refs_0_), channel_id=1, source_target_pairs={{0,4},{1,5},{2,6},{3,7},{4,8},{5,9},{6,10},{7,11},{8,12},{9,13},{1... | collective-permute-start | bytes 479240 | tf_op jit(solution)/shard_map/ppermute | solution.py:565
  25.5 19.1 %collective-permute-start.6 = (bf16[48,7424]{1,0:T(8,128)(2,1)S(1)}, bf16[48,7424]{1,0:T(8,128)(2,1)S(1)}, u32[]{:S(2)}, u32[]{:S(2)}) collective-permute-start(bf16[48,7424]{1,0:T(8,128)(2,1)S(1)} %pad_maximum_fusion.6), channel_id=1, source_target_pairs={{0,2},{1,3},{2,0},{3,1},{4,6},{5,7},{6,4},{7,5},{8,10},{9,11},{10,... | collective-permute-start | bytes 2138120 | tf_op jit(solution)/shard_map/ppermute | solution.py:569
  26.8 17.8 %collective-permute-start.5 = (bf16[48,7296]{1,0:T(8,128)(2,1)S(1)}, bf16[48,7296]{1,0:T(8,128)(2,1)S(1)}, u32[]{:S(2)}, u32[]{:S(2)}) collective-permute-start(bf16[48,7296]{1,0:T(8,128)(2,1)S(1)} %pad_maximum_fusion.7), channel_id=1, source_target_pairs={{0,1},{1,0},{2,3},{3,2},{4,5},{5,4},{6,7},{7,6},{8,9},{9,8},{10,11... | collective-permute-start | bytes 2101256 | tf_op jit(solution)/shard_map/ppermute | solution.py:569
  44.7 16.6 %collective-permute-start.13 = (bf16[48,7168]{1,0:T(8,128)(2,1)S(1)}, bf16[48,7168]{1,0:T(8,128)(2,1)S(1)}, u32[]{:S(2)}, u32[]{:S(2)}) collective-permute-start(bf16[48,7168]{1,0:T(8,128)(2,1)S(1)} %pad_maximum_fusion.8), channel_id=1, source_target_pairs={{0,2},{1,3},{2,0},{3,1},{4,6},{5,7},{6,4},{7,5},{8,10},{9,11},{10,... | collective-permute-start | bytes 2064392 | tf_op jit(solution)/shard_map/ppermute | solution.py:569
  45.0 16.3 %collective-permute-start.12 = (bf16[48,7040]{1,0:T(8,128)(2,1)S(1)}, bf16[48,7040]{1,0:T(8,128)(2,1)S(1)}, u32[]{:S(2)}, u32[]{:S(2)}) collective-permute-start(bf16[48,7040]{1,0:T(8,128)(2,1)S(1)} %pad_maximum_fusion.9), channel_id=1, source_target_pairs={{0,1},{1,0},{2,3},{3,2},{4,5},{5,4},{6,7},{7,6},{8,9},{9,8},{10,11... | collective-permute-start | bytes 2027528 | tf_op jit(solution)/shard_map/ppermute | solution.py:569
  49.6 11.7 %collective-permute-start.15 = (bf16[48,1536]{1,0:T(8,128)(2,1)S(1)}, bf16[48,1536]{1,0:T(8,128)(2,1)S(1)}, u32[]{:S(2)}, u32[]{:S(2)}) collective-permute-start(bf16[48,1536]{1,0:T(8,128)(2,1)S(1)} %get-tuple-element.284.refs_0_), channel_id=1, source_target_pairs={{0,4},{1,5},{2,6},{3,7},{4,8},{5,9},{6,10},{7,11},{8,12},{9,13},{1... | collective-permute-start | bytes 442376 | tf_op jit(solution)/shard_map/ppermute | solution.py:565
  61.5 15.2 %collective-permute-start.18 = (bf16[48,6912]{1,0:T(8,128)(2,1)S(1)}, bf16[48,6912]{1,0:T(8,128)(2,1)S(1)}, u32[]{:S(2)}, u32[]{:S(2)}) collective-permute-start(bf16[48,6912]{1,0:T(8,128)(2,1)S(1)} %get-tuple-element.288), channel_id=1, source_target_pairs={{0,1},{1,0},{2,3},{3,2},{4,5},{5,4},{6,7},{7,6},{8,9},{9,8},{10,11... | collective-permute-start | bytes 1990664 | tf_op jit(solution)/shard_map/ppermute | solution.py:569
  62.7 12.1 %collective-permute-start.32 = (bf16[48,1152]{1,0:T(8,128)(2,1)S(1)}, bf16[48,1152]{1,0:T(8,128)(2,1)S(1)}, u32[]{:S(2)}, u32[]{:S(2)}) collective-permute-start(bf16[48,1152]{1,0:T(8,128)(2,1)S(1)} %get-tuple-element.327), channel_id=1, source_target_pairs={{0,4},{1,5},{2,6},{3,7},{4,8},{5,9},{6,10},{7,11},{8,12},{9,13},{1... | collective-permute-start | bytes 331784 | tf_op jit(solution)/shard_map/ppermute | solution.py:565
  64.9 14.5 %collective-permute-start.19 = (bf16[48,6912]{1,0:T(8,128)(2,1)S(1)}, bf16[48,6912]{1,0:T(8,128)(2,1)S(1)}, u32[]{:S(2)}, u32[]{:S(2)}) collective-permute-start(bf16[48,6912]{1,0:T(8,128)(2,1)S(1)} %get-tuple-element.289), channel_id=1, source_target_pairs={{0,2},{1,3},{2,0},{3,1},{4,6},{5,7},{6,4},{7,5},{8,10},{9,11},{10,... | collective-permute-start | bytes 1990664 | tf_op jit(solution)/shard_map/ppermute | solution.py:569
  88.9 13.7 %collective-permute-start.35 = (bf16[48,4992]{1,0:T(8,128)(2,1)S(1)}, bf16[48,4992]{1,0:T(8,128)(2,1)S(1)}, u32[]{:S(2)}, u32[]{:S(2)}) collective-permute-start(bf16[48,4992]{1,0:T(8,128)(2,1)S(1)} %constant_dynamic-update-slice_fusion), channel_id=1, source_target_pairs={{0,1},{1,0},{2,3},{3,2},{4,5},{5,4},{6,7},{7,6},{8,9},{9,8},{10,11... | collective-permute-start | bytes 1437704 | tf_op jit(solution)/shard_map/ppermute | solution.py:569
  89.8 12.8 %collective-permute-start.36 = (bf16[48,4992]{1,0:T(8,128)(2,1)S(1)}, bf16[48,4992]{1,0:T(8,128)(2,1)S(1)}, u32[]{:S(2)}, u32[]{:S(2)}) collective-permute-start(bf16[48,4992]{1,0:T(8,128)(2,1)S(1)} %constant_dynamic-update-slice_fusion), channel_id=1, source_target_pairs={{0,2},{1,3},{2,0},{3,1},{4,6},{5,7},{6,4},{7,5},{8,10},{9,11},{10,... | collective-permute-start | bytes 1437704 | tf_op jit(solution)/shard_map/ppermute | solution.py:569
  119.6 15.0 %collective-permute-start.47 = (bf16[2,48,3072]{2,1,0:T(8,128)(2,1)S(1)}, bf16[2,48,3072]{2,1,0:T(8,128)(2,1)S(1)}, u32[]{:S(2)}, u32[]{:S(2)}) collective-permute-start(bf16[2,48,3072]{2,1,0:T(8,128)(2,1)S(1)} %get-tuple-element.372), channel_id=1, source_target_pairs={{0,2},{1,3},{2,0},{3,1},{4,6},{5,7},{6,4},{7,5},{8,10},{9,11},{10,... | collective-permute-start | bytes 1769480 | tf_op jit(solution)/shard_map/ppermute | solution.py:569
  120.6 14.6 %collective-permute-start.48 = (bf16[2,48,3072]{2,1,0:T(8,128)(2,1)S(1)}, bf16[2,48,3072]{2,1,0:T(8,128)(2,1)S(1)}, u32[]{:S(2)}, u32[]{:S(2)}) collective-permute-start(bf16[2,48,3072]{2,1,0:T(8,128)(2,1)S(1)} %get-tuple-element.374), channel_id=1, source_target_pairs={{0,1},{1,0},{2,3},{3,2},{4,5},{5,4},{6,7},{7,6},{8,9},{9,8},{10,11... | collective-permute-start | bytes 1769480 | tf_op jit(solution)/shard_map/ppermute | solution.py:569
  136.7 26.4 %collective-permute-start.58 = (bf16[4,48,3072]{2,1,0:T(8,128)(2,1)S(1)}, bf16[4,48,3072]{2,1,0:T(8,128)(2,1)S(1)}, u32[]{:S(2)}, u32[]{:S(2)}) collective-permute-start(bf16[4,48,3072]{2,1,0:T(8,128)(2,1)S(1)} %get-tuple-element.403), channel_id=1, source_target_pairs={{0,1},{1,0},{2,3},{3,2},{4,5},{5,4},{6,7},{7,6},{8,9},{9,8},{10,11... | collective-permute-start | bytes 3538952 | tf_op jit(solution)/shard_map/ppermute | solution.py:569
  137.4 26.1 %collective-permute-start.59 = (bf16[4,48,3072]{2,1,0:T(8,128)(2,1)S(1)}, bf16[4,48,3072]{2,1,0:T(8,128)(2,1)S(1)}, u32[]{:S(2)}, u32[]{:S(2)}) collective-permute-start(bf16[4,48,3072]{2,1,0:T(8,128)(2,1)S(1)} %get-tuple-element.404), channel_id=1, source_target_pairs={{0,2},{1,3},{2,0},{3,1},{4,6},{5,7},{6,4},{7,5},{8,10},{9,11},{10,... | collective-permute-start | bytes 3538952 | tf_op jit(solution)/shard_map/ppermute | solution.py:569
  164.9 18.1 %collective-permute-start.63 = (bf16[64,3072]{1,0:T(8,128)(2,1)S(1)}, bf16[64,3072]{1,0:T(8,128)(2,1)S(1)}, u32[]{:S(2)}, u32[]{:S(2)}) collective-permute-start(bf16[64,3072]{1,0:T(8,128)(2,1)S(1)} %get-tuple-element.430), channel_id=1, source_target_pairs={{0,12},{1,13},{2,14},{3,15},{4,0},{5,1},{6,2},{7,3},{8,4},{9,5},{1... | collective-permute-start | bytes 1179656 | tf_op jit(solution)/shard_map/ppermute | solution.py:565
  181.5 14.4 %collective-permute-start.66 = (f32[128,768]{1,0:T(8,128)S(1)}, f32[128,768]{1,0:T(8,128)S(1)}, u32[]{:S(2)}, u32[]{:S(2)}) collective-permute-start(f32[128,768]{1,0:T(8,128)S(1)} %get-tuple-element.440), channel_id=1, source_target_pairs={{0,16},{16,0},{1,17},{17,1},{2,18},{18,2},{3,19},{19,3},{4,20},{20... | collective-permute-start | bytes 1179656 | tf_op jit(solution)/shard_map/ppermute | solution.py:573
  183.0 12.9 %collective-permute-start.65 = (bf16[2,48,1536]{2,1,0:T(8,128)(2,1)S(1)}, bf16[2,48,1536]{2,1,0:T(8,128)(2,1)S(1)}, u32[]{:S(2)}, u32[]{:S(2)}) collective-permute-start(bf16[2,48,1536]{2,1,0:T(8,128)(2,1)S(1)} %get-tuple-element.433), channel_id=1, source_target_pairs={{0,1},{1,0},{2,3},{3,2},{4,5},{5,4},{6,7},{7,6},{8,9},{9,8},{10,11... | collective-permute-start | bytes 884744 | tf_op jit(solution)/shard_map/ppermute | solution.py:569
  184.3 11.6 %collective-permute-start.64 = (bf16[2,48,1536]{2,1,0:T(8,128)(2,1)S(1)}, bf16[2,48,1536]{2,1,0:T(8,128)(2,1)S(1)}, u32[]{:S(2)}, u32[]{:S(2)}) collective-permute-start(bf16[2,48,1536]{2,1,0:T(8,128)(2,1)S(1)} %get-tuple-element.431), channel_id=1, source_target_pairs={{0,2},{1,3},{2,0},{3,1},{4,6},{5,7},{6,4},{7,5},{8,10},{9,11},{10,... | collective-permute-start | bytes 884744 | tf_op jit(solution)/shard_map/ppermute | solution.py:569
  191.4 19.2 %collective-permute-start.79 = (bf16[64,3072]{1,0:T(8,128)(2,1)S(1)}, bf16[64,3072]{1,0:T(8,128)(2,1)S(1)}, u32[]{:S(2)}, u32[]{:S(2)}) collective-permute-start(bf16[64,3072]{1,0:T(8,128)(2,1)S(1)} %get-tuple-element.474), channel_id=1, source_target_pairs={{0,8},{1,9},{2,10},{3,11},{4,12},{5,13},{6,14},{7,15},{8,0},{9,1},... | collective-permute-start | bytes 1179656 | tf_op jit(solution)/shard_map/ppermute | solution.py:565
  197.3 15.8 %collective-permute-start.67 = (bf16[4,48,1536]{2,1,0:T(8,128)(2,1)S(1)}, bf16[4,48,1536]{2,1,0:T(8,128)(2,1)S(1)}, u32[]{:S(2)}, u32[]{:S(2)}) collective-permute-start(bf16[4,48,1536]{2,1,0:T(8,128)(2,1)S(1)} %get-tuple-element.445), channel_id=1, source_target_pairs={{0,1},{1,0},{2,3},{3,2},{4,5},{5,4},{6,7},{7,6},{8,9},{9,8},{10,11... | collective-permute-start | bytes 1769480 | tf_op jit(solution)/shard_map/ppermute | solution.py:569
  197.6 15.6 %collective-permute-start.68 = (bf16[4,48,1536]{2,1,0:T(8,128)(2,1)S(1)}, bf16[4,48,1536]{2,1,0:T(8,128)(2,1)S(1)}, u32[]{:S(2)}, u32[]{:S(2)}) collective-permute-start(bf16[4,48,1536]{2,1,0:T(8,128)(2,1)S(1)} %get-tuple-element.446), channel_id=1, source_target_pairs={{0,2},{1,3},{2,0},{3,1},{4,6},{5,7},{6,4},{7,5},{8,10},{9,11},{10,... | collective-permute-start | bytes 1769480 | tf_op jit(solution)/shard_map/ppermute | solution.py:569
  210.7 11.7 %collective-permute-start.80 = (bf16[64,3072]{1,0:T(8,128)(2,1)S(1)}, bf16[64,3072]{1,0:T(8,128)(2,1)S(1)}, u32[]{:S(2)}, u32[]{:S(2)}) collective-permute-start(bf16[64,3072]{1,0:T(8,128)(2,1)S(1)} %get-tuple-element.475), channel_id=1, source_target_pairs={{0,4},{1,5},{2,6},{3,7},{4,8},{5,9},{6,10},{7,11},{8,12},{9,13},{1... | collective-permute-start | bytes 1179656 | tf_op jit(solution)/shard_map/ppermute | solution.py:565
  213.9 11.6 %collective-permute-start.70 = (bf16[48,1536]{1,0:T(8,128)(2,1)S(1)}, bf16[48,1536]{1,0:T(8,128)(2,1)S(1)}, u32[]{:S(2)}, u32[]{:S(2)}) collective-permute-start(bf16[48,1536]{1,0:T(8,128)(2,1)S(1)} %get-tuple-element.454), channel_id=1, source_target_pairs={{0,4},{1,5},{2,6},{3,7},{4,8},{5,9},{6,10},{7,11},{8,12},{9,13},{1... | collective-permute-start | bytes 442376 | tf_op jit(solution)/shard_map/ppermute | solution.py:565
  216.8 13.7 %collective-permute-start.71 = (bf16[48,1536]{1,0:T(8,128)(2,1)S(1)}, bf16[48,1536]{1,0:T(8,128)(2,1)S(1)}, u32[]{:S(2)}, u32[]{:S(2)}) collective-permute-start(bf16[48,1536]{1,0:T(8,128)(2,1)S(1)} %get-tuple-element.455), channel_id=1, source_target_pairs={{0,8},{1,9},{2,10},{3,11},{4,12},{5,13},{6,14},{7,15},{8,0},{9,1},... | collective-permute-start | bytes 442376 | tf_op jit(solution)/shard_map/ppermute | solution.py:565
  218.0 19.7 %collective-permute-start.78 = (bf16[96,768]{1,0:T(8,128)(2,1)S(1)}, bf16[96,768]{1,0:T(8,128)(2,1)S(1)}, u32[]{:S(2)}, u32[]{:S(2)}) collective-permute-start(bf16[96,768]{1,0:T(8,128)(2,1)S(1)} %pad_maximum_fusion.11.refs_0_), channel_id=1, source_target_pairs={{0,3},{1,2},{2,1},{3,0},{4,7},{5,6},{6,5},{7,4},{8,11},{9,10},{10,... | collective-permute-start | bytes 442376 | tf_op jit(solution)/shard_map/ppermute | solution.py:569
  218.8 18.9 %collective-permute-start.77 = (bf16[96,768]{1,0:T(8,128)(2,1)S(1)}, bf16[96,768]{1,0:T(8,128)(2,1)S(1)}, u32[]{:S(2)}, u32[]{:S(2)}) collective-permute-start(bf16[96,768]{1,0:T(8,128)(2,1)S(1)} %pad_maximum_fusion.11.refs_0_), channel_id=1, source_target_pairs={{0,2},{1,3},{2,0},{3,1},{4,6},{5,7},{6,4},{7,5},{8,10},{9,11},{10,... | collective-permute-start | bytes 442376 | tf_op jit(solution)/shard_map/ppermute | solution.py:569
  222.4 15.3 %collective-permute-start.76 = (bf16[96,768]{1,0:T(8,128)(2,1)S(1)}, bf16[96,768]{1,0:T(8,128)(2,1)S(1)}, u32[]{:S(2)}, u32[]{:S(2)}) collective-permute-start(bf16[96,768]{1,0:T(8,128)(2,1)S(1)} %pad_maximum_fusion.11.refs_0_), channel_id=1, source_target_pairs={{0,1},{1,0},{2,3},{3,2},{4,5},{5,4},{6,7},{7,6},{8,9},{9,8},{10,11... | collective-permute-start | bytes 442376 | tf_op jit(solution)/shard_map/ppermute | solution.py:569
  225.5 12.2 %collective-permute-start.72 = (bf16[48,1536]{1,0:T(8,128)(2,1)S(1)}, bf16[48,1536]{1,0:T(8,128)(2,1)S(1)}, u32[]{:S(2)}, u32[]{:S(2)}) collective-permute-start(bf16[48,1536]{1,0:T(8,128)(2,1)S(1)} %get-tuple-element.456), channel_id=1, source_target_pairs={{0,12},{1,13},{2,14},{3,15},{4,0},{5,1},{6,2},{7,3},{8,4},{9,5},{1... | collective-permute-start | bytes 442376 | tf_op jit(solution)/shard_map/ppermute | solution.py:565
  (59 other events, 291.7 us)

commit v9 on v7

--- a/solution.py
+++ b/solution.py
@@ -1778,7 +1778,7 @@
     head_lines = line_parts(jnp.concatenate(head_planes))
     size = LINE // 2 * QUARTER_HALF
     cls_far = sent_both(
-        after(cls_y[:, size:], head_lines[3]), after(cls_x[:, :size], head_lines[3])
+        after(cls_y[:, size:], *head_planes[1:]), after(cls_x[:, :size], *head_planes[1:])
     )
 
     second_grad, second_low, second_sums = run_kernel(
@@ -2064,7 +2064,7 @@
         [pltpu.VMEM((LINE,) + pack.shape, LOW)],
     )[0]
     cls_got = other_core(cls_rows)
-    attn_plane = tuple(after(got, cls_got, output, input_grad, shared) for got in attn_plane)
+    attn_plane = tuple(after(got, output, input_grad, shared) for got in attn_plane)
     attn_own, *attn_sent = reduce_fold(where, attn_near[2], attn_plane)
     attn_lines = list(
         together(*(along_line(attn_sent[apart - 1], apart) for apart in range(1, LINE)))

time: 259 us -> 245 us (0.946)
  waiting for transfers between devices: 99 us -> 74.7 us
  starting transfers between devices: 102 us -> 113 us
    ppermute x28, waiting for transfers between devices: 25.8 us -> 7.37 us  [in_plane(): return lax.ppermute(value, 'fsdp', plane_pairs(mask))]
    ppermute x21, starting transfers between devices: 21.7 us -> 31.6 us  [other_core(): return lax.ppermute(value, 'rep', [(0, 1), (1, 0)])]
    ppermute x36, waiting for transfers between devices: 65.5 us -> 56.7 us  [along_line(): return lax.ppermute(value, 'fsdp', line_pairs(apart))]
    ppermute x21, waiting for transfers between devices: 7.7 us -> 10.7 us  [other_core(): return lax.ppermute(value, 'rep', [(0, 1), (1, 0)])]
  transfers between devices with their start and end apart: 85 -> 85, of which waited for: 44 -> 39; matrix products, arithmetic and copies ran while one was open for 0% -> 0% of each run, Pallas kernels for 13% -> 13%
where the time goes in v9:
time: 245 us; the launch traced here: 244 us
  starting transfers between devices  113 us (46%)
  waiting for transfers between devices  74.7 us (30%)
  Pallas kernels  48.2 us (20%)
  local copies, waits for them, and re-layouts  5.36 us (2%)
    ppermute x36, starting transfers between devices, along_line(): return lax.ppermute(value, 'fsdp', line_pairs(apart))  57.3 us
    ppermute x36, waiting for transfers between devices, along_line(): return lax.ppermute(value, 'fsdp', line_pairs(apart))  56.7 us
    pallas_call x26, Pallas kernels, run_kernel(): pl.pallas_call(body, name=name, out_shape=tuple(outs), in_specs=in_specs,...  48.2 us
    ppermute x21, starting transfers between devices, other_core(): return lax.ppermute(value, 'rep', [(0, 1), (1, 0)])  31.6 us
    ppermute x28, starting transfers between devices, in_plane(): return lax.ppermute(value, 'fsdp', plane_pairs(mask))  24 us
    ppermute x21, waiting for transfers between devices, other_core(): return lax.ppermute(value, 'rep', [(0, 1), (1, 0)])  10.7 us
    ppermute x28, waiting for transfers between devices, in_plane(): return lax.ppermute(value, 'fsdp', plane_pairs(mask))  7.37 us
  transfers between devices with their start and end apart: 85, of which 39 were waited for; matrix products, arithmetic and copies ran while one was open for 0% of the time, Pallas kernels for 13%

profile of v9, /device:TPU:13, one launch (start us, length us, event | category | flops | bytes accessed | tf_op | source)
XLA Modules:
  0.0 243.8 jit_solution(9550182211816024873)
XLA Ops:
  14.2 7.2 %collective-permute-done.1.refs_2_ = bf16[48,1664]{1,0:T(8,128)(2,1)S(1)} collective-permute-done((bf16[48,1664]{1,0:T(8,128)(2,1)S(1)}, bf16[48,1664]{1,0:T(8,128)(2,1)S(1)}, u32[]{:S(2)}, u32[]{:S(2)}) %collective-permute-start.1) | collective-permute-done | bytes 159776 | tf_op jit(solution)/shard_map/ppermute | solution.py:565
  21.4 3.9 %collective-permute-done.refs_1_ = bf16[48,1664]{1,0:T(8,128)(2,1)S(1)} collective-permute-done((bf16[48,1664]{1,0:T(8,128)(2,1)S(1)}, bf16[48,1664]{1,0:T(8,128)(2,1)S(1)}, u32[]{:S(2)}, u32[]{:S(2)}) %collective-permute-start) | collective-permute-done | bytes 159776 | tf_op jit(solution)/shard_map/ppermute | solution.py:565
  30.9 2.5 %collective-permute-start.10 = (bf16[48,1536]{1,0:T(8,128)(2,1)S(1)}, bf16[48,1536]{1,0:T(8,128)(2,1)S(1)}, u32[]{:S(2)}, u32[]{:S(2)}) collective-permute-start(bf16[48,1536]{1,0:T(8,128)(2,1)S(1)} %get-tuple-element.273.refs_0_), channel_id=1, source_target_pairs={{0,8},{1,9},{2,10},{3,11},{4,12},{5,13},{6,14},{7,15},{8,0},{9,1},... | collective-permute-start | bytes 442376 | tf_op jit(solution)/shard_map/ppermute | solution.py:565
  33.4 2.8 %collective-permute-done.11.refs_3_ = bf16[48,1536]{1,0:T(8,128)(2,1)S(1)} collective-permute-done((bf16[48,1536]{1,0:T(8,128)(2,1)S(1)}, bf16[48,1536]{1,0:T(8,128)(2,1)S(1)}, u32[]{:S(2)}, u32[]{:S(2)}) %collective-permute-start.11) | collective-permute-done | bytes 147488 | tf_op jit(solution)/shard_map/ppermute | solution.py:565
  36.2 5.2 %collective-permute-done.10.refs_2_ = bf16[48,1536]{1,0:T(8,128)(2,1)S(1)} collective-permute-done((bf16[48,1536]{1,0:T(8,128)(2,1)S(1)}, bf16[48,1536]{1,0:T(8,128)(2,1)S(1)}, u32[]{:S(2)}, u32[]{:S(2)}) %collective-permute-start.10) | collective-permute-done | bytes 147488 | tf_op jit(solution)/shard_map/ppermute | solution.py:565
  41.4 3.2 %collective-permute-done.9.refs_1_ = bf16[48,1536]{1,0:T(8,128)(2,1)S(1)} collective-permute-done((bf16[48,1536]{1,0:T(8,128)(2,1)S(1)}, bf16[48,1536]{1,0:T(8,128)(2,1)S(1)}, u32[]{:S(2)}, u32[]{:S(2)}) %collective-permute-start.9) | collective-permute-done | bytes 147488 | tf_op jit(solution)/shard_map/ppermute | solution.py:565
  51.6 6.6 %collective-permute-done.16.refs_2_ = bf16[48,1536]{1,0:T(8,128)(2,1)S(1)} collective-permute-done((bf16[48,1536]{1,0:T(8,128)(2,1)S(1)}, bf16[48,1536]{1,0:T(8,128)(2,1)S(1)}, u32[]{:S(2)}, u32[]{:S(2)}) %collective-permute-start.16) | collective-permute-done | bytes 147488 | tf_op jit(solution)/shard_map/ppermute | solution.py:565
  58.1 3.2 %collective-permute-done.15.refs_1_ = bf16[48,1536]{1,0:T(8,128)(2,1)S(1)} collective-permute-done((bf16[48,1536]{1,0:T(8,128)(2,1)S(1)}, bf16[48,1536]{1,0:T(8,128)(2,1)S(1)}, u32[]{:S(2)}, u32[]{:S(2)}) %collective-permute-start.15) | collective-permute-done | bytes 147488 | tf_op jit(solution)/shard_map/ppermute | solution.py:565
  67.7 3.9 %seg_qkv.1 = (bf16[16,48,1152]{2,1,0:T(8,128)(2,1)S(1)}, bf16[8,48,384]{2,1,0:T(8,128)(2,1)S(1)}, bf16[8,48,384]{2,1,0:T(8,128)(2,1)S(1)}, bf16[256,1152]{1,0:T(...) custom-call(s32[5]{0:T(128)S(1)} %stack.24.where, ...), custom_call_target="tpu_custom_call" | custom-call | flops 452984832 | bytes 11453440 | tf_op jit(solution)/shard_map/seg_qkv/pallas_call | solution.py:595
  71.6 3.2 %collective-permute-start.20 = (bf16[8,48,384]{2,1,0:T(8,128)(2,1)S(1)}, bf16[8,48,384]{2,1,0:T(8,128)(2,1)S(1)}, u32[]{:S(2)}, u32[]{:S(2)}) collective-permute-start(bf16[8,48,384]{2,1,0:T(8,128)(2,1)S(1)} %get-tuple-element.293.low), channel_id=1, source_target_pairs={{0,16},{16,0},{1,17},{17,1},{2,18},{18,2},{3,19},{19,3},{4,20},{20... | collective-permute-start | bytes 884744 | tf_op jit(solution)/shard_map/ppermute | solution.py:573
  82.6 3.3 %collective-permute-start.24 = (bf16[128,768]{1,0:T(8,128)(2,1)S(1)}, bf16[128,768]{1,0:T(8,128)(2,1)S(1)}, u32[]{:S(2)}, u32[]{:S(2)}) collective-permute-start(bf16[128,768]{1,0:T(8,128)(2,1)S(1)} %get-tuple-element.302.refs_12_.refs_0_.refs_6_), channel_id=1, source_target_pairs={{0,16},{16,0},{1,17},{17,1},{2,18},{18,2},{3,19},{19,3},{4,20},{20... | collective-permute-start | bytes 589832 | tf_op jit(solution)/shard_map/ppermute | solution.py:573
  91.9 3.1 %collective-permute-start.25 = (f32[128,768]{1,0:T(8,128)S(1)}, f32[128,768]{1,0:T(8,128)S(1)}, u32[]{:S(2)}, u32[]{:S(2)}) collective-permute-start(f32[128,768]{1,0:T(8,128)S(1)} %get-tuple-element.306), channel_id=1, source_target_pairs={{0,16},{16,0},{1,17},{17,1},{2,18},{18,2},{3,19},{19,3},{4,20},{20... | collective-permute-start | bytes 1179656 | tf_op jit(solution)/shard_map/ppermute | solution.py:573
  114.2 2.3 collective-permute-start.42
  116.5 3.1 %seg_mlp_weight.1 = (bf16[2,48,3072]{2,1,0:T(8,128)(2,1)S(1)}, bf16[2,48,3072]{2,1,0:T(8,128)(2,1)S(1)}, bf16[4,48,3072]{2,1,0:T(8,128)(2,1)S(1)}, bf16[4,48,307...) custom-call(s32[5]{0:T(128)S(1)} %stack.24.where, bf16[128,768]{1,0:T(8,128)(2,1)S(1)} %get-tuple-element.302.refs_12_.refs_0_.refs_6_, ...), custom_call_target="tpu_custom_call" | custom-call | flops 1207959552 | bytes 7077888 | tf_op jit(solution)/shard_map/seg_mlp_weight/pallas_call | solution.py:595
  125.8 2.9 %collective-permute-start.46 = (f32[16,768]{1,0:T(8,128)S(1)}, f32[16,768]{1,0:T(8,128)S(1)}, u32[]{:S(2)}, u32[]{:S(2)}) collective-permute-start(f32[16,768]{1,0:T(8,128)S(1)} %get-tuple-element.368.refs_1_), channel_id=1, source_target_pairs={{0,12},{1,13},{2,14},{3,15},{4,0},{5,1},{6,2},{7,3},{8,4},{9,5},{1... | collective-permute-start | bytes 147464 | tf_op jit(solution)/shard_map/ppermute | solution.py:565
  129.3 2.3 collective-permute-start.44
  131.6 3.0 %collective-permute-done.47.refs_7_ = bf16[2,48,3072]{2,1,0:T(8,128)(2,1)S(1)} collective-permute-done((bf16[2,48,3072]{2,1,0:T(8,128)(2,1)S(1)}, bf16[2,48,3072]{2,1,0:T(8,128)(2,1)S(1)}, u32[]{:S(2)}, u32[]{:S(2)}) %collective-permute-start.47) | collective-permute-done | bytes 589856 | tf_op jit(solution)/shard_map/ppermute | solution.py:569
  137.9 3.3 %collective-permute-start.51 = (f32[16,768]{1,0:T(8,128)S(1)}, f32[16,768]{1,0:T(8,128)S(1)}, u32[]{:S(2)}, u32[]{:S(2)}) collective-permute-start(f32[16,768]{1,0:T(8,128)S(1)} %get-tuple-element.379.refs_1_), channel_id=1, source_target_pairs={{0,12},{1,13},{2,14},{3,15},{4,0},{5,1},{6,2},{7,3},{8,4},{9,5},{1... | collective-permute-start | bytes 147464 | tf_op jit(solution)/shard_map/ppermute | solution.py:565
  141.3 2.4 collective-permute-start.49
  159.7 2.5 %collective-permute-done.56.refs_4_ = f32[16,768]{1,0:T(8,128)S(1)} collective-permute-done((f32[16,768]{1,0:T(8,128)S(1)}, f32[16,768]{1,0:T(8,128)S(1)}, u32[]{:S(2)}, u32[]{:S(2)}) %collective-permute-start.56) | collective-permute-done | bytes 49184 | tf_op jit(solution)/shard_map/ppermute | solution.py:565
  164.9 3.2 %collective-permute-start.63 = (bf16[64,3072]{1,0:T(8,128)(2,1)S(1)}, bf16[64,3072]{1,0:T(8,128)(2,1)S(1)}, u32[]{:S(2)}, u32[]{:S(2)}) collective-permute-start(bf16[64,3072]{1,0:T(8,128)(2,1)S(1)} %get-tuple-element.430), channel_id=1, source_target_pairs={{0,12},{1,13},{2,14},{3,15},{4,0},{5,1},{6,2},{7,3},{8,4},{9,5},{1... | collective-permute-start | bytes 1179656 | tf_op jit(solution)/shard_map/ppermute | solution.py:565
  168.1 2.7 %collective-permute-start.60 = (f32[1,768]{1,0:T(1,128)S(1)}, f32[1,768]{1,0:T(1,128)S(1)}, u32[]{:S(2)}, u32[]{:S(2)}) collective-permute-start(f32[1,768]{1,0:T(1,128)S(1)} %get-tuple-element.411.refs_0_.refs_3_), channel_id=1, source_target_pairs={{0,16},{16,0},{1,17},{17,1},{2,18},{18,2},{3,19},{19,3},{4,20},{20... | collective-permute-start | bytes 9224 | tf_op jit(solution)/shard_map/ppermute | solution.py:573
  177.1 4.4 %seg_attn_back.1 = (bf16[256,1152]{1,0:T(8,128)(2,1)S(1)}, f32[128,768]{1,0:T(8,128)S(1)}, f32[128,768]{1,0:T(8,128)S(1)}, bf16[24,768]{1,0:T(8,128)(2,1)S(1)}) custom-call(s32[5]{0:T(128)S(1)} %stack.24.where, bf16[256,1152]{1,0:T(8,128)(2,1)S(1)} %get-tuple-element.297.refs_0_, bf16[128,768]{1,0:T(8,128)(2,1)S(1)} %get-tuple-element.416.refs_1_, ...), custom_call_target="tpu_custom_call" | custom-call | flops 905969664 | bytes 4624384 | tf_op jit(solution)/shard_map/seg_attn_back/pallas_call | solution.py:595
  187.5 7.7 %collective-permute-done.66.refs_2_ = bf16[64,3072]{1,0:T(8,128)(2,1)S(1)} collective-permute-done((bf16[64,3072]{1,0:T(8,128)(2,1)S(1)}, bf16[64,3072]{1,0:T(8,128)(2,1)S(1)}, u32[]{:S(2)}, u32[]{:S(2)}) %collective-permute-start.66) | collective-permute-done | bytes 393248 | tf_op jit(solution)/shard_map/ppermute | solution.py:565
  198.4 2.8 %collective-permute-start.76 = (bf16[24,768]{1,0:T(8,128)(2,1)S(1)}, bf16[24,768]{1,0:T(8,128)(2,1)S(1)}, u32[]{:S(2)}, u32[]{:S(2)}) collective-permute-start(bf16[24,768]{1,0:T(8,128)(2,1)S(1)} %get-tuple-element.461), channel_id=1, source_target_pairs={{0,12},{1,13},{2,14},{3,15},{4,0},{5,1},{6,2},{7,3},{8,4},{9,5},{1... | collective-permute-start | bytes 110600 | tf_op jit(solution)/shard_map/ppermute | solution.py:565
  201.5 2.4 collective-permute-start.74
  213.2 4.0 %collective-permute-start.72 = (bf16[48,1536]{1,0:T(8,128)(2,1)S(1)}, bf16[48,1536]{1,0:T(8,128)(2,1)S(1)}, u32[]{:S(2)}, u32[]{:S(2)}) collective-permute-start(bf16[48,1536]{1,0:T(8,128)(2,1)S(1)} %get-tuple-element.457), channel_id=1, source_target_pairs={{0,8},{1,9},{2,10},{3,11},{4,12},{5,13},{6,14},{7,15},{8,0},{9,1},... | collective-permute-start | bytes 442376 | tf_op jit(solution)/shard_map/ppermute | solution.py:565
  221.8 3.9 %collective-permute-done.72 = bf16[48,1536]{1,0:T(8,128)(2,1)S(1)} collective-permute-done((bf16[48,1536]{1,0:T(8,128)(2,1)S(1)}, bf16[48,1536]{1,0:T(8,128)(2,1)S(1)}, u32[]{:S(2)}, u32[]{:S(2)}) %collective-permute-start.72) | collective-permute-done | bytes 147488 | tf_op jit(solution)/shard_map/ppermute | solution.py:565
  225.7 4.0 %collective-permute-start.81 = (bf16[16,12288]{1,0:T(8,128)(2,1)S(1)}, bf16[16,12288]{1,0:T(8,128)(2,1)S(1)}, u32[]{:S(2)}, u32[]{:S(2)}) collective-permute-start(bf16[16,12288]{1,0:T(8,128)(2,1)S(1)} %head_rows.1.refs_5_), channel_id=1, source_target_pairs={{0,16},{16,0},{1,17},{17,1},{2,18},{18,2},{3,19},{19,3},{4,20},{20... | collective-permute-start | bytes 1179656 | tf_op jit(solution)/shard_map/ppermute | solution.py:573
  231.1 4.4 %head_owner.1 = (f32[48,3072]{1,0:T(8,128)S(1)}, f32[16,768]{1,0:T(8,128)S(1)}, f32[48,9216]{1,0:T(8,128)}, f32[576]{0:T(1024)}, f32[16,768]{1,0:T(8,128)}, /*index=5*/f32[1,1]{1,0:T(1,128)}) custom-call(s32[5]{0:T(128)S(1)} %stack.24.where, bf16[96,768]{1,0:T(8,128)(2,1)S(1)} %pad_maximum_fusion.11.refs_0_, ...), custom_call_target="tpu_custom_call" | custom-call | flops 28311552 | bytes 4503812 | tf_op jit(solution)/shard_map/head_owner/pallas_call | solution.py:595
  235.5 2.7 %collective-permute-start.83 = (f32[48,3072]{1,0:T(8,128)S(1)}, f32[48,3072]{1,0:T(8,128)S(1)}, u32[]{:S(2)}, u32[]{:S(2)}) collective-permute-start(f32[48,3072]{1,0:T(8,128)S(1)} %get-tuple-element.482.mlp), channel_id=1, source_target_pairs={{0,16},{16,0},{1,17},{17,1},{2,18},{18,2},{3,19},{19,3},{4,20},{20... | collective-permute-start | bytes 1769480 | tf_op jit(solution)/shard_map/ppermute | solution.py:573
  240.3 3.3 %seg_owner.1 = (f32[48,9216]{1,0:T(8,128)}, f32[576]{0:T(1024)}) custom-call(s32[5]{0:T(128)S(1)} %stack.24.where, f32[48,1536]{1,0:T(8,128)S(1)} %convert_add_fusion.1.attn, f32[48,1536]{1,0:T(8,128)S(1)} %collective-permute-done.82.attn_got, f32[48,3072]{1,0:T(8,128)S(1)} %get-tuple-element.482.mlp, f32[48,3072]{1,0:T(8,128)S(1)} %collective-permute-done.83.mlp_got, ...), custom_call_target="tpu_custom_call" | custom-call | bytes 3639552 | tf_op jit(solution)/shard_map/seg_owner/pallas_call | solution.py:595
  (211 shorter events, 126.4 us)
Async XLA Ops:
  8.0 17.3 %collective-permute-start.3 = (bf16[48,4736]{1,0:T(8,128)(2,1)S(1)}, bf16[48,4736]{1,0:T(8,128)(2,1)S(1)}, u32[]{:S(2)}, u32[]{:S(2)}) collective-permute-start(bf16[48,4736]{1,0:T(8,128)(2,1)S(1)} %pad_maximum_fusion.10), channel_id=1, source_target_pairs={{0,1},{1,0},{2,3},{3,2},{4,5},{5,4},{6,7},{7,6},{8,9},{9,8},{10,11... | collective-permute-start | bytes 1363976 | tf_op jit(solution)/shard_map/ppermute | solution.py:569
  9.3 16.0 %collective-permute-start.4 = (bf16[48,4736]{1,0:T(8,128)(2,1)S(1)}, bf16[48,4736]{1,0:T(8,128)(2,1)S(1)}, u32[]{:S(2)}, u32[]{:S(2)}) collective-permute-start(bf16[48,4736]{1,0:T(8,128)(2,1)S(1)} %pad_maximum_fusion.10), channel_id=1, source_target_pairs={{0,2},{1,3},{2,0},{3,1},{4,6},{5,7},{6,4},{7,5},{8,10},{9,11},{10,... | collective-permute-start | bytes 1363976 | tf_op jit(solution)/shard_map/ppermute | solution.py:569
  9.7 11.7 %collective-permute-start.1 = (bf16[48,1664]{1,0:T(8,128)(2,1)S(1)}, bf16[48,1664]{1,0:T(8,128)(2,1)S(1)}, u32[]{:S(2)}, u32[]{:S(2)}) collective-permute-start(bf16[48,1664]{1,0:T(8,128)(2,1)S(1)} %get-tuple-element.253.refs_0_), channel_id=1, source_target_pairs={{0,8},{1,9},{2,10},{3,11},{4,12},{5,13},{6,14},{7,15},{8,0},{9,1},... | collective-permute-start | bytes 479240 | tf_op jit(solution)/shard_map/ppermute | solution.py:565
  12.0 13.3 %collective-permute-start = (bf16[48,1664]{1,0:T(8,128)(2,1)S(1)}, bf16[48,1664]{1,0:T(8,128)(2,1)S(1)}, u32[]{:S(2)}, u32[]{:S(2)}) collective-permute-start(bf16[48,1664]{1,0:T(8,128)(2,1)S(1)} %get-tuple-element.253.refs_0_), channel_id=1, source_target_pairs={{0,4},{1,5},{2,6},{3,7},{4,8},{5,9},{6,10},{7,11},{8,12},{9,13},{1... | collective-permute-start | bytes 479240 | tf_op jit(solution)/shard_map/ppermute | solution.py:565
  25.5 19.1 %collective-permute-start.6 = (bf16[48,7424]{1,0:T(8,128)(2,1)S(1)}, bf16[48,7424]{1,0:T(8,128)(2,1)S(1)}, u32[]{:S(2)}, u32[]{:S(2)}) collective-permute-start(bf16[48,7424]{1,0:T(8,128)(2,1)S(1)} %pad_maximum_fusion.6), channel_id=1, source_target_pairs={{0,2},{1,3},{2,0},{3,1},{4,6},{5,7},{6,4},{7,5},{8,10},{9,11},{10,... | collective-permute-start | bytes 2138120 | tf_op jit(solution)/shard_map/ppermute | solution.py:569
  26.8 17.8 %collective-permute-start.5 = (bf16[48,7296]{1,0:T(8,128)(2,1)S(1)}, bf16[48,7296]{1,0:T(8,128)(2,1)S(1)}, u32[]{:S(2)}, u32[]{:S(2)}) collective-permute-start(bf16[48,7296]{1,0:T(8,128)(2,1)S(1)} %pad_maximum_fusion.7), channel_id=1, source_target_pairs={{0,1},{1,0},{2,3},{3,2},{4,5},{5,4},{6,7},{7,6},{8,9},{9,8},{10,11... | collective-permute-start | bytes 2101256 | tf_op jit(solution)/shard_map/ppermute | solution.py:569
  33.4 11.1 %collective-permute-start.9 = (bf16[48,1536]{1,0:T(8,128)(2,1)S(1)}, bf16[48,1536]{1,0:T(8,128)(2,1)S(1)}, u32[]{:S(2)}, u32[]{:S(2)}) collective-permute-start(bf16[48,1536]{1,0:T(8,128)(2,1)S(1)} %get-tuple-element.273.refs_0_), channel_id=1, source_target_pairs={{0,4},{1,5},{2,6},{3,7},{4,8},{5,9},{6,10},{7,11},{8,12},{9,13},{1... | collective-permute-start | bytes 442376 | tf_op jit(solution)/shard_map/ppermute | solution.py:565
  44.7 16.6 %collective-permute-start.13 = (bf16[48,7168]{1,0:T(8,128)(2,1)S(1)}, bf16[48,7168]{1,0:T(8,128)(2,1)S(1)}, u32[]{:S(2)}, u32[]{:S(2)}) collective-permute-start(bf16[48,7168]{1,0:T(8,128)(2,1)S(1)} %pad_maximum_fusion.8), channel_id=1, source_target_pairs={{0,2},{1,3},{2,0},{3,1},{4,6},{5,7},{6,4},{7,5},{8,10},{9,11},{10,... | collective-permute-start | bytes 2064392 | tf_op jit(solution)/shard_map/ppermute | solution.py:569
  45.0 16.3 %collective-permute-start.12 = (bf16[48,7040]{1,0:T(8,128)(2,1)S(1)}, bf16[48,7040]{1,0:T(8,128)(2,1)S(1)}, u32[]{:S(2)}, u32[]{:S(2)}) collective-permute-start(bf16[48,7040]{1,0:T(8,128)(2,1)S(1)} %pad_maximum_fusion.9), channel_id=1, source_target_pairs={{0,1},{1,0},{2,3},{3,2},{4,5},{5,4},{6,7},{7,6},{8,9},{9,8},{10,11... | collective-permute-start | bytes 2027528 | tf_op jit(solution)/shard_map/ppermute | solution.py:569
  49.6 11.7 %collective-permute-start.15 = (bf16[48,1536]{1,0:T(8,128)(2,1)S(1)}, bf16[48,1536]{1,0:T(8,128)(2,1)S(1)}, u32[]{:S(2)}, u32[]{:S(2)}) collective-permute-start(bf16[48,1536]{1,0:T(8,128)(2,1)S(1)} %get-tuple-element.284.refs_0_), channel_id=1, source_target_pairs={{0,4},{1,5},{2,6},{3,7},{4,8},{5,9},{6,10},{7,11},{8,12},{9,13},{1... | collective-permute-start | bytes 442376 | tf_op jit(solution)/shard_map/ppermute | solution.py:565
  61.5 15.2 %collective-permute-start.18 = (bf16[48,6912]{1,0:T(8,128)(2,1)S(1)}, bf16[48,6912]{1,0:T(8,128)(2,1)S(1)}, u32[]{:S(2)}, u32[]{:S(2)}) collective-permute-start(bf16[48,6912]{1,0:T(8,128)(2,1)S(1)} %get-tuple-element.288), channel_id=1, source_target_pairs={{0,1},{1,0},{2,3},{3,2},{4,5},{5,4},{6,7},{7,6},{8,9},{9,8},{10,11... | collective-permute-start | bytes 1990664 | tf_op jit(solution)/shard_map/ppermute | solution.py:569
  62.7 12.1 %collective-permute-start.32 = (bf16[48,1152]{1,0:T(8,128)(2,1)S(1)}, bf16[48,1152]{1,0:T(8,128)(2,1)S(1)}, u32[]{:S(2)}, u32[]{:S(2)}) collective-permute-start(bf16[48,1152]{1,0:T(8,128)(2,1)S(1)} %get-tuple-element.327), channel_id=1, source_target_pairs={{0,4},{1,5},{2,6},{3,7},{4,8},{5,9},{6,10},{7,11},{8,12},{9,13},{1... | collective-permute-start | bytes 331784 | tf_op jit(solution)/shard_map/ppermute | solution.py:565
  64.9 14.5 %collective-permute-start.19 = (bf16[48,6912]{1,0:T(8,128)(2,1)S(1)}, bf16[48,6912]{1,0:T(8,128)(2,1)S(1)}, u32[]{:S(2)}, u32[]{:S(2)}) collective-permute-start(bf16[48,6912]{1,0:T(8,128)(2,1)S(1)} %get-tuple-element.289), channel_id=1, source_target_pairs={{0,2},{1,3},{2,0},{3,1},{4,6},{5,7},{6,4},{7,5},{8,10},{9,11},{10,... | collective-permute-start | bytes 1990664 | tf_op jit(solution)/shard_map/ppermute | solution.py:569
  74.9 11.0 %collective-permute-start.34 = (bf16[48,1152]{1,0:T(8,128)(2,1)S(1)}, bf16[48,1152]{1,0:T(8,128)(2,1)S(1)}, u32[]{:S(2)}, u32[]{:S(2)}) collective-permute-start(bf16[48,1152]{1,0:T(8,128)(2,1)S(1)} %get-tuple-element.331), channel_id=1, source_target_pairs={{0,12},{1,13},{2,14},{3,15},{4,0},{5,1},{6,2},{7,3},{8,4},{9,5},{1... | collective-permute-start | bytes 331784 | tf_op jit(solution)/shard_map/ppermute | solution.py:565
  88.9 13.7 %collective-permute-start.35 = (bf16[48,4992]{1,0:T(8,128)(2,1)S(1)}, bf16[48,4992]{1,0:T(8,128)(2,1)S(1)}, u32[]{:S(2)}, u32[]{:S(2)}) collective-permute-start(bf16[48,4992]{1,0:T(8,128)(2,1)S(1)} %constant_dynamic-update-slice_fusion), channel_id=1, source_target_pairs={{0,1},{1,0},{2,3},{3,2},{4,5},{5,4},{6,7},{7,6},{8,9},{9,8},{10,11... | collective-permute-start | bytes 1437704 | tf_op jit(solution)/shard_map/ppermute | solution.py:569
  89.8 12.8 %collective-permute-start.36 = (bf16[48,4992]{1,0:T(8,128)(2,1)S(1)}, bf16[48,4992]{1,0:T(8,128)(2,1)S(1)}, u32[]{:S(2)}, u32[]{:S(2)}) collective-permute-start(bf16[48,4992]{1,0:T(8,128)(2,1)S(1)} %constant_dynamic-update-slice_fusion), channel_id=1, source_target_pairs={{0,2},{1,3},{2,0},{3,1},{4,6},{5,7},{6,4},{7,5},{8,10},{9,11},{10,... | collective-permute-start | bytes 1437704 | tf_op jit(solution)/shard_map/ppermute | solution.py:569
  119.6 15.0 %collective-permute-start.47 = (bf16[2,48,3072]{2,1,0:T(8,128)(2,1)S(1)}, bf16[2,48,3072]{2,1,0:T(8,128)(2,1)S(1)}, u32[]{:S(2)}, u32[]{:S(2)}) collective-permute-start(bf16[2,48,3072]{2,1,0:T(8,128)(2,1)S(1)} %get-tuple-element.372), channel_id=1, source_target_pairs={{0,2},{1,3},{2,0},{3,1},{4,6},{5,7},{6,4},{7,5},{8,10},{9,11},{10,... | collective-permute-start | bytes 1769480 | tf_op jit(solution)/shard_map/ppermute | solution.py:569
  120.6 14.6 %collective-permute-start.48 = (bf16[2,48,3072]{2,1,0:T(8,128)(2,1)S(1)}, bf16[2,48,3072]{2,1,0:T(8,128)(2,1)S(1)}, u32[]{:S(2)}, u32[]{:S(2)}) collective-permute-start(bf16[2,48,3072]{2,1,0:T(8,128)(2,1)S(1)} %get-tuple-element.374), channel_id=1, source_target_pairs={{0,1},{1,0},{2,3},{3,2},{4,5},{5,4},{6,7},{7,6},{8,9},{9,8},{10,11... | collective-permute-start | bytes 1769480 | tf_op jit(solution)/shard_map/ppermute | solution.py:569
  136.7 26.4 %collective-permute-start.58 = (bf16[4,48,3072]{2,1,0:T(8,128)(2,1)S(1)}, bf16[4,48,3072]{2,1,0:T(8,128)(2,1)S(1)}, u32[]{:S(2)}, u32[]{:S(2)}) collective-permute-start(bf16[4,48,3072]{2,1,0:T(8,128)(2,1)S(1)} %get-tuple-element.403), channel_id=1, source_target_pairs={{0,1},{1,0},{2,3},{3,2},{4,5},{5,4},{6,7},{7,6},{8,9},{9,8},{10,11... | collective-permute-start | bytes 3538952 | tf_op jit(solution)/shard_map/ppermute | solution.py:569
  137.4 26.1 %collective-permute-start.59 = (bf16[4,48,3072]{2,1,0:T(8,128)(2,1)S(1)}, bf16[4,48,3072]{2,1,0:T(8,128)(2,1)S(1)}, u32[]{:S(2)}, u32[]{:S(2)}) collective-permute-start(bf16[4,48,3072]{2,1,0:T(8,128)(2,1)S(1)} %get-tuple-element.404), channel_id=1, source_target_pairs={{0,2},{1,3},{2,0},{3,1},{4,6},{5,7},{6,4},{7,5},{8,10},{9,11},{10,... | collective-permute-start | bytes 3538952 | tf_op jit(solution)/shard_map/ppermute | solution.py:569
  164.9 18.1 %collective-permute-start.63 = (bf16[64,3072]{1,0:T(8,128)(2,1)S(1)}, bf16[64,3072]{1,0:T(8,128)(2,1)S(1)}, u32[]{:S(2)}, u32[]{:S(2)}) collective-permute-start(bf16[64,3072]{1,0:T(8,128)(2,1)S(1)} %get-tuple-element.430), channel_id=1, source_target_pairs={{0,12},{1,13},{2,14},{3,15},{4,0},{5,1},{6,2},{7,3},{8,4},{9,5},{1... | collective-permute-start | bytes 1179656 | tf_op jit(solution)/shard_map/ppermute | solution.py:565
  176.0 19.2 %collective-permute-start.66 = (bf16[64,3072]{1,0:T(8,128)(2,1)S(1)}, bf16[64,3072]{1,0:T(8,128)(2,1)S(1)}, u32[]{:S(2)}, u32[]{:S(2)}) collective-permute-start(bf16[64,3072]{1,0:T(8,128)(2,1)S(1)} %get-tuple-element.439), channel_id=1, source_target_pairs={{0,8},{1,9},{2,10},{3,11},{4,12},{5,13},{6,14},{7,15},{8,0},{9,1},... | collective-permute-start | bytes 1179656 | tf_op jit(solution)/shard_map/ppermute | solution.py:565
  181.5 13.7 %collective-permute-start.67 = (f32[128,768]{1,0:T(8,128)S(1)}, f32[128,768]{1,0:T(8,128)S(1)}, u32[]{:S(2)}, u32[]{:S(2)}) collective-permute-start(f32[128,768]{1,0:T(8,128)S(1)} %get-tuple-element.442), channel_id=1, source_target_pairs={{0,16},{16,0},{1,17},{17,1},{2,18},{18,2},{3,19},{19,3},{4,20},{20... | collective-permute-start | bytes 1179656 | tf_op jit(solution)/shard_map/ppermute | solution.py:573
  183.0 12.2 %collective-permute-start.65 = (bf16[2,48,1536]{2,1,0:T(8,128)(2,1)S(1)}, bf16[2,48,1536]{2,1,0:T(8,128)(2,1)S(1)}, u32[]{:S(2)}, u32[]{:S(2)}) collective-permute-start(bf16[2,48,1536]{2,1,0:T(8,128)(2,1)S(1)} %get-tuple-element.433), channel_id=1, source_target_pairs={{0,1},{1,0},{2,3},{3,2},{4,5},{5,4},{6,7},{7,6},{8,9},{9,8},{10,11... | collective-permute-start | bytes 884744 | tf_op jit(solution)/shard_map/ppermute | solution.py:569
  184.3 10.9 %collective-permute-start.64 = (bf16[2,48,1536]{2,1,0:T(8,128)(2,1)S(1)}, bf16[2,48,1536]{2,1,0:T(8,128)(2,1)S(1)}, u32[]{:S(2)}, u32[]{:S(2)}) collective-permute-start(bf16[2,48,1536]{2,1,0:T(8,128)(2,1)S(1)} %get-tuple-element.431), channel_id=1, source_target_pairs={{0,2},{1,3},{2,0},{3,1},{4,6},{5,7},{6,4},{7,5},{8,10},{9,11},{10,... | collective-permute-start | bytes 884744 | tf_op jit(solution)/shard_map/ppermute | solution.py:569
  196.6 14.4 %collective-permute-start.68 = (bf16[4,48,1536]{2,1,0:T(8,128)(2,1)S(1)}, bf16[4,48,1536]{2,1,0:T(8,128)(2,1)S(1)}, u32[]{:S(2)}, u32[]{:S(2)}) collective-permute-start(bf16[4,48,1536]{2,1,0:T(8,128)(2,1)S(1)} %get-tuple-element.447), channel_id=1, source_target_pairs={{0,1},{1,0},{2,3},{3,2},{4,5},{5,4},{6,7},{7,6},{8,9},{9,8},{10,11... | collective-permute-start | bytes 1769480 | tf_op jit(solution)/shard_map/ppermute | solution.py:569
  197.8 14.1 %collective-permute-start.69 = (bf16[4,48,1536]{2,1,0:T(8,128)(2,1)S(1)}, bf16[4,48,1536]{2,1,0:T(8,128)(2,1)S(1)}, u32[]{:S(2)}, u32[]{:S(2)}) collective-permute-start(bf16[4,48,1536]{2,1,0:T(8,128)(2,1)S(1)} %get-tuple-element.448), channel_id=1, source_target_pairs={{0,2},{1,3},{2,0},{3,1},{4,6},{5,7},{6,4},{7,5},{8,10},{9,11},{10,... | collective-permute-start | bytes 1769480 | tf_op jit(solution)/shard_map/ppermute | solution.py:569
  205.5 13.3 %collective-permute-start.80 = (bf16[64,3072]{1,0:T(8,128)(2,1)S(1)}, bf16[64,3072]{1,0:T(8,128)(2,1)S(1)}, u32[]{:S(2)}, u32[]{:S(2)}) collective-permute-start(bf16[64,3072]{1,0:T(8,128)(2,1)S(1)} %get-tuple-element.475), channel_id=1, source_target_pairs={{0,4},{1,5},{2,6},{3,7},{4,8},{5,9},{6,10},{7,11},{8,12},{9,13},{1... | collective-permute-start | bytes 1179656 | tf_op jit(solution)/shard_map/ppermute | solution.py:565
  213.2 12.5 %collective-permute-start.72 = (bf16[48,1536]{1,0:T(8,128)(2,1)S(1)}, bf16[48,1536]{1,0:T(8,128)(2,1)S(1)}, u32[]{:S(2)}, u32[]{:S(2)}) collective-permute-start(bf16[48,1536]{1,0:T(8,128)(2,1)S(1)} %get-tuple-element.457), channel_id=1, source_target_pairs={{0,8},{1,9},{2,10},{3,11},{4,12},{5,13},{6,14},{7,15},{8,0},{9,1},... | collective-permute-start | bytes 442376 | tf_op jit(solution)/shard_map/ppermute | solution.py:565
  217.3 12.6 %collective-permute-start.79 = (bf16[96,768]{1,0:T(8,128)(2,1)S(1)}, bf16[96,768]{1,0:T(8,128)(2,1)S(1)}, u32[]{:S(2)}, u32[]{:S(2)}) collective-permute-start(bf16[96,768]{1,0:T(8,128)(2,1)S(1)} %pad_maximum_fusion.11.refs_0_), channel_id=1, source_target_pairs={{0,3},{1,2},{2,1},{3,0},{4,7},{5,6},{6,5},{7,4},{8,11},{9,10},{10,... | collective-permute-start | bytes 442376 | tf_op jit(solution)/shard_map/ppermute | solution.py:569
  218.3 11.6 %collective-permute-start.78 = (bf16[96,768]{1,0:T(8,128)(2,1)S(1)}, bf16[96,768]{1,0:T(8,128)(2,1)S(1)}, u32[]{:S(2)}, u32[]{:S(2)}) collective-permute-start(bf16[96,768]{1,0:T(8,128)(2,1)S(1)} %pad_maximum_fusion.11.refs_0_), channel_id=1, source_target_pairs={{0,2},{1,3},{2,0},{3,1},{4,6},{5,7},{6,4},{7,5},{8,10},{9,11},{10,... | collective-permute-start | bytes 442376 | tf_op jit(solution)/shard_map/ppermute | solution.py:569
  218.8 11.0 %collective-permute-start.77 = (bf16[96,768]{1,0:T(8,128)(2,1)S(1)}, bf16[96,768]{1,0:T(8,128)(2,1)S(1)}, u32[]{:S(2)}, u32[]{:S(2)}) collective-permute-start(bf16[96,768]{1,0:T(8,128)(2,1)S(1)} %pad_maximum_fusion.11.refs_0_), channel_id=1, source_target_pairs={{0,1},{1,0},{2,3},{3,2},{4,5},{5,4},{6,7},{7,6},{8,9},{9,8},{10,11... | collective-permute-start | bytes 442376 | tf_op jit(solution)/shard_map/ppermute | solution.py:569
  (59 other events, 291.5 us)

commit v10 on v9

--- a/solution.py
+++ b/solution.py
@@ -699,25 +699,26 @@
     return value.reshape(value.shape[0] * value.shape[1], value.shape[2])
 
 
-def prepare_first_kernel(where, seg, vecs, flags, out, live_out, sems):
+def prepare_first_kernel(where, seg, seg_vec, cls_vec, flags, out, live_out, sems):
     core_at = where[2]
     pairs = []
     for piece in range(4):
         source = seg.at[:, pl.ds(aligned(piece * MODEL + core_at * HALF), HALF)]
         pairs.append((source, out.at[:, piece * HALF : (piece + 1) * HALF]))
     run_copies(pairs, sems)
-    size = vecs.shape[1]
+    size = seg_vec.shape[0]
+    vecs = [vec[...].astype(WIDE).reshape(1, size) for vec in (seg_vec, cls_vec)]
     lines = -(-size // LANES)
     block = jnp.zeros((OWN, LANES), WIDE)
     row_at = lax.broadcasted_iota(jnp.int32, (OWN, LANES), 0)
     for which in range(2):
         for line in range(lines):
             width = min(LANES, size - line * LANES)
-            value = vecs[which : which + 1, line * LANES : line * LANES + width]
+            value = vecs[which][:, line * LANES : line * LANES + width]
             if width < LANES:
                 value = jnp.concatenate([value, jnp.zeros((1, LANES - width), WIDE)], axis=1)
             block = jnp.where(row_at == which * lines + line, value, block)
-    live = flags[...].astype(WIDE)
+    live = flags[...].astype(WIDE).reshape(1, SEG)
     live_out[...] = live
     count = jnp.sum(live, axis=1, keepdims=True)
     block = jnp.where(row_at == 2 * lines, count, block)
@@ -765,9 +766,10 @@
         order_out[:, mask * SPAN : (mask + 1) * SPAN] = (feature == source).astype(LOW)
 
 
-def prepare_kernel(where, seg, cls, vecs, flags, first_out, live_out, *refs):
+def prepare_kernel(where, seg, cls, *refs):
+    (seg_vec, cls_vec, flags, first_out, live_out), refs = refs[:5], refs[5:]
     rest, (first_sems, quarters, sems) = refs[:-3], refs[-3:]
-    prepare_first_kernel(where, seg, vecs, flags, first_out, live_out, first_sems)
+    prepare_first_kernel(where, seg, seg_vec, cls_vec, flags, first_out, live_out, first_sems)
     prepare_rest_kernel(where, seg, cls, *rest, quarters, sems)
 
 
@@ -1605,7 +1607,7 @@
         + [shape_of((own_rows, HALF), LOW), shape_of((MODEL, PLANE * SPAN), LOW)],
         where,
         (seg_mats, cls_mats),
-        (jnp.stack([seg_vecs, cls_vecs]).astype(WIDE), valid_flags[None]),
+        (seg_vecs, cls_vecs, valid_flags),
         [
             pltpu.SemaphoreType.DMA((4,)),
             pltpu.VMEM((LINE, own_rows, QUARTER), LOW),
@@ -1631,12 +1633,12 @@
     own_sent = joined(first_piece, second_piece, third_piece)
     own_x, own_y = sent_both(own_sent, own_sent)
     first_line = first_line[:1] + tuple(after(got, own_x, own_y) for got in first_line[1:])
-    to_x = joined(own_y[:, OWN_CUT:], *first_line[1:])
+    hidden_got = other_core(after(hidden_in, own_x, own_y))
+    live_got = other_core(after(live_row, own_x, own_y))
+    to_x = joined(after(own_y, hidden_got, live_got)[:, OWN_CUT:], *first_line[1:])
     to_y = joined(own_x[:, :OWN_CUT], *first_line[1:])
     first_x, first_y = sent_both(to_x, to_y)
-    hidden_got = other_core(after(hidden_in, to_x, to_y))
-    live_got = other_core(after(live_row, to_x, to_y))
-    second_line = line_parts(after(second_piece, hidden_got, live_got, to_x, to_y))
+    second_line = line_parts(after(second_piece, to_x, to_y))
 
     def halves(group, from_x, from_y):
         width, cut = WIDTHS[group], LINE_CUTS[group]

time: 245 us -> 244 us (level)
  starting transfers between devices: 113 us -> 106 us
  waiting for transfers between devices: 74.7 us -> 80.5 us
    ppermute x36, starting transfers between devices: 57.3 us -> 51.1 us  [along_line(): return lax.ppermute(value, 'fsdp', line_pairs(apart))]
    ppermute x28, waiting for transfers between devices: 7.37 us -> 12.8 us  [in_plane(): return lax.ppermute(value, 'fsdp', plane_pairs(mask))]
    ppermute x28, starting transfers between devices: 24 us -> 21.1 us  [in_plane(): return lax.ppermute(value, 'fsdp', plane_pairs(mask))]
    ppermute x21, starting transfers between devices: 31.6 us -> 34.3 us  [other_core(): return lax.ppermute(value, 'rep', [(0, 1), (1, 0)])]
  transfers between devices with their start and end apart: 85 -> 85, of which waited for: 39 -> 44; matrix products, arithmetic and copies ran while one was open for 0% -> 0% of each run, Pallas kernels for 13% -> 13%
where the time goes in v10:
time: 244 us; the launch traced here: 243 us
  starting transfers between devices  106 us (43%)
  waiting for transfers between devices  80.5 us (33%)
  Pallas kernels  48.2 us (20%)
  local copies, waits for them, and re-layouts  5.34 us (2%)
    ppermute x36, waiting for transfers between devices, along_line(): return lax.ppermute(value, 'fsdp', line_pairs(apart))  56.7 us
    ppermute x36, starting transfers between devices, along_line(): return lax.ppermute(value, 'fsdp', line_pairs(apart))  51.1 us
    pallas_call x26, Pallas kernels, run_kernel(): pl.pallas_call(body, name=name, out_shape=tuple(outs), in_specs=in_specs,...  48.2 us
    ppermute x21, starting transfers between devices, other_core(): return lax.ppermute(value, 'rep', [(0, 1), (1, 0)])  34.3 us
    ppermute x28, starting transfers between devices, in_plane(): return lax.ppermute(value, 'fsdp', plane_pairs(mask))  21.1 us
    ppermute x28, waiting for transfers between devices, in_plane(): return lax.ppermute(value, 'fsdp', plane_pairs(mask))  12.8 us
    ppermute x21, waiting for transfers between devices, other_core(): return lax.ppermute(value, 'rep', [(0, 1), (1, 0)])  11 us
  transfers between devices with their start and end apart: 85, of which 44 were waited for; matrix products, arithmetic and copies ran while one was open for 0% of the time, Pallas kernels for 13%

profile of v10, /device:TPU:13, one launch (start us, length us, event | category | flops | bytes accessed | tf_op | source)
XLA Modules:
  0.0 243.1 jit_solution(2394043984163813592)
XLA Ops:
  14.2 7.2 %collective-permute-done.1.refs_2_ = bf16[48,1664]{1,0:T(8,128)(2,1)S(1)} collective-permute-done((bf16[48,1664]{1,0:T(8,128)(2,1)S(1)}, bf16[48,1664]{1,0:T(8,128)(2,1)S(1)}, u32[]{:S(2)}, u32[]{:S(2)}) %collective-permute-start.1) | collective-permute-done | bytes 159776 | tf_op jit(solution)/shard_map/ppermute | solution.py:565
  21.4 3.9 %collective-permute-done.refs_1_ = bf16[48,1664]{1,0:T(8,128)(2,1)S(1)} collective-permute-done((bf16[48,1664]{1,0:T(8,128)(2,1)S(1)}, bf16[48,1664]{1,0:T(8,128)(2,1)S(1)}, u32[]{:S(2)}, u32[]{:S(2)}) %collective-permute-start) | collective-permute-done | bytes 159776 | tf_op jit(solution)/shard_map/ppermute | solution.py:565
  30.7 2.5 %collective-permute-start.10 = (bf16[48,1536]{1,0:T(8,128)(2,1)S(1)}, bf16[48,1536]{1,0:T(8,128)(2,1)S(1)}, u32[]{:S(2)}, u32[]{:S(2)}) collective-permute-start(bf16[48,1536]{1,0:T(8,128)(2,1)S(1)} %get-tuple-element.275.refs_0_), channel_id=1, source_target_pairs={{0,8},{1,9},{2,10},{3,11},{4,12},{5,13},{6,14},{7,15},{8,0},{9,1},... | collective-permute-start | bytes 442376 | tf_op jit(solution)/shard_map/ppermute | solution.py:565
  33.1 2.3 collective-permute-done.11.refs_3_
  35.5 5.6 %collective-permute-done.10.refs_2_ = bf16[48,1536]{1,0:T(8,128)(2,1)S(1)} collective-permute-done((bf16[48,1536]{1,0:T(8,128)(2,1)S(1)}, bf16[48,1536]{1,0:T(8,128)(2,1)S(1)}, u32[]{:S(2)}, u32[]{:S(2)}) %collective-permute-start.10) | collective-permute-done | bytes 147488 | tf_op jit(solution)/shard_map/ppermute | solution.py:565
  41.1 3.2 %collective-permute-done.9.refs_1_ = bf16[48,1536]{1,0:T(8,128)(2,1)S(1)} collective-permute-done((bf16[48,1536]{1,0:T(8,128)(2,1)S(1)}, bf16[48,1536]{1,0:T(8,128)(2,1)S(1)}, u32[]{:S(2)}, u32[]{:S(2)}) %collective-permute-start.9) | collective-permute-done | bytes 147488 | tf_op jit(solution)/shard_map/ppermute | solution.py:565
  48.3 2.5 %collective-permute-start.16 = (bf16[48,1536]{1,0:T(8,128)(2,1)S(1)}, bf16[48,1536]{1,0:T(8,128)(2,1)S(1)}, u32[]{:S(2)}, u32[]{:S(2)}) collective-permute-start(bf16[48,1536]{1,0:T(8,128)(2,1)S(1)} %get-tuple-element.286.refs_0_), channel_id=1, source_target_pairs={{0,8},{1,9},{2,10},{3,11},{4,12},{5,13},{6,14},{7,15},{8,0},{9,1},... | collective-permute-start | bytes 442376 | tf_op jit(solution)/shard_map/ppermute | solution.py:565
  52.4 6.4 %collective-permute-done.16.refs_2_ = bf16[48,1536]{1,0:T(8,128)(2,1)S(1)} collective-permute-done((bf16[48,1536]{1,0:T(8,128)(2,1)S(1)}, bf16[48,1536]{1,0:T(8,128)(2,1)S(1)}, u32[]{:S(2)}, u32[]{:S(2)}) %collective-permute-start.16) | collective-permute-done | bytes 147488 | tf_op jit(solution)/shard_map/ppermute | solution.py:565
  58.8 3.2 %collective-permute-done.15.refs_1_ = bf16[48,1536]{1,0:T(8,128)(2,1)S(1)} collective-permute-done((bf16[48,1536]{1,0:T(8,128)(2,1)S(1)}, bf16[48,1536]{1,0:T(8,128)(2,1)S(1)}, u32[]{:S(2)}, u32[]{:S(2)}) %collective-permute-start.15) | collective-permute-done | bytes 147488 | tf_op jit(solution)/shard_map/ppermute | solution.py:565
  66.7 3.9 %seg_qkv.1 = (bf16[16,48,1152]{2,1,0:T(8,128)(2,1)S(1)}, bf16[8,48,384]{2,1,0:T(8,128)(2,1)S(1)}, bf16[8,48,384]{2,1,0:T(8,128)(2,1)S(1)}, bf16[256,1152]{1,0:T(...) custom-call(s32[5]{0:T(128)S(1)} %stack.15.where, ...), custom_call_target="tpu_custom_call" | custom-call | flops 452984832 | bytes 11453440 | tf_op jit(solution)/shard_map/seg_qkv/pallas_call | solution.py:595
  70.6 4.0 %collective-permute-start.20 = (bf16[8,48,384]{2,1,0:T(8,128)(2,1)S(1)}, bf16[8,48,384]{2,1,0:T(8,128)(2,1)S(1)}, u32[]{:S(2)}, u32[]{:S(2)}) collective-permute-start(bf16[8,48,384]{2,1,0:T(8,128)(2,1)S(1)} %get-tuple-element.295.low), channel_id=1, source_target_pairs={{0,16},{16,0},{1,17},{17,1},{2,18},{18,2},{3,19},{19,3},{4,20},{20... | collective-permute-start | bytes 884744 | tf_op jit(solution)/shard_map/ppermute | solution.py:573
  77.0 3.1 %collective-permute-start.14 = (bf16[256,384]{1,0:T(8,128)(2,1)S(1)}, bf16[256,384]{1,0:T(8,128)(2,1)S(1)}, u32[]{:S(2)}, u32[]{:S(2)}) collective-permute-start(bf16[256,384]{1,0:T(8,128)(2,1)S(1)} %get-tuple-element.285.mixed), channel_id=1, source_target_pairs={{0,16},{16,0},{1,17},{17,1},{2,18},{18,2},{3,19},{19,3},{4,20},{20... | collective-permute-start | bytes 589832 | tf_op jit(solution)/shard_map/ppermute | solution.py:573
  83.2 3.3 %collective-permute-start.24 = (bf16[128,768]{1,0:T(8,128)(2,1)S(1)}, bf16[128,768]{1,0:T(8,128)(2,1)S(1)}, u32[]{:S(2)}, u32[]{:S(2)}) collective-permute-start(bf16[128,768]{1,0:T(8,128)(2,1)S(1)} %get-tuple-element.304.refs_12_.refs_0_.refs_6_), channel_id=1, source_target_pairs={{0,16},{16,0},{1,17},{17,1},{2,18},{18,2},{3,19},{19,3},{4,20},{20... | collective-permute-start | bytes 589832 | tf_op jit(solution)/shard_map/ppermute | solution.py:573
  92.6 3.0 %collective-permute-start.25 = (f32[128,768]{1,0:T(8,128)S(1)}, f32[128,768]{1,0:T(8,128)S(1)}, u32[]{:S(2)}, u32[]{:S(2)}) collective-permute-start(f32[128,768]{1,0:T(8,128)S(1)} %get-tuple-element.308), channel_id=1, source_target_pairs={{0,16},{16,0},{1,17},{17,1},{2,18},{18,2},{3,19},{19,3},{4,20},{20... | collective-permute-start | bytes 1179656 | tf_op jit(solution)/shard_map/ppermute | solution.py:573
  101.5 2.4 collective-permute-start.27
  105.6 2.9 %collective-permute-start.40 = (f32[4,1664]{1,0:T(4,128)S(1)}, f32[4,1664]{1,0:T(4,128)S(1)}, u32[]{:S(2)}, u32[]{:S(2)}) collective-permute-start(f32[4,1664]{1,0:T(4,128)S(1)} %pad_maximum_fusion.12.refs_0_), channel_id=1, source_target_pairs={{0,8},{1,9},{2,10},{3,11},{4,12},{5,13},{6,14},{7,15},{8,0},{9,1},... | collective-permute-start | bytes 79880 | tf_op jit(solution)/shard_map/ppermute | solution.py:565
  114.6 2.8 %collective-permute-start.42 = (bf16[16,48,1152]{2,1,0:T(8,128)(2,1)S(1)}, bf16[16,48,1152]{2,1,0:T(8,128)(2,1)S(1)}, u32[]{:S(2)}, u32[]{:S(2)}) collective-permute-start(bf16[16,48,1152]{2,1,0:T(8,128)(2,1)S(1)} %get-tuple-element.359.own), channel_id=1, source_target_pairs={{0,16},{16,0},{1,17},{17,1},{2,18},{18,2},{3,19},{19,3},{4,20},{20... | collective-permute-start | bytes 5308424 | tf_op jit(solution)/shard_map/ppermute | solution.py:573
  117.5 3.1 %seg_mlp_weight.1 = (bf16[2,48,3072]{2,1,0:T(8,128)(2,1)S(1)}, bf16[2,48,3072]{2,1,0:T(8,128)(2,1)S(1)}, bf16[4,48,3072]{2,1,0:T(8,128)(2,1)S(1)}, bf16[4,48,307...) custom-call(s32[5]{0:T(128)S(1)} %stack.15.where, bf16[128,768]{1,0:T(8,128)(2,1)S(1)} %get-tuple-element.304.refs_12_.refs_0_.refs_6_, ...), custom_call_target="tpu_custom_call" | custom-call | flops 1207959552 | bytes 7077888 | tf_op jit(solution)/shard_map/seg_mlp_weight/pallas_call | solution.py:595
  131.4 4.2 %collective-permute-done.47.refs_7_ = bf16[2,48,3072]{2,1,0:T(8,128)(2,1)S(1)} collective-permute-done((bf16[2,48,3072]{2,1,0:T(8,128)(2,1)S(1)}, bf16[2,48,3072]{2,1,0:T(8,128)(2,1)S(1)}, u32[]{:S(2)}, u32[]{:S(2)}) %collective-permute-start.47) | collective-permute-done | bytes 589856 | tf_op jit(solution)/shard_map/ppermute | solution.py:569
  141.4 2.4 collective-permute-start.49
  148.9 2.4 collective-permute-start.53
  167.8 3.1 %collective-permute-start.60 = (f32[1,768]{1,0:T(1,128)S(1)}, f32[1,768]{1,0:T(1,128)S(1)}, u32[]{:S(2)}, u32[]{:S(2)}) collective-permute-start(f32[1,768]{1,0:T(1,128)S(1)} %get-tuple-element.413.refs_0_.refs_3_), channel_id=1, source_target_pairs={{0,16},{16,0},{1,17},{17,1},{2,18},{18,2},{3,19},{19,3},{4,20},{20... | collective-permute-start | bytes 9224 | tf_op jit(solution)/shard_map/ppermute | solution.py:573
  177.3 4.4 %seg_attn_back.1 = (bf16[256,1152]{1,0:T(8,128)(2,1)S(1)}, f32[128,768]{1,0:T(8,128)S(1)}, f32[128,768]{1,0:T(8,128)S(1)}, bf16[24,768]{1,0:T(8,128)(2,1)S(1)}) custom-call(s32[5]{0:T(128)S(1)} %stack.15.where, bf16[256,1152]{1,0:T(8,128)(2,1)S(1)} %get-tuple-element.299.refs_0_, bf16[128,768]{1,0:T(8,128)(2,1)S(1)} %get-tuple-element.418.refs_1_, ...), custom_call_target="tpu_custom_call" | custom-call | flops 905969664 | bytes 4624384 | tf_op jit(solution)/shard_map/seg_attn_back/pallas_call | solution.py:595
  186.7 8.3 %collective-permute-done.66.refs_2_ = bf16[64,3072]{1,0:T(8,128)(2,1)S(1)} collective-permute-done((bf16[64,3072]{1,0:T(8,128)(2,1)S(1)}, bf16[64,3072]{1,0:T(8,128)(2,1)S(1)}, u32[]{:S(2)}, u32[]{:S(2)}) %collective-permute-start.66) | collective-permute-done | bytes 393248 | tf_op jit(solution)/shard_map/ppermute | solution.py:565
  197.7 2.6 %collective-permute-start.76 = (bf16[24,768]{1,0:T(8,128)(2,1)S(1)}, bf16[24,768]{1,0:T(8,128)(2,1)S(1)}, u32[]{:S(2)}, u32[]{:S(2)}) collective-permute-start(bf16[24,768]{1,0:T(8,128)(2,1)S(1)} %get-tuple-element.463), channel_id=1, source_target_pairs={{0,12},{1,13},{2,14},{3,15},{4,0},{5,1},{6,2},{7,3},{8,4},{9,5},{1... | collective-permute-start | bytes 110600 | tf_op jit(solution)/shard_map/ppermute | solution.py:565
  200.8 2.4 collective-permute-start.74
  212.6 4.0 %collective-permute-start.72 = (bf16[48,1536]{1,0:T(8,128)(2,1)S(1)}, bf16[48,1536]{1,0:T(8,128)(2,1)S(1)}, u32[]{:S(2)}, u32[]{:S(2)}) collective-permute-start(bf16[48,1536]{1,0:T(8,128)(2,1)S(1)} %get-tuple-element.459), channel_id=1, source_target_pairs={{0,8},{1,9},{2,10},{3,11},{4,12},{5,13},{6,14},{7,15},{8,0},{9,1},... | collective-permute-start | bytes 442376 | tf_op jit(solution)/shard_map/ppermute | solution.py:565
  221.4 3.7 %collective-permute-done.72 = bf16[48,1536]{1,0:T(8,128)(2,1)S(1)} collective-permute-done((bf16[48,1536]{1,0:T(8,128)(2,1)S(1)}, bf16[48,1536]{1,0:T(8,128)(2,1)S(1)}, u32[]{:S(2)}, u32[]{:S(2)}) %collective-permute-start.72) | collective-permute-done | bytes 147488 | tf_op jit(solution)/shard_map/ppermute | solution.py:565
  225.0 4.0 %collective-permute-start.81 = (bf16[16,12288]{1,0:T(8,128)(2,1)S(1)}, bf16[16,12288]{1,0:T(8,128)(2,1)S(1)}, u32[]{:S(2)}, u32[]{:S(2)}) collective-permute-start(bf16[16,12288]{1,0:T(8,128)(2,1)S(1)} %head_rows.1.refs_5_), channel_id=1, source_target_pairs={{0,16},{16,0},{1,17},{17,1},{2,18},{18,2},{3,19},{19,3},{4,20},{20... | collective-permute-start | bytes 1179656 | tf_op jit(solution)/shard_map/ppermute | solution.py:573
  230.4 4.4 %head_owner.1 = (f32[48,3072]{1,0:T(8,128)S(1)}, f32[16,768]{1,0:T(8,128)S(1)}, f32[48,9216]{1,0:T(8,128)}, f32[576]{0:T(1024)}, f32[16,768]{1,0:T(8,128)}, /*index=5*/f32[1,1]{1,0:T(1,128)}) custom-call(s32[5]{0:T(128)S(1)} %stack.15.where, bf16[96,768]{1,0:T(8,128)(2,1)S(1)} %pad_maximum_fusion.11.refs_0_, ...), custom_call_target="tpu_custom_call" | custom-call | flops 28311552 | bytes 4503812 | tf_op jit(solution)/shard_map/head_owner/pallas_call | solution.py:595
  234.8 2.7 %collective-permute-start.83 = (f32[48,3072]{1,0:T(8,128)S(1)}, f32[48,3072]{1,0:T(8,128)S(1)}, u32[]{:S(2)}, u32[]{:S(2)}) collective-permute-start(f32[48,3072]{1,0:T(8,128)S(1)} %get-tuple-element.484.mlp), channel_id=1, source_target_pairs={{0,16},{16,0},{1,17},{17,1},{2,18},{18,2},{3,19},{19,3},{4,20},{20... | collective-permute-start | bytes 1769480 | tf_op jit(solution)/shard_map/ppermute | solution.py:573
  239.6 3.3 %seg_owner.1 = (f32[48,9216]{1,0:T(8,128)}, f32[576]{0:T(1024)}) custom-call(s32[5]{0:T(128)S(1)} %stack.15.where, f32[48,1536]{1,0:T(8,128)S(1)} %convert_add_fusion.1.attn, f32[48,1536]{1,0:T(8,128)S(1)} %collective-permute-done.82.attn_got, f32[48,3072]{1,0:T(8,128)S(1)} %get-tuple-element.484.mlp, f32[48,3072]{1,0:T(8,128)S(1)} %collective-permute-done.83.mlp_got, ...), custom_call_target="tpu_custom_call" | custom-call | bytes 3639552 | tf_op jit(solution)/shard_map/seg_owner/pallas_call | solution.py:595
  (212 shorter events, 124.0 us)
Async XLA Ops:
  8.0 17.3 %collective-permute-start.3 = (bf16[48,4736]{1,0:T(8,128)(2,1)S(1)}, bf16[48,4736]{1,0:T(8,128)(2,1)S(1)}, u32[]{:S(2)}, u32[]{:S(2)}) collective-permute-start(bf16[48,4736]{1,0:T(8,128)(2,1)S(1)} %pad_maximum_fusion.10), channel_id=1, source_target_pairs={{0,1},{1,0},{2,3},{3,2},{4,5},{5,4},{6,7},{7,6},{8,9},{9,8},{10,11... | collective-permute-start | bytes 1363976 | tf_op jit(solution)/shard_map/ppermute | solution.py:569
  9.3 16.0 %collective-permute-start.4 = (bf16[48,4736]{1,0:T(8,128)(2,1)S(1)}, bf16[48,4736]{1,0:T(8,128)(2,1)S(1)}, u32[]{:S(2)}, u32[]{:S(2)}) collective-permute-start(bf16[48,4736]{1,0:T(8,128)(2,1)S(1)} %pad_maximum_fusion.10), channel_id=1, source_target_pairs={{0,2},{1,3},{2,0},{3,1},{4,6},{5,7},{6,4},{7,5},{8,10},{9,11},{10,... | collective-permute-start | bytes 1363976 | tf_op jit(solution)/shard_map/ppermute | solution.py:569
  9.7 11.7 %collective-permute-start.1 = (bf16[48,1664]{1,0:T(8,128)(2,1)S(1)}, bf16[48,1664]{1,0:T(8,128)(2,1)S(1)}, u32[]{:S(2)}, u32[]{:S(2)}) collective-permute-start(bf16[48,1664]{1,0:T(8,128)(2,1)S(1)} %get-tuple-element.254.refs_0_), channel_id=1, source_target_pairs={{0,8},{1,9},{2,10},{3,11},{4,12},{5,13},{6,14},{7,15},{8,0},{9,1},... | collective-permute-start | bytes 479240 | tf_op jit(solution)/shard_map/ppermute | solution.py:565
  12.0 13.3 %collective-permute-start = (bf16[48,1664]{1,0:T(8,128)(2,1)S(1)}, bf16[48,1664]{1,0:T(8,128)(2,1)S(1)}, u32[]{:S(2)}, u32[]{:S(2)}) collective-permute-start(bf16[48,1664]{1,0:T(8,128)(2,1)S(1)} %get-tuple-element.254.refs_0_), channel_id=1, source_target_pairs={{0,4},{1,5},{2,6},{3,7},{4,8},{5,9},{6,10},{7,11},{8,12},{9,13},{1... | collective-permute-start | bytes 479240 | tf_op jit(solution)/shard_map/ppermute | solution.py:565
  28.2 18.1 %collective-permute-start.8 = (bf16[48,7424]{1,0:T(8,128)(2,1)S(1)}, bf16[48,7424]{1,0:T(8,128)(2,1)S(1)}, u32[]{:S(2)}, u32[]{:S(2)}) collective-permute-start(bf16[48,7424]{1,0:T(8,128)(2,1)S(1)} %pad_maximum_fusion.6), channel_id=1, source_target_pairs={{0,2},{1,3},{2,0},{3,1},{4,6},{5,7},{6,4},{7,5},{8,10},{9,11},{10,... | collective-permute-start | bytes 2138120 | tf_op jit(solution)/shard_map/ppermute | solution.py:569
  29.5 16.8 %collective-permute-start.7 = (bf16[48,7296]{1,0:T(8,128)(2,1)S(1)}, bf16[48,7296]{1,0:T(8,128)(2,1)S(1)}, u32[]{:S(2)}, u32[]{:S(2)}) collective-permute-start(bf16[48,7296]{1,0:T(8,128)(2,1)S(1)} %pad_maximum_fusion.7), channel_id=1, source_target_pairs={{0,1},{1,0},{2,3},{3,2},{4,5},{5,4},{6,7},{7,6},{8,9},{9,8},{10,11... | collective-permute-start | bytes 2101256 | tf_op jit(solution)/shard_map/ppermute | solution.py:569
  33.1 11.1 %collective-permute-start.9 = (bf16[48,1536]{1,0:T(8,128)(2,1)S(1)}, bf16[48,1536]{1,0:T(8,128)(2,1)S(1)}, u32[]{:S(2)}, u32[]{:S(2)}) collective-permute-start(bf16[48,1536]{1,0:T(8,128)(2,1)S(1)} %get-tuple-element.275.refs_0_), channel_id=1, source_target_pairs={{0,4},{1,5},{2,6},{3,7},{4,8},{5,9},{6,10},{7,11},{8,12},{9,13},{1... | collective-permute-start | bytes 442376 | tf_op jit(solution)/shard_map/ppermute | solution.py:565
  46.5 16.1 %collective-permute-start.13 = (bf16[48,7168]{1,0:T(8,128)(2,1)S(1)}, bf16[48,7168]{1,0:T(8,128)(2,1)S(1)}, u32[]{:S(2)}, u32[]{:S(2)}) collective-permute-start(bf16[48,7168]{1,0:T(8,128)(2,1)S(1)} %pad_maximum_fusion.8), channel_id=1, source_target_pairs={{0,2},{1,3},{2,0},{3,1},{4,6},{5,7},{6,4},{7,5},{8,10},{9,11},{10,... | collective-permute-start | bytes 2064392 | tf_op jit(solution)/shard_map/ppermute | solution.py:569
  47.1 15.4 %collective-permute-start.12 = (bf16[48,7040]{1,0:T(8,128)(2,1)S(1)}, bf16[48,7040]{1,0:T(8,128)(2,1)S(1)}, u32[]{:S(2)}, u32[]{:S(2)}) collective-permute-start(bf16[48,7040]{1,0:T(8,128)(2,1)S(1)} %pad_maximum_fusion.9), channel_id=1, source_target_pairs={{0,1},{1,0},{2,3},{3,2},{4,5},{5,4},{6,7},{7,6},{8,9},{9,8},{10,11... | collective-permute-start | bytes 2027528 | tf_op jit(solution)/shard_map/ppermute | solution.py:569
  50.8 11.2 %collective-permute-start.15 = (bf16[48,1536]{1,0:T(8,128)(2,1)S(1)}, bf16[48,1536]{1,0:T(8,128)(2,1)S(1)}, u32[]{:S(2)}, u32[]{:S(2)}) collective-permute-start(bf16[48,1536]{1,0:T(8,128)(2,1)S(1)} %get-tuple-element.286.refs_0_), channel_id=1, source_target_pairs={{0,4},{1,5},{2,6},{3,7},{4,8},{5,9},{6,10},{7,11},{8,12},{9,13},{1... | collective-permute-start | bytes 442376 | tf_op jit(solution)/shard_map/ppermute | solution.py:565
  62.7 14.3 %collective-permute-start.18 = (bf16[48,6912]{1,0:T(8,128)(2,1)S(1)}, bf16[48,6912]{1,0:T(8,128)(2,1)S(1)}, u32[]{:S(2)}, u32[]{:S(2)}) collective-permute-start(bf16[48,6912]{1,0:T(8,128)(2,1)S(1)} %get-tuple-element.290), channel_id=1, source_target_pairs={{0,1},{1,0},{2,3},{3,2},{4,5},{5,4},{6,7},{7,6},{8,9},{9,8},{10,11... | collective-permute-start | bytes 1990664 | tf_op jit(solution)/shard_map/ppermute | solution.py:569
  63.4 11.2 %collective-permute-start.32 = (bf16[48,1152]{1,0:T(8,128)(2,1)S(1)}, bf16[48,1152]{1,0:T(8,128)(2,1)S(1)}, u32[]{:S(2)}, u32[]{:S(2)}) collective-permute-start(bf16[48,1152]{1,0:T(8,128)(2,1)S(1)} %get-tuple-element.329), channel_id=1, source_target_pairs={{0,4},{1,5},{2,6},{3,7},{4,8},{5,9},{6,10},{7,11},{8,12},{9,13},{1... | collective-permute-start | bytes 331784 | tf_op jit(solution)/shard_map/ppermute | solution.py:565
  65.6 14.5 %collective-permute-start.19 = (bf16[48,6912]{1,0:T(8,128)(2,1)S(1)}, bf16[48,6912]{1,0:T(8,128)(2,1)S(1)}, u32[]{:S(2)}, u32[]{:S(2)}) collective-permute-start(bf16[48,6912]{1,0:T(8,128)(2,1)S(1)} %get-tuple-element.291), channel_id=1, source_target_pairs={{0,2},{1,3},{2,0},{3,1},{4,6},{5,7},{6,4},{7,5},{8,10},{9,11},{10,... | collective-permute-start | bytes 1990664 | tf_op jit(solution)/shard_map/ppermute | solution.py:569
  70.6 11.2 %collective-permute-start.20 = (bf16[8,48,384]{2,1,0:T(8,128)(2,1)S(1)}, bf16[8,48,384]{2,1,0:T(8,128)(2,1)S(1)}, u32[]{:S(2)}, u32[]{:S(2)}) collective-permute-start(bf16[8,48,384]{2,1,0:T(8,128)(2,1)S(1)} %get-tuple-element.295.low), channel_id=1, source_target_pairs={{0,16},{16,0},{1,17},{17,1},{2,18},{18,2},{3,19},{19,3},{4,20},{20... | collective-permute-start | bytes 884744 | tf_op jit(solution)/shard_map/ppermute | solution.py:573
  74.7 11.8 %collective-permute-start.34 = (bf16[48,1152]{1,0:T(8,128)(2,1)S(1)}, bf16[48,1152]{1,0:T(8,128)(2,1)S(1)}, u32[]{:S(2)}, u32[]{:S(2)}) collective-permute-start(bf16[48,1152]{1,0:T(8,128)(2,1)S(1)} %get-tuple-element.333), channel_id=1, source_target_pairs={{0,12},{1,13},{2,14},{3,15},{4,0},{5,1},{6,2},{7,3},{8,4},{9,5},{1... | collective-permute-start | bytes 331784 | tf_op jit(solution)/shard_map/ppermute | solution.py:565
  89.5 14.4 %collective-permute-start.35 = (bf16[48,4992]{1,0:T(8,128)(2,1)S(1)}, bf16[48,4992]{1,0:T(8,128)(2,1)S(1)}, u32[]{:S(2)}, u32[]{:S(2)}) collective-permute-start(bf16[48,4992]{1,0:T(8,128)(2,1)S(1)} %constant_dynamic-update-slice_fusion), channel_id=1, source_target_pairs={{0,1},{1,0},{2,3},{3,2},{4,5},{5,4},{6,7},{7,6},{8,9},{9,8},{10,11... | collective-permute-start | bytes 1437704 | tf_op jit(solution)/shard_map/ppermute | solution.py:569
  90.5 13.5 %collective-permute-start.36 = (bf16[48,4992]{1,0:T(8,128)(2,1)S(1)}, bf16[48,4992]{1,0:T(8,128)(2,1)S(1)}, u32[]{:S(2)}, u32[]{:S(2)}) collective-permute-start(bf16[48,4992]{1,0:T(8,128)(2,1)S(1)} %constant_dynamic-update-slice_fusion), channel_id=1, source_target_pairs={{0,2},{1,3},{2,0},{3,1},{4,6},{5,7},{6,4},{7,5},{8,10},{9,11},{10,... | collective-permute-start | bytes 1437704 | tf_op jit(solution)/shard_map/ppermute | solution.py:569
  120.6 15.0 %collective-permute-start.47 = (bf16[2,48,3072]{2,1,0:T(8,128)(2,1)S(1)}, bf16[2,48,3072]{2,1,0:T(8,128)(2,1)S(1)}, u32[]{:S(2)}, u32[]{:S(2)}) collective-permute-start(bf16[2,48,3072]{2,1,0:T(8,128)(2,1)S(1)} %get-tuple-element.374), channel_id=1, source_target_pairs={{0,2},{1,3},{2,0},{3,1},{4,6},{5,7},{6,4},{7,5},{8,10},{9,11},{10,... | collective-permute-start | bytes 1769480 | tf_op jit(solution)/shard_map/ppermute | solution.py:569
  121.6 14.6 %collective-permute-start.48 = (bf16[2,48,3072]{2,1,0:T(8,128)(2,1)S(1)}, bf16[2,48,3072]{2,1,0:T(8,128)(2,1)S(1)}, u32[]{:S(2)}, u32[]{:S(2)}) collective-permute-start(bf16[2,48,3072]{2,1,0:T(8,128)(2,1)S(1)} %get-tuple-element.376), channel_id=1, source_target_pairs={{0,1},{1,0},{2,3},{3,2},{4,5},{5,4},{6,7},{7,6},{8,9},{9,8},{10,11... | collective-permute-start | bytes 1769480 | tf_op jit(solution)/shard_map/ppermute | solution.py:569
  137.6 26.4 %collective-permute-start.58 = (bf16[4,48,3072]{2,1,0:T(8,128)(2,1)S(1)}, bf16[4,48,3072]{2,1,0:T(8,128)(2,1)S(1)}, u32[]{:S(2)}, u32[]{:S(2)}) collective-permute-start(bf16[4,48,3072]{2,1,0:T(8,128)(2,1)S(1)} %get-tuple-element.405), channel_id=1, source_target_pairs={{0,1},{1,0},{2,3},{3,2},{4,5},{5,4},{6,7},{7,6},{8,9},{9,8},{10,11... | collective-permute-start | bytes 3538952 | tf_op jit(solution)/shard_map/ppermute | solution.py:569
  138.4 26.1 %collective-permute-start.59 = (bf16[4,48,3072]{2,1,0:T(8,128)(2,1)S(1)}, bf16[4,48,3072]{2,1,0:T(8,128)(2,1)S(1)}, u32[]{:S(2)}, u32[]{:S(2)}) collective-permute-start(bf16[4,48,3072]{2,1,0:T(8,128)(2,1)S(1)} %get-tuple-element.406), channel_id=1, source_target_pairs={{0,2},{1,3},{2,0},{3,1},{4,6},{5,7},{6,4},{7,5},{8,10},{9,11},{10,... | collective-permute-start | bytes 3538952 | tf_op jit(solution)/shard_map/ppermute | solution.py:569
  166.0 17.2 %collective-permute-start.63 = (bf16[64,3072]{1,0:T(8,128)(2,1)S(1)}, bf16[64,3072]{1,0:T(8,128)(2,1)S(1)}, u32[]{:S(2)}, u32[]{:S(2)}) collective-permute-start(bf16[64,3072]{1,0:T(8,128)(2,1)S(1)} %get-tuple-element.432), channel_id=1, source_target_pairs={{0,12},{1,13},{2,14},{3,15},{4,0},{5,1},{6,2},{7,3},{8,4},{9,5},{1... | collective-permute-start | bytes 1179656 | tf_op jit(solution)/shard_map/ppermute | solution.py:565
  176.2 18.8 %collective-permute-start.66 = (bf16[64,3072]{1,0:T(8,128)(2,1)S(1)}, bf16[64,3072]{1,0:T(8,128)(2,1)S(1)}, u32[]{:S(2)}, u32[]{:S(2)}) collective-permute-start(bf16[64,3072]{1,0:T(8,128)(2,1)S(1)} %get-tuple-element.441), channel_id=1, source_target_pairs={{0,8},{1,9},{2,10},{3,11},{4,12},{5,13},{6,14},{7,15},{8,0},{9,1},... | collective-permute-start | bytes 1179656 | tf_op jit(solution)/shard_map/ppermute | solution.py:565
  181.7 13.3 %collective-permute-start.67 = (f32[128,768]{1,0:T(8,128)S(1)}, f32[128,768]{1,0:T(8,128)S(1)}, u32[]{:S(2)}, u32[]{:S(2)}) collective-permute-start(f32[128,768]{1,0:T(8,128)S(1)} %get-tuple-element.444), channel_id=1, source_target_pairs={{0,16},{16,0},{1,17},{17,1},{2,18},{18,2},{3,19},{19,3},{4,20},{20... | collective-permute-start | bytes 1179656 | tf_op jit(solution)/shard_map/ppermute | solution.py:573
  183.1 11.8 %collective-permute-start.65 = (bf16[2,48,1536]{2,1,0:T(8,128)(2,1)S(1)}, bf16[2,48,1536]{2,1,0:T(8,128)(2,1)S(1)}, u32[]{:S(2)}, u32[]{:S(2)}) collective-permute-start(bf16[2,48,1536]{2,1,0:T(8,128)(2,1)S(1)} %get-tuple-element.435), channel_id=1, source_target_pairs={{0,1},{1,0},{2,3},{3,2},{4,5},{5,4},{6,7},{7,6},{8,9},{9,8},{10,11... | collective-permute-start | bytes 884744 | tf_op jit(solution)/shard_map/ppermute | solution.py:569
  183.6 11.3 %collective-permute-start.64 = (bf16[2,48,1536]{2,1,0:T(8,128)(2,1)S(1)}, bf16[2,48,1536]{2,1,0:T(8,128)(2,1)S(1)}, u32[]{:S(2)}, u32[]{:S(2)}) collective-permute-start(bf16[2,48,1536]{2,1,0:T(8,128)(2,1)S(1)} %get-tuple-element.433), channel_id=1, source_target_pairs={{0,2},{1,3},{2,0},{3,1},{4,6},{5,7},{6,4},{7,5},{8,10},{9,11},{10,... | collective-permute-start | bytes 884744 | tf_op jit(solution)/shard_map/ppermute | solution.py:569
  196.4 14.4 %collective-permute-start.68 = (bf16[4,48,1536]{2,1,0:T(8,128)(2,1)S(1)}, bf16[4,48,1536]{2,1,0:T(8,128)(2,1)S(1)}, u32[]{:S(2)}, u32[]{:S(2)}) collective-permute-start(bf16[4,48,1536]{2,1,0:T(8,128)(2,1)S(1)} %get-tuple-element.449), channel_id=1, source_target_pairs={{0,1},{1,0},{2,3},{3,2},{4,5},{5,4},{6,7},{7,6},{8,9},{9,8},{10,11... | collective-permute-start | bytes 1769480 | tf_op jit(solution)/shard_map/ppermute | solution.py:569
  197.0 14.1 %collective-permute-start.69 = (bf16[4,48,1536]{2,1,0:T(8,128)(2,1)S(1)}, bf16[4,48,1536]{2,1,0:T(8,128)(2,1)S(1)}, u32[]{:S(2)}, u32[]{:S(2)}) collective-permute-start(bf16[4,48,1536]{2,1,0:T(8,128)(2,1)S(1)} %get-tuple-element.450), channel_id=1, source_target_pairs={{0,2},{1,3},{2,0},{3,1},{4,6},{5,7},{6,4},{7,5},{8,10},{9,11},{10,... | collective-permute-start | bytes 1769480 | tf_op jit(solution)/shard_map/ppermute | solution.py:569
  204.9 14.0 %collective-permute-start.80 = (bf16[64,3072]{1,0:T(8,128)(2,1)S(1)}, bf16[64,3072]{1,0:T(8,128)(2,1)S(1)}, u32[]{:S(2)}, u32[]{:S(2)}) collective-permute-start(bf16[64,3072]{1,0:T(8,128)(2,1)S(1)} %get-tuple-element.477), channel_id=1, source_target_pairs={{0,4},{1,5},{2,6},{3,7},{4,8},{5,9},{6,10},{7,11},{8,12},{9,13},{1... | collective-permute-start | bytes 1179656 | tf_op jit(solution)/shard_map/ppermute | solution.py:565
  212.6 12.5 %collective-permute-start.72 = (bf16[48,1536]{1,0:T(8,128)(2,1)S(1)}, bf16[48,1536]{1,0:T(8,128)(2,1)S(1)}, u32[]{:S(2)}, u32[]{:S(2)}) collective-permute-start(bf16[48,1536]{1,0:T(8,128)(2,1)S(1)} %get-tuple-element.459), channel_id=1, source_target_pairs={{0,8},{1,9},{2,10},{3,11},{4,12},{5,13},{6,14},{7,15},{8,0},{9,1},... | collective-permute-start | bytes 442376 | tf_op jit(solution)/shard_map/ppermute | solution.py:565
  216.6 12.6 %collective-permute-start.79 = (bf16[96,768]{1,0:T(8,128)(2,1)S(1)}, bf16[96,768]{1,0:T(8,128)(2,1)S(1)}, u32[]{:S(2)}, u32[]{:S(2)}) collective-permute-start(bf16[96,768]{1,0:T(8,128)(2,1)S(1)} %pad_maximum_fusion.11.refs_0_), channel_id=1, source_target_pairs={{0,3},{1,2},{2,1},{3,0},{4,7},{5,6},{6,5},{7,4},{8,11},{9,10},{10,... | collective-permute-start | bytes 442376 | tf_op jit(solution)/shard_map/ppermute | solution.py:569
  218.0 11.3 %collective-permute-start.78 = (bf16[96,768]{1,0:T(8,128)(2,1)S(1)}, bf16[96,768]{1,0:T(8,128)(2,1)S(1)}, u32[]{:S(2)}, u32[]{:S(2)}) collective-permute-start(bf16[96,768]{1,0:T(8,128)(2,1)S(1)} %pad_maximum_fusion.11.refs_0_), channel_id=1, source_target_pairs={{0,2},{1,3},{2,0},{3,1},{4,6},{5,7},{6,4},{7,5},{8,10},{9,11},{10,... | collective-permute-start | bytes 442376 | tf_op jit(solution)/shard_map/ppermute | solution.py:569
  (61 other events, 315.2 us)

commit v11 on v10

--- a/solution.py
+++ b/solution.py
@@ -2050,8 +2050,8 @@
         + (after(grad_summed, got_two), input_own, other_core(input_send)),
     )
     attn_plane = sent_both(*attn_sent)
-    payload_parts = line_parts(after(payload, *attn_sent))
-    mlp_got[0] = along_line(after(mlp_last, *payload_parts[1:]), 1)
+    mlp_got[0] = along_line(after(mlp_last, *attn_sent), 1)
+    payload_parts = line_parts(after(payload, mlp_got[0]))
     mlp_got = [after(got, attn_plane[0]) for got in mlp_got]
     mlp_sum = reduce_line(mlp_own, mlp_got)
     shared = shared + other_core(after(shared, attn_sent[0]))

time: 244 us -> 243 us (level)
  starting transfers between devices: 106 us -> 98.8 us
  waiting for transfers between devices: 80.5 us -> 86.7 us
    ppermute x36, waiting for transfers between devices: 56.7 us -> 66.2 us  [along_line(): return lax.ppermute(value, 'fsdp', line_pairs(apart))]
    ppermute x36, starting transfers between devices: 51.1 us -> 46.3 us  [along_line(): return lax.ppermute(value, 'fsdp', line_pairs(apart))]
    ppermute x21, starting transfers between devices: 34.3 us -> 31.5 us  [other_core(): return lax.ppermute(value, 'rep', [(0, 1), (1, 0)])]
  transfers between devices with their start and end apart: 85 -> 85, of which waited for: 44 -> 39; matrix products, arithmetic and copies ran while one was open for 0% -> 0% of each run, Pallas kernels for 13% -> 13%
where the time goes in v11:
time: 243 us; the launch traced here: 242 us
  starting transfers between devices  98.8 us (41%)
  waiting for transfers between devices  86.7 us (36%)
  Pallas kernels  48.2 us (20%)
  local copies, waits for them, and re-layouts  5.34 us (2%)
    ppermute x36, waiting for transfers between devices, along_line(): return lax.ppermute(value, 'fsdp', line_pairs(apart))  66.2 us
    pallas_call x26, Pallas kernels, run_kernel(): pl.pallas_call(body, name=name, out_shape=tuple(outs), in_specs=in_specs,...  48.2 us
    ppermute x36, starting transfers between devices, along_line(): return lax.ppermute(value, 'fsdp', line_pairs(apart))  46.3 us
    ppermute x21, starting transfers between devices, other_core(): return lax.ppermute(value, 'rep', [(0, 1), (1, 0)])  31.5 us
    ppermute x28, starting transfers between devices, in_plane(): return lax.ppermute(value, 'fsdp', plane_pairs(mask))  21.1 us
    ppermute x28, waiting for transfers between devices, in_plane(): return lax.ppermute(value, 'fsdp', plane_pairs(mask))  11.6 us
    ppermute x21, waiting for transfers between devices, other_core(): return lax.ppermute(value, 'rep', [(0, 1), (1, 0)])  8.95 us
  transfers between devices with their start and end apart: 85, of which 39 were waited for; matrix products, arithmetic and copies ran while one was open for 0% of the time, Pallas kernels for 13%

profile of v11, /device:TPU:13, one launch (start us, length us, event | category | flops | bytes accessed | tf_op | source)
XLA Modules:
  0.0 241.7 jit_solution(11329122163351044157)
XLA Ops:
  14.2 7.2 %collective-permute-done.1.refs_2_ = bf16[48,1664]{1,0:T(8,128)(2,1)S(1)} collective-permute-done((bf16[48,1664]{1,0:T(8,128)(2,1)S(1)}, bf16[48,1664]{1,0:T(8,128)(2,1)S(1)}, u32[]{:S(2)}, u32[]{:S(2)}) %collective-permute-start.1) | collective-permute-done | bytes 159776 | tf_op jit(solution)/shard_map/ppermute | solution.py:565
  21.4 3.9 %collective-permute-done.refs_1_ = bf16[48,1664]{1,0:T(8,128)(2,1)S(1)} collective-permute-done((bf16[48,1664]{1,0:T(8,128)(2,1)S(1)}, bf16[48,1664]{1,0:T(8,128)(2,1)S(1)}, u32[]{:S(2)}, u32[]{:S(2)}) %collective-permute-start) | collective-permute-done | bytes 159776 | tf_op jit(solution)/shard_map/ppermute | solution.py:565
  30.7 2.5 %collective-permute-start.10 = (bf16[48,1536]{1,0:T(8,128)(2,1)S(1)}, bf16[48,1536]{1,0:T(8,128)(2,1)S(1)}, u32[]{:S(2)}, u32[]{:S(2)}) collective-permute-start(bf16[48,1536]{1,0:T(8,128)(2,1)S(1)} %get-tuple-element.275.refs_0_), channel_id=1, source_target_pairs={{0,8},{1,9},{2,10},{3,11},{4,12},{5,13},{6,14},{7,15},{8,0},{9,1},... | collective-permute-start | bytes 442376 | tf_op jit(solution)/shard_map/ppermute | solution.py:565
  33.1 2.3 collective-permute-done.11.refs_3_
  35.5 5.6 %collective-permute-done.10.refs_2_ = bf16[48,1536]{1,0:T(8,128)(2,1)S(1)} collective-permute-done((bf16[48,1536]{1,0:T(8,128)(2,1)S(1)}, bf16[48,1536]{1,0:T(8,128)(2,1)S(1)}, u32[]{:S(2)}, u32[]{:S(2)}) %collective-permute-start.10) | collective-permute-done | bytes 147488 | tf_op jit(solution)/shard_map/ppermute | solution.py:565
  41.1 3.2 %collective-permute-done.9.refs_1_ = bf16[48,1536]{1,0:T(8,128)(2,1)S(1)} collective-permute-done((bf16[48,1536]{1,0:T(8,128)(2,1)S(1)}, bf16[48,1536]{1,0:T(8,128)(2,1)S(1)}, u32[]{:S(2)}, u32[]{:S(2)}) %collective-permute-start.9) | collective-permute-done | bytes 147488 | tf_op jit(solution)/shard_map/ppermute | solution.py:565
  48.3 2.5 %collective-permute-start.16 = (bf16[48,1536]{1,0:T(8,128)(2,1)S(1)}, bf16[48,1536]{1,0:T(8,128)(2,1)S(1)}, u32[]{:S(2)}, u32[]{:S(2)}) collective-permute-start(bf16[48,1536]{1,0:T(8,128)(2,1)S(1)} %get-tuple-element.286.refs_0_), channel_id=1, source_target_pairs={{0,8},{1,9},{2,10},{3,11},{4,12},{5,13},{6,14},{7,15},{8,0},{9,1},... | collective-permute-start | bytes 442376 | tf_op jit(solution)/shard_map/ppermute | solution.py:565
  52.4 6.4 %collective-permute-done.16.refs_2_ = bf16[48,1536]{1,0:T(8,128)(2,1)S(1)} collective-permute-done((bf16[48,1536]{1,0:T(8,128)(2,1)S(1)}, bf16[48,1536]{1,0:T(8,128)(2,1)S(1)}, u32[]{:S(2)}, u32[]{:S(2)}) %collective-permute-start.16) | collective-permute-done | bytes 147488 | tf_op jit(solution)/shard_map/ppermute | solution.py:565
  58.8 3.2 %collective-permute-done.15.refs_1_ = bf16[48,1536]{1,0:T(8,128)(2,1)S(1)} collective-permute-done((bf16[48,1536]{1,0:T(8,128)(2,1)S(1)}, bf16[48,1536]{1,0:T(8,128)(2,1)S(1)}, u32[]{:S(2)}, u32[]{:S(2)}) %collective-permute-start.15) | collective-permute-done | bytes 147488 | tf_op jit(solution)/shard_map/ppermute | solution.py:565
  66.7 3.9 %seg_qkv.1 = (bf16[16,48,1152]{2,1,0:T(8,128)(2,1)S(1)}, bf16[8,48,384]{2,1,0:T(8,128)(2,1)S(1)}, bf16[8,48,384]{2,1,0:T(8,128)(2,1)S(1)}, bf16[256,1152]{1,0:T(...) custom-call(s32[5]{0:T(128)S(1)} %stack.15.where, ...), custom_call_target="tpu_custom_call" | custom-call | flops 452984832 | bytes 11453440 | tf_op jit(solution)/shard_map/seg_qkv/pallas_call | solution.py:595
  70.6 4.0 %collective-permute-start.20 = (bf16[8,48,384]{2,1,0:T(8,128)(2,1)S(1)}, bf16[8,48,384]{2,1,0:T(8,128)(2,1)S(1)}, u32[]{:S(2)}, u32[]{:S(2)}) collective-permute-start(bf16[8,48,384]{2,1,0:T(8,128)(2,1)S(1)} %get-tuple-element.295.low), channel_id=1, source_target_pairs={{0,16},{16,0},{1,17},{17,1},{2,18},{18,2},{3,19},{19,3},{4,20},{20... | collective-permute-start | bytes 884744 | tf_op jit(solution)/shard_map/ppermute | solution.py:573
  77.0 3.1 %collective-permute-start.14 = (bf16[256,384]{1,0:T(8,128)(2,1)S(1)}, bf16[256,384]{1,0:T(8,128)(2,1)S(1)}, u32[]{:S(2)}, u32[]{:S(2)}) collective-permute-start(bf16[256,384]{1,0:T(8,128)(2,1)S(1)} %get-tuple-element.285.mixed), channel_id=1, source_target_pairs={{0,16},{16,0},{1,17},{17,1},{2,18},{18,2},{3,19},{19,3},{4,20},{20... | collective-permute-start | bytes 589832 | tf_op jit(solution)/shard_map/ppermute | solution.py:573
  83.2 3.3 %collective-permute-start.24 = (bf16[128,768]{1,0:T(8,128)(2,1)S(1)}, bf16[128,768]{1,0:T(8,128)(2,1)S(1)}, u32[]{:S(2)}, u32[]{:S(2)}) collective-permute-start(bf16[128,768]{1,0:T(8,128)(2,1)S(1)} %get-tuple-element.304.refs_12_.refs_0_.refs_6_), channel_id=1, source_target_pairs={{0,16},{16,0},{1,17},{17,1},{2,18},{18,2},{3,19},{19,3},{4,20},{20... | collective-permute-start | bytes 589832 | tf_op jit(solution)/shard_map/ppermute | solution.py:573
  92.6 3.0 %collective-permute-start.25 = (f32[128,768]{1,0:T(8,128)S(1)}, f32[128,768]{1,0:T(8,128)S(1)}, u32[]{:S(2)}, u32[]{:S(2)}) collective-permute-start(f32[128,768]{1,0:T(8,128)S(1)} %get-tuple-element.308), channel_id=1, source_target_pairs={{0,16},{16,0},{1,17},{17,1},{2,18},{18,2},{3,19},{19,3},{4,20},{20... | collective-permute-start | bytes 1179656 | tf_op jit(solution)/shard_map/ppermute | solution.py:573
  101.5 2.4 collective-permute-start.27
  105.6 2.9 %collective-permute-start.40 = (f32[4,1664]{1,0:T(4,128)S(1)}, f32[4,1664]{1,0:T(4,128)S(1)}, u32[]{:S(2)}, u32[]{:S(2)}) collective-permute-start(f32[4,1664]{1,0:T(4,128)S(1)} %pad_maximum_fusion.12.refs_0_), channel_id=1, source_target_pairs={{0,8},{1,9},{2,10},{3,11},{4,12},{5,13},{6,14},{7,15},{8,0},{9,1},... | collective-permute-start | bytes 79880 | tf_op jit(solution)/shard_map/ppermute | solution.py:565
  114.6 2.8 %collective-permute-start.42 = (bf16[16,48,1152]{2,1,0:T(8,128)(2,1)S(1)}, bf16[16,48,1152]{2,1,0:T(8,128)(2,1)S(1)}, u32[]{:S(2)}, u32[]{:S(2)}) collective-permute-start(bf16[16,48,1152]{2,1,0:T(8,128)(2,1)S(1)} %get-tuple-element.359.own), channel_id=1, source_target_pairs={{0,16},{16,0},{1,17},{17,1},{2,18},{18,2},{3,19},{19,3},{4,20},{20... | collective-permute-start | bytes 5308424 | tf_op jit(solution)/shard_map/ppermute | solution.py:573
  117.5 3.1 %seg_mlp_weight.1 = (bf16[2,48,3072]{2,1,0:T(8,128)(2,1)S(1)}, bf16[2,48,3072]{2,1,0:T(8,128)(2,1)S(1)}, bf16[4,48,3072]{2,1,0:T(8,128)(2,1)S(1)}, bf16[4,48,307...) custom-call(s32[5]{0:T(128)S(1)} %stack.15.where, bf16[128,768]{1,0:T(8,128)(2,1)S(1)} %get-tuple-element.304.refs_12_.refs_0_.refs_6_, ...), custom_call_target="tpu_custom_call" | custom-call | flops 1207959552 | bytes 7077888 | tf_op jit(solution)/shard_map/seg_mlp_weight/pallas_call | solution.py:595
  129.1 2.3 collective-permute-start.44
  131.4 4.2 %collective-permute-done.47.refs_7_ = bf16[2,48,3072]{2,1,0:T(8,128)(2,1)S(1)} collective-permute-done((bf16[2,48,3072]{2,1,0:T(8,128)(2,1)S(1)}, bf16[2,48,3072]{2,1,0:T(8,128)(2,1)S(1)}, u32[]{:S(2)}, u32[]{:S(2)}) %collective-permute-start.47) | collective-permute-done | bytes 589856 | tf_op jit(solution)/shard_map/ppermute | solution.py:569
  141.4 2.4 collective-permute-start.49
  148.9 2.4 %collective-permute-start.53 = (f32[16,768]{1,0:T(8,128)S(1)}, f32[16,768]{1,0:T(8,128)S(1)}, u32[]{:S(2)}, u32[]{:S(2)}) collective-permute-start(f32[16,768]{1,0:T(8,128)S(1)} %get-tuple-element.387.refs_1_), channel_id=1, source_target_pairs={{0,8},{1,9},{2,10},{3,11},{4,12},{5,13},{6,14},{7,15},{8,0},{9,1},... | collective-permute-start | bytes 147464 | tf_op jit(solution)/shard_map/ppermute | solution.py:565
  160.3 2.3 collective-permute-done.56.refs_4_
  167.8 3.1 %collective-permute-start.60 = (f32[1,768]{1,0:T(1,128)S(1)}, f32[1,768]{1,0:T(1,128)S(1)}, u32[]{:S(2)}, u32[]{:S(2)}) collective-permute-start(f32[1,768]{1,0:T(1,128)S(1)} %get-tuple-element.413.refs_0_.refs_3_), channel_id=1, source_target_pairs={{0,16},{16,0},{1,17},{17,1},{2,18},{18,2},{3,19},{19,3},{4,20},{20... | collective-permute-start | bytes 9224 | tf_op jit(solution)/shard_map/ppermute | solution.py:573
  177.3 4.4 %seg_attn_back.1 = (bf16[256,1152]{1,0:T(8,128)(2,1)S(1)}, f32[128,768]{1,0:T(8,128)S(1)}, f32[128,768]{1,0:T(8,128)S(1)}, bf16[24,768]{1,0:T(8,128)(2,1)S(1)}) custom-call(s32[5]{0:T(128)S(1)} %stack.15.where, bf16[256,1152]{1,0:T(8,128)(2,1)S(1)} %get-tuple-element.299.refs_0_, bf16[128,768]{1,0:T(8,128)(2,1)S(1)} %get-tuple-element.418.refs_1_, ...), custom_call_target="tpu_custom_call" | custom-call | flops 905969664 | bytes 4624384 | tf_op jit(solution)/shard_map/seg_attn_back/pallas_call | solution.py:595
  186.7 8.3 %collective-permute-done.66.refs_2_ = bf16[64,3072]{1,0:T(8,128)(2,1)S(1)} collective-permute-done((bf16[64,3072]{1,0:T(8,128)(2,1)S(1)}, bf16[64,3072]{1,0:T(8,128)(2,1)S(1)}, u32[]{:S(2)}, u32[]{:S(2)}) %collective-permute-start.66) | collective-permute-done | bytes 393248 | tf_op jit(solution)/shard_map/ppermute | solution.py:565
  199.7 9.0 %collective-permute-done.74.refs_1_ = bf16[64,3072]{1,0:T(8,128)(2,1)S(1)} collective-permute-done((bf16[64,3072]{1,0:T(8,128)(2,1)S(1)}, bf16[64,3072]{1,0:T(8,128)(2,1)S(1)}, u32[]{:S(2)}, u32[]{:S(2)}) %collective-permute-start.74) | collective-permute-done | bytes 393248 | tf_op jit(solution)/shard_map/ppermute | solution.py:565
  208.8 2.9 %collective-permute-start.77 = (bf16[24,768]{1,0:T(8,128)(2,1)S(1)}, bf16[24,768]{1,0:T(8,128)(2,1)S(1)}, u32[]{:S(2)}, u32[]{:S(2)}) collective-permute-start(bf16[24,768]{1,0:T(8,128)(2,1)S(1)} %get-tuple-element.465), channel_id=1, source_target_pairs={{0,12},{1,13},{2,14},{3,15},{4,0},{5,1},{6,2},{7,3},{8,4},{9,5},{1... | collective-permute-start | bytes 110600 | tf_op jit(solution)/shard_map/ppermute | solution.py:565
  221.2 4.3 %collective-permute-done.72 = bf16[48,1536]{1,0:T(8,128)(2,1)S(1)} collective-permute-done((bf16[48,1536]{1,0:T(8,128)(2,1)S(1)}, bf16[48,1536]{1,0:T(8,128)(2,1)S(1)}, u32[]{:S(2)}, u32[]{:S(2)}) %collective-permute-start.72) | collective-permute-done | bytes 147488 | tf_op jit(solution)/shard_map/ppermute | solution.py:565
  229.2 4.4 %head_owner.1 = (f32[48,3072]{1,0:T(8,128)S(1)}, f32[16,768]{1,0:T(8,128)S(1)}, f32[48,9216]{1,0:T(8,128)}, f32[576]{0:T(1024)}, f32[16,768]{1,0:T(8,128)}, /*index=5*/f32[1,1]{1,0:T(1,128)}) custom-call(s32[5]{0:T(128)S(1)} %stack.15.where, bf16[96,768]{1,0:T(8,128)(2,1)S(1)} %pad_maximum_fusion.11.refs_0_, ...), custom_call_target="tpu_custom_call" | custom-call | flops 28311552 | bytes 4503812 | tf_op jit(solution)/shard_map/head_owner/pallas_call | solution.py:595
  233.6 2.4 collective-permute-start.83
  238.2 3.3 %seg_owner.1 = (f32[48,9216]{1,0:T(8,128)}, f32[576]{0:T(1024)}) custom-call(s32[5]{0:T(128)S(1)} %stack.15.where, f32[48,1536]{1,0:T(8,128)S(1)} %convert_add_fusion.1.attn, f32[48,1536]{1,0:T(8,128)S(1)} %collective-permute-done.82.attn_got, f32[48,3072]{1,0:T(8,128)S(1)} %get-tuple-element.484.mlp, f32[48,3072]{1,0:T(8,128)S(1)} %collective-permute-done.83.mlp_got, ...), custom_call_target="tpu_custom_call" | custom-call | bytes 3639552 | tf_op jit(solution)/shard_map/seg_owner/pallas_call | solution.py:595
  (212 shorter events, 118.5 us)
Async XLA Ops:
  8.0 17.3 %collective-permute-start.3 = (bf16[48,4736]{1,0:T(8,128)(2,1)S(1)}, bf16[48,4736]{1,0:T(8,128)(2,1)S(1)}, u32[]{:S(2)}, u32[]{:S(2)}) collective-permute-start(bf16[48,4736]{1,0:T(8,128)(2,1)S(1)} %pad_maximum_fusion.10), channel_id=1, source_target_pairs={{0,1},{1,0},{2,3},{3,2},{4,5},{5,4},{6,7},{7,6},{8,9},{9,8},{10,11... | collective-permute-start | bytes 1363976 | tf_op jit(solution)/shard_map/ppermute | solution.py:569
  9.3 16.0 %collective-permute-start.4 = (bf16[48,4736]{1,0:T(8,128)(2,1)S(1)}, bf16[48,4736]{1,0:T(8,128)(2,1)S(1)}, u32[]{:S(2)}, u32[]{:S(2)}) collective-permute-start(bf16[48,4736]{1,0:T(8,128)(2,1)S(1)} %pad_maximum_fusion.10), channel_id=1, source_target_pairs={{0,2},{1,3},{2,0},{3,1},{4,6},{5,7},{6,4},{7,5},{8,10},{9,11},{10,... | collective-permute-start | bytes 1363976 | tf_op jit(solution)/shard_map/ppermute | solution.py:569
  9.7 11.7 %collective-permute-start.1 = (bf16[48,1664]{1,0:T(8,128)(2,1)S(1)}, bf16[48,1664]{1,0:T(8,128)(2,1)S(1)}, u32[]{:S(2)}, u32[]{:S(2)}) collective-permute-start(bf16[48,1664]{1,0:T(8,128)(2,1)S(1)} %get-tuple-element.254.refs_0_), channel_id=1, source_target_pairs={{0,8},{1,9},{2,10},{3,11},{4,12},{5,13},{6,14},{7,15},{8,0},{9,1},... | collective-permute-start | bytes 479240 | tf_op jit(solution)/shard_map/ppermute | solution.py:565
  12.0 13.3 %collective-permute-start = (bf16[48,1664]{1,0:T(8,128)(2,1)S(1)}, bf16[48,1664]{1,0:T(8,128)(2,1)S(1)}, u32[]{:S(2)}, u32[]{:S(2)}) collective-permute-start(bf16[48,1664]{1,0:T(8,128)(2,1)S(1)} %get-tuple-element.254.refs_0_), channel_id=1, source_target_pairs={{0,4},{1,5},{2,6},{3,7},{4,8},{5,9},{6,10},{7,11},{8,12},{9,13},{1... | collective-permute-start | bytes 479240 | tf_op jit(solution)/shard_map/ppermute | solution.py:565
  28.2 18.1 %collective-permute-start.8 = (bf16[48,7424]{1,0:T(8,128)(2,1)S(1)}, bf16[48,7424]{1,0:T(8,128)(2,1)S(1)}, u32[]{:S(2)}, u32[]{:S(2)}) collective-permute-start(bf16[48,7424]{1,0:T(8,128)(2,1)S(1)} %pad_maximum_fusion.6), channel_id=1, source_target_pairs={{0,2},{1,3},{2,0},{3,1},{4,6},{5,7},{6,4},{7,5},{8,10},{9,11},{10,... | collective-permute-start | bytes 2138120 | tf_op jit(solution)/shard_map/ppermute | solution.py:569
  29.5 16.8 %collective-permute-start.7 = (bf16[48,7296]{1,0:T(8,128)(2,1)S(1)}, bf16[48,7296]{1,0:T(8,128)(2,1)S(1)}, u32[]{:S(2)}, u32[]{:S(2)}) collective-permute-start(bf16[48,7296]{1,0:T(8,128)(2,1)S(1)} %pad_maximum_fusion.7), channel_id=1, source_target_pairs={{0,1},{1,0},{2,3},{3,2},{4,5},{5,4},{6,7},{7,6},{8,9},{9,8},{10,11... | collective-permute-start | bytes 2101256 | tf_op jit(solution)/shard_map/ppermute | solution.py:569
  33.1 11.1 %collective-permute-start.9 = (bf16[48,1536]{1,0:T(8,128)(2,1)S(1)}, bf16[48,1536]{1,0:T(8,128)(2,1)S(1)}, u32[]{:S(2)}, u32[]{:S(2)}) collective-permute-start(bf16[48,1536]{1,0:T(8,128)(2,1)S(1)} %get-tuple-element.275.refs_0_), channel_id=1, source_target_pairs={{0,4},{1,5},{2,6},{3,7},{4,8},{5,9},{6,10},{7,11},{8,12},{9,13},{1... | collective-permute-start | bytes 442376 | tf_op jit(solution)/shard_map/ppermute | solution.py:565
  46.5 16.1 %collective-permute-start.13 = (bf16[48,7168]{1,0:T(8,128)(2,1)S(1)}, bf16[48,7168]{1,0:T(8,128)(2,1)S(1)}, u32[]{:S(2)}, u32[]{:S(2)}) collective-permute-start(bf16[48,7168]{1,0:T(8,128)(2,1)S(1)} %pad_maximum_fusion.8), channel_id=1, source_target_pairs={{0,2},{1,3},{2,0},{3,1},{4,6},{5,7},{6,4},{7,5},{8,10},{9,11},{10,... | collective-permute-start | bytes 2064392 | tf_op jit(solution)/shard_map/ppermute | solution.py:569
  47.1 15.4 %collective-permute-start.12 = (bf16[48,7040]{1,0:T(8,128)(2,1)S(1)}, bf16[48,7040]{1,0:T(8,128)(2,1)S(1)}, u32[]{:S(2)}, u32[]{:S(2)}) collective-permute-start(bf16[48,7040]{1,0:T(8,128)(2,1)S(1)} %pad_maximum_fusion.9), channel_id=1, source_target_pairs={{0,1},{1,0},{2,3},{3,2},{4,5},{5,4},{6,7},{7,6},{8,9},{9,8},{10,11... | collective-permute-start | bytes 2027528 | tf_op jit(solution)/shard_map/ppermute | solution.py:569
  50.8 11.2 %collective-permute-start.15 = (bf16[48,1536]{1,0:T(8,128)(2,1)S(1)}, bf16[48,1536]{1,0:T(8,128)(2,1)S(1)}, u32[]{:S(2)}, u32[]{:S(2)}) collective-permute-start(bf16[48,1536]{1,0:T(8,128)(2,1)S(1)} %get-tuple-element.286.refs_0_), channel_id=1, source_target_pairs={{0,4},{1,5},{2,6},{3,7},{4,8},{5,9},{6,10},{7,11},{8,12},{9,13},{1... | collective-permute-start | bytes 442376 | tf_op jit(solution)/shard_map/ppermute | solution.py:565
  62.7 14.3 %collective-permute-start.18 = (bf16[48,6912]{1,0:T(8,128)(2,1)S(1)}, bf16[48,6912]{1,0:T(8,128)(2,1)S(1)}, u32[]{:S(2)}, u32[]{:S(2)}) collective-permute-start(bf16[48,6912]{1,0:T(8,128)(2,1)S(1)} %get-tuple-element.290), channel_id=1, source_target_pairs={{0,1},{1,0},{2,3},{3,2},{4,5},{5,4},{6,7},{7,6},{8,9},{9,8},{10,11... | collective-permute-start | bytes 1990664 | tf_op jit(solution)/shard_map/ppermute | solution.py:569
  63.4 11.2 %collective-permute-start.32 = (bf16[48,1152]{1,0:T(8,128)(2,1)S(1)}, bf16[48,1152]{1,0:T(8,128)(2,1)S(1)}, u32[]{:S(2)}, u32[]{:S(2)}) collective-permute-start(bf16[48,1152]{1,0:T(8,128)(2,1)S(1)} %get-tuple-element.329), channel_id=1, source_target_pairs={{0,4},{1,5},{2,6},{3,7},{4,8},{5,9},{6,10},{7,11},{8,12},{9,13},{1... | collective-permute-start | bytes 331784 | tf_op jit(solution)/shard_map/ppermute | solution.py:565
  65.6 14.5 %collective-permute-start.19 = (bf16[48,6912]{1,0:T(8,128)(2,1)S(1)}, bf16[48,6912]{1,0:T(8,128)(2,1)S(1)}, u32[]{:S(2)}, u32[]{:S(2)}) collective-permute-start(bf16[48,6912]{1,0:T(8,128)(2,1)S(1)} %get-tuple-element.291), channel_id=1, source_target_pairs={{0,2},{1,3},{2,0},{3,1},{4,6},{5,7},{6,4},{7,5},{8,10},{9,11},{10,... | collective-permute-start | bytes 1990664 | tf_op jit(solution)/shard_map/ppermute | solution.py:569
  70.6 11.2 %collective-permute-start.20 = (bf16[8,48,384]{2,1,0:T(8,128)(2,1)S(1)}, bf16[8,48,384]{2,1,0:T(8,128)(2,1)S(1)}, u32[]{:S(2)}, u32[]{:S(2)}) collective-permute-start(bf16[8,48,384]{2,1,0:T(8,128)(2,1)S(1)} %get-tuple-element.295.low), channel_id=1, source_target_pairs={{0,16},{16,0},{1,17},{17,1},{2,18},{18,2},{3,19},{19,3},{4,20},{20... | collective-permute-start | bytes 884744 | tf_op jit(solution)/shard_map/ppermute | solution.py:573
  74.7 11.8 %collective-permute-start.34 = (bf16[48,1152]{1,0:T(8,128)(2,1)S(1)}, bf16[48,1152]{1,0:T(8,128)(2,1)S(1)}, u32[]{:S(2)}, u32[]{:S(2)}) collective-permute-start(bf16[48,1152]{1,0:T(8,128)(2,1)S(1)} %get-tuple-element.333), channel_id=1, source_target_pairs={{0,12},{1,13},{2,14},{3,15},{4,0},{5,1},{6,2},{7,3},{8,4},{9,5},{1... | collective-permute-start | bytes 331784 | tf_op jit(solution)/shard_map/ppermute | solution.py:565
  89.5 14.4 %collective-permute-start.35 = (bf16[48,4992]{1,0:T(8,128)(2,1)S(1)}, bf16[48,4992]{1,0:T(8,128)(2,1)S(1)}, u32[]{:S(2)}, u32[]{:S(2)}) collective-permute-start(bf16[48,4992]{1,0:T(8,128)(2,1)S(1)} %constant_dynamic-update-slice_fusion), channel_id=1, source_target_pairs={{0,1},{1,0},{2,3},{3,2},{4,5},{5,4},{6,7},{7,6},{8,9},{9,8},{10,11... | collective-permute-start | bytes 1437704 | tf_op jit(solution)/shard_map/ppermute | solution.py:569
  90.5 13.5 %collective-permute-start.36 = (bf16[48,4992]{1,0:T(8,128)(2,1)S(1)}, bf16[48,4992]{1,0:T(8,128)(2,1)S(1)}, u32[]{:S(2)}, u32[]{:S(2)}) collective-permute-start(bf16[48,4992]{1,0:T(8,128)(2,1)S(1)} %constant_dynamic-update-slice_fusion), channel_id=1, source_target_pairs={{0,2},{1,3},{2,0},{3,1},{4,6},{5,7},{6,4},{7,5},{8,10},{9,11},{10,... | collective-permute-start | bytes 1437704 | tf_op jit(solution)/shard_map/ppermute | solution.py:569
  120.6 15.0 %collective-permute-start.47 = (bf16[2,48,3072]{2,1,0:T(8,128)(2,1)S(1)}, bf16[2,48,3072]{2,1,0:T(8,128)(2,1)S(1)}, u32[]{:S(2)}, u32[]{:S(2)}) collective-permute-start(bf16[2,48,3072]{2,1,0:T(8,128)(2,1)S(1)} %get-tuple-element.374), channel_id=1, source_target_pairs={{0,2},{1,3},{2,0},{3,1},{4,6},{5,7},{6,4},{7,5},{8,10},{9,11},{10,... | collective-permute-start | bytes 1769480 | tf_op jit(solution)/shard_map/ppermute | solution.py:569
  121.6 14.6 %collective-permute-start.48 = (bf16[2,48,3072]{2,1,0:T(8,128)(2,1)S(1)}, bf16[2,48,3072]{2,1,0:T(8,128)(2,1)S(1)}, u32[]{:S(2)}, u32[]{:S(2)}) collective-permute-start(bf16[2,48,3072]{2,1,0:T(8,128)(2,1)S(1)} %get-tuple-element.376), channel_id=1, source_target_pairs={{0,1},{1,0},{2,3},{3,2},{4,5},{5,4},{6,7},{7,6},{8,9},{9,8},{10,11... | collective-permute-start | bytes 1769480 | tf_op jit(solution)/shard_map/ppermute | solution.py:569
  137.6 26.4 %collective-permute-start.58 = (bf16[4,48,3072]{2,1,0:T(8,128)(2,1)S(1)}, bf16[4,48,3072]{2,1,0:T(8,128)(2,1)S(1)}, u32[]{:S(2)}, u32[]{:S(2)}) collective-permute-start(bf16[4,48,3072]{2,1,0:T(8,128)(2,1)S(1)} %get-tuple-element.405), channel_id=1, source_target_pairs={{0,1},{1,0},{2,3},{3,2},{4,5},{5,4},{6,7},{7,6},{8,9},{9,8},{10,11... | collective-permute-start | bytes 3538952 | tf_op jit(solution)/shard_map/ppermute | solution.py:569
  138.4 26.1 %collective-permute-start.59 = (bf16[4,48,3072]{2,1,0:T(8,128)(2,1)S(1)}, bf16[4,48,3072]{2,1,0:T(8,128)(2,1)S(1)}, u32[]{:S(2)}, u32[]{:S(2)}) collective-permute-start(bf16[4,48,3072]{2,1,0:T(8,128)(2,1)S(1)} %get-tuple-element.406), channel_id=1, source_target_pairs={{0,2},{1,3},{2,0},{3,1},{4,6},{5,7},{6,4},{7,5},{8,10},{9,11},{10,... | collective-permute-start | bytes 3538952 | tf_op jit(solution)/shard_map/ppermute | solution.py:569
  166.0 17.2 %collective-permute-start.63 = (bf16[64,3072]{1,0:T(8,128)(2,1)S(1)}, bf16[64,3072]{1,0:T(8,128)(2,1)S(1)}, u32[]{:S(2)}, u32[]{:S(2)}) collective-permute-start(bf16[64,3072]{1,0:T(8,128)(2,1)S(1)} %get-tuple-element.432), channel_id=1, source_target_pairs={{0,12},{1,13},{2,14},{3,15},{4,0},{5,1},{6,2},{7,3},{8,4},{9,5},{1... | collective-permute-start | bytes 1179656 | tf_op jit(solution)/shard_map/ppermute | solution.py:565
  176.2 18.8 %collective-permute-start.66 = (bf16[64,3072]{1,0:T(8,128)(2,1)S(1)}, bf16[64,3072]{1,0:T(8,128)(2,1)S(1)}, u32[]{:S(2)}, u32[]{:S(2)}) collective-permute-start(bf16[64,3072]{1,0:T(8,128)(2,1)S(1)} %get-tuple-element.441), channel_id=1, source_target_pairs={{0,8},{1,9},{2,10},{3,11},{4,12},{5,13},{6,14},{7,15},{8,0},{9,1},... | collective-permute-start | bytes 1179656 | tf_op jit(solution)/shard_map/ppermute | solution.py:565
  181.7 13.3 %collective-permute-start.67 = (f32[128,768]{1,0:T(8,128)S(1)}, f32[128,768]{1,0:T(8,128)S(1)}, u32[]{:S(2)}, u32[]{:S(2)}) collective-permute-start(f32[128,768]{1,0:T(8,128)S(1)} %get-tuple-element.444), channel_id=1, source_target_pairs={{0,16},{16,0},{1,17},{17,1},{2,18},{18,2},{3,19},{19,3},{4,20},{20... | collective-permute-start | bytes 1179656 | tf_op jit(solution)/shard_map/ppermute | solution.py:573
  183.1 11.8 %collective-permute-start.65 = (bf16[2,48,1536]{2,1,0:T(8,128)(2,1)S(1)}, bf16[2,48,1536]{2,1,0:T(8,128)(2,1)S(1)}, u32[]{:S(2)}, u32[]{:S(2)}) collective-permute-start(bf16[2,48,1536]{2,1,0:T(8,128)(2,1)S(1)} %get-tuple-element.435), channel_id=1, source_target_pairs={{0,1},{1,0},{2,3},{3,2},{4,5},{5,4},{6,7},{7,6},{8,9},{9,8},{10,11... | collective-permute-start | bytes 884744 | tf_op jit(solution)/shard_map/ppermute | solution.py:569
  183.6 11.3 %collective-permute-start.64 = (bf16[2,48,1536]{2,1,0:T(8,128)(2,1)S(1)}, bf16[2,48,1536]{2,1,0:T(8,128)(2,1)S(1)}, u32[]{:S(2)}, u32[]{:S(2)}) collective-permute-start(bf16[2,48,1536]{2,1,0:T(8,128)(2,1)S(1)} %get-tuple-element.433), channel_id=1, source_target_pairs={{0,2},{1,3},{2,0},{3,1},{4,6},{5,7},{6,4},{7,5},{8,10},{9,11},{10,... | collective-permute-start | bytes 884744 | tf_op jit(solution)/shard_map/ppermute | solution.py:569
  196.4 16.5 %collective-permute-start.68 = (bf16[4,48,1536]{2,1,0:T(8,128)(2,1)S(1)}, bf16[4,48,1536]{2,1,0:T(8,128)(2,1)S(1)}, u32[]{:S(2)}, u32[]{:S(2)}) collective-permute-start(bf16[4,48,1536]{2,1,0:T(8,128)(2,1)S(1)} %get-tuple-element.449), channel_id=1, source_target_pairs={{0,1},{1,0},{2,3},{3,2},{4,5},{5,4},{6,7},{7,6},{8,9},{9,8},{10,11... | collective-permute-start | bytes 1769480 | tf_op jit(solution)/shard_map/ppermute | solution.py:569
  197.0 15.9 %collective-permute-start.69 = (bf16[4,48,1536]{2,1,0:T(8,128)(2,1)S(1)}, bf16[4,48,1536]{2,1,0:T(8,128)(2,1)S(1)}, u32[]{:S(2)}, u32[]{:S(2)}) collective-permute-start(bf16[4,48,1536]{2,1,0:T(8,128)(2,1)S(1)} %get-tuple-element.450), channel_id=1, source_target_pairs={{0,2},{1,3},{2,0},{3,1},{4,6},{5,7},{6,4},{7,5},{8,10},{9,11},{10,... | collective-permute-start | bytes 1769480 | tf_op jit(solution)/shard_map/ppermute | solution.py:569
  197.7 11.1 %collective-permute-start.74 = (bf16[64,3072]{1,0:T(8,128)(2,1)S(1)}, bf16[64,3072]{1,0:T(8,128)(2,1)S(1)}, u32[]{:S(2)}, u32[]{:S(2)}) collective-permute-start(bf16[64,3072]{1,0:T(8,128)(2,1)S(1)} %get-tuple-element.464), channel_id=1, source_target_pairs={{0,4},{1,5},{2,6},{3,7},{4,8},{5,9},{6,10},{7,11},{8,12},{9,13},{1... | collective-permute-start | bytes 1179656 | tf_op jit(solution)/shard_map/ppermute | solution.py:565
  198.4 13.3 %collective-permute-start.70 = (f32[24,768]{1,0:T(8,128)S(1)}, f32[24,768]{1,0:T(8,128)S(1)}, u32[]{:S(2)}, u32[]{:S(2)}) collective-permute-start(f32[24,768]{1,0:T(8,128)S(1)} %get-tuple-element.453), channel_id=1, source_target_pairs={{0,16},{16,0},{1,17},{17,1},{2,18},{18,2},{3,19},{19,3},{4,20},{20... | collective-permute-start | bytes 221192 | tf_op jit(solution)/shard_map/ppermute | solution.py:573
  216.6 12.6 %collective-permute-start.80 = (bf16[96,768]{1,0:T(8,128)(2,1)S(1)}, bf16[96,768]{1,0:T(8,128)(2,1)S(1)}, u32[]{:S(2)}, u32[]{:S(2)}) collective-permute-start(bf16[96,768]{1,0:T(8,128)(2,1)S(1)} %pad_maximum_fusion.11.refs_0_), channel_id=1, source_target_pairs={{0,3},{1,2},{2,1},{3,0},{4,7},{5,6},{6,5},{7,4},{8,11},{9,10},{10,... | collective-permute-start | bytes 442376 | tf_op jit(solution)/shard_map/ppermute | solution.py:569
  218.0 11.2 %collective-permute-start.79 = (bf16[96,768]{1,0:T(8,128)(2,1)S(1)}, bf16[96,768]{1,0:T(8,128)(2,1)S(1)}, u32[]{:S(2)}, u32[]{:S(2)}) collective-permute-start(bf16[96,768]{1,0:T(8,128)(2,1)S(1)} %pad_maximum_fusion.11.refs_0_), channel_id=1, source_target_pairs={{0,2},{1,3},{2,0},{3,1},{4,6},{5,7},{6,4},{7,5},{8,10},{9,11},{10,... | collective-permute-start | bytes 442376 | tf_op jit(solution)/shard_map/ppermute | solution.py:569
  (61 other events, 323.1 us)

commit v12 on v11

--- a/solution.py
+++ b/solution.py
@@ -1085,14 +1085,35 @@
 
 
 def attn_near_kernel(where, *refs):
-    top_row, out_rows, live_row = refs[5:8]
+    proj, (top_row, out_rows, live_row) = refs[2], refs[5:8]
+    weight, sums_first, sums_second, sums_up, head_top, head_normed, data = refs[8:15]
+    x_out, y_out, kept_out, output_out, own_out, send_out, payload_out, rows = refs[15:]
+    core_at = where[2]
+    partial = product_right(proj[...], whole_rows(weight))
+    own_out[...] = partial[:SEG]
+    send_out[...] = partial[SEG:]
     row_at = lax.broadcasted_iota(jnp.int32, (SEG, 1), 0)
     output = jnp.where(row_at == 0, top_row[...] * live_row[:, 0:1], out_rows[...])
-    refs[11][...] = output.astype(LOW)
-    for mask, out in ((1, refs[8]), (2, refs[9]), (0, refs[10])):
+    output_out[...] = output.astype(LOW)
+    for mask, out in ((1, x_out), (2, y_out), (0, kept_out)):
         for piece in range(4):
             columns = slice(piece * HALF, (piece + 1) * HALF)
             out[:, :, columns] = attn_product(where, refs[:5], mask, piece)
+    lanes = pl.ds(aligned(core_at * HALF), HALF)
+    rows[...] = jnp.zeros_like(rows)
+    rows[0:12, :] = data[0:12, :]
+    rows[12:13, lanes] = column_sum(proj[:, :HALF])
+    rows[13:14, lanes] = column_sum(proj[:, 2 * HALF :])
+    rows[14:15, :] = sums_first[0:1, :]
+    rows[15:16, :] = sums_second[0:1, :] + data[2:3, :]
+    rows[16:18, :] = sums_first[1:3, :]
+    rows[18:19, :] = sums_second[1:2, :] + head_top[...] * head_normed[0:1, :]
+    rows[19:20, :] = sums_second[2:3, :] + head_top[...]
+    for at in range(FF_HALF // MODEL):
+        total = sums_up[at : at + 1, :] + data[4 + 2 * at : 5 + 2 * at, :]
+        total = total + data[5 + 2 * at : 6 + 2 * at, :]
+        rows[pl.ds(20 + core_at * (FF_HALF // MODEL) + at, 1), :] = total
+    payload_out[...] = rows[...].astype(LOW)
 
 
 def fold_kernel(where, kept, got_x, got_y, *refs):
@@ -1197,9 +1218,7 @@
 
 
 def attn_back_kernel(where, *refs):
-    qkv, mixed_grad, got, live_row, live_got, weight = refs[:6]
-    sums_first, sums_second, sums_up, head_top, head_normed, data = refs[6:12]
-    proj_out, own_out, send_out, payload_out, rows = refs[12:]
+    qkv, mixed_grad, got, live_row, live_got, proj_out = refs
     core_at = where[2]
     lanes = pl.ds(aligned(core_at * HALF), HALF)
     for part, live in enumerate((live_row, live_got)):
@@ -1208,23 +1227,6 @@
         pieces = attend_tiles_back(qkv[at, :], grad, HALF, token_allowed(live[...]))
         for tile, value in enumerate(pieces):
             proj_out[at, tile * LANES : (tile + 1) * LANES] = value
-    partial = product_right(proj_out[...], whole_rows(weight))
-    own_out[...] = partial[:SEG]
-    send_out[...] = partial[SEG:]
-    rows[...] = jnp.zeros_like(rows)
-    rows[0:12, :] = data[0:12, :]
-    rows[12:13, lanes] = column_sum(proj_out[:, :HALF])
-    rows[13:14, lanes] = column_sum(proj_out[:, 2 * HALF :])
-    rows[14:15, :] = sums_first[0:1, :]
-    rows[15:16, :] = sums_second[0:1, :] + data[2:3, :]
-    rows[16:18, :] = sums_first[1:3, :]
-    rows[18:19, :] = sums_second[1:2, :] + head_top[...] * head_normed[0:1, :]
-    rows[19:20, :] = sums_second[2:3, :] + head_top[...]
-    for at in range(FF_HALF // MODEL):
-        total = sums_up[at : at + 1, :] + data[4 + 2 * at : 5 + 2 * at, :]
-        total = total + data[5 + 2 * at : 6 + 2 * at, :]
-        rows[pl.ds(20 + core_at * (FF_HALF // MODEL) + at, 1), :] = total
-    payload_out[...] = rows[...].astype(LOW)
 
 
 def cls_gather_kernel(where, *refs):
@@ -1420,6 +1422,12 @@
 def attn_add_kernel(where, *refs):
     far_low, far_high, to_x, to_y, grad, own, got, x_out, y_out, input_out = refs
     add_far_kernel(where, far_low, far_high, to_x, to_y, x_out, y_out)
+    input_out[...] = (grad[...] + own[...] + got[...]).astype(LOW)
+
+
+def rows_input_kernel(where, *refs):
+    cls_rows_kernel(where, *refs[:8], refs[11], refs[13])
+    grad, own, got, input_out = refs[8], refs[9], refs[10], refs[12]
     input_out[...] = (grad[...] + own[...] + got[...]).astype(LOW)
 
 
@@ -1990,34 +1998,15 @@
         ),
     )
     attn_got = other_core(attn_send)
-    proj, input_own, input_send, payload = run_kernel(
+    proj = run_kernel(
         attn_back_kernel,
         "seg_attn_back",
-        [
-            shape_of((both_rows, 3 * HALF), LOW),
-            shape_of((SEG, MODEL)),
-            shape_of((SEG, MODEL)),
-            shape_of((24, MODEL), LOW),
-        ],
-        where,
-        (),
-        (
-            qkv,
-            mixed_grad,
-            attn_got,
-            live_row,
-            live_got,
-            qkv_weight,
-            first_sums,
-            second_sums,
-            up_sums,
-            dheads,
-            normed_second,
-            head_data,
-        ),
-        [pltpu.VMEM((24, MODEL), WIDE)],
-        flops=4 * SEG * MODEL * 3 * MODEL,
-    )
+        [shape_of((both_rows, 3 * HALF), LOW)],
+        where,
+        (),
+        (qkv, mixed_grad, attn_got, live_row, live_got),
+        flops=2 * SEG * MODEL * 3 * MODEL,
+    )[0]
     attn_data = (hidden_ordered, mixed_ordered, proj, branch, attn_got)
     attn_far = run_kernel(
         attn_far_kernel,
@@ -2029,44 +2018,54 @@
         flops=SEG * MODEL * 2 * MODEL,
     )
     attn_far = reduce_far(tuple(after(part, mlp_got[-1]) for part in attn_far))
-    attn_near = run_kernel(
+    *attn_near, output, input_own, input_send, payload = run_kernel(
         attn_near_kernel,
         "seg_attn_near",
-        part_shapes(4 * HALF)[2:] + [shape_of((SEG, MODEL), LOW)],
-        where,
-        (),
-        attn_data + (top_row, out_rows, live_row),
+        part_shapes(4 * HALF)[2:]
+        + [
+            shape_of((SEG, MODEL), LOW),
+            shape_of((SEG, MODEL)),
+            shape_of((SEG, MODEL)),
+            shape_of((24, MODEL), LOW),
+        ],
+        where,
+        (),
+        attn_data
+        + (top_row, out_rows, live_row, qkv_weight, first_sums, second_sums, up_sums)
+        + (dheads, normed_second, head_data),
+        [pltpu.VMEM((24, MODEL), WIDE)],
         flops=3 * SEG * MODEL * 2 * MODEL,
     )
-    output = attn_near[3]
-    *attn_sent, input_grad = run_kernel(
-        attn_add_kernel,
+    attn_sent = run_kernel(
+        add_far_kernel,
         "seg_attn_add",
-        [shape_of(attn_near[0].shape, LOW)] * 2 + [shape_of((SEG, MODEL), LOW)],
-        where,
-        (),
-        attn_far
-        + tuple(attn_near[:2])
-        + (after(grad_summed, got_two), input_own, other_core(input_send)),
+        [shape_of(attn_near[0].shape, LOW)] * 2,
+        where,
+        (),
+        attn_far + (after(attn_near[0], got_two), attn_near[1]),
     )
     attn_plane = sent_both(*attn_sent)
     mlp_got[0] = along_line(after(mlp_last, *attn_sent), 1)
-    payload_parts = line_parts(after(payload, mlp_got[0]))
+    input_got = other_core(after(input_send, *attn_sent))
+    shared = shared + other_core(after(shared, attn_sent[0]))
+    payload_parts = line_parts(after(payload, mlp_got[0], input_got, shared))
     mlp_got = [after(got, attn_plane[0]) for got in mlp_got]
     mlp_sum = reduce_line(mlp_own, mlp_got)
-    shared = shared + other_core(after(shared, attn_sent[0]))
     row_width = 8 * MODEL + 2 * FF
-    cls_rows = run_kernel(
-        cls_rows_kernel,
+    cls_rows, input_grad = run_kernel(
+        rows_input_kernel,
         "head_rows",
-        [shape_of((GROUP, row_width), LOW)],
-        where,
-        (),
-        (pack,) + tuple(mlp_got) + (heads, cls_branch, cls_low, cls_second),
+        [shape_of((GROUP, row_width), LOW), shape_of((SEG, MODEL), LOW)],
+        where,
+        (),
+        (pack,)
+        + tuple(mlp_got)
+        + (heads, cls_branch, cls_low, cls_second)
+        + (grad_summed, input_own, input_got),
         [pltpu.VMEM((LINE,) + pack.shape, LOW)],
-    )[0]
+    )
     cls_got = other_core(cls_rows)
-    attn_plane = tuple(after(got, output, input_grad, shared) for got in attn_plane)
+    attn_plane = tuple(after(got, output, shared) for got in attn_plane)
     attn_own, *attn_sent = reduce_fold(where, attn_near[2], attn_plane)
     attn_lines = list(
         together(*(along_line(attn_sent[apart - 1], apart) for apart in range(1, LINE)))

time: 243 us -> 243 us (level)
  transfers between devices with their start and end apart: 85 -> 85, of which waited for: 39 -> 40; matrix products, arithmetic and copies ran while one was open for 0% -> 0% of each run, Pallas kernels for 13% -> 14%
where the time goes in v12:
time: 243 us; the launch traced here: 241 us
  starting transfers between devices  97.8 us (40%)
  waiting for transfers between devices  87.1 us (36%)
  Pallas kernels  48.2 us (20%)
  local copies, waits for them, and re-layouts  5.34 us (2%)
    ppermute x36, waiting for transfers between devices, along_line(): return lax.ppermute(value, 'fsdp', line_pairs(apart))  65 us
    pallas_call x26, Pallas kernels, run_kernel(): pl.pallas_call(body, name=name, out_shape=tuple(outs), in_specs=in_specs,...  48.2 us
    ppermute x36, starting transfers between devices, along_line(): return lax.ppermute(value, 'fsdp', line_pairs(apart))  45.5 us
    ppermute x21, starting transfers between devices, other_core(): return lax.ppermute(value, 'rep', [(0, 1), (1, 0)])  31.2 us
    ppermute x28, starting transfers between devices, in_plane(): return lax.ppermute(value, 'fsdp', plane_pairs(mask))  21.1 us
    ppermute x28, waiting for transfers between devices, in_plane(): return lax.ppermute(value, 'fsdp', plane_pairs(mask))  11.6 us
    ppermute x21, waiting for transfers between devices, other_core(): return lax.ppermute(value, 'rep', [(0, 1), (1, 0)])  10.4 us
  transfers between devices with their start and end apart: 85, of which 40 were waited for; matrix products, arithmetic and copies ran while one was open for 0% of the time, Pallas kernels for 14%

profile of v12, /device:TPU:13, one launch (start us, length us, event | category | flops | bytes accessed | tf_op | source)
XLA Modules:
  0.0 241.0 jit_solution(985161979533679402)
XLA Ops:
  14.2 7.2 %collective-permute-done.1.refs_2_ = bf16[48,1664]{1,0:T(8,128)(2,1)S(1)} collective-permute-done((bf16[48,1664]{1,0:T(8,128)(2,1)S(1)}, bf16[48,1664]{1,0:T(8,128)(2,1)S(1)}, u32[]{:S(2)}, u32[]{:S(2)}) %collective-permute-start.1) | collective-permute-done | bytes 159776 | tf_op jit(solution)/shard_map/ppermute | solution.py:565
  21.4 3.9 %collective-permute-done.refs_1_ = bf16[48,1664]{1,0:T(8,128)(2,1)S(1)} collective-permute-done((bf16[48,1664]{1,0:T(8,128)(2,1)S(1)}, bf16[48,1664]{1,0:T(8,128)(2,1)S(1)}, u32[]{:S(2)}, u32[]{:S(2)}) %collective-permute-start) | collective-permute-done | bytes 159776 | tf_op jit(solution)/shard_map/ppermute | solution.py:565
  30.7 2.5 %collective-permute-start.10 = (bf16[48,1536]{1,0:T(8,128)(2,1)S(1)}, bf16[48,1536]{1,0:T(8,128)(2,1)S(1)}, u32[]{:S(2)}, u32[]{:S(2)}) collective-permute-start(bf16[48,1536]{1,0:T(8,128)(2,1)S(1)} %get-tuple-element.276.refs_0_), channel_id=1, source_target_pairs={{0,8},{1,9},{2,10},{3,11},{4,12},{5,13},{6,14},{7,15},{8,0},{9,1},... | collective-permute-start | bytes 442376 | tf_op jit(solution)/shard_map/ppermute | solution.py:565
  33.1 2.3 collective-permute-done.11.refs_3_
  35.5 5.6 %collective-permute-done.10.refs_2_ = bf16[48,1536]{1,0:T(8,128)(2,1)S(1)} collective-permute-done((bf16[48,1536]{1,0:T(8,128)(2,1)S(1)}, bf16[48,1536]{1,0:T(8,128)(2,1)S(1)}, u32[]{:S(2)}, u32[]{:S(2)}) %collective-permute-start.10) | collective-permute-done | bytes 147488 | tf_op jit(solution)/shard_map/ppermute | solution.py:565
  41.1 3.2 %collective-permute-done.9.refs_1_ = bf16[48,1536]{1,0:T(8,128)(2,1)S(1)} collective-permute-done((bf16[48,1536]{1,0:T(8,128)(2,1)S(1)}, bf16[48,1536]{1,0:T(8,128)(2,1)S(1)}, u32[]{:S(2)}, u32[]{:S(2)}) %collective-permute-start.9) | collective-permute-done | bytes 147488 | tf_op jit(solution)/shard_map/ppermute | solution.py:565
  48.3 2.5 %collective-permute-start.16 = (bf16[48,1536]{1,0:T(8,128)(2,1)S(1)}, bf16[48,1536]{1,0:T(8,128)(2,1)S(1)}, u32[]{:S(2)}, u32[]{:S(2)}) collective-permute-start(bf16[48,1536]{1,0:T(8,128)(2,1)S(1)} %get-tuple-element.287.refs_0_), channel_id=1, source_target_pairs={{0,8},{1,9},{2,10},{3,11},{4,12},{5,13},{6,14},{7,15},{8,0},{9,1},... | collective-permute-start | bytes 442376 | tf_op jit(solution)/shard_map/ppermute | solution.py:565
  52.4 6.4 %collective-permute-done.16.refs_2_ = bf16[48,1536]{1,0:T(8,128)(2,1)S(1)} collective-permute-done((bf16[48,1536]{1,0:T(8,128)(2,1)S(1)}, bf16[48,1536]{1,0:T(8,128)(2,1)S(1)}, u32[]{:S(2)}, u32[]{:S(2)}) %collective-permute-start.16) | collective-permute-done | bytes 147488 | tf_op jit(solution)/shard_map/ppermute | solution.py:565
  58.8 3.2 %collective-permute-done.15.refs_1_ = bf16[48,1536]{1,0:T(8,128)(2,1)S(1)} collective-permute-done((bf16[48,1536]{1,0:T(8,128)(2,1)S(1)}, bf16[48,1536]{1,0:T(8,128)(2,1)S(1)}, u32[]{:S(2)}, u32[]{:S(2)}) %collective-permute-start.15) | collective-permute-done | bytes 147488 | tf_op jit(solution)/shard_map/ppermute | solution.py:565
  66.7 3.9 %seg_qkv.1 = (bf16[16,48,1152]{2,1,0:T(8,128)(2,1)S(1)}, bf16[8,48,384]{2,1,0:T(8,128)(2,1)S(1)}, bf16[8,48,384]{2,1,0:T(8,128)(2,1)S(1)}, bf16[256,1152]{1,0:T(...) custom-call(s32[5]{0:T(128)S(1)} %stack.15.where, ...), custom_call_target="tpu_custom_call" | custom-call | flops 452984832 | bytes 11453440 | tf_op jit(solution)/shard_map/seg_qkv/pallas_call | solution.py:595
  70.6 4.1 %collective-permute-start.20 = (bf16[8,48,384]{2,1,0:T(8,128)(2,1)S(1)}, bf16[8,48,384]{2,1,0:T(8,128)(2,1)S(1)}, u32[]{:S(2)}, u32[]{:S(2)}) collective-permute-start(bf16[8,48,384]{2,1,0:T(8,128)(2,1)S(1)} %get-tuple-element.296.low), channel_id=1, source_target_pairs={{0,16},{16,0},{1,17},{17,1},{2,18},{18,2},{3,19},{19,3},{4,20},{20... | collective-permute-start | bytes 884744 | tf_op jit(solution)/shard_map/ppermute | solution.py:573
  77.0 3.1 %collective-permute-start.14 = (bf16[256,384]{1,0:T(8,128)(2,1)S(1)}, bf16[256,384]{1,0:T(8,128)(2,1)S(1)}, u32[]{:S(2)}, u32[]{:S(2)}) collective-permute-start(bf16[256,384]{1,0:T(8,128)(2,1)S(1)} %get-tuple-element.286.mixed), channel_id=1, source_target_pairs={{0,16},{16,0},{1,17},{17,1},{2,18},{18,2},{3,19},{19,3},{4,20},{20... | collective-permute-start | bytes 589832 | tf_op jit(solution)/shard_map/ppermute | solution.py:573
  83.2 3.3 %collective-permute-start.24 = (bf16[128,768]{1,0:T(8,128)(2,1)S(1)}, bf16[128,768]{1,0:T(8,128)(2,1)S(1)}, u32[]{:S(2)}, u32[]{:S(2)}) collective-permute-start(bf16[128,768]{1,0:T(8,128)(2,1)S(1)} %get-tuple-element.305.refs_12_.refs_0_.refs_6_), channel_id=1, source_target_pairs={{0,16},{16,0},{1,17},{17,1},{2,18},{18,2},{3,19},{19,3},{4,20},{20... | collective-permute-start | bytes 589832 | tf_op jit(solution)/shard_map/ppermute | solution.py:573
  92.6 3.0 %collective-permute-start.25 = (f32[128,768]{1,0:T(8,128)S(1)}, f32[128,768]{1,0:T(8,128)S(1)}, u32[]{:S(2)}, u32[]{:S(2)}) collective-permute-start(f32[128,768]{1,0:T(8,128)S(1)} %get-tuple-element.309), channel_id=1, source_target_pairs={{0,16},{16,0},{1,17},{17,1},{2,18},{18,2},{3,19},{19,3},{4,20},{20... | collective-permute-start | bytes 1179656 | tf_op jit(solution)/shard_map/ppermute | solution.py:573
  101.5 2.4 collective-permute-start.27
  105.6 2.9 %collective-permute-start.40 = (f32[4,1664]{1,0:T(4,128)S(1)}, f32[4,1664]{1,0:T(4,128)S(1)}, u32[]{:S(2)}, u32[]{:S(2)}) collective-permute-start(f32[4,1664]{1,0:T(4,128)S(1)} %pad_maximum_fusion.12.refs_0_), channel_id=1, source_target_pairs={{0,8},{1,9},{2,10},{3,11},{4,12},{5,13},{6,14},{7,15},{8,0},{9,1},... | collective-permute-start | bytes 79880 | tf_op jit(solution)/shard_map/ppermute | solution.py:565
  114.6 2.8 %collective-permute-start.42 = (bf16[16,48,1152]{2,1,0:T(8,128)(2,1)S(1)}, bf16[16,48,1152]{2,1,0:T(8,128)(2,1)S(1)}, u32[]{:S(2)}, u32[]{:S(2)}) collective-permute-start(bf16[16,48,1152]{2,1,0:T(8,128)(2,1)S(1)} %get-tuple-element.360.own), channel_id=1, source_target_pairs={{0,16},{16,0},{1,17},{17,1},{2,18},{18,2},{3,19},{19,3},{4,20},{20... | collective-permute-start | bytes 5308424 | tf_op jit(solution)/shard_map/ppermute | solution.py:573
  117.5 3.1 %seg_mlp_weight.1 = (bf16[2,48,3072]{2,1,0:T(8,128)(2,1)S(1)}, bf16[2,48,3072]{2,1,0:T(8,128)(2,1)S(1)}, bf16[4,48,3072]{2,1,0:T(8,128)(2,1)S(1)}, bf16[4,48,307...) custom-call(s32[5]{0:T(128)S(1)} %stack.15.where, bf16[128,768]{1,0:T(8,128)(2,1)S(1)} %get-tuple-element.305.refs_12_.refs_0_.refs_6_, ...), custom_call_target="tpu_custom_call" | custom-call | flops 1207959552 | bytes 7077888 | tf_op jit(solution)/shard_map/seg_mlp_weight/pallas_call | solution.py:595
  131.4 4.2 %collective-permute-done.47.refs_7_ = bf16[2,48,3072]{2,1,0:T(8,128)(2,1)S(1)} collective-permute-done((bf16[2,48,3072]{2,1,0:T(8,128)(2,1)S(1)}, bf16[2,48,3072]{2,1,0:T(8,128)(2,1)S(1)}, u32[]{:S(2)}, u32[]{:S(2)}) %collective-permute-start.47) | collective-permute-done | bytes 589856 | tf_op jit(solution)/shard_map/ppermute | solution.py:569
  141.4 2.4 collective-permute-start.49
  148.9 2.4 %collective-permute-start.53 = (f32[16,768]{1,0:T(8,128)S(1)}, f32[16,768]{1,0:T(8,128)S(1)}, u32[]{:S(2)}, u32[]{:S(2)}) collective-permute-start(f32[16,768]{1,0:T(8,128)S(1)} %get-tuple-element.388.refs_1_), channel_id=1, source_target_pairs={{0,8},{1,9},{2,10},{3,11},{4,12},{5,13},{6,14},{7,15},{8,0},{9,1},... | collective-permute-start | bytes 147464 | tf_op jit(solution)/shard_map/ppermute | solution.py:565
  160.3 2.3 collective-permute-done.56.refs_4_
  167.8 3.1 %collective-permute-start.60 = (f32[1,768]{1,0:T(1,128)S(1)}, f32[1,768]{1,0:T(1,128)S(1)}, u32[]{:S(2)}, u32[]{:S(2)}) collective-permute-start(f32[1,768]{1,0:T(1,128)S(1)} %get-tuple-element.414.refs_0_.refs_3_), channel_id=1, source_target_pairs={{0,16},{16,0},{1,17},{17,1},{2,18},{18,2},{3,19},{19,3},{4,20},{20... | collective-permute-start | bytes 9224 | tf_op jit(solution)/shard_map/ppermute | solution.py:573
  177.2 3.8 %seg_attn_back.1.refs_2_ = bf16[256,1152]{1,0:T(8,128)(2,1)S(1)} custom-call(s32[5]{0:T(128)S(1)} %stack.15.where, bf16[256,1152]{1,0:T(8,128)(2,1)S(1)} %get-tuple-element.300.refs_0_, bf16[128,768]{1,0:T(8,128)(2,1)S(1)} %get-tuple-element.419.refs_1_, bf16[128,768]{1,0:T(8,128)(2,1)S(1)} %collective-permute-done.62.refs_2_.refs_4_, ...), custom_call_target="tpu_custom_call" | custom-call | flops 452984832 | bytes 1573888 | tf_op jit(solution)/shard_map/seg_attn_back/pallas_call | solution.py:595
  183.4 2.8 %seg_attn_near.1 = (bf16[4,48,1536]{2,1,0:T(8,128)(2,1)S(1)}, bf16[4,48,1536]{2,1,0:T(8,128)(2,1)S(1)}, bf16[4,48,1536]{2,1,0:T(8,128)(2,1)S(1)}, bf16[128,768]{...) custom-call(s32[5]{0:T(128)S(1)} %stack.15.where, ...), custom_call_target="tpu_custom_call" | custom-call | flops 452984832 | bytes 7444992 | tf_op jit(solution)/shard_map/seg_attn_near/pallas_call | solution.py:595
  186.2 8.8 %collective-permute-done.66.refs_2_ = bf16[64,3072]{1,0:T(8,128)(2,1)S(1)} collective-permute-done((bf16[64,3072]{1,0:T(8,128)(2,1)S(1)}, bf16[64,3072]{1,0:T(8,128)(2,1)S(1)}, u32[]{:S(2)}, u32[]{:S(2)}) %collective-permute-start.66) | collective-permute-done | bytes 393248 | tf_op jit(solution)/shard_map/ppermute | solution.py:565
  200.5 7.6 %collective-permute-done.67.refs_1_ = bf16[64,3072]{1,0:T(8,128)(2,1)S(1)} collective-permute-done((bf16[64,3072]{1,0:T(8,128)(2,1)S(1)}, bf16[64,3072]{1,0:T(8,128)(2,1)S(1)}, u32[]{:S(2)}, u32[]{:S(2)}) %collective-permute-start.67) | collective-permute-done | bytes 393248 | tf_op jit(solution)/shard_map/ppermute | solution.py:565
  208.1 2.9 %collective-permute-start.77 = (bf16[24,768]{1,0:T(8,128)(2,1)S(1)}, bf16[24,768]{1,0:T(8,128)(2,1)S(1)}, u32[]{:S(2)}, u32[]{:S(2)}) collective-permute-start(bf16[24,768]{1,0:T(8,128)(2,1)S(1)} %get-tuple-element.472), channel_id=1, source_target_pairs={{0,12},{1,13},{2,14},{3,15},{4,0},{5,1},{6,2},{7,3},{8,4},{9,5},{1... | collective-permute-start | bytes 110600 | tf_op jit(solution)/shard_map/ppermute | solution.py:565
  220.5 4.2 %collective-permute-done.73 = bf16[48,1536]{1,0:T(8,128)(2,1)S(1)} collective-permute-done((bf16[48,1536]{1,0:T(8,128)(2,1)S(1)}, bf16[48,1536]{1,0:T(8,128)(2,1)S(1)}, u32[]{:S(2)}, u32[]{:S(2)}) %collective-permute-start.73) | collective-permute-done | bytes 147488 | tf_op jit(solution)/shard_map/ppermute | solution.py:565
  228.5 4.4 %head_owner.1 = (f32[48,3072]{1,0:T(8,128)S(1)}, f32[16,768]{1,0:T(8,128)S(1)}, f32[48,9216]{1,0:T(8,128)}, f32[576]{0:T(1024)}, f32[16,768]{1,0:T(8,128)}, /*index=5*/f32[1,1]{1,0:T(1,128)}) custom-call(s32[5]{0:T(128)S(1)} %stack.15.where, bf16[96,768]{1,0:T(8,128)(2,1)S(1)} %pad_maximum_fusion.11.refs_0_, ...), custom_call_target="tpu_custom_call" | custom-call | flops 28311552 | bytes 4503812 | tf_op jit(solution)/shard_map/head_owner/pallas_call | solution.py:595
  233.0 2.4 collective-permute-start.83
  237.5 3.3 %seg_owner.1 = (f32[48,9216]{1,0:T(8,128)}, f32[576]{0:T(1024)}) custom-call(s32[5]{0:T(128)S(1)} %stack.15.where, f32[48,1536]{1,0:T(8,128)S(1)} %convert_add_fusion.1.attn, f32[48,1536]{1,0:T(8,128)S(1)} %collective-permute-done.82.attn_got, f32[48,3072]{1,0:T(8,128)S(1)} %get-tuple-element.486.mlp, f32[48,3072]{1,0:T(8,128)S(1)} %collective-permute-done.83.mlp_got, ...), custom_call_target="tpu_custom_call" | custom-call | bytes 3639552 | tf_op jit(solution)/shard_map/seg_owner/pallas_call | solution.py:595
  (212 shorter events, 119.1 us)
Async XLA Ops:
  8.0 17.3 %collective-permute-start.3 = (bf16[48,4736]{1,0:T(8,128)(2,1)S(1)}, bf16[48,4736]{1,0:T(8,128)(2,1)S(1)}, u32[]{:S(2)}, u32[]{:S(2)}) collective-permute-start(bf16[48,4736]{1,0:T(8,128)(2,1)S(1)} %pad_maximum_fusion.10), channel_id=1, source_target_pairs={{0,1},{1,0},{2,3},{3,2},{4,5},{5,4},{6,7},{7,6},{8,9},{9,8},{10,11... | collective-permute-start | bytes 1363976 | tf_op jit(solution)/shard_map/ppermute | solution.py:569
  9.3 16.0 %collective-permute-start.4 = (bf16[48,4736]{1,0:T(8,128)(2,1)S(1)}, bf16[48,4736]{1,0:T(8,128)(2,1)S(1)}, u32[]{:S(2)}, u32[]{:S(2)}) collective-permute-start(bf16[48,4736]{1,0:T(8,128)(2,1)S(1)} %pad_maximum_fusion.10), channel_id=1, source_target_pairs={{0,2},{1,3},{2,0},{3,1},{4,6},{5,7},{6,4},{7,5},{8,10},{9,11},{10,... | collective-permute-start | bytes 1363976 | tf_op jit(solution)/shard_map/ppermute | solution.py:569
  9.7 11.7 %collective-permute-start.1 = (bf16[48,1664]{1,0:T(8,128)(2,1)S(1)}, bf16[48,1664]{1,0:T(8,128)(2,1)S(1)}, u32[]{:S(2)}, u32[]{:S(2)}) collective-permute-start(bf16[48,1664]{1,0:T(8,128)(2,1)S(1)} %get-tuple-element.255.refs_0_), channel_id=1, source_target_pairs={{0,8},{1,9},{2,10},{3,11},{4,12},{5,13},{6,14},{7,15},{8,0},{9,1},... | collective-permute-start | bytes 479240 | tf_op jit(solution)/shard_map/ppermute | solution.py:565
  12.0 13.3 %collective-permute-start = (bf16[48,1664]{1,0:T(8,128)(2,1)S(1)}, bf16[48,1664]{1,0:T(8,128)(2,1)S(1)}, u32[]{:S(2)}, u32[]{:S(2)}) collective-permute-start(bf16[48,1664]{1,0:T(8,128)(2,1)S(1)} %get-tuple-element.255.refs_0_), channel_id=1, source_target_pairs={{0,4},{1,5},{2,6},{3,7},{4,8},{5,9},{6,10},{7,11},{8,12},{9,13},{1... | collective-permute-start | bytes 479240 | tf_op jit(solution)/shard_map/ppermute | solution.py:565
  28.2 18.1 %collective-permute-start.8 = (bf16[48,7424]{1,0:T(8,128)(2,1)S(1)}, bf16[48,7424]{1,0:T(8,128)(2,1)S(1)}, u32[]{:S(2)}, u32[]{:S(2)}) collective-permute-start(bf16[48,7424]{1,0:T(8,128)(2,1)S(1)} %pad_maximum_fusion.6), channel_id=1, source_target_pairs={{0,2},{1,3},{2,0},{3,1},{4,6},{5,7},{6,4},{7,5},{8,10},{9,11},{10,... | collective-permute-start | bytes 2138120 | tf_op jit(solution)/shard_map/ppermute | solution.py:569
  29.5 16.8 %collective-permute-start.7 = (bf16[48,7296]{1,0:T(8,128)(2,1)S(1)}, bf16[48,7296]{1,0:T(8,128)(2,1)S(1)}, u32[]{:S(2)}, u32[]{:S(2)}) collective-permute-start(bf16[48,7296]{1,0:T(8,128)(2,1)S(1)} %pad_maximum_fusion.7), channel_id=1, source_target_pairs={{0,1},{1,0},{2,3},{3,2},{4,5},{5,4},{6,7},{7,6},{8,9},{9,8},{10,11... | collective-permute-start | bytes 2101256 | tf_op jit(solution)/shard_map/ppermute | solution.py:569
  30.7 10.5 %collective-permute-start.10 = (bf16[48,1536]{1,0:T(8,128)(2,1)S(1)}, bf16[48,1536]{1,0:T(8,128)(2,1)S(1)}, u32[]{:S(2)}, u32[]{:S(2)}) collective-permute-start(bf16[48,1536]{1,0:T(8,128)(2,1)S(1)} %get-tuple-element.276.refs_0_), channel_id=1, source_target_pairs={{0,8},{1,9},{2,10},{3,11},{4,12},{5,13},{6,14},{7,15},{8,0},{9,1},... | collective-permute-start | bytes 442376 | tf_op jit(solution)/shard_map/ppermute | solution.py:565
  33.1 11.1 %collective-permute-start.9 = (bf16[48,1536]{1,0:T(8,128)(2,1)S(1)}, bf16[48,1536]{1,0:T(8,128)(2,1)S(1)}, u32[]{:S(2)}, u32[]{:S(2)}) collective-permute-start(bf16[48,1536]{1,0:T(8,128)(2,1)S(1)} %get-tuple-element.276.refs_0_), channel_id=1, source_target_pairs={{0,4},{1,5},{2,6},{3,7},{4,8},{5,9},{6,10},{7,11},{8,12},{9,13},{1... | collective-permute-start | bytes 442376 | tf_op jit(solution)/shard_map/ppermute | solution.py:565
  46.5 16.1 %collective-permute-start.13 = (bf16[48,7168]{1,0:T(8,128)(2,1)S(1)}, bf16[48,7168]{1,0:T(8,128)(2,1)S(1)}, u32[]{:S(2)}, u32[]{:S(2)}) collective-permute-start(bf16[48,7168]{1,0:T(8,128)(2,1)S(1)} %pad_maximum_fusion.8), channel_id=1, source_target_pairs={{0,2},{1,3},{2,0},{3,1},{4,6},{5,7},{6,4},{7,5},{8,10},{9,11},{10,... | collective-permute-start | bytes 2064392 | tf_op jit(solution)/shard_map/ppermute | solution.py:569
  47.1 15.4 %collective-permute-start.12 = (bf16[48,7040]{1,0:T(8,128)(2,1)S(1)}, bf16[48,7040]{1,0:T(8,128)(2,1)S(1)}, u32[]{:S(2)}, u32[]{:S(2)}) collective-permute-start(bf16[48,7040]{1,0:T(8,128)(2,1)S(1)} %pad_maximum_fusion.9), channel_id=1, source_target_pairs={{0,1},{1,0},{2,3},{3,2},{4,5},{5,4},{6,7},{7,6},{8,9},{9,8},{10,11... | collective-permute-start | bytes 2027528 | tf_op jit(solution)/shard_map/ppermute | solution.py:569
  48.3 10.5 %collective-permute-start.16 = (bf16[48,1536]{1,0:T(8,128)(2,1)S(1)}, bf16[48,1536]{1,0:T(8,128)(2,1)S(1)}, u32[]{:S(2)}, u32[]{:S(2)}) collective-permute-start(bf16[48,1536]{1,0:T(8,128)(2,1)S(1)} %get-tuple-element.287.refs_0_), channel_id=1, source_target_pairs={{0,8},{1,9},{2,10},{3,11},{4,12},{5,13},{6,14},{7,15},{8,0},{9,1},... | collective-permute-start | bytes 442376 | tf_op jit(solution)/shard_map/ppermute | solution.py:565
  50.8 11.2 %collective-permute-start.15 = (bf16[48,1536]{1,0:T(8,128)(2,1)S(1)}, bf16[48,1536]{1,0:T(8,128)(2,1)S(1)}, u32[]{:S(2)}, u32[]{:S(2)}) collective-permute-start(bf16[48,1536]{1,0:T(8,128)(2,1)S(1)} %get-tuple-element.287.refs_0_), channel_id=1, source_target_pairs={{0,4},{1,5},{2,6},{3,7},{4,8},{5,9},{6,10},{7,11},{8,12},{9,13},{1... | collective-permute-start | bytes 442376 | tf_op jit(solution)/shard_map/ppermute | solution.py:565
  62.7 14.3 %collective-permute-start.18 = (bf16[48,6912]{1,0:T(8,128)(2,1)S(1)}, bf16[48,6912]{1,0:T(8,128)(2,1)S(1)}, u32[]{:S(2)}, u32[]{:S(2)}) collective-permute-start(bf16[48,6912]{1,0:T(8,128)(2,1)S(1)} %get-tuple-element.291), channel_id=1, source_target_pairs={{0,1},{1,0},{2,3},{3,2},{4,5},{5,4},{6,7},{7,6},{8,9},{9,8},{10,11... | collective-permute-start | bytes 1990664 | tf_op jit(solution)/shard_map/ppermute | solution.py:569
  63.4 11.2 %collective-permute-start.32 = (bf16[48,1152]{1,0:T(8,128)(2,1)S(1)}, bf16[48,1152]{1,0:T(8,128)(2,1)S(1)}, u32[]{:S(2)}, u32[]{:S(2)}) collective-permute-start(bf16[48,1152]{1,0:T(8,128)(2,1)S(1)} %get-tuple-element.330), channel_id=1, source_target_pairs={{0,4},{1,5},{2,6},{3,7},{4,8},{5,9},{6,10},{7,11},{8,12},{9,13},{1... | collective-permute-start | bytes 331784 | tf_op jit(solution)/shard_map/ppermute | solution.py:565
  65.6 14.5 %collective-permute-start.19 = (bf16[48,6912]{1,0:T(8,128)(2,1)S(1)}, bf16[48,6912]{1,0:T(8,128)(2,1)S(1)}, u32[]{:S(2)}, u32[]{:S(2)}) collective-permute-start(bf16[48,6912]{1,0:T(8,128)(2,1)S(1)} %get-tuple-element.292), channel_id=1, source_target_pairs={{0,2},{1,3},{2,0},{3,1},{4,6},{5,7},{6,4},{7,5},{8,10},{9,11},{10,... | collective-permute-start | bytes 1990664 | tf_op jit(solution)/shard_map/ppermute | solution.py:569
  70.6 11.2 %collective-permute-start.20 = (bf16[8,48,384]{2,1,0:T(8,128)(2,1)S(1)}, bf16[8,48,384]{2,1,0:T(8,128)(2,1)S(1)}, u32[]{:S(2)}, u32[]{:S(2)}) collective-permute-start(bf16[8,48,384]{2,1,0:T(8,128)(2,1)S(1)} %get-tuple-element.296.low), channel_id=1, source_target_pairs={{0,16},{16,0},{1,17},{17,1},{2,18},{18,2},{3,19},{19,3},{4,20},{20... | collective-permute-start | bytes 884744 | tf_op jit(solution)/shard_map/ppermute | solution.py:573
  74.8 11.8 %collective-permute-start.34 = (bf16[48,1152]{1,0:T(8,128)(2,1)S(1)}, bf16[48,1152]{1,0:T(8,128)(2,1)S(1)}, u32[]{:S(2)}, u32[]{:S(2)}) collective-permute-start(bf16[48,1152]{1,0:T(8,128)(2,1)S(1)} %get-tuple-element.334), channel_id=1, source_target_pairs={{0,12},{1,13},{2,14},{3,15},{4,0},{5,1},{6,2},{7,3},{8,4},{9,5},{1... | collective-permute-start | bytes 331784 | tf_op jit(solution)/shard_map/ppermute | solution.py:565
  89.5 14.4 %collective-permute-start.35 = (bf16[48,4992]{1,0:T(8,128)(2,1)S(1)}, bf16[48,4992]{1,0:T(8,128)(2,1)S(1)}, u32[]{:S(2)}, u32[]{:S(2)}) collective-permute-start(bf16[48,4992]{1,0:T(8,128)(2,1)S(1)} %constant_dynamic-update-slice_fusion), channel_id=1, source_target_pairs={{0,1},{1,0},{2,3},{3,2},{4,5},{5,4},{6,7},{7,6},{8,9},{9,8},{10,11... | collective-permute-start | bytes 1437704 | tf_op jit(solution)/shard_map/ppermute | solution.py:569
  90.4 13.5 %collective-permute-start.36 = (bf16[48,4992]{1,0:T(8,128)(2,1)S(1)}, bf16[48,4992]{1,0:T(8,128)(2,1)S(1)}, u32[]{:S(2)}, u32[]{:S(2)}) collective-permute-start(bf16[48,4992]{1,0:T(8,128)(2,1)S(1)} %constant_dynamic-update-slice_fusion), channel_id=1, source_target_pairs={{0,2},{1,3},{2,0},{3,1},{4,6},{5,7},{6,4},{7,5},{8,10},{9,11},{10,... | collective-permute-start | bytes 1437704 | tf_op jit(solution)/shard_map/ppermute | solution.py:569
  120.6 15.0 %collective-permute-start.47 = (bf16[2,48,3072]{2,1,0:T(8,128)(2,1)S(1)}, bf16[2,48,3072]{2,1,0:T(8,128)(2,1)S(1)}, u32[]{:S(2)}, u32[]{:S(2)}) collective-permute-start(bf16[2,48,3072]{2,1,0:T(8,128)(2,1)S(1)} %get-tuple-element.375), channel_id=1, source_target_pairs={{0,2},{1,3},{2,0},{3,1},{4,6},{5,7},{6,4},{7,5},{8,10},{9,11},{10,... | collective-permute-start | bytes 1769480 | tf_op jit(solution)/shard_map/ppermute | solution.py:569
  121.6 14.6 %collective-permute-start.48 = (bf16[2,48,3072]{2,1,0:T(8,128)(2,1)S(1)}, bf16[2,48,3072]{2,1,0:T(8,128)(2,1)S(1)}, u32[]{:S(2)}, u32[]{:S(2)}) collective-permute-start(bf16[2,48,3072]{2,1,0:T(8,128)(2,1)S(1)} %get-tuple-element.377), channel_id=1, source_target_pairs={{0,1},{1,0},{2,3},{3,2},{4,5},{5,4},{6,7},{7,6},{8,9},{9,8},{10,11... | collective-permute-start | bytes 1769480 | tf_op jit(solution)/shard_map/ppermute | solution.py:569
  137.7 26.4 %collective-permute-start.58 = (bf16[4,48,3072]{2,1,0:T(8,128)(2,1)S(1)}, bf16[4,48,3072]{2,1,0:T(8,128)(2,1)S(1)}, u32[]{:S(2)}, u32[]{:S(2)}) collective-permute-start(bf16[4,48,3072]{2,1,0:T(8,128)(2,1)S(1)} %get-tuple-element.406), channel_id=1, source_target_pairs={{0,1},{1,0},{2,3},{3,2},{4,5},{5,4},{6,7},{7,6},{8,9},{9,8},{10,11... | collective-permute-start | bytes 3538952 | tf_op jit(solution)/shard_map/ppermute | solution.py:569
  138.4 26.1 %collective-permute-start.59 = (bf16[4,48,3072]{2,1,0:T(8,128)(2,1)S(1)}, bf16[4,48,3072]{2,1,0:T(8,128)(2,1)S(1)}, u32[]{:S(2)}, u32[]{:S(2)}) collective-permute-start(bf16[4,48,3072]{2,1,0:T(8,128)(2,1)S(1)} %get-tuple-element.407), channel_id=1, source_target_pairs={{0,2},{1,3},{2,0},{3,1},{4,6},{5,7},{6,4},{7,5},{8,10},{9,11},{10,... | collective-permute-start | bytes 3538952 | tf_op jit(solution)/shard_map/ppermute | solution.py:569
  166.0 16.1 %collective-permute-start.63 = (bf16[64,3072]{1,0:T(8,128)(2,1)S(1)}, bf16[64,3072]{1,0:T(8,128)(2,1)S(1)}, u32[]{:S(2)}, u32[]{:S(2)}) collective-permute-start(bf16[64,3072]{1,0:T(8,128)(2,1)S(1)} %get-tuple-element.433), channel_id=1, source_target_pairs={{0,12},{1,13},{2,14},{3,15},{4,0},{5,1},{6,2},{7,3},{8,4},{9,5},{1... | collective-permute-start | bytes 1179656 | tf_op jit(solution)/shard_map/ppermute | solution.py:565
  176.1 18.8 %collective-permute-start.66 = (bf16[64,3072]{1,0:T(8,128)(2,1)S(1)}, bf16[64,3072]{1,0:T(8,128)(2,1)S(1)}, u32[]{:S(2)}, u32[]{:S(2)}) collective-permute-start(bf16[64,3072]{1,0:T(8,128)(2,1)S(1)} %get-tuple-element.440), channel_id=1, source_target_pairs={{0,8},{1,9},{2,10},{3,11},{4,12},{5,13},{6,14},{7,15},{8,0},{9,1},... | collective-permute-start | bytes 1179656 | tf_op jit(solution)/shard_map/ppermute | solution.py:565
  182.1 12.9 %collective-permute-start.64 = (bf16[2,48,1536]{2,1,0:T(8,128)(2,1)S(1)}, bf16[2,48,1536]{2,1,0:T(8,128)(2,1)S(1)}, u32[]{:S(2)}, u32[]{:S(2)}) collective-permute-start(bf16[2,48,1536]{2,1,0:T(8,128)(2,1)S(1)} %get-tuple-element.434), channel_id=1, source_target_pairs={{0,2},{1,3},{2,0},{3,1},{4,6},{5,7},{6,4},{7,5},{8,10},{9,11},{10,... | collective-permute-start | bytes 884744 | tf_op jit(solution)/shard_map/ppermute | solution.py:569
  182.8 12.2 %collective-permute-start.65 = (bf16[2,48,1536]{2,1,0:T(8,128)(2,1)S(1)}, bf16[2,48,1536]{2,1,0:T(8,128)(2,1)S(1)}, u32[]{:S(2)}, u32[]{:S(2)}) collective-permute-start(bf16[2,48,1536]{2,1,0:T(8,128)(2,1)S(1)} %get-tuple-element.436), channel_id=1, source_target_pairs={{0,1},{1,0},{2,3},{3,2},{4,5},{5,4},{6,7},{7,6},{8,9},{9,8},{10,11... | collective-permute-start | bytes 884744 | tf_op jit(solution)/shard_map/ppermute | solution.py:569
  195.6 16.6 %collective-permute-start.68 = (bf16[4,48,1536]{2,1,0:T(8,128)(2,1)S(1)}, bf16[4,48,1536]{2,1,0:T(8,128)(2,1)S(1)}, u32[]{:S(2)}, u32[]{:S(2)}) collective-permute-start(bf16[4,48,1536]{2,1,0:T(8,128)(2,1)S(1)} %get-tuple-element.446), channel_id=1, source_target_pairs={{0,1},{1,0},{2,3},{3,2},{4,5},{5,4},{6,7},{7,6},{8,9},{9,8},{10,11... | collective-permute-start | bytes 1769480 | tf_op jit(solution)/shard_map/ppermute | solution.py:569
  196.3 15.9 %collective-permute-start.69 = (bf16[4,48,1536]{2,1,0:T(8,128)(2,1)S(1)}, bf16[4,48,1536]{2,1,0:T(8,128)(2,1)S(1)}, u32[]{:S(2)}, u32[]{:S(2)}) collective-permute-start(bf16[4,48,1536]{2,1,0:T(8,128)(2,1)S(1)} %get-tuple-element.447), channel_id=1, source_target_pairs={{0,2},{1,3},{2,0},{3,1},{4,6},{5,7},{6,4},{7,5},{8,10},{9,11},{10,... | collective-permute-start | bytes 1769480 | tf_op jit(solution)/shard_map/ppermute | solution.py:569
  197.0 11.0 %collective-permute-start.67 = (bf16[64,3072]{1,0:T(8,128)(2,1)S(1)}, bf16[64,3072]{1,0:T(8,128)(2,1)S(1)}, u32[]{:S(2)}, u32[]{:S(2)}) collective-permute-start(bf16[64,3072]{1,0:T(8,128)(2,1)S(1)} %get-tuple-element.445), channel_id=1, source_target_pairs={{0,4},{1,5},{2,6},{3,7},{4,8},{5,9},{6,10},{7,11},{8,12},{9,13},{1... | collective-permute-start | bytes 1179656 | tf_op jit(solution)/shard_map/ppermute | solution.py:565
  216.0 12.6 %collective-permute-start.80 = (bf16[96,768]{1,0:T(8,128)(2,1)S(1)}, bf16[96,768]{1,0:T(8,128)(2,1)S(1)}, u32[]{:S(2)}, u32[]{:S(2)}) collective-permute-start(bf16[96,768]{1,0:T(8,128)(2,1)S(1)} %pad_maximum_fusion.11.refs_0_), channel_id=1, source_target_pairs={{0,3},{1,2},{2,1},{3,0},{4,7},{5,6},{6,5},{7,4},{8,11},{9,10},{10,... | collective-permute-start | bytes 442376 | tf_op jit(solution)/shard_map/ppermute | solution.py:569
  217.4 11.2 %collective-permute-start.79 = (bf16[96,768]{1,0:T(8,128)(2,1)S(1)}, bf16[96,768]{1,0:T(8,128)(2,1)S(1)}, u32[]{:S(2)}, u32[]{:S(2)}) collective-permute-start(bf16[96,768]{1,0:T(8,128)(2,1)S(1)} %pad_maximum_fusion.11.refs_0_), channel_id=1, source_target_pairs={{0,2},{1,3},{2,0},{3,1},{4,6},{5,7},{6,4},{7,5},{8,10},{9,11},{10,... | collective-permute-start | bytes 442376 | tf_op jit(solution)/shard_map/ppermute | solution.py:569
  (61 other events, 314.1 us)

commit v13 on v12

--- a/solution.py
+++ b/solution.py
@@ -999,7 +999,9 @@
     head_out[:, 2 * MODEL :] = facts
 
 
-def second_norm_kernel(where, diff, count, normed, inv_dev, vectors, grad_out, low_out, sums_out):
+def second_norm_kernel(where, *refs):
+    diff, count, normed, inv_dev, vectors, first, first_got, order = refs[:8]
+    grad_out, low_out, sums_out, ordered_out, both = refs[8:]
     grad_top = diff[...] * ((SEG * GROUP * CORES) / count[0:1, 0:1])
     normed_rows = normed[...]
     grad = norm_rows_back(grad_top, normed_rows, inv_dev[...], vectors[6:7, :])
@@ -1009,6 +1011,9 @@
     sums_out[0:1, :] = column_sum(low)
     sums_out[1:2, :] = column_sum(grad_top * normed_rows)
     sums_out[2:3, :] = column_sum(grad_top)
+    both[:SEG] = first[...]
+    both[SEG:] = first_got[...]
+    ordered_out[...] = product_plain(both[...], order[...]).astype(LOW)
 
 
 def mlp_back_kernel(where, *refs):
@@ -1046,19 +1051,40 @@
     wait_all(copies)
 
 
-def mlp_weight_kernel(where, *refs):
-    first, first_got, second, second_got, pre, act = refs[:6]
-    outs = refs[6:11]
-    left, parts, sems = refs[11:]
-    for at, (own, got, right) in enumerate(((first, first_got, pre), (second, second_got, act))):
-        left[:SEG] = own[...]
-        left[SEG:] = got[...]
-        for piece in range(FF_HALF // MODEL):
-            start = piece * MODEL
-            product = product_left(left[...], right[:, start : start + MODEL]).astype(LOW)
-            target = at * FF_HALF + start
-            parts[:, :, target : target + MODEL] = product.reshape(GROUP, OWN, MODEL)
-    scatter_parts(where, parts, outs, sems)
+def mlp_products(refs, masks, both, store):
+    first, second, second_got, pre, act, order = refs
+    both[:SEG] = second[...]
+    both[SEG:] = second_got[...]
+    for mask in masks:
+        lanes = slice(mask * SPAN, (mask + 1) * SPAN)
+        turned = product_plain(both[...], order[:, lanes]).astype(LOW)
+        for at, (left, right) in enumerate(((first[:, lanes], pre), (turned, act))):
+            for piece in range(FF_HALF // MODEL):
+                start = piece * MODEL
+                product = product_left(left, right[:, start : start + MODEL])
+                product = product[: LINE * OWN].astype(LOW).reshape(LINE, OWN, MODEL)
+                target = at * FF_HALF + start
+                store(mask, slice(target, target + MODEL), product)
+
+
+def mlp_far_kernel(where, *refs):
+    low_out, high_out, both = refs[6:]
+    half = LINE // 2
+
+    def store(mask, columns, product):
+        low_out[:, :, columns] = product[:half]
+        high_out[:, :, columns] = product[half:]
+
+    mlp_products(refs[:6], (3,), both, store)
+
+
+def mlp_near_kernel(where, *refs):
+    outs, both = refs[6:9], refs[9]
+
+    def store(mask, columns, product):
+        outs[mask - 1][:, :, columns] = product
+
+    mlp_products(refs[:6], (1, 2, 0), both, store)
 
 
 def attn_product(where, refs, mask, piece):
@@ -1791,13 +1817,19 @@
         after(cls_y[:, size:], *head_planes[1:]), after(cls_x[:, :size], *head_planes[1:])
     )
 
-    second_grad, second_low, second_sums = run_kernel(
+    second_grad, second_low, second_sums, first_ordered = run_kernel(
         second_norm_kernel,
         "seg_second_norm",
-        [shape_of((SEG, MODEL)), shape_of((SEG, MODEL), LOW), shape_of((3, MODEL))],
-        where,
-        (),
-        (diff, count, normed_second, inv_second, vectors),
+        [
+            shape_of((SEG, MODEL)),
+            shape_of((SEG, MODEL), LOW),
+            shape_of((3, MODEL)),
+            shape_of((both_rows, PLANE * SPAN), LOW),
+        ],
+        where,
+        (),
+        (diff, count, normed_second, inv_second, vectors, first_low, first_got, order),
+        [pltpu.VMEM((both_rows, MODEL), LOW)],
     )
     second_got = other_core(second_low)
     pre, first_grad_own, first_grad_send, up_sums = run_kernel(
@@ -1836,20 +1868,28 @@
         (),
         cls_line + (cls_x, cls_y) + cls_far + (cls_out_piece,),
     )
-    mlp_parts = run_kernel(
-        mlp_weight_kernel,
-        "seg_mlp_weight",
-        part_shapes(FF),
-        where,
-        (),
-        (first_low, first_got, second_low, second_got, after(pre, cls_half), act),
-        [
-            pltpu.VMEM((both_rows, MODEL), LOW),
-            pltpu.VMEM((GROUP, own_rows, FF), LOW),
-            pltpu.SemaphoreType.DMA((GROUP,)),
-        ],
-        far=range(5),
-        flops=4 * SEG * MODEL * FF,
+    mlp_data = (first_ordered, second_low, second_got, after(pre, cls_half), act, order)
+    mlp_far = run_kernel(
+        mlp_far_kernel,
+        "seg_mlp_far",
+        part_shapes(FF)[:2],
+        where,
+        (),
+        mlp_data,
+        [pltpu.VMEM((both_rows, MODEL), LOW)],
+        flops=SEG * MODEL * FF,
+    )
+    mlp_parts = list(mlp_far) + list(
+        run_kernel(
+            mlp_near_kernel,
+            "seg_mlp_near",
+            part_shapes(FF)[2:],
+            where,
+            (),
+            mlp_data,
+            [pltpu.VMEM((both_rows, MODEL), LOW)],
+            flops=3 * SEG * MODEL * FF,
+        )
     )
     mlp_far = reduce_far(tuple(after(part, *cls_far) for part in mlp_parts[:2]))
     cls_weight, cls_out = run_kernel(

time: 243 us -> 241 us (level)
  waiting for transfers between devices: 87.1 us -> 84.6 us
    ppermute x28, waiting for transfers between devices: 11.6 us -> 9.17 us  [in_plane(): return lax.ppermute(value, 'fsdp', plane_pairs(mask))]
    pallas_call x26 -> x27, Pallas kernels: 48.2 us -> 49.2 us  [run_kernel(): pl.pallas_call(body, name=name, out_shape=tuple(outs), in_specs=in_specs,...]
where the time goes in v13:
time: 241 us; the launch traced here: 239 us
  starting transfers between devices  97.4 us (40%)
  waiting for transfers between devices  84.6 us (35%)
  Pallas kernels  49.2 us (20%)
  local copies, waits for them, and re-layouts  5.34 us (2%)
    ppermute x36, waiting for transfers between devices, along_line(): return lax.ppermute(value, 'fsdp', line_pairs(apart))  65 us
    pallas_call x27, Pallas kernels, run_kernel(): pl.pallas_call(body, name=name, out_shape=tuple(outs), in_specs=in_specs,...  49.2 us
    ppermute x36, starting transfers between devices, along_line(): return lax.ppermute(value, 'fsdp', line_pairs(apart))  45.5 us
    ppermute x21, starting transfers between devices, other_core(): return lax.ppermute(value, 'rep', [(0, 1), (1, 0)])  30.8 us
    ppermute x28, starting transfers between devices, in_plane(): return lax.ppermute(value, 'fsdp', plane_pairs(mask))  21.1 us
    ppermute x21, waiting for transfers between devices, other_core(): return lax.ppermute(value, 'rep', [(0, 1), (1, 0)])  10.4 us
    ppermute x28, waiting for transfers between devices, in_plane(): return lax.ppermute(value, 'fsdp', plane_pairs(mask))  9.17 us
  transfers between devices with their start and end apart: 85, of which 40 were waited for; matrix products, arithmetic and copies ran while one was open for 0% of the time, Pallas kernels for 14%

profile of v13, /device:TPU:13, one launch (start us, length us, event | category | flops | bytes accessed | tf_op | source)
XLA Modules:
  0.0 239.2 jit_solution(584220188822375901)
XLA Ops:
  9.7 2.3 collective-permute-start.1
  14.2 7.2 %collective-permute-done.1.refs_2_ = bf16[48,1664]{1,0:T(8,128)(2,1)S(1)} collective-permute-done((bf16[48,1664]{1,0:T(8,128)(2,1)S(1)}, bf16[48,1664]{1,0:T(8,128)(2,1)S(1)}, u32[]{:S(2)}, u32[]{:S(2)}) %collective-permute-start.1) | collective-permute-done | bytes 159776 | tf_op jit(solution)/shard_map/ppermute | solution.py:565
  21.4 3.9 %collective-permute-done.refs_1_ = bf16[48,1664]{1,0:T(8,128)(2,1)S(1)} collective-permute-done((bf16[48,1664]{1,0:T(8,128)(2,1)S(1)}, bf16[48,1664]{1,0:T(8,128)(2,1)S(1)}, u32[]{:S(2)}, u32[]{:S(2)}) %collective-permute-start) | collective-permute-done | bytes 159776 | tf_op jit(solution)/shard_map/ppermute | solution.py:565
  30.7 2.5 %collective-permute-start.10 = (bf16[48,1536]{1,0:T(8,128)(2,1)S(1)}, bf16[48,1536]{1,0:T(8,128)(2,1)S(1)}, u32[]{:S(2)}, u32[]{:S(2)}) collective-permute-start(bf16[48,1536]{1,0:T(8,128)(2,1)S(1)} %get-tuple-element.277.refs_0_), channel_id=1, source_target_pairs={{0,8},{1,9},{2,10},{3,11},{4,12},{5,13},{6,14},{7,15},{8,0},{9,1},... | collective-permute-start | bytes 442376 | tf_op jit(solution)/shard_map/ppermute | solution.py:565
  33.1 2.3 collective-permute-done.11.refs_3_
  35.5 5.6 %collective-permute-done.10.refs_2_ = bf16[48,1536]{1,0:T(8,128)(2,1)S(1)} collective-permute-done((bf16[48,1536]{1,0:T(8,128)(2,1)S(1)}, bf16[48,1536]{1,0:T(8,128)(2,1)S(1)}, u32[]{:S(2)}, u32[]{:S(2)}) %collective-permute-start.10) | collective-permute-done | bytes 147488 | tf_op jit(solution)/shard_map/ppermute | solution.py:565
  41.1 3.2 %collective-permute-done.9.refs_1_ = bf16[48,1536]{1,0:T(8,128)(2,1)S(1)} collective-permute-done((bf16[48,1536]{1,0:T(8,128)(2,1)S(1)}, bf16[48,1536]{1,0:T(8,128)(2,1)S(1)}, u32[]{:S(2)}, u32[]{:S(2)}) %collective-permute-start.9) | collective-permute-done | bytes 147488 | tf_op jit(solution)/shard_map/ppermute | solution.py:565
  48.3 2.5 %collective-permute-start.16 = (bf16[48,1536]{1,0:T(8,128)(2,1)S(1)}, bf16[48,1536]{1,0:T(8,128)(2,1)S(1)}, u32[]{:S(2)}, u32[]{:S(2)}) collective-permute-start(bf16[48,1536]{1,0:T(8,128)(2,1)S(1)} %get-tuple-element.288.refs_0_), channel_id=1, source_target_pairs={{0,8},{1,9},{2,10},{3,11},{4,12},{5,13},{6,14},{7,15},{8,0},{9,1},... | collective-permute-start | bytes 442376 | tf_op jit(solution)/shard_map/ppermute | solution.py:565
  52.4 6.4 %collective-permute-done.16.refs_2_ = bf16[48,1536]{1,0:T(8,128)(2,1)S(1)} collective-permute-done((bf16[48,1536]{1,0:T(8,128)(2,1)S(1)}, bf16[48,1536]{1,0:T(8,128)(2,1)S(1)}, u32[]{:S(2)}, u32[]{:S(2)}) %collective-permute-start.16) | collective-permute-done | bytes 147488 | tf_op jit(solution)/shard_map/ppermute | solution.py:565
  58.8 3.2 %collective-permute-done.15.refs_1_ = bf16[48,1536]{1,0:T(8,128)(2,1)S(1)} collective-permute-done((bf16[48,1536]{1,0:T(8,128)(2,1)S(1)}, bf16[48,1536]{1,0:T(8,128)(2,1)S(1)}, u32[]{:S(2)}, u32[]{:S(2)}) %collective-permute-start.15) | collective-permute-done | bytes 147488 | tf_op jit(solution)/shard_map/ppermute | solution.py:565
  66.7 3.9 %seg_qkv.1 = (bf16[16,48,1152]{2,1,0:T(8,128)(2,1)S(1)}, bf16[8,48,384]{2,1,0:T(8,128)(2,1)S(1)}, bf16[8,48,384]{2,1,0:T(8,128)(2,1)S(1)}, bf16[256,1152]{1,0:T(...) custom-call(s32[5]{0:T(128)S(1)} %stack.15.where, ...), custom_call_target="tpu_custom_call" | custom-call | flops 452984832 | bytes 11453440 | tf_op jit(solution)/shard_map/seg_qkv/pallas_call | solution.py:595
  70.6 4.1 %collective-permute-start.20 = (bf16[8,48,384]{2,1,0:T(8,128)(2,1)S(1)}, bf16[8,48,384]{2,1,0:T(8,128)(2,1)S(1)}, u32[]{:S(2)}, u32[]{:S(2)}) collective-permute-start(bf16[8,48,384]{2,1,0:T(8,128)(2,1)S(1)} %get-tuple-element.297.low), channel_id=1, source_target_pairs={{0,16},{16,0},{1,17},{17,1},{2,18},{18,2},{3,19},{19,3},{4,20},{20... | collective-permute-start | bytes 884744 | tf_op jit(solution)/shard_map/ppermute | solution.py:573
  77.0 3.1 %collective-permute-start.14 = (bf16[256,384]{1,0:T(8,128)(2,1)S(1)}, bf16[256,384]{1,0:T(8,128)(2,1)S(1)}, u32[]{:S(2)}, u32[]{:S(2)}) collective-permute-start(bf16[256,384]{1,0:T(8,128)(2,1)S(1)} %get-tuple-element.287.mixed), channel_id=1, source_target_pairs={{0,16},{16,0},{1,17},{17,1},{2,18},{18,2},{3,19},{19,3},{4,20},{20... | collective-permute-start | bytes 589832 | tf_op jit(solution)/shard_map/ppermute | solution.py:573
  83.2 3.3 %collective-permute-start.24 = (bf16[128,768]{1,0:T(8,128)(2,1)S(1)}, bf16[128,768]{1,0:T(8,128)(2,1)S(1)}, u32[]{:S(2)}, u32[]{:S(2)}) collective-permute-start(bf16[128,768]{1,0:T(8,128)(2,1)S(1)} %get-tuple-element.306.refs_12_.refs_5_.refs_6_), channel_id=1, source_target_pairs={{0,16},{16,0},{1,17},{17,1},{2,18},{18,2},{3,19},{19,3},{4,20},{20... | collective-permute-start | bytes 589832 | tf_op jit(solution)/shard_map/ppermute | solution.py:573
  92.6 3.0 %collective-permute-start.25 = (f32[128,768]{1,0:T(8,128)S(1)}, f32[128,768]{1,0:T(8,128)S(1)}, u32[]{:S(2)}, u32[]{:S(2)}) collective-permute-start(f32[128,768]{1,0:T(8,128)S(1)} %get-tuple-element.310), channel_id=1, source_target_pairs={{0,16},{16,0},{1,17},{17,1},{2,18},{18,2},{3,19},{19,3},{4,20},{20... | collective-permute-start | bytes 1179656 | tf_op jit(solution)/shard_map/ppermute | solution.py:573
  105.6 2.8 %collective-permute-start.40 = (f32[4,1664]{1,0:T(4,128)S(1)}, f32[4,1664]{1,0:T(4,128)S(1)}, u32[]{:S(2)}, u32[]{:S(2)}) collective-permute-start(f32[4,1664]{1,0:T(4,128)S(1)} %pad_maximum_fusion.12.refs_0_), channel_id=1, source_target_pairs={{0,8},{1,9},{2,10},{3,11},{4,12},{5,13},{6,14},{7,15},{8,0},{9,1},... | collective-permute-start | bytes 79880 | tf_op jit(solution)/shard_map/ppermute | solution.py:565
  114.6 2.8 %collective-permute-start.42 = (bf16[16,48,1152]{2,1,0:T(8,128)(2,1)S(1)}, bf16[16,48,1152]{2,1,0:T(8,128)(2,1)S(1)}, u32[]{:S(2)}, u32[]{:S(2)}) collective-permute-start(bf16[16,48,1152]{2,1,0:T(8,128)(2,1)S(1)} %get-tuple-element.362.own), channel_id=1, source_target_pairs={{0,16},{16,0},{1,17},{17,1},{2,18},{18,2},{3,19},{19,3},{4,20},{20... | collective-permute-start | bytes 5308424 | tf_op jit(solution)/shard_map/ppermute | solution.py:573
  127.2 2.3 collective-permute-start.44
  129.6 2.5 %seg_mlp_near.1 = (bf16[4,48,3072]{2,1,0:T(8,128)(2,1)S(1)}, bf16[4,48,3072]{2,1,0:T(8,128)(2,1)S(1)}, bf16[4,48,3072]{2,1,0:T(8,128)(2,1)S(1)}) custom-call(s32[5]{0:T(128)S(1)} %stack.15.where, bf16[256,1024]{1,0:T(8,128)(2,1)S(1)} %get-tuple-element.328.refs_0_, bf16[128,768]{1,0:T(8,128)(2,1)S(1)} %get-tuple-element.318.refs_0_.refs_1_, ...), custom_call_target="tpu_custom_call" | custom-call | flops 905969664 | bytes 7602176 | tf_op jit(solution)/shard_map/seg_mlp_near/pallas_call | solution.py:595
  139.6 2.4 collective-permute-start.49
  147.0 2.4 %collective-permute-start.53 = (f32[16,768]{1,0:T(8,128)S(1)}, f32[16,768]{1,0:T(8,128)S(1)}, u32[]{:S(2)}, u32[]{:S(2)}) collective-permute-start(f32[16,768]{1,0:T(8,128)S(1)} %get-tuple-element.390.refs_1_), channel_id=1, source_target_pairs={{0,8},{1,9},{2,10},{3,11},{4,12},{5,13},{6,14},{7,15},{8,0},{9,1},... | collective-permute-start | bytes 147464 | tf_op jit(solution)/shard_map/ppermute | solution.py:565
  158.4 2.3 collective-permute-done.56.refs_4_
  166.0 3.1 %collective-permute-start.60 = (f32[1,768]{1,0:T(1,128)S(1)}, f32[1,768]{1,0:T(1,128)S(1)}, u32[]{:S(2)}, u32[]{:S(2)}) collective-permute-start(f32[1,768]{1,0:T(1,128)S(1)} %get-tuple-element.416.refs_0_.refs_3_), channel_id=1, source_target_pairs={{0,16},{16,0},{1,17},{17,1},{2,18},{18,2},{3,19},{19,3},{4,20},{20... | collective-permute-start | bytes 9224 | tf_op jit(solution)/shard_map/ppermute | solution.py:573
  175.4 3.8 %seg_attn_back.1.refs_2_ = bf16[256,1152]{1,0:T(8,128)(2,1)S(1)} custom-call(s32[5]{0:T(128)S(1)} %stack.15.where, bf16[256,1152]{1,0:T(8,128)(2,1)S(1)} %get-tuple-element.301.refs_0_, bf16[128,768]{1,0:T(8,128)(2,1)S(1)} %get-tuple-element.421.refs_1_, bf16[128,768]{1,0:T(8,128)(2,1)S(1)} %collective-permute-done.62.refs_2_.refs_4_, ...), custom_call_target="tpu_custom_call" | custom-call | flops 452984832 | bytes 1573888 | tf_op jit(solution)/shard_map/seg_attn_back/pallas_call | solution.py:595
  181.5 2.8 %seg_attn_near.1 = (bf16[4,48,1536]{2,1,0:T(8,128)(2,1)S(1)}, bf16[4,48,1536]{2,1,0:T(8,128)(2,1)S(1)}, bf16[4,48,1536]{2,1,0:T(8,128)(2,1)S(1)}, bf16[128,768]{...) custom-call(s32[5]{0:T(128)S(1)} %stack.15.where, ...), custom_call_target="tpu_custom_call" | custom-call | flops 452984832 | bytes 7444992 | tf_op jit(solution)/shard_map/seg_attn_near/pallas_call | solution.py:595
  184.4 8.8 %collective-permute-done.66.refs_2_ = bf16[64,3072]{1,0:T(8,128)(2,1)S(1)} collective-permute-done((bf16[64,3072]{1,0:T(8,128)(2,1)S(1)}, bf16[64,3072]{1,0:T(8,128)(2,1)S(1)}, u32[]{:S(2)}, u32[]{:S(2)}) %collective-permute-start.66) | collective-permute-done | bytes 393248 | tf_op jit(solution)/shard_map/ppermute | solution.py:565
  198.7 7.6 %collective-permute-done.67.refs_1_ = bf16[64,3072]{1,0:T(8,128)(2,1)S(1)} collective-permute-done((bf16[64,3072]{1,0:T(8,128)(2,1)S(1)}, bf16[64,3072]{1,0:T(8,128)(2,1)S(1)}, u32[]{:S(2)}, u32[]{:S(2)}) %collective-permute-start.67) | collective-permute-done | bytes 393248 | tf_op jit(solution)/shard_map/ppermute | solution.py:565
  206.3 2.9 %collective-permute-start.77 = (bf16[24,768]{1,0:T(8,128)(2,1)S(1)}, bf16[24,768]{1,0:T(8,128)(2,1)S(1)}, u32[]{:S(2)}, u32[]{:S(2)}) collective-permute-start(bf16[24,768]{1,0:T(8,128)(2,1)S(1)} %get-tuple-element.474), channel_id=1, source_target_pairs={{0,12},{1,13},{2,14},{3,15},{4,0},{5,1},{6,2},{7,3},{8,4},{9,5},{1... | collective-permute-start | bytes 110600 | tf_op jit(solution)/shard_map/ppermute | solution.py:565
  218.7 4.2 %collective-permute-done.73 = bf16[48,1536]{1,0:T(8,128)(2,1)S(1)} collective-permute-done((bf16[48,1536]{1,0:T(8,128)(2,1)S(1)}, bf16[48,1536]{1,0:T(8,128)(2,1)S(1)}, u32[]{:S(2)}, u32[]{:S(2)}) %collective-permute-start.73) | collective-permute-done | bytes 147488 | tf_op jit(solution)/shard_map/ppermute | solution.py:565
  226.7 4.4 %head_owner.1 = (f32[48,3072]{1,0:T(8,128)S(1)}, f32[16,768]{1,0:T(8,128)S(1)}, f32[48,9216]{1,0:T(8,128)}, f32[576]{0:T(1024)}, f32[16,768]{1,0:T(8,128)}, /*index=5*/f32[1,1]{1,0:T(1,128)}) custom-call(s32[5]{0:T(128)S(1)} %stack.15.where, bf16[96,768]{1,0:T(8,128)(2,1)S(1)} %pad_maximum_fusion.11.refs_0_, ...), custom_call_target="tpu_custom_call" | custom-call | flops 28311552 | bytes 4503812 | tf_op jit(solution)/shard_map/head_owner/pallas_call | solution.py:595
  231.1 2.4 %collective-permute-start.83 = (f32[48,3072]{1,0:T(8,128)S(1)}, f32[48,3072]{1,0:T(8,128)S(1)}, u32[]{:S(2)}, u32[]{:S(2)}) collective-permute-start(f32[48,3072]{1,0:T(8,128)S(1)} %get-tuple-element.488.mlp), channel_id=1, source_target_pairs={{0,16},{16,0},{1,17},{17,1},{2,18},{18,2},{3,19},{19,3},{4,20},{20... | collective-permute-start | bytes 1769480 | tf_op jit(solution)/shard_map/ppermute | solution.py:573
  235.6 3.3 %seg_owner.1 = (f32[48,9216]{1,0:T(8,128)}, f32[576]{0:T(1024)}) custom-call(s32[5]{0:T(128)S(1)} %stack.15.where, f32[48,1536]{1,0:T(8,128)S(1)} %convert_add_fusion.1.attn, f32[48,1536]{1,0:T(8,128)S(1)} %collective-permute-done.82.attn_got, f32[48,3072]{1,0:T(8,128)S(1)} %get-tuple-element.488.mlp, f32[48,3072]{1,0:T(8,128)S(1)} %collective-permute-done.83.mlp_got, ...), custom_call_target="tpu_custom_call" | custom-call | bytes 3639552 | tf_op jit(solution)/shard_map/seg_owner/pallas_call | solution.py:595
  (213 shorter events, 119.8 us)
Async XLA Ops:
  8.0 17.3 %collective-permute-start.3 = (bf16[48,4736]{1,0:T(8,128)(2,1)S(1)}, bf16[48,4736]{1,0:T(8,128)(2,1)S(1)}, u32[]{:S(2)}, u32[]{:S(2)}) collective-permute-start(bf16[48,4736]{1,0:T(8,128)(2,1)S(1)} %pad_maximum_fusion.10), channel_id=1, source_target_pairs={{0,1},{1,0},{2,3},{3,2},{4,5},{5,4},{6,7},{7,6},{8,9},{9,8},{10,11... | collective-permute-start | bytes 1363976 | tf_op jit(solution)/shard_map/ppermute | solution.py:569
  9.3 16.0 %collective-permute-start.4 = (bf16[48,4736]{1,0:T(8,128)(2,1)S(1)}, bf16[48,4736]{1,0:T(8,128)(2,1)S(1)}, u32[]{:S(2)}, u32[]{:S(2)}) collective-permute-start(bf16[48,4736]{1,0:T(8,128)(2,1)S(1)} %pad_maximum_fusion.10), channel_id=1, source_target_pairs={{0,2},{1,3},{2,0},{3,1},{4,6},{5,7},{6,4},{7,5},{8,10},{9,11},{10,... | collective-permute-start | bytes 1363976 | tf_op jit(solution)/shard_map/ppermute | solution.py:569
  9.7 11.7 %collective-permute-start.1 = (bf16[48,1664]{1,0:T(8,128)(2,1)S(1)}, bf16[48,1664]{1,0:T(8,128)(2,1)S(1)}, u32[]{:S(2)}, u32[]{:S(2)}) collective-permute-start(bf16[48,1664]{1,0:T(8,128)(2,1)S(1)} %get-tuple-element.256.refs_0_), channel_id=1, source_target_pairs={{0,8},{1,9},{2,10},{3,11},{4,12},{5,13},{6,14},{7,15},{8,0},{9,1},... | collective-permute-start | bytes 479240 | tf_op jit(solution)/shard_map/ppermute | solution.py:565
  12.0 13.3 %collective-permute-start = (bf16[48,1664]{1,0:T(8,128)(2,1)S(1)}, bf16[48,1664]{1,0:T(8,128)(2,1)S(1)}, u32[]{:S(2)}, u32[]{:S(2)}) collective-permute-start(bf16[48,1664]{1,0:T(8,128)(2,1)S(1)} %get-tuple-element.256.refs_0_), channel_id=1, source_target_pairs={{0,4},{1,5},{2,6},{3,7},{4,8},{5,9},{6,10},{7,11},{8,12},{9,13},{1... | collective-permute-start | bytes 479240 | tf_op jit(solution)/shard_map/ppermute | solution.py:565
  28.2 18.1 %collective-permute-start.8 = (bf16[48,7424]{1,0:T(8,128)(2,1)S(1)}, bf16[48,7424]{1,0:T(8,128)(2,1)S(1)}, u32[]{:S(2)}, u32[]{:S(2)}) collective-permute-start(bf16[48,7424]{1,0:T(8,128)(2,1)S(1)} %pad_maximum_fusion.6), channel_id=1, source_target_pairs={{0,2},{1,3},{2,0},{3,1},{4,6},{5,7},{6,4},{7,5},{8,10},{9,11},{10,... | collective-permute-start | bytes 2138120 | tf_op jit(solution)/shard_map/ppermute | solution.py:569
  29.5 16.8 %collective-permute-start.7 = (bf16[48,7296]{1,0:T(8,128)(2,1)S(1)}, bf16[48,7296]{1,0:T(8,128)(2,1)S(1)}, u32[]{:S(2)}, u32[]{:S(2)}) collective-permute-start(bf16[48,7296]{1,0:T(8,128)(2,1)S(1)} %pad_maximum_fusion.7), channel_id=1, source_target_pairs={{0,1},{1,0},{2,3},{3,2},{4,5},{5,4},{6,7},{7,6},{8,9},{9,8},{10,11... | collective-permute-start | bytes 2101256 | tf_op jit(solution)/shard_map/ppermute | solution.py:569
  30.7 10.5 %collective-permute-start.10 = (bf16[48,1536]{1,0:T(8,128)(2,1)S(1)}, bf16[48,1536]{1,0:T(8,128)(2,1)S(1)}, u32[]{:S(2)}, u32[]{:S(2)}) collective-permute-start(bf16[48,1536]{1,0:T(8,128)(2,1)S(1)} %get-tuple-element.277.refs_0_), channel_id=1, source_target_pairs={{0,8},{1,9},{2,10},{3,11},{4,12},{5,13},{6,14},{7,15},{8,0},{9,1},... | collective-permute-start | bytes 442376 | tf_op jit(solution)/shard_map/ppermute | solution.py:565
  33.1 11.1 %collective-permute-start.9 = (bf16[48,1536]{1,0:T(8,128)(2,1)S(1)}, bf16[48,1536]{1,0:T(8,128)(2,1)S(1)}, u32[]{:S(2)}, u32[]{:S(2)}) collective-permute-start(bf16[48,1536]{1,0:T(8,128)(2,1)S(1)} %get-tuple-element.277.refs_0_), channel_id=1, source_target_pairs={{0,4},{1,5},{2,6},{3,7},{4,8},{5,9},{6,10},{7,11},{8,12},{9,13},{1... | collective-permute-start | bytes 442376 | tf_op jit(solution)/shard_map/ppermute | solution.py:565
  46.5 16.1 %collective-permute-start.13 = (bf16[48,7168]{1,0:T(8,128)(2,1)S(1)}, bf16[48,7168]{1,0:T(8,128)(2,1)S(1)}, u32[]{:S(2)}, u32[]{:S(2)}) collective-permute-start(bf16[48,7168]{1,0:T(8,128)(2,1)S(1)} %pad_maximum_fusion.8), channel_id=1, source_target_pairs={{0,2},{1,3},{2,0},{3,1},{4,6},{5,7},{6,4},{7,5},{8,10},{9,11},{10,... | collective-permute-start | bytes 2064392 | tf_op jit(solution)/shard_map/ppermute | solution.py:569
  47.1 15.4 %collective-permute-start.12 = (bf16[48,7040]{1,0:T(8,128)(2,1)S(1)}, bf16[48,7040]{1,0:T(8,128)(2,1)S(1)}, u32[]{:S(2)}, u32[]{:S(2)}) collective-permute-start(bf16[48,7040]{1,0:T(8,128)(2,1)S(1)} %pad_maximum_fusion.9), channel_id=1, source_target_pairs={{0,1},{1,0},{2,3},{3,2},{4,5},{5,4},{6,7},{7,6},{8,9},{9,8},{10,11... | collective-permute-start | bytes 2027528 | tf_op jit(solution)/shard_map/ppermute | solution.py:569
  48.3 10.5 %collective-permute-start.16 = (bf16[48,1536]{1,0:T(8,128)(2,1)S(1)}, bf16[48,1536]{1,0:T(8,128)(2,1)S(1)}, u32[]{:S(2)}, u32[]{:S(2)}) collective-permute-start(bf16[48,1536]{1,0:T(8,128)(2,1)S(1)} %get-tuple-element.288.refs_0_), channel_id=1, source_target_pairs={{0,8},{1,9},{2,10},{3,11},{4,12},{5,13},{6,14},{7,15},{8,0},{9,1},... | collective-permute-start | bytes 442376 | tf_op jit(solution)/shard_map/ppermute | solution.py:565
  50.8 11.2 %collective-permute-start.15 = (bf16[48,1536]{1,0:T(8,128)(2,1)S(1)}, bf16[48,1536]{1,0:T(8,128)(2,1)S(1)}, u32[]{:S(2)}, u32[]{:S(2)}) collective-permute-start(bf16[48,1536]{1,0:T(8,128)(2,1)S(1)} %get-tuple-element.288.refs_0_), channel_id=1, source_target_pairs={{0,4},{1,5},{2,6},{3,7},{4,8},{5,9},{6,10},{7,11},{8,12},{9,13},{1... | collective-permute-start | bytes 442376 | tf_op jit(solution)/shard_map/ppermute | solution.py:565
  62.7 14.3 %collective-permute-start.18 = (bf16[48,6912]{1,0:T(8,128)(2,1)S(1)}, bf16[48,6912]{1,0:T(8,128)(2,1)S(1)}, u32[]{:S(2)}, u32[]{:S(2)}) collective-permute-start(bf16[48,6912]{1,0:T(8,128)(2,1)S(1)} %get-tuple-element.292), channel_id=1, source_target_pairs={{0,1},{1,0},{2,3},{3,2},{4,5},{5,4},{6,7},{7,6},{8,9},{9,8},{10,11... | collective-permute-start | bytes 1990664 | tf_op jit(solution)/shard_map/ppermute | solution.py:569
  63.4 11.2 %collective-permute-start.32 = (bf16[48,1152]{1,0:T(8,128)(2,1)S(1)}, bf16[48,1152]{1,0:T(8,128)(2,1)S(1)}, u32[]{:S(2)}, u32[]{:S(2)}) collective-permute-start(bf16[48,1152]{1,0:T(8,128)(2,1)S(1)} %get-tuple-element.332), channel_id=1, source_target_pairs={{0,4},{1,5},{2,6},{3,7},{4,8},{5,9},{6,10},{7,11},{8,12},{9,13},{1... | collective-permute-start | bytes 331784 | tf_op jit(solution)/shard_map/ppermute | solution.py:565
  65.6 14.5 %collective-permute-start.19 = (bf16[48,6912]{1,0:T(8,128)(2,1)S(1)}, bf16[48,6912]{1,0:T(8,128)(2,1)S(1)}, u32[]{:S(2)}, u32[]{:S(2)}) collective-permute-start(bf16[48,6912]{1,0:T(8,128)(2,1)S(1)} %get-tuple-element.293), channel_id=1, source_target_pairs={{0,2},{1,3},{2,0},{3,1},{4,6},{5,7},{6,4},{7,5},{8,10},{9,11},{10,... | collective-permute-start | bytes 1990664 | tf_op jit(solution)/shard_map/ppermute | solution.py:569
  70.6 11.2 %collective-permute-start.20 = (bf16[8,48,384]{2,1,0:T(8,128)(2,1)S(1)}, bf16[8,48,384]{2,1,0:T(8,128)(2,1)S(1)}, u32[]{:S(2)}, u32[]{:S(2)}) collective-permute-start(bf16[8,48,384]{2,1,0:T(8,128)(2,1)S(1)} %get-tuple-element.297.low), channel_id=1, source_target_pairs={{0,16},{16,0},{1,17},{17,1},{2,18},{18,2},{3,19},{19,3},{4,20},{20... | collective-permute-start | bytes 884744 | tf_op jit(solution)/shard_map/ppermute | solution.py:573
  74.7 11.8 %collective-permute-start.34 = (bf16[48,1152]{1,0:T(8,128)(2,1)S(1)}, bf16[48,1152]{1,0:T(8,128)(2,1)S(1)}, u32[]{:S(2)}, u32[]{:S(2)}) collective-permute-start(bf16[48,1152]{1,0:T(8,128)(2,1)S(1)} %get-tuple-element.336), channel_id=1, source_target_pairs={{0,12},{1,13},{2,14},{3,15},{4,0},{5,1},{6,2},{7,3},{8,4},{9,5},{1... | collective-permute-start | bytes 331784 | tf_op jit(solution)/shard_map/ppermute | solution.py:565
  89.5 14.4 %collective-permute-start.35 = (bf16[48,4992]{1,0:T(8,128)(2,1)S(1)}, bf16[48,4992]{1,0:T(8,128)(2,1)S(1)}, u32[]{:S(2)}, u32[]{:S(2)}) collective-permute-start(bf16[48,4992]{1,0:T(8,128)(2,1)S(1)} %constant_dynamic-update-slice_fusion), channel_id=1, source_target_pairs={{0,1},{1,0},{2,3},{3,2},{4,5},{5,4},{6,7},{7,6},{8,9},{9,8},{10,11... | collective-permute-start | bytes 1437704 | tf_op jit(solution)/shard_map/ppermute | solution.py:569
  90.5 13.5 %collective-permute-start.36 = (bf16[48,4992]{1,0:T(8,128)(2,1)S(1)}, bf16[48,4992]{1,0:T(8,128)(2,1)S(1)}, u32[]{:S(2)}, u32[]{:S(2)}) collective-permute-start(bf16[48,4992]{1,0:T(8,128)(2,1)S(1)} %constant_dynamic-update-slice_fusion), channel_id=1, source_target_pairs={{0,2},{1,3},{2,0},{3,1},{4,6},{5,7},{6,4},{7,5},{8,10},{9,11},{10,... | collective-permute-start | bytes 1437704 | tf_op jit(solution)/shard_map/ppermute | solution.py:569
  118.7 15.0 %collective-permute-start.47 = (bf16[2,48,3072]{2,1,0:T(8,128)(2,1)S(1)}, bf16[2,48,3072]{2,1,0:T(8,128)(2,1)S(1)}, u32[]{:S(2)}, u32[]{:S(2)}) collective-permute-start(bf16[2,48,3072]{2,1,0:T(8,128)(2,1)S(1)} %get-tuple-element.377), channel_id=1, source_target_pairs={{0,2},{1,3},{2,0},{3,1},{4,6},{5,7},{6,4},{7,5},{8,10},{9,11},{10,... | collective-permute-start | bytes 1769480 | tf_op jit(solution)/shard_map/ppermute | solution.py:569
  119.7 14.6 %collective-permute-start.48 = (bf16[2,48,3072]{2,1,0:T(8,128)(2,1)S(1)}, bf16[2,48,3072]{2,1,0:T(8,128)(2,1)S(1)}, u32[]{:S(2)}, u32[]{:S(2)}) collective-permute-start(bf16[2,48,3072]{2,1,0:T(8,128)(2,1)S(1)} %get-tuple-element.379), channel_id=1, source_target_pairs={{0,1},{1,0},{2,3},{3,2},{4,5},{5,4},{6,7},{7,6},{8,9},{9,8},{10,11... | collective-permute-start | bytes 1769480 | tf_op jit(solution)/shard_map/ppermute | solution.py:569
  135.8 26.4 %collective-permute-start.58 = (bf16[4,48,3072]{2,1,0:T(8,128)(2,1)S(1)}, bf16[4,48,3072]{2,1,0:T(8,128)(2,1)S(1)}, u32[]{:S(2)}, u32[]{:S(2)}) collective-permute-start(bf16[4,48,3072]{2,1,0:T(8,128)(2,1)S(1)} %get-tuple-element.408), channel_id=1, source_target_pairs={{0,1},{1,0},{2,3},{3,2},{4,5},{5,4},{6,7},{7,6},{8,9},{9,8},{10,11... | collective-permute-start | bytes 3538952 | tf_op jit(solution)/shard_map/ppermute | solution.py:569
  136.6 26.1 %collective-permute-start.59 = (bf16[4,48,3072]{2,1,0:T(8,128)(2,1)S(1)}, bf16[4,48,3072]{2,1,0:T(8,128)(2,1)S(1)}, u32[]{:S(2)}, u32[]{:S(2)}) collective-permute-start(bf16[4,48,3072]{2,1,0:T(8,128)(2,1)S(1)} %get-tuple-element.409), channel_id=1, source_target_pairs={{0,2},{1,3},{2,0},{3,1},{4,6},{5,7},{6,4},{7,5},{8,10},{9,11},{10,... | collective-permute-start | bytes 3538952 | tf_op jit(solution)/shard_map/ppermute | solution.py:569
  164.1 16.2 %collective-permute-start.63 = (bf16[64,3072]{1,0:T(8,128)(2,1)S(1)}, bf16[64,3072]{1,0:T(8,128)(2,1)S(1)}, u32[]{:S(2)}, u32[]{:S(2)}) collective-permute-start(bf16[64,3072]{1,0:T(8,128)(2,1)S(1)} %get-tuple-element.435), channel_id=1, source_target_pairs={{0,12},{1,13},{2,14},{3,15},{4,0},{5,1},{6,2},{7,3},{8,4},{9,5},{1... | collective-permute-start | bytes 1179656 | tf_op jit(solution)/shard_map/ppermute | solution.py:565
  174.3 18.9 %collective-permute-start.66 = (bf16[64,3072]{1,0:T(8,128)(2,1)S(1)}, bf16[64,3072]{1,0:T(8,128)(2,1)S(1)}, u32[]{:S(2)}, u32[]{:S(2)}) collective-permute-start(bf16[64,3072]{1,0:T(8,128)(2,1)S(1)} %get-tuple-element.442), channel_id=1, source_target_pairs={{0,8},{1,9},{2,10},{3,11},{4,12},{5,13},{6,14},{7,15},{8,0},{9,1},... | collective-permute-start | bytes 1179656 | tf_op jit(solution)/shard_map/ppermute | solution.py:565
  180.3 12.9 %collective-permute-start.64 = (bf16[2,48,1536]{2,1,0:T(8,128)(2,1)S(1)}, bf16[2,48,1536]{2,1,0:T(8,128)(2,1)S(1)}, u32[]{:S(2)}, u32[]{:S(2)}) collective-permute-start(bf16[2,48,1536]{2,1,0:T(8,128)(2,1)S(1)} %get-tuple-element.436), channel_id=1, source_target_pairs={{0,2},{1,3},{2,0},{3,1},{4,6},{5,7},{6,4},{7,5},{8,10},{9,11},{10,... | collective-permute-start | bytes 884744 | tf_op jit(solution)/shard_map/ppermute | solution.py:569
  180.9 12.2 %collective-permute-start.65 = (bf16[2,48,1536]{2,1,0:T(8,128)(2,1)S(1)}, bf16[2,48,1536]{2,1,0:T(8,128)(2,1)S(1)}, u32[]{:S(2)}, u32[]{:S(2)}) collective-permute-start(bf16[2,48,1536]{2,1,0:T(8,128)(2,1)S(1)} %get-tuple-element.438), channel_id=1, source_target_pairs={{0,1},{1,0},{2,3},{3,2},{4,5},{5,4},{6,7},{7,6},{8,9},{9,8},{10,11... | collective-permute-start | bytes 884744 | tf_op jit(solution)/shard_map/ppermute | solution.py:569
  193.8 16.6 %collective-permute-start.68 = (bf16[4,48,1536]{2,1,0:T(8,128)(2,1)S(1)}, bf16[4,48,1536]{2,1,0:T(8,128)(2,1)S(1)}, u32[]{:S(2)}, u32[]{:S(2)}) collective-permute-start(bf16[4,48,1536]{2,1,0:T(8,128)(2,1)S(1)} %get-tuple-element.448), channel_id=1, source_target_pairs={{0,1},{1,0},{2,3},{3,2},{4,5},{5,4},{6,7},{7,6},{8,9},{9,8},{10,11... | collective-permute-start | bytes 1769480 | tf_op jit(solution)/shard_map/ppermute | solution.py:569
  194.5 15.9 %collective-permute-start.69 = (bf16[4,48,1536]{2,1,0:T(8,128)(2,1)S(1)}, bf16[4,48,1536]{2,1,0:T(8,128)(2,1)S(1)}, u32[]{:S(2)}, u32[]{:S(2)}) collective-permute-start(bf16[4,48,1536]{2,1,0:T(8,128)(2,1)S(1)} %get-tuple-element.449), channel_id=1, source_target_pairs={{0,2},{1,3},{2,0},{3,1},{4,6},{5,7},{6,4},{7,5},{8,10},{9,11},{10,... | collective-permute-start | bytes 1769480 | tf_op jit(solution)/shard_map/ppermute | solution.py:569
  195.2 11.0 %collective-permute-start.67 = (bf16[64,3072]{1,0:T(8,128)(2,1)S(1)}, bf16[64,3072]{1,0:T(8,128)(2,1)S(1)}, u32[]{:S(2)}, u32[]{:S(2)}) collective-permute-start(bf16[64,3072]{1,0:T(8,128)(2,1)S(1)} %get-tuple-element.447), channel_id=1, source_target_pairs={{0,4},{1,5},{2,6},{3,7},{4,8},{5,9},{6,10},{7,11},{8,12},{9,13},{1... | collective-permute-start | bytes 1179656 | tf_op jit(solution)/shard_map/ppermute | solution.py:565
  214.1 12.6 %collective-permute-start.80 = (bf16[96,768]{1,0:T(8,128)(2,1)S(1)}, bf16[96,768]{1,0:T(8,128)(2,1)S(1)}, u32[]{:S(2)}, u32[]{:S(2)}) collective-permute-start(bf16[96,768]{1,0:T(8,128)(2,1)S(1)} %pad_maximum_fusion.11.refs_0_), channel_id=1, source_target_pairs={{0,3},{1,2},{2,1},{3,0},{4,7},{5,6},{6,5},{7,4},{8,11},{9,10},{10,... | collective-permute-start | bytes 442376 | tf_op jit(solution)/shard_map/ppermute | solution.py:569
  215.5 11.2 %collective-permute-start.79 = (bf16[96,768]{1,0:T(8,128)(2,1)S(1)}, bf16[96,768]{1,0:T(8,128)(2,1)S(1)}, u32[]{:S(2)}, u32[]{:S(2)}) collective-permute-start(bf16[96,768]{1,0:T(8,128)(2,1)S(1)} %pad_maximum_fusion.11.refs_0_), channel_id=1, source_target_pairs={{0,2},{1,3},{2,0},{3,1},{4,6},{5,7},{6,4},{7,5},{8,10},{9,11},{10,... | collective-permute-start | bytes 442376 | tf_op jit(solution)/shard_map/ppermute | solution.py:569
  (61 other events, 312.2 us)

commit v14 on v13

--- a/solution.py
+++ b/solution.py
@@ -1855,8 +1855,7 @@
             for count_of in (LINE // 2, LINE // 2, LINE, LINE, LINE)
         ]
 
-    head_lines = head_lines[:1] + together(*(after(got, pre) for got in head_lines[1:]))
-    cls_far = together(*(after(got, *head_lines[1:]) for got in cls_far))
+    cls_far = together(*(after(got, second_got, *head_lines[1:]) for got in cls_far))
     cls_half, cls_out_half = run_kernel(
         cls_gather_kernel,
         "head_gather",

time: 241 us -> 241 us (level)
  no operation moved by 1% of the time
where the time goes in v14:
time: 241 us; the launch traced here: 239 us
  starting transfers between devices  97.4 us (40%)
  waiting for transfers between devices  84.6 us (35%)
  Pallas kernels  49.2 us (20%)
  local copies, waits for them, and re-layouts  5.34 us (2%)
    ppermute x36, waiting for transfers between devices, along_line(): return lax.ppermute(value, 'fsdp', line_pairs(apart))  65 us
    pallas_call x27, Pallas kernels, run_kernel(): pl.pallas_call(body, name=name, out_shape=tuple(outs), in_specs=in_specs,...  49.2 us
    ppermute x36, starting transfers between devices, along_line(): return lax.ppermute(value, 'fsdp', line_pairs(apart))  45.4 us
    ppermute x21, starting transfers between devices, other_core(): return lax.ppermute(value, 'rep', [(0, 1), (1, 0)])  30.8 us
    ppermute x28, starting transfers between devices, in_plane(): return lax.ppermute(value, 'fsdp', plane_pairs(mask))  21.1 us
    ppermute x21, waiting for transfers between devices, other_core(): return lax.ppermute(value, 'rep', [(0, 1), (1, 0)])  10.4 us
    ppermute x28, waiting for transfers between devices, in_plane(): return lax.ppermute(value, 'fsdp', plane_pairs(mask))  9.17 us
  transfers between devices with their start and end apart: 85, of which 40 were waited for; matrix products, arithmetic and copies ran while one was open for 0% of the time, Pallas kernels for 14%

profile of v14, /device:TPU:13, one launch (start us, length us, event | category | flops | bytes accessed | tf_op | source)
XLA Modules:
  0.0 239.2 jit_solution(218173430986793583)
XLA Ops:
  9.7 2.3 collective-permute-start.1
  14.2 7.2 %collective-permute-done.1.refs_2_ = bf16[48,1664]{1,0:T(8,128)(2,1)S(1)} collective-permute-done((bf16[48,1664]{1,0:T(8,128)(2,1)S(1)}, bf16[48,1664]{1,0:T(8,128)(2,1)S(1)}, u32[]{:S(2)}, u32[]{:S(2)}) %collective-permute-start.1) | collective-permute-done | bytes 159776 | tf_op jit(solution)/shard_map/ppermute | solution.py:565
  21.4 3.9 %collective-permute-done.refs_1_ = bf16[48,1664]{1,0:T(8,128)(2,1)S(1)} collective-permute-done((bf16[48,1664]{1,0:T(8,128)(2,1)S(1)}, bf16[48,1664]{1,0:T(8,128)(2,1)S(1)}, u32[]{:S(2)}, u32[]{:S(2)}) %collective-permute-start) | collective-permute-done | bytes 159776 | tf_op jit(solution)/shard_map/ppermute | solution.py:565
  30.7 2.5 %collective-permute-start.10 = (bf16[48,1536]{1,0:T(8,128)(2,1)S(1)}, bf16[48,1536]{1,0:T(8,128)(2,1)S(1)}, u32[]{:S(2)}, u32[]{:S(2)}) collective-permute-start(bf16[48,1536]{1,0:T(8,128)(2,1)S(1)} %get-tuple-element.271.refs_0_), channel_id=1, source_target_pairs={{0,8},{1,9},{2,10},{3,11},{4,12},{5,13},{6,14},{7,15},{8,0},{9,1},... | collective-permute-start | bytes 442376 | tf_op jit(solution)/shard_map/ppermute | solution.py:565
  33.1 2.3 collective-permute-done.11.refs_3_
  35.5 5.6 %collective-permute-done.10.refs_2_ = bf16[48,1536]{1,0:T(8,128)(2,1)S(1)} collective-permute-done((bf16[48,1536]{1,0:T(8,128)(2,1)S(1)}, bf16[48,1536]{1,0:T(8,128)(2,1)S(1)}, u32[]{:S(2)}, u32[]{:S(2)}) %collective-permute-start.10) | collective-permute-done | bytes 147488 | tf_op jit(solution)/shard_map/ppermute | solution.py:565
  41.1 3.2 %collective-permute-done.9.refs_1_ = bf16[48,1536]{1,0:T(8,128)(2,1)S(1)} collective-permute-done((bf16[48,1536]{1,0:T(8,128)(2,1)S(1)}, bf16[48,1536]{1,0:T(8,128)(2,1)S(1)}, u32[]{:S(2)}, u32[]{:S(2)}) %collective-permute-start.9) | collective-permute-done | bytes 147488 | tf_op jit(solution)/shard_map/ppermute | solution.py:565
  48.3 2.5 %collective-permute-start.16 = (bf16[48,1536]{1,0:T(8,128)(2,1)S(1)}, bf16[48,1536]{1,0:T(8,128)(2,1)S(1)}, u32[]{:S(2)}, u32[]{:S(2)}) collective-permute-start(bf16[48,1536]{1,0:T(8,128)(2,1)S(1)} %get-tuple-element.282.refs_0_), channel_id=1, source_target_pairs={{0,8},{1,9},{2,10},{3,11},{4,12},{5,13},{6,14},{7,15},{8,0},{9,1},... | collective-permute-start | bytes 442376 | tf_op jit(solution)/shard_map/ppermute | solution.py:565
  52.4 6.4 %collective-permute-done.16.refs_2_ = bf16[48,1536]{1,0:T(8,128)(2,1)S(1)} collective-permute-done((bf16[48,1536]{1,0:T(8,128)(2,1)S(1)}, bf16[48,1536]{1,0:T(8,128)(2,1)S(1)}, u32[]{:S(2)}, u32[]{:S(2)}) %collective-permute-start.16) | collective-permute-done | bytes 147488 | tf_op jit(solution)/shard_map/ppermute | solution.py:565
  58.8 3.2 %collective-permute-done.15.refs_1_ = bf16[48,1536]{1,0:T(8,128)(2,1)S(1)} collective-permute-done((bf16[48,1536]{1,0:T(8,128)(2,1)S(1)}, bf16[48,1536]{1,0:T(8,128)(2,1)S(1)}, u32[]{:S(2)}, u32[]{:S(2)}) %collective-permute-start.15) | collective-permute-done | bytes 147488 | tf_op jit(solution)/shard_map/ppermute | solution.py:565
  66.7 3.9 %seg_qkv.1 = (bf16[16,48,1152]{2,1,0:T(8,128)(2,1)S(1)}, bf16[8,48,384]{2,1,0:T(8,128)(2,1)S(1)}, bf16[8,48,384]{2,1,0:T(8,128)(2,1)S(1)}, bf16[256,1152]{1,0:T(...) custom-call(s32[5]{0:T(128)S(1)} %stack.15.where, ...), custom_call_target="tpu_custom_call" | custom-call | flops 452984832 | bytes 11453440 | tf_op jit(solution)/shard_map/seg_qkv/pallas_call | solution.py:595
  70.6 4.1 %collective-permute-start.20 = (bf16[8,48,384]{2,1,0:T(8,128)(2,1)S(1)}, bf16[8,48,384]{2,1,0:T(8,128)(2,1)S(1)}, u32[]{:S(2)}, u32[]{:S(2)}) collective-permute-start(bf16[8,48,384]{2,1,0:T(8,128)(2,1)S(1)} %get-tuple-element.291.low), channel_id=1, source_target_pairs={{0,16},{16,0},{1,17},{17,1},{2,18},{18,2},{3,19},{19,3},{4,20},{20... | collective-permute-start | bytes 884744 | tf_op jit(solution)/shard_map/ppermute | solution.py:573
  77.0 3.1 %collective-permute-start.14 = (bf16[256,384]{1,0:T(8,128)(2,1)S(1)}, bf16[256,384]{1,0:T(8,128)(2,1)S(1)}, u32[]{:S(2)}, u32[]{:S(2)}) collective-permute-start(bf16[256,384]{1,0:T(8,128)(2,1)S(1)} %get-tuple-element.281.mixed), channel_id=1, source_target_pairs={{0,16},{16,0},{1,17},{17,1},{2,18},{18,2},{3,19},{19,3},{4,20},{20... | collective-permute-start | bytes 589832 | tf_op jit(solution)/shard_map/ppermute | solution.py:573
  83.2 3.3 %collective-permute-start.24 = (bf16[128,768]{1,0:T(8,128)(2,1)S(1)}, bf16[128,768]{1,0:T(8,128)(2,1)S(1)}, u32[]{:S(2)}, u32[]{:S(2)}) collective-permute-start(bf16[128,768]{1,0:T(8,128)(2,1)S(1)} %get-tuple-element.300.refs_12_.refs_5_.refs_6_), channel_id=1, source_target_pairs={{0,16},{16,0},{1,17},{17,1},{2,18},{18,2},{3,19},{19,3},{4,20},{20... | collective-permute-start | bytes 589832 | tf_op jit(solution)/shard_map/ppermute | solution.py:573
  92.6 3.0 %collective-permute-start.25 = (f32[128,768]{1,0:T(8,128)S(1)}, f32[128,768]{1,0:T(8,128)S(1)}, u32[]{:S(2)}, u32[]{:S(2)}) collective-permute-start(f32[128,768]{1,0:T(8,128)S(1)} %get-tuple-element.304), channel_id=1, source_target_pairs={{0,16},{16,0},{1,17},{17,1},{2,18},{18,2},{3,19},{19,3},{4,20},{20... | collective-permute-start | bytes 1179656 | tf_op jit(solution)/shard_map/ppermute | solution.py:573
  105.6 2.8 %collective-permute-start.40 = (f32[4,1664]{1,0:T(4,128)S(1)}, f32[4,1664]{1,0:T(4,128)S(1)}, u32[]{:S(2)}, u32[]{:S(2)}) collective-permute-start(f32[4,1664]{1,0:T(4,128)S(1)} %pad_maximum_fusion.12.refs_0_), channel_id=1, source_target_pairs={{0,8},{1,9},{2,10},{3,11},{4,12},{5,13},{6,14},{7,15},{8,0},{9,1},... | collective-permute-start | bytes 79880 | tf_op jit(solution)/shard_map/ppermute | solution.py:565
  112.5 2.8 %collective-permute-start.42 = (bf16[16,48,1152]{2,1,0:T(8,128)(2,1)S(1)}, bf16[16,48,1152]{2,1,0:T(8,128)(2,1)S(1)}, u32[]{:S(2)}, u32[]{:S(2)}) collective-permute-start(bf16[16,48,1152]{2,1,0:T(8,128)(2,1)S(1)} %get-tuple-element.350.own), channel_id=1, source_target_pairs={{0,16},{16,0},{1,17},{17,1},{2,18},{18,2},{3,19},{19,3},{4,20},{20... | collective-permute-start | bytes 5308424 | tf_op jit(solution)/shard_map/ppermute | solution.py:573
  127.2 2.3 collective-permute-start.44
  129.5 2.5 %seg_mlp_near.1 = (bf16[4,48,3072]{2,1,0:T(8,128)(2,1)S(1)}, bf16[4,48,3072]{2,1,0:T(8,128)(2,1)S(1)}, bf16[4,48,3072]{2,1,0:T(8,128)(2,1)S(1)}) custom-call(s32[5]{0:T(128)S(1)} %stack.15.where, bf16[256,1024]{1,0:T(8,128)(2,1)S(1)} %get-tuple-element.322.refs_0_, bf16[128,768]{1,0:T(8,128)(2,1)S(1)} %get-tuple-element.312.refs_0_.refs_1_, ...), custom_call_target="tpu_custom_call" | custom-call | flops 905969664 | bytes 7602176 | tf_op jit(solution)/shard_map/seg_mlp_near/pallas_call | solution.py:595
  139.6 2.4 collective-permute-start.49
  147.0 2.4 %collective-permute-start.53 = (f32[16,768]{1,0:T(8,128)S(1)}, f32[16,768]{1,0:T(8,128)S(1)}, u32[]{:S(2)}, u32[]{:S(2)}) collective-permute-start(f32[16,768]{1,0:T(8,128)S(1)} %get-tuple-element.378.refs_1_), channel_id=1, source_target_pairs={{0,8},{1,9},{2,10},{3,11},{4,12},{5,13},{6,14},{7,15},{8,0},{9,1},... | collective-permute-start | bytes 147464 | tf_op jit(solution)/shard_map/ppermute | solution.py:565
  158.4 2.4 collective-permute-done.56.refs_4_
  166.0 3.1 %collective-permute-start.60 = (f32[1,768]{1,0:T(1,128)S(1)}, f32[1,768]{1,0:T(1,128)S(1)}, u32[]{:S(2)}, u32[]{:S(2)}) collective-permute-start(f32[1,768]{1,0:T(1,128)S(1)} %get-tuple-element.404.refs_0_.refs_3_), channel_id=1, source_target_pairs={{0,16},{16,0},{1,17},{17,1},{2,18},{18,2},{3,19},{19,3},{4,20},{20... | collective-permute-start | bytes 9224 | tf_op jit(solution)/shard_map/ppermute | solution.py:573
  175.4 3.8 %seg_attn_back.1.refs_2_ = bf16[256,1152]{1,0:T(8,128)(2,1)S(1)} custom-call(s32[5]{0:T(128)S(1)} %stack.15.where, bf16[256,1152]{1,0:T(8,128)(2,1)S(1)} %get-tuple-element.295.refs_0_, bf16[128,768]{1,0:T(8,128)(2,1)S(1)} %get-tuple-element.409.refs_1_, bf16[128,768]{1,0:T(8,128)(2,1)S(1)} %collective-permute-done.62.refs_2_.refs_4_, ...), custom_call_target="tpu_custom_call" | custom-call | flops 452984832 | bytes 1573888 | tf_op jit(solution)/shard_map/seg_attn_back/pallas_call | solution.py:595
  181.5 2.8 %seg_attn_near.1 = (bf16[4,48,1536]{2,1,0:T(8,128)(2,1)S(1)}, bf16[4,48,1536]{2,1,0:T(8,128)(2,1)S(1)}, bf16[4,48,1536]{2,1,0:T(8,128)(2,1)S(1)}, bf16[128,768]{...) custom-call(s32[5]{0:T(128)S(1)} %stack.15.where, ...), custom_call_target="tpu_custom_call" | custom-call | flops 452984832 | bytes 7444992 | tf_op jit(solution)/shard_map/seg_attn_near/pallas_call | solution.py:595
  184.4 8.8 %collective-permute-done.66.refs_2_ = bf16[64,3072]{1,0:T(8,128)(2,1)S(1)} collective-permute-done((bf16[64,3072]{1,0:T(8,128)(2,1)S(1)}, bf16[64,3072]{1,0:T(8,128)(2,1)S(1)}, u32[]{:S(2)}, u32[]{:S(2)}) %collective-permute-start.66) | collective-permute-done | bytes 393248 | tf_op jit(solution)/shard_map/ppermute | solution.py:565
  198.7 7.6 %collective-permute-done.67.refs_1_ = bf16[64,3072]{1,0:T(8,128)(2,1)S(1)} collective-permute-done((bf16[64,3072]{1,0:T(8,128)(2,1)S(1)}, bf16[64,3072]{1,0:T(8,128)(2,1)S(1)}, u32[]{:S(2)}, u32[]{:S(2)}) %collective-permute-start.67) | collective-permute-done | bytes 393248 | tf_op jit(solution)/shard_map/ppermute | solution.py:565
  206.3 2.9 %collective-permute-start.77 = (bf16[24,768]{1,0:T(8,128)(2,1)S(1)}, bf16[24,768]{1,0:T(8,128)(2,1)S(1)}, u32[]{:S(2)}, u32[]{:S(2)}) collective-permute-start(bf16[24,768]{1,0:T(8,128)(2,1)S(1)} %get-tuple-element.462), channel_id=1, source_target_pairs={{0,12},{1,13},{2,14},{3,15},{4,0},{5,1},{6,2},{7,3},{8,4},{9,5},{1... | collective-permute-start | bytes 110600 | tf_op jit(solution)/shard_map/ppermute | solution.py:565
  218.7 4.2 %collective-permute-done.73 = bf16[48,1536]{1,0:T(8,128)(2,1)S(1)} collective-permute-done((bf16[48,1536]{1,0:T(8,128)(2,1)S(1)}, bf16[48,1536]{1,0:T(8,128)(2,1)S(1)}, u32[]{:S(2)}, u32[]{:S(2)}) %collective-permute-start.73) | collective-permute-done | bytes 147488 | tf_op jit(solution)/shard_map/ppermute | solution.py:565
  226.7 4.4 %head_owner.1 = (f32[48,3072]{1,0:T(8,128)S(1)}, f32[16,768]{1,0:T(8,128)S(1)}, f32[48,9216]{1,0:T(8,128)}, f32[576]{0:T(1024)}, f32[16,768]{1,0:T(8,128)}, /*index=5*/f32[1,1]{1,0:T(1,128)}) custom-call(s32[5]{0:T(128)S(1)} %stack.15.where, bf16[96,768]{1,0:T(8,128)(2,1)S(1)} %pad_maximum_fusion.11.refs_0_, ...), custom_call_target="tpu_custom_call" | custom-call | flops 28311552 | bytes 4503812 | tf_op jit(solution)/shard_map/head_owner/pallas_call | solution.py:595
  231.1 2.4 collective-permute-start.83
  235.6 3.3 %seg_owner.1 = (f32[48,9216]{1,0:T(8,128)}, f32[576]{0:T(1024)}) custom-call(s32[5]{0:T(128)S(1)} %stack.15.where, f32[48,1536]{1,0:T(8,128)S(1)} %convert_add_fusion.1.attn, f32[48,1536]{1,0:T(8,128)S(1)} %collective-permute-done.82.attn_got, f32[48,3072]{1,0:T(8,128)S(1)} %get-tuple-element.476.mlp, f32[48,3072]{1,0:T(8,128)S(1)} %collective-permute-done.83.mlp_got, ...), custom_call_target="tpu_custom_call" | custom-call | bytes 3639552 | tf_op jit(solution)/shard_map/seg_owner/pallas_call | solution.py:595
  (213 shorter events, 119.8 us)
Async XLA Ops:
  8.0 17.3 %collective-permute-start.3 = (bf16[48,4736]{1,0:T(8,128)(2,1)S(1)}, bf16[48,4736]{1,0:T(8,128)(2,1)S(1)}, u32[]{:S(2)}, u32[]{:S(2)}) collective-permute-start(bf16[48,4736]{1,0:T(8,128)(2,1)S(1)} %pad_maximum_fusion.10), channel_id=1, source_target_pairs={{0,1},{1,0},{2,3},{3,2},{4,5},{5,4},{6,7},{7,6},{8,9},{9,8},{10,11... | collective-permute-start | bytes 1363976 | tf_op jit(solution)/shard_map/ppermute | solution.py:569
  9.3 16.0 %collective-permute-start.4 = (bf16[48,4736]{1,0:T(8,128)(2,1)S(1)}, bf16[48,4736]{1,0:T(8,128)(2,1)S(1)}, u32[]{:S(2)}, u32[]{:S(2)}) collective-permute-start(bf16[48,4736]{1,0:T(8,128)(2,1)S(1)} %pad_maximum_fusion.10), channel_id=1, source_target_pairs={{0,2},{1,3},{2,0},{3,1},{4,6},{5,7},{6,4},{7,5},{8,10},{9,11},{10,... | collective-permute-start | bytes 1363976 | tf_op jit(solution)/shard_map/ppermute | solution.py:569
  9.7 11.7 %collective-permute-start.1 = (bf16[48,1664]{1,0:T(8,128)(2,1)S(1)}, bf16[48,1664]{1,0:T(8,128)(2,1)S(1)}, u32[]{:S(2)}, u32[]{:S(2)}) collective-permute-start(bf16[48,1664]{1,0:T(8,128)(2,1)S(1)} %get-tuple-element.250.refs_0_), channel_id=1, source_target_pairs={{0,8},{1,9},{2,10},{3,11},{4,12},{5,13},{6,14},{7,15},{8,0},{9,1},... | collective-permute-start | bytes 479240 | tf_op jit(solution)/shard_map/ppermute | solution.py:565
  12.0 13.3 %collective-permute-start = (bf16[48,1664]{1,0:T(8,128)(2,1)S(1)}, bf16[48,1664]{1,0:T(8,128)(2,1)S(1)}, u32[]{:S(2)}, u32[]{:S(2)}) collective-permute-start(bf16[48,1664]{1,0:T(8,128)(2,1)S(1)} %get-tuple-element.250.refs_0_), channel_id=1, source_target_pairs={{0,4},{1,5},{2,6},{3,7},{4,8},{5,9},{6,10},{7,11},{8,12},{9,13},{1... | collective-permute-start | bytes 479240 | tf_op jit(solution)/shard_map/ppermute | solution.py:565
  28.2 18.1 %collective-permute-start.8 = (bf16[48,7424]{1,0:T(8,128)(2,1)S(1)}, bf16[48,7424]{1,0:T(8,128)(2,1)S(1)}, u32[]{:S(2)}, u32[]{:S(2)}) collective-permute-start(bf16[48,7424]{1,0:T(8,128)(2,1)S(1)} %pad_maximum_fusion.6), channel_id=1, source_target_pairs={{0,2},{1,3},{2,0},{3,1},{4,6},{5,7},{6,4},{7,5},{8,10},{9,11},{10,... | collective-permute-start | bytes 2138120 | tf_op jit(solution)/shard_map/ppermute | solution.py:569
  29.5 16.8 %collective-permute-start.7 = (bf16[48,7296]{1,0:T(8,128)(2,1)S(1)}, bf16[48,7296]{1,0:T(8,128)(2,1)S(1)}, u32[]{:S(2)}, u32[]{:S(2)}) collective-permute-start(bf16[48,7296]{1,0:T(8,128)(2,1)S(1)} %pad_maximum_fusion.7), channel_id=1, source_target_pairs={{0,1},{1,0},{2,3},{3,2},{4,5},{5,4},{6,7},{7,6},{8,9},{9,8},{10,11... | collective-permute-start | bytes 2101256 | tf_op jit(solution)/shard_map/ppermute | solution.py:569
  30.7 10.5 %collective-permute-start.10 = (bf16[48,1536]{1,0:T(8,128)(2,1)S(1)}, bf16[48,1536]{1,0:T(8,128)(2,1)S(1)}, u32[]{:S(2)}, u32[]{:S(2)}) collective-permute-start(bf16[48,1536]{1,0:T(8,128)(2,1)S(1)} %get-tuple-element.271.refs_0_), channel_id=1, source_target_pairs={{0,8},{1,9},{2,10},{3,11},{4,12},{5,13},{6,14},{7,15},{8,0},{9,1},... | collective-permute-start | bytes 442376 | tf_op jit(solution)/shard_map/ppermute | solution.py:565
  33.1 11.1 %collective-permute-start.9 = (bf16[48,1536]{1,0:T(8,128)(2,1)S(1)}, bf16[48,1536]{1,0:T(8,128)(2,1)S(1)}, u32[]{:S(2)}, u32[]{:S(2)}) collective-permute-start(bf16[48,1536]{1,0:T(8,128)(2,1)S(1)} %get-tuple-element.271.refs_0_), channel_id=1, source_target_pairs={{0,4},{1,5},{2,6},{3,7},{4,8},{5,9},{6,10},{7,11},{8,12},{9,13},{1... | collective-permute-start | bytes 442376 | tf_op jit(solution)/shard_map/ppermute | solution.py:565
  46.5 16.1 %collective-permute-start.13 = (bf16[48,7168]{1,0:T(8,128)(2,1)S(1)}, bf16[48,7168]{1,0:T(8,128)(2,1)S(1)}, u32[]{:S(2)}, u32[]{:S(2)}) collective-permute-start(bf16[48,7168]{1,0:T(8,128)(2,1)S(1)} %pad_maximum_fusion.8), channel_id=1, source_target_pairs={{0,2},{1,3},{2,0},{3,1},{4,6},{5,7},{6,4},{7,5},{8,10},{9,11},{10,... | collective-permute-start | bytes 2064392 | tf_op jit(solution)/shard_map/ppermute | solution.py:569
  47.1 15.4 %collective-permute-start.12 = (bf16[48,7040]{1,0:T(8,128)(2,1)S(1)}, bf16[48,7040]{1,0:T(8,128)(2,1)S(1)}, u32[]{:S(2)}, u32[]{:S(2)}) collective-permute-start(bf16[48,7040]{1,0:T(8,128)(2,1)S(1)} %pad_maximum_fusion.9), channel_id=1, source_target_pairs={{0,1},{1,0},{2,3},{3,2},{4,5},{5,4},{6,7},{7,6},{8,9},{9,8},{10,11... | collective-permute-start | bytes 2027528 | tf_op jit(solution)/shard_map/ppermute | solution.py:569
  48.3 10.5 %collective-permute-start.16 = (bf16[48,1536]{1,0:T(8,128)(2,1)S(1)}, bf16[48,1536]{1,0:T(8,128)(2,1)S(1)}, u32[]{:S(2)}, u32[]{:S(2)}) collective-permute-start(bf16[48,1536]{1,0:T(8,128)(2,1)S(1)} %get-tuple-element.282.refs_0_), channel_id=1, source_target_pairs={{0,8},{1,9},{2,10},{3,11},{4,12},{5,13},{6,14},{7,15},{8,0},{9,1},... | collective-permute-start | bytes 442376 | tf_op jit(solution)/shard_map/ppermute | solution.py:565
  50.8 11.2 %collective-permute-start.15 = (bf16[48,1536]{1,0:T(8,128)(2,1)S(1)}, bf16[48,1536]{1,0:T(8,128)(2,1)S(1)}, u32[]{:S(2)}, u32[]{:S(2)}) collective-permute-start(bf16[48,1536]{1,0:T(8,128)(2,1)S(1)} %get-tuple-element.282.refs_0_), channel_id=1, source_target_pairs={{0,4},{1,5},{2,6},{3,7},{4,8},{5,9},{6,10},{7,11},{8,12},{9,13},{1... | collective-permute-start | bytes 442376 | tf_op jit(solution)/shard_map/ppermute | solution.py:565
  62.7 14.3 %collective-permute-start.18 = (bf16[48,6912]{1,0:T(8,128)(2,1)S(1)}, bf16[48,6912]{1,0:T(8,128)(2,1)S(1)}, u32[]{:S(2)}, u32[]{:S(2)}) collective-permute-start(bf16[48,6912]{1,0:T(8,128)(2,1)S(1)} %get-tuple-element.286), channel_id=1, source_target_pairs={{0,1},{1,0},{2,3},{3,2},{4,5},{5,4},{6,7},{7,6},{8,9},{9,8},{10,11... | collective-permute-start | bytes 1990664 | tf_op jit(solution)/shard_map/ppermute | solution.py:569
  63.4 11.2 %collective-permute-start.32 = (bf16[48,1152]{1,0:T(8,128)(2,1)S(1)}, bf16[48,1152]{1,0:T(8,128)(2,1)S(1)}, u32[]{:S(2)}, u32[]{:S(2)}) collective-permute-start(bf16[48,1152]{1,0:T(8,128)(2,1)S(1)} %get-tuple-element.326), channel_id=1, source_target_pairs={{0,4},{1,5},{2,6},{3,7},{4,8},{5,9},{6,10},{7,11},{8,12},{9,13},{1... | collective-permute-start | bytes 331784 | tf_op jit(solution)/shard_map/ppermute | solution.py:565
  65.6 14.5 %collective-permute-start.19 = (bf16[48,6912]{1,0:T(8,128)(2,1)S(1)}, bf16[48,6912]{1,0:T(8,128)(2,1)S(1)}, u32[]{:S(2)}, u32[]{:S(2)}) collective-permute-start(bf16[48,6912]{1,0:T(8,128)(2,1)S(1)} %get-tuple-element.287), channel_id=1, source_target_pairs={{0,2},{1,3},{2,0},{3,1},{4,6},{5,7},{6,4},{7,5},{8,10},{9,11},{10,... | collective-permute-start | bytes 1990664 | tf_op jit(solution)/shard_map/ppermute | solution.py:569
  70.6 11.2 %collective-permute-start.20 = (bf16[8,48,384]{2,1,0:T(8,128)(2,1)S(1)}, bf16[8,48,384]{2,1,0:T(8,128)(2,1)S(1)}, u32[]{:S(2)}, u32[]{:S(2)}) collective-permute-start(bf16[8,48,384]{2,1,0:T(8,128)(2,1)S(1)} %get-tuple-element.291.low), channel_id=1, source_target_pairs={{0,16},{16,0},{1,17},{17,1},{2,18},{18,2},{3,19},{19,3},{4,20},{20... | collective-permute-start | bytes 884744 | tf_op jit(solution)/shard_map/ppermute | solution.py:573
  74.7 11.8 %collective-permute-start.34 = (bf16[48,1152]{1,0:T(8,128)(2,1)S(1)}, bf16[48,1152]{1,0:T(8,128)(2,1)S(1)}, u32[]{:S(2)}, u32[]{:S(2)}) collective-permute-start(bf16[48,1152]{1,0:T(8,128)(2,1)S(1)} %get-tuple-element.330), channel_id=1, source_target_pairs={{0,12},{1,13},{2,14},{3,15},{4,0},{5,1},{6,2},{7,3},{8,4},{9,5},{1... | collective-permute-start | bytes 331784 | tf_op jit(solution)/shard_map/ppermute | solution.py:565
  89.5 14.4 %collective-permute-start.35 = (bf16[48,4992]{1,0:T(8,128)(2,1)S(1)}, bf16[48,4992]{1,0:T(8,128)(2,1)S(1)}, u32[]{:S(2)}, u32[]{:S(2)}) collective-permute-start(bf16[48,4992]{1,0:T(8,128)(2,1)S(1)} %constant_dynamic-update-slice_fusion), channel_id=1, source_target_pairs={{0,1},{1,0},{2,3},{3,2},{4,5},{5,4},{6,7},{7,6},{8,9},{9,8},{10,11... | collective-permute-start | bytes 1437704 | tf_op jit(solution)/shard_map/ppermute | solution.py:569
  90.5 13.5 %collective-permute-start.36 = (bf16[48,4992]{1,0:T(8,128)(2,1)S(1)}, bf16[48,4992]{1,0:T(8,128)(2,1)S(1)}, u32[]{:S(2)}, u32[]{:S(2)}) collective-permute-start(bf16[48,4992]{1,0:T(8,128)(2,1)S(1)} %constant_dynamic-update-slice_fusion), channel_id=1, source_target_pairs={{0,2},{1,3},{2,0},{3,1},{4,6},{5,7},{6,4},{7,5},{8,10},{9,11},{10,... | collective-permute-start | bytes 1437704 | tf_op jit(solution)/shard_map/ppermute | solution.py:569
  118.7 15.0 %collective-permute-start.47 = (bf16[2,48,3072]{2,1,0:T(8,128)(2,1)S(1)}, bf16[2,48,3072]{2,1,0:T(8,128)(2,1)S(1)}, u32[]{:S(2)}, u32[]{:S(2)}) collective-permute-start(bf16[2,48,3072]{2,1,0:T(8,128)(2,1)S(1)} %get-tuple-element.365), channel_id=1, source_target_pairs={{0,2},{1,3},{2,0},{3,1},{4,6},{5,7},{6,4},{7,5},{8,10},{9,11},{10,... | collective-permute-start | bytes 1769480 | tf_op jit(solution)/shard_map/ppermute | solution.py:569
  119.7 14.6 %collective-permute-start.48 = (bf16[2,48,3072]{2,1,0:T(8,128)(2,1)S(1)}, bf16[2,48,3072]{2,1,0:T(8,128)(2,1)S(1)}, u32[]{:S(2)}, u32[]{:S(2)}) collective-permute-start(bf16[2,48,3072]{2,1,0:T(8,128)(2,1)S(1)} %get-tuple-element.367), channel_id=1, source_target_pairs={{0,1},{1,0},{2,3},{3,2},{4,5},{5,4},{6,7},{7,6},{8,9},{9,8},{10,11... | collective-permute-start | bytes 1769480 | tf_op jit(solution)/shard_map/ppermute | solution.py:569
  135.8 26.4 %collective-permute-start.58 = (bf16[4,48,3072]{2,1,0:T(8,128)(2,1)S(1)}, bf16[4,48,3072]{2,1,0:T(8,128)(2,1)S(1)}, u32[]{:S(2)}, u32[]{:S(2)}) collective-permute-start(bf16[4,48,3072]{2,1,0:T(8,128)(2,1)S(1)} %get-tuple-element.396), channel_id=1, source_target_pairs={{0,1},{1,0},{2,3},{3,2},{4,5},{5,4},{6,7},{7,6},{8,9},{9,8},{10,11... | collective-permute-start | bytes 3538952 | tf_op jit(solution)/shard_map/ppermute | solution.py:569
  136.6 26.1 %collective-permute-start.59 = (bf16[4,48,3072]{2,1,0:T(8,128)(2,1)S(1)}, bf16[4,48,3072]{2,1,0:T(8,128)(2,1)S(1)}, u32[]{:S(2)}, u32[]{:S(2)}) collective-permute-start(bf16[4,48,3072]{2,1,0:T(8,128)(2,1)S(1)} %get-tuple-element.397), channel_id=1, source_target_pairs={{0,2},{1,3},{2,0},{3,1},{4,6},{5,7},{6,4},{7,5},{8,10},{9,11},{10,... | collective-permute-start | bytes 3538952 | tf_op jit(solution)/shard_map/ppermute | solution.py:569
  164.1 16.2 %collective-permute-start.63 = (bf16[64,3072]{1,0:T(8,128)(2,1)S(1)}, bf16[64,3072]{1,0:T(8,128)(2,1)S(1)}, u32[]{:S(2)}, u32[]{:S(2)}) collective-permute-start(bf16[64,3072]{1,0:T(8,128)(2,1)S(1)} %get-tuple-element.423), channel_id=1, source_target_pairs={{0,12},{1,13},{2,14},{3,15},{4,0},{5,1},{6,2},{7,3},{8,4},{9,5},{1... | collective-permute-start | bytes 1179656 | tf_op jit(solution)/shard_map/ppermute | solution.py:565
  174.3 18.9 %collective-permute-start.66 = (bf16[64,3072]{1,0:T(8,128)(2,1)S(1)}, bf16[64,3072]{1,0:T(8,128)(2,1)S(1)}, u32[]{:S(2)}, u32[]{:S(2)}) collective-permute-start(bf16[64,3072]{1,0:T(8,128)(2,1)S(1)} %get-tuple-element.430), channel_id=1, source_target_pairs={{0,8},{1,9},{2,10},{3,11},{4,12},{5,13},{6,14},{7,15},{8,0},{9,1},... | collective-permute-start | bytes 1179656 | tf_op jit(solution)/shard_map/ppermute | solution.py:565
  180.3 12.9 %collective-permute-start.64 = (bf16[2,48,1536]{2,1,0:T(8,128)(2,1)S(1)}, bf16[2,48,1536]{2,1,0:T(8,128)(2,1)S(1)}, u32[]{:S(2)}, u32[]{:S(2)}) collective-permute-start(bf16[2,48,1536]{2,1,0:T(8,128)(2,1)S(1)} %get-tuple-element.424), channel_id=1, source_target_pairs={{0,2},{1,3},{2,0},{3,1},{4,6},{5,7},{6,4},{7,5},{8,10},{9,11},{10,... | collective-permute-start | bytes 884744 | tf_op jit(solution)/shard_map/ppermute | solution.py:569
  180.9 12.2 %collective-permute-start.65 = (bf16[2,48,1536]{2,1,0:T(8,128)(2,1)S(1)}, bf16[2,48,1536]{2,1,0:T(8,128)(2,1)S(1)}, u32[]{:S(2)}, u32[]{:S(2)}) collective-permute-start(bf16[2,48,1536]{2,1,0:T(8,128)(2,1)S(1)} %get-tuple-element.426), channel_id=1, source_target_pairs={{0,1},{1,0},{2,3},{3,2},{4,5},{5,4},{6,7},{7,6},{8,9},{9,8},{10,11... | collective-permute-start | bytes 884744 | tf_op jit(solution)/shard_map/ppermute | solution.py:569
  193.8 16.6 %collective-permute-start.68 = (bf16[4,48,1536]{2,1,0:T(8,128)(2,1)S(1)}, bf16[4,48,1536]{2,1,0:T(8,128)(2,1)S(1)}, u32[]{:S(2)}, u32[]{:S(2)}) collective-permute-start(bf16[4,48,1536]{2,1,0:T(8,128)(2,1)S(1)} %get-tuple-element.436), channel_id=1, source_target_pairs={{0,1},{1,0},{2,3},{3,2},{4,5},{5,4},{6,7},{7,6},{8,9},{9,8},{10,11... | collective-permute-start | bytes 1769480 | tf_op jit(solution)/shard_map/ppermute | solution.py:569
  194.5 15.9 %collective-permute-start.69 = (bf16[4,48,1536]{2,1,0:T(8,128)(2,1)S(1)}, bf16[4,48,1536]{2,1,0:T(8,128)(2,1)S(1)}, u32[]{:S(2)}, u32[]{:S(2)}) collective-permute-start(bf16[4,48,1536]{2,1,0:T(8,128)(2,1)S(1)} %get-tuple-element.437), channel_id=1, source_target_pairs={{0,2},{1,3},{2,0},{3,1},{4,6},{5,7},{6,4},{7,5},{8,10},{9,11},{10,... | collective-permute-start | bytes 1769480 | tf_op jit(solution)/shard_map/ppermute | solution.py:569
  195.2 11.0 %collective-permute-start.67 = (bf16[64,3072]{1,0:T(8,128)(2,1)S(1)}, bf16[64,3072]{1,0:T(8,128)(2,1)S(1)}, u32[]{:S(2)}, u32[]{:S(2)}) collective-permute-start(bf16[64,3072]{1,0:T(8,128)(2,1)S(1)} %get-tuple-element.435), channel_id=1, source_target_pairs={{0,4},{1,5},{2,6},{3,7},{4,8},{5,9},{6,10},{7,11},{8,12},{9,13},{1... | collective-permute-start | bytes 1179656 | tf_op jit(solution)/shard_map/ppermute | solution.py:565
  214.1 12.6 %collective-permute-start.80 = (bf16[96,768]{1,0:T(8,128)(2,1)S(1)}, bf16[96,768]{1,0:T(8,128)(2,1)S(1)}, u32[]{:S(2)}, u32[]{:S(2)}) collective-permute-start(bf16[96,768]{1,0:T(8,128)(2,1)S(1)} %pad_maximum_fusion.11.refs_0_), channel_id=1, source_target_pairs={{0,3},{1,2},{2,1},{3,0},{4,7},{5,6},{6,5},{7,4},{8,11},{9,10},{10,... | collective-permute-start | bytes 442376 | tf_op jit(solution)/shard_map/ppermute | solution.py:569
  215.5 11.2 %collective-permute-start.79 = (bf16[96,768]{1,0:T(8,128)(2,1)S(1)}, bf16[96,768]{1,0:T(8,128)(2,1)S(1)}, u32[]{:S(2)}, u32[]{:S(2)}) collective-permute-start(bf16[96,768]{1,0:T(8,128)(2,1)S(1)} %pad_maximum_fusion.11.refs_0_), channel_id=1, source_target_pairs={{0,2},{1,3},{2,0},{3,1},{4,6},{5,7},{6,4},{7,5},{8,10},{9,11},{10,... | collective-permute-start | bytes 442376 | tf_op jit(solution)/shard_map/ppermute | solution.py:569
  (61 other events, 310.1 us)

commit v15 on v13

--- a/solution.py
+++ b/solution.py
@@ -1811,7 +1811,6 @@
         ),
     )
     head_planes = plane_parts(head_row)
-    head_lines = line_parts(jnp.concatenate(head_planes))
     size = LINE // 2 * QUARTER_HALF
     cls_far = sent_both(
         after(cls_y[:, size:], *head_planes[1:]), after(cls_x[:, :size], *head_planes[1:])
@@ -1832,6 +1831,7 @@
         [pltpu.VMEM((both_rows, MODEL), LOW)],
     )
     second_got = other_core(second_low)
+    head_lines = line_parts(after(jnp.concatenate(head_planes), second_got))
     pre, first_grad_own, first_grad_send, up_sums = run_kernel(
         mlp_back_kernel,
         "seg_mlp_back",
@@ -1855,7 +1855,20 @@
             for count_of in (LINE // 2, LINE // 2, LINE, LINE, LINE)
         ]
 
-    head_lines = head_lines[:1] + together(*(after(got, pre) for got in head_lines[1:]))
+    mlp_data = (first_ordered, second_low, second_got, pre, act, order)
+    mlp_far = run_kernel(
+        mlp_far_kernel,
+        "seg_mlp_far",
+        part_shapes(FF)[:2],
+        where,
+        (),
+        mlp_data,
+        [pltpu.VMEM((both_rows, MODEL), LOW)],
+        flops=SEG * MODEL * FF,
+    )
+    head_lines = head_lines[:1] + together(
+        *(after(got, mlp_far[0]) for got in head_lines[1:])
+    )
     cls_far = together(*(after(got, *head_lines[1:]) for got in cls_far))
     cls_half, cls_out_half = run_kernel(
         cls_gather_kernel,
@@ -1867,17 +1880,6 @@
         where,
         (),
         cls_line + (cls_x, cls_y) + cls_far + (cls_out_piece,),
-    )
-    mlp_data = (first_ordered, second_low, second_got, after(pre, cls_half), act, order)
-    mlp_far = run_kernel(
-        mlp_far_kernel,
-        "seg_mlp_far",
-        part_shapes(FF)[:2],
-        where,
-        (),
-        mlp_data,
-        [pltpu.VMEM((both_rows, MODEL), LOW)],
-        flops=SEG * MODEL * FF,
     )
     mlp_parts = list(mlp_far) + list(
         run_kernel(

time: 241 us -> 237 us (0.983)
  waiting for transfers between devices: 84.6 us -> 81.1 us
    ppermute x36, waiting for transfers between devices: 65 us -> 59.9 us  [along_line(): return lax.ppermute(value, 'fsdp', line_pairs(apart))]
  transfers between devices with their start and end apart: 85 -> 85, of which waited for: 40 -> 36; matrix products, arithmetic and copies ran while one was open for 0% -> 0% of each run, Pallas kernels for 14% -> 14%
where the time goes in v15:
time: 237 us; the launch traced here: 235 us
  starting transfers between devices  96.4 us (41%)
  waiting for transfers between devices  81.1 us (34%)
  Pallas kernels  49.2 us (21%)
  local copies, waits for them, and re-layouts  5.34 us (2%)
    ppermute x36, waiting for transfers between devices, along_line(): return lax.ppermute(value, 'fsdp', line_pairs(apart))  59.9 us
    pallas_call x27, Pallas kernels, run_kernel(): pl.pallas_call(body, name=name, out_shape=tuple(outs), in_specs=in_specs,...  49.2 us
    ppermute x36, starting transfers between devices, along_line(): return lax.ppermute(value, 'fsdp', line_pairs(apart))  44.4 us
    ppermute x21, starting transfers between devices, other_core(): return lax.ppermute(value, 'rep', [(0, 1), (1, 0)])  30.3 us
    ppermute x28, starting transfers between devices, in_plane(): return lax.ppermute(value, 'fsdp', plane_pairs(mask))  21.7 us
    ppermute x21, waiting for transfers between devices, other_core(): return lax.ppermute(value, 'rep', [(0, 1), (1, 0)])  10.8 us
    ppermute x28, waiting for transfers between devices, in_plane(): return lax.ppermute(value, 'fsdp', plane_pairs(mask))  10.4 us
  transfers between devices with their start and end apart: 85, of which 36 were waited for; matrix products, arithmetic and copies ran while one was open for 0% of the time, Pallas kernels for 14%

profile of v15, /device:TPU:13, one launch (start us, length us, event | category | flops | bytes accessed | tf_op | source)
XLA Modules:
  0.0 234.7 jit_solution(15395315998758202539)
XLA Ops:
  9.7 2.3 collective-permute-start.1
  14.2 7.2 %collective-permute-done.1.refs_2_ = bf16[48,1664]{1,0:T(8,128)(2,1)S(1)} collective-permute-done((bf16[48,1664]{1,0:T(8,128)(2,1)S(1)}, bf16[48,1664]{1,0:T(8,128)(2,1)S(1)}, u32[]{:S(2)}, u32[]{:S(2)}) %collective-permute-start.1) | collective-permute-done | bytes 159776 | tf_op jit(solution)/shard_map/ppermute | solution.py:565
  21.4 3.9 %collective-permute-done.refs_1_ = bf16[48,1664]{1,0:T(8,128)(2,1)S(1)} collective-permute-done((bf16[48,1664]{1,0:T(8,128)(2,1)S(1)}, bf16[48,1664]{1,0:T(8,128)(2,1)S(1)}, u32[]{:S(2)}, u32[]{:S(2)}) %collective-permute-start) | collective-permute-done | bytes 159776 | tf_op jit(solution)/shard_map/ppermute | solution.py:565
  30.7 2.5 %collective-permute-start.10 = (bf16[48,1536]{1,0:T(8,128)(2,1)S(1)}, bf16[48,1536]{1,0:T(8,128)(2,1)S(1)}, u32[]{:S(2)}, u32[]{:S(2)}) collective-permute-start(bf16[48,1536]{1,0:T(8,128)(2,1)S(1)} %get-tuple-element.277.refs_0_), channel_id=1, source_target_pairs={{0,8},{1,9},{2,10},{3,11},{4,12},{5,13},{6,14},{7,15},{8,0},{9,1},... | collective-permute-start | bytes 442376 | tf_op jit(solution)/shard_map/ppermute | solution.py:565
  33.1 2.3 collective-permute-done.11.refs_3_
  35.5 5.6 %collective-permute-done.10.refs_2_ = bf16[48,1536]{1,0:T(8,128)(2,1)S(1)} collective-permute-done((bf16[48,1536]{1,0:T(8,128)(2,1)S(1)}, bf16[48,1536]{1,0:T(8,128)(2,1)S(1)}, u32[]{:S(2)}, u32[]{:S(2)}) %collective-permute-start.10) | collective-permute-done | bytes 147488 | tf_op jit(solution)/shard_map/ppermute | solution.py:565
  41.1 3.2 %collective-permute-done.9.refs_1_ = bf16[48,1536]{1,0:T(8,128)(2,1)S(1)} collective-permute-done((bf16[48,1536]{1,0:T(8,128)(2,1)S(1)}, bf16[48,1536]{1,0:T(8,128)(2,1)S(1)}, u32[]{:S(2)}, u32[]{:S(2)}) %collective-permute-start.9) | collective-permute-done | bytes 147488 | tf_op jit(solution)/shard_map/ppermute | solution.py:565
  48.3 2.5 %collective-permute-start.16 = (bf16[48,1536]{1,0:T(8,128)(2,1)S(1)}, bf16[48,1536]{1,0:T(8,128)(2,1)S(1)}, u32[]{:S(2)}, u32[]{:S(2)}) collective-permute-start(bf16[48,1536]{1,0:T(8,128)(2,1)S(1)} %get-tuple-element.288.refs_0_), channel_id=1, source_target_pairs={{0,8},{1,9},{2,10},{3,11},{4,12},{5,13},{6,14},{7,15},{8,0},{9,1},... | collective-permute-start | bytes 442376 | tf_op jit(solution)/shard_map/ppermute | solution.py:565
  52.4 6.4 %collective-permute-done.16.refs_2_ = bf16[48,1536]{1,0:T(8,128)(2,1)S(1)} collective-permute-done((bf16[48,1536]{1,0:T(8,128)(2,1)S(1)}, bf16[48,1536]{1,0:T(8,128)(2,1)S(1)}, u32[]{:S(2)}, u32[]{:S(2)}) %collective-permute-start.16) | collective-permute-done | bytes 147488 | tf_op jit(solution)/shard_map/ppermute | solution.py:565
  58.8 3.2 %collective-permute-done.15.refs_1_ = bf16[48,1536]{1,0:T(8,128)(2,1)S(1)} collective-permute-done((bf16[48,1536]{1,0:T(8,128)(2,1)S(1)}, bf16[48,1536]{1,0:T(8,128)(2,1)S(1)}, u32[]{:S(2)}, u32[]{:S(2)}) %collective-permute-start.15) | collective-permute-done | bytes 147488 | tf_op jit(solution)/shard_map/ppermute | solution.py:565
  66.7 3.9 %seg_qkv.1 = (bf16[16,48,1152]{2,1,0:T(8,128)(2,1)S(1)}, bf16[8,48,384]{2,1,0:T(8,128)(2,1)S(1)}, bf16[8,48,384]{2,1,0:T(8,128)(2,1)S(1)}, bf16[256,1152]{1,0:T(...) custom-call(s32[5]{0:T(128)S(1)} %stack.15.where, ...), custom_call_target="tpu_custom_call" | custom-call | flops 452984832 | bytes 11453440 | tf_op jit(solution)/shard_map/seg_qkv/pallas_call | solution.py:595
  70.6 4.1 %collective-permute-start.20 = (bf16[8,48,384]{2,1,0:T(8,128)(2,1)S(1)}, bf16[8,48,384]{2,1,0:T(8,128)(2,1)S(1)}, u32[]{:S(2)}, u32[]{:S(2)}) collective-permute-start(bf16[8,48,384]{2,1,0:T(8,128)(2,1)S(1)} %get-tuple-element.297.low), channel_id=1, source_target_pairs={{0,16},{16,0},{1,17},{17,1},{2,18},{18,2},{3,19},{19,3},{4,20},{20... | collective-permute-start | bytes 884744 | tf_op jit(solution)/shard_map/ppermute | solution.py:573
  74.8 2.2 collective-permute-done.18.refs_10_.refs_8_
  77.0 3.1 %collective-permute-start.14 = (bf16[256,384]{1,0:T(8,128)(2,1)S(1)}, bf16[256,384]{1,0:T(8,128)(2,1)S(1)}, u32[]{:S(2)}, u32[]{:S(2)}) collective-permute-start(bf16[256,384]{1,0:T(8,128)(2,1)S(1)} %get-tuple-element.287.mixed), channel_id=1, source_target_pairs={{0,16},{16,0},{1,17},{17,1},{2,18},{18,2},{3,19},{19,3},{4,20},{20... | collective-permute-start | bytes 589832 | tf_op jit(solution)/shard_map/ppermute | solution.py:573
  83.2 3.3 %collective-permute-start.24 = (bf16[128,768]{1,0:T(8,128)(2,1)S(1)}, bf16[128,768]{1,0:T(8,128)(2,1)S(1)}, u32[]{:S(2)}, u32[]{:S(2)}) collective-permute-start(bf16[128,768]{1,0:T(8,128)(2,1)S(1)} %get-tuple-element.306.refs_12_.refs_5_.refs_6_), channel_id=1, source_target_pairs={{0,16},{16,0},{1,17},{17,1},{2,18},{18,2},{3,19},{19,3},{4,20},{20... | collective-permute-start | bytes 589832 | tf_op jit(solution)/shard_map/ppermute | solution.py:573
  92.6 3.0 %collective-permute-start.25 = (f32[128,768]{1,0:T(8,128)S(1)}, f32[128,768]{1,0:T(8,128)S(1)}, u32[]{:S(2)}, u32[]{:S(2)}) collective-permute-start(f32[128,768]{1,0:T(8,128)S(1)} %get-tuple-element.310), channel_id=1, source_target_pairs={{0,16},{16,0},{1,17},{17,1},{2,18},{18,2},{3,19},{19,3},{4,20},{20... | collective-permute-start | bytes 1179656 | tf_op jit(solution)/shard_map/ppermute | solution.py:573
  105.6 2.8 %collective-permute-start.33 = (f32[4,1664]{1,0:T(4,128)S(1)}, f32[4,1664]{1,0:T(4,128)S(1)}, u32[]{:S(2)}, u32[]{:S(2)}) collective-permute-start(f32[4,1664]{1,0:T(4,128)S(1)} %pad_maximum_fusion.12.refs_0_), channel_id=1, source_target_pairs={{0,8},{1,9},{2,10},{3,11},{4,12},{5,13},{6,14},{7,15},{8,0},{9,1},... | collective-permute-start | bytes 79880 | tf_op jit(solution)/shard_map/ppermute | solution.py:565
  125.3 2.5 %seg_mlp_near.1 = (bf16[4,48,3072]{2,1,0:T(8,128)(2,1)S(1)}, bf16[4,48,3072]{2,1,0:T(8,128)(2,1)S(1)}, bf16[4,48,3072]{2,1,0:T(8,128)(2,1)S(1)}) custom-call(s32[5]{0:T(128)S(1)} %stack.15.where, bf16[256,1024]{1,0:T(8,128)(2,1)S(1)} %get-tuple-element.329.refs_0_, bf16[128,768]{1,0:T(8,128)(2,1)S(1)} %get-tuple-element.318.refs_0_.refs_1_, ...), custom_call_target="tpu_custom_call" | custom-call | flops 905969664 | bytes 7602176 | tf_op jit(solution)/shard_map/seg_mlp_near/pallas_call | solution.py:595
  140.4 2.3 collective-permute-start.54
  146.5 2.3 head_attend_back.1
  154.9 2.8 %collective-permute-done.58.refs_13_ = bf16[4,48,3072]{2,1,0:T(8,128)(2,1)S(1)} collective-permute-done((bf16[4,48,3072]{2,1,0:T(8,128)(2,1)S(1)}, bf16[4,48,3072]{2,1,0:T(8,128)(2,1)S(1)}, u32[]{:S(2)}, u32[]{:S(2)}) %collective-permute-start.58) | collective-permute-done | bytes 1179680 | tf_op jit(solution)/shard_map/ppermute | solution.py:569
  161.6 3.0 %collective-permute-start.60 = (f32[1,768]{1,0:T(1,128)S(1)}, f32[1,768]{1,0:T(1,128)S(1)}, u32[]{:S(2)}, u32[]{:S(2)}) collective-permute-start(f32[1,768]{1,0:T(1,128)S(1)} %get-tuple-element.416.refs_0_.refs_3_), channel_id=1, source_target_pairs={{0,16},{16,0},{1,17},{17,1},{2,18},{18,2},{3,19},{19,3},{4,20},{20... | collective-permute-start | bytes 9224 | tf_op jit(solution)/shard_map/ppermute | solution.py:573
  170.9 3.8 %seg_attn_back.1.refs_2_ = bf16[256,1152]{1,0:T(8,128)(2,1)S(1)} custom-call(s32[5]{0:T(128)S(1)} %stack.15.where, bf16[256,1152]{1,0:T(8,128)(2,1)S(1)} %get-tuple-element.301.refs_0_, bf16[128,768]{1,0:T(8,128)(2,1)S(1)} %get-tuple-element.421.refs_1_, bf16[128,768]{1,0:T(8,128)(2,1)S(1)} %collective-permute-done.62.refs_2_.refs_4_, ...), custom_call_target="tpu_custom_call" | custom-call | flops 452984832 | bytes 1573888 | tf_op jit(solution)/shard_map/seg_attn_back/pallas_call | solution.py:595
  177.3 2.8 %seg_attn_near.1 = (bf16[4,48,1536]{2,1,0:T(8,128)(2,1)S(1)}, bf16[4,48,1536]{2,1,0:T(8,128)(2,1)S(1)}, bf16[4,48,1536]{2,1,0:T(8,128)(2,1)S(1)}, bf16[128,768]{...) custom-call(s32[5]{0:T(128)S(1)} %stack.15.where, ...), custom_call_target="tpu_custom_call" | custom-call | flops 452984832 | bytes 7444992 | tf_op jit(solution)/shard_map/seg_attn_near/pallas_call | solution.py:595
  180.1 8.2 %collective-permute-done.66.refs_2_ = bf16[64,3072]{1,0:T(8,128)(2,1)S(1)} collective-permute-done((bf16[64,3072]{1,0:T(8,128)(2,1)S(1)}, bf16[64,3072]{1,0:T(8,128)(2,1)S(1)}, u32[]{:S(2)}, u32[]{:S(2)}) %collective-permute-start.66) | collective-permute-done | bytes 393248 | tf_op jit(solution)/shard_map/ppermute | solution.py:565
  194.4 7.4 %collective-permute-done.67.refs_1_ = bf16[64,3072]{1,0:T(8,128)(2,1)S(1)} collective-permute-done((bf16[64,3072]{1,0:T(8,128)(2,1)S(1)}, bf16[64,3072]{1,0:T(8,128)(2,1)S(1)}, u32[]{:S(2)}, u32[]{:S(2)}) %collective-permute-start.67) | collective-permute-done | bytes 393248 | tf_op jit(solution)/shard_map/ppermute | solution.py:565
  201.8 3.0 %collective-permute-start.77 = (bf16[24,768]{1,0:T(8,128)(2,1)S(1)}, bf16[24,768]{1,0:T(8,128)(2,1)S(1)}, u32[]{:S(2)}, u32[]{:S(2)}) collective-permute-start(bf16[24,768]{1,0:T(8,128)(2,1)S(1)} %get-tuple-element.474), channel_id=1, source_target_pairs={{0,12},{1,13},{2,14},{3,15},{4,0},{5,1},{6,2},{7,3},{8,4},{9,5},{1... | collective-permute-start | bytes 110600 | tf_op jit(solution)/shard_map/ppermute | solution.py:565
  214.3 4.0 %collective-permute-done.73 = bf16[48,1536]{1,0:T(8,128)(2,1)S(1)} collective-permute-done((bf16[48,1536]{1,0:T(8,128)(2,1)S(1)}, bf16[48,1536]{1,0:T(8,128)(2,1)S(1)}, u32[]{:S(2)}, u32[]{:S(2)}) %collective-permute-start.73) | collective-permute-done | bytes 147488 | tf_op jit(solution)/shard_map/ppermute | solution.py:565
  218.3 2.3 collective-permute-start.81
  222.2 4.4 %head_owner.1 = (f32[48,3072]{1,0:T(8,128)S(1)}, f32[16,768]{1,0:T(8,128)S(1)}, f32[48,9216]{1,0:T(8,128)}, f32[576]{0:T(1024)}, f32[16,768]{1,0:T(8,128)}, /*index=5*/f32[1,1]{1,0:T(1,128)}) custom-call(s32[5]{0:T(128)S(1)} %stack.15.where, bf16[96,768]{1,0:T(8,128)(2,1)S(1)} %pad_maximum_fusion.11.refs_0_, ...), custom_call_target="tpu_custom_call" | custom-call | flops 28311552 | bytes 4503812 | tf_op jit(solution)/shard_map/head_owner/pallas_call | solution.py:595
  226.6 2.4 %collective-permute-start.83 = (f32[48,3072]{1,0:T(8,128)S(1)}, f32[48,3072]{1,0:T(8,128)S(1)}, u32[]{:S(2)}, u32[]{:S(2)}) collective-permute-start(f32[48,3072]{1,0:T(8,128)S(1)} %get-tuple-element.488.mlp), channel_id=1, source_target_pairs={{0,16},{16,0},{1,17},{17,1},{2,18},{18,2},{3,19},{19,3},{4,20},{20... | collective-permute-start | bytes 1769480 | tf_op jit(solution)/shard_map/ppermute | solution.py:573
  231.2 3.3 %seg_owner.1 = (f32[48,9216]{1,0:T(8,128)}, f32[576]{0:T(1024)}) custom-call(s32[5]{0:T(128)S(1)} %stack.15.where, f32[48,1536]{1,0:T(8,128)S(1)} %convert_add_fusion.1.attn, f32[48,1536]{1,0:T(8,128)S(1)} %collective-permute-done.82.attn_got, f32[48,3072]{1,0:T(8,128)S(1)} %get-tuple-element.488.mlp, f32[48,3072]{1,0:T(8,128)S(1)} %collective-permute-done.83.mlp_got, ...), custom_call_target="tpu_custom_call" | custom-call | bytes 3639552 | tf_op jit(solution)/shard_map/seg_owner/pallas_call | solution.py:595
  (213 shorter events, 116.8 us)
Async XLA Ops:
  8.0 17.3 %collective-permute-start.3 = (bf16[48,4736]{1,0:T(8,128)(2,1)S(1)}, bf16[48,4736]{1,0:T(8,128)(2,1)S(1)}, u32[]{:S(2)}, u32[]{:S(2)}) collective-permute-start(bf16[48,4736]{1,0:T(8,128)(2,1)S(1)} %pad_maximum_fusion.10), channel_id=1, source_target_pairs={{0,1},{1,0},{2,3},{3,2},{4,5},{5,4},{6,7},{7,6},{8,9},{9,8},{10,11... | collective-permute-start | bytes 1363976 | tf_op jit(solution)/shard_map/ppermute | solution.py:569
  9.3 16.0 %collective-permute-start.4 = (bf16[48,4736]{1,0:T(8,128)(2,1)S(1)}, bf16[48,4736]{1,0:T(8,128)(2,1)S(1)}, u32[]{:S(2)}, u32[]{:S(2)}) collective-permute-start(bf16[48,4736]{1,0:T(8,128)(2,1)S(1)} %pad_maximum_fusion.10), channel_id=1, source_target_pairs={{0,2},{1,3},{2,0},{3,1},{4,6},{5,7},{6,4},{7,5},{8,10},{9,11},{10,... | collective-permute-start | bytes 1363976 | tf_op jit(solution)/shard_map/ppermute | solution.py:569
  9.7 11.7 %collective-permute-start.1 = (bf16[48,1664]{1,0:T(8,128)(2,1)S(1)}, bf16[48,1664]{1,0:T(8,128)(2,1)S(1)}, u32[]{:S(2)}, u32[]{:S(2)}) collective-permute-start(bf16[48,1664]{1,0:T(8,128)(2,1)S(1)} %get-tuple-element.256.refs_0_), channel_id=1, source_target_pairs={{0,8},{1,9},{2,10},{3,11},{4,12},{5,13},{6,14},{7,15},{8,0},{9,1},... | collective-permute-start | bytes 479240 | tf_op jit(solution)/shard_map/ppermute | solution.py:565
  12.0 13.3 %collective-permute-start = (bf16[48,1664]{1,0:T(8,128)(2,1)S(1)}, bf16[48,1664]{1,0:T(8,128)(2,1)S(1)}, u32[]{:S(2)}, u32[]{:S(2)}) collective-permute-start(bf16[48,1664]{1,0:T(8,128)(2,1)S(1)} %get-tuple-element.256.refs_0_), channel_id=1, source_target_pairs={{0,4},{1,5},{2,6},{3,7},{4,8},{5,9},{6,10},{7,11},{8,12},{9,13},{1... | collective-permute-start | bytes 479240 | tf_op jit(solution)/shard_map/ppermute | solution.py:565
  28.2 18.1 %collective-permute-start.8 = (bf16[48,7424]{1,0:T(8,128)(2,1)S(1)}, bf16[48,7424]{1,0:T(8,128)(2,1)S(1)}, u32[]{:S(2)}, u32[]{:S(2)}) collective-permute-start(bf16[48,7424]{1,0:T(8,128)(2,1)S(1)} %pad_maximum_fusion.6), channel_id=1, source_target_pairs={{0,2},{1,3},{2,0},{3,1},{4,6},{5,7},{6,4},{7,5},{8,10},{9,11},{10,... | collective-permute-start | bytes 2138120 | tf_op jit(solution)/shard_map/ppermute | solution.py:569
  29.5 16.8 %collective-permute-start.7 = (bf16[48,7296]{1,0:T(8,128)(2,1)S(1)}, bf16[48,7296]{1,0:T(8,128)(2,1)S(1)}, u32[]{:S(2)}, u32[]{:S(2)}) collective-permute-start(bf16[48,7296]{1,0:T(8,128)(2,1)S(1)} %pad_maximum_fusion.7), channel_id=1, source_target_pairs={{0,1},{1,0},{2,3},{3,2},{4,5},{5,4},{6,7},{7,6},{8,9},{9,8},{10,11... | collective-permute-start | bytes 2101256 | tf_op jit(solution)/shard_map/ppermute | solution.py:569
  33.1 11.1 %collective-permute-start.9 = (bf16[48,1536]{1,0:T(8,128)(2,1)S(1)}, bf16[48,1536]{1,0:T(8,128)(2,1)S(1)}, u32[]{:S(2)}, u32[]{:S(2)}) collective-permute-start(bf16[48,1536]{1,0:T(8,128)(2,1)S(1)} %get-tuple-element.277.refs_0_), channel_id=1, source_target_pairs={{0,4},{1,5},{2,6},{3,7},{4,8},{5,9},{6,10},{7,11},{8,12},{9,13},{1... | collective-permute-start | bytes 442376 | tf_op jit(solution)/shard_map/ppermute | solution.py:565
  46.5 16.1 %collective-permute-start.13 = (bf16[48,7168]{1,0:T(8,128)(2,1)S(1)}, bf16[48,7168]{1,0:T(8,128)(2,1)S(1)}, u32[]{:S(2)}, u32[]{:S(2)}) collective-permute-start(bf16[48,7168]{1,0:T(8,128)(2,1)S(1)} %pad_maximum_fusion.8), channel_id=1, source_target_pairs={{0,2},{1,3},{2,0},{3,1},{4,6},{5,7},{6,4},{7,5},{8,10},{9,11},{10,... | collective-permute-start | bytes 2064392 | tf_op jit(solution)/shard_map/ppermute | solution.py:569
  47.1 15.4 %collective-permute-start.12 = (bf16[48,7040]{1,0:T(8,128)(2,1)S(1)}, bf16[48,7040]{1,0:T(8,128)(2,1)S(1)}, u32[]{:S(2)}, u32[]{:S(2)}) collective-permute-start(bf16[48,7040]{1,0:T(8,128)(2,1)S(1)} %pad_maximum_fusion.9), channel_id=1, source_target_pairs={{0,1},{1,0},{2,3},{3,2},{4,5},{5,4},{6,7},{7,6},{8,9},{9,8},{10,11... | collective-permute-start | bytes 2027528 | tf_op jit(solution)/shard_map/ppermute | solution.py:569
  48.3 10.5 %collective-permute-start.16 = (bf16[48,1536]{1,0:T(8,128)(2,1)S(1)}, bf16[48,1536]{1,0:T(8,128)(2,1)S(1)}, u32[]{:S(2)}, u32[]{:S(2)}) collective-permute-start(bf16[48,1536]{1,0:T(8,128)(2,1)S(1)} %get-tuple-element.288.refs_0_), channel_id=1, source_target_pairs={{0,8},{1,9},{2,10},{3,11},{4,12},{5,13},{6,14},{7,15},{8,0},{9,1},... | collective-permute-start | bytes 442376 | tf_op jit(solution)/shard_map/ppermute | solution.py:565
  50.8 11.2 %collective-permute-start.15 = (bf16[48,1536]{1,0:T(8,128)(2,1)S(1)}, bf16[48,1536]{1,0:T(8,128)(2,1)S(1)}, u32[]{:S(2)}, u32[]{:S(2)}) collective-permute-start(bf16[48,1536]{1,0:T(8,128)(2,1)S(1)} %get-tuple-element.288.refs_0_), channel_id=1, source_target_pairs={{0,4},{1,5},{2,6},{3,7},{4,8},{5,9},{6,10},{7,11},{8,12},{9,13},{1... | collective-permute-start | bytes 442376 | tf_op jit(solution)/shard_map/ppermute | solution.py:565
  62.7 14.3 %collective-permute-start.18 = (bf16[48,6912]{1,0:T(8,128)(2,1)S(1)}, bf16[48,6912]{1,0:T(8,128)(2,1)S(1)}, u32[]{:S(2)}, u32[]{:S(2)}) collective-permute-start(bf16[48,6912]{1,0:T(8,128)(2,1)S(1)} %get-tuple-element.292), channel_id=1, source_target_pairs={{0,1},{1,0},{2,3},{3,2},{4,5},{5,4},{6,7},{7,6},{8,9},{9,8},{10,11... | collective-permute-start | bytes 1990664 | tf_op jit(solution)/shard_map/ppermute | solution.py:569
  63.4 11.2 %collective-permute-start.35 = (bf16[48,1152]{1,0:T(8,128)(2,1)S(1)}, bf16[48,1152]{1,0:T(8,128)(2,1)S(1)}, u32[]{:S(2)}, u32[]{:S(2)}) collective-permute-start(bf16[48,1152]{1,0:T(8,128)(2,1)S(1)} %get-tuple-element.347), channel_id=1, source_target_pairs={{0,4},{1,5},{2,6},{3,7},{4,8},{5,9},{6,10},{7,11},{8,12},{9,13},{1... | collective-permute-start | bytes 331784 | tf_op jit(solution)/shard_map/ppermute | solution.py:565
  65.6 14.5 %collective-permute-start.19 = (bf16[48,6912]{1,0:T(8,128)(2,1)S(1)}, bf16[48,6912]{1,0:T(8,128)(2,1)S(1)}, u32[]{:S(2)}, u32[]{:S(2)}) collective-permute-start(bf16[48,6912]{1,0:T(8,128)(2,1)S(1)} %get-tuple-element.293), channel_id=1, source_target_pairs={{0,2},{1,3},{2,0},{3,1},{4,6},{5,7},{6,4},{7,5},{8,10},{9,11},{10,... | collective-permute-start | bytes 1990664 | tf_op jit(solution)/shard_map/ppermute | solution.py:569
  70.6 11.2 %collective-permute-start.20 = (bf16[8,48,384]{2,1,0:T(8,128)(2,1)S(1)}, bf16[8,48,384]{2,1,0:T(8,128)(2,1)S(1)}, u32[]{:S(2)}, u32[]{:S(2)}) collective-permute-start(bf16[8,48,384]{2,1,0:T(8,128)(2,1)S(1)} %get-tuple-element.297.low), channel_id=1, source_target_pairs={{0,16},{16,0},{1,17},{17,1},{2,18},{18,2},{3,19},{19,3},{4,20},{20... | collective-permute-start | bytes 884744 | tf_op jit(solution)/shard_map/ppermute | solution.py:573
  74.7 11.8 %collective-permute-start.37 = (bf16[48,1152]{1,0:T(8,128)(2,1)S(1)}, bf16[48,1152]{1,0:T(8,128)(2,1)S(1)}, u32[]{:S(2)}, u32[]{:S(2)}) collective-permute-start(bf16[48,1152]{1,0:T(8,128)(2,1)S(1)} %get-tuple-element.351), channel_id=1, source_target_pairs={{0,12},{1,13},{2,14},{3,15},{4,0},{5,1},{6,2},{7,3},{8,4},{9,5},{1... | collective-permute-start | bytes 331784 | tf_op jit(solution)/shard_map/ppermute | solution.py:565
  89.5 14.4 %collective-permute-start.38 = (bf16[48,4992]{1,0:T(8,128)(2,1)S(1)}, bf16[48,4992]{1,0:T(8,128)(2,1)S(1)}, u32[]{:S(2)}, u32[]{:S(2)}) collective-permute-start(bf16[48,4992]{1,0:T(8,128)(2,1)S(1)} %constant_dynamic-update-slice_fusion), channel_id=1, source_target_pairs={{0,1},{1,0},{2,3},{3,2},{4,5},{5,4},{6,7},{7,6},{8,9},{9,8},{10,11... | collective-permute-start | bytes 1437704 | tf_op jit(solution)/shard_map/ppermute | solution.py:569
  90.5 13.5 %collective-permute-start.39 = (bf16[48,4992]{1,0:T(8,128)(2,1)S(1)}, bf16[48,4992]{1,0:T(8,128)(2,1)S(1)}, u32[]{:S(2)}, u32[]{:S(2)}) collective-permute-start(bf16[48,4992]{1,0:T(8,128)(2,1)S(1)} %constant_dynamic-update-slice_fusion), channel_id=1, source_target_pairs={{0,2},{1,3},{2,0},{3,1},{4,6},{5,7},{6,4},{7,5},{8,10},{9,11},{10,... | collective-permute-start | bytes 1437704 | tf_op jit(solution)/shard_map/ppermute | solution.py:569
  114.6 14.9 %collective-permute-start.47 = (bf16[2,48,3072]{2,1,0:T(8,128)(2,1)S(1)}, bf16[2,48,3072]{2,1,0:T(8,128)(2,1)S(1)}, u32[]{:S(2)}, u32[]{:S(2)}) collective-permute-start(bf16[2,48,3072]{2,1,0:T(8,128)(2,1)S(1)} %get-tuple-element.377), channel_id=1, source_target_pairs={{0,2},{1,3},{2,0},{3,1},{4,6},{5,7},{6,4},{7,5},{8,10},{9,11},{10,... | collective-permute-start | bytes 1769480 | tf_op jit(solution)/shard_map/ppermute | solution.py:569
  115.3 14.6 %collective-permute-start.48 = (bf16[2,48,3072]{2,1,0:T(8,128)(2,1)S(1)}, bf16[2,48,3072]{2,1,0:T(8,128)(2,1)S(1)}, u32[]{:S(2)}, u32[]{:S(2)}) collective-permute-start(bf16[2,48,3072]{2,1,0:T(8,128)(2,1)S(1)} %get-tuple-element.379), channel_id=1, source_target_pairs={{0,1},{1,0},{2,3},{3,2},{4,5},{5,4},{6,7},{7,6},{8,9},{9,8},{10,11... | collective-permute-start | bytes 1769480 | tf_op jit(solution)/shard_map/ppermute | solution.py:569
  131.3 26.4 %collective-permute-start.58 = (bf16[4,48,3072]{2,1,0:T(8,128)(2,1)S(1)}, bf16[4,48,3072]{2,1,0:T(8,128)(2,1)S(1)}, u32[]{:S(2)}, u32[]{:S(2)}) collective-permute-start(bf16[4,48,3072]{2,1,0:T(8,128)(2,1)S(1)} %get-tuple-element.408), channel_id=1, source_target_pairs={{0,1},{1,0},{2,3},{3,2},{4,5},{5,4},{6,7},{7,6},{8,9},{9,8},{10,11... | collective-permute-start | bytes 3538952 | tf_op jit(solution)/shard_map/ppermute | solution.py:569
  132.3 26.0 %collective-permute-start.59 = (bf16[4,48,3072]{2,1,0:T(8,128)(2,1)S(1)}, bf16[4,48,3072]{2,1,0:T(8,128)(2,1)S(1)}, u32[]{:S(2)}, u32[]{:S(2)}) collective-permute-start(bf16[4,48,3072]{2,1,0:T(8,128)(2,1)S(1)} %get-tuple-element.409), channel_id=1, source_target_pairs={{0,2},{1,3},{2,0},{3,1},{4,6},{5,7},{6,4},{7,5},{8,10},{9,11},{10,... | collective-permute-start | bytes 3538952 | tf_op jit(solution)/shard_map/ppermute | solution.py:569
  159.8 16.0 %collective-permute-start.63 = (bf16[64,3072]{1,0:T(8,128)(2,1)S(1)}, bf16[64,3072]{1,0:T(8,128)(2,1)S(1)}, u32[]{:S(2)}, u32[]{:S(2)}) collective-permute-start(bf16[64,3072]{1,0:T(8,128)(2,1)S(1)} %get-tuple-element.435), channel_id=1, source_target_pairs={{0,12},{1,13},{2,14},{3,15},{4,0},{5,1},{6,2},{7,3},{8,4},{9,5},{1... | collective-permute-start | bytes 1179656 | tf_op jit(solution)/shard_map/ppermute | solution.py:565
  169.8 18.5 %collective-permute-start.66 = (bf16[64,3072]{1,0:T(8,128)(2,1)S(1)}, bf16[64,3072]{1,0:T(8,128)(2,1)S(1)}, u32[]{:S(2)}, u32[]{:S(2)}) collective-permute-start(bf16[64,3072]{1,0:T(8,128)(2,1)S(1)} %get-tuple-element.442), channel_id=1, source_target_pairs={{0,8},{1,9},{2,10},{3,11},{4,12},{5,13},{6,14},{7,15},{8,0},{9,1},... | collective-permute-start | bytes 1179656 | tf_op jit(solution)/shard_map/ppermute | solution.py:565
  175.8 12.5 %collective-permute-start.64 = (bf16[2,48,1536]{2,1,0:T(8,128)(2,1)S(1)}, bf16[2,48,1536]{2,1,0:T(8,128)(2,1)S(1)}, u32[]{:S(2)}, u32[]{:S(2)}) collective-permute-start(bf16[2,48,1536]{2,1,0:T(8,128)(2,1)S(1)} %get-tuple-element.436), channel_id=1, source_target_pairs={{0,2},{1,3},{2,0},{3,1},{4,6},{5,7},{6,4},{7,5},{8,10},{9,11},{10,... | collective-permute-start | bytes 884744 | tf_op jit(solution)/shard_map/ppermute | solution.py:569
  176.6 11.7 %collective-permute-start.65 = (bf16[2,48,1536]{2,1,0:T(8,128)(2,1)S(1)}, bf16[2,48,1536]{2,1,0:T(8,128)(2,1)S(1)}, u32[]{:S(2)}, u32[]{:S(2)}) collective-permute-start(bf16[2,48,1536]{2,1,0:T(8,128)(2,1)S(1)} %get-tuple-element.438), channel_id=1, source_target_pairs={{0,1},{1,0},{2,3},{3,2},{4,5},{5,4},{6,7},{7,6},{8,9},{9,8},{10,11... | collective-permute-start | bytes 884744 | tf_op jit(solution)/shard_map/ppermute | solution.py:569
  189.0 16.9 %collective-permute-start.68 = (bf16[4,48,1536]{2,1,0:T(8,128)(2,1)S(1)}, bf16[4,48,1536]{2,1,0:T(8,128)(2,1)S(1)}, u32[]{:S(2)}, u32[]{:S(2)}) collective-permute-start(bf16[4,48,1536]{2,1,0:T(8,128)(2,1)S(1)} %get-tuple-element.448), channel_id=1, source_target_pairs={{0,1},{1,0},{2,3},{3,2},{4,5},{5,4},{6,7},{7,6},{8,9},{9,8},{10,11... | collective-permute-start | bytes 1769480 | tf_op jit(solution)/shard_map/ppermute | solution.py:569
  189.9 16.0 %collective-permute-start.69 = (bf16[4,48,1536]{2,1,0:T(8,128)(2,1)S(1)}, bf16[4,48,1536]{2,1,0:T(8,128)(2,1)S(1)}, u32[]{:S(2)}, u32[]{:S(2)}) collective-permute-start(bf16[4,48,1536]{2,1,0:T(8,128)(2,1)S(1)} %get-tuple-element.449), channel_id=1, source_target_pairs={{0,2},{1,3},{2,0},{3,1},{4,6},{5,7},{6,4},{7,5},{8,10},{9,11},{10,... | collective-permute-start | bytes 1769480 | tf_op jit(solution)/shard_map/ppermute | solution.py:569
  190.5 11.2 %collective-permute-start.67 = (bf16[64,3072]{1,0:T(8,128)(2,1)S(1)}, bf16[64,3072]{1,0:T(8,128)(2,1)S(1)}, u32[]{:S(2)}, u32[]{:S(2)}) collective-permute-start(bf16[64,3072]{1,0:T(8,128)(2,1)S(1)} %get-tuple-element.447), channel_id=1, source_target_pairs={{0,4},{1,5},{2,6},{3,7},{4,8},{5,9},{6,10},{7,11},{8,12},{9,13},{1... | collective-permute-start | bytes 1179656 | tf_op jit(solution)/shard_map/ppermute | solution.py:565
  209.7 12.5 %collective-permute-start.80 = (bf16[96,768]{1,0:T(8,128)(2,1)S(1)}, bf16[96,768]{1,0:T(8,128)(2,1)S(1)}, u32[]{:S(2)}, u32[]{:S(2)}) collective-permute-start(bf16[96,768]{1,0:T(8,128)(2,1)S(1)} %pad_maximum_fusion.11.refs_0_), channel_id=1, source_target_pairs={{0,3},{1,2},{2,1},{3,0},{4,7},{5,6},{6,5},{7,4},{8,11},{9,10},{10,... | collective-permute-start | bytes 442376 | tf_op jit(solution)/shard_map/ppermute | solution.py:569
  210.9 11.3 %collective-permute-start.79 = (bf16[96,768]{1,0:T(8,128)(2,1)S(1)}, bf16[96,768]{1,0:T(8,128)(2,1)S(1)}, u32[]{:S(2)}, u32[]{:S(2)}) collective-permute-start(bf16[96,768]{1,0:T(8,128)(2,1)S(1)} %pad_maximum_fusion.11.refs_0_), channel_id=1, source_target_pairs={{0,2},{1,3},{2,0},{3,1},{4,6},{5,7},{6,4},{7,5},{8,10},{9,11},{10,... | collective-permute-start | bytes 442376 | tf_op jit(solution)/shard_map/ppermute | solution.py:569
  211.7 10.5 %collective-permute-start.78 = (bf16[96,768]{1,0:T(8,128)(2,1)S(1)}, bf16[96,768]{1,0:T(8,128)(2,1)S(1)}, u32[]{:S(2)}, u32[]{:S(2)}) collective-permute-start(bf16[96,768]{1,0:T(8,128)(2,1)S(1)} %pad_maximum_fusion.11.refs_0_), channel_id=1, source_target_pairs={{0,1},{1,0},{2,3},{3,2},{4,5},{5,4},{6,7},{7,6},{8,9},{9,8},{10,11... | collective-permute-start | bytes 442376 | tf_op jit(solution)/shard_map/ppermute | solution.py:569
  (61 other events, 301.8 us)

commit v16 on v15

--- a/solution.py
+++ b/solution.py
@@ -2109,11 +2109,16 @@
     cls_got = other_core(cls_rows)
     attn_plane = tuple(after(got, output, shared) for got in attn_plane)
     attn_own, *attn_sent = reduce_fold(where, attn_near[2], attn_plane)
-    attn_lines = list(
-        together(*(along_line(attn_sent[apart - 1], apart) for apart in range(1, LINE)))
+    next_line = along_line(attn_sent[0], 1)
+    attn_lines = [next_line] + list(
+        together(*(along_line(attn_sent[apart - 1], apart) for apart in range(2, LINE)))
     )
     flat = pltpu.VMEM((1, 8 * MODEL + FF), WIDE)
-    payload_line = jnp.concatenate(payload_parts)
+    payload_line = after(jnp.concatenate(payload_parts), *attn_plane)
+    payload_plane = [payload_line] + [
+        in_plane(after(payload_line, next_line) if apart == PLANE - 1 else payload_line, apart)
+        for apart in range(1, PLANE)
+    ]
     mlp_mine, own_vecs, cls_mats_grad, cls_vec_grad, pos_total, loss_value = run_kernel(
         share_owner_kernel,
         "head_owner",
@@ -2127,7 +2132,7 @@
         ],
         where,
         (),
-        tuple(after(got, attn_own) for got in plane_parts(after(payload_line, *attn_plane)))
+        tuple(after(got, attn_own) for got in payload_plane)
         + (mlp_sum, cls_rows, cls_got, shared, count),
         [
             pltpu.VMEM((GROUP * 24, MODEL), LOW),

time: 237 us -> 241 us (1.017)
  starting transfers between devices: 96.4 us -> 102 us
    ppermute x21, starting transfers between devices: 30.3 us -> 35.9 us  [other_core(): return lax.ppermute(value, 'rep', [(0, 1), (1, 0)])]
where the time goes in v16:
time: 241 us; the launch traced here: 238 us
  starting transfers between devices  102 us (42%)
  waiting for transfers between devices  79.2 us (33%)
  Pallas kernels  49.2 us (20%)
  local copies, waits for them, and re-layouts  5.34 us (2%)
    ppermute x36, waiting for transfers between devices, along_line(): return lax.ppermute(value, 'fsdp', line_pairs(apart))  57.7 us
    pallas_call x27, Pallas kernels, run_kernel(): pl.pallas_call(body, name=name, out_shape=tuple(outs), in_specs=in_specs,...  49.2 us
    ppermute x36, starting transfers between devices, along_line(): return lax.ppermute(value, 'fsdp', line_pairs(apart))  44.3 us
    ppermute x21, starting transfers between devices, other_core(): return lax.ppermute(value, 'rep', [(0, 1), (1, 0)])  35.9 us
    ppermute x28, starting transfers between devices, in_plane(): return lax.ppermute(value, 'fsdp', plane_pairs(mask))  21.7 us
    ppermute x21, waiting for transfers between devices, other_core(): return lax.ppermute(value, 'rep', [(0, 1), (1, 0)])  10.8 us
    ppermute x28, waiting for transfers between devices, in_plane(): return lax.ppermute(value, 'fsdp', plane_pairs(mask))  10.8 us
  transfers between devices with their start and end apart: 85, of which 36 were waited for; matrix products, arithmetic and copies ran while one was open for 0% of the time, Pallas kernels for 14%

profile of v16, /device:TPU:13, one launch (start us, length us, event | category | flops | bytes accessed | tf_op | source)
XLA Modules:
  0.0 238.3 jit_solution(12226480596538067844)
XLA Ops:
  9.7 2.3 collective-permute-start.1
  14.2 7.2 %collective-permute-done.1.refs_2_ = bf16[48,1664]{1,0:T(8,128)(2,1)S(1)} collective-permute-done((bf16[48,1664]{1,0:T(8,128)(2,1)S(1)}, bf16[48,1664]{1,0:T(8,128)(2,1)S(1)}, u32[]{:S(2)}, u32[]{:S(2)}) %collective-permute-start.1) | collective-permute-done | bytes 159776 | tf_op jit(solution)/shard_map/ppermute | solution.py:565
  21.4 3.9 %collective-permute-done.refs_1_ = bf16[48,1664]{1,0:T(8,128)(2,1)S(1)} collective-permute-done((bf16[48,1664]{1,0:T(8,128)(2,1)S(1)}, bf16[48,1664]{1,0:T(8,128)(2,1)S(1)}, u32[]{:S(2)}, u32[]{:S(2)}) %collective-permute-start) | collective-permute-done | bytes 159776 | tf_op jit(solution)/shard_map/ppermute | solution.py:565
  30.7 2.5 %collective-permute-start.10 = (bf16[48,1536]{1,0:T(8,128)(2,1)S(1)}, bf16[48,1536]{1,0:T(8,128)(2,1)S(1)}, u32[]{:S(2)}, u32[]{:S(2)}) collective-permute-start(bf16[48,1536]{1,0:T(8,128)(2,1)S(1)} %get-tuple-element.274.refs_0_), channel_id=1, source_target_pairs={{0,8},{1,9},{2,10},{3,11},{4,12},{5,13},{6,14},{7,15},{8,0},{9,1},... | collective-permute-start | bytes 442376 | tf_op jit(solution)/shard_map/ppermute | solution.py:565
  33.1 2.3 collective-permute-done.11.refs_3_
  35.5 5.6 %collective-permute-done.10.refs_2_ = bf16[48,1536]{1,0:T(8,128)(2,1)S(1)} collective-permute-done((bf16[48,1536]{1,0:T(8,128)(2,1)S(1)}, bf16[48,1536]{1,0:T(8,128)(2,1)S(1)}, u32[]{:S(2)}, u32[]{:S(2)}) %collective-permute-start.10) | collective-permute-done | bytes 147488 | tf_op jit(solution)/shard_map/ppermute | solution.py:565
  41.1 3.2 %collective-permute-done.9.refs_1_ = bf16[48,1536]{1,0:T(8,128)(2,1)S(1)} collective-permute-done((bf16[48,1536]{1,0:T(8,128)(2,1)S(1)}, bf16[48,1536]{1,0:T(8,128)(2,1)S(1)}, u32[]{:S(2)}, u32[]{:S(2)}) %collective-permute-start.9) | collective-permute-done | bytes 147488 | tf_op jit(solution)/shard_map/ppermute | solution.py:565
  48.3 2.5 %collective-permute-start.16 = (bf16[48,1536]{1,0:T(8,128)(2,1)S(1)}, bf16[48,1536]{1,0:T(8,128)(2,1)S(1)}, u32[]{:S(2)}, u32[]{:S(2)}) collective-permute-start(bf16[48,1536]{1,0:T(8,128)(2,1)S(1)} %get-tuple-element.285.refs_0_), channel_id=1, source_target_pairs={{0,8},{1,9},{2,10},{3,11},{4,12},{5,13},{6,14},{7,15},{8,0},{9,1},... | collective-permute-start | bytes 442376 | tf_op jit(solution)/shard_map/ppermute | solution.py:565
  52.4 6.4 %collective-permute-done.16.refs_2_ = bf16[48,1536]{1,0:T(8,128)(2,1)S(1)} collective-permute-done((bf16[48,1536]{1,0:T(8,128)(2,1)S(1)}, bf16[48,1536]{1,0:T(8,128)(2,1)S(1)}, u32[]{:S(2)}, u32[]{:S(2)}) %collective-permute-start.16) | collective-permute-done | bytes 147488 | tf_op jit(solution)/shard_map/ppermute | solution.py:565
  58.8 3.2 %collective-permute-done.15.refs_1_ = bf16[48,1536]{1,0:T(8,128)(2,1)S(1)} collective-permute-done((bf16[48,1536]{1,0:T(8,128)(2,1)S(1)}, bf16[48,1536]{1,0:T(8,128)(2,1)S(1)}, u32[]{:S(2)}, u32[]{:S(2)}) %collective-permute-start.15) | collective-permute-done | bytes 147488 | tf_op jit(solution)/shard_map/ppermute | solution.py:565
  66.7 3.9 %seg_qkv.1 = (bf16[16,48,1152]{2,1,0:T(8,128)(2,1)S(1)}, bf16[8,48,384]{2,1,0:T(8,128)(2,1)S(1)}, bf16[8,48,384]{2,1,0:T(8,128)(2,1)S(1)}, bf16[256,1152]{1,0:T(...) custom-call(s32[5]{0:T(128)S(1)} %stack.15.where, ...), custom_call_target="tpu_custom_call" | custom-call | flops 452984832 | bytes 11453440 | tf_op jit(solution)/shard_map/seg_qkv/pallas_call | solution.py:595
  70.6 4.1 %collective-permute-start.20 = (bf16[8,48,384]{2,1,0:T(8,128)(2,1)S(1)}, bf16[8,48,384]{2,1,0:T(8,128)(2,1)S(1)}, u32[]{:S(2)}, u32[]{:S(2)}) collective-permute-start(bf16[8,48,384]{2,1,0:T(8,128)(2,1)S(1)} %get-tuple-element.294.low), channel_id=1, source_target_pairs={{0,16},{16,0},{1,17},{17,1},{2,18},{18,2},{3,19},{19,3},{4,20},{20... | collective-permute-start | bytes 884744 | tf_op jit(solution)/shard_map/ppermute | solution.py:573
  74.8 2.2 collective-permute-done.18.refs_10_.refs_8_
  77.0 3.1 %collective-permute-start.14 = (bf16[256,384]{1,0:T(8,128)(2,1)S(1)}, bf16[256,384]{1,0:T(8,128)(2,1)S(1)}, u32[]{:S(2)}, u32[]{:S(2)}) collective-permute-start(bf16[256,384]{1,0:T(8,128)(2,1)S(1)} %get-tuple-element.284.mixed), channel_id=1, source_target_pairs={{0,16},{16,0},{1,17},{17,1},{2,18},{18,2},{3,19},{19,3},{4,20},{20... | collective-permute-start | bytes 589832 | tf_op jit(solution)/shard_map/ppermute | solution.py:573
  83.2 3.3 %collective-permute-start.24 = (bf16[128,768]{1,0:T(8,128)(2,1)S(1)}, bf16[128,768]{1,0:T(8,128)(2,1)S(1)}, u32[]{:S(2)}, u32[]{:S(2)}) collective-permute-start(bf16[128,768]{1,0:T(8,128)(2,1)S(1)} %get-tuple-element.303.refs_12_.refs_5_.refs_6_), channel_id=1, source_target_pairs={{0,16},{16,0},{1,17},{17,1},{2,18},{18,2},{3,19},{19,3},{4,20},{20... | collective-permute-start | bytes 589832 | tf_op jit(solution)/shard_map/ppermute | solution.py:573
  92.6 3.0 %collective-permute-start.25 = (f32[128,768]{1,0:T(8,128)S(1)}, f32[128,768]{1,0:T(8,128)S(1)}, u32[]{:S(2)}, u32[]{:S(2)}) collective-permute-start(f32[128,768]{1,0:T(8,128)S(1)} %get-tuple-element.307), channel_id=1, source_target_pairs={{0,16},{16,0},{1,17},{17,1},{2,18},{18,2},{3,19},{19,3},{4,20},{20... | collective-permute-start | bytes 1179656 | tf_op jit(solution)/shard_map/ppermute | solution.py:573
  105.6 2.8 %collective-permute-start.33 = (f32[4,1664]{1,0:T(4,128)S(1)}, f32[4,1664]{1,0:T(4,128)S(1)}, u32[]{:S(2)}, u32[]{:S(2)}) collective-permute-start(f32[4,1664]{1,0:T(4,128)S(1)} %pad_maximum_fusion.12.refs_0_), channel_id=1, source_target_pairs={{0,8},{1,9},{2,10},{3,11},{4,12},{5,13},{6,14},{7,15},{8,0},{9,1},... | collective-permute-start | bytes 79880 | tf_op jit(solution)/shard_map/ppermute | solution.py:565
  125.3 2.5 %seg_mlp_near.1 = (bf16[4,48,3072]{2,1,0:T(8,128)(2,1)S(1)}, bf16[4,48,3072]{2,1,0:T(8,128)(2,1)S(1)}, bf16[4,48,3072]{2,1,0:T(8,128)(2,1)S(1)}) custom-call(s32[5]{0:T(128)S(1)} %stack.15.where, bf16[256,1024]{1,0:T(8,128)(2,1)S(1)} %get-tuple-element.326.refs_0_, bf16[128,768]{1,0:T(8,128)(2,1)S(1)} %get-tuple-element.315.refs_0_.refs_1_, ...), custom_call_target="tpu_custom_call" | custom-call | flops 905969664 | bytes 7602176 | tf_op jit(solution)/shard_map/seg_mlp_near/pallas_call | solution.py:595
  140.4 2.3 collective-permute-start.54
  146.5 2.3 head_attend_back.1
  154.9 2.8 %collective-permute-done.58.refs_13_ = bf16[4,48,3072]{2,1,0:T(8,128)(2,1)S(1)} collective-permute-done((bf16[4,48,3072]{2,1,0:T(8,128)(2,1)S(1)}, bf16[4,48,3072]{2,1,0:T(8,128)(2,1)S(1)}, u32[]{:S(2)}, u32[]{:S(2)}) %collective-permute-start.58) | collective-permute-done | bytes 1179680 | tf_op jit(solution)/shard_map/ppermute | solution.py:569
  161.6 3.0 %collective-permute-start.60 = (f32[1,768]{1,0:T(1,128)S(1)}, f32[1,768]{1,0:T(1,128)S(1)}, u32[]{:S(2)}, u32[]{:S(2)}) collective-permute-start(f32[1,768]{1,0:T(1,128)S(1)} %get-tuple-element.413.refs_0_.refs_3_), channel_id=1, source_target_pairs={{0,16},{16,0},{1,17},{17,1},{2,18},{18,2},{3,19},{19,3},{4,20},{20... | collective-permute-start | bytes 9224 | tf_op jit(solution)/shard_map/ppermute | solution.py:573
  170.9 3.8 %seg_attn_back.1.refs_2_ = bf16[256,1152]{1,0:T(8,128)(2,1)S(1)} custom-call(s32[5]{0:T(128)S(1)} %stack.15.where, bf16[256,1152]{1,0:T(8,128)(2,1)S(1)} %get-tuple-element.298.refs_0_, bf16[128,768]{1,0:T(8,128)(2,1)S(1)} %get-tuple-element.418.refs_1_, bf16[128,768]{1,0:T(8,128)(2,1)S(1)} %collective-permute-done.62.refs_2_.refs_4_, ...), custom_call_target="tpu_custom_call" | custom-call | flops 452984832 | bytes 1573888 | tf_op jit(solution)/shard_map/seg_attn_back/pallas_call | solution.py:595
  177.3 2.8 %seg_attn_near.1 = (bf16[4,48,1536]{2,1,0:T(8,128)(2,1)S(1)}, bf16[4,48,1536]{2,1,0:T(8,128)(2,1)S(1)}, bf16[4,48,1536]{2,1,0:T(8,128)(2,1)S(1)}, bf16[128,768]{...) custom-call(s32[5]{0:T(128)S(1)} %stack.15.where, ...), custom_call_target="tpu_custom_call" | custom-call | flops 452984832 | bytes 7444992 | tf_op jit(solution)/shard_map/seg_attn_near/pallas_call | solution.py:595
  180.1 8.2 %collective-permute-done.66.refs_2_ = bf16[64,3072]{1,0:T(8,128)(2,1)S(1)} collective-permute-done((bf16[64,3072]{1,0:T(8,128)(2,1)S(1)}, bf16[64,3072]{1,0:T(8,128)(2,1)S(1)}, u32[]{:S(2)}, u32[]{:S(2)}) %collective-permute-start.66) | collective-permute-done | bytes 393248 | tf_op jit(solution)/shard_map/ppermute | solution.py:565
  194.4 7.4 %collective-permute-done.67.refs_1_ = bf16[64,3072]{1,0:T(8,128)(2,1)S(1)} collective-permute-done((bf16[64,3072]{1,0:T(8,128)(2,1)S(1)}, bf16[64,3072]{1,0:T(8,128)(2,1)S(1)}, u32[]{:S(2)}, u32[]{:S(2)}) %collective-permute-start.67) | collective-permute-done | bytes 393248 | tf_op jit(solution)/shard_map/ppermute | solution.py:565
  201.8 3.0 %collective-permute-start.75 = (bf16[24,768]{1,0:T(8,128)(2,1)S(1)}, bf16[24,768]{1,0:T(8,128)(2,1)S(1)}, u32[]{:S(2)}, u32[]{:S(2)}) collective-permute-start(bf16[24,768]{1,0:T(8,128)(2,1)S(1)} %get-tuple-element.468), channel_id=1, source_target_pairs={{0,12},{1,13},{2,14},{3,15},{4,0},{5,1},{6,2},{7,3},{8,4},{9,5},{1... | collective-permute-start | bytes 110600 | tf_op jit(solution)/shard_map/ppermute | solution.py:565
  213.0 6.1 %collective-permute-start.79 = (bf16[16,12288]{1,0:T(8,128)(2,1)S(1)}, bf16[16,12288]{1,0:T(8,128)(2,1)S(1)}, u32[]{:S(2)}, u32[]{:S(2)}) collective-permute-start(bf16[16,12288]{1,0:T(8,128)(2,1)S(1)} %get-tuple-element.479.refs_5_), channel_id=1, source_target_pairs={{0,16},{16,0},{1,17},{17,1},{2,18},{18,2},{3,19},{19,3},{4,20},{20... | collective-permute-start | bytes 1179656 | tf_op jit(solution)/shard_map/ppermute | solution.py:573
  220.4 3.2 %collective-permute-done.81 = bf16[48,1536]{1,0:T(8,128)(2,1)S(1)} collective-permute-done((bf16[48,1536]{1,0:T(8,128)(2,1)S(1)}, bf16[48,1536]{1,0:T(8,128)(2,1)S(1)}, u32[]{:S(2)}, u32[]{:S(2)}) %collective-permute-start.81) | collective-permute-done | bytes 147488 | tf_op jit(solution)/shard_map/ppermute | solution.py:565
  224.0 4.4 %head_owner.1 = (f32[48,3072]{1,0:T(8,128)S(1)}, f32[16,768]{1,0:T(8,128)S(1)}, f32[48,9216]{1,0:T(8,128)}, f32[576]{0:T(1024)}, f32[16,768]{1,0:T(8,128)}, /*index=5*/f32[1,1]{1,0:T(1,128)}) custom-call(s32[5]{0:T(128)S(1)} %stack.15.where, bf16[96,768]{1,0:T(8,128)(2,1)S(1)} %pad_maximum_fusion.11.refs_0_, ...), custom_call_target="tpu_custom_call" | custom-call | flops 28311552 | bytes 4503812 | tf_op jit(solution)/shard_map/head_owner/pallas_call | solution.py:595
  228.4 4.3 %collective-permute-start.83 = (f32[48,3072]{1,0:T(8,128)S(1)}, f32[48,3072]{1,0:T(8,128)S(1)}, u32[]{:S(2)}, u32[]{:S(2)}) collective-permute-start(f32[48,3072]{1,0:T(8,128)S(1)} %get-tuple-element.480.mlp), channel_id=1, source_target_pairs={{0,16},{16,0},{1,17},{17,1},{2,18},{18,2},{3,19},{19,3},{4,20},{20... | collective-permute-start | bytes 1769480 | tf_op jit(solution)/shard_map/ppermute | solution.py:573
  234.8 3.3 %seg_owner.1 = (f32[48,9216]{1,0:T(8,128)}, f32[576]{0:T(1024)}) custom-call(s32[5]{0:T(128)S(1)} %stack.15.where, f32[48,1536]{1,0:T(8,128)S(1)} %convert_add_fusion.1.attn, f32[48,1536]{1,0:T(8,128)S(1)} %collective-permute-done.82.attn_got, f32[48,3072]{1,0:T(8,128)S(1)} %get-tuple-element.480.mlp, f32[48,3072]{1,0:T(8,128)S(1)} %collective-permute-done.83.mlp_got, ...), custom_call_target="tpu_custom_call" | custom-call | bytes 3639552 | tf_op jit(solution)/shard_map/seg_owner/pallas_call | solution.py:595
  (213 shorter events, 115.6 us)
Async XLA Ops:
  8.0 17.3 %collective-permute-start.3 = (bf16[48,4736]{1,0:T(8,128)(2,1)S(1)}, bf16[48,4736]{1,0:T(8,128)(2,1)S(1)}, u32[]{:S(2)}, u32[]{:S(2)}) collective-permute-start(bf16[48,4736]{1,0:T(8,128)(2,1)S(1)} %pad_maximum_fusion.10), channel_id=1, source_target_pairs={{0,1},{1,0},{2,3},{3,2},{4,5},{5,4},{6,7},{7,6},{8,9},{9,8},{10,11... | collective-permute-start | bytes 1363976 | tf_op jit(solution)/shard_map/ppermute | solution.py:569
  9.3 16.0 %collective-permute-start.4 = (bf16[48,4736]{1,0:T(8,128)(2,1)S(1)}, bf16[48,4736]{1,0:T(8,128)(2,1)S(1)}, u32[]{:S(2)}, u32[]{:S(2)}) collective-permute-start(bf16[48,4736]{1,0:T(8,128)(2,1)S(1)} %pad_maximum_fusion.10), channel_id=1, source_target_pairs={{0,2},{1,3},{2,0},{3,1},{4,6},{5,7},{6,4},{7,5},{8,10},{9,11},{10,... | collective-permute-start | bytes 1363976 | tf_op jit(solution)/shard_map/ppermute | solution.py:569
  9.7 11.7 %collective-permute-start.1 = (bf16[48,1664]{1,0:T(8,128)(2,1)S(1)}, bf16[48,1664]{1,0:T(8,128)(2,1)S(1)}, u32[]{:S(2)}, u32[]{:S(2)}) collective-permute-start(bf16[48,1664]{1,0:T(8,128)(2,1)S(1)} %get-tuple-element.253.refs_0_), channel_id=1, source_target_pairs={{0,8},{1,9},{2,10},{3,11},{4,12},{5,13},{6,14},{7,15},{8,0},{9,1},... | collective-permute-start | bytes 479240 | tf_op jit(solution)/shard_map/ppermute | solution.py:565
  12.0 13.3 %collective-permute-start = (bf16[48,1664]{1,0:T(8,128)(2,1)S(1)}, bf16[48,1664]{1,0:T(8,128)(2,1)S(1)}, u32[]{:S(2)}, u32[]{:S(2)}) collective-permute-start(bf16[48,1664]{1,0:T(8,128)(2,1)S(1)} %get-tuple-element.253.refs_0_), channel_id=1, source_target_pairs={{0,4},{1,5},{2,6},{3,7},{4,8},{5,9},{6,10},{7,11},{8,12},{9,13},{1... | collective-permute-start | bytes 479240 | tf_op jit(solution)/shard_map/ppermute | solution.py:565
  28.2 18.1 %collective-permute-start.8 = (bf16[48,7424]{1,0:T(8,128)(2,1)S(1)}, bf16[48,7424]{1,0:T(8,128)(2,1)S(1)}, u32[]{:S(2)}, u32[]{:S(2)}) collective-permute-start(bf16[48,7424]{1,0:T(8,128)(2,1)S(1)} %pad_maximum_fusion.6), channel_id=1, source_target_pairs={{0,2},{1,3},{2,0},{3,1},{4,6},{5,7},{6,4},{7,5},{8,10},{9,11},{10,... | collective-permute-start | bytes 2138120 | tf_op jit(solution)/shard_map/ppermute | solution.py:569
  29.5 16.8 %collective-permute-start.7 = (bf16[48,7296]{1,0:T(8,128)(2,1)S(1)}, bf16[48,7296]{1,0:T(8,128)(2,1)S(1)}, u32[]{:S(2)}, u32[]{:S(2)}) collective-permute-start(bf16[48,7296]{1,0:T(8,128)(2,1)S(1)} %pad_maximum_fusion.7), channel_id=1, source_target_pairs={{0,1},{1,0},{2,3},{3,2},{4,5},{5,4},{6,7},{7,6},{8,9},{9,8},{10,11... | collective-permute-start | bytes 2101256 | tf_op jit(solution)/shard_map/ppermute | solution.py:569
  33.1 11.1 %collective-permute-start.9 = (bf16[48,1536]{1,0:T(8,128)(2,1)S(1)}, bf16[48,1536]{1,0:T(8,128)(2,1)S(1)}, u32[]{:S(2)}, u32[]{:S(2)}) collective-permute-start(bf16[48,1536]{1,0:T(8,128)(2,1)S(1)} %get-tuple-element.274.refs_0_), channel_id=1, source_target_pairs={{0,4},{1,5},{2,6},{3,7},{4,8},{5,9},{6,10},{7,11},{8,12},{9,13},{1... | collective-permute-start | bytes 442376 | tf_op jit(solution)/shard_map/ppermute | solution.py:565
  46.5 16.1 %collective-permute-start.13 = (bf16[48,7168]{1,0:T(8,128)(2,1)S(1)}, bf16[48,7168]{1,0:T(8,128)(2,1)S(1)}, u32[]{:S(2)}, u32[]{:S(2)}) collective-permute-start(bf16[48,7168]{1,0:T(8,128)(2,1)S(1)} %pad_maximum_fusion.8), channel_id=1, source_target_pairs={{0,2},{1,3},{2,0},{3,1},{4,6},{5,7},{6,4},{7,5},{8,10},{9,11},{10,... | collective-permute-start | bytes 2064392 | tf_op jit(solution)/shard_map/ppermute | solution.py:569
  47.1 15.4 %collective-permute-start.12 = (bf16[48,7040]{1,0:T(8,128)(2,1)S(1)}, bf16[48,7040]{1,0:T(8,128)(2,1)S(1)}, u32[]{:S(2)}, u32[]{:S(2)}) collective-permute-start(bf16[48,7040]{1,0:T(8,128)(2,1)S(1)} %pad_maximum_fusion.9), channel_id=1, source_target_pairs={{0,1},{1,0},{2,3},{3,2},{4,5},{5,4},{6,7},{7,6},{8,9},{9,8},{10,11... | collective-permute-start | bytes 2027528 | tf_op jit(solution)/shard_map/ppermute | solution.py:569
  50.8 11.2 %collective-permute-start.15 = (bf16[48,1536]{1,0:T(8,128)(2,1)S(1)}, bf16[48,1536]{1,0:T(8,128)(2,1)S(1)}, u32[]{:S(2)}, u32[]{:S(2)}) collective-permute-start(bf16[48,1536]{1,0:T(8,128)(2,1)S(1)} %get-tuple-element.285.refs_0_), channel_id=1, source_target_pairs={{0,4},{1,5},{2,6},{3,7},{4,8},{5,9},{6,10},{7,11},{8,12},{9,13},{1... | collective-permute-start | bytes 442376 | tf_op jit(solution)/shard_map/ppermute | solution.py:565
  62.7 14.3 %collective-permute-start.18 = (bf16[48,6912]{1,0:T(8,128)(2,1)S(1)}, bf16[48,6912]{1,0:T(8,128)(2,1)S(1)}, u32[]{:S(2)}, u32[]{:S(2)}) collective-permute-start(bf16[48,6912]{1,0:T(8,128)(2,1)S(1)} %get-tuple-element.289), channel_id=1, source_target_pairs={{0,1},{1,0},{2,3},{3,2},{4,5},{5,4},{6,7},{7,6},{8,9},{9,8},{10,11... | collective-permute-start | bytes 1990664 | tf_op jit(solution)/shard_map/ppermute | solution.py:569
  63.4 11.2 %collective-permute-start.35 = (bf16[48,1152]{1,0:T(8,128)(2,1)S(1)}, bf16[48,1152]{1,0:T(8,128)(2,1)S(1)}, u32[]{:S(2)}, u32[]{:S(2)}) collective-permute-start(bf16[48,1152]{1,0:T(8,128)(2,1)S(1)} %get-tuple-element.344), channel_id=1, source_target_pairs={{0,4},{1,5},{2,6},{3,7},{4,8},{5,9},{6,10},{7,11},{8,12},{9,13},{1... | collective-permute-start | bytes 331784 | tf_op jit(solution)/shard_map/ppermute | solution.py:565
  65.6 14.5 %collective-permute-start.19 = (bf16[48,6912]{1,0:T(8,128)(2,1)S(1)}, bf16[48,6912]{1,0:T(8,128)(2,1)S(1)}, u32[]{:S(2)}, u32[]{:S(2)}) collective-permute-start(bf16[48,6912]{1,0:T(8,128)(2,1)S(1)} %get-tuple-element.290), channel_id=1, source_target_pairs={{0,2},{1,3},{2,0},{3,1},{4,6},{5,7},{6,4},{7,5},{8,10},{9,11},{10,... | collective-permute-start | bytes 1990664 | tf_op jit(solution)/shard_map/ppermute | solution.py:569
  70.6 11.2 %collective-permute-start.20 = (bf16[8,48,384]{2,1,0:T(8,128)(2,1)S(1)}, bf16[8,48,384]{2,1,0:T(8,128)(2,1)S(1)}, u32[]{:S(2)}, u32[]{:S(2)}) collective-permute-start(bf16[8,48,384]{2,1,0:T(8,128)(2,1)S(1)} %get-tuple-element.294.low), channel_id=1, source_target_pairs={{0,16},{16,0},{1,17},{17,1},{2,18},{18,2},{3,19},{19,3},{4,20},{20... | collective-permute-start | bytes 884744 | tf_op jit(solution)/shard_map/ppermute | solution.py:573
  74.7 11.8 %collective-permute-start.37 = (bf16[48,1152]{1,0:T(8,128)(2,1)S(1)}, bf16[48,1152]{1,0:T(8,128)(2,1)S(1)}, u32[]{:S(2)}, u32[]{:S(2)}) collective-permute-start(bf16[48,1152]{1,0:T(8,128)(2,1)S(1)} %get-tuple-element.348), channel_id=1, source_target_pairs={{0,12},{1,13},{2,14},{3,15},{4,0},{5,1},{6,2},{7,3},{8,4},{9,5},{1... | collective-permute-start | bytes 331784 | tf_op jit(solution)/shard_map/ppermute | solution.py:565
  89.5 14.4 %collective-permute-start.38 = (bf16[48,4992]{1,0:T(8,128)(2,1)S(1)}, bf16[48,4992]{1,0:T(8,128)(2,1)S(1)}, u32[]{:S(2)}, u32[]{:S(2)}) collective-permute-start(bf16[48,4992]{1,0:T(8,128)(2,1)S(1)} %constant_dynamic-update-slice_fusion), channel_id=1, source_target_pairs={{0,1},{1,0},{2,3},{3,2},{4,5},{5,4},{6,7},{7,6},{8,9},{9,8},{10,11... | collective-permute-start | bytes 1437704 | tf_op jit(solution)/shard_map/ppermute | solution.py:569
  90.5 13.5 %collective-permute-start.39 = (bf16[48,4992]{1,0:T(8,128)(2,1)S(1)}, bf16[48,4992]{1,0:T(8,128)(2,1)S(1)}, u32[]{:S(2)}, u32[]{:S(2)}) collective-permute-start(bf16[48,4992]{1,0:T(8,128)(2,1)S(1)} %constant_dynamic-update-slice_fusion), channel_id=1, source_target_pairs={{0,2},{1,3},{2,0},{3,1},{4,6},{5,7},{6,4},{7,5},{8,10},{9,11},{10,... | collective-permute-start | bytes 1437704 | tf_op jit(solution)/shard_map/ppermute | solution.py:569
  114.6 14.9 %collective-permute-start.47 = (bf16[2,48,3072]{2,1,0:T(8,128)(2,1)S(1)}, bf16[2,48,3072]{2,1,0:T(8,128)(2,1)S(1)}, u32[]{:S(2)}, u32[]{:S(2)}) collective-permute-start(bf16[2,48,3072]{2,1,0:T(8,128)(2,1)S(1)} %get-tuple-element.374), channel_id=1, source_target_pairs={{0,2},{1,3},{2,0},{3,1},{4,6},{5,7},{6,4},{7,5},{8,10},{9,11},{10,... | collective-permute-start | bytes 1769480 | tf_op jit(solution)/shard_map/ppermute | solution.py:569
  115.3 14.6 %collective-permute-start.48 = (bf16[2,48,3072]{2,1,0:T(8,128)(2,1)S(1)}, bf16[2,48,3072]{2,1,0:T(8,128)(2,1)S(1)}, u32[]{:S(2)}, u32[]{:S(2)}) collective-permute-start(bf16[2,48,3072]{2,1,0:T(8,128)(2,1)S(1)} %get-tuple-element.376), channel_id=1, source_target_pairs={{0,1},{1,0},{2,3},{3,2},{4,5},{5,4},{6,7},{7,6},{8,9},{9,8},{10,11... | collective-permute-start | bytes 1769480 | tf_op jit(solution)/shard_map/ppermute | solution.py:569
  131.3 26.4 %collective-permute-start.58 = (bf16[4,48,3072]{2,1,0:T(8,128)(2,1)S(1)}, bf16[4,48,3072]{2,1,0:T(8,128)(2,1)S(1)}, u32[]{:S(2)}, u32[]{:S(2)}) collective-permute-start(bf16[4,48,3072]{2,1,0:T(8,128)(2,1)S(1)} %get-tuple-element.405), channel_id=1, source_target_pairs={{0,1},{1,0},{2,3},{3,2},{4,5},{5,4},{6,7},{7,6},{8,9},{9,8},{10,11... | collective-permute-start | bytes 3538952 | tf_op jit(solution)/shard_map/ppermute | solution.py:569
  132.3 26.0 %collective-permute-start.59 = (bf16[4,48,3072]{2,1,0:T(8,128)(2,1)S(1)}, bf16[4,48,3072]{2,1,0:T(8,128)(2,1)S(1)}, u32[]{:S(2)}, u32[]{:S(2)}) collective-permute-start(bf16[4,48,3072]{2,1,0:T(8,128)(2,1)S(1)} %get-tuple-element.406), channel_id=1, source_target_pairs={{0,2},{1,3},{2,0},{3,1},{4,6},{5,7},{6,4},{7,5},{8,10},{9,11},{10,... | collective-permute-start | bytes 3538952 | tf_op jit(solution)/shard_map/ppermute | solution.py:569
  159.8 16.0 %collective-permute-start.63 = (bf16[64,3072]{1,0:T(8,128)(2,1)S(1)}, bf16[64,3072]{1,0:T(8,128)(2,1)S(1)}, u32[]{:S(2)}, u32[]{:S(2)}) collective-permute-start(bf16[64,3072]{1,0:T(8,128)(2,1)S(1)} %get-tuple-element.432), channel_id=1, source_target_pairs={{0,12},{1,13},{2,14},{3,15},{4,0},{5,1},{6,2},{7,3},{8,4},{9,5},{1... | collective-permute-start | bytes 1179656 | tf_op jit(solution)/shard_map/ppermute | solution.py:565
  169.8 18.5 %collective-permute-start.66 = (bf16[64,3072]{1,0:T(8,128)(2,1)S(1)}, bf16[64,3072]{1,0:T(8,128)(2,1)S(1)}, u32[]{:S(2)}, u32[]{:S(2)}) collective-permute-start(bf16[64,3072]{1,0:T(8,128)(2,1)S(1)} %get-tuple-element.439), channel_id=1, source_target_pairs={{0,8},{1,9},{2,10},{3,11},{4,12},{5,13},{6,14},{7,15},{8,0},{9,1},... | collective-permute-start | bytes 1179656 | tf_op jit(solution)/shard_map/ppermute | solution.py:565
  175.8 12.5 %collective-permute-start.64 = (bf16[2,48,1536]{2,1,0:T(8,128)(2,1)S(1)}, bf16[2,48,1536]{2,1,0:T(8,128)(2,1)S(1)}, u32[]{:S(2)}, u32[]{:S(2)}) collective-permute-start(bf16[2,48,1536]{2,1,0:T(8,128)(2,1)S(1)} %get-tuple-element.433), channel_id=1, source_target_pairs={{0,2},{1,3},{2,0},{3,1},{4,6},{5,7},{6,4},{7,5},{8,10},{9,11},{10,... | collective-permute-start | bytes 884744 | tf_op jit(solution)/shard_map/ppermute | solution.py:569
  176.6 11.7 %collective-permute-start.65 = (bf16[2,48,1536]{2,1,0:T(8,128)(2,1)S(1)}, bf16[2,48,1536]{2,1,0:T(8,128)(2,1)S(1)}, u32[]{:S(2)}, u32[]{:S(2)}) collective-permute-start(bf16[2,48,1536]{2,1,0:T(8,128)(2,1)S(1)} %get-tuple-element.435), channel_id=1, source_target_pairs={{0,1},{1,0},{2,3},{3,2},{4,5},{5,4},{6,7},{7,6},{8,9},{9,8},{10,11... | collective-permute-start | bytes 884744 | tf_op jit(solution)/shard_map/ppermute | solution.py:569
  189.0 16.9 %collective-permute-start.68 = (bf16[4,48,1536]{2,1,0:T(8,128)(2,1)S(1)}, bf16[4,48,1536]{2,1,0:T(8,128)(2,1)S(1)}, u32[]{:S(2)}, u32[]{:S(2)}) collective-permute-start(bf16[4,48,1536]{2,1,0:T(8,128)(2,1)S(1)} %get-tuple-element.445), channel_id=1, source_target_pairs={{0,1},{1,0},{2,3},{3,2},{4,5},{5,4},{6,7},{7,6},{8,9},{9,8},{10,11... | collective-permute-start | bytes 1769480 | tf_op jit(solution)/shard_map/ppermute | solution.py:569
  189.9 16.0 %collective-permute-start.69 = (bf16[4,48,1536]{2,1,0:T(8,128)(2,1)S(1)}, bf16[4,48,1536]{2,1,0:T(8,128)(2,1)S(1)}, u32[]{:S(2)}, u32[]{:S(2)}) collective-permute-start(bf16[4,48,1536]{2,1,0:T(8,128)(2,1)S(1)} %get-tuple-element.446), channel_id=1, source_target_pairs={{0,2},{1,3},{2,0},{3,1},{4,6},{5,7},{6,4},{7,5},{8,10},{9,11},{10,... | collective-permute-start | bytes 1769480 | tf_op jit(solution)/shard_map/ppermute | solution.py:569
  190.5 11.2 %collective-permute-start.67 = (bf16[64,3072]{1,0:T(8,128)(2,1)S(1)}, bf16[64,3072]{1,0:T(8,128)(2,1)S(1)}, u32[]{:S(2)}, u32[]{:S(2)}) collective-permute-start(bf16[64,3072]{1,0:T(8,128)(2,1)S(1)} %get-tuple-element.444), channel_id=1, source_target_pairs={{0,4},{1,5},{2,6},{3,7},{4,8},{5,9},{6,10},{7,11},{8,12},{9,13},{1... | collective-permute-start | bytes 1179656 | tf_op jit(solution)/shard_map/ppermute | solution.py:565
  209.7 13.9 %collective-permute-start.77 = (bf16[96,768]{1,0:T(8,128)(2,1)S(1)}, bf16[96,768]{1,0:T(8,128)(2,1)S(1)}, u32[]{:S(2)}, u32[]{:S(2)}) collective-permute-start(bf16[96,768]{1,0:T(8,128)(2,1)S(1)} %pad_maximum_fusion.11.refs_0_), channel_id=1, source_target_pairs={{0,2},{1,3},{2,0},{3,1},{4,6},{5,7},{6,4},{7,5},{8,10},{9,11},{10,... | collective-permute-start | bytes 442376 | tf_op jit(solution)/shard_map/ppermute | solution.py:569
  210.5 13.2 %collective-permute-start.76 = (bf16[96,768]{1,0:T(8,128)(2,1)S(1)}, bf16[96,768]{1,0:T(8,128)(2,1)S(1)}, u32[]{:S(2)}, u32[]{:S(2)}) collective-permute-start(bf16[96,768]{1,0:T(8,128)(2,1)S(1)} %pad_maximum_fusion.11.refs_0_), channel_id=1, source_target_pairs={{0,1},{1,0},{2,3},{3,2},{4,5},{5,4},{6,7},{7,6},{8,9},{9,8},{10,11... | collective-permute-start | bytes 442376 | tf_op jit(solution)/shard_map/ppermute | solution.py:569
  211.2 12.4 %collective-permute-start.81 = (bf16[48,1536]{1,0:T(8,128)(2,1)S(1)}, bf16[48,1536]{1,0:T(8,128)(2,1)S(1)}, u32[]{:S(2)}, u32[]{:S(2)}) collective-permute-start(bf16[48,1536]{1,0:T(8,128)(2,1)S(1)} %get-tuple-element.483), channel_id=1, source_target_pairs={{0,12},{1,13},{2,14},{3,15},{4,0},{5,1},{6,2},{7,3},{8,4},{9,5},{1... | collective-permute-start | bytes 442376 | tf_op jit(solution)/shard_map/ppermute | solution.py:565
  213.0 11.0 %collective-permute-start.79 = (bf16[16,12288]{1,0:T(8,128)(2,1)S(1)}, bf16[16,12288]{1,0:T(8,128)(2,1)S(1)}, u32[]{:S(2)}, u32[]{:S(2)}) collective-permute-start(bf16[16,12288]{1,0:T(8,128)(2,1)S(1)} %get-tuple-element.479.refs_5_), channel_id=1, source_target_pairs={{0,16},{16,0},{1,17},{17,1},{2,18},{18,2},{3,19},{19,3},{4,20},{20... | collective-permute-start | bytes 1179656 | tf_op jit(solution)/shard_map/ppermute | solution.py:573
  (61 other events, 306.7 us)

commit v17 on v15

--- a/solution.py
+++ b/solution.py
@@ -2087,7 +2087,7 @@
         attn_far + (after(attn_near[0], got_two), attn_near[1]),
     )
     attn_plane = sent_both(*attn_sent)
-    mlp_got[0] = along_line(after(mlp_last, *attn_sent), 1)
+    mlp_got[0] = along_line(after(mlp_last, got_two), 1)
     input_got = other_core(after(input_send, *attn_sent))
     shared = shared + other_core(after(shared, attn_sent[0]))
     payload_parts = line_parts(after(payload, mlp_got[0], input_got, shared))

time: 237 us -> 237 us (level)
  no operation moved by 1% of the time
where the time goes in v17:
time: 237 us; the launch traced here: 235 us
  starting transfers between devices  96.4 us (41%)
  waiting for transfers between devices  81.1 us (34%)
  Pallas kernels  49.2 us (21%)
  local copies, waits for them, and re-layouts  5.34 us (2%)
    ppermute x36, waiting for transfers between devices, along_line(): return lax.ppermute(value, 'fsdp', line_pairs(apart))  59.9 us
    pallas_call x27, Pallas kernels, run_kernel(): pl.pallas_call(body, name=name, out_shape=tuple(outs), in_specs=in_specs,...  49.2 us
    ppermute x36, starting transfers between devices, along_line(): return lax.ppermute(value, 'fsdp', line_pairs(apart))  44.4 us
    ppermute x21, starting transfers between devices, other_core(): return lax.ppermute(value, 'rep', [(0, 1), (1, 0)])  30.3 us
    ppermute x28, starting transfers between devices, in_plane(): return lax.ppermute(value, 'fsdp', plane_pairs(mask))  21.7 us
    ppermute x21, waiting for transfers between devices, other_core(): return lax.ppermute(value, 'rep', [(0, 1), (1, 0)])  10.8 us
    ppermute x28, waiting for transfers between devices, in_plane(): return lax.ppermute(value, 'fsdp', plane_pairs(mask))  10.4 us
  transfers between devices with their start and end apart: 85, of which 36 were waited for; matrix products, arithmetic and copies ran while one was open for 0% of the time, Pallas kernels for 14%

profile of v17, /device:TPU:13, one launch (start us, length us, event | category | flops | bytes accessed | tf_op | source)
XLA Modules:
  0.0 234.7 jit_solution(14930504342375389292)
XLA Ops:
  9.7 2.3 collective-permute-start.1
  14.2 7.2 %collective-permute-done.1.refs_2_ = bf16[48,1664]{1,0:T(8,128)(2,1)S(1)} collective-permute-done((bf16[48,1664]{1,0:T(8,128)(2,1)S(1)}, bf16[48,1664]{1,0:T(8,128)(2,1)S(1)}, u32[]{:S(2)}, u32[]{:S(2)}) %collective-permute-start.1) | collective-permute-done | bytes 159776 | tf_op jit(solution)/shard_map/ppermute | solution.py:565
  21.4 3.9 %collective-permute-done.refs_1_ = bf16[48,1664]{1,0:T(8,128)(2,1)S(1)} collective-permute-done((bf16[48,1664]{1,0:T(8,128)(2,1)S(1)}, bf16[48,1664]{1,0:T(8,128)(2,1)S(1)}, u32[]{:S(2)}, u32[]{:S(2)}) %collective-permute-start) | collective-permute-done | bytes 159776 | tf_op jit(solution)/shard_map/ppermute | solution.py:565
  30.7 2.5 %collective-permute-start.10 = (bf16[48,1536]{1,0:T(8,128)(2,1)S(1)}, bf16[48,1536]{1,0:T(8,128)(2,1)S(1)}, u32[]{:S(2)}, u32[]{:S(2)}) collective-permute-start(bf16[48,1536]{1,0:T(8,128)(2,1)S(1)} %get-tuple-element.276.refs_0_), channel_id=1, source_target_pairs={{0,8},{1,9},{2,10},{3,11},{4,12},{5,13},{6,14},{7,15},{8,0},{9,1},... | collective-permute-start | bytes 442376 | tf_op jit(solution)/shard_map/ppermute | solution.py:565
  33.1 2.3 collective-permute-done.11.refs_3_
  35.5 5.6 %collective-permute-done.10.refs_2_ = bf16[48,1536]{1,0:T(8,128)(2,1)S(1)} collective-permute-done((bf16[48,1536]{1,0:T(8,128)(2,1)S(1)}, bf16[48,1536]{1,0:T(8,128)(2,1)S(1)}, u32[]{:S(2)}, u32[]{:S(2)}) %collective-permute-start.10) | collective-permute-done | bytes 147488 | tf_op jit(solution)/shard_map/ppermute | solution.py:565
  41.1 3.2 %collective-permute-done.9.refs_1_ = bf16[48,1536]{1,0:T(8,128)(2,1)S(1)} collective-permute-done((bf16[48,1536]{1,0:T(8,128)(2,1)S(1)}, bf16[48,1536]{1,0:T(8,128)(2,1)S(1)}, u32[]{:S(2)}, u32[]{:S(2)}) %collective-permute-start.9) | collective-permute-done | bytes 147488 | tf_op jit(solution)/shard_map/ppermute | solution.py:565
  48.3 2.5 %collective-permute-start.16 = (bf16[48,1536]{1,0:T(8,128)(2,1)S(1)}, bf16[48,1536]{1,0:T(8,128)(2,1)S(1)}, u32[]{:S(2)}, u32[]{:S(2)}) collective-permute-start(bf16[48,1536]{1,0:T(8,128)(2,1)S(1)} %get-tuple-element.287.refs_0_), channel_id=1, source_target_pairs={{0,8},{1,9},{2,10},{3,11},{4,12},{5,13},{6,14},{7,15},{8,0},{9,1},... | collective-permute-start | bytes 442376 | tf_op jit(solution)/shard_map/ppermute | solution.py:565
  52.4 6.4 %collective-permute-done.16.refs_2_ = bf16[48,1536]{1,0:T(8,128)(2,1)S(1)} collective-permute-done((bf16[48,1536]{1,0:T(8,128)(2,1)S(1)}, bf16[48,1536]{1,0:T(8,128)(2,1)S(1)}, u32[]{:S(2)}, u32[]{:S(2)}) %collective-permute-start.16) | collective-permute-done | bytes 147488 | tf_op jit(solution)/shard_map/ppermute | solution.py:565
  58.8 3.2 %collective-permute-done.15.refs_1_ = bf16[48,1536]{1,0:T(8,128)(2,1)S(1)} collective-permute-done((bf16[48,1536]{1,0:T(8,128)(2,1)S(1)}, bf16[48,1536]{1,0:T(8,128)(2,1)S(1)}, u32[]{:S(2)}, u32[]{:S(2)}) %collective-permute-start.15) | collective-permute-done | bytes 147488 | tf_op jit(solution)/shard_map/ppermute | solution.py:565
  66.7 3.9 %seg_qkv.1 = (bf16[16,48,1152]{2,1,0:T(8,128)(2,1)S(1)}, bf16[8,48,384]{2,1,0:T(8,128)(2,1)S(1)}, bf16[8,48,384]{2,1,0:T(8,128)(2,1)S(1)}, bf16[256,1152]{1,0:T(...) custom-call(s32[5]{0:T(128)S(1)} %stack.15.where, ...), custom_call_target="tpu_custom_call" | custom-call | flops 452984832 | bytes 11453440 | tf_op jit(solution)/shard_map/seg_qkv/pallas_call | solution.py:595
  70.6 4.1 %collective-permute-start.20 = (bf16[8,48,384]{2,1,0:T(8,128)(2,1)S(1)}, bf16[8,48,384]{2,1,0:T(8,128)(2,1)S(1)}, u32[]{:S(2)}, u32[]{:S(2)}) collective-permute-start(bf16[8,48,384]{2,1,0:T(8,128)(2,1)S(1)} %get-tuple-element.296.low), channel_id=1, source_target_pairs={{0,16},{16,0},{1,17},{17,1},{2,18},{18,2},{3,19},{19,3},{4,20},{20... | collective-permute-start | bytes 884744 | tf_op jit(solution)/shard_map/ppermute | solution.py:573
  74.8 2.2 collective-permute-done.18.refs_10_.refs_8_
  77.0 3.1 %collective-permute-start.14 = (bf16[256,384]{1,0:T(8,128)(2,1)S(1)}, bf16[256,384]{1,0:T(8,128)(2,1)S(1)}, u32[]{:S(2)}, u32[]{:S(2)}) collective-permute-start(bf16[256,384]{1,0:T(8,128)(2,1)S(1)} %get-tuple-element.286.mixed), channel_id=1, source_target_pairs={{0,16},{16,0},{1,17},{17,1},{2,18},{18,2},{3,19},{19,3},{4,20},{20... | collective-permute-start | bytes 589832 | tf_op jit(solution)/shard_map/ppermute | solution.py:573
  83.2 3.3 %collective-permute-start.24 = (bf16[128,768]{1,0:T(8,128)(2,1)S(1)}, bf16[128,768]{1,0:T(8,128)(2,1)S(1)}, u32[]{:S(2)}, u32[]{:S(2)}) collective-permute-start(bf16[128,768]{1,0:T(8,128)(2,1)S(1)} %get-tuple-element.305.refs_12_.refs_5_.refs_6_), channel_id=1, source_target_pairs={{0,16},{16,0},{1,17},{17,1},{2,18},{18,2},{3,19},{19,3},{4,20},{20... | collective-permute-start | bytes 589832 | tf_op jit(solution)/shard_map/ppermute | solution.py:573
  92.6 3.0 %collective-permute-start.25 = (f32[128,768]{1,0:T(8,128)S(1)}, f32[128,768]{1,0:T(8,128)S(1)}, u32[]{:S(2)}, u32[]{:S(2)}) collective-permute-start(f32[128,768]{1,0:T(8,128)S(1)} %get-tuple-element.309), channel_id=1, source_target_pairs={{0,16},{16,0},{1,17},{17,1},{2,18},{18,2},{3,19},{19,3},{4,20},{20... | collective-permute-start | bytes 1179656 | tf_op jit(solution)/shard_map/ppermute | solution.py:573
  105.6 2.8 %collective-permute-start.33 = (f32[4,1664]{1,0:T(4,128)S(1)}, f32[4,1664]{1,0:T(4,128)S(1)}, u32[]{:S(2)}, u32[]{:S(2)}) collective-permute-start(f32[4,1664]{1,0:T(4,128)S(1)} %pad_maximum_fusion.12.refs_0_), channel_id=1, source_target_pairs={{0,8},{1,9},{2,10},{3,11},{4,12},{5,13},{6,14},{7,15},{8,0},{9,1},... | collective-permute-start | bytes 79880 | tf_op jit(solution)/shard_map/ppermute | solution.py:565
  125.3 2.5 %seg_mlp_near.1 = (bf16[4,48,3072]{2,1,0:T(8,128)(2,1)S(1)}, bf16[4,48,3072]{2,1,0:T(8,128)(2,1)S(1)}, bf16[4,48,3072]{2,1,0:T(8,128)(2,1)S(1)}) custom-call(s32[5]{0:T(128)S(1)} %stack.15.where, bf16[256,1024]{1,0:T(8,128)(2,1)S(1)} %get-tuple-element.328.refs_0_, bf16[128,768]{1,0:T(8,128)(2,1)S(1)} %get-tuple-element.317.refs_0_.refs_1_, ...), custom_call_target="tpu_custom_call" | custom-call | flops 905969664 | bytes 7602176 | tf_op jit(solution)/shard_map/seg_mlp_near/pallas_call | solution.py:595
  140.4 2.3 collective-permute-start.54
  146.5 2.3 head_attend_back.1
  154.9 2.8 %collective-permute-done.58.refs_13_ = bf16[4,48,3072]{2,1,0:T(8,128)(2,1)S(1)} collective-permute-done((bf16[4,48,3072]{2,1,0:T(8,128)(2,1)S(1)}, bf16[4,48,3072]{2,1,0:T(8,128)(2,1)S(1)}, u32[]{:S(2)}, u32[]{:S(2)}) %collective-permute-start.58) | collective-permute-done | bytes 1179680 | tf_op jit(solution)/shard_map/ppermute | solution.py:569
  161.6 3.0 %collective-permute-start.60 = (f32[1,768]{1,0:T(1,128)S(1)}, f32[1,768]{1,0:T(1,128)S(1)}, u32[]{:S(2)}, u32[]{:S(2)}) collective-permute-start(f32[1,768]{1,0:T(1,128)S(1)} %get-tuple-element.415.refs_0_.refs_3_), channel_id=1, source_target_pairs={{0,16},{16,0},{1,17},{17,1},{2,18},{18,2},{3,19},{19,3},{4,20},{20... | collective-permute-start | bytes 9224 | tf_op jit(solution)/shard_map/ppermute | solution.py:573
  170.9 3.8 %seg_attn_back.1.refs_2_ = bf16[256,1152]{1,0:T(8,128)(2,1)S(1)} custom-call(s32[5]{0:T(128)S(1)} %stack.15.where, bf16[256,1152]{1,0:T(8,128)(2,1)S(1)} %get-tuple-element.300.refs_0_, bf16[128,768]{1,0:T(8,128)(2,1)S(1)} %get-tuple-element.420.refs_1_, bf16[128,768]{1,0:T(8,128)(2,1)S(1)} %collective-permute-done.62.refs_2_.refs_4_, ...), custom_call_target="tpu_custom_call" | custom-call | flops 452984832 | bytes 1573888 | tf_op jit(solution)/shard_map/seg_attn_back/pallas_call | solution.py:595
  177.3 2.8 %seg_attn_near.1 = (bf16[4,48,1536]{2,1,0:T(8,128)(2,1)S(1)}, bf16[4,48,1536]{2,1,0:T(8,128)(2,1)S(1)}, bf16[4,48,1536]{2,1,0:T(8,128)(2,1)S(1)}, bf16[128,768]{...) custom-call(s32[5]{0:T(128)S(1)} %stack.15.where, ...), custom_call_target="tpu_custom_call" | custom-call | flops 452984832 | bytes 7444992 | tf_op jit(solution)/shard_map/seg_attn_near/pallas_call | solution.py:595
  180.1 8.2 %collective-permute-done.63.refs_2_ = bf16[64,3072]{1,0:T(8,128)(2,1)S(1)} collective-permute-done((bf16[64,3072]{1,0:T(8,128)(2,1)S(1)}, bf16[64,3072]{1,0:T(8,128)(2,1)S(1)}, u32[]{:S(2)}, u32[]{:S(2)}) %collective-permute-start.63) | collective-permute-done | bytes 393248 | tf_op jit(solution)/shard_map/ppermute | solution.py:565
  194.4 7.4 %collective-permute-done.64.refs_1_ = bf16[64,3072]{1,0:T(8,128)(2,1)S(1)} collective-permute-done((bf16[64,3072]{1,0:T(8,128)(2,1)S(1)}, bf16[64,3072]{1,0:T(8,128)(2,1)S(1)}, u32[]{:S(2)}, u32[]{:S(2)}) %collective-permute-start.64) | collective-permute-done | bytes 393248 | tf_op jit(solution)/shard_map/ppermute | solution.py:565
  201.8 3.0 %collective-permute-start.77 = (bf16[24,768]{1,0:T(8,128)(2,1)S(1)}, bf16[24,768]{1,0:T(8,128)(2,1)S(1)}, u32[]{:S(2)}, u32[]{:S(2)}) collective-permute-start(bf16[24,768]{1,0:T(8,128)(2,1)S(1)} %get-tuple-element.472), channel_id=1, source_target_pairs={{0,12},{1,13},{2,14},{3,15},{4,0},{5,1},{6,2},{7,3},{8,4},{9,5},{1... | collective-permute-start | bytes 110600 | tf_op jit(solution)/shard_map/ppermute | solution.py:565
  214.3 4.0 %collective-permute-done.73 = bf16[48,1536]{1,0:T(8,128)(2,1)S(1)} collective-permute-done((bf16[48,1536]{1,0:T(8,128)(2,1)S(1)}, bf16[48,1536]{1,0:T(8,128)(2,1)S(1)}, u32[]{:S(2)}, u32[]{:S(2)}) %collective-permute-start.73) | collective-permute-done | bytes 147488 | tf_op jit(solution)/shard_map/ppermute | solution.py:565
  218.3 2.3 collective-permute-start.81
  222.2 4.4 %head_owner.1 = (f32[48,3072]{1,0:T(8,128)S(1)}, f32[16,768]{1,0:T(8,128)S(1)}, f32[48,9216]{1,0:T(8,128)}, f32[576]{0:T(1024)}, f32[16,768]{1,0:T(8,128)}, /*index=5*/f32[1,1]{1,0:T(1,128)}) custom-call(s32[5]{0:T(128)S(1)} %stack.15.where, bf16[96,768]{1,0:T(8,128)(2,1)S(1)} %pad_maximum_fusion.11.refs_0_, ...), custom_call_target="tpu_custom_call" | custom-call | flops 28311552 | bytes 4503812 | tf_op jit(solution)/shard_map/head_owner/pallas_call | solution.py:595
  226.6 2.4 %collective-permute-start.83 = (f32[48,3072]{1,0:T(8,128)S(1)}, f32[48,3072]{1,0:T(8,128)S(1)}, u32[]{:S(2)}, u32[]{:S(2)}) collective-permute-start(f32[48,3072]{1,0:T(8,128)S(1)} %get-tuple-element.486.mlp), channel_id=1, source_target_pairs={{0,16},{16,0},{1,17},{17,1},{2,18},{18,2},{3,19},{19,3},{4,20},{20... | collective-permute-start | bytes 1769480 | tf_op jit(solution)/shard_map/ppermute | solution.py:573
  231.2 3.3 %seg_owner.1 = (f32[48,9216]{1,0:T(8,128)}, f32[576]{0:T(1024)}) custom-call(s32[5]{0:T(128)S(1)} %stack.15.where, f32[48,1536]{1,0:T(8,128)S(1)} %convert_add_fusion.1.attn, f32[48,1536]{1,0:T(8,128)S(1)} %collective-permute-done.82.attn_got, f32[48,3072]{1,0:T(8,128)S(1)} %get-tuple-element.486.mlp, f32[48,3072]{1,0:T(8,128)S(1)} %collective-permute-done.83.mlp_got, ...), custom_call_target="tpu_custom_call" | custom-call | bytes 3639552 | tf_op jit(solution)/shard_map/seg_owner/pallas_call | solution.py:595
  (213 shorter events, 116.8 us)
Async XLA Ops:
  8.0 17.3 %collective-permute-start.3 = (bf16[48,4736]{1,0:T(8,128)(2,1)S(1)}, bf16[48,4736]{1,0:T(8,128)(2,1)S(1)}, u32[]{:S(2)}, u32[]{:S(2)}) collective-permute-start(bf16[48,4736]{1,0:T(8,128)(2,1)S(1)} %pad_maximum_fusion.10), channel_id=1, source_target_pairs={{0,1},{1,0},{2,3},{3,2},{4,5},{5,4},{6,7},{7,6},{8,9},{9,8},{10,11... | collective-permute-start | bytes 1363976 | tf_op jit(solution)/shard_map/ppermute | solution.py:569
  9.3 16.0 %collective-permute-start.4 = (bf16[48,4736]{1,0:T(8,128)(2,1)S(1)}, bf16[48,4736]{1,0:T(8,128)(2,1)S(1)}, u32[]{:S(2)}, u32[]{:S(2)}) collective-permute-start(bf16[48,4736]{1,0:T(8,128)(2,1)S(1)} %pad_maximum_fusion.10), channel_id=1, source_target_pairs={{0,2},{1,3},{2,0},{3,1},{4,6},{5,7},{6,4},{7,5},{8,10},{9,11},{10,... | collective-permute-start | bytes 1363976 | tf_op jit(solution)/shard_map/ppermute | solution.py:569
  9.7 11.7 %collective-permute-start.1 = (bf16[48,1664]{1,0:T(8,128)(2,1)S(1)}, bf16[48,1664]{1,0:T(8,128)(2,1)S(1)}, u32[]{:S(2)}, u32[]{:S(2)}) collective-permute-start(bf16[48,1664]{1,0:T(8,128)(2,1)S(1)} %get-tuple-element.255.refs_0_), channel_id=1, source_target_pairs={{0,8},{1,9},{2,10},{3,11},{4,12},{5,13},{6,14},{7,15},{8,0},{9,1},... | collective-permute-start | bytes 479240 | tf_op jit(solution)/shard_map/ppermute | solution.py:565
  12.0 13.3 %collective-permute-start = (bf16[48,1664]{1,0:T(8,128)(2,1)S(1)}, bf16[48,1664]{1,0:T(8,128)(2,1)S(1)}, u32[]{:S(2)}, u32[]{:S(2)}) collective-permute-start(bf16[48,1664]{1,0:T(8,128)(2,1)S(1)} %get-tuple-element.255.refs_0_), channel_id=1, source_target_pairs={{0,4},{1,5},{2,6},{3,7},{4,8},{5,9},{6,10},{7,11},{8,12},{9,13},{1... | collective-permute-start | bytes 479240 | tf_op jit(solution)/shard_map/ppermute | solution.py:565
  28.2 18.1 %collective-permute-start.8 = (bf16[48,7424]{1,0:T(8,128)(2,1)S(1)}, bf16[48,7424]{1,0:T(8,128)(2,1)S(1)}, u32[]{:S(2)}, u32[]{:S(2)}) collective-permute-start(bf16[48,7424]{1,0:T(8,128)(2,1)S(1)} %pad_maximum_fusion.6), channel_id=1, source_target_pairs={{0,2},{1,3},{2,0},{3,1},{4,6},{5,7},{6,4},{7,5},{8,10},{9,11},{10,... | collective-permute-start | bytes 2138120 | tf_op jit(solution)/shard_map/ppermute | solution.py:569
  29.5 16.8 %collective-permute-start.7 = (bf16[48,7296]{1,0:T(8,128)(2,1)S(1)}, bf16[48,7296]{1,0:T(8,128)(2,1)S(1)}, u32[]{:S(2)}, u32[]{:S(2)}) collective-permute-start(bf16[48,7296]{1,0:T(8,128)(2,1)S(1)} %pad_maximum_fusion.7), channel_id=1, source_target_pairs={{0,1},{1,0},{2,3},{3,2},{4,5},{5,4},{6,7},{7,6},{8,9},{9,8},{10,11... | collective-permute-start | bytes 2101256 | tf_op jit(solution)/shard_map/ppermute | solution.py:569
  33.1 11.1 %collective-permute-start.9 = (bf16[48,1536]{1,0:T(8,128)(2,1)S(1)}, bf16[48,1536]{1,0:T(8,128)(2,1)S(1)}, u32[]{:S(2)}, u32[]{:S(2)}) collective-permute-start(bf16[48,1536]{1,0:T(8,128)(2,1)S(1)} %get-tuple-element.276.refs_0_), channel_id=1, source_target_pairs={{0,4},{1,5},{2,6},{3,7},{4,8},{5,9},{6,10},{7,11},{8,12},{9,13},{1... | collective-permute-start | bytes 442376 | tf_op jit(solution)/shard_map/ppermute | solution.py:565
  46.5 16.1 %collective-permute-start.13 = (bf16[48,7168]{1,0:T(8,128)(2,1)S(1)}, bf16[48,7168]{1,0:T(8,128)(2,1)S(1)}, u32[]{:S(2)}, u32[]{:S(2)}) collective-permute-start(bf16[48,7168]{1,0:T(8,128)(2,1)S(1)} %pad_maximum_fusion.8), channel_id=1, source_target_pairs={{0,2},{1,3},{2,0},{3,1},{4,6},{5,7},{6,4},{7,5},{8,10},{9,11},{10,... | collective-permute-start | bytes 2064392 | tf_op jit(solution)/shard_map/ppermute | solution.py:569
  47.1 15.4 %collective-permute-start.12 = (bf16[48,7040]{1,0:T(8,128)(2,1)S(1)}, bf16[48,7040]{1,0:T(8,128)(2,1)S(1)}, u32[]{:S(2)}, u32[]{:S(2)}) collective-permute-start(bf16[48,7040]{1,0:T(8,128)(2,1)S(1)} %pad_maximum_fusion.9), channel_id=1, source_target_pairs={{0,1},{1,0},{2,3},{3,2},{4,5},{5,4},{6,7},{7,6},{8,9},{9,8},{10,11... | collective-permute-start | bytes 2027528 | tf_op jit(solution)/shard_map/ppermute | solution.py:569
  48.3 10.5 %collective-permute-start.16 = (bf16[48,1536]{1,0:T(8,128)(2,1)S(1)}, bf16[48,1536]{1,0:T(8,128)(2,1)S(1)}, u32[]{:S(2)}, u32[]{:S(2)}) collective-permute-start(bf16[48,1536]{1,0:T(8,128)(2,1)S(1)} %get-tuple-element.287.refs_0_), channel_id=1, source_target_pairs={{0,8},{1,9},{2,10},{3,11},{4,12},{5,13},{6,14},{7,15},{8,0},{9,1},... | collective-permute-start | bytes 442376 | tf_op jit(solution)/shard_map/ppermute | solution.py:565
  50.8 11.2 %collective-permute-start.15 = (bf16[48,1536]{1,0:T(8,128)(2,1)S(1)}, bf16[48,1536]{1,0:T(8,128)(2,1)S(1)}, u32[]{:S(2)}, u32[]{:S(2)}) collective-permute-start(bf16[48,1536]{1,0:T(8,128)(2,1)S(1)} %get-tuple-element.287.refs_0_), channel_id=1, source_target_pairs={{0,4},{1,5},{2,6},{3,7},{4,8},{5,9},{6,10},{7,11},{8,12},{9,13},{1... | collective-permute-start | bytes 442376 | tf_op jit(solution)/shard_map/ppermute | solution.py:565
  62.7 14.3 %collective-permute-start.18 = (bf16[48,6912]{1,0:T(8,128)(2,1)S(1)}, bf16[48,6912]{1,0:T(8,128)(2,1)S(1)}, u32[]{:S(2)}, u32[]{:S(2)}) collective-permute-start(bf16[48,6912]{1,0:T(8,128)(2,1)S(1)} %get-tuple-element.291), channel_id=1, source_target_pairs={{0,1},{1,0},{2,3},{3,2},{4,5},{5,4},{6,7},{7,6},{8,9},{9,8},{10,11... | collective-permute-start | bytes 1990664 | tf_op jit(solution)/shard_map/ppermute | solution.py:569
  63.4 11.2 %collective-permute-start.35 = (bf16[48,1152]{1,0:T(8,128)(2,1)S(1)}, bf16[48,1152]{1,0:T(8,128)(2,1)S(1)}, u32[]{:S(2)}, u32[]{:S(2)}) collective-permute-start(bf16[48,1152]{1,0:T(8,128)(2,1)S(1)} %get-tuple-element.346), channel_id=1, source_target_pairs={{0,4},{1,5},{2,6},{3,7},{4,8},{5,9},{6,10},{7,11},{8,12},{9,13},{1... | collective-permute-start | bytes 331784 | tf_op jit(solution)/shard_map/ppermute | solution.py:565
  65.6 14.5 %collective-permute-start.19 = (bf16[48,6912]{1,0:T(8,128)(2,1)S(1)}, bf16[48,6912]{1,0:T(8,128)(2,1)S(1)}, u32[]{:S(2)}, u32[]{:S(2)}) collective-permute-start(bf16[48,6912]{1,0:T(8,128)(2,1)S(1)} %get-tuple-element.292), channel_id=1, source_target_pairs={{0,2},{1,3},{2,0},{3,1},{4,6},{5,7},{6,4},{7,5},{8,10},{9,11},{10,... | collective-permute-start | bytes 1990664 | tf_op jit(solution)/shard_map/ppermute | solution.py:569
  70.6 11.2 %collective-permute-start.20 = (bf16[8,48,384]{2,1,0:T(8,128)(2,1)S(1)}, bf16[8,48,384]{2,1,0:T(8,128)(2,1)S(1)}, u32[]{:S(2)}, u32[]{:S(2)}) collective-permute-start(bf16[8,48,384]{2,1,0:T(8,128)(2,1)S(1)} %get-tuple-element.296.low), channel_id=1, source_target_pairs={{0,16},{16,0},{1,17},{17,1},{2,18},{18,2},{3,19},{19,3},{4,20},{20... | collective-permute-start | bytes 884744 | tf_op jit(solution)/shard_map/ppermute | solution.py:573
  74.7 11.8 %collective-permute-start.37 = (bf16[48,1152]{1,0:T(8,128)(2,1)S(1)}, bf16[48,1152]{1,0:T(8,128)(2,1)S(1)}, u32[]{:S(2)}, u32[]{:S(2)}) collective-permute-start(bf16[48,1152]{1,0:T(8,128)(2,1)S(1)} %get-tuple-element.350), channel_id=1, source_target_pairs={{0,12},{1,13},{2,14},{3,15},{4,0},{5,1},{6,2},{7,3},{8,4},{9,5},{1... | collective-permute-start | bytes 331784 | tf_op jit(solution)/shard_map/ppermute | solution.py:565
  89.5 14.4 %collective-permute-start.38 = (bf16[48,4992]{1,0:T(8,128)(2,1)S(1)}, bf16[48,4992]{1,0:T(8,128)(2,1)S(1)}, u32[]{:S(2)}, u32[]{:S(2)}) collective-permute-start(bf16[48,4992]{1,0:T(8,128)(2,1)S(1)} %constant_dynamic-update-slice_fusion), channel_id=1, source_target_pairs={{0,1},{1,0},{2,3},{3,2},{4,5},{5,4},{6,7},{7,6},{8,9},{9,8},{10,11... | collective-permute-start | bytes 1437704 | tf_op jit(solution)/shard_map/ppermute | solution.py:569
  90.5 13.5 %collective-permute-start.39 = (bf16[48,4992]{1,0:T(8,128)(2,1)S(1)}, bf16[48,4992]{1,0:T(8,128)(2,1)S(1)}, u32[]{:S(2)}, u32[]{:S(2)}) collective-permute-start(bf16[48,4992]{1,0:T(8,128)(2,1)S(1)} %constant_dynamic-update-slice_fusion), channel_id=1, source_target_pairs={{0,2},{1,3},{2,0},{3,1},{4,6},{5,7},{6,4},{7,5},{8,10},{9,11},{10,... | collective-permute-start | bytes 1437704 | tf_op jit(solution)/shard_map/ppermute | solution.py:569
  114.6 14.9 %collective-permute-start.47 = (bf16[2,48,3072]{2,1,0:T(8,128)(2,1)S(1)}, bf16[2,48,3072]{2,1,0:T(8,128)(2,1)S(1)}, u32[]{:S(2)}, u32[]{:S(2)}) collective-permute-start(bf16[2,48,3072]{2,1,0:T(8,128)(2,1)S(1)} %get-tuple-element.376), channel_id=1, source_target_pairs={{0,2},{1,3},{2,0},{3,1},{4,6},{5,7},{6,4},{7,5},{8,10},{9,11},{10,... | collective-permute-start | bytes 1769480 | tf_op jit(solution)/shard_map/ppermute | solution.py:569
  115.3 14.6 %collective-permute-start.48 = (bf16[2,48,3072]{2,1,0:T(8,128)(2,1)S(1)}, bf16[2,48,3072]{2,1,0:T(8,128)(2,1)S(1)}, u32[]{:S(2)}, u32[]{:S(2)}) collective-permute-start(bf16[2,48,3072]{2,1,0:T(8,128)(2,1)S(1)} %get-tuple-element.378), channel_id=1, source_target_pairs={{0,1},{1,0},{2,3},{3,2},{4,5},{5,4},{6,7},{7,6},{8,9},{9,8},{10,11... | collective-permute-start | bytes 1769480 | tf_op jit(solution)/shard_map/ppermute | solution.py:569
  131.3 26.4 %collective-permute-start.58 = (bf16[4,48,3072]{2,1,0:T(8,128)(2,1)S(1)}, bf16[4,48,3072]{2,1,0:T(8,128)(2,1)S(1)}, u32[]{:S(2)}, u32[]{:S(2)}) collective-permute-start(bf16[4,48,3072]{2,1,0:T(8,128)(2,1)S(1)} %get-tuple-element.407), channel_id=1, source_target_pairs={{0,1},{1,0},{2,3},{3,2},{4,5},{5,4},{6,7},{7,6},{8,9},{9,8},{10,11... | collective-permute-start | bytes 3538952 | tf_op jit(solution)/shard_map/ppermute | solution.py:569
  132.3 26.0 %collective-permute-start.59 = (bf16[4,48,3072]{2,1,0:T(8,128)(2,1)S(1)}, bf16[4,48,3072]{2,1,0:T(8,128)(2,1)S(1)}, u32[]{:S(2)}, u32[]{:S(2)}) collective-permute-start(bf16[4,48,3072]{2,1,0:T(8,128)(2,1)S(1)} %get-tuple-element.408), channel_id=1, source_target_pairs={{0,2},{1,3},{2,0},{3,1},{4,6},{5,7},{6,4},{7,5},{8,10},{9,11},{10,... | collective-permute-start | bytes 3538952 | tf_op jit(solution)/shard_map/ppermute | solution.py:569
  159.8 16.0 %collective-permute-start.65 = (bf16[64,3072]{1,0:T(8,128)(2,1)S(1)}, bf16[64,3072]{1,0:T(8,128)(2,1)S(1)}, u32[]{:S(2)}, u32[]{:S(2)}) collective-permute-start(bf16[64,3072]{1,0:T(8,128)(2,1)S(1)} %get-tuple-element.436), channel_id=1, source_target_pairs={{0,12},{1,13},{2,14},{3,15},{4,0},{5,1},{6,2},{7,3},{8,4},{9,5},{1... | collective-permute-start | bytes 1179656 | tf_op jit(solution)/shard_map/ppermute | solution.py:565
  169.8 18.5 %collective-permute-start.63 = (bf16[64,3072]{1,0:T(8,128)(2,1)S(1)}, bf16[64,3072]{1,0:T(8,128)(2,1)S(1)}, u32[]{:S(2)}, u32[]{:S(2)}) collective-permute-start(bf16[64,3072]{1,0:T(8,128)(2,1)S(1)} %get-tuple-element.433), channel_id=1, source_target_pairs={{0,8},{1,9},{2,10},{3,11},{4,12},{5,13},{6,14},{7,15},{8,0},{9,1},... | collective-permute-start | bytes 1179656 | tf_op jit(solution)/shard_map/ppermute | solution.py:565
  175.8 12.5 %collective-permute-start.66 = (bf16[2,48,1536]{2,1,0:T(8,128)(2,1)S(1)}, bf16[2,48,1536]{2,1,0:T(8,128)(2,1)S(1)}, u32[]{:S(2)}, u32[]{:S(2)}) collective-permute-start(bf16[2,48,1536]{2,1,0:T(8,128)(2,1)S(1)} %get-tuple-element.437), channel_id=1, source_target_pairs={{0,2},{1,3},{2,0},{3,1},{4,6},{5,7},{6,4},{7,5},{8,10},{9,11},{10,... | collective-permute-start | bytes 884744 | tf_op jit(solution)/shard_map/ppermute | solution.py:569
  176.6 11.7 %collective-permute-start.67 = (bf16[2,48,1536]{2,1,0:T(8,128)(2,1)S(1)}, bf16[2,48,1536]{2,1,0:T(8,128)(2,1)S(1)}, u32[]{:S(2)}, u32[]{:S(2)}) collective-permute-start(bf16[2,48,1536]{2,1,0:T(8,128)(2,1)S(1)} %get-tuple-element.439), channel_id=1, source_target_pairs={{0,1},{1,0},{2,3},{3,2},{4,5},{5,4},{6,7},{7,6},{8,9},{9,8},{10,11... | collective-permute-start | bytes 884744 | tf_op jit(solution)/shard_map/ppermute | solution.py:569
  189.0 16.9 %collective-permute-start.68 = (bf16[4,48,1536]{2,1,0:T(8,128)(2,1)S(1)}, bf16[4,48,1536]{2,1,0:T(8,128)(2,1)S(1)}, u32[]{:S(2)}, u32[]{:S(2)}) collective-permute-start(bf16[4,48,1536]{2,1,0:T(8,128)(2,1)S(1)} %get-tuple-element.445), channel_id=1, source_target_pairs={{0,1},{1,0},{2,3},{3,2},{4,5},{5,4},{6,7},{7,6},{8,9},{9,8},{10,11... | collective-permute-start | bytes 1769480 | tf_op jit(solution)/shard_map/ppermute | solution.py:569
  189.9 16.0 %collective-permute-start.69 = (bf16[4,48,1536]{2,1,0:T(8,128)(2,1)S(1)}, bf16[4,48,1536]{2,1,0:T(8,128)(2,1)S(1)}, u32[]{:S(2)}, u32[]{:S(2)}) collective-permute-start(bf16[4,48,1536]{2,1,0:T(8,128)(2,1)S(1)} %get-tuple-element.446), channel_id=1, source_target_pairs={{0,2},{1,3},{2,0},{3,1},{4,6},{5,7},{6,4},{7,5},{8,10},{9,11},{10,... | collective-permute-start | bytes 1769480 | tf_op jit(solution)/shard_map/ppermute | solution.py:569
  190.5 11.2 %collective-permute-start.64 = (bf16[64,3072]{1,0:T(8,128)(2,1)S(1)}, bf16[64,3072]{1,0:T(8,128)(2,1)S(1)}, u32[]{:S(2)}, u32[]{:S(2)}) collective-permute-start(bf16[64,3072]{1,0:T(8,128)(2,1)S(1)} %get-tuple-element.434), channel_id=1, source_target_pairs={{0,4},{1,5},{2,6},{3,7},{4,8},{5,9},{6,10},{7,11},{8,12},{9,13},{1... | collective-permute-start | bytes 1179656 | tf_op jit(solution)/shard_map/ppermute | solution.py:565
  209.7 12.5 %collective-permute-start.80 = (bf16[96,768]{1,0:T(8,128)(2,1)S(1)}, bf16[96,768]{1,0:T(8,128)(2,1)S(1)}, u32[]{:S(2)}, u32[]{:S(2)}) collective-permute-start(bf16[96,768]{1,0:T(8,128)(2,1)S(1)} %pad_maximum_fusion.11.refs_0_), channel_id=1, source_target_pairs={{0,3},{1,2},{2,1},{3,0},{4,7},{5,6},{6,5},{7,4},{8,11},{9,10},{10,... | collective-permute-start | bytes 442376 | tf_op jit(solution)/shard_map/ppermute | solution.py:569
  210.9 11.3 %collective-permute-start.79 = (bf16[96,768]{1,0:T(8,128)(2,1)S(1)}, bf16[96,768]{1,0:T(8,128)(2,1)S(1)}, u32[]{:S(2)}, u32[]{:S(2)}) collective-permute-start(bf16[96,768]{1,0:T(8,128)(2,1)S(1)} %pad_maximum_fusion.11.refs_0_), channel_id=1, source_target_pairs={{0,2},{1,3},{2,0},{3,1},{4,6},{5,7},{6,4},{7,5},{8,10},{9,11},{10,... | collective-permute-start | bytes 442376 | tf_op jit(solution)/shard_map/ppermute | solution.py:569
  211.7 10.5 %collective-permute-start.78 = (bf16[96,768]{1,0:T(8,128)(2,1)S(1)}, bf16[96,768]{1,0:T(8,128)(2,1)S(1)}, u32[]{:S(2)}, u32[]{:S(2)}) collective-permute-start(bf16[96,768]{1,0:T(8,128)(2,1)S(1)} %pad_maximum_fusion.11.refs_0_), channel_id=1, source_target_pairs={{0,1},{1,0},{2,3},{3,2},{4,5},{5,4},{6,7},{7,6},{8,9},{9,8},{10,11... | collective-permute-start | bytes 442376 | tf_op jit(solution)/shard_map/ppermute | solution.py:569
  (61 other events, 301.8 us)
